TPU v7x, 256 devices: a whole 4x4x8 slice. The times are simulated.
256 devices in a mesh: ctx: 16 (over y_hi, z), head: 8 (over x, core), rep: 2 (over y_lo).
Axes of the slice: x: 4, y: 4 (y_hi: 2, y_lo: 2; y = y_hi * 2 + y_lo), z: 8, core: 2. Of those that a mesh axis runs over, the one named last changes fastest.
Arguments:
- query_latent: bfloat16 [8192, 1536], P(('rep', 'ctx')), parts along dimension 0, may hold values from -6 to 6
- key_rows: bfloat16 [8192, 576], P(('rep', 'ctx')), parts along dimension 0, may hold values from -640 to 640
- key_cache: bfloat16 [1024, 576], P('rep'), parts along dimension 0, may hold values from -640 to 640
- prompt_start: int32 [2], P('rep'), parts along dimension 0, may hold values from 0 to 512
- w_query: bfloat16 [1536, 12288], P(None, 'head'), may hold values from -0.15625 to 0.15625
- w_key_up: bfloat16 [64, 128, 512], P('head'), may hold values from -0.5 to 0.5
- w_value_up: bfloat16 [64, 512, 128], P('head'), may hold values from -0.25 to 0.25
- w_output: bfloat16 [64, 128, 7168], P('head', 'ctx'), may hold values from -0.09375 to 0.09375
Outputs:
- layer_out: bfloat16 [8192, 7168], P(('rep', 'ctx'), 'head'), parts along dimension 0
There are 2 independent parts, one for each index of `rep`. A program takes and returns all parts, laid end to end along the dimension named above; an argument that names none is the same for every part. Nothing has to cross between parts.
All inputs are finite; a program needn't handle non-finite values.
Results may differ from a plain program's by a relative error of at most 0.017.
The roundings to bfloat16 on the way count: a program that leaves them out, or rounds other values in their place, can miss the bound.
Values may be sent and summed in bfloat16 or wider, within the bound.
No kernel may reach another device: no remote copies, remote signals or barrier semaphores. Data moves between devices by JAX's collectives and lax.ppermute only.
A program may use at most 128 MiB of HBM per device.

v0:
```python
import jax
import jax.numpy as jnp
from jax import lax
from jax.sharding import PartitionSpec as P


def passed_along(x, axis, by):
    devices = lax.axis_size(axis)
    pairs = [(i, i + by) for i in range(devices) if 0 <= i + by < devices]
    return lax.ppermute(x, axis, pairs)


def rotate(values, positions):
    half_dim = values.shape[-1] // 2
    inverse = jnp.power(
        jnp.float32(10000.0), -jnp.arange(half_dim, dtype=jnp.float32) * (2.0 / values.shape[-1])
    )
    angles = positions[..., None] * inverse
    cosine = jnp.cos(angles)
    sines = jnp.sin(angles)
    lower_half = values[..., :half_dim]
    upper_half = values[..., half_dim:]
    return jnp.concatenate(
        [lower_half * cosine - upper_half * sines, lower_half * sines + upper_half * cosine], -1
    )


def local(query_latent, key_rows, key_cache, prompt_start, w_query, w_key_up, w_value_up, w_output):
    tok_rows = query_latent.shape[0]
    heads_dev, nope_dim, latent = w_key_up.shape
    rope_dim = key_rows.shape[1] - latent
    window = key_cache.shape[0]
    slab_index = lax.axis_index("ctx")
    queries = jnp.dot(query_latent, w_query, preferred_element_type=jnp.float32).astype(
        jnp.bfloat16
    )
    queries = queries.reshape(tok_rows, heads_dev, nope_dim + rope_dim)
    query_lat = jnp.einsum(
        "thn,hnl->thl", queries[..., :nope_dim], w_key_up, preferred_element_type=jnp.float32
    ).astype(jnp.bfloat16)
    token_pos = (slab_index * tok_rows + jnp.arange(tok_rows, dtype=jnp.int32)).astype(jnp.float32)
    query_rot = rotate(queries[..., nope_dim:].astype(jnp.float32), token_pos[:, None]).astype(
        jnp.bfloat16
    )
    key_rot = rotate(key_rows[:, latent:].astype(jnp.float32), token_pos).astype(jnp.bfloat16)
    own_keys = jnp.concatenate([key_rows[:, :latent], key_rot], 1)
    piece_rows = min(tok_rows, window)
    hop_count = window // piece_rows
    received = []
    for hop_number in range(hop_count):
        received.append(passed_along(own_keys, "ctx", hop_number + 1))
    key_blocks = []
    for hop_number in range(hop_count):
        distance = hop_number + 1
        cache_slot = jnp.clip(hop_count - distance + slab_index, 0, hop_count - 1)
        cached = lax.dynamic_slice_in_dim(key_cache, cache_slot * piece_rows, piece_rows, 0)
        key_blocks.append(jnp.where(slab_index < distance, cached, received[hop_number]))
    all_keys = jnp.concatenate(key_blocks[::-1] + [own_keys], 0)
    key_span = all_keys.shape[0]
    key_lat = all_keys[:, :latent]
    score_scale = (nope_dim + rope_dim) ** (-0.5)
    scores = jnp.einsum("thl,kl->htk", query_lat, key_lat, preferred_element_type=jnp.float32)
    scores = scores + jnp.einsum(
        "thr,kr->htk", query_rot, all_keys[:, latent:], preferred_element_type=jnp.float32
    )
    scores = scores * score_scale
    key_pos = jnp.arange(key_span, dtype=jnp.int32) - window
    row_ids = jnp.arange(tok_rows, dtype=jnp.int32)
    relative = key_pos[None, :] - row_ids[:, None]
    in_prompt = slab_index * tok_rows + key_pos >= -prompt_start[0]
    visible = (relative <= 0) & (relative > -window) & in_prompt[None, :]
    scores = jnp.where(visible[None], scores, -1e30)
    row_max = jnp.max(scores, axis=-1, keepdims=True)
    powers = jnp.exp(scores - row_max)
    weights = (powers / jnp.sum(powers, axis=-1, keepdims=True)).astype(jnp.bfloat16)
    mixed_lat = jnp.einsum(
        "htk,kl->thl", weights, key_lat, preferred_element_type=jnp.float32
    ).astype(jnp.bfloat16)
    attention = jnp.einsum(
        "thl,hlv->thv", mixed_lat, w_value_up, preferred_element_type=jnp.float32
    ).astype(jnp.bfloat16)
    full_rows = lax.all_gather(w_output, "ctx", axis=1, tiled=True)
    flat_attention = attention.reshape(tok_rows, -1)
    flat_rows = full_rows.reshape(-1, full_rows.shape[2])
    partial_value = jnp.dot(flat_attention, flat_rows, preferred_element_type=jnp.float32)
    return lax.psum_scatter(partial_value, "head", scatter_dimension=1, tiled=True).astype(
        jnp.bfloat16
    )


def solution(mesh):
    return jax.shard_map(
        local,
        mesh=mesh,
        in_specs=(
            P(("rep", "ctx"), None),
            P(("rep", "ctx"), None),
            P("rep", None),
            P("rep"),
            P(None, "head"),
            P("head", None, None),
            P("head", None, None),
            P("head", "ctx", None),
        ),
        out_specs=P(("rep", "ctx"), "head"),
        check_vma=False,
    )
```

profile of v0, /device:TPU:1, one launch (start us, length us, event | category | flops | bytes accessed | tf_op | source)
XLA Modules:
  0.0 288.0 jit_solution(6459296274716134943)
XLA Ops:
  6.5 0.0 copy-start
  6.5 0.0 all-gather.2.cloned.1.call-start
  6.5 0.7 all-gather.2.cloned.1.call-update
  7.3 0.0 reduce-scatter.2.cloned.1.call-start
  7.3 1.0 slice.30
  8.3 0.8 slice_convert_fusion.1
  9.1 0.2 multiply_cosine_fusion
  9.3 0.1 copy.27
  9.4 0.1 copy.28
  9.5 0.1 copy.43
  9.7 0.8 pad_maximum_fusion
  10.5 6.4 %collective-permute-start = (bf16[256,576]{1,0:T(8,128)(2,1)}, bf16[256,576]{1,0:T(8,128)(2,1)}, u32[]{:S(2)}, u32[]{:S(2)}) collective-permute-start(bf16[256,576]{1,0:T(8,128)(2,1)} %pad_maximum_fusion), channel_id=1, source_target_pairs={{0,32},{16,48},{32,64},{48,80},{64,96},{80,112},{96,128},{112,144}... | collective-permute-start | bytes 884744 | tf_op jit(solution)/shard_map/ppermute | solution.py:10
  16.9 4.3 %collective-permute-start.1 = (bf16[256,576]{1,0:T(8,128)(2,1)}, bf16[256,576]{1,0:T(8,128)(2,1)}, u32[]{:S(2)}, u32[]{:S(2)}) collective-permute-start(bf16[256,576]{1,0:T(8,128)(2,1)} %pad_maximum_fusion), channel_id=1, source_target_pairs={{0,16},{16,32},{32,48},{48,64},{64,80},{80,96},{96,112},{112,128},... | collective-permute-start | bytes 884744 | tf_op jit(solution)/shard_map/ppermute | solution.py:10
  21.2 4.0 %convolution_convert_fusion = bf16[256,1536]{1,0:T(8,128)(2,1)S(1)} fusion(bf16[256,1536]{1,0:T(8,128)(2,1)} %param.8, bf16[1536,1536]{1,0:T(8,128)(2,1)} %param.12), kind=kOutput, calls=%fused_computation.6 | convolution fusion | flops 1208352768 | bytes 6291456 | tf_op jit(solution)/shard_map/dot_general | solution.py:34
  25.2 0.3 copy.30
  26.2 0.7 subtract_convert_fusion
  26.9 0.3 fusion.18
  27.2 1.1 constant_dynamic-slice_fusion.1
  28.4 0.2 copy.42
  28.6 0.2 copy.44
  28.8 0.0 collective-permute-done
  28.8 0.1 broadcast_select_fusion.1
  28.8 11.8 %collective-permute-done.1 = bf16[256,576]{1,0:T(8,128)(2,1)} collective-permute-done((bf16[256,576]{1,0:T(8,128)(2,1)}, bf16[256,576]{1,0:T(8,128)(2,1)}, u32[]{:S(2)}, u32[]{:S(2)}) %collective-permute-start.1) | collective-permute-done | bytes 294944 | tf_op jit(solution)/shard_map/ppermute | solution.py:10
  40.7 0.0 copy-start.3
  40.7 1.1 maximum_maximum_fusion
  41.8 0.0 copy-done
  41.8 6.1 %fusion.2 = f32[768,256,8]{1,0,2:T(8,128)} fusion(bf16[8,128,512]{2,1,0:T(8,128)(2,1)S(1)} %copy-done, bf16[768,576]{1,0:T(8,128)(2,1)} %maximum_maximum_fusion, bf16[256,8,192]{0,2,1:T(8,128)(2,1)S(1)} %bitcast.29), kind=kOutput, calls=%fused_computation.7 | convolution fusion | flops 1880096768 | bytes 8650752 | tf_op jit(solution)/shard_map/thl,kl->htk/dot_general | solution.py:62
  47.9 0.0 copy-done.3
  47.9 4.0 %bitcast_select_fusion = f32[8,256,768]{1,2,0:T(8,128)S(1)} fusion(f32[768,256,8]{1,0,2:T(8,128)} %fusion.2, pred[256,768]{0,1:T(8,128)(4,1)S(1)} %fusion.18, bf16[256,8,32]{0,2,1:T(8,128)(2,1)S(1)} %copy-done.3, bf16[256,8,32]{0,2,1:T(8,128)(2,1)S(1)} %get-tuple-element.5, bf16[256,32]{1,0:T(8,128)(2,1)S(1)} %copy.28, ...), kind=kOutput, calls=%fused_computation.2 | convolution fusion | flops 207060992 | bytes 13926400 | tf_op jit(solution)/shard_map/thr,kr->htk/dot_general | solution.py:63
  52.0 0.0 copy-start.1
  52.0 2.6 copy-done.1
  54.5 0.0 copy-start.2
  54.5 1.1 fusion.35
  55.7 0.1 copy-done.2
  55.8 7.8 %fusion.12 = bf16[256,8,128]{2,0,1:T(8,128)(2,1)S(1)} fusion(bf16[8,512,128]{2,1,0:T(8,128)(2,1)} %param.14, f32[8,256]{1,0:T(8,128)S(1)} %fusion.35, bf16[768,576]{1,0:T(8,128)(2,1)S(1)} %copy-done.2, f32[8,256,768]{1,2,0:T(8,128)} %copy-done.1), kind=kOutput, calls=%fused_computation.14 | convolution fusion | flops 1885080320 | bytes 14950400 | tf_op jit(solution)/shard_map/thl,hlv->thv/dot_general | solution.py:79
  63.5 159.8 %all-gather.2.cloned.1.call-done = bf16[8,128,7168]{2,1,0:T(8,128)(2,1)} async-done(((bf16[8,8,7168]{2,1,0:T(8,128)(2,1)}), bf16[8,128,7168]{2,1,0:T(8,128)(2,1)}) %all-gather.2.cloned.1.call-update) | async-done | bytes 14680080 | tf_op jit(solution)/shard_map/all_gather | solution.py:82
  223.3 9.1 %convolution_bitcast_fusion = f32[256,7168]{1,0:T(8,128)} fusion(bf16[256,8,128]{2,0,1:T(8,128)(2,1)S(1)} %fusion.12, bf16[8,128,7168]{2,1,0:T(8,128)(2,1)} %all-gather.2.cloned.1.call-done), kind=kOutput, calls=%fused_computation.1 | convolution fusion | flops 3758096384 | bytes 22544384 | tf_op jit(solution)/shard_map/dot_general | solution.py:85
  232.4 0.0 reduce-scatter.2.cloned.1.call-update
  232.4 46.8 %reduce-scatter.2.cloned.1.call-done = f32[256,896]{1,0:T(8,128)} async-done(((f32[256,7168]{1,0:T(8,128)}), f32[256,896]{1,0:T(8,128)}) %reduce-scatter.2.cloned.1.call-update) | async-done | bytes 917520 | tf_op jit(solution)/shard_map/reduce_scatter | solution.py:86
  279.2 2.0 convert_element_type.54
  (6 shorter events, 0.1 us)
Async XLA Ops:
  6.5 35.3 %copy-start = (bf16[8,128,512]{2,1,0:T(8,128)(2,1)S(1)}, bf16[8,128,512]{2,1,0:T(8,128)(2,1)}, u32[]{:S(2)}) copy-start(bf16[8,128,512]{2,1,0:T(8,128)(2,1)} %param.13) | copy-start | bytes 3145732
  6.5 216.8 %all-gather.2.cloned.1.call-start = ((), (), s32[]{:S(2)}) async-start(), calls=%async_computation.1 | async-start | bytes 15597568 | tf_op jit(solution)/shard_map/all_gather | solution.py:82
  7.3 271.9 %reduce-scatter.2.cloned.1.call-start = ((), (), s32[]{:S(2)}) async-start(), calls=%async_computation.2 | async-start | bytes 8257536 | tf_op jit(solution)/shard_map/reduce_scatter | solution.py:86
  10.5 18.3 %collective-permute-start = (bf16[256,576]{1,0:T(8,128)(2,1)}, bf16[256,576]{1,0:T(8,128)(2,1)}, u32[]{:S(2)}, u32[]{:S(2)}) collective-permute-start(bf16[256,576]{1,0:T(8,128)(2,1)} %pad_maximum_fusion), channel_id=1, source_target_pairs={{0,32},{16,48},{32,64},{48,80},{64,96},{80,112},{96,128},{112,144}... | collective-permute-start | bytes 884744 | tf_op jit(solution)/shard_map/ppermute | solution.py:10
  16.9 23.7 %collective-permute-start.1 = (bf16[256,576]{1,0:T(8,128)(2,1)}, bf16[256,576]{1,0:T(8,128)(2,1)}, u32[]{:S(2)}, u32[]{:S(2)}) collective-permute-start(bf16[256,576]{1,0:T(8,128)(2,1)} %pad_maximum_fusion), channel_id=1, source_target_pairs={{0,16},{16,32},{32,48},{48,64},{64,80},{80,96},{96,112},{112,128},... | collective-permute-start | bytes 884744 | tf_op jit(solution)/shard_map/ppermute | solution.py:10
  40.7 7.2 %copy-start.3 = (bf16[256,8,32]{0,2,1:T(8,128)(2,1)S(1)}, bf16[256,8,32]{0,2,1:T(8,128)(2,1)}, u32[]{:S(2)}) copy-start(bf16[256,8,32]{0,2,1:T(8,128)(2,1)} %get-tuple-element.6) | copy-start | bytes 393220
  52.0 2.6 copy-start.1
  54.5 1.2 copy-start.2
Sparse Core Ops, SparseCore 0:
  10.0 213.2 all-gather.1
  232.5 46.6 reduce-scatter.1
where the time goes:
time: 289 us; the launch traced here: 288 us
  waiting for transfers between devices  219 us (76%)
  matrix products  30.9 us (11%)
  between operations  14.2 us (5%)
  starting transfers between devices  10.8 us (4%)
  other arithmetic  7.18 us (2%)
  local copies, waits for them, and re-layouts  5.8 us (2%)
    all_gather x1, waiting for transfers between devices, local(): full_rows = lax.all_gather(w_output, 'ctx', axis=1, tiled=True)  160 us
    reduce_scatter x1, waiting for transfers between devices, local(): lax.psum_scatter(partial_value, 'head', scatter_dimension=1, tiled=True)  46.8 us
    ppermute x2, waiting for transfers between devices, passed_along(): return lax.ppermute(x, axis, pairs)  11.8 us
    ppermute x2, starting transfers between devices, passed_along(): return lax.ppermute(x, axis, pairs)  10.7 us
    dot_general x1, matrix products, local(): jnp.dot(flat_attention, flat_rows, preferred_element_type=jnp.float32)  9.08 us
    dot_general x1, matrix products, local(): jnp.einsum('thl,hlv->thv', mixed_lat, w_value_up, preferred_element_type=...  7.75 us
    dot_general x1, matrix products, local(): jnp.einsum('thl,kl->htk', query_lat, key_lat, preferred_element_type=jnp....  6.09 us
  transfers between devices with their start and end apart: 4, of which 3 were waited for; matrix products, arithmetic and copies ran while one was open for 10% of the time, Pallas kernels for 0%

commit v1 on v0

v1 whole, which is shorter than its diff:
```python
import functools

import jax
import jax.numpy as jnp
from jax import lax
from jax.experimental import pallas as pl
from jax.experimental.pallas import tpu as pltpu
from jax.sharding import Mesh
from jax.sharding import PartitionSpec as P

AXES = ("yh", "z", "x", "c", "yl")
SIZES = (2, 8, 4, 2, 2)
CTX = ("yh", "z")
HEAD = ("x", "c")
BF = jnp.bfloat16
F32 = jnp.float32
VMEM = pltpu.MemorySpace.VMEM


def number_of(yh, z, x, c, yl):
    return (((yh * 8 + z) * 4 + x) * 2 + c) * 2 + yl


def moved(a, target):
    pairs = []
    for yh in range(2):
        for z in range(8):
            for x in range(4):
                for c in range(2):
                    for yl in range(2):
                        t = target(yh, z, x, c, yl)
                        pairs.append((number_of(yh, z, x, c, yl), number_of(*t)))
    return lax.ppermute(a, AXES, pairs)


def up_z(a):
    return moved(a, lambda yh, z, x, c, yl: (yh, (z + 1) % 8, x, c, yl))


def down_z(a):
    return moved(a, lambda yh, z, x, c, yl: (yh, (z - 1) % 8, x, c, yl))


def xor_y(a, q):
    return moved(a, lambda yh, z, x, c, yl: (yh ^ (q >> 1), z, x, c, yl ^ (q & 1)))


def other_core(a):
    return moved(a, lambda yh, z, x, c, yl: (yh, z, x, 1 - c, yl))


def along_x(a, d):
    return moved(a, lambda yh, z, x, c, yl: (yh, z, (x + d) % 4, c, yl))


def home(a, r):
    return moved(a, lambda yh, z, x, c, yl: (yh ^ c, z, x, yh, yl ^ r))


def passed_along(x, by):
    pairs = [(i, i + by) for i in range(16) if i + by < 16]
    return lax.ppermute(x, CTX, pairs)


def rotate(values, positions):
    half_dim = values.shape[-1] // 2
    inverse = jnp.power(
        jnp.float32(10000.0), -jnp.arange(half_dim, dtype=jnp.float32) * (2.0 / values.shape[-1])
    )
    angles = positions[..., None] * inverse
    cosine = jnp.cos(angles)
    sines = jnp.sin(angles)
    lower_half = values[..., :half_dim]
    upper_half = values[..., half_dim:]
    return jnp.concatenate(
        [lower_half * cosine - upper_half * sines, lower_half * sines + upper_half * cosine], -1
    )


def attention_of(query_latent, key_rows, key_cache, prompt_start, w_query, w_key_up, w_value_up):
    tok_rows = query_latent.shape[0]
    heads_dev, nope_dim, latent = w_key_up.shape
    rope_dim = key_rows.shape[1] - latent
    window = key_cache.shape[0]
    slab_index = lax.axis_index(CTX)
    queries = jnp.dot(query_latent, w_query, preferred_element_type=F32).astype(BF)
    queries = queries.reshape(tok_rows, heads_dev, nope_dim + rope_dim)
    query_lat = jnp.einsum(
        "thn,hnl->thl", queries[..., :nope_dim], w_key_up, preferred_element_type=F32
    ).astype(BF)
    token_pos = (slab_index * tok_rows + jnp.arange(tok_rows, dtype=jnp.int32)).astype(F32)
    query_rot = rotate(queries[..., nope_dim:].astype(F32), token_pos[:, None]).astype(BF)
    key_rot = rotate(key_rows[:, latent:].astype(F32), token_pos).astype(BF)
    own_keys = jnp.concatenate([key_rows[:, :latent], key_rot], 1)
    received = [passed_along(own_keys, 1), passed_along(own_keys, 2)]
    key_blocks = []
    for distance in (1, 2):
        cache_slot = jnp.clip(2 - distance + slab_index, 0, 1)
        cached = lax.dynamic_slice_in_dim(key_cache, cache_slot * tok_rows, tok_rows, 0)
        key_blocks.append(jnp.where(slab_index < distance, cached, received[distance - 1]))
    all_keys = jnp.concatenate(key_blocks[::-1] + [own_keys], 0)
    key_span = all_keys.shape[0]
    key_lat = all_keys[:, :latent]
    score_scale = (nope_dim + rope_dim) ** (-0.5)
    scores = jnp.einsum("thl,kl->htk", query_lat, key_lat, preferred_element_type=F32)
    scores = scores + jnp.einsum(
        "thr,kr->htk", query_rot, all_keys[:, latent:], preferred_element_type=F32
    )
    scores = scores * score_scale
    key_pos = jnp.arange(key_span, dtype=jnp.int32) - window
    row_ids = jnp.arange(tok_rows, dtype=jnp.int32)
    relative = key_pos[None, :] - row_ids[:, None]
    in_prompt = slab_index * tok_rows + key_pos >= -prompt_start[0]
    visible = (relative <= 0) & (relative > -window) & in_prompt[None, :]
    scores = jnp.where(visible[None], scores, -1e30)
    row_max = jnp.max(scores, axis=-1, keepdims=True)
    powers = jnp.exp(scores - row_max)
    weights = (powers / jnp.sum(powers, axis=-1, keepdims=True)).astype(BF)
    mixed_lat = jnp.einsum("htk,kl->thl", weights, key_lat, preferred_element_type=F32).astype(BF)
    attention = jnp.einsum("thl,hlv->thv", mixed_lat, w_value_up, preferred_element_type=F32)
    return attention.astype(BF).reshape(tok_rows, -1)


def quarter_kernel(place, rows, own, other):
    for out, flip in ((own, 0), (other, 3)):
        y = place[1] ^ flip
        odd = y % 2
        base = 896 * (y // 2) + 384 * odd
        pieces = []
        for d in range(4):
            start = pl.multiple_of(1792 * ((place[0] + d) % 4) + base, 128)
            wide = rows[:, pl.ds(start, 512)]
            pieces.append(jnp.where(odd == 1, wide[:, 64:], wide[:, :448]))
        out[...] = jnp.concatenate(pieces, 1)


def project_kernel(theirs, place, *refs):
    groups, blocks, (out, rows, total) = refs[:4], refs[4:20], refs[20:]
    first = 2 * (place[0] ^ theirs)
    for pick in (0, 2):

        @pl.when(first == pick)
        def _():
            for g in range(2):
                for p in range(2):
                    half = pl.ds(pl.multiple_of(512 * (place[1] ^ p), 512), 512)
                    rows[pl.ds(256 * g, 256), pl.ds(512 * p, 512)] = groups[pick + g][:, half]

    def step(n, carry):
        columns = pl.ds(pl.multiple_of(n * 256, 256), 256)
        weights = jnp.concatenate([block[:, columns] for block in blocks], 0)
        total[:, columns] = jnp.dot(rows[...], weights, preferred_element_type=F32)
        return carry

    lax.fori_loop(0, 7, step, 0)
    for d in range(4):
        span = slice(448 * d, 448 * d + 448)
        out[d] = jnp.concatenate([total[:256, span], total[256:, span]], 1).astype(out.dtype)


def whole(n):
    return [pl.BlockSpec(memory_space=VMEM)] * n


def scalars(n=1):
    return [pl.BlockSpec(memory_space=pltpu.MemorySpace.SMEM)] * n


def quarters(rows, x, y):
    return pl.pallas_call(
        quarter_kernel,
        out_shape=[jax.ShapeDtypeStruct((64, 1792), BF)] * 2,
        in_specs=scalars() + whole(1),
        out_specs=whole(2),
        name="quarters",
        cost_estimate=pl.CostEstimate(flops=0, bytes_accessed=2 << 20, transcendentals=0),
    )(jnp.stack([x, y]), rows)


def project(theirs, place, groups, blocks, kind):
    return pl.pallas_call(
        functools.partial(project_kernel, theirs),
        out_shape=jax.ShapeDtypeStruct((4, 256, 896), kind),
        in_specs=scalars() + whole(20),
        out_specs=whole(1)[0],
        scratch_shapes=[pltpu.VMEM((512, 1024), BF), pltpu.VMEM((512, 1792), F32)],
        compiler_params=pltpu.CompilerParams(vmem_limit_bytes=40 << 20),
        name="project",
        cost_estimate=pl.CostEstimate(
            flops=2 * 512 * 1024 * 1792, bytes_accessed=8 << 20, transcendentals=0
        ),
    )(place, *groups, *blocks)


def local(query_latent, key_rows, key_cache, prompt_start, w_query, w_key_up, w_value_up, w_output):
    yh, z, x, c, yl = (lax.axis_index(a) for a in AXES)
    y = 2 * yh + yl
    own, given = quarters(w_output.reshape(64, 7168), x, y)
    other = xor_y(given, 3)
    blocks = [[own] + [None] * 7, [other] + [None] * 7]
    for p in range(2):
        up = down = blocks[p][0]
        for s in range(1, 5):
            if s < 4 or p == 0:
                up = up_z(up)
                blocks[p][8 - s] = up
            if s < 4 or p == 1:
                down = down_z(down)
                blocks[p][s] = down
    attention = attention_of(
        query_latent, key_rows, key_cache, prompt_start, w_query, w_key_up, w_value_up
    )
    column = jnp.arange(1024, dtype=jnp.int32)
    source = (
        (column // 8 % 8) * 128 + (column // 512) * 64 + ((z + column // 64) % 8) * 8 + column % 8
    )
    reorder = (jnp.arange(1024, dtype=jnp.int32)[:, None] == source[None, :]).astype(BF)
    rows = jnp.dot(attention, reorder, preferred_element_type=F32).astype(BF)
    groups = [rows] + [xor_y(rows, q) for q in (1, 2, 3)]
    place = jnp.stack([c, yh])
    flat = blocks[0] + blocks[1]
    theirs = other_core(project(1, place, groups, flat, BF))
    mine = project(0, place, groups, flat, F32)
    sums = mine + theirs.astype(F32)
    result = sums[0]
    for d in (2, 1, 3):
        result = result + along_x(sums[d].astype(BF), d).astype(F32)
    result = result.astype(BF)
    pieces = [home(result[:, 448 * r : 448 * r + 448], r) for r in range(2)]
    even = yl == 0
    return jnp.concatenate(
        [jnp.where(even, pieces[0], pieces[1]), jnp.where(even, pieces[1], pieces[0])], 1
    )


def solution(mesh):
    cut = Mesh(mesh.devices.reshape(SIZES), AXES) if hasattr(mesh, "devices") else mesh
    tokens = ("yl", "yh", "z")
    return jax.shard_map(
        local,
        mesh=cut,
        in_specs=(
            P(tokens, None),
            P(tokens, None),
            P("yl", None),
            P("yl"),
            P(None, HEAD),
            P(HEAD, None, None),
            P(HEAD, None, None),
            P(HEAD, CTX, None),
        ),
        out_specs=P(tokens, HEAD),
        check_vma=False,
    )
```

time: 289 us -> 157 us (0.54)
  waiting for transfers between devices: 219 us -> 51.8 us
  starting transfers between devices: 10.8 us -> 39 us
  between operations: 14.2 us -> 1.02 us
  Pallas kernels: 0 us -> 12.9 us
  local copies, waits for them, and re-layouts: 5.8 us -> 16.3 us
  matrix products: 30.9 us -> 25.4 us
  other arithmetic: 7.18 us -> 10.3 us
    all_gather x1 -> x0, waiting for transfers between devices: 160 us -> none  [local(): full_rows = lax.all_gather(w_output, 'ctx', axis=1, tiled=True)]
    reduce_scatter x1 -> x0, waiting for transfers between devices: 46.8 us -> none  [local(): lax.psum_scatter(partial_value, 'head', scatter_dimension=1, tiled=True)]
    ppermute x2 -> x26, waiting for transfers between devices: 11.8 us -> 51.8 us  [the longest x24 51.7 us: moved(): return lax.ppermute(a, AXES, pairs)]
    ppermute x2 -> x26, starting transfers between devices: 10.7 us -> 39 us  [the longest x24 28.3 us: moved(): return lax.ppermute(a, AXES, pairs)]
    pallas_call x0 -> x3, Pallas kernels: none -> 12.9 us  [the longest x2 10.6 us: project(): pl.pallas_call(functools.partial(project_kernel, theirs), out_shape=jax.S...]
    unnamed x11 -> x43, local copies, waits for them, and re-layouts: 3.2 us -> 12.4 us
    dot_general x5, matrix products: 30.9 us -> 25.4 us  [the longest x1 8.19 us: attention_of(): jnp.einsum('thl,hlv->thv', mixed_lat, w_value_up, preferred_element_type=...]
  transfers between devices with their start and end apart: 4 -> 26, of which waited for: 3 -> 11; matrix products, arithmetic and copies ran while one was open for 10% -> 23% of each run, Pallas kernels for 0% -> 5%
where the time goes in v1:
time: 157 us
  waiting for transfers between devices  51.8 us (33%)
  starting transfers between devices  39 us (25%)
  matrix products  25.4 us (16%)
  local copies, waits for them, and re-layouts  16.3 us (10%)
  Pallas kernels  12.9 us (8%)
  other arithmetic  10.3 us (7%)
    ppermute x24, waiting for transfers between devices, moved(): return lax.ppermute(a, AXES, pairs)  51.7 us
    ppermute x24, starting transfers between devices, moved(): return lax.ppermute(a, AXES, pairs)  28.3 us
    unnamed x43, local copies, waits for them, and re-layouts  12.4 us
    ppermute x2, starting transfers between devices, passed_along(): return lax.ppermute(x, CTX, pairs)  10.7 us
    pallas_call x2, Pallas kernels, project(): pl.pallas_call(functools.partial(project_kernel, theirs), out_shape=jax.S...  10.6 us
    dot_general x1, matrix products, attention_of(): jnp.einsum('thl,hlv->thv', mixed_lat, w_value_up, preferred_element_type=...  8.19 us
    dot_general x1, matrix products, attention_of(): jnp.einsum('thl,kl->htk', query_lat, key_lat, preferred_element_type=F32)  6.39 us
    dot_general x1, matrix products, attention_of(): jnp.dot(query_latent, w_query, preferred_element_type=F32).astype(BF)  4.87 us
  transfers between devices with their start and end apart: 26, of which 11 were waited for; matrix products, arithmetic and copies ran while one was open for 23% of the time, Pallas kernels for 5%

profile of v1, /device:TPU:1, one launch (start us, length us, event | category | flops | bytes accessed | tf_op | source)
XLA Modules:
  0.0 156.7 jit_solution(1416703429581021908)
XLA Ops:
  0.9 1.0 slice.51
  3.3 6.4 %collective-permute-start = (bf16[256,576]{1,0:T(8,128)(2,1)}, bf16[256,576]{1,0:T(8,128)(2,1)}, u32[]{:S(2)}, u32[]{:S(2)}) collective-permute-start(bf16[256,576]{1,0:T(8,128)(2,1)} %pad_maximum_fusion.1), channel_id=1, source_target_pairs={{0,32},{16,48},{32,64},{48,80},{64,96},{80,112},{96,128},{112,144}... | collective-permute-start | bytes 884744 | tf_op jit(solution)/shard_map/ppermute | solution.py:62
  9.7 4.3 %collective-permute-start.1 = (bf16[256,576]{1,0:T(8,128)(2,1)}, bf16[256,576]{1,0:T(8,128)(2,1)}, u32[]{:S(2)}, u32[]{:S(2)}) collective-permute-start(bf16[256,576]{1,0:T(8,128)(2,1)} %pad_maximum_fusion.1), channel_id=1, source_target_pairs={{0,16},{16,32},{32,48},{48,64},{64,80},{80,96},{96,112},{112,128},... | collective-permute-start | bytes 884744 | tf_op jit(solution)/shard_map/ppermute | solution.py:62
  14.6 2.3 %quarters.1 = (bf16[64,1792]{1,0:T(8,128)(2,1)}, bf16[64,1792]{1,0:T(8,128)(2,1)}) custom-call(s32[2]{0:T(128)} %pad_add_fusion.1.place, bf16[64,7168]{1,0:T(8,128)(2,1)} %bitcast.49), custom_call_target="tpu_custom_call" | custom-call | bytes 2097152 | tf_op jit(solution)/shard_map/quarters/pallas_call | solution.py:170
  16.9 1.4 collective-permute-start.8
  18.3 1.2 collective-permute-start.5
  19.6 1.5 collective-permute-start.12
  21.1 4.9 %convolution_convert_fusion = bf16[256,1536]{1,0:T(8,128)(2,1)} fusion(bf16[256,1536]{1,0:T(8,128)(2,1)} %param.8, bf16[1536,1536]{1,0:T(8,128)(2,1)} %param.12), kind=kOutput, calls=%fused_computation.8 | convolution fusion | flops 1208352768 | bytes 6291456 | tf_op jit(solution)/shard_map/dot_general | solution.py:86
  25.9 1.4 copy.32
  28.9 0.9 fusion.22
  29.8 1.1 constant_dynamic-slice_fusion.1
  32.8 6.8 %collective-permute-done.8.refs_11_ = bf16[64,1792]{1,0:T(8,128)(2,1)S(1)} collective-permute-done((bf16[64,1792]{1,0:T(8,128)(2,1)}, bf16[64,1792]{1,0:T(8,128)(2,1)S(1)}, u32[]{:S(2)}, u32[]{:S(2)}) %collective-permute-start.8) | collective-permute-done | bytes 229408 | tf_op jit(solution)/shard_map/ppermute | solution.py:33
  39.7 2.8 %collective-permute-start.6 = (bf16[64,1792]{1,0:T(8,128)(2,1)S(1)}, bf16[64,1792]{1,0:T(8,128)(2,1)}, u32[]{:S(2)}, u32[]{:S(2)}) collective-permute-start(bf16[64,1792]{1,0:T(8,128)(2,1)S(1)} %collective-permute-done.5.refs_5_), channel_id=1, source_target_pairs={{0,112},{1,113},{2,114},{3,115},{4,116},{5,117},{6,118},{7,119},{8... | collective-permute-start | bytes 688136 | tf_op jit(solution)/shard_map/ppermute | solution.py:33
  42.5 1.0 broadcast_select_fusion.1
  43.5 1.0 broadcast_select_fusion
  44.6 1.1 maximum_maximum_fusion
  45.7 6.4 %fusion.3 = f32[768,256,8]{1,0,2:T(8,128)} fusion(bf16[8,128,512]{2,1,0:T(8,128)(2,1)S(1)} %copy-done, bf16[768,576]{1,0:T(8,128)(2,1)} %maximum_maximum_fusion, bf16[256,8,192]{0,2,1:T(8,128)(2,1)} %bitcast.48), kind=kOutput, calls=%fused_computation.9 | convolution fusion | flops 1880096768 | bytes 8650752 | tf_op jit(solution)/shard_map/thl,kl->htk/dot_general | solution.py:105
  52.1 4.0 %bitcast_select_fusion = f32[8,256,768]{1,2,0:T(8,128)S(1)} fusion(f32[768,256,8]{1,0,2:T(8,128)} %fusion.3, pred[256,768]{0,1:T(8,128)(4,1)S(1)} %copy-done.17, bf16[256,8,32]{0,2,1:T(8,128)(2,1)S(1)} %copy-done.19, bf16[256,8,32]{0,2,1:T(8,128)(2,1)S(1)} %copy-done.18, bf16[256,32]{1,0:T(8,128)(2,1)S(1)} %copy.30, ...), kind=kOutput, calls=%fused_computation.1 | convolution fusion | flops 207060992 | bytes 13926400 | tf_op jit(solution)/shard_map/thr,kr->htk/dot_general | solution.py:106
  56.1 2.7 %copy-done.14 = f32[8,256,768]{1,2,0:T(8,128)} copy-done((f32[8,256,768]{1,2,0:T(8,128)}, f32[8,256,768]{1,2,0:T(8,128)S(1)}, u32[]{:S(2)}) %copy-start.14) | copy-done | bytes 6291480
  58.8 1.1 fusion.61
  60.0 8.2 %fusion.11 = bf16[8,256,128]{1,2,0:T(8,128)(2,1)} fusion(bf16[8,512,128]{2,1,0:T(8,128)(2,1)} %param.14, f32[8,256]{1,0:T(8,128)S(1)} %fusion.61, bf16[768,576]{1,0:T(8,128)(2,1)S(1)} %copy-done.16, f32[8,256,768]{1,2,0:T(8,128)} %copy-done.14), kind=kOutput, calls=%fused_computation.16 | convolution fusion | flops 1885080320 | bytes 14950400 | tf_op jit(solution)/shard_map/thl,hlv->thv/dot_general | solution.py:120
  68.2 1.9 %fusion.14.refs_0_ = bf16[256,1024]{1,0:T(8,128)(2,1)S(1)} fusion(bf16[256,1024]{0,1:T(8,128)(2,1)} %bitcast.50, s32[1024]{0:T(1024)S(1)} %fusion.46), kind=kOutput, calls=%fused_computation.17 | convolution fusion | flops 538181632 | bytes 1052672 | tf_op jit(solution)/shard_map/dot_general | solution.py:218
  70.1 1.3 collective-permute-start.14
  73.5 2.6 %collective-permute-start.3 = (bf16[256,1024]{1,0:T(8,128)(2,1)S(1)}, bf16[256,1024]{1,0:T(8,128)(2,1)S(1)}, u32[]{:S(2)}, u32[]{:S(2)}) collective-permute-start(bf16[256,1024]{1,0:T(8,128)(2,1)S(1)} %fusion.14.refs_0_), channel_id=1, source_target_pairs={{0,128},{1,129},{2,130},{3,131},{4,132},{5,133},{6,134},{7,135},{8... | collective-permute-start | bytes 1572872 | tf_op jit(solution)/shard_map/ppermute | solution.py:33
  76.3 2.7 %collective-permute-done.10.refs_9_ = bf16[64,1792]{1,0:T(8,128)(2,1)} collective-permute-done((bf16[64,1792]{1,0:T(8,128)(2,1)}, bf16[64,1792]{1,0:T(8,128)(2,1)}, u32[]{:S(2)}, u32[]{:S(2)}) %collective-permute-start.10) | collective-permute-done | bytes 229408 | tf_op jit(solution)/shard_map/ppermute | solution.py:33
  79.0 5.0 %collective-permute-done.18.refs_18_ = bf16[64,1792]{1,0:T(8,128)(2,1)} collective-permute-done((bf16[64,1792]{1,0:T(8,128)(2,1)}, bf16[64,1792]{1,0:T(8,128)(2,1)}, u32[]{:S(2)}, u32[]{:S(2)}) %collective-permute-start.18) | collective-permute-done | bytes 229408 | tf_op jit(solution)/shard_map/ppermute | solution.py:33
  85.4 1.5 collective-permute-start.11
  86.9 3.4 %collective-permute-done.15.refs_15_ = bf16[64,1792]{1,0:T(8,128)(2,1)} collective-permute-done((bf16[64,1792]{1,0:T(8,128)(2,1)S(1)}, bf16[64,1792]{1,0:T(8,128)(2,1)}, u32[]{:S(2)}, u32[]{:S(2)}) %collective-permute-start.15) | collective-permute-done | bytes 229408 | tf_op jit(solution)/shard_map/ppermute | solution.py:33
  90.3 1.5 collective-permute-start.16
  91.9 3.6 %collective-permute-done.3.refs_2_ = bf16[256,1024]{1,0:T(8,128)(2,1)S(1)} collective-permute-done((bf16[256,1024]{1,0:T(8,128)(2,1)S(1)}, bf16[256,1024]{1,0:T(8,128)(2,1)S(1)}, u32[]{:S(2)}, u32[]{:S(2)}) %collective-permute-start.3) | collective-permute-done | bytes 524320 | tf_op jit(solution)/shard_map/ppermute | solution.py:33
  95.5 4.1 %collective-permute-done.4.refs_3_ = bf16[256,1024]{1,0:T(8,128)(2,1)S(1)} collective-permute-done((bf16[256,1024]{1,0:T(8,128)(2,1)S(1)}, bf16[256,1024]{1,0:T(8,128)(2,1)S(1)}, u32[]{:S(2)}, u32[]{:S(2)}) %collective-permute-start.4) | collective-permute-done | bytes 524320 | tf_op jit(solution)/shard_map/ppermute | solution.py:33
  99.7 0.9 copy-done.3
  100.6 0.9 copy-done.5
  101.5 0.9 copy-done.7
  102.5 0.9 copy-done.9
  103.4 0.9 copy-done.11
  104.3 0.9 copy-done.13
  105.3 5.2 %project.3 = bf16[4,256,896]{2,1,0:T(8,128)(2,1)S(1)} custom-call(s32[2]{0:T(128)S(1)} %pad_add_fusion.place, bf16[256,1024]{1,0:T(8,128)(2,1)S(1)} %fusion.14.refs_0_, bf16[256,1024]{1,0:T(8,128)(2,1)S(1)} %collective-permute-done.2.refs_1_, bf16[256,1024]{1,0:T(8,128)(2,1)S(1)} %collective-permute-done.3.refs_2_, ...), custom_call_target="tpu_custom_call" | custom-call | flops 1879048192 | bytes 8388608 | tf_op jit(solution)/shard_map/project/pallas_call | solution.py:181
  110.5 3.5 %collective-permute-start.20 = (bf16[4,256,896]{2,1,0:T(8,128)(2,1)S(1)}, bf16[4,256,896]{2,1,0:T(8,128)(2,1)S(1)}, u32[]{:S(2)}, u32[]{:S(2)}) collective-permute-start(bf16[4,256,896]{2,1,0:T(8,128)(2,1)S(1)} %project.3), channel_id=1, source_target_pairs={{0,2},{1,3},{2,0},{3,1},{4,6},{5,7},{6,4},{7,5},{8,10},{9,11},{10,... | collective-permute-start | bytes 5505032 | tf_op jit(solution)/shard_map/ppermute | solution.py:33
  113.9 5.5 %project.2 = f32[4,256,896]{2,1,0:T(8,128)S(1)} custom-call(s32[2]{0:T(128)S(1)} %pad_add_fusion.place, bf16[256,1024]{1,0:T(8,128)(2,1)S(1)} %fusion.14.refs_0_, bf16[256,1024]{1,0:T(8,128)(2,1)S(1)} %collective-permute-done.2.refs_1_, bf16[256,1024]{1,0:T(8,128)(2,1)S(1)} %collective-permute-done.3.refs_2_, ...), custom_call_target="tpu_custom_call" | custom-call | flops 1879048192 | bytes 8388608 | tf_op jit(solution)/shard_map/project/pallas_call | solution.py:181
  120.1 2.8 %collective-permute-start.21 = (bf16[256,896]{1,0:T(8,128)(2,1)S(1)}, bf16[256,896]{1,0:T(8,128)(2,1)S(1)}, u32[]{:S(2)}, u32[]{:S(2)}) collective-permute-start(bf16[256,896]{1,0:T(8,128)(2,1)S(1)} %get-tuple-element.11), channel_id=1, source_target_pairs={{0,8},{1,9},{2,10},{3,11},{4,12},{5,13},{6,14},{7,15},{8,0},{9,1},... | collective-permute-start | bytes 1376264 | tf_op jit(solution)/shard_map/ppermute | solution.py:33
  123.2 2.3 %collective-permute-start.23 = (bf16[256,896]{1,0:T(8,128)(2,1)S(1)}, bf16[256,896]{1,0:T(8,128)(2,1)S(1)}, u32[]{:S(2)}, u32[]{:S(2)}) collective-permute-start(bf16[256,896]{1,0:T(8,128)(2,1)S(1)} %get-tuple-element.12), channel_id=1, source_target_pairs={{0,12},{1,13},{2,14},{3,15},{4,0},{5,1},{6,2},{7,3},{8,4},{9,5},{1... | collective-permute-start | bytes 1376264 | tf_op jit(solution)/shard_map/ppermute | solution.py:33
  125.6 8.2 %collective-permute-done.21 = bf16[256,896]{1,0:T(8,128)(2,1)S(1)} collective-permute-done((bf16[256,896]{1,0:T(8,128)(2,1)S(1)}, bf16[256,896]{1,0:T(8,128)(2,1)S(1)}, u32[]{:S(2)}, u32[]{:S(2)}) %collective-permute-start.21) | collective-permute-done | bytes 458784 | tf_op jit(solution)/shard_map/ppermute | solution.py:33
  133.8 10.1 %collective-permute-done.22 = bf16[256,896]{1,0:T(8,128)(2,1)S(1)} collective-permute-done((bf16[256,896]{1,0:T(8,128)(2,1)S(1)}, bf16[256,896]{1,0:T(8,128)(2,1)S(1)}, u32[]{:S(2)}, u32[]{:S(2)}) %collective-permute-start.22) | collective-permute-done | bytes 458784 | tf_op jit(solution)/shard_map/ppermute | solution.py:33
  144.3 3.6 %collective-permute-start.24 = (bf16[256,448]{1,0:T(8,128)(2,1)S(1)}, bf16[256,448]{1,0:T(8,128)(2,1)S(1)}, u32[]{:S(2)}, u32[]{:S(2)}) collective-permute-start(bf16[256,448]{1,0:T(8,128)(2,1)S(1)} %get-tuple-element.20), channel_id=1, source_target_pairs={{0,0},{1,1},{2,128},{3,129},{4,4},{5,5},{6,132},{7,133},{8,8},{9,9... | collective-permute-start | bytes 688136 | tf_op jit(solution)/shard_map/ppermute | solution.py:33
  148.0 5.4 %collective-permute-done.24 = bf16[256,448]{1,0:T(8,128)(2,1)S(1)} collective-permute-done((bf16[256,448]{1,0:T(8,128)(2,1)S(1)}, bf16[256,448]{1,0:T(8,128)(2,1)S(1)}, u32[]{:S(2)}, u32[]{:S(2)}) %collective-permute-start.24) | collective-permute-done | bytes 229408 | tf_op jit(solution)/shard_map/ppermute | solution.py:33
  153.4 2.3 %collective-permute-done.25 = bf16[256,448]{1,0:T(8,128)(2,1)S(1)} collective-permute-done((bf16[256,448]{1,0:T(8,128)(2,1)S(1)}, bf16[256,448]{1,0:T(8,128)(2,1)S(1)}, u32[]{:S(2)}, u32[]{:S(2)}) %collective-permute-start.25) | collective-permute-done | bytes 229408 | tf_op jit(solution)/shard_map/ppermute | solution.py:33
  155.8 0.9 pad_maximum_fusion
  (83 shorter events, 11.0 us)
Async XLA Ops:
  0.0 45.6 %copy-start = (bf16[8,128,512]{2,1,0:T(8,128)(2,1)S(1)}, bf16[8,128,512]{2,1,0:T(8,128)(2,1)}, u32[]{:S(2)}) copy-start(bf16[8,128,512]{2,1,0:T(8,128)(2,1)} %param.13) | copy-start | bytes 3145732
  3.3 36.4 %collective-permute-start = (bf16[256,576]{1,0:T(8,128)(2,1)}, bf16[256,576]{1,0:T(8,128)(2,1)}, u32[]{:S(2)}, u32[]{:S(2)}) collective-permute-start(bf16[256,576]{1,0:T(8,128)(2,1)} %pad_maximum_fusion.1), channel_id=1, source_target_pairs={{0,32},{16,48},{32,64},{48,80},{64,96},{80,112},{96,128},{112,144}... | collective-permute-start | bytes 884744 | tf_op jit(solution)/shard_map/ppermute | solution.py:62
  9.7 33.8 %collective-permute-start.1 = (bf16[256,576]{1,0:T(8,128)(2,1)}, bf16[256,576]{1,0:T(8,128)(2,1)}, u32[]{:S(2)}, u32[]{:S(2)}) collective-permute-start(bf16[256,576]{1,0:T(8,128)(2,1)} %pad_maximum_fusion.1), channel_id=1, source_target_pairs={{0,16},{16,32},{32,48},{48,64},{64,80},{80,96},{96,112},{112,128},... | collective-permute-start | bytes 884744 | tf_op jit(solution)/shard_map/ppermute | solution.py:62
  16.9 22.6 %collective-permute-start.8 = (bf16[64,1792]{1,0:T(8,128)(2,1)}, bf16[64,1792]{1,0:T(8,128)(2,1)S(1)}, u32[]{:S(2)}, u32[]{:S(2)}) collective-permute-start(bf16[64,1792]{1,0:T(8,128)(2,1)} %get-tuple-element.7.refs_4_), channel_id=1, source_target_pairs={{0,16},{1,17},{2,18},{3,19},{4,20},{5,21},{6,22},{7,23},{8,24},{9,... | collective-permute-start | bytes 688136 | tf_op jit(solution)/shard_map/ppermute | solution.py:33
  18.3 21.2 %collective-permute-start.5 = (bf16[64,1792]{1,0:T(8,128)(2,1)}, bf16[64,1792]{1,0:T(8,128)(2,1)S(1)}, u32[]{:S(2)}, u32[]{:S(2)}) collective-permute-start(bf16[64,1792]{1,0:T(8,128)(2,1)} %get-tuple-element.7.refs_4_), channel_id=1, source_target_pairs={{0,112},{1,113},{2,114},{3,115},{4,116},{5,117},{6,118},{7,119},{8... | collective-permute-start | bytes 688136 | tf_op jit(solution)/shard_map/ppermute | solution.py:33
  19.6 13.2 %collective-permute-start.12 = (bf16[64,1792]{1,0:T(8,128)(2,1)}, bf16[64,1792]{1,0:T(8,128)(2,1)S(1)}, u32[]{:S(2)}, u32[]{:S(2)}) collective-permute-start(bf16[64,1792]{1,0:T(8,128)(2,1)} %get-tuple-element.8), channel_id=1, source_target_pairs={{0,129},{1,128},{2,131},{3,130},{4,133},{5,132},{6,135},{7,134},{8... | collective-permute-start | bytes 688136 | tf_op jit(solution)/shard_map/ppermute | solution.py:33
  27.3 12.3 %copy-start.15 = (bf16[256,1536]{0,1:T(8,128)(2,1)}, bf16[256,1536]{0,1:T(8,128)(2,1)S(1)}, u32[]{:S(2)}) copy-start(bf16[256,1536]{0,1:T(8,128)(2,1)S(1)} %copy.32) | copy-start | bytes 2359300
  32.7 19.3 %copy-start.6 = (bf16[64,1792]{1,0:T(8,128)(2,1)}, bf16[64,1792]{1,0:T(8,128)(2,1)S(1)}, u32[]{:S(2)}) copy-start(bf16[64,1792]{1,0:T(8,128)(2,1)S(1)} %collective-permute-done.12.refs_12_) | copy-start | bytes 688132
  32.8 37.4 %collective-permute-start.13 = (bf16[64,1792]{1,0:T(8,128)(2,1)S(1)}, bf16[64,1792]{1,0:T(8,128)(2,1)S(1)}, u32[]{:S(2)}, u32[]{:S(2)}) collective-permute-start(bf16[64,1792]{1,0:T(8,128)(2,1)S(1)} %collective-permute-done.12.refs_12_), channel_id=1, source_target_pairs={{0,112},{1,113},{2,114},{3,115},{4,116},{5,117},{6,118},{7,119},{8... | collective-permute-start | bytes 688136 | tf_op jit(solution)/shard_map/ppermute | solution.py:33
  39.5 12.5 %copy-start.2 = (bf16[64,1792]{1,0:T(8,128)(2,1)}, bf16[64,1792]{1,0:T(8,128)(2,1)S(1)}, u32[]{:S(2)}) copy-start(bf16[64,1792]{1,0:T(8,128)(2,1)S(1)} %collective-permute-done.8.refs_11_) | copy-start | bytes 688132
  39.5 33.4 %collective-permute-start.17 = (bf16[64,1792]{1,0:T(8,128)(2,1)S(1)}, bf16[64,1792]{1,0:T(8,128)(2,1)}, u32[]{:S(2)}, u32[]{:S(2)}) collective-permute-start(bf16[64,1792]{1,0:T(8,128)(2,1)S(1)} %collective-permute-done.12.refs_12_), channel_id=1, source_target_pairs={{0,16},{1,17},{2,18},{3,19},{4,20},{5,21},{6,22},{7,23},{8,24},{9,... | collective-permute-start | bytes 688136 | tf_op jit(solution)/shard_map/ppermute | solution.py:33
  39.5 12.5 %copy-start.4 = (bf16[64,1792]{1,0:T(8,128)(2,1)}, bf16[64,1792]{1,0:T(8,128)(2,1)S(1)}, u32[]{:S(2)}) copy-start(bf16[64,1792]{1,0:T(8,128)(2,1)S(1)} %collective-permute-done.5.refs_5_) | copy-start | bytes 688132
  39.6 33.1 %collective-permute-start.9 = (bf16[64,1792]{1,0:T(8,128)(2,1)S(1)}, bf16[64,1792]{1,0:T(8,128)(2,1)}, u32[]{:S(2)}, u32[]{:S(2)}) collective-permute-start(bf16[64,1792]{1,0:T(8,128)(2,1)S(1)} %collective-permute-done.8.refs_11_), channel_id=1, source_target_pairs={{0,16},{1,17},{2,18},{3,19},{4,20},{5,21},{6,22},{7,23},{8,24},{9,... | collective-permute-start | bytes 688136 | tf_op jit(solution)/shard_map/ppermute | solution.py:33
  39.7 33.9 %collective-permute-start.6 = (bf16[64,1792]{1,0:T(8,128)(2,1)S(1)}, bf16[64,1792]{1,0:T(8,128)(2,1)}, u32[]{:S(2)}, u32[]{:S(2)}) collective-permute-start(bf16[64,1792]{1,0:T(8,128)(2,1)S(1)} %collective-permute-done.5.refs_5_), channel_id=1, source_target_pairs={{0,112},{1,113},{2,114},{3,115},{4,116},{5,117},{6,118},{7,119},{8... | collective-permute-start | bytes 688136 | tf_op jit(solution)/shard_map/ppermute | solution.py:33
  45.6 6.4 %copy-start.17 = (pred[256,768]{0,1:T(8,128)(4,1)S(1)}, pred[256,768]{0,1:T(8,128)(4,1)}, u32[]{:S(2)}) copy-start(pred[256,768]{0,1:T(8,128)(4,1)} %fusion.22) | copy-start | bytes 589828
  45.6 6.4 %copy-start.18 = (bf16[256,8,32]{0,2,1:T(8,128)(2,1)S(1)}, bf16[256,8,32]{0,2,1:T(8,128)(2,1)}, u32[]{:S(2)}) copy-start(bf16[256,8,32]{0,2,1:T(8,128)(2,1)} %get-tuple-element.14) | copy-start | bytes 393220
  45.6 6.4 %copy-start.19 = (bf16[256,8,32]{0,2,1:T(8,128)(2,1)S(1)}, bf16[256,8,32]{0,2,1:T(8,128)(2,1)}, u32[]{:S(2)}) copy-start(bf16[256,8,32]{0,2,1:T(8,128)(2,1)} %get-tuple-element.15) | copy-start | bytes 393220
  56.1 2.7 %copy-start.14 = (f32[8,256,768]{1,2,0:T(8,128)}, f32[8,256,768]{1,2,0:T(8,128)S(1)}, u32[]{:S(2)}) copy-start(f32[8,256,768]{1,2,0:T(8,128)S(1)} %bitcast_select_fusion) | copy-start | bytes 18874372
  58.8 1.2 copy-start.16
  60.0 39.6 %copy-start.1 = (bf16[64,1792]{1,0:T(8,128)(2,1)S(1)}, bf16[64,1792]{1,0:T(8,128)(2,1)}, u32[]{:S(2)}) copy-start(bf16[64,1792]{1,0:T(8,128)(2,1)} %get-tuple-element.7.refs_4_) | copy-start | bytes 688132
  70.1 6.1 %collective-permute-start.14 = (bf16[64,1792]{1,0:T(8,128)(2,1)S(1)}, bf16[64,1792]{1,0:T(8,128)(2,1)S(1)}, u32[]{:S(2)}, u32[]{:S(2)}) collective-permute-start(bf16[64,1792]{1,0:T(8,128)(2,1)S(1)} %collective-permute-done.13.refs_13_), channel_id=1, source_target_pairs={{0,112},{1,113},{2,114},{3,115},{4,116},{5,117},{6,118},{7,119},{8... | collective-permute-start | bytes 688136 | tf_op jit(solution)/shard_map/ppermute | solution.py:33
  71.4 0.7 copy-start.8
  72.1 14.7 %collective-permute-start.2 = (bf16[256,1024]{1,0:T(8,128)(2,1)S(1)}, bf16[256,1024]{1,0:T(8,128)(2,1)S(1)}, u32[]{:S(2)}, u32[]{:S(2)}) collective-permute-start(bf16[256,1024]{1,0:T(8,128)(2,1)S(1)} %fusion.14.refs_0_), channel_id=1, source_target_pairs={{0,1},{1,0},{2,3},{3,2},{4,5},{5,4},{6,7},{7,6},{8,9},{9,8},{10,11... | collective-permute-start | bytes 1572872 | tf_op jit(solution)/shard_map/ppermute | solution.py:33
  72.6 6.4 %collective-permute-start.10 = (bf16[64,1792]{1,0:T(8,128)(2,1)}, bf16[64,1792]{1,0:T(8,128)(2,1)}, u32[]{:S(2)}, u32[]{:S(2)}) collective-permute-start(bf16[64,1792]{1,0:T(8,128)(2,1)} %collective-permute-done.9.refs_10_), channel_id=1, source_target_pairs={{0,16},{1,17},{2,18},{3,19},{4,20},{5,21},{6,22},{7,23},{8,24},{9,... | collective-permute-start | bytes 688136 | tf_op jit(solution)/shard_map/ppermute | solution.py:33
  73.0 11.0 %collective-permute-start.18 = (bf16[64,1792]{1,0:T(8,128)(2,1)}, bf16[64,1792]{1,0:T(8,128)(2,1)}, u32[]{:S(2)}, u32[]{:S(2)}) collective-permute-start(bf16[64,1792]{1,0:T(8,128)(2,1)} %collective-permute-done.17.refs_19_), channel_id=1, source_target_pairs={{0,16},{1,17},{2,18},{3,19},{4,20},{5,21},{6,22},{7,23},{8,24},{9,... | collective-permute-start | bytes 688136 | tf_op jit(solution)/shard_map/ppermute | solution.py:33
  73.5 22.0 %collective-permute-start.3 = (bf16[256,1024]{1,0:T(8,128)(2,1)S(1)}, bf16[256,1024]{1,0:T(8,128)(2,1)S(1)}, u32[]{:S(2)}, u32[]{:S(2)}) collective-permute-start(bf16[256,1024]{1,0:T(8,128)(2,1)S(1)} %fusion.14.refs_0_), channel_id=1, source_target_pairs={{0,128},{1,129},{2,130},{3,131},{4,132},{5,133},{6,134},{7,135},{8... | collective-permute-start | bytes 1572872 | tf_op jit(solution)/shard_map/ppermute | solution.py:33
  76.2 23.4 %collective-permute-start.4 = (bf16[256,1024]{1,0:T(8,128)(2,1)S(1)}, bf16[256,1024]{1,0:T(8,128)(2,1)S(1)}, u32[]{:S(2)}, u32[]{:S(2)}) collective-permute-start(bf16[256,1024]{1,0:T(8,128)(2,1)S(1)} %fusion.14.refs_0_), channel_id=1, source_target_pairs={{0,129},{1,128},{2,131},{3,130},{4,133},{5,132},{6,135},{7,134},{8... | collective-permute-start | bytes 1572872 | tf_op jit(solution)/shard_map/ppermute | solution.py:33
  79.0 5.7 %collective-permute-start.7 = (bf16[64,1792]{1,0:T(8,128)(2,1)}, bf16[64,1792]{1,0:T(8,128)(2,1)S(1)}, u32[]{:S(2)}, u32[]{:S(2)}) collective-permute-start(bf16[64,1792]{1,0:T(8,128)(2,1)} %collective-permute-done.6.refs_6_), channel_id=1, source_target_pairs={{0,112},{1,113},{2,114},{3,115},{4,116},{5,117},{6,118},{7,119},{8... | collective-permute-start | bytes 688136 | tf_op jit(solution)/shard_map/ppermute | solution.py:33
  84.0 6.3 %collective-permute-start.15 = (bf16[64,1792]{1,0:T(8,128)(2,1)S(1)}, bf16[64,1792]{1,0:T(8,128)(2,1)}, u32[]{:S(2)}, u32[]{:S(2)}) collective-permute-start(bf16[64,1792]{1,0:T(8,128)(2,1)S(1)} %collective-permute-done.14.refs_14_), channel_id=1, source_target_pairs={{0,112},{1,113},{2,114},{3,115},{4,116},{5,117},{6,118},{7,119},{8... | collective-permute-start | bytes 688136 | tf_op jit(solution)/shard_map/ppermute | solution.py:33
  84.0 0.7 copy-start.10
  84.7 0.7 copy-start.12
  85.4 14.2 %collective-permute-start.11 = (bf16[64,1792]{1,0:T(8,128)(2,1)}, bf16[64,1792]{1,0:T(8,128)(2,1)}, u32[]{:S(2)}, u32[]{:S(2)}) collective-permute-start(bf16[64,1792]{1,0:T(8,128)(2,1)} %collective-permute-done.10.refs_9_), channel_id=1, source_target_pairs={{0,16},{1,17},{2,18},{3,19},{4,20},{5,21},{6,22},{7,23},{8,24},{9,... | collective-permute-start | bytes 688136 | tf_op jit(solution)/shard_map/ppermute | solution.py:33
  86.9 12.8 %collective-permute-start.19 = (bf16[64,1792]{1,0:T(8,128)(2,1)}, bf16[64,1792]{1,0:T(8,128)(2,1)}, u32[]{:S(2)}, u32[]{:S(2)}) collective-permute-start(bf16[64,1792]{1,0:T(8,128)(2,1)} %collective-permute-done.18.refs_18_), channel_id=1, source_target_pairs={{0,16},{1,17},{2,18},{3,19},{4,20},{5,21},{6,22},{7,23},{8,24},{9,... | collective-permute-start | bytes 688136 | tf_op jit(solution)/shard_map/ppermute | solution.py:33
  90.3 9.4 %collective-permute-start.16 = (bf16[64,1792]{1,0:T(8,128)(2,1)}, bf16[64,1792]{1,0:T(8,128)(2,1)}, u32[]{:S(2)}, u32[]{:S(2)}) collective-permute-start(bf16[64,1792]{1,0:T(8,128)(2,1)} %collective-permute-done.15.refs_15_), channel_id=1, source_target_pairs={{0,112},{1,113},{2,114},{3,115},{4,116},{5,117},{6,118},{7,119},{8... | collective-permute-start | bytes 688136 | tf_op jit(solution)/shard_map/ppermute | solution.py:33
  99.6 0.9 copy-start.3
  100.6 0.9 copy-start.5
  101.5 0.9 copy-start.7
  102.5 0.9 copy-start.9
  103.4 0.9 copy-start.11
  104.3 0.9 copy-start.13
  110.5 9.0 %collective-permute-start.20 = (bf16[4,256,896]{2,1,0:T(8,128)(2,1)S(1)}, bf16[4,256,896]{2,1,0:T(8,128)(2,1)S(1)}, u32[]{:S(2)}, u32[]{:S(2)}) collective-permute-start(bf16[4,256,896]{2,1,0:T(8,128)(2,1)S(1)} %project.3), channel_id=1, source_target_pairs={{0,2},{1,3},{2,0},{3,1},{4,6},{5,7},{6,4},{7,5},{8,10},{9,11},{10,... | collective-permute-start | bytes 5505032 | tf_op jit(solution)/shard_map/ppermute | solution.py:33
  120.1 13.8 %collective-permute-start.21 = (bf16[256,896]{1,0:T(8,128)(2,1)S(1)}, bf16[256,896]{1,0:T(8,128)(2,1)S(1)}, u32[]{:S(2)}, u32[]{:S(2)}) collective-permute-start(bf16[256,896]{1,0:T(8,128)(2,1)S(1)} %get-tuple-element.11), channel_id=1, source_target_pairs={{0,8},{1,9},{2,10},{3,11},{4,12},{5,13},{6,14},{7,15},{8,0},{9,1},... | collective-permute-start | bytes 1376264 | tf_op jit(solution)/shard_map/ppermute | solution.py:33
  122.9 21.1 %collective-permute-start.22 = (bf16[256,896]{1,0:T(8,128)(2,1)S(1)}, bf16[256,896]{1,0:T(8,128)(2,1)S(1)}, u32[]{:S(2)}, u32[]{:S(2)}) collective-permute-start(bf16[256,896]{1,0:T(8,128)(2,1)S(1)} %get-tuple-element.13), channel_id=1, source_target_pairs={{0,4},{1,5},{2,6},{3,7},{4,8},{5,9},{6,10},{7,11},{8,12},{9,13},{1... | collective-permute-start | bytes 1376264 | tf_op jit(solution)/shard_map/ppermute | solution.py:33
  123.2 20.7 %collective-permute-start.23 = (bf16[256,896]{1,0:T(8,128)(2,1)S(1)}, bf16[256,896]{1,0:T(8,128)(2,1)S(1)}, u32[]{:S(2)}, u32[]{:S(2)}) collective-permute-start(bf16[256,896]{1,0:T(8,128)(2,1)S(1)} %get-tuple-element.12), channel_id=1, source_target_pairs={{0,12},{1,13},{2,14},{3,15},{4,0},{5,1},{6,2},{7,3},{8,4},{9,5},{1... | collective-permute-start | bytes 1376264 | tf_op jit(solution)/shard_map/ppermute | solution.py:33
  144.3 9.1 %collective-permute-start.24 = (bf16[256,448]{1,0:T(8,128)(2,1)S(1)}, bf16[256,448]{1,0:T(8,128)(2,1)S(1)}, u32[]{:S(2)}, u32[]{:S(2)}) collective-permute-start(bf16[256,448]{1,0:T(8,128)(2,1)S(1)} %get-tuple-element.20), channel_id=1, source_target_pairs={{0,0},{1,1},{2,128},{3,129},{4,4},{5,5},{6,132},{7,133},{8,8},{9,9... | collective-permute-start | bytes 688136 | tf_op jit(solution)/shard_map/ppermute | solution.py:33
  147.9 7.8 %collective-permute-start.25 = (bf16[256,448]{1,0:T(8,128)(2,1)S(1)}, bf16[256,448]{1,0:T(8,128)(2,1)S(1)}, u32[]{:S(2)}, u32[]{:S(2)}) collective-permute-start(bf16[256,448]{1,0:T(8,128)(2,1)S(1)} %get-tuple-element.21), channel_id=1, source_target_pairs={{0,1},{1,0},{2,129},{3,128},{4,5},{5,4},{6,133},{7,132},{8,9},{9,8... | collective-permute-start | bytes 688136 | tf_op jit(solution)/shard_map/ppermute | solution.py:33

commit v2 on v1

v2 whole, which is shorter than its diff:
```python
import functools

import jax
import jax.numpy as jnp
from jax import lax
from jax.experimental import pallas as pl
from jax.experimental.pallas import tpu as pltpu
from jax.sharding import Mesh
from jax.sharding import PartitionSpec as P

AXES = ("yh", "z", "x", "c", "yl")
SIZES = (2, 8, 4, 2, 2)
CTX = ("yh", "z")
HEAD = ("x", "c")
BF = jnp.bfloat16
F32 = jnp.float32
VMEM = pltpu.MemorySpace.VMEM


def number_of(yh, z, x, c, yl):
    return (((yh * 8 + z) * 4 + x) * 2 + c) * 2 + yl


def moved(a, target):
    pairs = []
    for yh in range(2):
        for z in range(8):
            for x in range(4):
                for c in range(2):
                    for yl in range(2):
                        t = target(yh, z, x, c, yl)
                        pairs.append((number_of(yh, z, x, c, yl), number_of(*t)))
    return lax.ppermute(a, AXES, pairs)


def up_z(a):
    return moved(a, lambda yh, z, x, c, yl: (yh, (z + 1) % 8, x, c, yl))


def down_z(a):
    return moved(a, lambda yh, z, x, c, yl: (yh, (z - 1) % 8, x, c, yl))


def xor_y(a, q):
    return moved(a, lambda yh, z, x, c, yl: (yh ^ (q >> 1), z, x, c, yl ^ (q & 1)))


def other_core(a):
    return moved(a, lambda yh, z, x, c, yl: (yh, z, x, 1 - c, yl))


def along_x(a, d):
    return moved(a, lambda yh, z, x, c, yl: (yh, z, (x + d) % 4, c, yl))


def home(a, r):
    return moved(a, lambda yh, z, x, c, yl: (yh ^ c, z, x, yh, yl ^ r))


def queries_kernel(rows, w_query, w_key_up, turn, out):
    cosine, sine = turn[:, :64], turn[:, 64:]
    for part in range(2):
        span = slice(768 * part, 768 * part + 768)
        queries = jnp.dot(rows[...], w_query[:, span], preferred_element_type=F32).astype(BF)
        for i in range(4):
            h = 4 * part + i
            plain = queries[:, 192 * i : 192 * i + 128]
            lat = jnp.dot(plain, w_key_up[h], preferred_element_type=F32)
            rot = queries[:, 192 * i + 128 : 192 * i + 192].astype(F32)
            other = jnp.concatenate([rot[:, 32:], rot[:, :32]], 1)
            rot = rot * cosine + other * sine
            tokens = slice(256 * h, 256 * h + 256)
            out[tokens, :512] = lat.astype(BF)
            out[tokens, 512:] = jnp.concatenate([rot, jnp.zeros_like(rot)], 1).astype(BF)


def keys_kernel(place, own, near, far, swapped, cache, turn, keys, hidden):
    c, slab, start = place[0], place[1], place[2]
    mine = pl.ds(pl.multiple_of(128 * c, 128), 128)
    theirs = pl.ds(pl.multiple_of(128 * (1 - c), 128), 128)
    keys[512:, :576] = own[...]
    keys[pl.ds(pl.multiple_of(256 + 128 * c, 128), 128), :576] = near[...]
    keys[pl.ds(pl.multiple_of(384 - 128 * c, 128), 128), :576] = swapped[:128]
    keys[mine, :576] = far[...]
    keys[theirs, :576] = swapped[128:]
    rot = keys[:, 512:576].astype(F32)
    other = jnp.concatenate([rot[:, 32:], rot[:, :32]], 1)
    rot = rot * turn[:, :64] + other * turn[:, 64:]
    keys[:, 512:] = jnp.concatenate([rot, jnp.zeros_like(rot)], 1).astype(BF)

    @pl.when(slab == 0)
    def _():
        keys[:512, :576] = cache[...]

    @pl.when(slab == 1)
    def _():
        keys[:256, :576] = cache[256:]

    row = lax.broadcasted_iota(jnp.int32, (256, 768), 0)
    col = lax.broadcasted_iota(jnp.int32, (256, 768), 1)
    relative = col - 512 - row
    visible = (relative <= 0) & (relative > -512) & (slab * 256 + col - 512 >= -start)
    hidden[...] = jnp.where(visible, 0.0, -1e30)


def attend_kernel(group, queries, keys, hidden, w_value_up, reorder, out):
    scale = 192.0**-0.5 * 1.4426950408889634
    latent = keys[:, :512]
    heads = []
    for pair in range(2):
        scores = lax.dot_general(
            queries[1024 * group + 512 * pair : 1024 * group + 512 * pair + 512, :],
            keys[...],
            (((1,), (1,)), ((), ())),
            preferred_element_type=F32,
        )
        for i in range(2):
            part = scores[256 * i : 256 * i + 256] * scale + hidden[...]
            top = jnp.max(part, axis=1, keepdims=True)
            powers = jnp.exp2(part - top)
            share = 1.0 / jnp.sum(powers, axis=1, keepdims=True)
            mixed = jnp.dot(powers.astype(BF), latent, preferred_element_type=F32) * share
            attention = jnp.dot(
                mixed.astype(BF), w_value_up[4 * group + 2 * pair + i], preferred_element_type=F32
            )
            heads.append(attention.astype(BF))
    rows = jnp.concatenate(heads, 1)
    out[...] = jnp.dot(rows, reorder[...], preferred_element_type=F32).astype(BF)


def turn_of(positions):
    inverse = jnp.power(jnp.float32(10000.0), -jnp.arange(32, dtype=F32) * (2.0 / 64))
    angles = positions.astype(F32)[:, None] * inverse
    cosine, sine = jnp.cos(angles), jnp.sin(angles)
    return jnp.concatenate([cosine, cosine, -sine, sine], 1)


def quarter_kernel(place, rows, own, other):
    for out, flip in ((own, 0), (other, 3)):
        y = place[1] ^ flip
        odd = y % 2
        base = 896 * (y // 2) + 384 * odd
        pieces = []
        for d in range(4):
            start = pl.multiple_of(1792 * ((place[0] + d) % 4) + base, 128)
            wide = rows[:, pl.ds(start, 512)]
            pieces.append(jnp.where(odd == 1, wide[:, 64:], wide[:, :448]))
        out[...] = jnp.concatenate(pieces, 1)


def project_kernel(theirs, place, *refs):
    groups, blocks, (out, rows, weights, total, sem) = refs[:8], refs[8:24], refs[24:]
    copies = []
    for p in range(2):
        for k in range(8):
            for g in range(2):
                at = 512 * g + 256 * p + 32 * k
                copies.append(
                    pltpu.make_async_copy(
                        blocks[8 * p + k].at[pl.ds(32 * g, 32)],
                        weights.at[pl.ds(at, 32)],
                        sem.at[len(copies)],
                    )
                )
    for copy in copies:
        copy.start()
    first = 2 * (place[0] ^ theirs)
    for pick in (0, 2):

        @pl.when(first == pick)
        def _():
            for g in range(2):
                for j in range(2):
                    for p in range(2):
                        half = pl.ds(pl.multiple_of(256 * (place[1] ^ p), 256), 256)
                        rows[256 * j : 256 * j + 256, 512 * g + 256 * p : 512 * g + 256 * p + 256] = (
                            groups[2 * (pick + j) + g][:, half]
                        )

    for copy in copies:
        copy.wait()

    def step(n, carry):
        columns = pl.ds(pl.multiple_of(n * 256, 256), 256)
        total[:, columns] = jnp.dot(rows[...], weights[:, columns], preferred_element_type=F32)
        return carry

    lax.fori_loop(0, 7, step, 0)
    for d in range(4):
        span = slice(448 * d, 448 * d + 448)
        out[d] = jnp.concatenate([total[:256, span], total[256:, span]], 1).astype(out.dtype)


def whole(n):
    return [pl.BlockSpec(memory_space=VMEM)] * n


def scalars(n=1):
    return [pl.BlockSpec(memory_space=pltpu.MemorySpace.SMEM)] * n


def quarters(rows, x, y):
    return pl.pallas_call(
        quarter_kernel,
        out_shape=[jax.ShapeDtypeStruct((64, 1792), BF)] * 2,
        in_specs=scalars() + whole(1),
        out_specs=whole(2),
        name="quarters",
        cost_estimate=pl.CostEstimate(flops=0, bytes_accessed=2 << 20, transcendentals=0),
    )(jnp.stack([x, y]), rows)


def call(kernel, shapes, specs, args, name, flops, moved_bytes, scratch=()):
    many = isinstance(shapes, list)
    return pl.pallas_call(
        kernel,
        out_shape=shapes,
        in_specs=specs,
        out_specs=whole(len(shapes)) if many else whole(1)[0],
        scratch_shapes=list(scratch),
        compiler_params=pltpu.CompilerParams(vmem_limit_bytes=40 << 20),
        name=name,
        cost_estimate=pl.CostEstimate(
            flops=flops, bytes_accessed=moved_bytes, transcendentals=0
        ),
    )(*args)


def array(shape, kind=BF):
    return jax.ShapeDtypeStruct(shape, kind)


def project(theirs, place, groups, blocks, kind):
    return call(
        functools.partial(project_kernel, theirs),
        array((4, 256, 896), kind),
        scalars() + whole(8) + [pl.BlockSpec(memory_space=pl.ANY)] * 16,
        (place, *groups, *blocks),
        "project",
        2 * 512 * 1024 * 1792,
        8 << 20,
        [
            pltpu.VMEM((512, 1024), BF),
            pltpu.VMEM((1024, 1792), BF),
            pltpu.VMEM((512, 1792), F32),
            pltpu.SemaphoreType.DMA((32,)),
        ],
    )


def local(query_latent, key_rows, key_cache, prompt_start, w_query, w_key_up, w_value_up, w_output):
    yh, z, x, c, yl = (lax.axis_index(a) for a in AXES)
    y = 2 * yh + yl
    slab = 8 * yh + z
    own, given = quarters(w_output.reshape(64, 7168), x, y)

    half = lax.dynamic_slice_in_dim(key_rows, 128 * c, 128, 0)
    near, far = (
        lax.ppermute(half, CTX, [(i, i + by) for i in range(16 - by)]) for by in (1, 2)
    )
    swapped = other_core(jnp.concatenate([near, far], 0))

    other = xor_y(given, 3)
    blocks = [[own] + [None] * 7, [other] + [None] * 7]
    for p in range(2):
        up = down = blocks[p][0]
        for s in range(1, 5):
            if s < 4 or p == 0:
                up = up_z(up)
                blocks[p][8 - s] = up
            if s < 4 or p == 1:
                down = down_z(down)
                blocks[p][s] = down

    turn = turn_of(slab * 256 + jnp.arange(768, dtype=jnp.int32) - 512)
    queries = call(
        queries_kernel,
        array((2048, 640)),
        whole(4),
        (query_latent, w_query, w_key_up, turn[512:]),
        "queries",
        2 * 256 * 1536 * 1536 + 2 * 2048 * 128 * 512,
        8 << 20,
    )
    keys, hidden = call(
        keys_kernel,
        [array((768, 640)), array((256, 768), F32)],
        scalars() + whole(6),
        (jnp.stack([c, slab, prompt_start[0]]), key_rows, near, far, swapped, key_cache, turn),
        "keys",
        768 * 640 * 8,
        4 << 20,
    )
    column = jnp.arange(512, dtype=jnp.int32)
    source = (
        (column // 8 % 4) * 128 + (column // 256) * 64 + ((z + column // 32) % 8) * 8 + column % 8
    )
    reorder = (column[:, None] == source[None, :]).astype(BF)
    groups = [[None] * 2 for _ in range(4)]
    for g in range(2):
        rows = call(
            functools.partial(attend_kernel, g),
            array((256, 512)),
            whole(5),
            (queries, keys, hidden, w_value_up, reorder),
            "attend",
            2 * 1024 * 768 * 1152 + 2 * 1024 * 512 * 128,
            5 << 20,
        )
        groups[0][g] = rows
        for q in (2, 1, 3):
            groups[q][g] = xor_y(rows, q)
    place = jnp.stack([c, yh])
    rows = [part for slot in groups for part in slot]
    flat = blocks[0] + blocks[1]
    theirs = other_core(project(1, place, rows, flat, BF))
    mine = project(0, place, rows, flat, F32)
    sums = mine + theirs.astype(F32)
    result = sums[0]
    for d in (2, 1, 3):
        result = result + along_x(sums[d].astype(BF), d).astype(F32)
    result = result.astype(BF)
    pieces = [home(result[:, 448 * r : 448 * r + 448], r) for r in range(2)]
    even = yl == 0
    return jnp.concatenate(
        [jnp.where(even, pieces[0], pieces[1]), jnp.where(even, pieces[1], pieces[0])], 1
    )


def solution(mesh):
    cut = Mesh(mesh.devices.reshape(SIZES), AXES) if hasattr(mesh, "devices") else mesh
    tokens = ("yl", "yh", "z")
    return jax.shard_map(
        local,
        mesh=cut,
        in_specs=(
            P(tokens, None),
            P(tokens, None),
            P("yl", None),
            P("yl"),
            P(None, HEAD),
            P(HEAD, None, None),
            P(HEAD, None, None),
            P(HEAD, CTX, None),
        ),
        out_specs=P(tokens, HEAD),
        check_vma=False,
    )
```

time: 157 us -> 146 us (0.930)
  matrix products: 25.4 us -> 0 us
  Pallas kernels: 12.9 us -> 30.3 us
  starting transfers between devices: 39 us -> 55.2 us
  waiting for transfers between devices: 51.8 us -> 40.7 us
  local copies, waits for them, and re-layouts: 16.3 us -> 12 us
  other arithmetic: 10.3 us -> 6.07 us
    dot_general x5 -> x0, matrix products: 25.4 us -> none  [the longest x1 8.19 us: attention_of(): jnp.einsum('thl,hlv->thv', mixed_lat, w_value_up, preferred_element_type=...]
    ppermute x24 -> x28, starting transfers between devices: 28.3 us -> 45.9 us  [moved(): return lax.ppermute(a, AXES, pairs)]
    pallas_call x2 -> x6, Pallas kernels: 10.6 us -> 28.1 us  [call(): pl.pallas_call(kernel, out_shape=shapes, in_specs=specs, out_specs=whole(...]
    ppermute x24 -> x28, waiting for transfers between devices: 51.7 us -> 40.7 us  [moved(): return lax.ppermute(a, AXES, pairs)]
    select_n x2 -> x0, other arithmetic: 2.04 us -> none  [attention_of(): jnp.where(slab_index < distance, cached, received[distance - 1])]
    unnamed x43 -> x32, local copies, waits for them, and re-layouts: 12.4 us -> 11.7 us
  transfers between devices with their start and end apart: 26 -> 30, of which waited for: 11 -> 10; matrix products, arithmetic and copies ran while one was open for 23% -> 4% of each run, Pallas kernels for 5% -> 15%
where the time goes in v2:
time: 146 us; the launch traced here: 145 us
  starting transfers between devices  55.2 us (38%)
  waiting for transfers between devices  40.7 us (28%)
  Pallas kernels  30.3 us (21%)
  local copies, waits for them, and re-layouts  12 us (8%)
  other arithmetic  6.07 us (4%)
    ppermute x28, starting transfers between devices, moved(): return lax.ppermute(a, AXES, pairs)  45.9 us
    ppermute x28, waiting for transfers between devices, moved(): return lax.ppermute(a, AXES, pairs)  40.7 us
    pallas_call x6, Pallas kernels, call(): pl.pallas_call(kernel, out_shape=shapes, in_specs=specs, out_specs=whole(...  28.1 us
    unnamed x32, local copies, waits for them, and re-layouts  11.7 us
    ppermute x2, starting transfers between devices, local(): lax.ppermute(half, CTX, [(i, i + by) for i in range(16 - by)])  9.29 us
  transfers between devices with their start and end apart: 30, of which 10 were waited for; matrix products, arithmetic and copies ran while one was open for 4% of the time, Pallas kernels for 15%

profile of v2, /device:TPU:1, one launch (start us, length us, event | category | flops | bytes accessed | tf_op | source)
XLA Modules:
  0.0 145.2 jit_solution(8053122774774216284)
XLA Ops:
  0.0 1.2 copy.14.own
  1.2 5.7 %collective-permute-start.1 = (bf16[128,576]{1,0:T(8,128)(2,1)S(1)}, bf16[128,576]{1,0:T(8,128)(2,1)S(1)}, u32[]{:S(2)}, u32[]{:S(2)}) collective-permute-start(bf16[128,576]{1,0:T(8,128)(2,1)S(1)} %constant_dynamic-slice_fusion), channel_id=1, source_target_pairs={{0,32},{16,48},{32,64},{48,80},{64,96},{80,112},{96,128},{112,144}... | collective-permute-start | bytes 442376 | tf_op jit(solution)/shard_map/ppermute | solution.py:259
  6.9 3.6 %collective-permute-start = (bf16[128,576]{1,0:T(8,128)(2,1)S(1)}, bf16[128,576]{1,0:T(8,128)(2,1)S(1)}, u32[]{:S(2)}, u32[]{:S(2)}) collective-permute-start(bf16[128,576]{1,0:T(8,128)(2,1)S(1)} %constant_dynamic-slice_fusion), channel_id=1, source_target_pairs={{0,16},{16,32},{32,48},{48,64},{64,80},{80,96},{96,112},{112,128},... | collective-permute-start | bytes 442376 | tf_op jit(solution)/shard_map/ppermute | solution.py:259
  11.2 2.2 %quarters.1 = (bf16[64,1792]{1,0:T(8,128)(2,1)}, bf16[64,1792]{1,0:T(8,128)(2,1)}) custom-call(s32[2]{0:T(128)} %pad_add_fusion.2.place, bf16[64,7168]{1,0:T(8,128)(2,1)} %bitcast.22), custom_call_target="tpu_custom_call" | custom-call | bytes 2097152 | tf_op jit(solution)/shard_map/quarters/pallas_call | solution.py:203
  13.4 2.8 %collective-permute-start.12 = (bf16[64,1792]{1,0:T(8,128)(2,1)}, bf16[64,1792]{1,0:T(8,128)(2,1)S(1)}, u32[]{:S(2)}, u32[]{:S(2)}) collective-permute-start(bf16[64,1792]{1,0:T(8,128)(2,1)} %get-tuple-element.11.refs_8_), channel_id=1, source_target_pairs={{0,16},{1,17},{2,18},{3,19},{4,20},{5,21},{6,22},{7,23},{8,24},{9,... | collective-permute-start | bytes 688136 | tf_op jit(solution)/shard_map/ppermute | solution.py:33
  17.0 1.9 %collective-permute-start.16 = (bf16[64,1792]{1,0:T(8,128)(2,1)}, bf16[64,1792]{1,0:T(8,128)(2,1)}, u32[]{:S(2)}, u32[]{:S(2)}) collective-permute-start(bf16[64,1792]{1,0:T(8,128)(2,1)} %get-tuple-element.12), channel_id=1, source_target_pairs={{0,129},{1,128},{2,131},{3,130},{4,133},{5,132},{6,135},{7,134},{8... | collective-permute-start | bytes 688136 | tf_op jit(solution)/shard_map/ppermute | solution.py:33
  19.0 1.4 multiply_cosine_fusion
  20.5 0.9 fusion.reorder
  21.4 0.8 pad_maximum_fusion.2
  22.3 1.9 %collective-permute-start.2 = (bf16[256,576]{1,0:T(8,128)(2,1)}, bf16[256,576]{1,0:T(8,128)(2,1)}, u32[]{:S(2)}, u32[]{:S(2)}) collective-permute-start(bf16[256,576]{1,0:T(8,128)(2,1)} %pad_maximum_fusion.2), channel_id=1, source_target_pairs={{0,2},{1,3},{2,0},{3,1},{4,6},{5,7},{6,4},{7,5},{8,10},{9,11},{10,... | collective-permute-start | bytes 884744 | tf_op jit(solution)/shard_map/ppermute | solution.py:33
  24.2 2.0 %collective-permute-done.16.refs_16_ = bf16[64,1792]{1,0:T(8,128)(2,1)} collective-permute-done((bf16[64,1792]{1,0:T(8,128)(2,1)}, bf16[64,1792]{1,0:T(8,128)(2,1)}, u32[]{:S(2)}, u32[]{:S(2)}) %collective-permute-start.16) | collective-permute-done | bytes 229408 | tf_op jit(solution)/shard_map/ppermute | solution.py:33
  27.9 2.7 %collective-permute-start.17 = (bf16[64,1792]{1,0:T(8,128)(2,1)}, bf16[64,1792]{1,0:T(8,128)(2,1)}, u32[]{:S(2)}, u32[]{:S(2)}) collective-permute-start(bf16[64,1792]{1,0:T(8,128)(2,1)} %collective-permute-done.16.refs_16_), channel_id=1, source_target_pairs={{0,112},{1,113},{2,114},{3,115},{4,116},{5,117},{6,118},{7,119},{8... | collective-permute-start | bytes 688136 | tf_op jit(solution)/shard_map/ppermute | solution.py:33
  30.6 2.7 %collective-permute-start.10 = (bf16[64,1792]{1,0:T(8,128)(2,1)}, bf16[64,1792]{1,0:T(8,128)(2,1)}, u32[]{:S(2)}, u32[]{:S(2)}) collective-permute-start(bf16[64,1792]{1,0:T(8,128)(2,1)} %collective-permute-done.9.refs_9_), channel_id=1, source_target_pairs={{0,112},{1,113},{2,114},{3,115},{4,116},{5,117},{6,118},{7,119},{8... | collective-permute-start | bytes 688136 | tf_op jit(solution)/shard_map/ppermute | solution.py:33
  33.3 2.3 %copy-done = bf16[1536,1536]{1,0:T(8,128)(2,1)S(1)} copy-done((bf16[1536,1536]{1,0:T(8,128)(2,1)S(1)}, bf16[1536,1536]{1,0:T(8,128)(2,1)}, u32[]{:S(2)}) %copy-start) | copy-done | bytes 4718616
  35.6 2.3 %queries.1 = bf16[2048,640]{1,0:T(8,128)(2,1)S(1)} custom-call(bf16[256,1536]{1,0:T(8,128)(2,1)S(1)} %copy-done.7, bf16[1536,1536]{1,0:T(8,128)(2,1)S(1)} %copy-done, bf16[8,128,512]{2,1,0:T(8,128)(2,1)S(1)} %copy-done.5, f32[256,128]{1,0:T(8,128)S(1)} %slice.31.turn), custom_call_target="tpu_custom_call" | custom-call | flops 1476395008 | bytes 8388608 | tf_op jit(solution)/shard_map/queries/pallas_call | solution.py:215
  38.2 1.4 copy.15.cache
  39.6 1.0 copy-done.2
  40.6 1.0 copy-done.4
  41.5 0.9 copy-done.9
  42.5 0.9 copy-done.11
  43.4 1.5 %keys.1 = (bf16[768,640]{1,0:T(8,128)(2,1)S(1)}, f32[256,768]{1,0:T(8,128)S(1)}) custom-call(s32[3]{0:T(128)S(1)} %pad_add_fusion.1.place, bf16[256,576]{1,0:T(8,128)(2,1)S(1)} %copy-done.4, bf16[128,576]{1,0:T(8,128)(2,1)S(1)} %copy-done.11, bf16[128,576]{1,0:T(8,128)(2,1)S(1)} %copy-done.9, bf16[256,576]{1,0:T(8,128)(2,1)} %collective-permute-done.2.swapped, ...), custom_call_target="tpu_custom_call" | custom-call | flops 3932160 | bytes 4194304 | tf_op jit(solution)/shard_map/keys/pallas_call | solution.py:215
  44.9 2.9 %collective-permute-start.18 = (bf16[64,1792]{1,0:T(8,128)(2,1)}, bf16[64,1792]{1,0:T(8,128)(2,1)S(1)}, u32[]{:S(2)}, u32[]{:S(2)}) collective-permute-start(bf16[64,1792]{1,0:T(8,128)(2,1)} %collective-permute-done.17.refs_17_), channel_id=1, source_target_pairs={{0,112},{1,113},{2,114},{3,115},{4,116},{5,117},{6,118},{7,119},{8... | collective-permute-start | bytes 688136 | tf_op jit(solution)/shard_map/ppermute | solution.py:33
  47.8 2.7 %collective-permute-start.11 = (bf16[64,1792]{1,0:T(8,128)(2,1)}, bf16[64,1792]{1,0:T(8,128)(2,1)S(1)}, u32[]{:S(2)}, u32[]{:S(2)}) collective-permute-start(bf16[64,1792]{1,0:T(8,128)(2,1)} %collective-permute-done.10.refs_10_), channel_id=1, source_target_pairs={{0,112},{1,113},{2,114},{3,115},{4,116},{5,117},{6,118},{7,119},{8... | collective-permute-start | bytes 688136 | tf_op jit(solution)/shard_map/ppermute | solution.py:33
  50.5 1.0 copy-done.12
  51.5 1.2 copy-done.14
  52.7 3.9 %attend.2.refs_0_ = bf16[256,512]{1,0:T(8,128)(2,1)S(1)} custom-call(bf16[2048,640]{1,0:T(8,128)(2,1)S(1)} %queries.1, bf16[768,640]{1,0:T(8,128)(2,1)S(1)} %get-tuple-element.9.keys, f32[256,768]{1,0:T(8,128)S(1)} %get-tuple-element.10.hidden, bf16[8,512,128]{2,1,0:T(8,128)(2,1)S(1)} %copy-done.14, bf16[512,512]{1,0:T(8,128)(2,1)S(1)} %copy-done.12), custom_call_target="tpu_custom_call" | custom-call | flops 1946157056 | bytes 5242880 | tf_op jit(solution)/shard_map/attend/pallas_call | solution.py:215
  56.6 3.5 %collective-permute-start.7 = (bf16[256,512]{1,0:T(8,128)(2,1)S(1)}, bf16[256,512]{1,0:T(8,128)(2,1)S(1)}, u32[]{:S(2)}, u32[]{:S(2)}) collective-permute-start(bf16[256,512]{1,0:T(8,128)(2,1)S(1)} %attend.2.refs_0_), channel_id=1, source_target_pairs={{0,129},{1,128},{2,131},{3,130},{4,133},{5,132},{6,135},{7,134},{8... | collective-permute-start | bytes 786440 | tf_op jit(solution)/shard_map/ppermute | solution.py:33
  60.2 3.9 %attend.3.refs_1_ = bf16[256,512]{1,0:T(8,128)(2,1)S(1)} custom-call(bf16[2048,640]{1,0:T(8,128)(2,1)S(1)} %queries.1, bf16[768,640]{1,0:T(8,128)(2,1)S(1)} %get-tuple-element.9.keys, f32[256,768]{1,0:T(8,128)S(1)} %get-tuple-element.10.hidden, bf16[8,512,128]{2,1,0:T(8,128)(2,1)S(1)} %copy-done.14, bf16[512,512]{1,0:T(8,128)(2,1)S(1)} %copy-done.13), custom_call_target="tpu_custom_call" | custom-call | flops 1946157056 | bytes 5242880 | tf_op jit(solution)/shard_map/attend/pallas_call | solution.py:215
  64.8 2.6 %collective-permute-start.8 = (bf16[256,512]{1,0:T(8,128)(2,1)S(1)}, bf16[256,512]{1,0:T(8,128)(2,1)S(1)}, u32[]{:S(2)}, u32[]{:S(2)}) collective-permute-start(bf16[256,512]{1,0:T(8,128)(2,1)S(1)} %attend.3.refs_1_), channel_id=1, source_target_pairs={{0,129},{1,128},{2,131},{3,130},{4,133},{5,132},{6,135},{7,134},{8... | collective-permute-start | bytes 786440 | tf_op jit(solution)/shard_map/ppermute | solution.py:33
  67.4 3.8 %collective-permute-done.7.refs_6_ = bf16[256,512]{1,0:T(8,128)(2,1)S(1)} collective-permute-done((bf16[256,512]{1,0:T(8,128)(2,1)S(1)}, bf16[256,512]{1,0:T(8,128)(2,1)S(1)}, u32[]{:S(2)}, u32[]{:S(2)}) %collective-permute-start.7) | collective-permute-done | bytes 262176 | tf_op jit(solution)/shard_map/ppermute | solution.py:33
  71.2 1.1 collective-permute-start.6
  72.3 2.9 %collective-permute-start.4 = (bf16[256,512]{1,0:T(8,128)(2,1)S(1)}, bf16[256,512]{1,0:T(8,128)(2,1)S(1)}, u32[]{:S(2)}, u32[]{:S(2)}) collective-permute-start(bf16[256,512]{1,0:T(8,128)(2,1)S(1)} %attend.3.refs_1_), channel_id=1, source_target_pairs={{0,1},{1,0},{2,3},{3,2},{4,5},{5,4},{6,7},{7,6},{8,9},{9,8},{10,11... | collective-permute-start | bytes 786440 | tf_op jit(solution)/shard_map/ppermute | solution.py:33
  75.2 5.8 %collective-permute-done.8.refs_7_ = bf16[256,512]{1,0:T(8,128)(2,1)S(1)} collective-permute-done((bf16[256,512]{1,0:T(8,128)(2,1)S(1)}, bf16[256,512]{1,0:T(8,128)(2,1)S(1)}, u32[]{:S(2)}, u32[]{:S(2)}) %collective-permute-start.8) | collective-permute-done | bytes 262176 | tf_op jit(solution)/shard_map/ppermute | solution.py:33
  81.0 2.7 %collective-permute-start.20 = (bf16[64,1792]{1,0:T(8,128)(2,1)S(1)}, bf16[64,1792]{1,0:T(8,128)(2,1)S(1)}, u32[]{:S(2)}, u32[]{:S(2)}) collective-permute-start(bf16[64,1792]{1,0:T(8,128)(2,1)S(1)} %collective-permute-done.19.refs_19_), channel_id=1, source_target_pairs={{0,112},{1,113},{2,114},{3,115},{4,116},{5,117},{6,118},{7,119},{8... | collective-permute-start | bytes 688136 | tf_op jit(solution)/shard_map/ppermute | solution.py:33
  83.8 1.7 %collective-permute-done.4.refs_3_ = bf16[256,512]{1,0:T(8,128)(2,1)S(1)} collective-permute-done((bf16[256,512]{1,0:T(8,128)(2,1)S(1)}, bf16[256,512]{1,0:T(8,128)(2,1)S(1)}, u32[]{:S(2)}, u32[]{:S(2)}) %collective-permute-start.4) | collective-permute-done | bytes 262176 | tf_op jit(solution)/shard_map/ppermute | solution.py:33
  85.4 1.7 %collective-permute-done.15.refs_12_ = bf16[64,1792]{1,0:T(8,128)(2,1)S(1)} collective-permute-done((bf16[64,1792]{1,0:T(8,128)(2,1)S(1)}, bf16[64,1792]{1,0:T(8,128)(2,1)S(1)}, u32[]{:S(2)}, u32[]{:S(2)}) %collective-permute-start.15) | collective-permute-done | bytes 229408 | tf_op jit(solution)/shard_map/ppermute | solution.py:33
  87.1 8.1 %project.3 = bf16[4,256,896]{2,1,0:T(8,128)(2,1)S(1)} custom-call(s32[2]{0:T(128)S(1)} %pad_add_fusion.place, bf16[256,512]{1,0:T(8,128)(2,1)S(1)} %attend.2.refs_0_, bf16[256,512]{1,0:T(8,128)(2,1)S(1)} %attend.3.refs_1_, bf16[256,512]{1,0:T(8,128)(2,1)S(1)} %collective-permute-done.3.refs_2_, bf16[256,512]{1,0:T(8,128)(2,1)S(1)} %collective-permute-done.4.refs_3_, ...), custom_call_target="tpu_custom_call" | custom-call | flops 1879048192 | bytes 8388608 | tf_op jit(solution)/shard_map/project/pallas_call | solution.py:215
  95.2 3.4 %collective-permute-start.24 = (bf16[4,256,896]{2,1,0:T(8,128)(2,1)S(1)}, bf16[4,256,896]{2,1,0:T(8,128)(2,1)S(1)}, u32[]{:S(2)}, u32[]{:S(2)}) collective-permute-start(bf16[4,256,896]{2,1,0:T(8,128)(2,1)S(1)} %project.3), channel_id=1, source_target_pairs={{0,2},{1,3},{2,0},{3,1},{4,6},{5,7},{6,4},{7,5},{8,10},{9,11},{10,... | collective-permute-start | bytes 5505032 | tf_op jit(solution)/shard_map/ppermute | solution.py:33
  98.6 8.4 %project.2 = f32[4,256,896]{2,1,0:T(8,128)S(1)} custom-call(s32[2]{0:T(128)S(1)} %pad_add_fusion.place, bf16[256,512]{1,0:T(8,128)(2,1)S(1)} %attend.2.refs_0_, bf16[256,512]{1,0:T(8,128)(2,1)S(1)} %attend.3.refs_1_, bf16[256,512]{1,0:T(8,128)(2,1)S(1)} %collective-permute-done.3.refs_2_, bf16[256,512]{1,0:T(8,128)(2,1)S(1)} %collective-permute-done.4.refs_3_, ...), custom_call_target="tpu_custom_call" | custom-call | flops 1879048192 | bytes 8388608 | tf_op jit(solution)/shard_map/project/pallas_call | solution.py:215
  107.6 2.8 %collective-permute-start.25 = (bf16[256,896]{1,0:T(8,128)(2,1)S(1)}, bf16[256,896]{1,0:T(8,128)(2,1)S(1)}, u32[]{:S(2)}, u32[]{:S(2)}) collective-permute-start(bf16[256,896]{1,0:T(8,128)(2,1)S(1)} %get-tuple-element.15), channel_id=1, source_target_pairs={{0,8},{1,9},{2,10},{3,11},{4,12},{5,13},{6,14},{7,15},{8,0},{9,1},... | collective-permute-start | bytes 1376264 | tf_op jit(solution)/shard_map/ppermute | solution.py:33
  110.4 0.9 collective-permute-start.27
  111.9 9.5 %collective-permute-done.25 = bf16[256,896]{1,0:T(8,128)(2,1)S(1)} collective-permute-done((bf16[256,896]{1,0:T(8,128)(2,1)S(1)}, bf16[256,896]{1,0:T(8,128)(2,1)S(1)}, u32[]{:S(2)}, u32[]{:S(2)}) %collective-permute-start.25) | collective-permute-done | bytes 458784 | tf_op jit(solution)/shard_map/ppermute | solution.py:33
  121.3 9.9 %collective-permute-done.27 = bf16[256,896]{1,0:T(8,128)(2,1)S(1)} collective-permute-done((bf16[256,896]{1,0:T(8,128)(2,1)S(1)}, bf16[256,896]{1,0:T(8,128)(2,1)S(1)}, u32[]{:S(2)}, u32[]{:S(2)}) %collective-permute-start.27) | collective-permute-done | bytes 458784 | tf_op jit(solution)/shard_map/ppermute | solution.py:33
  131.8 4.9 %collective-permute-start.28 = (bf16[256,448]{1,0:T(8,128)(2,1)S(1)}, bf16[256,448]{1,0:T(8,128)(2,1)S(1)}, u32[]{:S(2)}, u32[]{:S(2)}) collective-permute-start(bf16[256,448]{1,0:T(8,128)(2,1)S(1)} %get-tuple-element.20), channel_id=1, source_target_pairs={{0,0},{1,1},{2,128},{3,129},{4,4},{5,5},{6,132},{7,133},{8,8},{9,9... | collective-permute-start | bytes 688136 | tf_op jit(solution)/shard_map/ppermute | solution.py:33
  136.7 1.3 collective-permute-start.29
  138.1 2.4 %collective-permute-done.28 = bf16[256,448]{1,0:T(8,128)(2,1)S(1)} collective-permute-done((bf16[256,448]{1,0:T(8,128)(2,1)S(1)}, bf16[256,448]{1,0:T(8,128)(2,1)S(1)}, u32[]{:S(2)}, u32[]{:S(2)}) %collective-permute-start.28) | collective-permute-done | bytes 229408 | tf_op jit(solution)/shard_map/ppermute | solution.py:33
  140.5 3.7 %collective-permute-done.29 = bf16[256,448]{1,0:T(8,128)(2,1)S(1)} collective-permute-done((bf16[256,448]{1,0:T(8,128)(2,1)S(1)}, bf16[256,448]{1,0:T(8,128)(2,1)S(1)}, u32[]{:S(2)}, u32[]{:S(2)}) %collective-permute-start.29) | collective-permute-done | bytes 229408 | tf_op jit(solution)/shard_map/ppermute | solution.py:33
  144.2 0.9 pad_maximum_fusion
  (69 shorter events, 5.6 us)
Async XLA Ops:
  1.2 36.8 %copy-start.3 = (bf16[256,576]{1,0:T(8,128)(2,1)}, bf16[256,576]{1,0:T(8,128)(2,1)S(1)}, u32[]{:S(2)}) copy-start(bf16[256,576]{1,0:T(8,128)(2,1)S(1)} %copy.14.own) | copy-start | bytes 884740
  1.2 20.2 %collective-permute-start.1 = (bf16[128,576]{1,0:T(8,128)(2,1)S(1)}, bf16[128,576]{1,0:T(8,128)(2,1)S(1)}, u32[]{:S(2)}, u32[]{:S(2)}) collective-permute-start(bf16[128,576]{1,0:T(8,128)(2,1)S(1)} %constant_dynamic-slice_fusion), channel_id=1, source_target_pairs={{0,32},{16,48},{32,64},{48,80},{64,96},{80,112},{96,128},{112,144}... | collective-permute-start | bytes 442376 | tf_op jit(solution)/shard_map/ppermute | solution.py:259
  6.9 14.5 %collective-permute-start = (bf16[128,576]{1,0:T(8,128)(2,1)S(1)}, bf16[128,576]{1,0:T(8,128)(2,1)S(1)}, u32[]{:S(2)}, u32[]{:S(2)}) collective-permute-start(bf16[128,576]{1,0:T(8,128)(2,1)S(1)} %constant_dynamic-slice_fusion), channel_id=1, source_target_pairs={{0,16},{16,32},{32,48},{48,64},{64,80},{80,96},{96,112},{112,128},... | collective-permute-start | bytes 442376 | tf_op jit(solution)/shard_map/ppermute | solution.py:259
  13.4 17.2 %collective-permute-start.12 = (bf16[64,1792]{1,0:T(8,128)(2,1)}, bf16[64,1792]{1,0:T(8,128)(2,1)S(1)}, u32[]{:S(2)}, u32[]{:S(2)}) collective-permute-start(bf16[64,1792]{1,0:T(8,128)(2,1)} %get-tuple-element.11.refs_8_), channel_id=1, source_target_pairs={{0,16},{1,17},{2,18},{3,19},{4,20},{5,21},{6,22},{7,23},{8,24},{9,... | collective-permute-start | bytes 688136 | tf_op jit(solution)/shard_map/ppermute | solution.py:33
  16.2 14.4 %collective-permute-start.9 = (bf16[64,1792]{1,0:T(8,128)(2,1)}, bf16[64,1792]{1,0:T(8,128)(2,1)}, u32[]{:S(2)}, u32[]{:S(2)}) collective-permute-start(bf16[64,1792]{1,0:T(8,128)(2,1)} %get-tuple-element.11.refs_8_), channel_id=1, source_target_pairs={{0,112},{1,113},{2,114},{3,115},{4,116},{5,117},{6,118},{7,119},{8... | collective-permute-start | bytes 688136 | tf_op jit(solution)/shard_map/ppermute | solution.py:33
  17.0 9.1 %collective-permute-start.16 = (bf16[64,1792]{1,0:T(8,128)(2,1)}, bf16[64,1792]{1,0:T(8,128)(2,1)}, u32[]{:S(2)}, u32[]{:S(2)}) collective-permute-start(bf16[64,1792]{1,0:T(8,128)(2,1)} %get-tuple-element.12), channel_id=1, source_target_pairs={{0,129},{1,128},{2,131},{3,130},{4,133},{5,132},{6,135},{7,134},{8... | collective-permute-start | bytes 688136 | tf_op jit(solution)/shard_map/ppermute | solution.py:33
  19.0 14.3 %copy-start.5 = (bf16[8,128,512]{2,1,0:T(8,128)(2,1)S(1)}, bf16[8,128,512]{2,1,0:T(8,128)(2,1)}, u32[]{:S(2)}) copy-start(bf16[8,128,512]{2,1,0:T(8,128)(2,1)} %w_key_up.1) | copy-start | bytes 3145732
  19.0 14.3 %copy-start.7 = (bf16[256,1536]{1,0:T(8,128)(2,1)S(1)}, bf16[256,1536]{1,0:T(8,128)(2,1)}, u32[]{:S(2)}) copy-start(bf16[256,1536]{1,0:T(8,128)(2,1)} %rows.1) | copy-start | bytes 2359300
  21.4 16.6 %copy-start.8 = (bf16[128,576]{1,0:T(8,128)(2,1)}, bf16[128,576]{1,0:T(8,128)(2,1)S(1)}, u32[]{:S(2)}) copy-start(bf16[128,576]{1,0:T(8,128)(2,1)S(1)} %collective-permute-done.1.far) | copy-start | bytes 442372
  21.4 16.6 %copy-start.10 = (bf16[128,576]{1,0:T(8,128)(2,1)}, bf16[128,576]{1,0:T(8,128)(2,1)S(1)}, u32[]{:S(2)}) copy-start(bf16[128,576]{1,0:T(8,128)(2,1)S(1)} %collective-permute-done.near) | copy-start | bytes 442372
  22.3 17.3 %collective-permute-start.2 = (bf16[256,576]{1,0:T(8,128)(2,1)}, bf16[256,576]{1,0:T(8,128)(2,1)}, u32[]{:S(2)}, u32[]{:S(2)}) collective-permute-start(bf16[256,576]{1,0:T(8,128)(2,1)} %pad_maximum_fusion.2), channel_id=1, source_target_pairs={{0,2},{1,3},{2,0},{3,1},{4,6},{5,7},{6,4},{7,5},{8,10},{9,11},{10,... | collective-permute-start | bytes 884744 | tf_op jit(solution)/shard_map/ppermute | solution.py:33
  26.1 11.9 %collective-permute-start.21 = (bf16[64,1792]{1,0:T(8,128)(2,1)}, bf16[64,1792]{1,0:T(8,128)(2,1)}, u32[]{:S(2)}, u32[]{:S(2)}) collective-permute-start(bf16[64,1792]{1,0:T(8,128)(2,1)} %collective-permute-done.16.refs_16_), channel_id=1, source_target_pairs={{0,16},{1,17},{2,18},{3,19},{4,20},{5,21},{6,22},{7,23},{8,24},{9,... | collective-permute-start | bytes 688136 | tf_op jit(solution)/shard_map/ppermute | solution.py:33
  27.2 0.7 copy-start.1
  27.9 17.0 %collective-permute-start.17 = (bf16[64,1792]{1,0:T(8,128)(2,1)}, bf16[64,1792]{1,0:T(8,128)(2,1)}, u32[]{:S(2)}, u32[]{:S(2)}) collective-permute-start(bf16[64,1792]{1,0:T(8,128)(2,1)} %collective-permute-done.16.refs_16_), channel_id=1, source_target_pairs={{0,112},{1,113},{2,114},{3,115},{4,116},{5,117},{6,118},{7,119},{8... | collective-permute-start | bytes 688136 | tf_op jit(solution)/shard_map/ppermute | solution.py:33
  30.6 17.2 %collective-permute-start.13 = (bf16[64,1792]{1,0:T(8,128)(2,1)S(1)}, bf16[64,1792]{1,0:T(8,128)(2,1)}, u32[]{:S(2)}, u32[]{:S(2)}) collective-permute-start(bf16[64,1792]{1,0:T(8,128)(2,1)S(1)} %collective-permute-done.12.refs_15_), channel_id=1, source_target_pairs={{0,16},{1,17},{2,18},{3,19},{4,20},{5,21},{6,22},{7,23},{8,24},{9,... | collective-permute-start | bytes 688136 | tf_op jit(solution)/shard_map/ppermute | solution.py:33
  30.6 17.2 %collective-permute-start.10 = (bf16[64,1792]{1,0:T(8,128)(2,1)}, bf16[64,1792]{1,0:T(8,128)(2,1)}, u32[]{:S(2)}, u32[]{:S(2)}) collective-permute-start(bf16[64,1792]{1,0:T(8,128)(2,1)} %collective-permute-done.9.refs_9_), channel_id=1, source_target_pairs={{0,112},{1,113},{2,114},{3,115},{4,116},{5,117},{6,118},{7,119},{8... | collective-permute-start | bytes 688136 | tf_op jit(solution)/shard_map/ppermute | solution.py:33
  33.3 2.3 %copy-start = (bf16[1536,1536]{1,0:T(8,128)(2,1)S(1)}, bf16[1536,1536]{1,0:T(8,128)(2,1)}, u32[]{:S(2)}) copy-start(bf16[1536,1536]{1,0:T(8,128)(2,1)} %w_query.1) | copy-start | bytes 14155780
  38.0 22.1 %collective-permute-start.22 = (bf16[64,1792]{1,0:T(8,128)(2,1)}, bf16[64,1792]{1,0:T(8,128)(2,1)}, u32[]{:S(2)}, u32[]{:S(2)}) collective-permute-start(bf16[64,1792]{1,0:T(8,128)(2,1)} %collective-permute-done.21.refs_23_), channel_id=1, source_target_pairs={{0,16},{1,17},{2,18},{3,19},{4,20},{5,21},{6,22},{7,23},{8,24},{9,... | collective-permute-start | bytes 688136 | tf_op jit(solution)/shard_map/ppermute | solution.py:33
  39.6 1.0 copy-start.2
  40.6 1.0 copy-start.4
  41.5 0.9 copy-start.9
  42.5 0.9 copy-start.11
  43.4 16.8 %copy-start.13 = (bf16[512,512]{1,0:T(8,128)(2,1)S(1)}, bf16[512,512]{1,0:T(8,128)(2,1)}, u32[]{:S(2)}) copy-start(bf16[512,512]{1,0:T(8,128)(2,1)} %fusion.reorder) | copy-start | bytes 1572868
  44.9 19.2 %collective-permute-start.18 = (bf16[64,1792]{1,0:T(8,128)(2,1)}, bf16[64,1792]{1,0:T(8,128)(2,1)S(1)}, u32[]{:S(2)}, u32[]{:S(2)}) collective-permute-start(bf16[64,1792]{1,0:T(8,128)(2,1)} %collective-permute-done.17.refs_17_), channel_id=1, source_target_pairs={{0,112},{1,113},{2,114},{3,115},{4,116},{5,117},{6,118},{7,119},{8... | collective-permute-start | bytes 688136 | tf_op jit(solution)/shard_map/ppermute | solution.py:33
  47.8 17.0 %collective-permute-start.14 = (bf16[64,1792]{1,0:T(8,128)(2,1)}, bf16[64,1792]{1,0:T(8,128)(2,1)S(1)}, u32[]{:S(2)}, u32[]{:S(2)}) collective-permute-start(bf16[64,1792]{1,0:T(8,128)(2,1)} %collective-permute-done.13.refs_14_), channel_id=1, source_target_pairs={{0,16},{1,17},{2,18},{3,19},{4,20},{5,21},{6,22},{7,23},{8,24},{9,... | collective-permute-start | bytes 688136 | tf_op jit(solution)/shard_map/ppermute | solution.py:33
  47.8 19.6 %collective-permute-start.11 = (bf16[64,1792]{1,0:T(8,128)(2,1)}, bf16[64,1792]{1,0:T(8,128)(2,1)S(1)}, u32[]{:S(2)}, u32[]{:S(2)}) collective-permute-start(bf16[64,1792]{1,0:T(8,128)(2,1)} %collective-permute-done.10.refs_10_), channel_id=1, source_target_pairs={{0,112},{1,113},{2,114},{3,115},{4,116},{5,117},{6,118},{7,119},{8... | collective-permute-start | bytes 688136 | tf_op jit(solution)/shard_map/ppermute | solution.py:33
  50.5 1.0 copy-start.12
  51.5 1.2 copy-start.14
  56.6 30.5 %copy-start.6 = (bf16[64,1792]{1,0:T(8,128)(2,1)S(1)}, bf16[64,1792]{1,0:T(8,128)(2,1)}, u32[]{:S(2)}) copy-start(bf16[64,1792]{1,0:T(8,128)(2,1)} %get-tuple-element.11.refs_8_) | copy-start | bytes 688132
  56.6 14.5 %collective-permute-start.7 = (bf16[256,512]{1,0:T(8,128)(2,1)S(1)}, bf16[256,512]{1,0:T(8,128)(2,1)S(1)}, u32[]{:S(2)}, u32[]{:S(2)}) collective-permute-start(bf16[256,512]{1,0:T(8,128)(2,1)S(1)} %attend.2.refs_0_), channel_id=1, source_target_pairs={{0,129},{1,128},{2,131},{3,130},{4,133},{5,132},{6,135},{7,134},{8... | collective-permute-start | bytes 786440 | tf_op jit(solution)/shard_map/ppermute | solution.py:33
  60.1 12.1 %collective-permute-start.5 = (bf16[256,512]{1,0:T(8,128)(2,1)S(1)}, bf16[256,512]{1,0:T(8,128)(2,1)S(1)}, u32[]{:S(2)}, u32[]{:S(2)}) collective-permute-start(bf16[256,512]{1,0:T(8,128)(2,1)S(1)} %attend.2.refs_0_), channel_id=1, source_target_pairs={{0,128},{1,129},{2,130},{3,131},{4,132},{5,133},{6,134},{7,135},{8... | collective-permute-start | bytes 786440 | tf_op jit(solution)/shard_map/ppermute | solution.py:33
  64.1 11.1 %collective-permute-start.3 = (bf16[256,512]{1,0:T(8,128)(2,1)S(1)}, bf16[256,512]{1,0:T(8,128)(2,1)S(1)}, u32[]{:S(2)}, u32[]{:S(2)}) collective-permute-start(bf16[256,512]{1,0:T(8,128)(2,1)S(1)} %attend.2.refs_0_), channel_id=1, source_target_pairs={{0,1},{1,0},{2,3},{3,2},{4,5},{5,4},{6,7},{7,6},{8,9},{9,8},{10,11... | collective-permute-start | bytes 786440 | tf_op jit(solution)/shard_map/ppermute | solution.py:33
  64.8 16.2 %collective-permute-start.8 = (bf16[256,512]{1,0:T(8,128)(2,1)S(1)}, bf16[256,512]{1,0:T(8,128)(2,1)S(1)}, u32[]{:S(2)}, u32[]{:S(2)}) collective-permute-start(bf16[256,512]{1,0:T(8,128)(2,1)S(1)} %attend.3.refs_1_), channel_id=1, source_target_pairs={{0,129},{1,128},{2,131},{3,130},{4,133},{5,132},{6,135},{7,134},{8... | collective-permute-start | bytes 786440 | tf_op jit(solution)/shard_map/ppermute | solution.py:33
  67.4 13.6 %collective-permute-start.19 = (bf16[64,1792]{1,0:T(8,128)(2,1)S(1)}, bf16[64,1792]{1,0:T(8,128)(2,1)S(1)}, u32[]{:S(2)}, u32[]{:S(2)}) collective-permute-start(bf16[64,1792]{1,0:T(8,128)(2,1)S(1)} %collective-permute-done.18.refs_18_), channel_id=1, source_target_pairs={{0,112},{1,113},{2,114},{3,115},{4,116},{5,117},{6,118},{7,119},{8... | collective-permute-start | bytes 688136 | tf_op jit(solution)/shard_map/ppermute | solution.py:33
  71.2 12.6 %collective-permute-start.6 = (bf16[256,512]{1,0:T(8,128)(2,1)S(1)}, bf16[256,512]{1,0:T(8,128)(2,1)S(1)}, u32[]{:S(2)}, u32[]{:S(2)}) collective-permute-start(bf16[256,512]{1,0:T(8,128)(2,1)S(1)} %attend.3.refs_1_), channel_id=1, source_target_pairs={{0,128},{1,129},{2,130},{3,131},{4,132},{5,133},{6,134},{7,135},{8... | collective-permute-start | bytes 786440 | tf_op jit(solution)/shard_map/ppermute | solution.py:33
  72.3 13.2 %collective-permute-start.4 = (bf16[256,512]{1,0:T(8,128)(2,1)S(1)}, bf16[256,512]{1,0:T(8,128)(2,1)S(1)}, u32[]{:S(2)}, u32[]{:S(2)}) collective-permute-start(bf16[256,512]{1,0:T(8,128)(2,1)S(1)} %attend.3.refs_1_), channel_id=1, source_target_pairs={{0,1},{1,0},{2,3},{3,2},{4,5},{5,4},{6,7},{7,6},{8,9},{9,8},{10,11... | collective-permute-start | bytes 786440 | tf_op jit(solution)/shard_map/ppermute | solution.py:33
  75.2 10.3 %collective-permute-start.23 = (bf16[64,1792]{1,0:T(8,128)(2,1)}, bf16[64,1792]{1,0:T(8,128)(2,1)S(1)}, u32[]{:S(2)}, u32[]{:S(2)}) collective-permute-start(bf16[64,1792]{1,0:T(8,128)(2,1)} %collective-permute-done.22.refs_22_), channel_id=1, source_target_pairs={{0,16},{1,17},{2,18},{3,19},{4,20},{5,21},{6,22},{7,23},{8,24},{9,... | collective-permute-start | bytes 688136 | tf_op jit(solution)/shard_map/ppermute | solution.py:33
  81.0 6.1 %collective-permute-start.15 = (bf16[64,1792]{1,0:T(8,128)(2,1)S(1)}, bf16[64,1792]{1,0:T(8,128)(2,1)S(1)}, u32[]{:S(2)}, u32[]{:S(2)}) collective-permute-start(bf16[64,1792]{1,0:T(8,128)(2,1)S(1)} %collective-permute-done.14.refs_13_), channel_id=1, source_target_pairs={{0,16},{1,17},{2,18},{3,19},{4,20},{5,21},{6,22},{7,23},{8,24},{9,... | collective-permute-start | bytes 688136 | tf_op jit(solution)/shard_map/ppermute | solution.py:33
  81.0 6.1 %collective-permute-start.20 = (bf16[64,1792]{1,0:T(8,128)(2,1)S(1)}, bf16[64,1792]{1,0:T(8,128)(2,1)S(1)}, u32[]{:S(2)}, u32[]{:S(2)}) collective-permute-start(bf16[64,1792]{1,0:T(8,128)(2,1)S(1)} %collective-permute-done.19.refs_19_), channel_id=1, source_target_pairs={{0,112},{1,113},{2,114},{3,115},{4,116},{5,117},{6,118},{7,119},{8... | collective-permute-start | bytes 688136 | tf_op jit(solution)/shard_map/ppermute | solution.py:33
  95.2 11.8 %collective-permute-start.24 = (bf16[4,256,896]{2,1,0:T(8,128)(2,1)S(1)}, bf16[4,256,896]{2,1,0:T(8,128)(2,1)S(1)}, u32[]{:S(2)}, u32[]{:S(2)}) collective-permute-start(bf16[4,256,896]{2,1,0:T(8,128)(2,1)S(1)} %project.3), channel_id=1, source_target_pairs={{0,2},{1,3},{2,0},{3,1},{4,6},{5,7},{6,4},{7,5},{8,10},{9,11},{10,... | collective-permute-start | bytes 5505032 | tf_op jit(solution)/shard_map/ppermute | solution.py:33
  107.6 13.7 %collective-permute-start.25 = (bf16[256,896]{1,0:T(8,128)(2,1)S(1)}, bf16[256,896]{1,0:T(8,128)(2,1)S(1)}, u32[]{:S(2)}, u32[]{:S(2)}) collective-permute-start(bf16[256,896]{1,0:T(8,128)(2,1)S(1)} %get-tuple-element.15), channel_id=1, source_target_pairs={{0,8},{1,9},{2,10},{3,11},{4,12},{5,13},{6,14},{7,15},{8,0},{9,1},... | collective-permute-start | bytes 1376264 | tf_op jit(solution)/shard_map/ppermute | solution.py:33
  110.4 20.8 %collective-permute-start.27 = (bf16[256,896]{1,0:T(8,128)(2,1)S(1)}, bf16[256,896]{1,0:T(8,128)(2,1)S(1)}, u32[]{:S(2)}, u32[]{:S(2)}) collective-permute-start(bf16[256,896]{1,0:T(8,128)(2,1)S(1)} %get-tuple-element.16), channel_id=1, source_target_pairs={{0,12},{1,13},{2,14},{3,15},{4,0},{5,1},{6,2},{7,3},{8,4},{9,5},{1... | collective-permute-start | bytes 1376264 | tf_op jit(solution)/shard_map/ppermute | solution.py:33
  111.3 20.2 %collective-permute-start.26 = (bf16[256,896]{1,0:T(8,128)(2,1)S(1)}, bf16[256,896]{1,0:T(8,128)(2,1)S(1)}, u32[]{:S(2)}, u32[]{:S(2)}) collective-permute-start(bf16[256,896]{1,0:T(8,128)(2,1)S(1)} %get-tuple-element.17), channel_id=1, source_target_pairs={{0,4},{1,5},{2,6},{3,7},{4,8},{5,9},{6,10},{7,11},{8,12},{9,13},{1... | collective-permute-start | bytes 1376264 | tf_op jit(solution)/shard_map/ppermute | solution.py:33
  131.8 8.7 %collective-permute-start.28 = (bf16[256,448]{1,0:T(8,128)(2,1)S(1)}, bf16[256,448]{1,0:T(8,128)(2,1)S(1)}, u32[]{:S(2)}, u32[]{:S(2)}) collective-permute-start(bf16[256,448]{1,0:T(8,128)(2,1)S(1)} %get-tuple-element.20), channel_id=1, source_target_pairs={{0,0},{1,1},{2,128},{3,129},{4,4},{5,5},{6,132},{7,133},{8,8},{9,9... | collective-permute-start | bytes 688136 | tf_op jit(solution)/shard_map/ppermute | solution.py:33
  136.7 7.5 %collective-permute-start.29 = (bf16[256,448]{1,0:T(8,128)(2,1)S(1)}, bf16[256,448]{1,0:T(8,128)(2,1)S(1)}, u32[]{:S(2)}, u32[]{:S(2)}) collective-permute-start(bf16[256,448]{1,0:T(8,128)(2,1)S(1)} %get-tuple-element.21), channel_id=1, source_target_pairs={{0,1},{1,0},{2,129},{3,128},{4,5},{5,4},{6,133},{7,132},{8,9},{9,8... | collective-permute-start | bytes 688136 | tf_op jit(solution)/shard_map/ppermute | solution.py:33

commit v3 on v2

--- a/solution.py
+++ b/solution.py
@@ -103,29 +103,35 @@
     hidden[...] = jnp.where(visible, 0.0, -1e30)
 
 
-def attend_kernel(group, queries, keys, hidden, w_value_up, reorder, out):
+def attend_kernel(queries, keys, hidden, w_value_up, reorder, out):
     scale = 192.0**-0.5 * 1.4426950408889634
     latent = keys[:, :512]
-    heads = []
-    for pair in range(2):
-        scores = lax.dot_general(
-            queries[1024 * group + 512 * pair : 1024 * group + 512 * pair + 512, :],
-            keys[...],
-            (((1,), (1,)), ((), ())),
-            preferred_element_type=F32,
-        )
-        for i in range(2):
-            part = scores[256 * i : 256 * i + 256] * scale + hidden[...]
-            top = jnp.max(part, axis=1, keepdims=True)
-            powers = jnp.exp2(part - top)
-            share = 1.0 / jnp.sum(powers, axis=1, keepdims=True)
-            mixed = jnp.dot(powers.astype(BF), latent, preferred_element_type=F32) * share
-            attention = jnp.dot(
-                mixed.astype(BF), w_value_up[4 * group + 2 * pair + i], preferred_element_type=F32
+    for group in range(2):
+        heads = []
+        for pair in range(2):
+            first = 1024 * group + 512 * pair
+            scores = lax.dot_general(
+                queries[first : first + 512, :],
+                keys[...],
+                (((1,), (1,)), ((), ())),
+                preferred_element_type=F32,
             )
-            heads.append(attention.astype(BF))
-    rows = jnp.concatenate(heads, 1)
-    out[...] = jnp.dot(rows, reorder[...], preferred_element_type=F32).astype(BF)
+            for i in range(2):
+                part = scores[256 * i : 256 * i + 256] * scale + hidden[...]
+                top = jnp.max(part, axis=1, keepdims=True)
+                powers = jnp.exp2(part - top)
+                share = 1.0 / jnp.sum(powers, axis=1, keepdims=True)
+                mixed = jnp.dot(powers.astype(BF), latent, preferred_element_type=F32) * share
+                attention = jnp.dot(
+                    mixed.astype(BF),
+                    w_value_up[4 * group + 2 * pair + i],
+                    preferred_element_type=F32,
+                )
+                heads.append(attention.astype(BF))
+        rows = jnp.concatenate(heads, 1)
+        out[:, 512 * group : 512 * group + 512] = jnp.dot(
+            rows, reorder[...], preferred_element_type=F32
+        ).astype(BF)
 
 
 def turn_of(positions):
@@ -149,17 +155,22 @@
 
 
 def project_kernel(theirs, place, *refs):
-    groups, blocks, (out, rows, weights, total, sem) = refs[:8], refs[8:24], refs[24:]
+    groups, gathered, blocks, (out, rows, weights, total, sem) = (
+        refs[:4],
+        refs[4],
+        refs[5:13],
+        refs[13:],
+    )
     copies = []
     for p in range(2):
         for k in range(8):
+            slot = k if p == 0 else (place[2] + k) % 8
             for g in range(2):
-                at = 512 * g + 256 * p + 32 * k
+                at = pl.multiple_of(512 * g + 256 * p + 32 * slot, 32)
+                block = gathered.at[k] if p == 0 else blocks[k]
                 copies.append(
                     pltpu.make_async_copy(
-                        blocks[8 * p + k].at[pl.ds(32 * g, 32)],
-                        weights.at[pl.ds(at, 32)],
-                        sem.at[len(copies)],
+                        block.at[pl.ds(32 * g, 32)], weights.at[pl.ds(at, 32)], sem.at[len(copies)]
                     )
                 )
     for copy in copies:
@@ -172,9 +183,9 @@
             for g in range(2):
                 for j in range(2):
                     for p in range(2):
-                        half = pl.ds(pl.multiple_of(256 * (place[1] ^ p), 256), 256)
+                        half = pl.ds(pl.multiple_of(512 * g + 256 * (place[1] ^ p), 256), 256)
                         rows[256 * j : 256 * j + 256, 512 * g + 256 * p : 512 * g + 256 * p + 256] = (
-                            groups[2 * (pick + j) + g][:, half]
+                            groups[pick + j][:, half]
                         )
 
     for copy in copies:
@@ -210,7 +221,7 @@
     )(jnp.stack([x, y]), rows)
 
 
-def call(kernel, shapes, specs, args, name, flops, moved_bytes, scratch=()):
+def call(kernel, shapes, specs, args, name, flops, moved_bytes, room, scratch=()):
     many = isinstance(shapes, list)
     return pl.pallas_call(
         kernel,
@@ -218,7 +229,7 @@
         in_specs=specs,
         out_specs=whole(len(shapes)) if many else whole(1)[0],
         scratch_shapes=list(scratch),
-        compiler_params=pltpu.CompilerParams(vmem_limit_bytes=40 << 20),
+        compiler_params=pltpu.CompilerParams(vmem_limit_bytes=room << 20),
         name=name,
         cost_estimate=pl.CostEstimate(
             flops=flops, bytes_accessed=moved_bytes, transcendentals=0
@@ -230,15 +241,16 @@
     return jax.ShapeDtypeStruct(shape, kind)
 
 
-def project(theirs, place, groups, blocks, kind):
+def project(theirs, place, groups, gathered, blocks, kind):
     return call(
         functools.partial(project_kernel, theirs),
         array((4, 256, 896), kind),
-        scalars() + whole(8) + [pl.BlockSpec(memory_space=pl.ANY)] * 16,
-        (place, *groups, *blocks),
+        scalars() + whole(4) + [pl.BlockSpec(memory_space=pl.ANY)] * 9,
+        (place, *groups, gathered, *blocks),
         "project",
         2 * 512 * 1024 * 1792,
         8 << 20,
+        20,
         [
             pltpu.VMEM((512, 1024), BF),
             pltpu.VMEM((1024, 1792), BF),
@@ -260,17 +272,16 @@
     )
     swapped = other_core(jnp.concatenate([near, far], 0))
 
+    gathered = lax.all_gather(own, "z", axis=0)
     other = xor_y(given, 3)
-    blocks = [[own] + [None] * 7, [other] + [None] * 7]
-    for p in range(2):
-        up = down = blocks[p][0]
-        for s in range(1, 5):
-            if s < 4 or p == 0:
-                up = up_z(up)
-                blocks[p][8 - s] = up
-            if s < 4 or p == 1:
-                down = down_z(down)
-                blocks[p][s] = down
+    blocks = [other] + [None] * 7
+    up = down = other
+    for s in range(1, 5):
+        up = up_z(up)
+        blocks[8 - s] = up
+        if s < 4:
+            down = down_z(down)
+            blocks[s] = down
 
     turn = turn_of(slab * 256 + jnp.arange(768, dtype=jnp.int32) - 512)
     queries = call(
@@ -281,6 +292,7 @@
         "queries",
         2 * 256 * 1536 * 1536 + 2 * 2048 * 128 * 512,
         8 << 20,
+        14,
     )
     keys, hidden = call(
         keys_kernel,
@@ -290,34 +302,30 @@
         "keys",
         768 * 640 * 8,
         4 << 20,
+        8,
     )
     column = jnp.arange(512, dtype=jnp.int32)
     source = (
-        (column // 8 % 4) * 128 + (column // 256) * 64 + ((z + column // 32) % 8) * 8 + column % 8
+        (column // 8 % 4) * 128 + (column // 256) * 64 + (column // 32 % 8) * 8 + column % 8
     )
     reorder = (column[:, None] == source[None, :]).astype(BF)
-    groups = [[None] * 2 for _ in range(4)]
-    for g in range(2):
-        rows = call(
-            functools.partial(attend_kernel, g),
-            array((256, 512)),
-            whole(5),
-            (queries, keys, hidden, w_value_up, reorder),
-            "attend",
-            2 * 1024 * 768 * 1152 + 2 * 1024 * 512 * 128,
-            5 << 20,
-        )
-        groups[0][g] = rows
-        for q in (2, 1, 3):
-            groups[q][g] = xor_y(rows, q)
-    place = jnp.stack([c, yh])
-    rows = [part for slot in groups for part in slot]
-    flat = blocks[0] + blocks[1]
-    theirs = other_core(project(1, place, rows, flat, BF))
-    mine = project(0, place, rows, flat, F32)
+    rows = call(
+        attend_kernel,
+        array((256, 1024)),
+        whole(5),
+        (queries, keys, hidden, w_value_up, reorder),
+        "attend",
+        4 * 1024 * 768 * 1152 + 4 * 1024 * 512 * 128,
+        9 << 20,
+        18,
+    )
+    groups = [rows] + [xor_y(rows, q) for q in (1, 2, 3)]
+    place = jnp.stack([c, yh, z])
+    theirs = other_core(project(1, place, groups, gathered, blocks, BF))
+    mine = project(0, place, groups, gathered, blocks, F32)
     sums = mine + theirs.astype(F32)
     result = sums[0]
-    for d in (2, 1, 3):
+    for d in (1, 3, 2):
         result = result + along_x(sums[d].astype(BF), d).astype(F32)
     result = result.astype(BF)
     pieces = [home(result[:, 448 * r : 448 * r + 448], r) for r in range(2)]

time: 146 us -> 157 us (1.075)
  starting transfers between devices: 55.2 us -> 41.6 us
  between operations: 0.98 us -> 14.3 us
  waiting for transfers between devices: 40.7 us -> 49.3 us
  Pallas kernels: 30.3 us -> 33 us
    ppermute x28 -> x18, starting transfers between devices: 45.9 us -> 31 us  [moved(): return lax.ppermute(a, AXES, pairs)]
    ppermute x28 -> x18, waiting for transfers between devices: 40.7 us -> 49.3 us  [moved(): return lax.ppermute(a, AXES, pairs)]
    pallas_call x6 -> x5, Pallas kernels: 28.1 us -> 30.7 us  [call(): pl.pallas_call(kernel, out_shape=shapes, in_specs=specs, out_specs=whole(...]
    unnamed x32 -> x24, local copies, waits for them, and re-layouts: 11.7 us -> 11.4 us
  transfers between devices with their start and end apart: 30 -> 21, of which waited for: 10 -> 9; matrix products, arithmetic and copies ran while one was open for 4% -> 4% of each run, Pallas kernels for 15% -> 13%
where the time goes in v3:
time: 157 us; the launch traced here: 156 us
  waiting for transfers between devices  49.3 us (31%)
  starting transfers between devices  41.6 us (26%)
  Pallas kernels  33 us (21%)
  between operations  14.3 us (9%)
  local copies, waits for them, and re-layouts  12.4 us (8%)
  other arithmetic  5.53 us (4%)
    ppermute x18, waiting for transfers between devices, moved(): return lax.ppermute(a, AXES, pairs)  49.3 us
    ppermute x18, starting transfers between devices, moved(): return lax.ppermute(a, AXES, pairs)  31 us
    pallas_call x5, Pallas kernels, call(): pl.pallas_call(kernel, out_shape=shapes, in_specs=specs, out_specs=whole(...  30.7 us
    unnamed x24, local copies, waits for them, and re-layouts  11.4 us
    ppermute x2, starting transfers between devices, local(): lax.ppermute(half, CTX, [(i, i + by) for i in range(16 - by)])  10.6 us
  transfers between devices with their start and end apart: 21, of which 9 were waited for; matrix products, arithmetic and copies ran while one was open for 4% of the time, Pallas kernels for 13%

profile of v3, /device:TPU:1, one launch (start us, length us, event | category | flops | bytes accessed | tf_op | source)
XLA Modules:
  0.0 156.1 jit_solution(3838413858036058208)
XLA Ops:
  6.5 0.7 pad_add_fusion.2.place
  7.2 2.2 %quarters.1 = (bf16[64,1792]{1,0:T(8,128)(2,1)}, bf16[64,1792]{1,0:T(8,128)(2,1)}) custom-call(s32[2]{0:T(128)} %pad_add_fusion.2.place, bf16[64,7168]{1,0:T(8,128)(2,1)} %bitcast.26), custom_call_target="tpu_custom_call" | custom-call | bytes 2097152 | tf_op jit(solution)/shard_map/quarters/pallas_call | solution.py:214
  9.5 1.3 copy.14.own
  10.8 0.7 constant_dynamic-slice_fusion
  11.5 6.4 %collective-permute-start.1 = (bf16[128,576]{1,0:T(8,128)(2,1)}, bf16[128,576]{1,0:T(8,128)(2,1)}, u32[]{:S(2)}, u32[]{:S(2)}) collective-permute-start(bf16[128,576]{1,0:T(8,128)(2,1)} %constant_dynamic-slice_fusion), channel_id=1, source_target_pairs={{0,32},{16,48},{32,64},{48,80},{64,96},{80,112},{96,128},{112,144}... | collective-permute-start | bytes 442376 | tf_op jit(solution)/shard_map/ppermute | solution.py:271
  17.9 4.2 %collective-permute-start = (bf16[128,576]{1,0:T(8,128)(2,1)}, bf16[128,576]{1,0:T(8,128)(2,1)}, u32[]{:S(2)}, u32[]{:S(2)}) collective-permute-start(bf16[128,576]{1,0:T(8,128)(2,1)} %constant_dynamic-slice_fusion), channel_id=1, source_target_pairs={{0,16},{16,32},{32,48},{48,64},{64,80},{80,96},{96,112},{112,128},... | collective-permute-start | bytes 442376 | tf_op jit(solution)/shard_map/ppermute | solution.py:271
  22.1 1.5 collective-permute-start.6
  23.6 1.5 multiply_cosine_fusion
  25.1 0.4 pad_maximum_fusion.1.turn
  26.1 1.4 copy.15.cache
  27.5 2.3 %copy-done.1 = bf16[1536,1536]{1,0:T(8,128)(2,1)S(1)} copy-done((bf16[1536,1536]{1,0:T(8,128)(2,1)S(1)}, bf16[1536,1536]{1,0:T(8,128)(2,1)}, u32[]{:S(2)}) %copy-start.1) | copy-done | bytes 4718616
  29.8 2.3 %queries.1 = bf16[2048,640]{1,0:T(8,128)(2,1)S(1)} custom-call(bf16[256,1536]{1,0:T(8,128)(2,1)S(1)} %copy-done.9, bf16[1536,1536]{1,0:T(8,128)(2,1)S(1)} %copy-done.1, bf16[8,128,512]{2,1,0:T(8,128)(2,1)S(1)} %copy-done.2, f32[256,128]{1,0:T(8,128)S(1)} %slice.31.turn), custom_call_target="tpu_custom_call" | custom-call | flops 1476395008 | bytes 8388608 | tf_op jit(solution)/shard_map/queries/pallas_call | solution.py:226
  32.2 1.1 pad_maximum_fusion.2
  33.3 1.6 %collective-permute-start.2 = (bf16[256,576]{1,0:T(8,128)(2,1)S(1)}, bf16[256,576]{1,0:T(8,128)(2,1)S(1)}, u32[]{:S(2)}, u32[]{:S(2)}) collective-permute-start(bf16[256,576]{1,0:T(8,128)(2,1)S(1)} %pad_maximum_fusion.2), channel_id=1, source_target_pairs={{0,2},{1,3},{2,0},{3,1},{4,6},{5,7},{6,4},{7,5},{8,10},{9,11},{10,... | collective-permute-start | bytes 884744 | tf_op jit(solution)/shard_map/ppermute | solution.py:33
  35.0 2.9 %collective-permute-start.10 = (bf16[64,1792]{1,0:T(8,128)(2,1)S(1)}, bf16[64,1792]{1,0:T(8,128)(2,1)S(1)}, u32[]{:S(2)}, u32[]{:S(2)}) collective-permute-start(bf16[64,1792]{1,0:T(8,128)(2,1)S(1)} %collective-permute-done.6.refs_5_), channel_id=1, source_target_pairs={{0,16},{1,17},{2,18},{3,19},{4,20},{5,21},{6,22},{7,23},{8,24},{9,... | collective-permute-start | bytes 688136 | tf_op jit(solution)/shard_map/ppermute | solution.py:33
  38.2 1.5 keys.1
  39.6 8.7 %collective-permute-done.10.refs_12_ = bf16[64,1792]{1,0:T(8,128)(2,1)S(1)} collective-permute-done((bf16[64,1792]{1,0:T(8,128)(2,1)S(1)}, bf16[64,1792]{1,0:T(8,128)(2,1)S(1)}, u32[]{:S(2)}, u32[]{:S(2)}) %collective-permute-start.10) | collective-permute-done | bytes 229408 | tf_op jit(solution)/shard_map/ppermute | solution.py:33
  48.3 2.8 %collective-permute-start.11 = (bf16[64,1792]{1,0:T(8,128)(2,1)S(1)}, bf16[64,1792]{1,0:T(8,128)(2,1)S(1)}, u32[]{:S(2)}, u32[]{:S(2)}) collective-permute-start(bf16[64,1792]{1,0:T(8,128)(2,1)S(1)} %collective-permute-done.10.refs_12_), channel_id=1, source_target_pairs={{0,16},{1,17},{2,18},{3,19},{4,20},{5,21},{6,22},{7,23},{8,24},{9,... | collective-permute-start | bytes 688136 | tf_op jit(solution)/shard_map/ppermute | solution.py:33
  51.1 7.4 %attend.1.refs_0_ = bf16[256,1024]{1,0:T(8,128)(2,1)S(1)} custom-call(bf16[2048,640]{1,0:T(8,128)(2,1)S(1)} %queries.1, bf16[768,640]{1,0:T(8,128)(2,1)S(1)} %get-tuple-element.9.keys, f32[256,768]{1,0:T(8,128)S(1)} %get-tuple-element.10.hidden, bf16[8,512,128]{2,1,0:T(8,128)(2,1)S(1)} %copy-done.10, bf16[512,512]{1,0:T(8,128)(2,1)S(1)} %fusion.reorder), custom_call_target="tpu_custom_call" | custom-call | flops 3892314112 | bytes 9437184 | tf_op jit(solution)/shard_map/attend/pallas_call | solution.py:226
  58.5 3.0 %collective-permute-start.5 = (bf16[256,1024]{1,0:T(8,128)(2,1)S(1)}, bf16[256,1024]{1,0:T(8,128)(2,1)S(1)}, u32[]{:S(2)}, u32[]{:S(2)}) collective-permute-start(bf16[256,1024]{1,0:T(8,128)(2,1)S(1)} %attend.1.refs_0_), channel_id=1, source_target_pairs={{0,129},{1,128},{2,131},{3,130},{4,133},{5,132},{6,135},{7,134},{8... | collective-permute-start | bytes 1572872 | tf_op jit(solution)/shard_map/ppermute | solution.py:33
  61.5 0.3 collective-permute-start.4
  61.8 0.4 collective-permute-start.3
  62.2 2.7 %collective-permute-start.8 = (bf16[64,1792]{1,0:T(8,128)(2,1)S(1)}, bf16[64,1792]{1,0:T(8,128)(2,1)S(1)}, u32[]{:S(2)}, u32[]{:S(2)}) collective-permute-start(bf16[64,1792]{1,0:T(8,128)(2,1)S(1)} %collective-permute-done.7.refs_6_), channel_id=1, source_target_pairs={{0,112},{1,113},{2,114},{3,115},{4,116},{5,117},{6,118},{7,119},{8... | collective-permute-start | bytes 688136 | tf_op jit(solution)/shard_map/ppermute | solution.py:33
  64.9 3.5 %collective-permute-done.8.refs_7_ = bf16[64,1792]{1,0:T(8,128)(2,1)S(1)} collective-permute-done((bf16[64,1792]{1,0:T(8,128)(2,1)S(1)}, bf16[64,1792]{1,0:T(8,128)(2,1)S(1)}, u32[]{:S(2)}, u32[]{:S(2)}) %collective-permute-start.8) | collective-permute-done | bytes 229408 | tf_op jit(solution)/shard_map/ppermute | solution.py:33
  68.4 3.3 %collective-permute-start.9 = (bf16[64,1792]{1,0:T(8,128)(2,1)S(1)}, bf16[64,1792]{1,0:T(8,128)(2,1)S(1)}, u32[]{:S(2)}, u32[]{:S(2)}) collective-permute-start(bf16[64,1792]{1,0:T(8,128)(2,1)S(1)} %collective-permute-done.8.refs_7_), channel_id=1, source_target_pairs={{0,112},{1,113},{2,114},{3,115},{4,116},{5,117},{6,118},{7,119},{8... | collective-permute-start | bytes 688136 | tf_op jit(solution)/shard_map/ppermute | solution.py:33
  71.7 0.7 copy-done.3
  72.5 2.2 %collective-permute-done.9.refs_8_ = bf16[64,1792]{1,0:T(8,128)(2,1)S(1)} collective-permute-done((bf16[64,1792]{1,0:T(8,128)(2,1)S(1)}, bf16[64,1792]{1,0:T(8,128)(2,1)S(1)}, u32[]{:S(2)}, u32[]{:S(2)}) %collective-permute-start.9) | collective-permute-done | bytes 229408 | tf_op jit(solution)/shard_map/ppermute | solution.py:33
  74.7 0.7 copy-done.5
  75.4 8.7 %collective-permute-done.5.refs_3_ = bf16[256,1024]{1,0:T(8,128)(2,1)S(1)} collective-permute-done((bf16[256,1024]{1,0:T(8,128)(2,1)S(1)}, bf16[256,1024]{1,0:T(8,128)(2,1)S(1)}, u32[]{:S(2)}, u32[]{:S(2)}) %collective-permute-start.5) | collective-permute-done | bytes 524320 | tf_op jit(solution)/shard_map/ppermute | solution.py:33
  84.0 0.5 collective-permute-done.3.refs_1_
  84.6 0.7 copy-done.7
  85.3 1.5 copy-done
  86.8 0.9 copy-done.4
  87.7 0.9 copy-done.6
  88.7 0.9 copy-done.8
  89.6 9.7 %project.3 = bf16[4,256,896]{2,1,0:T(8,128)(2,1)S(1)} custom-call(s32[3]{0:T(128)S(1)} %pad_add_fusion.place, bf16[256,1024]{1,0:T(8,128)(2,1)S(1)} %attend.1.refs_0_, bf16[256,1024]{1,0:T(8,128)(2,1)S(1)} %collective-permute-done.3.refs_1_, bf16[256,1024]{1,0:T(8,128)(2,1)S(1)} %collective-permute-done.4.refs_2_, ...), custom_call_target="tpu_custom_call" | custom-call | flops 1879048192 | bytes 8388608 | tf_op jit(solution)/shard_map/project/pallas_call | solution.py:226
  99.3 1.9 %collective-permute-start.14 = (bf16[4,256,896]{2,1,0:T(8,128)(2,1)S(1)}, bf16[4,256,896]{2,1,0:T(8,128)(2,1)S(1)}, u32[]{:S(2)}, u32[]{:S(2)}) collective-permute-start(bf16[4,256,896]{2,1,0:T(8,128)(2,1)S(1)} %project.3), channel_id=1, source_target_pairs={{0,2},{1,3},{2,0},{3,1},{4,6},{5,7},{6,4},{7,5},{8,10},{9,11},{10,... | collective-permute-start | bytes 5505032 | tf_op jit(solution)/shard_map/ppermute | solution.py:33
  101.2 9.8 %project.2 = f32[4,256,896]{2,1,0:T(8,128)S(1)} custom-call(s32[3]{0:T(128)S(1)} %pad_add_fusion.place, bf16[256,1024]{1,0:T(8,128)(2,1)S(1)} %attend.1.refs_0_, bf16[256,1024]{1,0:T(8,128)(2,1)S(1)} %collective-permute-done.3.refs_1_, bf16[256,1024]{1,0:T(8,128)(2,1)S(1)} %collective-permute-done.4.refs_2_, ...), custom_call_target="tpu_custom_call" | custom-call | flops 1879048192 | bytes 8388608 | tf_op jit(solution)/shard_map/project/pallas_call | solution.py:226
  111.0 0.5 fusion.24
  111.6 1.2 collective-permute-start.15
  112.8 2.5 %collective-permute-start.17 = (bf16[256,896]{1,0:T(8,128)(2,1)S(1)}, bf16[256,896]{1,0:T(8,128)(2,1)S(1)}, u32[]{:S(2)}, u32[]{:S(2)}) collective-permute-start(bf16[256,896]{1,0:T(8,128)(2,1)S(1)} %get-tuple-element.16), channel_id=1, source_target_pairs={{0,8},{1,9},{2,10},{3,11},{4,12},{5,13},{6,14},{7,15},{8,0},{9,1},... | collective-permute-start | bytes 1376264 | tf_op jit(solution)/shard_map/ppermute | solution.py:33
  115.4 1.2 collective-permute-start.16
  116.5 8.4 %collective-permute-done.15 = bf16[256,896]{1,0:T(8,128)(2,1)S(1)} collective-permute-done((bf16[256,896]{1,0:T(8,128)(2,1)S(1)}, bf16[256,896]{1,0:T(8,128)(2,1)S(1)}, u32[]{:S(2)}, u32[]{:S(2)}) %collective-permute-start.15) | collective-permute-done | bytes 458784 | tf_op jit(solution)/shard_map/ppermute | solution.py:33
  125.0 10.8 %collective-permute-done.17 = bf16[256,896]{1,0:T(8,128)(2,1)S(1)} collective-permute-done((bf16[256,896]{1,0:T(8,128)(2,1)S(1)}, bf16[256,896]{1,0:T(8,128)(2,1)S(1)}, u32[]{:S(2)}, u32[]{:S(2)}) %collective-permute-start.17) | collective-permute-done | bytes 458784 | tf_op jit(solution)/shard_map/ppermute | solution.py:33
  136.2 5.6 %collective-permute-start.18 = (bf16[256,448]{1,0:T(8,128)(2,1)S(1)}, bf16[256,448]{1,0:T(8,128)(2,1)S(1)}, u32[]{:S(2)}, u32[]{:S(2)}) collective-permute-start(bf16[256,448]{1,0:T(8,128)(2,1)S(1)} %get-tuple-element.20), channel_id=1, source_target_pairs={{0,0},{1,1},{2,128},{3,129},{4,4},{5,5},{6,132},{7,133},{8,8},{9,9... | collective-permute-start | bytes 688136 | tf_op jit(solution)/shard_map/ppermute | solution.py:33
  141.9 3.8 %collective-permute-done.18 = bf16[256,448]{1,0:T(8,128)(2,1)S(1)} collective-permute-done((bf16[256,448]{1,0:T(8,128)(2,1)S(1)}, bf16[256,448]{1,0:T(8,128)(2,1)S(1)}, u32[]{:S(2)}, u32[]{:S(2)}) %collective-permute-start.18) | collective-permute-done | bytes 229408 | tf_op jit(solution)/shard_map/ppermute | solution.py:33
  145.7 2.6 %collective-permute-done.19 = bf16[256,448]{1,0:T(8,128)(2,1)S(1)} collective-permute-done((bf16[256,448]{1,0:T(8,128)(2,1)S(1)}, bf16[256,448]{1,0:T(8,128)(2,1)S(1)}, u32[]{:S(2)}, u32[]{:S(2)}) %collective-permute-start.19) | collective-permute-done | bytes 229408 | tf_op jit(solution)/shard_map/ppermute | solution.py:33
  148.4 0.9 pad_maximum_fusion
  (43 shorter events, 1.1 us)
Async XLA Ops:
  6.5 78.8 %all-gather.3.cloned.1.call-start = ((), (), s32[]{:S(2)}) async-start(), calls=%async_computation | async-start | bytes 2064384 | tf_op jit(solution)/shard_map/all_gather | solution.py:275
  9.5 18.0 %copy-start.2 = (bf16[8,128,512]{2,1,0:T(8,128)(2,1)S(1)}, bf16[8,128,512]{2,1,0:T(8,128)(2,1)}, u32[]{:S(2)}) copy-start(bf16[8,128,512]{2,1,0:T(8,128)(2,1)} %w_key_up.1) | copy-start | bytes 3145732
  9.5 18.0 %copy-start.9 = (bf16[256,1536]{1,0:T(8,128)(2,1)S(1)}, bf16[256,1536]{1,0:T(8,128)(2,1)}, u32[]{:S(2)}) copy-start(bf16[256,1536]{1,0:T(8,128)(2,1)} %rows.1) | copy-start | bytes 2359300
  11.5 20.7 %collective-permute-start.1 = (bf16[128,576]{1,0:T(8,128)(2,1)}, bf16[128,576]{1,0:T(8,128)(2,1)}, u32[]{:S(2)}, u32[]{:S(2)}) collective-permute-start(bf16[128,576]{1,0:T(8,128)(2,1)} %constant_dynamic-slice_fusion), channel_id=1, source_target_pairs={{0,32},{16,48},{32,64},{48,80},{64,96},{80,112},{96,128},{112,144}... | collective-permute-start | bytes 442376 | tf_op jit(solution)/shard_map/ppermute | solution.py:271
  17.9 14.3 %collective-permute-start = (bf16[128,576]{1,0:T(8,128)(2,1)}, bf16[128,576]{1,0:T(8,128)(2,1)}, u32[]{:S(2)}, u32[]{:S(2)}) collective-permute-start(bf16[128,576]{1,0:T(8,128)(2,1)} %constant_dynamic-slice_fusion), channel_id=1, source_target_pairs={{0,16},{16,32},{32,48},{48,64},{64,80},{80,96},{96,112},{112,128},... | collective-permute-start | bytes 442376 | tf_op jit(solution)/shard_map/ppermute | solution.py:271
  22.1 12.9 %collective-permute-start.6 = (bf16[64,1792]{1,0:T(8,128)(2,1)}, bf16[64,1792]{1,0:T(8,128)(2,1)S(1)}, u32[]{:S(2)}, u32[]{:S(2)}) collective-permute-start(bf16[64,1792]{1,0:T(8,128)(2,1)} %get-tuple-element.12), channel_id=1, source_target_pairs={{0,129},{1,128},{2,131},{3,130},{4,133},{5,132},{6,135},{7,134},{8... | collective-permute-start | bytes 688136 | tf_op jit(solution)/shard_map/ppermute | solution.py:33
  27.5 2.3 %copy-start.1 = (bf16[1536,1536]{1,0:T(8,128)(2,1)S(1)}, bf16[1536,1536]{1,0:T(8,128)(2,1)}, u32[]{:S(2)}) copy-start(bf16[1536,1536]{1,0:T(8,128)(2,1)} %w_query.1) | copy-start | bytes 14155780
  32.2 18.9 %copy-start.10 = (bf16[8,512,128]{2,1,0:T(8,128)(2,1)S(1)}, bf16[8,512,128]{2,1,0:T(8,128)(2,1)}, u32[]{:S(2)}) copy-start(bf16[8,512,128]{2,1,0:T(8,128)(2,1)} %w_value_up.1) | copy-start | bytes 3145732
  33.3 4.8 %collective-permute-start.2 = (bf16[256,576]{1,0:T(8,128)(2,1)S(1)}, bf16[256,576]{1,0:T(8,128)(2,1)S(1)}, u32[]{:S(2)}, u32[]{:S(2)}) collective-permute-start(bf16[256,576]{1,0:T(8,128)(2,1)S(1)} %pad_maximum_fusion.2), channel_id=1, source_target_pairs={{0,2},{1,3},{2,0},{3,1},{4,6},{5,7},{6,4},{7,5},{8,10},{9,11},{10,... | collective-permute-start | bytes 884744 | tf_op jit(solution)/shard_map/ppermute | solution.py:33
  35.0 13.3 %collective-permute-start.10 = (bf16[64,1792]{1,0:T(8,128)(2,1)S(1)}, bf16[64,1792]{1,0:T(8,128)(2,1)S(1)}, u32[]{:S(2)}, u32[]{:S(2)}) collective-permute-start(bf16[64,1792]{1,0:T(8,128)(2,1)S(1)} %collective-permute-done.6.refs_5_), channel_id=1, source_target_pairs={{0,16},{1,17},{2,18},{3,19},{4,20},{5,21},{6,22},{7,23},{8,24},{9,... | collective-permute-start | bytes 688136 | tf_op jit(solution)/shard_map/ppermute | solution.py:33
  38.1 24.1 %collective-permute-start.7 = (bf16[64,1792]{1,0:T(8,128)(2,1)S(1)}, bf16[64,1792]{1,0:T(8,128)(2,1)S(1)}, u32[]{:S(2)}, u32[]{:S(2)}) collective-permute-start(bf16[64,1792]{1,0:T(8,128)(2,1)S(1)} %collective-permute-done.6.refs_5_), channel_id=1, source_target_pairs={{0,112},{1,113},{2,114},{3,115},{4,116},{5,117},{6,118},{7,119},{8... | collective-permute-start | bytes 688136 | tf_op jit(solution)/shard_map/ppermute | solution.py:33
  48.3 16.5 %collective-permute-start.11 = (bf16[64,1792]{1,0:T(8,128)(2,1)S(1)}, bf16[64,1792]{1,0:T(8,128)(2,1)S(1)}, u32[]{:S(2)}, u32[]{:S(2)}) collective-permute-start(bf16[64,1792]{1,0:T(8,128)(2,1)S(1)} %collective-permute-done.10.refs_12_), channel_id=1, source_target_pairs={{0,16},{1,17},{2,18},{3,19},{4,20},{5,21},{6,22},{7,23},{8,24},{9,... | collective-permute-start | bytes 688136 | tf_op jit(solution)/shard_map/ppermute | solution.py:33
  58.5 25.5 %collective-permute-start.5 = (bf16[256,1024]{1,0:T(8,128)(2,1)S(1)}, bf16[256,1024]{1,0:T(8,128)(2,1)S(1)}, u32[]{:S(2)}, u32[]{:S(2)}) collective-permute-start(bf16[256,1024]{1,0:T(8,128)(2,1)S(1)} %attend.1.refs_0_), channel_id=1, source_target_pairs={{0,129},{1,128},{2,131},{3,130},{4,133},{5,132},{6,135},{7,134},{8... | collective-permute-start | bytes 1572872 | tf_op jit(solution)/shard_map/ppermute | solution.py:33
  61.5 22.5 %collective-permute-start.4 = (bf16[256,1024]{1,0:T(8,128)(2,1)S(1)}, bf16[256,1024]{1,0:T(8,128)(2,1)S(1)}, u32[]{:S(2)}, u32[]{:S(2)}) collective-permute-start(bf16[256,1024]{1,0:T(8,128)(2,1)S(1)} %attend.1.refs_0_), channel_id=1, source_target_pairs={{0,128},{1,129},{2,130},{3,131},{4,132},{5,133},{6,134},{7,135},{8... | collective-permute-start | bytes 1572872 | tf_op jit(solution)/shard_map/ppermute | solution.py:33
  61.8 22.8 %collective-permute-start.3 = (bf16[256,1024]{1,0:T(8,128)(2,1)S(1)}, bf16[256,1024]{1,0:T(8,128)(2,1)S(1)}, u32[]{:S(2)}, u32[]{:S(2)}) collective-permute-start(bf16[256,1024]{1,0:T(8,128)(2,1)S(1)} %attend.1.refs_0_), channel_id=1, source_target_pairs={{0,1},{1,0},{2,3},{3,2},{4,5},{5,4},{6,7},{7,6},{8,9},{9,8},{10,11... | collective-permute-start | bytes 1572872 | tf_op jit(solution)/shard_map/ppermute | solution.py:33
  62.2 6.2 %collective-permute-start.8 = (bf16[64,1792]{1,0:T(8,128)(2,1)S(1)}, bf16[64,1792]{1,0:T(8,128)(2,1)S(1)}, u32[]{:S(2)}, u32[]{:S(2)}) collective-permute-start(bf16[64,1792]{1,0:T(8,128)(2,1)S(1)} %collective-permute-done.7.refs_6_), channel_id=1, source_target_pairs={{0,112},{1,113},{2,114},{3,115},{4,116},{5,117},{6,118},{7,119},{8... | collective-permute-start | bytes 688136 | tf_op jit(solution)/shard_map/ppermute | solution.py:33
  64.9 6.9 %collective-permute-start.12 = (bf16[64,1792]{1,0:T(8,128)(2,1)S(1)}, bf16[64,1792]{1,0:T(8,128)(2,1)S(1)}, u32[]{:S(2)}, u32[]{:S(2)}) collective-permute-start(bf16[64,1792]{1,0:T(8,128)(2,1)S(1)} %collective-permute-done.11.refs_11_), channel_id=1, source_target_pairs={{0,16},{1,17},{2,18},{3,19},{4,20},{5,21},{6,22},{7,23},{8,24},{9,... | collective-permute-start | bytes 688136 | tf_op jit(solution)/shard_map/ppermute | solution.py:33
  68.4 6.3 %collective-permute-start.9 = (bf16[64,1792]{1,0:T(8,128)(2,1)S(1)}, bf16[64,1792]{1,0:T(8,128)(2,1)S(1)}, u32[]{:S(2)}, u32[]{:S(2)}) collective-permute-start(bf16[64,1792]{1,0:T(8,128)(2,1)S(1)} %collective-permute-done.8.refs_7_), channel_id=1, source_target_pairs={{0,112},{1,113},{2,114},{3,115},{4,116},{5,117},{6,118},{7,119},{8... | collective-permute-start | bytes 688136 | tf_op jit(solution)/shard_map/ppermute | solution.py:33
  71.7 12.9 %collective-permute-start.13 = (bf16[64,1792]{1,0:T(8,128)(2,1)S(1)}, bf16[64,1792]{1,0:T(8,128)(2,1)S(1)}, u32[]{:S(2)}, u32[]{:S(2)}) collective-permute-start(bf16[64,1792]{1,0:T(8,128)(2,1)S(1)} %collective-permute-done.12.refs_10_), channel_id=1, source_target_pairs={{0,16},{1,17},{2,18},{3,19},{4,20},{5,21},{6,22},{7,23},{8,24},{9,... | collective-permute-start | bytes 688136 | tf_op jit(solution)/shard_map/ppermute | solution.py:33
  71.7 0.7 copy-start.3
  74.7 0.7 copy-start.5
  84.6 0.7 copy-start.7
  85.3 1.5 copy-start
  86.8 0.9 copy-start.4
  87.7 0.9 copy-start.6
  88.7 0.9 copy-start.8
  99.3 11.7 %collective-permute-start.14 = (bf16[4,256,896]{2,1,0:T(8,128)(2,1)S(1)}, bf16[4,256,896]{2,1,0:T(8,128)(2,1)S(1)}, u32[]{:S(2)}, u32[]{:S(2)}) collective-permute-start(bf16[4,256,896]{2,1,0:T(8,128)(2,1)S(1)} %project.3), channel_id=1, source_target_pairs={{0,2},{1,3},{2,0},{3,1},{4,6},{5,7},{6,4},{7,5},{8,10},{9,11},{10,... | collective-permute-start | bytes 5505032 | tf_op jit(solution)/shard_map/ppermute | solution.py:33
  111.6 13.4 %collective-permute-start.15 = (bf16[256,896]{1,0:T(8,128)(2,1)S(1)}, bf16[256,896]{1,0:T(8,128)(2,1)S(1)}, u32[]{:S(2)}, u32[]{:S(2)}) collective-permute-start(bf16[256,896]{1,0:T(8,128)(2,1)S(1)} %get-tuple-element.15), channel_id=1, source_target_pairs={{0,4},{1,5},{2,6},{3,7},{4,8},{5,9},{6,10},{7,11},{8,12},{9,13},{1... | collective-permute-start | bytes 1376264 | tf_op jit(solution)/shard_map/ppermute | solution.py:33
  112.8 23.0 %collective-permute-start.17 = (bf16[256,896]{1,0:T(8,128)(2,1)S(1)}, bf16[256,896]{1,0:T(8,128)(2,1)S(1)}, u32[]{:S(2)}, u32[]{:S(2)}) collective-permute-start(bf16[256,896]{1,0:T(8,128)(2,1)S(1)} %get-tuple-element.16), channel_id=1, source_target_pairs={{0,8},{1,9},{2,10},{3,11},{4,12},{5,13},{6,14},{7,15},{8,0},{9,1},... | collective-permute-start | bytes 1376264 | tf_op jit(solution)/shard_map/ppermute | solution.py:33
  115.4 20.5 %collective-permute-start.16 = (bf16[256,896]{1,0:T(8,128)(2,1)S(1)}, bf16[256,896]{1,0:T(8,128)(2,1)S(1)}, u32[]{:S(2)}, u32[]{:S(2)}) collective-permute-start(bf16[256,896]{1,0:T(8,128)(2,1)S(1)} %get-tuple-element.17), channel_id=1, source_target_pairs={{0,12},{1,13},{2,14},{3,15},{4,0},{5,1},{6,2},{7,3},{8,4},{9,5},{1... | collective-permute-start | bytes 1376264 | tf_op jit(solution)/shard_map/ppermute | solution.py:33
  136.2 9.5 %collective-permute-start.18 = (bf16[256,448]{1,0:T(8,128)(2,1)S(1)}, bf16[256,448]{1,0:T(8,128)(2,1)S(1)}, u32[]{:S(2)}, u32[]{:S(2)}) collective-permute-start(bf16[256,448]{1,0:T(8,128)(2,1)S(1)} %get-tuple-element.20), channel_id=1, source_target_pairs={{0,0},{1,1},{2,128},{3,129},{4,4},{5,5},{6,132},{7,133},{8,8},{9,9... | collective-permute-start | bytes 688136 | tf_op jit(solution)/shard_map/ppermute | solution.py:33
  141.8 6.5 %collective-permute-start.19 = (bf16[256,448]{1,0:T(8,128)(2,1)S(1)}, bf16[256,448]{1,0:T(8,128)(2,1)S(1)}, u32[]{:S(2)}, u32[]{:S(2)}) collective-permute-start(bf16[256,448]{1,0:T(8,128)(2,1)S(1)} %get-tuple-element.21), channel_id=1, source_target_pairs={{0,1},{1,0},{2,129},{3,128},{4,5},{5,4},{6,133},{7,132},{8,9},{9,8... | collective-permute-start | bytes 688136 | tf_op jit(solution)/shard_map/ppermute | solution.py:33
Sparse Core Ops, SparseCore 0:
  9.6 50.2 all-gather.2

commit v4 on v3

v4 whole, which is shorter than its diff:
```python
import functools

import jax
import jax.numpy as jnp
from jax import lax
from jax.experimental import pallas as pl
from jax.experimental.pallas import tpu as pltpu
from jax.sharding import Mesh
from jax.sharding import PartitionSpec as P

AXES = ("yh", "z", "x", "c", "yl")
SIZES = (2, 8, 4, 2, 2)
CTX = ("yh", "z")
HEAD = ("x", "c")
BF = jnp.bfloat16
F32 = jnp.float32
VMEM = pltpu.MemorySpace.VMEM


def number_of(yh, z, x, c, yl):
    return (((yh * 8 + z) * 4 + x) * 2 + c) * 2 + yl


def moved(a, target):
    pairs = []
    for yh in range(2):
        for z in range(8):
            for x in range(4):
                for c in range(2):
                    for yl in range(2):
                        t = target(yh, z, x, c, yl)
                        pairs.append((number_of(yh, z, x, c, yl), number_of(*t)))
    return lax.ppermute(a, AXES, pairs)


def up_z(a):
    return moved(a, lambda yh, z, x, c, yl: (yh, (z + 1) % 8, x, c, yl))


def down_z(a):
    return moved(a, lambda yh, z, x, c, yl: (yh, (z - 1) % 8, x, c, yl))


def xor_y(a, q):
    return moved(a, lambda yh, z, x, c, yl: (yh ^ (q >> 1), z, x, c, yl ^ (q & 1)))


def other_core(a):
    return moved(a, lambda yh, z, x, c, yl: (yh, z, x, 1 - c, yl))


def along_x(a, d):
    return moved(a, lambda yh, z, x, c, yl: (yh, z, (x + d) % 4, c, yl))


def home(a, r):
    return moved(a, lambda yh, z, x, c, yl: (yh ^ c, z, x, yh, yl ^ r))


def queries_kernel(rows, w_query, w_key_up, turn, out, held, sem):
    copies = [
        pltpu.make_async_copy(w_query.at[:, pl.ds(768 * part, 768)], held.at[part], sem.at[part])
        for part in range(2)
    ]
    for copy in copies:
        copy.start()
    cosine, sine = turn[512:, :64], turn[512:, 64:]
    for part in range(2):
        copies[part].wait()
        queries = jnp.dot(rows[...], held[part], preferred_element_type=F32).astype(BF)
        for i in range(4):
            h = 4 * part + i
            plain = queries[:, 192 * i : 192 * i + 128]
            lat = jnp.dot(plain, w_key_up[h], preferred_element_type=F32)
            rot = queries[:, 192 * i + 128 : 192 * i + 192].astype(F32)
            other = jnp.concatenate([rot[:, 32:], rot[:, :32]], 1)
            rot = rot * cosine + other * sine
            tokens = slice(256 * h, 256 * h + 256)
            out[tokens, :512] = lat.astype(BF)
            out[tokens, 512:] = jnp.concatenate([rot, jnp.zeros_like(rot)], 1).astype(BF)


def keys_kernel(start, own, near, far, swapped, cache, turn, keys, hidden, raw, sem):
    c = lax.axis_index("c")
    slab = 8 * lax.axis_index("yh") + lax.axis_index("z")

    def at(row, rows):
        return raw.at[pl.ds(pl.multiple_of(row, 128), rows)]

    copies = [
        pltpu.make_async_copy(own, at(512, 256), sem.at[0]),
        pltpu.make_async_copy(near, at(256 + 128 * c, 128), sem.at[1]),
        pltpu.make_async_copy(swapped.at[pl.ds(0, 128)], at(384 - 128 * c, 128), sem.at[2]),
        pltpu.make_async_copy(far, at(128 * c, 128), sem.at[3]),
        pltpu.make_async_copy(swapped.at[pl.ds(128, 128)], at(128 - 128 * c, 128), sem.at[4]),
    ]
    for copy in copies:
        copy.start()
    row = lax.broadcasted_iota(jnp.int32, (256, 768), 0)
    col = lax.broadcasted_iota(jnp.int32, (256, 768), 1)
    relative = col - 512 - row
    visible = (relative <= 0) & (relative > -512) & (slab * 256 + col - 512 >= -start[0])
    hidden[...] = jnp.where(visible, 0.0, -1e30)
    for copy in copies:
        copy.wait()
    rot = raw[:, 512:].astype(F32)
    other = jnp.concatenate([rot[:, 32:], rot[:, :32]], 1)
    rot = rot * turn[:, :64] + other * turn[:, 64:]
    keys[:, :512] = raw[:, :512]
    keys[:, 512:] = jnp.concatenate([rot, jnp.zeros_like(rot)], 1).astype(BF)

    @pl.when(slab < 2)
    def _():
        copy = pltpu.make_async_copy(cache, at(0, 512), sem.at[0])
        copy.start()
        copy.wait()

    @pl.when(slab == 0)
    def _():
        keys[:512, :576] = raw[:512]

    @pl.when(slab == 1)
    def _():
        keys[:256, :576] = raw[256:512]


def attend_kernel(queries, keys, hidden, w_value_up, reorder, out):
    scale = 192.0**-0.5 * 1.4426950408889634
    latent = keys[:, :512]

    def step(group, carry):
        heads = []
        for pair in range(2):
            first = pl.multiple_of(1024 * group + 512 * pair, 512)
            scores = lax.dot_general(
                queries[pl.ds(first, 512), :],
                keys[...],
                (((1,), (1,)), ((), ())),
                preferred_element_type=F32,
            )
            for i in range(2):
                part = scores[256 * i : 256 * i + 256] * scale + hidden[...]
                top = jnp.max(part, axis=1, keepdims=True)
                powers = jnp.exp2(part - top)
                share = 1.0 / jnp.sum(powers, axis=1, keepdims=True)
                mixed = jnp.dot(powers.astype(BF), latent, preferred_element_type=F32) * share
                attention = jnp.dot(
                    mixed.astype(BF),
                    w_value_up[4 * group + 2 * pair + i],
                    preferred_element_type=F32,
                )
                heads.append(attention.astype(BF))
        rows = jnp.concatenate(heads, 1)
        columns = pl.ds(pl.multiple_of(512 * group, 512), 512)
        out[:, columns] = jnp.dot(rows, reorder[...], preferred_element_type=F32).astype(BF)
        return carry

    lax.fori_loop(0, 2, step, 0)


def turn_of(positions):
    inverse = jnp.power(jnp.float32(10000.0), -jnp.arange(32, dtype=F32) * (2.0 / 64))
    angles = positions.astype(F32)[:, None] * inverse
    cosine, sine = jnp.cos(angles), jnp.sin(angles)
    return jnp.concatenate([cosine, cosine, -sine, sine], 1)


def quarter_kernel(rows, own, other):
    x = lax.axis_index("x")
    for out, flip in ((own, 0), (other, 1)):
        odd = lax.axis_index("yl") ^ flip
        base = 896 * (lax.axis_index("yh") ^ flip) + 384 * odd
        pieces = []
        for d in range(4):
            start = pl.multiple_of(1792 * ((x + d) % 4) + base, 128)
            wide = rows[:, pl.ds(start, 512)]
            pieces.append(jnp.where(odd == 1, wide[:, 64:], wide[:, :448]))
        out[...] = jnp.concatenate(pieces, 1)


def project_kernel(theirs, *refs):
    groups, blocks, (out, rows, total) = refs[:4], refs[4:20], refs[20:]
    first = 2 * (lax.axis_index("c") ^ theirs)
    yh = lax.axis_index("yh")
    for pick in (0, 2):

        @pl.when(first == pick)
        def _():
            for g in range(2):
                for j in range(2):
                    for p in range(2):
                        half = pl.ds(pl.multiple_of(512 * g + 256 * (yh ^ p), 256), 256)
                        rows[256 * j : 256 * j + 256, 512 * g + 256 * p : 512 * g + 256 * p + 256] = (
                            groups[pick + j][:, half]
                        )

    for n in range(7):
        columns = slice(256 * n, 256 * n + 256)
        weights = jnp.concatenate(
            [
                block[32 * g : 32 * g + 32, columns]
                for g in range(2)
                for block in blocks
            ],
            0,
        )
        total[:, columns] = jnp.dot(rows[...], weights, preferred_element_type=F32)
    for d in range(4):
        span = slice(448 * d, 448 * d + 448)
        for j in range(2):
            top = total[256 * j : 256 * j + 128, span]
            low = total[256 * j + 128 : 256 * j + 256, span]
            out[d, 128 * j : 128 * j + 128] = jnp.concatenate([top, low], 1).astype(out.dtype)


def whole(n):
    return [pl.BlockSpec(memory_space=VMEM)] * n


def placed(n):
    return [pl.BlockSpec(memory_space=pl.ANY)] * n


def scalars(n=1):
    return [pl.BlockSpec(memory_space=pltpu.MemorySpace.SMEM)] * n


def quarters(rows):
    return pl.pallas_call(
        quarter_kernel,
        out_shape=[jax.ShapeDtypeStruct((64, 1792), BF)] * 2,
        in_specs=whole(1),
        out_specs=whole(2),
        name="quarters",
        cost_estimate=pl.CostEstimate(flops=0, bytes_accessed=2 << 20, transcendentals=0),
    )(rows)


def call(kernel, shapes, specs, args, name, flops, moved_bytes, room, scratch=()):
    many = isinstance(shapes, list)
    return pl.pallas_call(
        kernel,
        out_shape=shapes,
        in_specs=specs,
        out_specs=whole(len(shapes)) if many else whole(1)[0],
        scratch_shapes=list(scratch),
        compiler_params=pltpu.CompilerParams(vmem_limit_bytes=room << 20),
        name=name,
        cost_estimate=pl.CostEstimate(
            flops=flops, bytes_accessed=moved_bytes, transcendentals=0
        ),
    )(*args)


def array(shape, kind=BF):
    return jax.ShapeDtypeStruct(shape, kind)


def after(value, *others):
    return lax.optimization_barrier((value, *others))[0]


def project(theirs, groups, blocks, kind):
    return call(
        functools.partial(project_kernel, theirs),
        array((4, 256, 896), kind),
        whole(20),
        (*groups, *blocks),
        "project",
        2 * 512 * 1024 * 1792,
        8 << 20,
        12,
        [pltpu.VMEM((512, 1024), BF), pltpu.VMEM((512, 1792), F32)],
    )


def local(query_latent, key_rows, key_cache, prompt_start, w_query, w_key_up, w_value_up, w_output):
    yh, z, x, c, yl = (lax.axis_index(a) for a in AXES)
    slab = 8 * yh + z
    own, given = quarters(w_output.reshape(64, 7168))
    other = xor_y(given, 3)
    ups, downs = [up_z(own)], [down_z(own)]

    half = lax.dynamic_slice_in_dim(key_rows, 128 * c, 128, 0)
    near, far = (
        lax.ppermute(half, CTX, [(i, i + by) for i in range(16 - by)]) for by in (1, 2)
    )
    turn = turn_of(slab * 256 + jnp.arange(768, dtype=jnp.int32) - 512)
    queries = call(
        queries_kernel,
        array((2048, 640)),
        whole(1) + placed(1) + whole(2),
        (query_latent, w_query, w_key_up, turn),
        "queries",
        2 * 256 * 1536 * 1536 + 2 * 2048 * 128 * 512,
        8 << 20,
        14,
        [pltpu.VMEM((2, 1536, 768), BF), pltpu.SemaphoreType.DMA((2,))],
    )
    swapped = other_core(jnp.concatenate([near, far], 0))
    ups.append(up_z(after(ups[0], queries)))
    downs.append(down_z(after(downs[0], queries)))
    ups_other, downs_other = [up_z(other)], [down_z(other)]

    keys, hidden = call(
        keys_kernel,
        [array((768, 640)), array((256, 768), F32)],
        scalars() + placed(5) + whole(1),
        (prompt_start, key_rows, near, far, swapped, key_cache, turn),
        "keys",
        768 * 640 * 8,
        4 << 20,
        8,
        [pltpu.VMEM((768, 576), BF), pltpu.SemaphoreType.DMA((5,))],
    )
    column = jnp.arange(512, dtype=jnp.int32)
    source = (
        (column // 8 % 4) * 128 + (column // 256) * 64 + ((z + column // 32) % 8) * 8 + column % 8
    )
    reorder = (column[:, None] == source[None, :]).astype(BF)
    rows = call(
        attend_kernel,
        array((256, 1024)),
        whole(5),
        (queries, keys, hidden, w_value_up, reorder),
        "attend",
        4 * 1024 * 768 * 1152 + 4 * 1024 * 512 * 128,
        9 << 20,
        18,
    )
    groups = [rows] + [xor_y(rows, q) for q in (2, 1, 3)]
    groups = [groups[i] for i in (0, 2, 1, 3)]
    ups.append(up_z(after(ups[1], rows)))
    downs.append(down_z(after(downs[1], rows)))
    ups_other.append(up_z(after(ups_other[0], rows)))
    downs_other.append(down_z(after(downs_other[0], rows)))
    ups.append(up_z(ups[2]))
    ups_other.append(up_z(ups_other[1]))
    downs_other.append(down_z(downs_other[1]))
    downs_other.append(down_z(downs_other[2]))
    blocks = [own, *downs, *ups[::-1], other, *downs_other, *ups_other[::-1]]

    theirs = project(1, groups, blocks, BF)
    first = other_core(theirs[2])
    rest = other_core(jnp.concatenate([theirs[:2], theirs[3:]], 0))
    mine = project(0, groups, blocks, F32)
    sums = [None] * 4
    sums[2] = (mine[2] + first.astype(F32)).astype(BF)
    for i, d in enumerate((0, 1, 3)):
        sums[d] = mine[d] + rest[i].astype(F32)
    passing_up = along_x(sums[2][:128], 1)
    passing_down = along_x(sums[2][128:], 3)
    early_up = along_x(sums[1][128:].astype(BF), 1)
    early_down = along_x(sums[3][:128].astype(BF), 3)
    late_up = along_x((sums[1][:128] + passing_up.astype(F32)).astype(BF), 1)
    late_down = along_x((sums[3][128:] + passing_down.astype(F32)).astype(BF), 3)
    pieces = [
        home((sums[0][:128] + late_up.astype(F32) + early_down.astype(F32)).astype(BF), 0),
        home((sums[0][128:] + early_up.astype(F32) + late_down.astype(F32)).astype(BF), 1),
    ]
    even = yl == 0
    pair = jnp.where(even, pieces[0], pieces[1]), jnp.where(even, pieces[1], pieces[0])
    return jnp.concatenate(
        [jnp.concatenate([p[:, 448 * i : 448 * i + 448] for p in pair], 1) for i in range(2)], 0
    )


def solution(mesh):
    cut = Mesh(mesh.devices.reshape(SIZES), AXES) if hasattr(mesh, "devices") else mesh
    tokens = ("yl", "yh", "z")
    return jax.shard_map(
        local,
        mesh=cut,
        in_specs=(
            P(tokens, None),
            P(tokens, None),
            P("yl", None),
            P("yl"),
            P(None, HEAD),
            P(HEAD, None, None),
            P(HEAD, None, None),
            P(HEAD, CTX, None),
        ),
        out_specs=P(tokens, HEAD),
        check_vma=False,
    )
```

time: 157 us -> 120 us (0.76)
  Pallas kernels: 33 us -> 19.7 us
  between operations: 14.3 us -> 1 us
  waiting for transfers between devices: 49.3 us -> 39.4 us
  starting transfers between devices: 41.6 us -> 49.3 us
  local copies, waits for them, and re-layouts: 12.4 us -> 7.08 us
  other arithmetic: 5.53 us -> 3.7 us
    pallas_call x5, Pallas kernels: 30.7 us -> 17.5 us  [call(): pl.pallas_call(kernel, out_shape=shapes, in_specs=specs, out_specs=whole(...]
    ppermute x18 -> x29, waiting for transfers between devices: 49.3 us -> 39.4 us  [moved(): return lax.ppermute(a, AXES, pairs)]
    ppermute x18 -> x29, starting transfers between devices: 31 us -> 40 us  [moved(): return lax.ppermute(a, AXES, pairs)]
    unnamed x24 -> x12, local copies, waits for them, and re-layouts: 11.4 us -> 6 us
  transfers between devices with their start and end apart: 21 -> 31, of which waited for: 9 -> 16; matrix products, arithmetic and copies ran while one was open for 4% -> 3% of each run, Pallas kernels for 13% -> 14%
where the time goes in v4:
time: 120 us
  starting transfers between devices  49.3 us (41%)
  waiting for transfers between devices  39.4 us (33%)
  Pallas kernels  19.7 us (16%)
  local copies, waits for them, and re-layouts  7.08 us (6%)
  other arithmetic  3.7 us (3%)
    ppermute x29, starting transfers between devices, moved(): return lax.ppermute(a, AXES, pairs)  40 us
    ppermute x29, waiting for transfers between devices, moved(): return lax.ppermute(a, AXES, pairs)  39.4 us
    pallas_call x5, Pallas kernels, call(): pl.pallas_call(kernel, out_shape=shapes, in_specs=specs, out_specs=whole(...  17.5 us
    ppermute x2, starting transfers between devices, local(): lax.ppermute(half, CTX, [(i, i + by) for i in range(16 - by)])  9.27 us
    unnamed x12, local copies, waits for them, and re-layouts  6 us
  transfers between devices with their start and end apart: 31, of which 16 were waited for; matrix products, arithmetic and copies ran while one was open for 3% of the time, Pallas kernels for 14%

profile of v4, /device:TPU:1, one launch (start us, length us, event | category | flops | bytes accessed | tf_op | source)
XLA Modules:
  0.0 120.1 jit_solution(3379355592218740424)
XLA Ops:
  0.0 1.2 copy.14.own
  1.2 0.7 constant_dynamic-slice_fusion
  1.9 5.7 %collective-permute-start.1 = (bf16[128,576]{1,0:T(8,128)(2,1)}, bf16[128,576]{1,0:T(8,128)(2,1)S(1)}, u32[]{:S(2)}, u32[]{:S(2)}) collective-permute-start(bf16[128,576]{1,0:T(8,128)(2,1)} %constant_dynamic-slice_fusion), channel_id=1, source_target_pairs={{0,32},{16,48},{32,64},{48,80},{64,96},{80,112},{96,128},{112,144}... | collective-permute-start | bytes 442376 | tf_op jit(solution)/shard_map/ppermute | solution.py:286
  7.6 3.6 %collective-permute-start = (bf16[128,576]{1,0:T(8,128)(2,1)}, bf16[128,576]{1,0:T(8,128)(2,1)S(1)}, u32[]{:S(2)}, u32[]{:S(2)}) collective-permute-start(bf16[128,576]{1,0:T(8,128)(2,1)} %constant_dynamic-slice_fusion), channel_id=1, source_target_pairs={{0,16},{16,32},{32,48},{48,64},{64,80},{80,96},{96,112},{112,128},... | collective-permute-start | bytes 442376 | tf_op jit(solution)/shard_map/ppermute | solution.py:286
  11.1 2.2 %quarters.1 = (bf16[64,1792]{1,0:T(8,128)(2,1)}, bf16[64,1792]{1,0:T(8,128)(2,1)}) custom-call(bf16[64,7168]{1,0:T(8,128)(2,1)} %bitcast.41), custom_call_target="tpu_custom_call" | custom-call | bytes 2097152 | tf_op jit(solution)/shard_map/quarters/pallas_call | solution.py:229
  13.3 2.8 %collective-permute-start.9 = (bf16[64,1792]{1,0:T(8,128)(2,1)}, bf16[64,1792]{1,0:T(8,128)(2,1)S(1)}, u32[]{:S(2)}, u32[]{:S(2)}) collective-permute-start(bf16[64,1792]{1,0:T(8,128)(2,1)} %get-tuple-element.17.refs_4_), channel_id=1, source_target_pairs={{0,16},{1,17},{2,18},{3,19},{4,20},{5,21},{6,22},{7,23},{8,24},{9,... | collective-permute-start | bytes 688136 | tf_op jit(solution)/shard_map/ppermute | solution.py:33
  16.2 0.8 collective-permute-start.6
  17.0 1.9 %collective-permute-start.13 = (bf16[64,1792]{1,0:T(8,128)(2,1)}, bf16[64,1792]{1,0:T(8,128)(2,1)S(1)}, u32[]{:S(2)}, u32[]{:S(2)}) collective-permute-start(bf16[64,1792]{1,0:T(8,128)(2,1)} %get-tuple-element.22), channel_id=1, source_target_pairs={{0,129},{1,128},{2,131},{3,130},{4,133},{5,132},{6,135},{7,134},{8... | collective-permute-start | bytes 688136 | tf_op jit(solution)/shard_map/ppermute | solution.py:33
  18.9 1.4 %multiply_cosine_fusion = (f32[768,32]{1,0:T(8,128)S(1)}, f32[768,32]{1,0:T(8,128)S(1)}, f32[768,32]{1,0:T(8,128)S(1)}) fusion(f32[768]{0:T(1024)S(1)} %add_convert_fusion, f32[32]{0:T(128)S(1)} %multiply_power_fusion), kind=kLoop, calls=%fused_computation.10 | loop fusion | flops 49152 | bytes 298112 | tf_op jit(solution)/shard_map/cos | solution.py:164
  21.4 1.4 %copy.15.cache = bf16[512,576]{1,0:T(8,128)(2,1)S(1)} copy(bf16[512,576]{0,1:T(8,128)(2,1)} %param.10) | data formatting | bytes 1179648 | tf_op args[2]
  22.8 2.3 %copy-done = bf16[1536,1536]{1,0:T(8,128)(2,1)S(1)} copy-done((bf16[1536,1536]{1,0:T(8,128)(2,1)S(1)}, bf16[1536,1536]{1,0:T(8,128)(2,1)}, u32[]{:S(2)}) %copy-start) | copy-done | bytes 4718616
  25.1 1.1 copy-done.3
  26.3 2.9 %queries.1 = bf16[2048,640]{1,0:T(8,128)(2,1)S(1)} custom-call(bf16[256,1536]{1,0:T(8,128)(2,1)S(1)} %copy-done.3, bf16[1536,1536]{1,0:T(8,128)(2,1)S(1)} %copy-done, bf16[8,128,512]{2,1,0:T(8,128)(2,1)S(1)} %copy-done.1, f32[768,128]{1,0:T(8,128)S(1)} %pad_maximum_fusion.1.turn), custom_call_target="tpu_custom_call" | custom-call | flops 1476395008 | bytes 8388608 | tf_op jit(solution)/shard_map/queries/pallas_call | solution.py:241
  29.3 2.0 %collective-permute-start.2 = (bf16[256,576]{1,0:T(8,128)(2,1)S(1)}, bf16[256,576]{1,0:T(8,128)(2,1)S(1)}, u32[]{:S(2)}, u32[]{:S(2)}) collective-permute-start(bf16[256,576]{1,0:T(8,128)(2,1)S(1)} %pad_maximum_fusion.2), channel_id=1, source_target_pairs={{0,2},{1,3},{2,0},{3,1},{4,6},{5,7},{6,4},{7,5},{8,10},{9,11},{10,... | collective-permute-start | bytes 884744 | tf_op jit(solution)/shard_map/ppermute | solution.py:33
  31.5 1.7 %collective-permute-start.10 = (bf16[64,1792]{1,0:T(8,128)(2,1)S(1)}, bf16[64,1792]{1,0:T(8,128)(2,1)S(1)}, u32[]{:S(2)}, u32[]{:S(2)}) collective-permute-start(bf16[64,1792]{1,0:T(8,128)(2,1)S(1)} %collective-permute-done.9.refs_11_), channel_id=1, source_target_pairs={{0,16},{1,17},{2,18},{3,19},{4,20},{5,21},{6,22},{7,23},{8,24},{9,... | collective-permute-start | bytes 688136 | tf_op jit(solution)/shard_map/ppermute | solution.py:33
  33.2 1.4 %collective-permute-start.18 = (bf16[64,1792]{1,0:T(8,128)(2,1)S(1)}, bf16[64,1792]{1,0:T(8,128)(2,1)S(1)}, u32[]{:S(2)}, u32[]{:S(2)}) collective-permute-start(bf16[64,1792]{1,0:T(8,128)(2,1)S(1)} %collective-permute-done.13.refs_12_), channel_id=1, source_target_pairs={{0,16},{1,17},{2,18},{3,19},{4,20},{5,21},{6,22},{7,23},{8,24},{9,... | collective-permute-start | bytes 688136 | tf_op jit(solution)/shard_map/ppermute | solution.py:33
  34.6 1.3 %collective-permute-start.14 = (bf16[64,1792]{1,0:T(8,128)(2,1)S(1)}, bf16[64,1792]{1,0:T(8,128)(2,1)S(1)}, u32[]{:S(2)}, u32[]{:S(2)}) collective-permute-start(bf16[64,1792]{1,0:T(8,128)(2,1)S(1)} %collective-permute-done.13.refs_12_), channel_id=1, source_target_pairs={{0,112},{1,113},{2,114},{3,115},{4,116},{5,117},{6,118},{7,119},{8... | collective-permute-start | bytes 688136 | tf_op jit(solution)/shard_map/ppermute | solution.py:33
  35.9 1.8 %keys.1 = (bf16[768,640]{1,0:T(8,128)(2,1)S(1)}, f32[256,768]{1,0:T(8,128)S(1)}) custom-call(s32[1]{0:T(128)S(6)} %copy.16.start, bf16[256,576]{1,0:T(8,128)(2,1)S(1)} %copy.14.own, bf16[128,576]{1,0:T(8,128)(2,1)S(1)} %collective-permute-done.near, bf16[128,576]{1,0:T(8,128)(2,1)S(1)} %collective-permute-done.1.far, ...), custom_call_target="tpu_custom_call" | custom-call | flops 3932160 | bytes 4194304 | tf_op jit(solution)/shard_map/keys/pallas_call | solution.py:241
  37.8 7.9 %attend.1.refs_0_ = bf16[256,1024]{1,0:T(8,128)(2,1)S(1)} custom-call(bf16[2048,640]{1,0:T(8,128)(2,1)S(1)} %queries.1, bf16[768,640]{1,0:T(8,128)(2,1)S(1)} %get-tuple-element.15.keys, f32[256,768]{1,0:T(8,128)S(1)} %get-tuple-element.16.hidden, bf16[8,512,128]{2,1,0:T(8,128)(2,1)S(1)} %copy-done.4, bf16[512,512]{1,0:T(8,128)(2,1)S(1)} %fusion.reorder), custom_call_target="tpu_custom_call" | custom-call | flops 3892314112 | bytes 9437184 | tf_op jit(solution)/shard_map/attend/pallas_call | solution.py:241
  45.7 1.4 %collective-permute-start.11 = (bf16[64,1792]{1,0:T(8,128)(2,1)S(1)}, bf16[64,1792]{1,0:T(8,128)(2,1)S(1)}, u32[]{:S(2)}, u32[]{:S(2)}) collective-permute-start(bf16[64,1792]{1,0:T(8,128)(2,1)S(1)} %collective-permute-done.10.refs_10_), channel_id=1, source_target_pairs={{0,16},{1,17},{2,18},{3,19},{4,20},{5,21},{6,22},{7,23},{8,24},{9,... | collective-permute-start | bytes 688136 | tf_op jit(solution)/shard_map/ppermute | solution.py:33
  47.2 1.3 %collective-permute-start.15 = (bf16[64,1792]{1,0:T(8,128)(2,1)S(1)}, bf16[64,1792]{1,0:T(8,128)(2,1)S(1)}, u32[]{:S(2)}, u32[]{:S(2)}) collective-permute-start(bf16[64,1792]{1,0:T(8,128)(2,1)S(1)} %collective-permute-done.14.refs_13_), channel_id=1, source_target_pairs={{0,112},{1,113},{2,114},{3,115},{4,116},{5,117},{6,118},{7,119},{8... | collective-permute-start | bytes 688136 | tf_op jit(solution)/shard_map/ppermute | solution.py:33
  48.7 1.6 %collective-permute-start.5 = (bf16[256,1024]{1,0:T(8,128)(2,1)S(1)}, bf16[256,1024]{1,0:T(8,128)(2,1)S(1)}, u32[]{:S(2)}, u32[]{:S(2)}) collective-permute-start(bf16[256,1024]{1,0:T(8,128)(2,1)S(1)} %attend.1.refs_0_), channel_id=1, source_target_pairs={{0,129},{1,128},{2,131},{3,130},{4,133},{5,132},{6,135},{7,134},{8... | collective-permute-start | bytes 1572872 | tf_op jit(solution)/shard_map/ppermute | solution.py:33
  50.3 1.7 %collective-permute-done.8.refs_7_ = bf16[64,1792]{1,0:T(8,128)(2,1)S(1)} collective-permute-done((bf16[64,1792]{1,0:T(8,128)(2,1)S(1)}, bf16[64,1792]{1,0:T(8,128)(2,1)S(1)}, u32[]{:S(2)}, u32[]{:S(2)}) %collective-permute-start.8) | collective-permute-done | bytes 229408 | tf_op jit(solution)/shard_map/ppermute | solution.py:33
  52.1 1.2 %collective-permute-done.11.refs_9_ = bf16[64,1792]{1,0:T(8,128)(2,1)S(1)} collective-permute-done((bf16[64,1792]{1,0:T(8,128)(2,1)S(1)}, bf16[64,1792]{1,0:T(8,128)(2,1)S(1)}, u32[]{:S(2)}, u32[]{:S(2)}) %collective-permute-start.11) | collective-permute-done | bytes 229408 | tf_op jit(solution)/shard_map/ppermute | solution.py:33
  53.3 3.6 %collective-permute-done.15.refs_14_ = bf16[64,1792]{1,0:T(8,128)(2,1)S(1)} collective-permute-done((bf16[64,1792]{1,0:T(8,128)(2,1)S(1)}, bf16[64,1792]{1,0:T(8,128)(2,1)S(1)}, u32[]{:S(2)}, u32[]{:S(2)}) %collective-permute-start.15) | collective-permute-done | bytes 229408 | tf_op jit(solution)/shard_map/ppermute | solution.py:33
  56.9 1.3 %collective-permute-done.19.refs_18_ = bf16[64,1792]{1,0:T(8,128)(2,1)S(1)} collective-permute-done((bf16[64,1792]{1,0:T(8,128)(2,1)S(1)}, bf16[64,1792]{1,0:T(8,128)(2,1)S(1)}, u32[]{:S(2)}, u32[]{:S(2)}) %collective-permute-start.19) | collective-permute-done | bytes 229408 | tf_op jit(solution)/shard_map/ppermute | solution.py:33
  58.2 1.4 %collective-permute-start.16 = (bf16[64,1792]{1,0:T(8,128)(2,1)S(1)}, bf16[64,1792]{1,0:T(8,128)(2,1)S(1)}, u32[]{:S(2)}, u32[]{:S(2)}) collective-permute-start(bf16[64,1792]{1,0:T(8,128)(2,1)S(1)} %collective-permute-done.15.refs_14_), channel_id=1, source_target_pairs={{0,112},{1,113},{2,114},{3,115},{4,116},{5,117},{6,118},{7,119},{8... | collective-permute-start | bytes 688136 | tf_op jit(solution)/shard_map/ppermute | solution.py:33
  59.6 3.8 %collective-permute-done.12.refs_8_ = bf16[64,1792]{1,0:T(8,128)(2,1)S(1)} collective-permute-done((bf16[64,1792]{1,0:T(8,128)(2,1)S(1)}, bf16[64,1792]{1,0:T(8,128)(2,1)S(1)}, u32[]{:S(2)}, u32[]{:S(2)}) %collective-permute-start.12) | collective-permute-done | bytes 229408 | tf_op jit(solution)/shard_map/ppermute | solution.py:33
  63.5 2.6 %collective-permute-start.17 = (bf16[64,1792]{1,0:T(8,128)(2,1)S(1)}, bf16[64,1792]{1,0:T(8,128)(2,1)S(1)}, u32[]{:S(2)}, u32[]{:S(2)}) collective-permute-start(bf16[64,1792]{1,0:T(8,128)(2,1)S(1)} %collective-permute-done.16.refs_15_), channel_id=1, source_target_pairs={{0,112},{1,113},{2,114},{3,115},{4,116},{5,117},{6,118},{7,119},{8... | collective-permute-start | bytes 688136 | tf_op jit(solution)/shard_map/ppermute | solution.py:33
  66.1 3.7 %collective-permute-done.20.refs_17_ = bf16[64,1792]{1,0:T(8,128)(2,1)S(1)} collective-permute-done((bf16[64,1792]{1,0:T(8,128)(2,1)S(1)}, bf16[64,1792]{1,0:T(8,128)(2,1)S(1)}, u32[]{:S(2)}, u32[]{:S(2)}) %collective-permute-start.20) | collective-permute-done | bytes 229408 | tf_op jit(solution)/shard_map/ppermute | solution.py:33
  69.8 2.7 %collective-permute-done.5.refs_3_ = bf16[256,1024]{1,0:T(8,128)(2,1)S(1)} collective-permute-done((bf16[256,1024]{1,0:T(8,128)(2,1)S(1)}, bf16[256,1024]{1,0:T(8,128)(2,1)S(1)}, u32[]{:S(2)}, u32[]{:S(2)}) %collective-permute-start.5) | collective-permute-done | bytes 524320 | tf_op jit(solution)/shard_map/ppermute | solution.py:33
  72.5 0.7 collective-permute-done.3.refs_1_
  73.2 2.5 %project.3 = bf16[4,256,896]{2,1,0:T(8,128)(2,1)S(1)} custom-call(bf16[256,1024]{1,0:T(8,128)(2,1)S(1)} %attend.1.refs_0_, bf16[256,1024]{1,0:T(8,128)(2,1)S(1)} %collective-permute-done.3.refs_1_, bf16[256,1024]{1,0:T(8,128)(2,1)S(1)} %collective-permute-done.4.refs_2_, bf16[256,1024]{1,0:T(8,128)(2,1)S(1)} %collective-permute-done.5.refs_3_, ...), custom_call_target="tpu_custom_call" | custom-call | flops 1879048192 | bytes 8388608 | tf_op jit(solution)/shard_map/project/pallas_call | solution.py:241
  76.0 4.1 %collective-permute-start.21 = (bf16[3,256,896]{2,1,0:T(8,128)(2,1)S(1)}, bf16[3,256,896]{2,1,0:T(8,128)(2,1)S(1)}, u32[]{:S(2)}, u32[]{:S(2)}) collective-permute-start(bf16[3,256,896]{2,1,0:T(8,128)(2,1)S(1)} %pad_maximum_fusion), channel_id=1, source_target_pairs={{0,2},{1,3},{2,0},{3,1},{4,6},{5,7},{6,4},{7,5},{8,10},{9,11},{10,... | collective-permute-start | bytes 4128776 | tf_op jit(solution)/shard_map/ppermute | solution.py:33
  80.2 2.4 %project.2 = f32[4,256,896]{2,1,0:T(8,128)S(1)} custom-call(bf16[256,1024]{1,0:T(8,128)(2,1)S(1)} %attend.1.refs_0_, bf16[256,1024]{1,0:T(8,128)(2,1)S(1)} %collective-permute-done.3.refs_1_, bf16[256,1024]{1,0:T(8,128)(2,1)S(1)} %collective-permute-done.4.refs_2_, bf16[256,1024]{1,0:T(8,128)(2,1)S(1)} %collective-permute-done.5.refs_3_, ...), custom_call_target="tpu_custom_call" | custom-call | flops 1879048192 | bytes 8388608 | tf_op jit(solution)/shard_map/project/pallas_call | solution.py:241
  82.6 0.9 collective-permute-done.22
  83.7 1.3 %collective-permute-start.23 = (bf16[128,896]{1,0:T(8,128)(2,1)S(1)}, bf16[128,896]{1,0:T(8,128)(2,1)S(1)}, u32[]{:S(2)}, u32[]{:S(2)}) collective-permute-start(bf16[128,896]{1,0:T(8,128)(2,1)S(1)} %get-tuple-element.34), channel_id=1, source_target_pairs={{0,4},{1,5},{2,6},{3,7},{4,8},{5,9},{6,10},{7,11},{8,12},{9,13},{1... | collective-permute-start | bytes 688136 | tf_op jit(solution)/shard_map/ppermute | solution.py:33
  85.0 1.5 %collective-permute-start.28 = (bf16[128,896]{1,0:T(8,128)(2,1)S(1)}, bf16[128,896]{1,0:T(8,128)(2,1)S(1)}, u32[]{:S(2)}, u32[]{:S(2)}) collective-permute-start(bf16[128,896]{1,0:T(8,128)(2,1)S(1)} %get-tuple-element.35), channel_id=1, source_target_pairs={{0,12},{1,13},{2,14},{3,15},{4,0},{5,1},{6,2},{7,3},{8,4},{9,5},{1... | collective-permute-start | bytes 688136 | tf_op jit(solution)/shard_map/ppermute | solution.py:33
  86.7 1.3 %collective-permute-start.25 = (bf16[128,896]{1,0:T(8,128)(2,1)S(1)}, bf16[128,896]{1,0:T(8,128)(2,1)S(1)}, u32[]{:S(2)}, u32[]{:S(2)}) collective-permute-start(bf16[128,896]{1,0:T(8,128)(2,1)S(1)} %fusion.13), channel_id=1, source_target_pairs={{0,12},{1,13},{2,14},{3,15},{4,0},{5,1},{6,2},{7,3},{8,4},{9,5},{1... | collective-permute-start | bytes 688136 | tf_op jit(solution)/shard_map/ppermute | solution.py:33
  88.0 3.4 %collective-permute-done.28 = bf16[128,896]{1,0:T(8,128)(2,1)S(1)} collective-permute-done((bf16[128,896]{1,0:T(8,128)(2,1)S(1)}, bf16[128,896]{1,0:T(8,128)(2,1)S(1)}, u32[]{:S(2)}, u32[]{:S(2)}) %collective-permute-start.28) | collective-permute-done | bytes 229408 | tf_op jit(solution)/shard_map/ppermute | solution.py:33
  91.5 2.8 %collective-permute-start.29 = (bf16[128,896]{1,0:T(8,128)(2,1)S(1)}, bf16[128,896]{1,0:T(8,128)(2,1)S(1)}, u32[]{:S(2)}, u32[]{:S(2)}) collective-permute-start(bf16[128,896]{1,0:T(8,128)(2,1)S(1)} %fusion.4), channel_id=1, source_target_pairs={{0,12},{1,13},{2,14},{3,15},{4,0},{5,1},{6,2},{7,3},{8,4},{9,5},{1... | collective-permute-start | bytes 688136 | tf_op jit(solution)/shard_map/ppermute | solution.py:33
  94.5 1.8 %collective-permute-done.25 = bf16[128,896]{1,0:T(8,128)(2,1)S(1)} collective-permute-done((bf16[128,896]{1,0:T(8,128)(2,1)S(1)}, bf16[128,896]{1,0:T(8,128)(2,1)S(1)}, u32[]{:S(2)}, u32[]{:S(2)}) %collective-permute-start.25) | collective-permute-done | bytes 229408 | tf_op jit(solution)/shard_map/ppermute | solution.py:33
  96.4 4.9 %collective-permute-done.29 = bf16[128,896]{1,0:T(8,128)(2,1)S(1)} collective-permute-done((bf16[128,896]{1,0:T(8,128)(2,1)S(1)}, bf16[128,896]{1,0:T(8,128)(2,1)S(1)}, u32[]{:S(2)}, u32[]{:S(2)}) %collective-permute-start.29) | collective-permute-done | bytes 229408 | tf_op jit(solution)/shard_map/ppermute | solution.py:33
  101.3 3.4 %collective-permute-done.24 = bf16[128,896]{1,0:T(8,128)(2,1)S(1)} collective-permute-done((bf16[128,896]{1,0:T(8,128)(2,1)S(1)}, bf16[128,896]{1,0:T(8,128)(2,1)S(1)}, u32[]{:S(2)}, u32[]{:S(2)}) %collective-permute-start.24) | collective-permute-done | bytes 229408 | tf_op jit(solution)/shard_map/ppermute | solution.py:33
  104.8 8.0 %collective-permute-start.26 = (bf16[128,896]{1,0:T(8,128)(2,1)S(1)}, bf16[128,896]{1,0:T(8,128)(2,1)S(1)}, u32[]{:S(2)}, u32[]{:S(2)}) collective-permute-start(bf16[128,896]{1,0:T(8,128)(2,1)S(1)} %get-tuple-element.30), channel_id=1, source_target_pairs={{0,0},{1,1},{2,128},{3,129},{4,4},{5,5},{6,132},{7,133},{8,8},{9,9... | collective-permute-start | bytes 688136 | tf_op jit(solution)/shard_map/ppermute | solution.py:33
  112.9 2.9 %collective-permute-done.26 = bf16[128,896]{1,0:T(8,128)(2,1)S(1)} collective-permute-done((bf16[128,896]{1,0:T(8,128)(2,1)S(1)}, bf16[128,896]{1,0:T(8,128)(2,1)S(1)}, u32[]{:S(2)}, u32[]{:S(2)}) %collective-permute-start.26) | collective-permute-done | bytes 229408 | tf_op jit(solution)/shard_map/ppermute | solution.py:33
  115.9 3.1 %collective-permute-done.30 = bf16[128,896]{1,0:T(8,128)(2,1)S(1)} collective-permute-done((bf16[128,896]{1,0:T(8,128)(2,1)S(1)}, bf16[128,896]{1,0:T(8,128)(2,1)S(1)}, u32[]{:S(2)}, u32[]{:S(2)}) %collective-permute-start.30) | collective-permute-done | bytes 229408 | tf_op jit(solution)/shard_map/ppermute | solution.py:33
  119.2 0.9 maximum_maximum_fusion
  (54 shorter events, 2.7 us)
Async XLA Ops:
  1.9 27.4 %collective-permute-start.1 = (bf16[128,576]{1,0:T(8,128)(2,1)}, bf16[128,576]{1,0:T(8,128)(2,1)S(1)}, u32[]{:S(2)}, u32[]{:S(2)}) collective-permute-start(bf16[128,576]{1,0:T(8,128)(2,1)} %constant_dynamic-slice_fusion), channel_id=1, source_target_pairs={{0,32},{16,48},{32,64},{48,80},{64,96},{80,112},{96,128},{112,144}... | collective-permute-start | bytes 442376 | tf_op jit(solution)/shard_map/ppermute | solution.py:286
  7.6 21.6 %collective-permute-start = (bf16[128,576]{1,0:T(8,128)(2,1)}, bf16[128,576]{1,0:T(8,128)(2,1)S(1)}, u32[]{:S(2)}, u32[]{:S(2)}) collective-permute-start(bf16[128,576]{1,0:T(8,128)(2,1)} %constant_dynamic-slice_fusion), channel_id=1, source_target_pairs={{0,16},{16,32},{32,48},{48,64},{64,80},{80,96},{96,112},{112,128},... | collective-permute-start | bytes 442376 | tf_op jit(solution)/shard_map/ppermute | solution.py:286
  13.3 18.1 %collective-permute-start.9 = (bf16[64,1792]{1,0:T(8,128)(2,1)}, bf16[64,1792]{1,0:T(8,128)(2,1)S(1)}, u32[]{:S(2)}, u32[]{:S(2)}) collective-permute-start(bf16[64,1792]{1,0:T(8,128)(2,1)} %get-tuple-element.17.refs_4_), channel_id=1, source_target_pairs={{0,16},{1,17},{2,18},{3,19},{4,20},{5,21},{6,22},{7,23},{8,24},{9,... | collective-permute-start | bytes 688136 | tf_op jit(solution)/shard_map/ppermute | solution.py:33
  16.2 15.2 %collective-permute-start.6 = (bf16[64,1792]{1,0:T(8,128)(2,1)}, bf16[64,1792]{1,0:T(8,128)(2,1)S(1)}, u32[]{:S(2)}, u32[]{:S(2)}) collective-permute-start(bf16[64,1792]{1,0:T(8,128)(2,1)} %get-tuple-element.17.refs_4_), channel_id=1, source_target_pairs={{0,112},{1,113},{2,114},{3,115},{4,116},{5,117},{6,118},{7,119},{8... | collective-permute-start | bytes 688136 | tf_op jit(solution)/shard_map/ppermute | solution.py:33
  17.0 16.2 %collective-permute-start.13 = (bf16[64,1792]{1,0:T(8,128)(2,1)}, bf16[64,1792]{1,0:T(8,128)(2,1)S(1)}, u32[]{:S(2)}, u32[]{:S(2)}) collective-permute-start(bf16[64,1792]{1,0:T(8,128)(2,1)} %get-tuple-element.22), channel_id=1, source_target_pairs={{0,129},{1,128},{2,131},{3,130},{4,133},{5,132},{6,135},{7,134},{8... | collective-permute-start | bytes 688136 | tf_op jit(solution)/shard_map/ppermute | solution.py:33
  18.9 3.9 %copy-start.1 = (bf16[8,128,512]{2,1,0:T(8,128)(2,1)S(1)}, bf16[8,128,512]{2,1,0:T(8,128)(2,1)}, u32[]{:S(2)}) copy-start(bf16[8,128,512]{2,1,0:T(8,128)(2,1)} %w_key_up.1) | copy-start | bytes 3145732
  22.8 2.3 %copy-start = (bf16[1536,1536]{1,0:T(8,128)(2,1)S(1)}, bf16[1536,1536]{1,0:T(8,128)(2,1)}, u32[]{:S(2)}) copy-start(bf16[1536,1536]{1,0:T(8,128)(2,1)} %w_query.1) | copy-start | bytes 14155780
  25.1 1.1 copy-start.3
  29.2 8.6 %copy-start.4 = (bf16[8,512,128]{2,1,0:T(8,128)(2,1)S(1)}, bf16[8,512,128]{2,1,0:T(8,128)(2,1)}, u32[]{:S(2)}) copy-start(bf16[8,512,128]{2,1,0:T(8,128)(2,1)} %w_value_up.1) | copy-start | bytes 3145732
  29.3 6.7 %collective-permute-start.2 = (bf16[256,576]{1,0:T(8,128)(2,1)S(1)}, bf16[256,576]{1,0:T(8,128)(2,1)S(1)}, u32[]{:S(2)}, u32[]{:S(2)}) collective-permute-start(bf16[256,576]{1,0:T(8,128)(2,1)S(1)} %pad_maximum_fusion.2), channel_id=1, source_target_pairs={{0,2},{1,3},{2,0},{3,1},{4,6},{5,7},{6,4},{7,5},{8,10},{9,11},{10,... | collective-permute-start | bytes 884744 | tf_op jit(solution)/shard_map/ppermute | solution.py:33
  31.4 14.2 %collective-permute-start.7 = (bf16[64,1792]{1,0:T(8,128)(2,1)S(1)}, bf16[64,1792]{1,0:T(8,128)(2,1)S(1)}, u32[]{:S(2)}, u32[]{:S(2)}) collective-permute-start(bf16[64,1792]{1,0:T(8,128)(2,1)S(1)} %collective-permute-done.6.refs_5_), channel_id=1, source_target_pairs={{0,112},{1,113},{2,114},{3,115},{4,116},{5,117},{6,118},{7,119},{8... | collective-permute-start | bytes 688136 | tf_op jit(solution)/shard_map/ppermute | solution.py:33
  31.5 14.2 %collective-permute-start.10 = (bf16[64,1792]{1,0:T(8,128)(2,1)S(1)}, bf16[64,1792]{1,0:T(8,128)(2,1)S(1)}, u32[]{:S(2)}, u32[]{:S(2)}) collective-permute-start(bf16[64,1792]{1,0:T(8,128)(2,1)S(1)} %collective-permute-done.9.refs_11_), channel_id=1, source_target_pairs={{0,16},{1,17},{2,18},{3,19},{4,20},{5,21},{6,22},{7,23},{8,24},{9,... | collective-permute-start | bytes 688136 | tf_op jit(solution)/shard_map/ppermute | solution.py:33
  33.2 15.3 %collective-permute-start.18 = (bf16[64,1792]{1,0:T(8,128)(2,1)S(1)}, bf16[64,1792]{1,0:T(8,128)(2,1)S(1)}, u32[]{:S(2)}, u32[]{:S(2)}) collective-permute-start(bf16[64,1792]{1,0:T(8,128)(2,1)S(1)} %collective-permute-done.13.refs_12_), channel_id=1, source_target_pairs={{0,16},{1,17},{2,18},{3,19},{4,20},{5,21},{6,22},{7,23},{8,24},{9,... | collective-permute-start | bytes 688136 | tf_op jit(solution)/shard_map/ppermute | solution.py:33
  34.6 12.6 %collective-permute-start.14 = (bf16[64,1792]{1,0:T(8,128)(2,1)S(1)}, bf16[64,1792]{1,0:T(8,128)(2,1)S(1)}, u32[]{:S(2)}, u32[]{:S(2)}) collective-permute-start(bf16[64,1792]{1,0:T(8,128)(2,1)S(1)} %collective-permute-done.13.refs_12_), channel_id=1, source_target_pairs={{0,112},{1,113},{2,114},{3,115},{4,116},{5,117},{6,118},{7,119},{8... | collective-permute-start | bytes 688136 | tf_op jit(solution)/shard_map/ppermute | solution.py:33
  37.8 35.4 %copy-start.2 = (bf16[64,1792]{1,0:T(8,128)(2,1)S(1)}, bf16[64,1792]{1,0:T(8,128)(2,1)}, u32[]{:S(2)}) copy-start(bf16[64,1792]{1,0:T(8,128)(2,1)} %get-tuple-element.17.refs_4_) | copy-start | bytes 688132
  45.6 6.3 %collective-permute-start.8 = (bf16[64,1792]{1,0:T(8,128)(2,1)S(1)}, bf16[64,1792]{1,0:T(8,128)(2,1)S(1)}, u32[]{:S(2)}, u32[]{:S(2)}) collective-permute-start(bf16[64,1792]{1,0:T(8,128)(2,1)S(1)} %collective-permute-done.7.refs_6_), channel_id=1, source_target_pairs={{0,112},{1,113},{2,114},{3,115},{4,116},{5,117},{6,118},{7,119},{8... | collective-permute-start | bytes 688136 | tf_op jit(solution)/shard_map/ppermute | solution.py:33
  45.7 7.5 %collective-permute-start.11 = (bf16[64,1792]{1,0:T(8,128)(2,1)S(1)}, bf16[64,1792]{1,0:T(8,128)(2,1)S(1)}, u32[]{:S(2)}, u32[]{:S(2)}) collective-permute-start(bf16[64,1792]{1,0:T(8,128)(2,1)S(1)} %collective-permute-done.10.refs_10_), channel_id=1, source_target_pairs={{0,16},{1,17},{2,18},{3,19},{4,20},{5,21},{6,22},{7,23},{8,24},{9,... | collective-permute-start | bytes 688136 | tf_op jit(solution)/shard_map/ppermute | solution.py:33
  47.2 9.7 %collective-permute-start.15 = (bf16[64,1792]{1,0:T(8,128)(2,1)S(1)}, bf16[64,1792]{1,0:T(8,128)(2,1)S(1)}, u32[]{:S(2)}, u32[]{:S(2)}) collective-permute-start(bf16[64,1792]{1,0:T(8,128)(2,1)S(1)} %collective-permute-done.14.refs_13_), channel_id=1, source_target_pairs={{0,112},{1,113},{2,114},{3,115},{4,116},{5,117},{6,118},{7,119},{8... | collective-permute-start | bytes 688136 | tf_op jit(solution)/shard_map/ppermute | solution.py:33
  48.5 9.7 %collective-permute-start.19 = (bf16[64,1792]{1,0:T(8,128)(2,1)S(1)}, bf16[64,1792]{1,0:T(8,128)(2,1)S(1)}, u32[]{:S(2)}, u32[]{:S(2)}) collective-permute-start(bf16[64,1792]{1,0:T(8,128)(2,1)S(1)} %collective-permute-done.18.refs_19_), channel_id=1, source_target_pairs={{0,16},{1,17},{2,18},{3,19},{4,20},{5,21},{6,22},{7,23},{8,24},{9,... | collective-permute-start | bytes 688136 | tf_op jit(solution)/shard_map/ppermute | solution.py:33
  48.7 23.9 %collective-permute-start.5 = (bf16[256,1024]{1,0:T(8,128)(2,1)S(1)}, bf16[256,1024]{1,0:T(8,128)(2,1)S(1)}, u32[]{:S(2)}, u32[]{:S(2)}) collective-permute-start(bf16[256,1024]{1,0:T(8,128)(2,1)S(1)} %attend.1.refs_0_), channel_id=1, source_target_pairs={{0,129},{1,128},{2,131},{3,130},{4,133},{5,132},{6,135},{7,134},{8... | collective-permute-start | bytes 1572872 | tf_op jit(solution)/shard_map/ppermute | solution.py:33
  52.0 20.6 %collective-permute-start.4 = (bf16[256,1024]{1,0:T(8,128)(2,1)S(1)}, bf16[256,1024]{1,0:T(8,128)(2,1)S(1)}, u32[]{:S(2)}, u32[]{:S(2)}) collective-permute-start(bf16[256,1024]{1,0:T(8,128)(2,1)S(1)} %attend.1.refs_0_), channel_id=1, source_target_pairs={{0,128},{1,129},{2,130},{3,131},{4,132},{5,133},{6,134},{7,135},{8... | collective-permute-start | bytes 1572872 | tf_op jit(solution)/shard_map/ppermute | solution.py:33
  53.3 19.9 %collective-permute-start.3 = (bf16[256,1024]{1,0:T(8,128)(2,1)S(1)}, bf16[256,1024]{1,0:T(8,128)(2,1)S(1)}, u32[]{:S(2)}, u32[]{:S(2)}) collective-permute-start(bf16[256,1024]{1,0:T(8,128)(2,1)S(1)} %attend.1.refs_0_), channel_id=1, source_target_pairs={{0,1},{1,0},{2,3},{3,2},{4,5},{5,4},{6,7},{7,6},{8,9},{9,8},{10,11... | collective-permute-start | bytes 1572872 | tf_op jit(solution)/shard_map/ppermute | solution.py:33
  56.9 6.5 %collective-permute-start.12 = (bf16[64,1792]{1,0:T(8,128)(2,1)S(1)}, bf16[64,1792]{1,0:T(8,128)(2,1)S(1)}, u32[]{:S(2)}, u32[]{:S(2)}) collective-permute-start(bf16[64,1792]{1,0:T(8,128)(2,1)S(1)} %collective-permute-done.11.refs_9_), channel_id=1, source_target_pairs={{0,16},{1,17},{2,18},{3,19},{4,20},{5,21},{6,22},{7,23},{8,24},{9,... | collective-permute-start | bytes 688136 | tf_op jit(solution)/shard_map/ppermute | solution.py:33
  58.2 5.3 %collective-permute-start.16 = (bf16[64,1792]{1,0:T(8,128)(2,1)S(1)}, bf16[64,1792]{1,0:T(8,128)(2,1)S(1)}, u32[]{:S(2)}, u32[]{:S(2)}) collective-permute-start(bf16[64,1792]{1,0:T(8,128)(2,1)S(1)} %collective-permute-done.15.refs_14_), channel_id=1, source_target_pairs={{0,112},{1,113},{2,114},{3,115},{4,116},{5,117},{6,118},{7,119},{8... | collective-permute-start | bytes 688136 | tf_op jit(solution)/shard_map/ppermute | solution.py:33
  63.4 6.4 %collective-permute-start.20 = (bf16[64,1792]{1,0:T(8,128)(2,1)S(1)}, bf16[64,1792]{1,0:T(8,128)(2,1)S(1)}, u32[]{:S(2)}, u32[]{:S(2)}) collective-permute-start(bf16[64,1792]{1,0:T(8,128)(2,1)S(1)} %collective-permute-done.19.refs_18_), channel_id=1, source_target_pairs={{0,16},{1,17},{2,18},{3,19},{4,20},{5,21},{6,22},{7,23},{8,24},{9,... | collective-permute-start | bytes 688136 | tf_op jit(solution)/shard_map/ppermute | solution.py:33
  63.5 9.7 %collective-permute-start.17 = (bf16[64,1792]{1,0:T(8,128)(2,1)S(1)}, bf16[64,1792]{1,0:T(8,128)(2,1)S(1)}, u32[]{:S(2)}, u32[]{:S(2)}) collective-permute-start(bf16[64,1792]{1,0:T(8,128)(2,1)S(1)} %collective-permute-done.16.refs_15_), channel_id=1, source_target_pairs={{0,112},{1,113},{2,114},{3,115},{4,116},{5,117},{6,118},{7,119},{8... | collective-permute-start | bytes 688136 | tf_op jit(solution)/shard_map/ppermute | solution.py:33
  76.0 10.4 %collective-permute-start.21 = (bf16[3,256,896]{2,1,0:T(8,128)(2,1)S(1)}, bf16[3,256,896]{2,1,0:T(8,128)(2,1)S(1)}, u32[]{:S(2)}, u32[]{:S(2)}) collective-permute-start(bf16[3,256,896]{2,1,0:T(8,128)(2,1)S(1)} %pad_maximum_fusion), channel_id=1, source_target_pairs={{0,2},{1,3},{2,0},{3,1},{4,6},{5,7},{6,4},{7,5},{8,10},{9,11},{10,... | collective-permute-start | bytes 4128776 | tf_op jit(solution)/shard_map/ppermute | solution.py:33
  80.1 3.4 %collective-permute-start.22 = (bf16[256,896]{1,0:T(8,128)(2,1)S(1)}, bf16[256,896]{1,0:T(8,128)(2,1)S(1)}, u32[]{:S(2)}, u32[]{:S(2)}) collective-permute-start(bf16[256,896]{1,0:T(8,128)(2,1)S(1)} %get-tuple-element.28), channel_id=1, source_target_pairs={{0,2},{1,3},{2,0},{3,1},{4,6},{5,7},{6,4},{7,5},{8,10},{9,11},{10,... | collective-permute-start | bytes 1376264 | tf_op jit(solution)/shard_map/ppermute | solution.py:33
  83.7 10.7 %collective-permute-start.23 = (bf16[128,896]{1,0:T(8,128)(2,1)S(1)}, bf16[128,896]{1,0:T(8,128)(2,1)S(1)}, u32[]{:S(2)}, u32[]{:S(2)}) collective-permute-start(bf16[128,896]{1,0:T(8,128)(2,1)S(1)} %get-tuple-element.34), channel_id=1, source_target_pairs={{0,4},{1,5},{2,6},{3,7},{4,8},{5,9},{6,10},{7,11},{8,12},{9,13},{1... | collective-permute-start | bytes 688136 | tf_op jit(solution)/shard_map/ppermute | solution.py:33
  85.0 6.5 %collective-permute-start.28 = (bf16[128,896]{1,0:T(8,128)(2,1)S(1)}, bf16[128,896]{1,0:T(8,128)(2,1)S(1)}, u32[]{:S(2)}, u32[]{:S(2)}) collective-permute-start(bf16[128,896]{1,0:T(8,128)(2,1)S(1)} %get-tuple-element.35), channel_id=1, source_target_pairs={{0,12},{1,13},{2,14},{3,15},{4,0},{5,1},{6,2},{7,3},{8,4},{9,5},{1... | collective-permute-start | bytes 688136 | tf_op jit(solution)/shard_map/ppermute | solution.py:33
  86.7 9.7 %collective-permute-start.25 = (bf16[128,896]{1,0:T(8,128)(2,1)S(1)}, bf16[128,896]{1,0:T(8,128)(2,1)S(1)}, u32[]{:S(2)}, u32[]{:S(2)}) collective-permute-start(bf16[128,896]{1,0:T(8,128)(2,1)S(1)} %fusion.13), channel_id=1, source_target_pairs={{0,12},{1,13},{2,14},{3,15},{4,0},{5,1},{6,2},{7,3},{8,4},{9,5},{1... | collective-permute-start | bytes 688136 | tf_op jit(solution)/shard_map/ppermute | solution.py:33
  91.5 9.8 %collective-permute-start.29 = (bf16[128,896]{1,0:T(8,128)(2,1)S(1)}, bf16[128,896]{1,0:T(8,128)(2,1)S(1)}, u32[]{:S(2)}, u32[]{:S(2)}) collective-permute-start(bf16[128,896]{1,0:T(8,128)(2,1)S(1)} %fusion.4), channel_id=1, source_target_pairs={{0,12},{1,13},{2,14},{3,15},{4,0},{5,1},{6,2},{7,3},{8,4},{9,5},{1... | collective-permute-start | bytes 688136 | tf_op jit(solution)/shard_map/ppermute | solution.py:33
  94.3 7.0 %collective-permute-start.27 = (bf16[128,896]{1,0:T(8,128)(2,1)S(1)}, bf16[128,896]{1,0:T(8,128)(2,1)S(1)}, u32[]{:S(2)}, u32[]{:S(2)}) collective-permute-start(bf16[128,896]{1,0:T(8,128)(2,1)S(1)} %fusion.14), channel_id=1, source_target_pairs={{0,4},{1,5},{2,6},{3,7},{4,8},{5,9},{6,10},{7,11},{8,12},{9,13},{1... | collective-permute-start | bytes 688136 | tf_op jit(solution)/shard_map/ppermute | solution.py:33
  94.4 10.2 %collective-permute-start.24 = (bf16[128,896]{1,0:T(8,128)(2,1)S(1)}, bf16[128,896]{1,0:T(8,128)(2,1)S(1)}, u32[]{:S(2)}, u32[]{:S(2)}) collective-permute-start(bf16[128,896]{1,0:T(8,128)(2,1)S(1)} %fusion.9), channel_id=1, source_target_pairs={{0,4},{1,5},{2,6},{3,7},{4,8},{5,9},{6,10},{7,11},{8,12},{9,13},{1... | collective-permute-start | bytes 688136 | tf_op jit(solution)/shard_map/ppermute | solution.py:33
  104.8 11.0 %collective-permute-start.26 = (bf16[128,896]{1,0:T(8,128)(2,1)S(1)}, bf16[128,896]{1,0:T(8,128)(2,1)S(1)}, u32[]{:S(2)}, u32[]{:S(2)}) collective-permute-start(bf16[128,896]{1,0:T(8,128)(2,1)S(1)} %get-tuple-element.30), channel_id=1, source_target_pairs={{0,0},{1,1},{2,128},{3,129},{4,4},{5,5},{6,132},{7,133},{8,8},{9,9... | collective-permute-start | bytes 688136 | tf_op jit(solution)/shard_map/ppermute | solution.py:33
  112.8 6.2 %collective-permute-start.30 = (bf16[128,896]{1,0:T(8,128)(2,1)S(1)}, bf16[128,896]{1,0:T(8,128)(2,1)S(1)}, u32[]{:S(2)}, u32[]{:S(2)}) collective-permute-start(bf16[128,896]{1,0:T(8,128)(2,1)S(1)} %get-tuple-element.31), channel_id=1, source_target_pairs={{0,1},{1,0},{2,129},{3,128},{4,5},{5,4},{6,133},{7,132},{8,9},{9,8... | collective-permute-start | bytes 688136 | tf_op jit(solution)/shard_map/ppermute | solution.py:33

commit v5 on v4

--- a/solution.py
+++ b/solution.py
@@ -57,30 +57,43 @@
     return moved(a, lambda yh, z, x, c, yl: (yh ^ c, z, x, yh, yl ^ r))
 
 
-def queries_kernel(rows, w_query, w_key_up, turn, out, held, sem):
+def turn_of(table, block):
+    rows = slice(64 * block, 64 * block + 64)
+    return jnp.concatenate([table[rows, 32 * i : 32 * i + 32] for i in range(4)], 0)
+
+
+def turned(rot, cosine, sine):
+    other = jnp.concatenate([rot[:, 32:], rot[:, :32]], 1)
+    cosine = jnp.concatenate([cosine, cosine], 1)
+    sine = jnp.concatenate([-sine, sine], 1)
+    rot = rot * cosine + other * sine
+    return jnp.concatenate([rot, jnp.zeros_like(rot)], 1).astype(BF)
+
+
+def queries_kernel(rows, w_query, w_key_up, cosines, sines, out, held, rows_held, sem):
     copies = [
         pltpu.make_async_copy(w_query.at[:, pl.ds(768 * part, 768)], held.at[part], sem.at[part])
         for part in range(2)
     ]
-    for copy in copies:
-        copy.start()
-    cosine, sine = turn[512:, :64], turn[512:, 64:]
+    copies.append(pltpu.make_async_copy(rows, rows_held, sem.at[2]))
+    for i in (2, 0, 1):
+        copies[i].start()
+    cosine, sine = turn_of(cosines, 2), turn_of(sines, 2)
+    copies[2].wait()
     for part in range(2):
         copies[part].wait()
-        queries = jnp.dot(rows[...], held[part], preferred_element_type=F32).astype(BF)
+        queries = jnp.dot(rows_held[...], held[part], preferred_element_type=F32).astype(BF)
         for i in range(4):
             h = 4 * part + i
             plain = queries[:, 192 * i : 192 * i + 128]
             lat = jnp.dot(plain, w_key_up[h], preferred_element_type=F32)
             rot = queries[:, 192 * i + 128 : 192 * i + 192].astype(F32)
-            other = jnp.concatenate([rot[:, 32:], rot[:, :32]], 1)
-            rot = rot * cosine + other * sine
             tokens = slice(256 * h, 256 * h + 256)
             out[tokens, :512] = lat.astype(BF)
-            out[tokens, 512:] = jnp.concatenate([rot, jnp.zeros_like(rot)], 1).astype(BF)
-
-
-def keys_kernel(start, own, near, far, swapped, cache, turn, keys, hidden, raw, sem):
+            out[tokens, 512:] = turned(rot, cosine, sine)
+
+
+def keys_kernel(start, own, near, far, swapped, cache, cosines, sines, keys, hidden, raw, sem):
     c = lax.axis_index("c")
     slab = 8 * lax.axis_index("yh") + lax.axis_index("z")
 
@@ -103,11 +116,12 @@
     hidden[...] = jnp.where(visible, 0.0, -1e30)
     for copy in copies:
         copy.wait()
-    rot = raw[:, 512:].astype(F32)
-    other = jnp.concatenate([rot[:, 32:], rot[:, :32]], 1)
-    rot = rot * turn[:, :64] + other * turn[:, 64:]
     keys[:, :512] = raw[:, :512]
-    keys[:, 512:] = jnp.concatenate([rot, jnp.zeros_like(rot)], 1).astype(BF)
+    for block in range(3):
+        tokens = slice(256 * block, 256 * block + 256)
+        keys[tokens, 512:] = turned(
+            raw[tokens, 512:].astype(F32), turn_of(cosines, block), turn_of(sines, block)
+        )
 
     @pl.when(slab < 2)
     def _():
@@ -158,11 +172,13 @@
     lax.fori_loop(0, 2, step, 0)
 
 
-def turn_of(positions):
+def turns(first):
     inverse = jnp.power(jnp.float32(10000.0), -jnp.arange(32, dtype=F32) * (2.0 / 64))
-    angles = positions.astype(F32)[:, None] * inverse
-    cosine, sine = jnp.cos(angles), jnp.sin(angles)
-    return jnp.concatenate([cosine, cosine, -sine, sine], 1)
+    row = lax.broadcasted_iota(jnp.int32, (192, 128), 0)
+    lane = lax.broadcasted_iota(jnp.int32, (192, 128), 1)
+    place = first + (row // 64) * 256 + (lane // 32) * 64 + row % 64
+    angles = place.astype(F32) * jnp.tile(inverse, 4)[None, :]
+    return jnp.cos(angles), jnp.sin(angles)
 
 
 def quarter_kernel(rows, own, other):
@@ -179,7 +195,10 @@
 
 
 def project_kernel(theirs, *refs):
-    groups, blocks, (out, rows, total) = refs[:4], refs[4:20], refs[20:]
+    groups, held, (out, rows, total) = refs[:4], refs[4:17], refs[17:]
+    own, d1, d2, d3, u4, u3, u2, u1, other, e1, e3, e4, v1 = held
+    blocks = [own, d1, d2, d3.at[:64], u4.at[:64], u3.at[:64], u2, u1]
+    blocks += [other, e1, d3.at[64:], e3, e4, u4.at[64:], u3.at[64:], v1]
     first = 2 * (lax.axis_index("c") ^ theirs)
     yh = lax.axis_index("yh")
     for pick in (0, 2):
@@ -221,6 +240,10 @@
     return [pl.BlockSpec(memory_space=pl.ANY)] * n
 
 
+def kept(n=1):
+    return [pl.BlockSpec(memory_space=pltpu.MemorySpace.HBM)] * n
+
+
 def scalars(n=1):
     return [pl.BlockSpec(memory_space=pltpu.MemorySpace.SMEM)] * n
 
@@ -264,7 +287,7 @@
     return call(
         functools.partial(project_kernel, theirs),
         array((4, 256, 896), kind),
-        whole(20),
+        whole(17),
         (*groups, *blocks),
         "project",
         2 * 512 * 1024 * 1792,
@@ -279,34 +302,37 @@
     slab = 8 * yh + z
     own, given = quarters(w_output.reshape(64, 7168))
     other = xor_y(given, 3)
-    ups, downs = [up_z(own)], [down_z(own)]
+    u1, d1 = up_z(own), down_z(own)
 
     half = lax.dynamic_slice_in_dim(key_rows, 128 * c, 128, 0)
     near, far = (
         lax.ppermute(half, CTX, [(i, i + by) for i in range(16 - by)]) for by in (1, 2)
     )
-    turn = turn_of(slab * 256 + jnp.arange(768, dtype=jnp.int32) - 512)
+    cosines, sines = turns(slab * 256 - 512)
     queries = call(
         queries_kernel,
         array((2048, 640)),
-        whole(1) + placed(1) + whole(2),
-        (query_latent, w_query, w_key_up, turn),
+        kept(2) + whole(3),
+        (query_latent, w_query, w_key_up, cosines, sines),
         "queries",
         2 * 256 * 1536 * 1536 + 2 * 2048 * 128 * 512,
         8 << 20,
         14,
-        [pltpu.VMEM((2, 1536, 768), BF), pltpu.SemaphoreType.DMA((2,))],
+        [
+            pltpu.VMEM((2, 1536, 768), BF),
+            pltpu.VMEM((256, 1536), BF),
+            pltpu.SemaphoreType.DMA((3,)),
+        ],
     )
     swapped = other_core(jnp.concatenate([near, far], 0))
-    ups.append(up_z(after(ups[0], queries)))
-    downs.append(down_z(after(downs[0], queries)))
-    ups_other, downs_other = [up_z(other)], [down_z(other)]
+    u2, d2 = up_z(after(u1, queries)), down_z(after(d1, queries))
+    v1, e1 = up_z(other), down_z(other)
 
     keys, hidden = call(
         keys_kernel,
         [array((768, 640)), array((256, 768), F32)],
-        scalars() + placed(5) + whole(1),
-        (prompt_start, key_rows, near, far, swapped, key_cache, turn),
+        scalars() + kept() + placed(3) + kept() + whole(2),
+        (prompt_start, key_rows, near, far, swapped, key_cache, cosines, sines),
         "keys",
         768 * 640 * 8,
         4 << 20,
@@ -330,30 +356,25 @@
     )
     groups = [rows] + [xor_y(rows, q) for q in (2, 1, 3)]
     groups = [groups[i] for i in (0, 2, 1, 3)]
-    ups.append(up_z(after(ups[1], rows)))
-    downs.append(down_z(after(downs[1], rows)))
-    ups_other.append(up_z(after(ups_other[0], rows)))
-    downs_other.append(down_z(after(downs_other[0], rows)))
-    ups.append(up_z(ups[2]))
-    ups_other.append(up_z(ups_other[1]))
-    downs_other.append(down_z(downs_other[1]))
-    downs_other.append(down_z(downs_other[2]))
-    blocks = [own, *downs, *ups[::-1], other, *downs_other, *ups_other[::-1]]
-
-    theirs = project(1, groups, blocks, BF)
-    first = other_core(theirs[2])
-    rest = other_core(jnp.concatenate([theirs[:2], theirs[3:]], 0))
+    u3 = up_z(after(jnp.concatenate([u2, v1], 0), rows))
+    d3 = down_z(after(jnp.concatenate([d2, e1], 0), rows))
+    u4 = up_z(u3)
+    e3 = down_z(d3[64:])
+    e4 = down_z(e3)
+    blocks = [own, d1, d2, d3, u4, u3, u2, u1, other, e1, e3, e4, v1]
+
+    theirs = other_core(project(1, groups, blocks, BF))
     mine = project(0, groups, blocks, F32)
-    sums = [None] * 4
-    sums[2] = (mine[2] + first.astype(F32)).astype(BF)
-    for i, d in enumerate((0, 1, 3)):
-        sums[d] = mine[d] + rest[i].astype(F32)
-    passing_up = along_x(sums[2][:128], 1)
-    passing_down = along_x(sums[2][128:], 3)
-    early_up = along_x(sums[1][128:].astype(BF), 1)
-    early_down = along_x(sums[3][:128].astype(BF), 3)
+    far_sum = (mine[2] + theirs[2].astype(F32)).astype(BF)
+    passing_up = along_x(far_sum[:128], 1)
+    passing_down = along_x(far_sum[128:], 3)
+    sums = [mine[d] + theirs[d].astype(F32) for d in (0, 1, 3)]
+    early_up, early_down = lax.optimization_barrier(
+        (sums[1][128:].astype(BF), sums[2][:128].astype(BF))
+    )
+    early_up, early_down = along_x(early_up, 1), along_x(early_down, 3)
     late_up = along_x((sums[1][:128] + passing_up.astype(F32)).astype(BF), 1)
-    late_down = along_x((sums[3][128:] + passing_down.astype(F32)).astype(BF), 3)
+    late_down = along_x((sums[2][128:] + passing_down.astype(F32)).astype(BF), 3)
     pieces = [
         home((sums[0][:128] + late_up.astype(F32) + early_down.astype(F32)).astype(BF), 0),
         home((sums[0][128:] + early_up.astype(F32) + late_down.astype(F32)).astype(BF), 1),

time: 120 us -> 112 us (0.933)
  waiting for transfers between devices: 39.4 us -> 34.2 us
  starting transfers between devices: 49.3 us -> 47.4 us
  other arithmetic: 3.7 us -> 2.28 us
    ppermute x29 -> x25, waiting for transfers between devices: 39.4 us -> 34.2 us  [moved(): return lax.ppermute(a, AXES, pairs)]
    ppermute x29 -> x25, starting transfers between devices: 40 us -> 38.1 us  [moved(): return lax.ppermute(a, AXES, pairs)]
    cos x1 -> x0, other arithmetic: 1.45 us -> none  [turn_of(): cosine, sine = (jnp.cos(angles), jnp.sin(angles))]
  transfers between devices with their start and end apart: 31 -> 27, of which waited for: 16 -> 11; matrix products, arithmetic and copies ran while one was open for 3% -> 2% of each run, Pallas kernels for 14% -> 16%
where the time goes in v5:
time: 112 us; the launch traced here: 111 us
  starting transfers between devices  47.4 us (42%)
  waiting for transfers between devices  34.2 us (31%)
  Pallas kernels  19.8 us (18%)
  local copies, waits for them, and re-layouts  6.52 us (6%)
  other arithmetic  2.28 us (2%)
    ppermute x25, starting transfers between devices, moved(): return lax.ppermute(a, AXES, pairs)  38.1 us
    ppermute x25, waiting for transfers between devices, moved(): return lax.ppermute(a, AXES, pairs)  34.2 us
    pallas_call x5, Pallas kernels, call(): pl.pallas_call(kernel, out_shape=shapes, in_specs=specs, out_specs=whole(...  17.6 us
    ppermute x2, starting transfers between devices, local(): lax.ppermute(half, CTX, [(i, i + by) for i in range(16 - by)])  9.29 us
    unnamed x12, local copies, waits for them, and re-layouts  6.09 us
  transfers between devices with their start and end apart: 27, of which 11 were waited for; matrix products, arithmetic and copies ran while one was open for 2% of the time, Pallas kernels for 16%

profile of v5, /device:TPU:1, one launch (start us, length us, event | category | flops | bytes accessed | tf_op | source)
XLA Modules:
  0.0 111.2 jit_solution(10604078930854766657)
XLA Ops:
  0.0 1.2 %copy.10.own = bf16[256,576]{1,0:T(8,128)(2,1)S(1)} copy(bf16[256,576]{0,1:T(8,128)(2,1)} %param.9) | data formatting | bytes 589824 | tf_op args[1]
  1.3 5.7 %collective-permute-start.1 = (bf16[128,576]{1,0:T(8,128)(2,1)S(1)}, bf16[128,576]{1,0:T(8,128)(2,1)S(1)}, u32[]{:S(2)}, u32[]{:S(2)}) collective-permute-start(bf16[128,576]{1,0:T(8,128)(2,1)S(1)} %constant_dynamic-slice_fusion), channel_id=1, source_target_pairs={{0,32},{16,48},{32,64},{48,80},{64,96},{80,112},{96,128},{112,144}... | collective-permute-start | bytes 442376 | tf_op jit(solution)/shard_map/ppermute | solution.py:309
  7.0 3.6 %collective-permute-start = (bf16[128,576]{1,0:T(8,128)(2,1)S(1)}, bf16[128,576]{1,0:T(8,128)(2,1)S(1)}, u32[]{:S(2)}, u32[]{:S(2)}) collective-permute-start(bf16[128,576]{1,0:T(8,128)(2,1)S(1)} %constant_dynamic-slice_fusion), channel_id=1, source_target_pairs={{0,16},{16,32},{32,48},{48,64},{64,80},{80,96},{96,112},{112,128},... | collective-permute-start | bytes 442376 | tf_op jit(solution)/shard_map/ppermute | solution.py:309
  10.6 2.2 %quarters.1 = (bf16[64,1792]{1,0:T(8,128)(2,1)}, bf16[64,1792]{1,0:T(8,128)(2,1)}) custom-call(bf16[64,7168]{1,0:T(8,128)(2,1)} %bitcast.37), custom_call_target="tpu_custom_call" | custom-call | bytes 2097152 | tf_op jit(solution)/shard_map/quarters/pallas_call | solution.py:252
  12.8 2.8 %collective-permute-start.11 = (bf16[64,1792]{1,0:T(8,128)(2,1)}, bf16[64,1792]{1,0:T(8,128)(2,1)S(1)}, u32[]{:S(2)}, u32[]{:S(2)}) collective-permute-start(bf16[64,1792]{1,0:T(8,128)(2,1)} %get-tuple-element.17.refs_4_), channel_id=1, source_target_pairs={{0,16},{1,17},{2,18},{3,19},{4,20},{5,21},{6,22},{7,23},{8,24},{9,... | collective-permute-start | bytes 688136 | tf_op jit(solution)/shard_map/ppermute | solution.py:33
  15.6 0.8 collective-permute-start.6
  16.5 1.9 %collective-permute-start.8 = (bf16[64,1792]{1,0:T(8,128)(2,1)}, bf16[64,1792]{1,0:T(8,128)(2,1)S(1)}, u32[]{:S(2)}, u32[]{:S(2)}) collective-permute-start(bf16[64,1792]{1,0:T(8,128)(2,1)} %get-tuple-element.19), channel_id=1, source_target_pairs={{0,129},{1,128},{2,131},{3,130},{4,133},{5,132},{6,135},{7,134},{8... | collective-permute-start | bytes 688136 | tf_op jit(solution)/shard_map/ppermute | solution.py:33
  18.5 0.5 fusion.14
  19.7 1.4 %copy.11.cache = bf16[512,576]{1,0:T(8,128)(2,1)S(1)} copy(bf16[512,576]{0,1:T(8,128)(2,1)} %param.10) | data formatting | bytes 1179648 | tf_op args[2]
  21.1 2.3 %copy-done = bf16[1536,1536]{1,0:T(8,128)(2,1)S(1)} copy-done((bf16[1536,1536]{1,0:T(8,128)(2,1)S(1)}, bf16[1536,1536]{1,0:T(8,128)(2,1)}, u32[]{:S(2)}) %copy-start) | copy-done | bytes 4718616
  23.4 1.1 %copy-done.3 = bf16[256,1536]{1,0:T(8,128)(2,1)S(1)} copy-done((bf16[256,1536]{1,0:T(8,128)(2,1)S(1)}, bf16[256,1536]{1,0:T(8,128)(2,1)}, u32[]{:S(2)}) %copy-start.3) | copy-done | bytes 786456
  24.5 3.1 %queries.1 = bf16[2048,640]{1,0:T(8,128)(2,1)S(1)} custom-call(bf16[256,1536]{1,0:T(8,128)(2,1)S(1)} %copy-done.3, bf16[1536,1536]{1,0:T(8,128)(2,1)S(1)} %copy-done, bf16[8,128,512]{2,1,0:T(8,128)(2,1)S(1)} %copy-done.1, f32[192,128]{1,0:T(8,128)S(1)} %get-tuple-element.40.cosines, f32[192,128]{1,0:T(8,128)S(1)} %get-tuple-element.39.sines), custom_call_target="tpu_custom_call" | custom-call | flops 1476395008 | bytes 8388608 | tf_op jit(solution)/shard_map/queries/pallas_call | solution.py:264
  27.7 2.0 %collective-permute-start.2 = (bf16[256,576]{1,0:T(8,128)(2,1)S(1)}, bf16[256,576]{1,0:T(8,128)(2,1)S(1)}, u32[]{:S(2)}, u32[]{:S(2)}) collective-permute-start(bf16[256,576]{1,0:T(8,128)(2,1)S(1)} %pad_maximum_fusion.2), channel_id=1, source_target_pairs={{0,2},{1,3},{2,0},{3,1},{4,6},{5,7},{6,4},{7,5},{8,10},{9,11},{10,... | collective-permute-start | bytes 884744 | tf_op jit(solution)/shard_map/ppermute | solution.py:33
  29.7 0.1 fusion.reorder
  29.9 1.7 %collective-permute-start.12 = (bf16[64,1792]{1,0:T(8,128)(2,1)S(1)}, bf16[64,1792]{1,0:T(8,128)(2,1)S(1)}, u32[]{:S(2)}, u32[]{:S(2)}) collective-permute-start(bf16[64,1792]{1,0:T(8,128)(2,1)S(1)} %collective-permute-done.11.refs_11_), channel_id=1, source_target_pairs={{0,16},{1,17},{2,18},{3,19},{4,20},{5,21},{6,22},{7,23},{8,24},{9,... | collective-permute-start | bytes 688136 | tf_op jit(solution)/shard_map/ppermute | solution.py:33
  31.7 1.4 %collective-permute-start.13 = (bf16[64,1792]{1,0:T(8,128)(2,1)S(1)}, bf16[64,1792]{1,0:T(8,128)(2,1)S(1)}, u32[]{:S(2)}, u32[]{:S(2)}) collective-permute-start(bf16[64,1792]{1,0:T(8,128)(2,1)S(1)} %collective-permute-done.8.refs_12_), channel_id=1, source_target_pairs={{0,16},{1,17},{2,18},{3,19},{4,20},{5,21},{6,22},{7,23},{8,24},{9,... | collective-permute-start | bytes 688136 | tf_op jit(solution)/shard_map/ppermute | solution.py:33
  33.0 1.3 %collective-permute-start.9 = (bf16[64,1792]{1,0:T(8,128)(2,1)S(1)}, bf16[64,1792]{1,0:T(8,128)(2,1)S(1)}, u32[]{:S(2)}, u32[]{:S(2)}) collective-permute-start(bf16[64,1792]{1,0:T(8,128)(2,1)S(1)} %collective-permute-done.8.refs_12_), channel_id=1, source_target_pairs={{0,112},{1,113},{2,114},{3,115},{4,116},{5,117},{6,118},{7,119},{8... | collective-permute-start | bytes 688136 | tf_op jit(solution)/shard_map/ppermute | solution.py:33
  34.3 2.0 %keys.1 = (bf16[768,640]{1,0:T(8,128)(2,1)S(1)}, f32[256,768]{1,0:T(8,128)S(1)}) custom-call(s32[1]{0:T(128)S(6)} %copy.12.start, bf16[256,576]{1,0:T(8,128)(2,1)S(1)} %copy.10.own, bf16[128,576]{1,0:T(8,128)(2,1)S(1)} %collective-permute-done.near, bf16[128,576]{1,0:T(8,128)(2,1)S(1)} %collective-permute-done.1.far, ...), custom_call_target="tpu_custom_call" | custom-call | flops 3932160 | bytes 4194304 | tf_op jit(solution)/shard_map/keys/pallas_call | solution.py:264
  36.4 7.6 %attend.1.refs_0_ = bf16[256,1024]{1,0:T(8,128)(2,1)S(1)} custom-call(bf16[2048,640]{1,0:T(8,128)(2,1)S(1)} %queries.1, bf16[768,640]{1,0:T(8,128)(2,1)S(1)} %get-tuple-element.15.keys, f32[256,768]{1,0:T(8,128)S(1)} %get-tuple-element.16.hidden, bf16[8,512,128]{2,1,0:T(8,128)(2,1)S(1)} %copy-done.4, bf16[512,512]{1,0:T(8,128)(2,1)S(1)} %fusion.reorder), custom_call_target="tpu_custom_call" | custom-call | flops 3892314112 | bytes 9437184 | tf_op jit(solution)/shard_map/attend/pallas_call | solution.py:264
  44.3 1.5 %collective-permute-start.14 = (bf16[128,1792]{1,0:T(8,128)(2,1)S(1)}, bf16[128,1792]{1,0:T(8,128)(2,1)S(1)}, u32[]{:S(2)}, u32[]{:S(2)}) collective-permute-start(bf16[128,1792]{1,0:T(8,128)(2,1)S(1)} %pad_maximum_fusion.1), channel_id=1, source_target_pairs={{0,16},{1,17},{2,18},{3,19},{4,20},{5,21},{6,22},{7,23},{8,24},{9,... | collective-permute-start | bytes 1376264 | tf_op jit(solution)/shard_map/ppermute | solution.py:33
  45.7 1.3 %collective-permute-start.5 = (bf16[256,1024]{1,0:T(8,128)(2,1)S(1)}, bf16[256,1024]{1,0:T(8,128)(2,1)S(1)}, u32[]{:S(2)}, u32[]{:S(2)}) collective-permute-start(bf16[256,1024]{1,0:T(8,128)(2,1)S(1)} %attend.1.refs_0_), channel_id=1, source_target_pairs={{0,129},{1,128},{2,131},{3,130},{4,133},{5,132},{6,135},{7,134},{8... | collective-permute-start | bytes 1572872 | tf_op jit(solution)/shard_map/ppermute | solution.py:33
  47.0 0.4 collective-permute-start.4
  47.4 1.6 %collective-permute-start.3 = (bf16[256,1024]{1,0:T(8,128)(2,1)S(1)}, bf16[256,1024]{1,0:T(8,128)(2,1)S(1)}, u32[]{:S(2)}, u32[]{:S(2)}) collective-permute-start(bf16[256,1024]{1,0:T(8,128)(2,1)S(1)} %attend.1.refs_0_), channel_id=1, source_target_pairs={{0,1},{1,0},{2,3},{3,2},{4,5},{5,4},{6,7},{7,6},{8,9},{9,8},{10,11... | collective-permute-start | bytes 1572872 | tf_op jit(solution)/shard_map/ppermute | solution.py:33
  49.0 6.4 %collective-permute-done.10.refs_7_ = bf16[128,1792]{1,0:T(8,128)(2,1)S(1)} collective-permute-done((bf16[128,1792]{1,0:T(8,128)(2,1)S(1)}, bf16[128,1792]{1,0:T(8,128)(2,1)S(1)}, u32[]{:S(2)}, u32[]{:S(2)}) %collective-permute-start.10) | collective-permute-done | bytes 458784 | tf_op jit(solution)/shard_map/ppermute | solution.py:33
  55.4 1.6 %collective-permute-start.16 = (bf16[64,1792]{1,0:T(8,128)(2,1)S(1)}, bf16[64,1792]{1,0:T(8,128)(2,1)S(1)}, u32[]{:S(2)}, u32[]{:S(2)}) collective-permute-start(bf16[64,1792]{1,0:T(8,128)(2,1)S(1)} %slice.112), channel_id=1, source_target_pairs={{0,112},{1,113},{2,114},{3,115},{4,116},{5,117},{6,118},{7,119},{8... | collective-permute-start | bytes 688136 | tf_op jit(solution)/shard_map/ppermute | solution.py:33
  57.1 3.8 %collective-permute-done.16.refs_14_ = bf16[64,1792]{1,0:T(8,128)(2,1)S(1)} collective-permute-done((bf16[64,1792]{1,0:T(8,128)(2,1)S(1)}, bf16[64,1792]{1,0:T(8,128)(2,1)S(1)}, u32[]{:S(2)}, u32[]{:S(2)}) %collective-permute-start.16) | collective-permute-done | bytes 229408 | tf_op jit(solution)/shard_map/ppermute | solution.py:33
  60.9 3.1 %collective-permute-start.17 = (bf16[64,1792]{1,0:T(8,128)(2,1)S(1)}, bf16[64,1792]{1,0:T(8,128)(2,1)S(1)}, u32[]{:S(2)}, u32[]{:S(2)}) collective-permute-start(bf16[64,1792]{1,0:T(8,128)(2,1)S(1)} %collective-permute-done.16.refs_14_), channel_id=1, source_target_pairs={{0,112},{1,113},{2,114},{3,115},{4,116},{5,117},{6,118},{7,119},{8... | collective-permute-start | bytes 688136 | tf_op jit(solution)/shard_map/ppermute | solution.py:33
  63.9 6.4 %collective-permute-done.5.refs_3_ = bf16[256,1024]{1,0:T(8,128)(2,1)S(1)} collective-permute-done((bf16[256,1024]{1,0:T(8,128)(2,1)S(1)}, bf16[256,1024]{1,0:T(8,128)(2,1)S(1)}, u32[]{:S(2)}, u32[]{:S(2)}) %collective-permute-start.5) | collective-permute-done | bytes 524320 | tf_op jit(solution)/shard_map/ppermute | solution.py:33
  70.4 0.2 collective-permute-done.3.refs_1_
  70.6 2.3 %project.3 = bf16[4,256,896]{2,1,0:T(8,128)(2,1)S(1)} custom-call(bf16[256,1024]{1,0:T(8,128)(2,1)S(1)} %attend.1.refs_0_, bf16[256,1024]{1,0:T(8,128)(2,1)S(1)} %collective-permute-done.3.refs_1_, bf16[256,1024]{1,0:T(8,128)(2,1)S(1)} %collective-permute-done.4.refs_2_, bf16[256,1024]{1,0:T(8,128)(2,1)S(1)} %collective-permute-done.5.refs_3_, ...), custom_call_target="tpu_custom_call" | custom-call | flops 1879048192 | bytes 8388608 | tf_op jit(solution)/shard_map/project/pallas_call | solution.py:264
  72.9 2.7 %collective-permute-start.18 = (bf16[4,256,896]{2,1,0:T(8,128)(2,1)S(1)}, bf16[4,256,896]{2,1,0:T(8,128)(2,1)S(1)}, u32[]{:S(2)}, u32[]{:S(2)}) collective-permute-start(bf16[4,256,896]{2,1,0:T(8,128)(2,1)S(1)} %project.3), channel_id=1, source_target_pairs={{0,2},{1,3},{2,0},{3,1},{4,6},{5,7},{6,4},{7,5},{8,10},{9,11},{10,... | collective-permute-start | bytes 5505032 | tf_op jit(solution)/shard_map/ppermute | solution.py:33
  75.5 2.5 %project.2 = f32[4,256,896]{2,1,0:T(8,128)S(1)} custom-call(bf16[256,1024]{1,0:T(8,128)(2,1)S(1)} %attend.1.refs_0_, bf16[256,1024]{1,0:T(8,128)(2,1)S(1)} %collective-permute-done.3.refs_1_, bf16[256,1024]{1,0:T(8,128)(2,1)S(1)} %collective-permute-done.4.refs_2_, bf16[256,1024]{1,0:T(8,128)(2,1)S(1)} %collective-permute-done.5.refs_3_, ...), custom_call_target="tpu_custom_call" | custom-call | flops 1879048192 | bytes 8388608 | tf_op jit(solution)/shard_map/project/pallas_call | solution.py:264
  78.1 0.9 collective-permute-done.18
  78.9 0.3 slice_add_fusion.2
  79.3 1.3 %collective-permute-start.19 = (bf16[128,896]{1,0:T(8,128)(2,1)S(1)}, bf16[128,896]{1,0:T(8,128)(2,1)S(1)}, u32[]{:S(2)}, u32[]{:S(2)}) collective-permute-start(bf16[128,896]{1,0:T(8,128)(2,1)S(1)} %get-tuple-element.33), channel_id=1, source_target_pairs={{0,4},{1,5},{2,6},{3,7},{4,8},{5,9},{6,10},{7,11},{8,12},{9,13},{1... | collective-permute-start | bytes 688136 | tf_op jit(solution)/shard_map/ppermute | solution.py:33
  80.6 1.5 %collective-permute-start.21 = (bf16[128,896]{1,0:T(8,128)(2,1)S(1)}, bf16[128,896]{1,0:T(8,128)(2,1)S(1)}, u32[]{:S(2)}, u32[]{:S(2)}) collective-permute-start(bf16[128,896]{1,0:T(8,128)(2,1)S(1)} %fusion.13), channel_id=1, source_target_pairs={{0,12},{1,13},{2,14},{3,15},{4,0},{5,1},{6,2},{7,3},{8,4},{9,5},{1... | collective-permute-start | bytes 688136 | tf_op jit(solution)/shard_map/ppermute | solution.py:33
  82.2 2.7 %collective-permute-start.24 = (bf16[128,896]{1,0:T(8,128)(2,1)S(1)}, bf16[128,896]{1,0:T(8,128)(2,1)S(1)}, u32[]{:S(2)}, u32[]{:S(2)}) collective-permute-start(bf16[128,896]{1,0:T(8,128)(2,1)S(1)} %get-tuple-element.34), channel_id=1, source_target_pairs={{0,12},{1,13},{2,14},{3,15},{4,0},{5,1},{6,2},{7,3},{8,4},{9,5},{1... | collective-permute-start | bytes 688136 | tf_op jit(solution)/shard_map/ppermute | solution.py:33
  84.9 2.6 %collective-permute-done.19 = bf16[128,896]{1,0:T(8,128)(2,1)S(1)} collective-permute-done((bf16[128,896]{1,0:T(8,128)(2,1)S(1)}, bf16[128,896]{1,0:T(8,128)(2,1)S(1)}, u32[]{:S(2)}, u32[]{:S(2)}) %collective-permute-start.19) | collective-permute-done | bytes 229408 | tf_op jit(solution)/shard_map/ppermute | solution.py:33
  87.6 4.5 %collective-permute-done.24 = bf16[128,896]{1,0:T(8,128)(2,1)S(1)} collective-permute-done((bf16[128,896]{1,0:T(8,128)(2,1)S(1)}, bf16[128,896]{1,0:T(8,128)(2,1)S(1)}, u32[]{:S(2)}, u32[]{:S(2)}) %collective-permute-start.24) | collective-permute-done | bytes 229408 | tf_op jit(solution)/shard_map/ppermute | solution.py:33
  92.2 2.8 %collective-permute-start.25 = (bf16[128,896]{1,0:T(8,128)(2,1)S(1)}, bf16[128,896]{1,0:T(8,128)(2,1)S(1)}, u32[]{:S(2)}, u32[]{:S(2)}) collective-permute-start(bf16[128,896]{1,0:T(8,128)(2,1)S(1)} %fusion.3), channel_id=1, source_target_pairs={{0,12},{1,13},{2,14},{3,15},{4,0},{5,1},{6,2},{7,3},{8,4},{9,5},{1... | collective-permute-start | bytes 688136 | tf_op jit(solution)/shard_map/ppermute | solution.py:33
  94.9 2.3 %collective-permute-done.20 = bf16[128,896]{1,0:T(8,128)(2,1)S(1)} collective-permute-done((bf16[128,896]{1,0:T(8,128)(2,1)S(1)}, bf16[128,896]{1,0:T(8,128)(2,1)S(1)}, u32[]{:S(2)}, u32[]{:S(2)}) %collective-permute-start.20) | collective-permute-done | bytes 229408 | tf_op jit(solution)/shard_map/ppermute | solution.py:33
  97.3 1.1 collective-permute-done.25
  98.3 0.1 fusion.11
  98.5 5.0 %collective-permute-start.22 = (bf16[128,896]{1,0:T(8,128)(2,1)S(1)}, bf16[128,896]{1,0:T(8,128)(2,1)S(1)}, u32[]{:S(2)}, u32[]{:S(2)}) collective-permute-start(bf16[128,896]{1,0:T(8,128)(2,1)S(1)} %get-tuple-element.29), channel_id=1, source_target_pairs={{0,0},{1,1},{2,128},{3,129},{4,4},{5,5},{6,132},{7,133},{8,8},{9,9... | collective-permute-start | bytes 688136 | tf_op jit(solution)/shard_map/ppermute | solution.py:33
  103.5 0.6 collective-permute-start.26
  104.1 3.9 %collective-permute-done.22 = bf16[128,896]{1,0:T(8,128)(2,1)S(1)} collective-permute-done((bf16[128,896]{1,0:T(8,128)(2,1)S(1)}, bf16[128,896]{1,0:T(8,128)(2,1)S(1)}, u32[]{:S(2)}, u32[]{:S(2)}) %collective-permute-start.22) | collective-permute-done | bytes 229408 | tf_op jit(solution)/shard_map/ppermute | solution.py:33
  108.0 2.0 %collective-permute-done.26 = bf16[128,896]{1,0:T(8,128)(2,1)S(1)} collective-permute-done((bf16[128,896]{1,0:T(8,128)(2,1)S(1)}, bf16[128,896]{1,0:T(8,128)(2,1)S(1)}, u32[]{:S(2)}, u32[]{:S(2)}) %collective-permute-start.26) | collective-permute-done | bytes 229408 | tf_op jit(solution)/shard_map/ppermute | solution.py:33
  110.3 0.9 maximum_maximum_fusion
  (51 shorter events, 1.1 us)
Async XLA Ops:
  0.0 21.0 %copy-start.1 = (bf16[8,128,512]{2,1,0:T(8,128)(2,1)S(1)}, bf16[8,128,512]{2,1,0:T(8,128)(2,1)}, u32[]{:S(2)}) copy-start(bf16[8,128,512]{2,1,0:T(8,128)(2,1)} %w_key_up.1) | copy-start | bytes 3145732
  1.3 26.3 %collective-permute-start.1 = (bf16[128,576]{1,0:T(8,128)(2,1)S(1)}, bf16[128,576]{1,0:T(8,128)(2,1)S(1)}, u32[]{:S(2)}, u32[]{:S(2)}) collective-permute-start(bf16[128,576]{1,0:T(8,128)(2,1)S(1)} %constant_dynamic-slice_fusion), channel_id=1, source_target_pairs={{0,32},{16,48},{32,64},{48,80},{64,96},{80,112},{96,128},{112,144}... | collective-permute-start | bytes 442376 | tf_op jit(solution)/shard_map/ppermute | solution.py:309
  7.0 20.6 %collective-permute-start = (bf16[128,576]{1,0:T(8,128)(2,1)S(1)}, bf16[128,576]{1,0:T(8,128)(2,1)S(1)}, u32[]{:S(2)}, u32[]{:S(2)}) collective-permute-start(bf16[128,576]{1,0:T(8,128)(2,1)S(1)} %constant_dynamic-slice_fusion), channel_id=1, source_target_pairs={{0,16},{16,32},{32,48},{48,64},{64,80},{80,96},{96,112},{112,128},... | collective-permute-start | bytes 442376 | tf_op jit(solution)/shard_map/ppermute | solution.py:309
  12.8 17.1 %collective-permute-start.11 = (bf16[64,1792]{1,0:T(8,128)(2,1)}, bf16[64,1792]{1,0:T(8,128)(2,1)S(1)}, u32[]{:S(2)}, u32[]{:S(2)}) collective-permute-start(bf16[64,1792]{1,0:T(8,128)(2,1)} %get-tuple-element.17.refs_4_), channel_id=1, source_target_pairs={{0,16},{1,17},{2,18},{3,19},{4,20},{5,21},{6,22},{7,23},{8,24},{9,... | collective-permute-start | bytes 688136 | tf_op jit(solution)/shard_map/ppermute | solution.py:33
  15.6 14.2 %collective-permute-start.6 = (bf16[64,1792]{1,0:T(8,128)(2,1)}, bf16[64,1792]{1,0:T(8,128)(2,1)S(1)}, u32[]{:S(2)}, u32[]{:S(2)}) collective-permute-start(bf16[64,1792]{1,0:T(8,128)(2,1)} %get-tuple-element.17.refs_4_), channel_id=1, source_target_pairs={{0,112},{1,113},{2,114},{3,115},{4,116},{5,117},{6,118},{7,119},{8... | collective-permute-start | bytes 688136 | tf_op jit(solution)/shard_map/ppermute | solution.py:33
  16.5 15.2 %collective-permute-start.8 = (bf16[64,1792]{1,0:T(8,128)(2,1)}, bf16[64,1792]{1,0:T(8,128)(2,1)S(1)}, u32[]{:S(2)}, u32[]{:S(2)}) collective-permute-start(bf16[64,1792]{1,0:T(8,128)(2,1)} %get-tuple-element.19), channel_id=1, source_target_pairs={{0,129},{1,128},{2,131},{3,130},{4,133},{5,132},{6,135},{7,134},{8... | collective-permute-start | bytes 688136 | tf_op jit(solution)/shard_map/ppermute | solution.py:33
  21.1 2.3 %copy-start = (bf16[1536,1536]{1,0:T(8,128)(2,1)S(1)}, bf16[1536,1536]{1,0:T(8,128)(2,1)}, u32[]{:S(2)}) copy-start(bf16[1536,1536]{1,0:T(8,128)(2,1)} %w_query.1) | copy-start | bytes 14155780
  23.4 1.1 %copy-start.3 = (bf16[256,1536]{1,0:T(8,128)(2,1)S(1)}, bf16[256,1536]{1,0:T(8,128)(2,1)}, u32[]{:S(2)}) copy-start(bf16[256,1536]{1,0:T(8,128)(2,1)} %rows.1) | copy-start | bytes 2359300
  27.6 8.8 %copy-start.4 = (bf16[8,512,128]{2,1,0:T(8,128)(2,1)S(1)}, bf16[8,512,128]{2,1,0:T(8,128)(2,1)}, u32[]{:S(2)}) copy-start(bf16[8,512,128]{2,1,0:T(8,128)(2,1)} %w_value_up.1) | copy-start | bytes 3145732
  27.7 6.7 %collective-permute-start.2 = (bf16[256,576]{1,0:T(8,128)(2,1)S(1)}, bf16[256,576]{1,0:T(8,128)(2,1)S(1)}, u32[]{:S(2)}, u32[]{:S(2)}) collective-permute-start(bf16[256,576]{1,0:T(8,128)(2,1)S(1)} %pad_maximum_fusion.2), channel_id=1, source_target_pairs={{0,2},{1,3},{2,0},{3,1},{4,6},{5,7},{6,4},{7,5},{8,10},{9,11},{10,... | collective-permute-start | bytes 884744 | tf_op jit(solution)/shard_map/ppermute | solution.py:33
  29.9 14.3 %collective-permute-start.7 = (bf16[64,1792]{1,0:T(8,128)(2,1)S(1)}, bf16[64,1792]{1,0:T(8,128)(2,1)S(1)}, u32[]{:S(2)}, u32[]{:S(2)}) collective-permute-start(bf16[64,1792]{1,0:T(8,128)(2,1)S(1)} %collective-permute-done.6.refs_5_), channel_id=1, source_target_pairs={{0,112},{1,113},{2,114},{3,115},{4,116},{5,117},{6,118},{7,119},{8... | collective-permute-start | bytes 688136 | tf_op jit(solution)/shard_map/ppermute | solution.py:33
  29.9 14.1 %collective-permute-start.12 = (bf16[64,1792]{1,0:T(8,128)(2,1)S(1)}, bf16[64,1792]{1,0:T(8,128)(2,1)S(1)}, u32[]{:S(2)}, u32[]{:S(2)}) collective-permute-start(bf16[64,1792]{1,0:T(8,128)(2,1)S(1)} %collective-permute-done.11.refs_11_), channel_id=1, source_target_pairs={{0,16},{1,17},{2,18},{3,19},{4,20},{5,21},{6,22},{7,23},{8,24},{9,... | collective-permute-start | bytes 688136 | tf_op jit(solution)/shard_map/ppermute | solution.py:33
  31.7 12.4 %collective-permute-start.13 = (bf16[64,1792]{1,0:T(8,128)(2,1)S(1)}, bf16[64,1792]{1,0:T(8,128)(2,1)S(1)}, u32[]{:S(2)}, u32[]{:S(2)}) collective-permute-start(bf16[64,1792]{1,0:T(8,128)(2,1)S(1)} %collective-permute-done.8.refs_12_), channel_id=1, source_target_pairs={{0,16},{1,17},{2,18},{3,19},{4,20},{5,21},{6,22},{7,23},{8,24},{9,... | collective-permute-start | bytes 688136 | tf_op jit(solution)/shard_map/ppermute | solution.py:33
  33.0 11.1 %collective-permute-start.9 = (bf16[64,1792]{1,0:T(8,128)(2,1)S(1)}, bf16[64,1792]{1,0:T(8,128)(2,1)S(1)}, u32[]{:S(2)}, u32[]{:S(2)}) collective-permute-start(bf16[64,1792]{1,0:T(8,128)(2,1)S(1)} %collective-permute-done.8.refs_12_), channel_id=1, source_target_pairs={{0,112},{1,113},{2,114},{3,115},{4,116},{5,117},{6,118},{7,119},{8... | collective-permute-start | bytes 688136 | tf_op jit(solution)/shard_map/ppermute | solution.py:33
  36.4 34.2 %copy-start.2 = (bf16[64,1792]{1,0:T(8,128)(2,1)S(1)}, bf16[64,1792]{1,0:T(8,128)(2,1)}, u32[]{:S(2)}) copy-start(bf16[64,1792]{1,0:T(8,128)(2,1)} %get-tuple-element.17.refs_4_) | copy-start | bytes 688132
  44.2 11.2 %collective-permute-start.10 = (bf16[128,1792]{1,0:T(8,128)(2,1)S(1)}, bf16[128,1792]{1,0:T(8,128)(2,1)S(1)}, u32[]{:S(2)}, u32[]{:S(2)}) collective-permute-start(bf16[128,1792]{1,0:T(8,128)(2,1)S(1)} %pad_maximum_fusion), channel_id=1, source_target_pairs={{0,112},{1,113},{2,114},{3,115},{4,116},{5,117},{6,118},{7,119},{8... | collective-permute-start | bytes 1376264 | tf_op jit(solution)/shard_map/ppermute | solution.py:33
  44.3 12.8 %collective-permute-start.14 = (bf16[128,1792]{1,0:T(8,128)(2,1)S(1)}, bf16[128,1792]{1,0:T(8,128)(2,1)S(1)}, u32[]{:S(2)}, u32[]{:S(2)}) collective-permute-start(bf16[128,1792]{1,0:T(8,128)(2,1)S(1)} %pad_maximum_fusion.1), channel_id=1, source_target_pairs={{0,16},{1,17},{2,18},{3,19},{4,20},{5,21},{6,22},{7,23},{8,24},{9,... | collective-permute-start | bytes 1376264 | tf_op jit(solution)/shard_map/ppermute | solution.py:33
  45.7 24.6 %collective-permute-start.5 = (bf16[256,1024]{1,0:T(8,128)(2,1)S(1)}, bf16[256,1024]{1,0:T(8,128)(2,1)S(1)}, u32[]{:S(2)}, u32[]{:S(2)}) collective-permute-start(bf16[256,1024]{1,0:T(8,128)(2,1)S(1)} %attend.1.refs_0_), channel_id=1, source_target_pairs={{0,129},{1,128},{2,131},{3,130},{4,133},{5,132},{6,135},{7,134},{8... | collective-permute-start | bytes 1572872 | tf_op jit(solution)/shard_map/ppermute | solution.py:33
  47.0 23.3 %collective-permute-start.4 = (bf16[256,1024]{1,0:T(8,128)(2,1)S(1)}, bf16[256,1024]{1,0:T(8,128)(2,1)S(1)}, u32[]{:S(2)}, u32[]{:S(2)}) collective-permute-start(bf16[256,1024]{1,0:T(8,128)(2,1)S(1)} %attend.1.refs_0_), channel_id=1, source_target_pairs={{0,128},{1,129},{2,130},{3,131},{4,132},{5,133},{6,134},{7,135},{8... | collective-permute-start | bytes 1572872 | tf_op jit(solution)/shard_map/ppermute | solution.py:33
  47.4 23.2 %collective-permute-start.3 = (bf16[256,1024]{1,0:T(8,128)(2,1)S(1)}, bf16[256,1024]{1,0:T(8,128)(2,1)S(1)}, u32[]{:S(2)}, u32[]{:S(2)}) collective-permute-start(bf16[256,1024]{1,0:T(8,128)(2,1)S(1)} %attend.1.refs_0_), channel_id=1, source_target_pairs={{0,1},{1,0},{2,3},{3,2},{4,5},{5,4},{6,7},{7,6},{8,9},{9,8},{10,11... | collective-permute-start | bytes 1572872 | tf_op jit(solution)/shard_map/ppermute | solution.py:33
  55.4 5.4 %collective-permute-start.16 = (bf16[64,1792]{1,0:T(8,128)(2,1)S(1)}, bf16[64,1792]{1,0:T(8,128)(2,1)S(1)}, u32[]{:S(2)}, u32[]{:S(2)}) collective-permute-start(bf16[64,1792]{1,0:T(8,128)(2,1)S(1)} %slice.112), channel_id=1, source_target_pairs={{0,112},{1,113},{2,114},{3,115},{4,116},{5,117},{6,118},{7,119},{8... | collective-permute-start | bytes 688136 | tf_op jit(solution)/shard_map/ppermute | solution.py:33
  57.1 13.5 %collective-permute-start.15 = (bf16[128,1792]{1,0:T(8,128)(2,1)S(1)}, bf16[128,1792]{1,0:T(8,128)(2,1)S(1)}, u32[]{:S(2)}, u32[]{:S(2)}) collective-permute-start(bf16[128,1792]{1,0:T(8,128)(2,1)S(1)} %collective-permute-done.14.refs_9_), channel_id=1, source_target_pairs={{0,16},{1,17},{2,18},{3,19},{4,20},{5,21},{6,22},{7,23},{8,24},{9,... | collective-permute-start | bytes 1376264 | tf_op jit(solution)/shard_map/ppermute | solution.py:33
  60.9 9.7 %collective-permute-start.17 = (bf16[64,1792]{1,0:T(8,128)(2,1)S(1)}, bf16[64,1792]{1,0:T(8,128)(2,1)S(1)}, u32[]{:S(2)}, u32[]{:S(2)}) collective-permute-start(bf16[64,1792]{1,0:T(8,128)(2,1)S(1)} %collective-permute-done.16.refs_14_), channel_id=1, source_target_pairs={{0,112},{1,113},{2,114},{3,115},{4,116},{5,117},{6,118},{7,119},{8... | collective-permute-start | bytes 688136 | tf_op jit(solution)/shard_map/ppermute | solution.py:33
  72.9 6.1 %collective-permute-start.18 = (bf16[4,256,896]{2,1,0:T(8,128)(2,1)S(1)}, bf16[4,256,896]{2,1,0:T(8,128)(2,1)S(1)}, u32[]{:S(2)}, u32[]{:S(2)}) collective-permute-start(bf16[4,256,896]{2,1,0:T(8,128)(2,1)S(1)} %project.3), channel_id=1, source_target_pairs={{0,2},{1,3},{2,0},{3,1},{4,6},{5,7},{6,4},{7,5},{8,10},{9,11},{10,... | collective-permute-start | bytes 5505032 | tf_op jit(solution)/shard_map/ppermute | solution.py:33
  79.3 8.1 %collective-permute-start.19 = (bf16[128,896]{1,0:T(8,128)(2,1)S(1)}, bf16[128,896]{1,0:T(8,128)(2,1)S(1)}, u32[]{:S(2)}, u32[]{:S(2)}) collective-permute-start(bf16[128,896]{1,0:T(8,128)(2,1)S(1)} %get-tuple-element.33), channel_id=1, source_target_pairs={{0,4},{1,5},{2,6},{3,7},{4,8},{5,9},{6,10},{7,11},{8,12},{9,13},{1... | collective-permute-start | bytes 688136 | tf_op jit(solution)/shard_map/ppermute | solution.py:33
  80.6 14.3 %collective-permute-start.21 = (bf16[128,896]{1,0:T(8,128)(2,1)S(1)}, bf16[128,896]{1,0:T(8,128)(2,1)S(1)}, u32[]{:S(2)}, u32[]{:S(2)}) collective-permute-start(bf16[128,896]{1,0:T(8,128)(2,1)S(1)} %fusion.13), channel_id=1, source_target_pairs={{0,12},{1,13},{2,14},{3,15},{4,0},{5,1},{6,2},{7,3},{8,4},{9,5},{1... | collective-permute-start | bytes 688136 | tf_op jit(solution)/shard_map/ppermute | solution.py:33
  82.2 12.8 %collective-permute-start.23 = (bf16[128,896]{1,0:T(8,128)(2,1)S(1)}, bf16[128,896]{1,0:T(8,128)(2,1)S(1)}, u32[]{:S(2)}, u32[]{:S(2)}) collective-permute-start(bf16[128,896]{1,0:T(8,128)(2,1)S(1)} %fusion.12), channel_id=1, source_target_pairs={{0,4},{1,5},{2,6},{3,7},{4,8},{5,9},{6,10},{7,11},{8,12},{9,13},{1... | collective-permute-start | bytes 688136 | tf_op jit(solution)/shard_map/ppermute | solution.py:33
  82.2 9.9 %collective-permute-start.24 = (bf16[128,896]{1,0:T(8,128)(2,1)S(1)}, bf16[128,896]{1,0:T(8,128)(2,1)S(1)}, u32[]{:S(2)}, u32[]{:S(2)}) collective-permute-start(bf16[128,896]{1,0:T(8,128)(2,1)S(1)} %get-tuple-element.34), channel_id=1, source_target_pairs={{0,12},{1,13},{2,14},{3,15},{4,0},{5,1},{6,2},{7,3},{8,4},{9,5},{1... | collective-permute-start | bytes 688136 | tf_op jit(solution)/shard_map/ppermute | solution.py:33
  87.5 9.8 %collective-permute-start.20 = (bf16[128,896]{1,0:T(8,128)(2,1)S(1)}, bf16[128,896]{1,0:T(8,128)(2,1)S(1)}, u32[]{:S(2)}, u32[]{:S(2)}) collective-permute-start(bf16[128,896]{1,0:T(8,128)(2,1)S(1)} %fusion.8), channel_id=1, source_target_pairs={{0,4},{1,5},{2,6},{3,7},{4,8},{5,9},{6,10},{7,11},{8,12},{9,13},{1... | collective-permute-start | bytes 688136 | tf_op jit(solution)/shard_map/ppermute | solution.py:33
  92.2 6.1 %collective-permute-start.25 = (bf16[128,896]{1,0:T(8,128)(2,1)S(1)}, bf16[128,896]{1,0:T(8,128)(2,1)S(1)}, u32[]{:S(2)}, u32[]{:S(2)}) collective-permute-start(bf16[128,896]{1,0:T(8,128)(2,1)S(1)} %fusion.3), channel_id=1, source_target_pairs={{0,12},{1,13},{2,14},{3,15},{4,0},{5,1},{6,2},{7,3},{8,4},{9,5},{1... | collective-permute-start | bytes 688136 | tf_op jit(solution)/shard_map/ppermute | solution.py:33
  98.5 9.6 %collective-permute-start.22 = (bf16[128,896]{1,0:T(8,128)(2,1)S(1)}, bf16[128,896]{1,0:T(8,128)(2,1)S(1)}, u32[]{:S(2)}, u32[]{:S(2)}) collective-permute-start(bf16[128,896]{1,0:T(8,128)(2,1)S(1)} %get-tuple-element.29), channel_id=1, source_target_pairs={{0,0},{1,1},{2,128},{3,129},{4,4},{5,5},{6,132},{7,133},{8,8},{9,9... | collective-permute-start | bytes 688136 | tf_op jit(solution)/shard_map/ppermute | solution.py:33
  103.5 6.6 %collective-permute-start.26 = (bf16[128,896]{1,0:T(8,128)(2,1)S(1)}, bf16[128,896]{1,0:T(8,128)(2,1)S(1)}, u32[]{:S(2)}, u32[]{:S(2)}) collective-permute-start(bf16[128,896]{1,0:T(8,128)(2,1)S(1)} %get-tuple-element.30), channel_id=1, source_target_pairs={{0,1},{1,0},{2,129},{3,128},{4,5},{5,4},{6,133},{7,132},{8,9},{9,8... | collective-permute-start | bytes 688136 | tf_op jit(solution)/shard_map/ppermute | solution.py:33

commit v6 on v5

--- a/solution.py
+++ b/solution.py
@@ -57,9 +57,8 @@
     return moved(a, lambda yh, z, x, c, yl: (yh ^ c, z, x, yh, yl ^ r))
 
 
-def turn_of(table, block):
-    rows = slice(64 * block, 64 * block + 64)
-    return jnp.concatenate([table[rows, 32 * i : 32 * i + 32] for i in range(4)], 0)
+def turn_of(table):
+    return jnp.concatenate([table[:, 32 * i : 32 * i + 32] for i in range(4)], 0)
 
 
 def turned(rot, cosine, sine):
@@ -70,7 +69,7 @@
     return jnp.concatenate([rot, jnp.zeros_like(rot)], 1).astype(BF)
 
 
-def queries_kernel(rows, w_query, w_key_up, cosines, sines, out, held, rows_held, sem):
+def queries_kernel(rows, w_query, w_key_up, cosines, sines, out, out_next, held, rows_held, sem):
     copies = [
         pltpu.make_async_copy(w_query.at[:, pl.ds(768 * part, 768)], held.at[part], sem.at[part])
         for part in range(2)
@@ -78,7 +77,7 @@
     copies.append(pltpu.make_async_copy(rows, rows_held, sem.at[2]))
     for i in (2, 0, 1):
         copies[i].start()
-    cosine, sine = turn_of(cosines, 2), turn_of(sines, 2)
+    cosine, sine = turn_of(cosines), turn_of(sines)
     copies[2].wait()
     for part in range(2):
         copies[part].wait()
@@ -88,24 +87,25 @@
             plain = queries[:, 192 * i : 192 * i + 128]
             lat = jnp.dot(plain, w_key_up[h], preferred_element_type=F32)
             rot = queries[:, 192 * i + 128 : 192 * i + 192].astype(F32)
-            tokens = slice(256 * h, 256 * h + 256)
-            out[tokens, :512] = lat.astype(BF)
-            out[tokens, 512:] = turned(rot, cosine, sine)
+            tokens = slice(256 * i, 256 * i + 256)
+            to = out_next if part else out
+            to[tokens, :512] = lat.astype(BF)
+            to[tokens, 512:] = turned(rot, cosine, sine)
 
 
 def keys_kernel(start, own, near, far, swapped, cache, cosines, sines, keys, hidden, raw, sem):
     c = lax.axis_index("c")
     slab = 8 * lax.axis_index("yh") + lax.axis_index("z")
 
-    def at(row, rows):
-        return raw.at[pl.ds(pl.multiple_of(row, 128), rows)]
+    def at(column, columns):
+        return raw.at[:, pl.ds(pl.multiple_of(column, 128), columns)]
 
     copies = [
         pltpu.make_async_copy(own, at(512, 256), sem.at[0]),
         pltpu.make_async_copy(near, at(256 + 128 * c, 128), sem.at[1]),
-        pltpu.make_async_copy(swapped.at[pl.ds(0, 128)], at(384 - 128 * c, 128), sem.at[2]),
+        pltpu.make_async_copy(swapped.at[:, pl.ds(0, 128)], at(384 - 128 * c, 128), sem.at[2]),
         pltpu.make_async_copy(far, at(128 * c, 128), sem.at[3]),
-        pltpu.make_async_copy(swapped.at[pl.ds(128, 128)], at(128 - 128 * c, 128), sem.at[4]),
+        pltpu.make_async_copy(swapped.at[:, pl.ds(128, 128)], at(128 - 128 * c, 128), sem.at[4]),
     ]
     for copy in copies:
         copy.start()
@@ -116,12 +116,12 @@
     hidden[...] = jnp.where(visible, 0.0, -1e30)
     for copy in copies:
         copy.wait()
-    keys[:, :512] = raw[:, :512]
-    for block in range(3):
-        tokens = slice(256 * block, 256 * block + 256)
-        keys[tokens, 512:] = turned(
-            raw[tokens, 512:].astype(F32), turn_of(cosines, block), turn_of(sines, block)
-        )
+    low, high = raw[512:544, :].astype(F32), raw[544:, :].astype(F32)
+    cosine, sine = cosines[...], sines[...]
+    keys[:512, :] = raw[:512, :]
+    keys[512:544, :] = (low * cosine - high * sine).astype(BF)
+    keys[544:576, :] = (low * sine + high * cosine).astype(BF)
+    keys[576:, :] = jnp.zeros((64, 768), BF)
 
     @pl.when(slab < 2)
     def _():
@@ -131,54 +131,49 @@
 
     @pl.when(slab == 0)
     def _():
-        keys[:512, :576] = raw[:512]
+        keys[:576, :512] = raw[:, :512]
 
     @pl.when(slab == 1)
     def _():
-        keys[:256, :576] = raw[256:512]
-
-
-def attend_kernel(queries, keys, hidden, w_value_up, reorder, out):
+        keys[:576, :256] = raw[:, 256:512]
+
+
+def attend_kernel(group, queries, keys, hidden, w_value_up, reorder, out):
     scale = 192.0**-0.5 * 1.4426950408889634
-    latent = keys[:, :512]
-
-    def step(group, carry):
-        heads = []
-        for pair in range(2):
-            first = pl.multiple_of(1024 * group + 512 * pair, 512)
-            scores = lax.dot_general(
-                queries[pl.ds(first, 512), :],
-                keys[...],
+    heads = []
+    for pair in range(2):
+        scores = jnp.dot(
+            queries[512 * pair : 512 * pair + 512, :], keys[...], preferred_element_type=F32
+        )
+        for i in range(2):
+            part = scores[256 * i : 256 * i + 256] * scale + hidden[...]
+            top = jnp.max(part, axis=1, keepdims=True)
+            powers = jnp.exp2(part - top)
+            share = 1.0 / jnp.sum(powers, axis=1, keepdims=True)
+            mixed = lax.dot_general(
+                powers.astype(BF),
+                keys[:512, :],
                 (((1,), (1,)), ((), ())),
                 preferred_element_type=F32,
             )
-            for i in range(2):
-                part = scores[256 * i : 256 * i + 256] * scale + hidden[...]
-                top = jnp.max(part, axis=1, keepdims=True)
-                powers = jnp.exp2(part - top)
-                share = 1.0 / jnp.sum(powers, axis=1, keepdims=True)
-                mixed = jnp.dot(powers.astype(BF), latent, preferred_element_type=F32) * share
-                attention = jnp.dot(
-                    mixed.astype(BF),
-                    w_value_up[4 * group + 2 * pair + i],
-                    preferred_element_type=F32,
-                )
-                heads.append(attention.astype(BF))
-        rows = jnp.concatenate(heads, 1)
-        columns = pl.ds(pl.multiple_of(512 * group, 512), 512)
-        out[:, columns] = jnp.dot(rows, reorder[...], preferred_element_type=F32).astype(BF)
-        return carry
-
-    lax.fori_loop(0, 2, step, 0)
+            attention = jnp.dot(
+                (mixed * share).astype(BF),
+                w_value_up[4 * group + 2 * pair + i],
+                preferred_element_type=F32,
+            )
+            heads.append(attention.astype(BF))
+    rows = jnp.concatenate(heads, 1)
+    out[...] = jnp.dot(rows, reorder[...], preferred_element_type=F32).astype(BF)
 
 
 def turns(first):
     inverse = jnp.power(jnp.float32(10000.0), -jnp.arange(32, dtype=F32) * (2.0 / 64))
-    row = lax.broadcasted_iota(jnp.int32, (192, 128), 0)
-    lane = lax.broadcasted_iota(jnp.int32, (192, 128), 1)
-    place = first + (row // 64) * 256 + (lane // 32) * 64 + row % 64
-    angles = place.astype(F32) * jnp.tile(inverse, 4)[None, :]
-    return jnp.cos(angles), jnp.sin(angles)
+    row = lax.broadcasted_iota(jnp.int32, (64, 128), 0)
+    lane = lax.broadcasted_iota(jnp.int32, (64, 128), 1)
+    own = (first + (lane // 32) * 64 + row).astype(F32) * jnp.tile(inverse, 4)[None, :]
+    place = first - 512 + lax.broadcasted_iota(jnp.int32, (32, 768), 1)
+    every = place.astype(F32) * inverse[:, None]
+    return jnp.cos(own), jnp.sin(own), jnp.cos(every), jnp.sin(every)
 
 
 def quarter_kernel(rows, own, other):
@@ -195,7 +190,7 @@
 
 
 def project_kernel(theirs, *refs):
-    groups, held, (out, rows, total) = refs[:4], refs[4:17], refs[17:]
+    groups, held, outs, (rows, total) = refs[:8], refs[8:21], refs[21:-2], refs[-2:]
     own, d1, d2, d3, u4, u3, u2, u1, other, e1, e3, e4, v1 = held
     blocks = [own, d1, d2, d3.at[:64], u4.at[:64], u3.at[:64], u2, u1]
     blocks += [other, e1, d3.at[64:], e3, e4, u4.at[64:], u3.at[64:], v1]
@@ -208,9 +203,9 @@
             for g in range(2):
                 for j in range(2):
                     for p in range(2):
-                        half = pl.ds(pl.multiple_of(512 * g + 256 * (yh ^ p), 256), 256)
+                        half = pl.ds(pl.multiple_of(256 * (yh ^ p), 256), 256)
                         rows[256 * j : 256 * j + 256, 512 * g + 256 * p : 512 * g + 256 * p + 256] = (
-                            groups[pick + j][:, half]
+                            groups[2 * (pick + j) + g][:, half]
                         )
 
     for n in range(7):
@@ -224,12 +219,12 @@
             0,
         )
         total[:, columns] = jnp.dot(rows[...], weights, preferred_element_type=F32)
-    for d in range(4):
+    for out, d in zip((outs[0], *(outs[1].at[i] for i in range(3))), (2, 0, 1, 3)):
         span = slice(448 * d, 448 * d + 448)
         for j in range(2):
             top = total[256 * j : 256 * j + 128, span]
             low = total[256 * j + 128 : 256 * j + 256, span]
-            out[d, 128 * j : 128 * j + 128] = jnp.concatenate([top, low], 1).astype(out.dtype)
+            out[128 * j : 128 * j + 128, :] = jnp.concatenate([top, low], 1).astype(out.dtype)
 
 
 def whole(n):
@@ -286,8 +281,8 @@
 def project(theirs, groups, blocks, kind):
     return call(
         functools.partial(project_kernel, theirs),
-        array((4, 256, 896), kind),
-        whole(17),
+        [array((256, 896), kind), array((3, 256, 896), kind)],
+        whole(21),
         (*groups, *blocks),
         "project",
         2 * 512 * 1024 * 1792,
@@ -304,71 +299,78 @@
     other = xor_y(given, 3)
     u1, d1 = up_z(own), down_z(own)
 
-    half = lax.dynamic_slice_in_dim(key_rows, 128 * c, 128, 0)
+    own_keys = key_rows.T
+    half = lax.dynamic_slice_in_dim(own_keys, 128 * c, 128, 1)
     near, far = (
         lax.ppermute(half, CTX, [(i, i + by) for i in range(16 - by)]) for by in (1, 2)
     )
-    cosines, sines = turns(slab * 256 - 512)
+    cosines, sines, all_cosines, all_sines = turns(slab * 256)
     queries = call(
         queries_kernel,
-        array((2048, 640)),
+        [array((1024, 640))] * 2,
         kept(2) + whole(3),
         (query_latent, w_query, w_key_up, cosines, sines),
         "queries",
         2 * 256 * 1536 * 1536 + 2 * 2048 * 128 * 512,
         8 << 20,
-        14,
+        60,
         [
             pltpu.VMEM((2, 1536, 768), BF),
             pltpu.VMEM((256, 1536), BF),
             pltpu.SemaphoreType.DMA((3,)),
         ],
     )
-    swapped = other_core(jnp.concatenate([near, far], 0))
-    u2, d2 = up_z(after(u1, queries)), down_z(after(d1, queries))
+    swapped = other_core(jnp.concatenate([near, far], 1))
+    u2, d2 = up_z(after(u1, queries[0])), down_z(after(d1, queries[0]))
     v1, e1 = up_z(other), down_z(other)
 
     keys, hidden = call(
         keys_kernel,
-        [array((768, 640)), array((256, 768), F32)],
+        [array((640, 768)), array((256, 768), F32)],
         scalars() + kept() + placed(3) + kept() + whole(2),
-        (prompt_start, key_rows, near, far, swapped, key_cache, cosines, sines),
+        (prompt_start, own_keys, near, far, swapped, key_cache.T, all_cosines, all_sines),
         "keys",
         768 * 640 * 8,
         4 << 20,
         8,
-        [pltpu.VMEM((768, 576), BF), pltpu.SemaphoreType.DMA((5,))],
+        [pltpu.VMEM((576, 768), BF), pltpu.SemaphoreType.DMA((5,))],
     )
     column = jnp.arange(512, dtype=jnp.int32)
     source = (
         (column // 8 % 4) * 128 + (column // 256) * 64 + ((z + column // 32) % 8) * 8 + column % 8
     )
     reorder = (column[:, None] == source[None, :]).astype(BF)
-    rows = call(
-        attend_kernel,
-        array((256, 1024)),
-        whole(5),
-        (queries, keys, hidden, w_value_up, reorder),
-        "attend",
-        4 * 1024 * 768 * 1152 + 4 * 1024 * 512 * 128,
-        9 << 20,
-        18,
-    )
-    groups = [rows] + [xor_y(rows, q) for q in (2, 1, 3)]
-    groups = [groups[i] for i in (0, 2, 1, 3)]
-    u3 = up_z(after(jnp.concatenate([u2, v1], 0), rows))
-    d3 = down_z(after(jnp.concatenate([d2, e1], 0), rows))
+    rows = [
+        call(
+            functools.partial(attend_kernel, g),
+            array((256, 512)),
+            whole(5),
+            (queries[g], keys, hidden, w_value_up, reorder),
+            "attend",
+            2 * 1024 * 768 * 1152 + 2 * 1024 * 512 * 128,
+            5 << 20,
+            14,
+        )
+        for g in range(2)
+    ]
+    one = [xor_y(part, 1) for part in rows]
+    three = [xor_y(part, 3) for part in rows]
+    two = [xor_y(one[0], 3), xor_y(three[1], 1)]
+    groups = [*rows, *one, *two, *three]
+    u3 = up_z(after(jnp.concatenate([u2, v1], 0), rows[0]))
+    d3 = down_z(after(jnp.concatenate([d2, e1], 0), rows[0]))
     u4 = up_z(u3)
     e3 = down_z(d3[64:])
     e4 = down_z(e3)
     blocks = [own, d1, d2, d3, u4, u3, u2, u1, other, e1, e3, e4, v1]
 
-    theirs = other_core(project(1, groups, blocks, BF))
-    mine = project(0, groups, blocks, F32)
-    far_sum = (mine[2] + theirs[2].astype(F32)).astype(BF)
+    first, rest = project(1, groups, blocks, BF)
+    first, rest = other_core(first), other_core(rest)
+    mine, mine_rest = project(0, groups, blocks, F32)
+    far_sum = (mine + first.astype(F32)).astype(BF)
     passing_up = along_x(far_sum[:128], 1)
     passing_down = along_x(far_sum[128:], 3)
-    sums = [mine[d] + theirs[d].astype(F32) for d in (0, 1, 3)]
+    sums = [mine_rest[i] + rest[i].astype(F32) for i in range(3)]
     early_up, early_down = lax.optimization_barrier(
         (sums[1][128:].astype(BF), sums[2][:128].astype(BF))
     )

time: 112 us -> 110 us (0.982)
  local copies, waits for them, and re-layouts: 6.52 us -> 1.35 us
  starting transfers between devices: 47.4 us -> 51.4 us
  waiting for transfers between devices: 34.2 us -> 30.7 us
  Pallas kernels: 19.8 us -> 21.9 us
    unnamed x12, local copies, waits for them, and re-layouts: 6.09 us -> 0.03 us
    ppermute x25 -> x29, starting transfers between devices: 38.1 us -> 42.1 us  [moved(): return lax.ppermute(a, AXES, pairs)]
    ppermute x25 -> x29, waiting for transfers between devices: 34.2 us -> 30.7 us  [moved(): return lax.ppermute(a, AXES, pairs)]
    pallas_call x5 -> x6, Pallas kernels: 17.6 us -> 19.7 us  [call(): pl.pallas_call(kernel, out_shape=shapes, in_specs=specs, out_specs=whole(...]
  transfers between devices with their start and end apart: 27 -> 31, of which waited for: 11 -> 13; matrix products, arithmetic and copies ran while one was open for 2% -> 2% of each run, Pallas kernels for 16% -> 18%
where the time goes in v6:
time: 110 us; the launch traced here: 109 us
  starting transfers between devices  51.4 us (47%)
  waiting for transfers between devices  30.7 us (28%)
  Pallas kernels  21.9 us (20%)
  other arithmetic  2.98 us (3%)
  local copies, waits for them, and re-layouts  1.35 us (1%)
    ppermute x29, starting transfers between devices, moved(): return lax.ppermute(a, AXES, pairs)  42.1 us
    ppermute x29, waiting for transfers between devices, moved(): return lax.ppermute(a, AXES, pairs)  30.7 us
    pallas_call x6, Pallas kernels, call(): pl.pallas_call(kernel, out_shape=shapes, in_specs=specs, out_specs=whole(...  19.7 us
    ppermute x2, starting transfers between devices, local(): lax.ppermute(half, CTX, [(i, i + by) for i in range(16 - by)])  9.28 us
    pallas_call x1, Pallas kernels, quarters(): pl.pallas_call(quarter_kernel, out_shape=[jax.ShapeDtypeStruct((64, 1792)...  2.22 us
  transfers between devices with their start and end apart: 31, of which 13 were waited for; matrix products, arithmetic and copies ran while one was open for 2% of the time, Pallas kernels for 18%

profile of v6, /device:TPU:1, one launch (start us, length us, event | category | flops | bytes accessed | tf_op | source)
XLA Modules:
  0.0 109.3 jit_solution(13507946499978998091)
XLA Ops:
  0.0 0.9 dynamic-slice_bitcast_fusion
  0.9 5.7 %collective-permute-start.1 = (bf16[576,128]{1,0:T(8,128)(2,1)S(1)}, bf16[576,128]{1,0:T(8,128)(2,1)S(1)}, u32[]{:S(2)}, u32[]{:S(2)}) collective-permute-start(bf16[576,128]{1,0:T(8,128)(2,1)S(1)} %dynamic-slice_bitcast_fusion), channel_id=1, source_target_pairs={{0,32},{16,48},{32,64},{48,80},{64,96},{80,112},{96,128},{112,144}... | collective-permute-start | bytes 442376 | tf_op jit(solution)/shard_map/ppermute | solution.py:305
  6.7 3.5 %collective-permute-start = (bf16[576,128]{1,0:T(8,128)(2,1)S(1)}, bf16[576,128]{1,0:T(8,128)(2,1)S(1)}, u32[]{:S(2)}, u32[]{:S(2)}) collective-permute-start(bf16[576,128]{1,0:T(8,128)(2,1)S(1)} %dynamic-slice_bitcast_fusion), channel_id=1, source_target_pairs={{0,16},{16,32},{32,48},{48,64},{64,80},{80,96},{96,112},{112,128},... | collective-permute-start | bytes 442376 | tf_op jit(solution)/shard_map/ppermute | solution.py:305
  10.2 2.2 %quarters.1 = (bf16[64,1792]{1,0:T(8,128)(2,1)}, bf16[64,1792]{1,0:T(8,128)(2,1)}) custom-call(bf16[64,7168]{1,0:T(8,128)(2,1)} %bitcast.39), custom_call_target="tpu_custom_call" | custom-call | bytes 2097152 | tf_op jit(solution)/shard_map/quarters/pallas_call | solution.py:247
  12.4 2.8 %collective-permute-start.14 = (bf16[64,1792]{1,0:T(8,128)(2,1)}, bf16[64,1792]{1,0:T(8,128)(2,1)S(1)}, u32[]{:S(2)}, u32[]{:S(2)}) collective-permute-start(bf16[64,1792]{1,0:T(8,128)(2,1)} %get-tuple-element.25.refs_8_), channel_id=1, source_target_pairs={{0,16},{1,17},{2,18},{3,19},{4,20},{5,21},{6,22},{7,23},{8,24},{9,... | collective-permute-start | bytes 688136 | tf_op jit(solution)/shard_map/ppermute | solution.py:33
  15.3 0.8 collective-permute-start.9
  16.1 1.9 %collective-permute-start.11 = (bf16[64,1792]{1,0:T(8,128)(2,1)}, bf16[64,1792]{1,0:T(8,128)(2,1)S(1)}, u32[]{:S(2)}, u32[]{:S(2)}) collective-permute-start(bf16[64,1792]{1,0:T(8,128)(2,1)} %get-tuple-element.27), channel_id=1, source_target_pairs={{0,129},{1,128},{2,131},{3,130},{4,133},{5,132},{6,135},{7,134},{8... | collective-permute-start | bytes 688136 | tf_op jit(solution)/shard_map/ppermute | solution.py:33
  18.3 0.8 fusion.13
  19.1 6.9 %queries.1 = (bf16[1024,640]{1,0:T(8,128)(2,1)}, bf16[1024,640]{1,0:T(8,128)(2,1)}) custom-call(bf16[256,1536]{1,0:T(8,128)(2,1)} %rows.1, bf16[1536,1536]{1,0:T(8,128)(2,1)} %w_query.1, bf16[8,128,512]{2,1,0:T(8,128)(2,1)} %w_key_up.1, f32[64,128]{1,0:T(8,128)} %get-tuple-element.53.cosines, f32[64,128]{1,0:T(8,128)} %get-tuple-element.52.sines), custom_call_target="tpu_custom_call" | custom-call | flops 1476395008 | bytes 8388608 | tf_op jit(solution)/shard_map/queries/pallas_call | solution.py:259
  26.1 2.0 %collective-permute-start.2 = (bf16[576,256]{1,0:T(8,128)(2,1)S(1)}, bf16[576,256]{1,0:T(8,128)(2,1)S(1)}, u32[]{:S(2)}, u32[]{:S(2)}) collective-permute-start(bf16[576,256]{1,0:T(8,128)(2,1)S(1)} %pad_maximum_fusion.2), channel_id=1, source_target_pairs={{0,2},{1,3},{2,0},{3,1},{4,6},{5,7},{6,4},{7,5},{8,10},{9,11},{10,... | collective-permute-start | bytes 884744 | tf_op jit(solution)/shard_map/ppermute | solution.py:33
  28.1 1.7 %collective-permute-start.15 = (bf16[64,1792]{1,0:T(8,128)(2,1)S(1)}, bf16[64,1792]{1,0:T(8,128)(2,1)S(1)}, u32[]{:S(2)}, u32[]{:S(2)}) collective-permute-start(bf16[64,1792]{1,0:T(8,128)(2,1)S(1)} %collective-permute-done.14.refs_15_), channel_id=1, source_target_pairs={{0,16},{1,17},{2,18},{3,19},{4,20},{5,21},{6,22},{7,23},{8,24},{9,... | collective-permute-start | bytes 688136 | tf_op jit(solution)/shard_map/ppermute | solution.py:33
  29.8 0.7 collective-permute-start.16
  30.5 0.4 multiply_sine_fusion
  31.6 2.0 %collective-permute-start.10 = (bf16[64,1792]{1,0:T(8,128)(2,1)S(1)}, bf16[64,1792]{1,0:T(8,128)(2,1)S(1)}, u32[]{:S(2)}, u32[]{:S(2)}) collective-permute-start(bf16[64,1792]{1,0:T(8,128)(2,1)S(1)} %collective-permute-done.9.refs_9_), channel_id=1, source_target_pairs={{0,112},{1,113},{2,114},{3,115},{4,116},{5,117},{6,118},{7,119},{8... | collective-permute-start | bytes 688136 | tf_op jit(solution)/shard_map/ppermute | solution.py:33
  33.7 0.6 keys.1
  34.3 3.8 %attend.2.refs_0_ = bf16[256,512]{1,0:T(8,128)(2,1)S(1)} custom-call(bf16[1024,640]{1,0:T(8,128)(2,1)S(1)} %copy-done.3, bf16[640,768]{1,0:T(8,128)(2,1)S(1)} %get-tuple-element.22.keys, f32[256,768]{1,0:T(8,128)S(1)} %get-tuple-element.23.hidden, bf16[8,512,128]{2,1,0:T(8,128)(2,1)S(1)} %copy-done.4, bf16[512,512]{1,0:T(8,128)(2,1)S(1)} %fusion.reorder), custom_call_target="tpu_custom_call" | custom-call | flops 1946157056 | bytes 5242880 | tf_op jit(solution)/shard_map/attend/pallas_call | solution.py:259
  38.1 3.3 %collective-permute-done.16.refs_20_ = bf16[64,1792]{1,0:T(8,128)(2,1)S(1)} collective-permute-done((bf16[64,1792]{1,0:T(8,128)(2,1)S(1)}, bf16[64,1792]{1,0:T(8,128)(2,1)S(1)}, u32[]{:S(2)}, u32[]{:S(2)}) %collective-permute-start.16) | collective-permute-done | bytes 229408 | tf_op jit(solution)/shard_map/ppermute | solution.py:33
  41.4 1.7 %collective-permute-done.12.refs_17_ = bf16[64,1792]{1,0:T(8,128)(2,1)S(1)} collective-permute-done((bf16[64,1792]{1,0:T(8,128)(2,1)S(1)}, bf16[64,1792]{1,0:T(8,128)(2,1)S(1)}, u32[]{:S(2)}, u32[]{:S(2)}) %collective-permute-start.12) | collective-permute-done | bytes 229408 | tf_op jit(solution)/shard_map/ppermute | solution.py:33
  43.1 3.2 %collective-permute-start.13 = (bf16[128,1792]{1,0:T(8,128)(2,1)S(1)}, bf16[128,1792]{1,0:T(8,128)(2,1)S(1)}, u32[]{:S(2)}, u32[]{:S(2)}) collective-permute-start(bf16[128,1792]{1,0:T(8,128)(2,1)S(1)} %pad_maximum_fusion), channel_id=1, source_target_pairs={{0,112},{1,113},{2,114},{3,115},{4,116},{5,117},{6,118},{7,119},{8... | collective-permute-start | bytes 1376264 | tf_op jit(solution)/shard_map/ppermute | solution.py:33
  46.4 3.8 %attend.3.refs_1_ = bf16[256,512]{1,0:T(8,128)(2,1)S(1)} custom-call(bf16[1024,640]{1,0:T(8,128)(2,1)S(1)} %copy-done.2, bf16[640,768]{1,0:T(8,128)(2,1)S(1)} %get-tuple-element.22.keys, f32[256,768]{1,0:T(8,128)S(1)} %get-tuple-element.23.hidden, bf16[8,512,128]{2,1,0:T(8,128)(2,1)S(1)} %copy-done.4, bf16[512,512]{1,0:T(8,128)(2,1)S(1)} %fusion.reorder), custom_call_target="tpu_custom_call" | custom-call | flops 1946157056 | bytes 5242880 | tf_op jit(solution)/shard_map/attend/pallas_call | solution.py:259
  50.2 2.7 %collective-permute-start.6 = (bf16[256,512]{1,0:T(8,128)(2,1)S(1)}, bf16[256,512]{1,0:T(8,128)(2,1)S(1)}, u32[]{:S(2)}, u32[]{:S(2)}) collective-permute-start(bf16[256,512]{1,0:T(8,128)(2,1)S(1)} %attend.3.refs_1_), channel_id=1, source_target_pairs={{0,129},{1,128},{2,131},{3,130},{4,133},{5,132},{6,135},{7,134},{8... | collective-permute-start | bytes 786440 | tf_op jit(solution)/shard_map/ppermute | solution.py:33
  52.9 1.7 %collective-permute-done.13.refs_11_ = bf16[128,1792]{1,0:T(8,128)(2,1)S(1)} collective-permute-done((bf16[128,1792]{1,0:T(8,128)(2,1)S(1)}, bf16[128,1792]{1,0:T(8,128)(2,1)S(1)}, u32[]{:S(2)}, u32[]{:S(2)}) %collective-permute-start.13) | collective-permute-done | bytes 458784 | tf_op jit(solution)/shard_map/ppermute | solution.py:33
  54.7 3.5 %collective-permute-start.19 = (bf16[64,1792]{1,0:T(8,128)(2,1)S(1)}, bf16[64,1792]{1,0:T(8,128)(2,1)S(1)}, u32[]{:S(2)}, u32[]{:S(2)}) collective-permute-start(bf16[64,1792]{1,0:T(8,128)(2,1)S(1)} %slice.96), channel_id=1, source_target_pairs={{0,112},{1,113},{2,114},{3,115},{4,116},{5,117},{6,118},{7,119},{8... | collective-permute-start | bytes 688136 | tf_op jit(solution)/shard_map/ppermute | solution.py:33
  58.3 0.6 collective-permute-start.5
  58.9 1.0 collective-permute-done.6.refs_7_
  59.8 0.2 collective-permute-start.7
  60.0 1.1 collective-permute-done.19.refs_18_
  61.1 3.1 %collective-permute-start.20 = (bf16[64,1792]{1,0:T(8,128)(2,1)S(1)}, bf16[64,1792]{1,0:T(8,128)(2,1)S(1)}, u32[]{:S(2)}, u32[]{:S(2)}) collective-permute-start(bf16[64,1792]{1,0:T(8,128)(2,1)S(1)} %collective-permute-done.19.refs_18_), channel_id=1, source_target_pairs={{0,112},{1,113},{2,114},{3,115},{4,116},{5,117},{6,118},{7,119},{8... | collective-permute-start | bytes 688136 | tf_op jit(solution)/shard_map/ppermute | solution.py:33
  64.2 0.6 collective-permute-done.5.refs_4_
  64.8 4.2 %collective-permute-done.7.refs_5_ = bf16[256,512]{1,0:T(8,128)(2,1)S(1)} collective-permute-done((bf16[256,512]{1,0:T(8,128)(2,1)S(1)}, bf16[256,512]{1,0:T(8,128)(2,1)S(1)}, u32[]{:S(2)}, u32[]{:S(2)}) %collective-permute-start.7) | collective-permute-done | bytes 262176 | tf_op jit(solution)/shard_map/ppermute | solution.py:33
  69.0 2.3 %project.3 = (bf16[256,896]{1,0:T(8,128)(2,1)S(1)}, bf16[3,256,896]{2,1,0:T(8,128)(2,1)S(1)}) custom-call(bf16[256,512]{1,0:T(8,128)(2,1)S(1)} %attend.2.refs_0_, bf16[256,512]{1,0:T(8,128)(2,1)S(1)} %attend.3.refs_1_, bf16[256,512]{1,0:T(8,128)(2,1)S(1)} %collective-permute-done.3.refs_2_, bf16[256,512]{1,0:T(8,128)(2,1)S(1)} %collective-permute-done.4.refs_3_, ...), custom_call_target="tpu_custom_call" | custom-call | flops 1879048192 | bytes 8388608 | tf_op jit(solution)/shard_map/project/pallas_call | solution.py:259
  71.3 3.7 %collective-permute-start.21 = (bf16[3,256,896]{2,1,0:T(8,128)(2,1)S(1)}, bf16[3,256,896]{2,1,0:T(8,128)(2,1)S(1)}, u32[]{:S(2)}, u32[]{:S(2)}) collective-permute-start(bf16[3,256,896]{2,1,0:T(8,128)(2,1)S(1)} %get-tuple-element.32), channel_id=1, source_target_pairs={{0,2},{1,3},{2,0},{3,1},{4,6},{5,7},{6,4},{7,5},{8,10},{9,11},{10,... | collective-permute-start | bytes 4128776 | tf_op jit(solution)/shard_map/ppermute | solution.py:33
  75.1 2.3 %project.2 = (f32[256,896]{1,0:T(8,128)S(1)}, f32[3,256,896]{2,1,0:T(8,128)S(1)}) custom-call(bf16[256,512]{1,0:T(8,128)(2,1)S(1)} %attend.2.refs_0_, bf16[256,512]{1,0:T(8,128)(2,1)S(1)} %attend.3.refs_1_, bf16[256,512]{1,0:T(8,128)(2,1)S(1)} %collective-permute-done.3.refs_2_, bf16[256,512]{1,0:T(8,128)(2,1)S(1)} %collective-permute-done.4.refs_3_, ...), custom_call_target="tpu_custom_call" | custom-call | flops 1879048192 | bytes 8388608 | tf_op jit(solution)/shard_map/project/pallas_call | solution.py:259
  77.4 1.0 collective-permute-done.22
  78.5 1.3 %collective-permute-start.23 = (bf16[128,896]{1,0:T(8,128)(2,1)S(1)}, bf16[128,896]{1,0:T(8,128)(2,1)S(1)}, u32[]{:S(2)}, u32[]{:S(2)}) collective-permute-start(bf16[128,896]{1,0:T(8,128)(2,1)S(1)} %get-tuple-element.44), channel_id=1, source_target_pairs={{0,4},{1,5},{2,6},{3,7},{4,8},{5,9},{6,10},{7,11},{8,12},{9,13},{1... | collective-permute-start | bytes 688136 | tf_op jit(solution)/shard_map/ppermute | solution.py:33
  79.8 1.5 %collective-permute-start.28 = (bf16[128,896]{1,0:T(8,128)(2,1)S(1)}, bf16[128,896]{1,0:T(8,128)(2,1)S(1)}, u32[]{:S(2)}, u32[]{:S(2)}) collective-permute-start(bf16[128,896]{1,0:T(8,128)(2,1)S(1)} %get-tuple-element.45), channel_id=1, source_target_pairs={{0,12},{1,13},{2,14},{3,15},{4,0},{5,1},{6,2},{7,3},{8,4},{9,5},{1... | collective-permute-start | bytes 688136 | tf_op jit(solution)/shard_map/ppermute | solution.py:33
  81.3 0.2 convert_add_fusion.1
  81.6 1.3 %collective-permute-start.25 = (bf16[128,896]{1,0:T(8,128)(2,1)S(1)}, bf16[128,896]{1,0:T(8,128)(2,1)S(1)}, u32[]{:S(2)}, u32[]{:S(2)}) collective-permute-start(bf16[128,896]{1,0:T(8,128)(2,1)S(1)} %fusion.12), channel_id=1, source_target_pairs={{0,12},{1,13},{2,14},{3,15},{4,0},{5,1},{6,2},{7,3},{8,4},{9,5},{1... | collective-permute-start | bytes 688136 | tf_op jit(solution)/shard_map/ppermute | solution.py:33
  83.0 0.2 collective-permute-start.27
  83.1 3.2 %collective-permute-done.28 = bf16[128,896]{1,0:T(8,128)(2,1)S(1)} collective-permute-done((bf16[128,896]{1,0:T(8,128)(2,1)S(1)}, bf16[128,896]{1,0:T(8,128)(2,1)S(1)}, u32[]{:S(2)}, u32[]{:S(2)}) %collective-permute-start.28) | collective-permute-done | bytes 229408 | tf_op jit(solution)/shard_map/ppermute | solution.py:33
  86.4 2.8 %collective-permute-start.29 = (bf16[128,896]{1,0:T(8,128)(2,1)S(1)}, bf16[128,896]{1,0:T(8,128)(2,1)S(1)}, u32[]{:S(2)}, u32[]{:S(2)}) collective-permute-start(bf16[128,896]{1,0:T(8,128)(2,1)S(1)} %fusion.2), channel_id=1, source_target_pairs={{0,12},{1,13},{2,14},{3,15},{4,0},{5,1},{6,2},{7,3},{8,4},{9,5},{1... | collective-permute-start | bytes 688136 | tf_op jit(solution)/shard_map/ppermute | solution.py:33
  89.3 2.0 %collective-permute-done.25 = bf16[128,896]{1,0:T(8,128)(2,1)S(1)} collective-permute-done((bf16[128,896]{1,0:T(8,128)(2,1)S(1)}, bf16[128,896]{1,0:T(8,128)(2,1)S(1)}, u32[]{:S(2)}, u32[]{:S(2)}) %collective-permute-start.25) | collective-permute-done | bytes 229408 | tf_op jit(solution)/shard_map/ppermute | solution.py:33
  91.2 4.9 %collective-permute-done.29 = bf16[128,896]{1,0:T(8,128)(2,1)S(1)} collective-permute-done((bf16[128,896]{1,0:T(8,128)(2,1)S(1)}, bf16[128,896]{1,0:T(8,128)(2,1)S(1)}, u32[]{:S(2)}, u32[]{:S(2)}) %collective-permute-start.29) | collective-permute-done | bytes 229408 | tf_op jit(solution)/shard_map/ppermute | solution.py:33
  96.2 0.2 fusion.10
  96.3 5.5 %collective-permute-start.26 = (bf16[128,896]{1,0:T(8,128)(2,1)S(1)}, bf16[128,896]{1,0:T(8,128)(2,1)S(1)}, u32[]{:S(2)}, u32[]{:S(2)}) collective-permute-start(bf16[128,896]{1,0:T(8,128)(2,1)S(1)} %get-tuple-element.40), channel_id=1, source_target_pairs={{0,0},{1,1},{2,128},{3,129},{4,4},{5,5},{6,132},{7,133},{8,8},{9,9... | collective-permute-start | bytes 688136 | tf_op jit(solution)/shard_map/ppermute | solution.py:33
  101.9 4.3 %collective-permute-done.26 = bf16[128,896]{1,0:T(8,128)(2,1)S(1)} collective-permute-done((bf16[128,896]{1,0:T(8,128)(2,1)S(1)}, bf16[128,896]{1,0:T(8,128)(2,1)S(1)}, u32[]{:S(2)}, u32[]{:S(2)}) %collective-permute-start.26) | collective-permute-done | bytes 229408 | tf_op jit(solution)/shard_map/ppermute | solution.py:33
  106.2 1.9 %collective-permute-done.30 = bf16[128,896]{1,0:T(8,128)(2,1)S(1)} collective-permute-done((bf16[128,896]{1,0:T(8,128)(2,1)S(1)}, bf16[128,896]{1,0:T(8,128)(2,1)S(1)}, u32[]{:S(2)}, u32[]{:S(2)}) %collective-permute-start.30) | collective-permute-done | bytes 229408 | tf_op jit(solution)/shard_map/ppermute | solution.py:33
  108.4 0.9 maximum_maximum_fusion
  (60 shorter events, 1.4 us)
Async XLA Ops:
  0.9 25.1 %collective-permute-start.1 = (bf16[576,128]{1,0:T(8,128)(2,1)S(1)}, bf16[576,128]{1,0:T(8,128)(2,1)S(1)}, u32[]{:S(2)}, u32[]{:S(2)}) collective-permute-start(bf16[576,128]{1,0:T(8,128)(2,1)S(1)} %dynamic-slice_bitcast_fusion), channel_id=1, source_target_pairs={{0,32},{16,48},{32,64},{48,80},{64,96},{80,112},{96,128},{112,144}... | collective-permute-start | bytes 442376 | tf_op jit(solution)/shard_map/ppermute | solution.py:305
  6.7 19.4 %collective-permute-start = (bf16[576,128]{1,0:T(8,128)(2,1)S(1)}, bf16[576,128]{1,0:T(8,128)(2,1)S(1)}, u32[]{:S(2)}, u32[]{:S(2)}) collective-permute-start(bf16[576,128]{1,0:T(8,128)(2,1)S(1)} %dynamic-slice_bitcast_fusion), channel_id=1, source_target_pairs={{0,16},{16,32},{32,48},{48,64},{64,80},{80,96},{96,112},{112,128},... | collective-permute-start | bytes 442376 | tf_op jit(solution)/shard_map/ppermute | solution.py:305
  12.4 15.6 %collective-permute-start.14 = (bf16[64,1792]{1,0:T(8,128)(2,1)}, bf16[64,1792]{1,0:T(8,128)(2,1)S(1)}, u32[]{:S(2)}, u32[]{:S(2)}) collective-permute-start(bf16[64,1792]{1,0:T(8,128)(2,1)} %get-tuple-element.25.refs_8_), channel_id=1, source_target_pairs={{0,16},{1,17},{2,18},{3,19},{4,20},{5,21},{6,22},{7,23},{8,24},{9,... | collective-permute-start | bytes 688136 | tf_op jit(solution)/shard_map/ppermute | solution.py:33
  15.3 16.3 %collective-permute-start.9 = (bf16[64,1792]{1,0:T(8,128)(2,1)}, bf16[64,1792]{1,0:T(8,128)(2,1)S(1)}, u32[]{:S(2)}, u32[]{:S(2)}) collective-permute-start(bf16[64,1792]{1,0:T(8,128)(2,1)} %get-tuple-element.25.refs_8_), channel_id=1, source_target_pairs={{0,112},{1,113},{2,114},{3,115},{4,116},{5,117},{6,118},{7,119},{8... | collective-permute-start | bytes 688136 | tf_op jit(solution)/shard_map/ppermute | solution.py:33
  16.1 13.6 %collective-permute-start.11 = (bf16[64,1792]{1,0:T(8,128)(2,1)}, bf16[64,1792]{1,0:T(8,128)(2,1)S(1)}, u32[]{:S(2)}, u32[]{:S(2)}) collective-permute-start(bf16[64,1792]{1,0:T(8,128)(2,1)} %get-tuple-element.27), channel_id=1, source_target_pairs={{0,129},{1,128},{2,131},{3,130},{4,133},{5,132},{6,135},{7,134},{8... | collective-permute-start | bytes 688136 | tf_op jit(solution)/shard_map/ppermute | solution.py:33
  19.1 14.6 %copy-start = (bf16[256,576]{0,1:T(8,128)(2,1)S(1)}, bf16[256,576]{0,1:T(8,128)(2,1)}, u32[]{:S(2)}) copy-start(bf16[256,576]{0,1:T(8,128)(2,1)} %param.9) | copy-start | bytes 884740
  19.1 14.6 %copy-start.1 = (bf16[512,576]{0,1:T(8,128)(2,1)S(1)}, bf16[512,576]{0,1:T(8,128)(2,1)}, u32[]{:S(2)}) copy-start(bf16[512,576]{0,1:T(8,128)(2,1)} %param.10) | copy-start | bytes 1769476
  26.0 8.3 %copy-start.3 = (bf16[1024,640]{1,0:T(8,128)(2,1)S(1)}, bf16[1024,640]{1,0:T(8,128)(2,1)}, u32[]{:S(2)}) copy-start(bf16[1024,640]{1,0:T(8,128)(2,1)} %get-tuple-element.21.queries) | copy-start | bytes 3932164
  26.0 8.3 %copy-start.4 = (bf16[8,512,128]{2,1,0:T(8,128)(2,1)S(1)}, bf16[8,512,128]{2,1,0:T(8,128)(2,1)}, u32[]{:S(2)}) copy-start(bf16[8,512,128]{2,1,0:T(8,128)(2,1)} %w_value_up.3) | copy-start | bytes 3145732
  26.1 7.6 %collective-permute-start.2 = (bf16[576,256]{1,0:T(8,128)(2,1)S(1)}, bf16[576,256]{1,0:T(8,128)(2,1)S(1)}, u32[]{:S(2)}, u32[]{:S(2)}) collective-permute-start(bf16[576,256]{1,0:T(8,128)(2,1)S(1)} %pad_maximum_fusion.2), channel_id=1, source_target_pairs={{0,2},{1,3},{2,0},{3,1},{4,6},{5,7},{6,4},{7,5},{8,10},{9,11},{10,... | collective-permute-start | bytes 884744 | tf_op jit(solution)/shard_map/ppermute | solution.py:33
  28.1 13.3 %collective-permute-start.15 = (bf16[64,1792]{1,0:T(8,128)(2,1)S(1)}, bf16[64,1792]{1,0:T(8,128)(2,1)S(1)}, u32[]{:S(2)}, u32[]{:S(2)}) collective-permute-start(bf16[64,1792]{1,0:T(8,128)(2,1)S(1)} %collective-permute-done.14.refs_15_), channel_id=1, source_target_pairs={{0,16},{1,17},{2,18},{3,19},{4,20},{5,21},{6,22},{7,23},{8,24},{9,... | collective-permute-start | bytes 688136 | tf_op jit(solution)/shard_map/ppermute | solution.py:33
  29.8 11.6 %collective-permute-start.16 = (bf16[64,1792]{1,0:T(8,128)(2,1)S(1)}, bf16[64,1792]{1,0:T(8,128)(2,1)S(1)}, u32[]{:S(2)}, u32[]{:S(2)}) collective-permute-start(bf16[64,1792]{1,0:T(8,128)(2,1)S(1)} %collective-permute-done.11.refs_16_), channel_id=1, source_target_pairs={{0,16},{1,17},{2,18},{3,19},{4,20},{5,21},{6,22},{7,23},{8,24},{9,... | collective-permute-start | bytes 688136 | tf_op jit(solution)/shard_map/ppermute | solution.py:33
  31.6 11.5 %collective-permute-start.10 = (bf16[64,1792]{1,0:T(8,128)(2,1)S(1)}, bf16[64,1792]{1,0:T(8,128)(2,1)S(1)}, u32[]{:S(2)}, u32[]{:S(2)}) collective-permute-start(bf16[64,1792]{1,0:T(8,128)(2,1)S(1)} %collective-permute-done.9.refs_9_), channel_id=1, source_target_pairs={{0,112},{1,113},{2,114},{3,115},{4,116},{5,117},{6,118},{7,119},{8... | collective-permute-start | bytes 688136 | tf_op jit(solution)/shard_map/ppermute | solution.py:33
  33.6 9.5 %collective-permute-start.12 = (bf16[64,1792]{1,0:T(8,128)(2,1)S(1)}, bf16[64,1792]{1,0:T(8,128)(2,1)S(1)}, u32[]{:S(2)}, u32[]{:S(2)}) collective-permute-start(bf16[64,1792]{1,0:T(8,128)(2,1)S(1)} %collective-permute-done.11.refs_16_), channel_id=1, source_target_pairs={{0,112},{1,113},{2,114},{3,115},{4,116},{5,117},{6,118},{7,119},{8... | collective-permute-start | bytes 688136 | tf_op jit(solution)/shard_map/ppermute | solution.py:33
  38.1 8.3 %copy-start.2 = (bf16[1024,640]{1,0:T(8,128)(2,1)S(1)}, bf16[1024,640]{1,0:T(8,128)(2,1)}, u32[]{:S(2)}) copy-start(bf16[1024,640]{1,0:T(8,128)(2,1)} %get-tuple-element.24.queries) | copy-start | bytes 3932164
  43.1 11.5 %collective-permute-start.13 = (bf16[128,1792]{1,0:T(8,128)(2,1)S(1)}, bf16[128,1792]{1,0:T(8,128)(2,1)S(1)}, u32[]{:S(2)}, u32[]{:S(2)}) collective-permute-start(bf16[128,1792]{1,0:T(8,128)(2,1)S(1)} %pad_maximum_fusion), channel_id=1, source_target_pairs={{0,112},{1,113},{2,114},{3,115},{4,116},{5,117},{6,118},{7,119},{8... | collective-permute-start | bytes 1376264 | tf_op jit(solution)/shard_map/ppermute | solution.py:33
  46.3 11.8 %collective-permute-start.17 = (bf16[128,1792]{1,0:T(8,128)(2,1)S(1)}, bf16[128,1792]{1,0:T(8,128)(2,1)S(1)}, u32[]{:S(2)}, u32[]{:S(2)}) collective-permute-start(bf16[128,1792]{1,0:T(8,128)(2,1)S(1)} %pad_maximum_fusion.1), channel_id=1, source_target_pairs={{0,16},{1,17},{2,18},{3,19},{4,20},{5,21},{6,22},{7,23},{8,24},{9,... | collective-permute-start | bytes 1376264 | tf_op jit(solution)/shard_map/ppermute | solution.py:33
  46.3 11.8 %collective-permute-start.8 = (bf16[256,512]{1,0:T(8,128)(2,1)S(1)}, bf16[256,512]{1,0:T(8,128)(2,1)S(1)}, u32[]{:S(2)}, u32[]{:S(2)}) collective-permute-start(bf16[256,512]{1,0:T(8,128)(2,1)S(1)} %attend.2.refs_0_), channel_id=1, source_target_pairs={{0,129},{1,128},{2,131},{3,130},{4,133},{5,132},{6,135},{7,134},{8... | collective-permute-start | bytes 786440 | tf_op jit(solution)/shard_map/ppermute | solution.py:33
  46.4 11.9 %collective-permute-start.3 = (bf16[256,512]{1,0:T(8,128)(2,1)S(1)}, bf16[256,512]{1,0:T(8,128)(2,1)S(1)}, u32[]{:S(2)}, u32[]{:S(2)}) collective-permute-start(bf16[256,512]{1,0:T(8,128)(2,1)S(1)} %attend.2.refs_0_), channel_id=1, source_target_pairs={{0,1},{1,0},{2,3},{3,2},{4,5},{5,4},{6,7},{7,6},{8,9},{9,8},{10,11... | collective-permute-start | bytes 786440 | tf_op jit(solution)/shard_map/ppermute | solution.py:33
  46.4 22.6 %copy-start.5 = (bf16[64,1792]{1,0:T(8,128)(2,1)S(1)}, bf16[64,1792]{1,0:T(8,128)(2,1)}, u32[]{:S(2)}) copy-start(bf16[64,1792]{1,0:T(8,128)(2,1)} %get-tuple-element.25.refs_8_) | copy-start | bytes 688132
  50.2 9.7 %collective-permute-start.6 = (bf16[256,512]{1,0:T(8,128)(2,1)S(1)}, bf16[256,512]{1,0:T(8,128)(2,1)S(1)}, u32[]{:S(2)}, u32[]{:S(2)}) collective-permute-start(bf16[256,512]{1,0:T(8,128)(2,1)S(1)} %attend.3.refs_1_), channel_id=1, source_target_pairs={{0,129},{1,128},{2,131},{3,130},{4,133},{5,132},{6,135},{7,134},{8... | collective-permute-start | bytes 786440 | tf_op jit(solution)/shard_map/ppermute | solution.py:33
  54.7 6.5 %collective-permute-start.19 = (bf16[64,1792]{1,0:T(8,128)(2,1)S(1)}, bf16[64,1792]{1,0:T(8,128)(2,1)S(1)}, u32[]{:S(2)}, u32[]{:S(2)}) collective-permute-start(bf16[64,1792]{1,0:T(8,128)(2,1)S(1)} %slice.96), channel_id=1, source_target_pairs={{0,112},{1,113},{2,114},{3,115},{4,116},{5,117},{6,118},{7,119},{8... | collective-permute-start | bytes 688136 | tf_op jit(solution)/shard_map/ppermute | solution.py:33
  58.2 10.8 %collective-permute-start.18 = (bf16[128,1792]{1,0:T(8,128)(2,1)S(1)}, bf16[128,1792]{1,0:T(8,128)(2,1)S(1)}, u32[]{:S(2)}, u32[]{:S(2)}) collective-permute-start(bf16[128,1792]{1,0:T(8,128)(2,1)S(1)} %collective-permute-done.17.refs_13_), channel_id=1, source_target_pairs={{0,16},{1,17},{2,18},{3,19},{4,20},{5,21},{6,22},{7,23},{8,24},{9,... | collective-permute-start | bytes 1376264 | tf_op jit(solution)/shard_map/ppermute | solution.py:33
  58.2 6.1 %collective-permute-start.4 = (bf16[256,512]{1,0:T(8,128)(2,1)S(1)}, bf16[256,512]{1,0:T(8,128)(2,1)S(1)}, u32[]{:S(2)}, u32[]{:S(2)}) collective-permute-start(bf16[256,512]{1,0:T(8,128)(2,1)S(1)} %attend.3.refs_1_), channel_id=1, source_target_pairs={{0,1},{1,0},{2,3},{3,2},{4,5},{5,4},{6,7},{7,6},{8,9},{9,8},{10,11... | collective-permute-start | bytes 786440 | tf_op jit(solution)/shard_map/ppermute | solution.py:33
  58.3 6.5 %collective-permute-start.5 = (bf16[256,512]{1,0:T(8,128)(2,1)S(1)}, bf16[256,512]{1,0:T(8,128)(2,1)S(1)}, u32[]{:S(2)}, u32[]{:S(2)}) collective-permute-start(bf16[256,512]{1,0:T(8,128)(2,1)S(1)} %collective-permute-done.3.refs_2_), channel_id=1, source_target_pairs={{0,129},{1,128},{2,131},{3,130},{4,133},{5,132},{6,135},{7,134},{8... | collective-permute-start | bytes 786440 | tf_op jit(solution)/shard_map/ppermute | solution.py:33
  59.8 9.1 %collective-permute-start.7 = (bf16[256,512]{1,0:T(8,128)(2,1)S(1)}, bf16[256,512]{1,0:T(8,128)(2,1)S(1)}, u32[]{:S(2)}, u32[]{:S(2)}) collective-permute-start(bf16[256,512]{1,0:T(8,128)(2,1)S(1)} %collective-permute-done.6.refs_7_), channel_id=1, source_target_pairs={{0,1},{1,0},{2,3},{3,2},{4,5},{5,4},{6,7},{7,6},{8,9},{9,8},{10,11... | collective-permute-start | bytes 786440 | tf_op jit(solution)/shard_map/ppermute | solution.py:33
  61.1 7.8 %collective-permute-start.20 = (bf16[64,1792]{1,0:T(8,128)(2,1)S(1)}, bf16[64,1792]{1,0:T(8,128)(2,1)S(1)}, u32[]{:S(2)}, u32[]{:S(2)}) collective-permute-start(bf16[64,1792]{1,0:T(8,128)(2,1)S(1)} %collective-permute-done.19.refs_18_), channel_id=1, source_target_pairs={{0,112},{1,113},{2,114},{3,115},{4,116},{5,117},{6,118},{7,119},{8... | collective-permute-start | bytes 688136 | tf_op jit(solution)/shard_map/ppermute | solution.py:33
  71.3 10.0 %collective-permute-start.21 = (bf16[3,256,896]{2,1,0:T(8,128)(2,1)S(1)}, bf16[3,256,896]{2,1,0:T(8,128)(2,1)S(1)}, u32[]{:S(2)}, u32[]{:S(2)}) collective-permute-start(bf16[3,256,896]{2,1,0:T(8,128)(2,1)S(1)} %get-tuple-element.32), channel_id=1, source_target_pairs={{0,2},{1,3},{2,0},{3,1},{4,6},{5,7},{6,4},{7,5},{8,10},{9,11},{10,... | collective-permute-start | bytes 4128776 | tf_op jit(solution)/shard_map/ppermute | solution.py:33
  75.0 3.4 %collective-permute-start.22 = (bf16[256,896]{1,0:T(8,128)(2,1)S(1)}, bf16[256,896]{1,0:T(8,128)(2,1)S(1)}, u32[]{:S(2)}, u32[]{:S(2)}) collective-permute-start(bf16[256,896]{1,0:T(8,128)(2,1)S(1)} %get-tuple-element.34), channel_id=1, source_target_pairs={{0,2},{1,3},{2,0},{3,1},{4,6},{5,7},{6,4},{7,5},{8,10},{9,11},{10,... | collective-permute-start | bytes 1376264 | tf_op jit(solution)/shard_map/ppermute | solution.py:33
  78.5 10.6 %collective-permute-start.23 = (bf16[128,896]{1,0:T(8,128)(2,1)S(1)}, bf16[128,896]{1,0:T(8,128)(2,1)S(1)}, u32[]{:S(2)}, u32[]{:S(2)}) collective-permute-start(bf16[128,896]{1,0:T(8,128)(2,1)S(1)} %get-tuple-element.44), channel_id=1, source_target_pairs={{0,4},{1,5},{2,6},{3,7},{4,8},{5,9},{6,10},{7,11},{8,12},{9,13},{1... | collective-permute-start | bytes 688136 | tf_op jit(solution)/shard_map/ppermute | solution.py:33
  79.8 6.5 %collective-permute-start.28 = (bf16[128,896]{1,0:T(8,128)(2,1)S(1)}, bf16[128,896]{1,0:T(8,128)(2,1)S(1)}, u32[]{:S(2)}, u32[]{:S(2)}) collective-permute-start(bf16[128,896]{1,0:T(8,128)(2,1)S(1)} %get-tuple-element.45), channel_id=1, source_target_pairs={{0,12},{1,13},{2,14},{3,15},{4,0},{5,1},{6,2},{7,3},{8,4},{9,5},{1... | collective-permute-start | bytes 688136 | tf_op jit(solution)/shard_map/ppermute | solution.py:33
  81.6 9.6 %collective-permute-start.25 = (bf16[128,896]{1,0:T(8,128)(2,1)S(1)}, bf16[128,896]{1,0:T(8,128)(2,1)S(1)}, u32[]{:S(2)}, u32[]{:S(2)}) collective-permute-start(bf16[128,896]{1,0:T(8,128)(2,1)S(1)} %fusion.12), channel_id=1, source_target_pairs={{0,12},{1,13},{2,14},{3,15},{4,0},{5,1},{6,2},{7,3},{8,4},{9,5},{1... | collective-permute-start | bytes 688136 | tf_op jit(solution)/shard_map/ppermute | solution.py:33
  83.0 8.3 %collective-permute-start.27 = (bf16[128,896]{1,0:T(8,128)(2,1)S(1)}, bf16[128,896]{1,0:T(8,128)(2,1)S(1)}, u32[]{:S(2)}, u32[]{:S(2)}) collective-permute-start(bf16[128,896]{1,0:T(8,128)(2,1)S(1)} %fusion.11), channel_id=1, source_target_pairs={{0,4},{1,5},{2,6},{3,7},{4,8},{5,9},{6,10},{7,11},{8,12},{9,13},{1... | collective-permute-start | bytes 688136 | tf_op jit(solution)/shard_map/ppermute | solution.py:33
  86.4 9.8 %collective-permute-start.29 = (bf16[128,896]{1,0:T(8,128)(2,1)S(1)}, bf16[128,896]{1,0:T(8,128)(2,1)S(1)}, u32[]{:S(2)}, u32[]{:S(2)}) collective-permute-start(bf16[128,896]{1,0:T(8,128)(2,1)S(1)} %fusion.2), channel_id=1, source_target_pairs={{0,12},{1,13},{2,14},{3,15},{4,0},{5,1},{6,2},{7,3},{8,4},{9,5},{1... | collective-permute-start | bytes 688136 | tf_op jit(solution)/shard_map/ppermute | solution.py:33
  89.2 7.0 %collective-permute-start.24 = (bf16[128,896]{1,0:T(8,128)(2,1)S(1)}, bf16[128,896]{1,0:T(8,128)(2,1)S(1)}, u32[]{:S(2)}, u32[]{:S(2)}) collective-permute-start(bf16[128,896]{1,0:T(8,128)(2,1)S(1)} %fusion.7), channel_id=1, source_target_pairs={{0,4},{1,5},{2,6},{3,7},{4,8},{5,9},{6,10},{7,11},{8,12},{9,13},{1... | collective-permute-start | bytes 688136 | tf_op jit(solution)/shard_map/ppermute | solution.py:33
  96.3 9.9 %collective-permute-start.26 = (bf16[128,896]{1,0:T(8,128)(2,1)S(1)}, bf16[128,896]{1,0:T(8,128)(2,1)S(1)}, u32[]{:S(2)}, u32[]{:S(2)}) collective-permute-start(bf16[128,896]{1,0:T(8,128)(2,1)S(1)} %get-tuple-element.40), channel_id=1, source_target_pairs={{0,0},{1,1},{2,128},{3,129},{4,4},{5,5},{6,132},{7,133},{8,8},{9,9... | collective-permute-start | bytes 688136 | tf_op jit(solution)/shard_map/ppermute | solution.py:33
  101.8 6.3 %collective-permute-start.30 = (bf16[128,896]{1,0:T(8,128)(2,1)S(1)}, bf16[128,896]{1,0:T(8,128)(2,1)S(1)}, u32[]{:S(2)}, u32[]{:S(2)}) collective-permute-start(bf16[128,896]{1,0:T(8,128)(2,1)S(1)} %get-tuple-element.41), channel_id=1, source_target_pairs={{0,1},{1,0},{2,129},{3,128},{4,5},{5,4},{6,133},{7,132},{8,9},{9,8... | collective-permute-start | bytes 688136 | tf_op jit(solution)/shard_map/ppermute | solution.py:33

commit v7 on v6

--- a/solution.py
+++ b/solution.py
@@ -69,28 +69,36 @@
     return jnp.concatenate([rot, jnp.zeros_like(rot)], 1).astype(BF)
 
 
-def queries_kernel(rows, w_query, w_key_up, cosines, sines, out, out_next, held, rows_held, sem):
+def queries_kernel(
+    rows, w_query, w_key_up, cosines, sines, out, out_next, w_held, rows_held, up_held, total, sem
+):
     copies = [
-        pltpu.make_async_copy(w_query.at[:, pl.ds(768 * part, 768)], held.at[part], sem.at[part])
-        for part in range(2)
+        pltpu.make_async_copy(
+            w_query.at[pl.ds(384 * part, 384)], w_held.at[pl.ds(384 * part, 384)], sem.at[part]
+        )
+        for part in range(4)
     ]
-    copies.append(pltpu.make_async_copy(rows, rows_held, sem.at[2]))
-    for i in (2, 0, 1):
+    copies.append(pltpu.make_async_copy(rows, rows_held, sem.at[4]))
+    copies.append(pltpu.make_async_copy(w_key_up, up_held, sem.at[5]))
+    for i in (4, 0, 1, 2, 3, 5):
         copies[i].start()
     cosine, sine = turn_of(cosines), turn_of(sines)
-    copies[2].wait()
-    for part in range(2):
+    copies[4].wait()
+    for part in range(4):
         copies[part].wait()
-        queries = jnp.dot(rows_held[...], held[part], preferred_element_type=F32).astype(BF)
-        for i in range(4):
-            h = 4 * part + i
-            plain = queries[:, 192 * i : 192 * i + 128]
-            lat = jnp.dot(plain, w_key_up[h], preferred_element_type=F32)
-            rot = queries[:, 192 * i + 128 : 192 * i + 192].astype(F32)
-            tokens = slice(256 * i, 256 * i + 256)
-            to = out_next if part else out
-            to[tokens, :512] = lat.astype(BF)
-            to[tokens, 512:] = turned(rot, cosine, sine)
+        span = slice(384 * part, 384 * part + 384)
+        sums = jnp.dot(rows_held[:, span], w_held[span, :], preferred_element_type=F32)
+        total[...] = total[...] + sums if part else sums
+    copies[5].wait()
+    for h in range(8):
+        queries = total[:, 192 * h : 192 * h + 192]
+        lat = jnp.dot(queries[:, :128].astype(BF), up_held[h], preferred_element_type=F32)
+        rot = queries[:, 128:].astype(BF).astype(F32)
+        i = h % 4
+        tokens = slice(256 * i, 256 * i + 256)
+        to = out_next if h >= 4 else out
+        to[tokens, :512] = lat.astype(BF)
+        to[tokens, 512:] = turned(rot, cosine, sine)
 
 
 def keys_kernel(start, own, near, far, swapped, cache, cosines, sines, keys, hidden, raw, sem):
@@ -176,24 +184,31 @@
     return jnp.cos(own), jnp.sin(own), jnp.cos(every), jnp.sin(every)
 
 
-def quarter_kernel(rows, own, other):
+def quarter_kernel(flip, rows, out, wide, sem):
     x = lax.axis_index("x")
-    for out, flip in ((own, 0), (other, 1)):
-        odd = lax.axis_index("yl") ^ flip
-        base = 896 * (lax.axis_index("yh") ^ flip) + 384 * odd
-        pieces = []
-        for d in range(4):
-            start = pl.multiple_of(1792 * ((x + d) % 4) + base, 128)
-            wide = rows[:, pl.ds(start, 512)]
-            pieces.append(jnp.where(odd == 1, wide[:, 64:], wide[:, :448]))
-        out[...] = jnp.concatenate(pieces, 1)
+    odd = lax.axis_index("yl") ^ flip
+    base = 896 * (lax.axis_index("yh") ^ flip) + 384 * odd
+    copies = [
+        pltpu.make_async_copy(
+            rows.at[:, pl.ds(pl.multiple_of(1792 * ((x + d) % 4) + base, 128), 512)],
+            wide.at[d],
+            sem.at[d],
+        )
+        for d in range(4)
+    ]
+    for copy in copies:
+        copy.start()
+    for copy in copies:
+        copy.wait()
+    pieces = [jnp.where(odd == 1, wide[d, :, 64:], wide[d, :, :448]) for d in range(4)]
+    out[...] = jnp.concatenate(pieces, 1)
 
 
 def project_kernel(theirs, *refs):
-    groups, held, outs, (rows, total) = refs[:8], refs[8:21], refs[21:-2], refs[-2:]
-    own, d1, d2, d3, u4, u3, u2, u1, other, e1, e3, e4, v1 = held
-    blocks = [own, d1, d2, d3.at[:64], u4.at[:64], u3.at[:64], u2, u1]
-    blocks += [other, e1, d3.at[64:], e3, e4, u4.at[64:], u3.at[64:], v1]
+    groups, held, outs, (rows, total) = refs[:8], refs[8:19], refs[19:-2], refs[-2:]
+    own, d1, d2, d3, u4, u3, u2, u1, other, e3, e4 = held
+    blocks = [own, d1, *(both.at[:64] for both in (d2, d3, u4, u3, u2)), u1]
+    blocks += [other, d2.at[64:], d3.at[64:], e3, e4, *(both.at[64:] for both in (u4, u3, u2))]
     first = 2 * (lax.axis_index("c") ^ theirs)
     yh = lax.axis_index("yh")
     for pick in (0, 2):
@@ -243,17 +258,6 @@
     return [pl.BlockSpec(memory_space=pltpu.MemorySpace.SMEM)] * n
 
 
-def quarters(rows):
-    return pl.pallas_call(
-        quarter_kernel,
-        out_shape=[jax.ShapeDtypeStruct((64, 1792), BF)] * 2,
-        in_specs=whole(1),
-        out_specs=whole(2),
-        name="quarters",
-        cost_estimate=pl.CostEstimate(flops=0, bytes_accessed=2 << 20, transcendentals=0),
-    )(rows)
-
-
 def call(kernel, shapes, specs, args, name, flops, moved_bytes, room, scratch=()):
     many = isinstance(shapes, list)
     return pl.pallas_call(
@@ -274,6 +278,20 @@
     return jax.ShapeDtypeStruct(shape, kind)
 
 
+def quarter(flip, rows):
+    return call(
+        functools.partial(quarter_kernel, flip),
+        array((64, 1792)),
+        kept(),
+        (rows,),
+        "quarter",
+        0,
+        1 << 19,
+        62,
+        [pltpu.VMEM((4, 64, 512), BF), pltpu.SemaphoreType.DMA((4,))],
+    )
+
+
 def after(value, *others):
     return lax.optimization_barrier((value, *others))[0]
 
@@ -282,7 +300,7 @@
     return call(
         functools.partial(project_kernel, theirs),
         [array((256, 896), kind), array((3, 256, 896), kind)],
-        whole(21),
+        whole(19),
         (*groups, *blocks),
         "project",
         2 * 512 * 1024 * 1792,
@@ -295,12 +313,13 @@
 def local(query_latent, key_rows, key_cache, prompt_start, w_query, w_key_up, w_value_up, w_output):
     yh, z, x, c, yl = (lax.axis_index(a) for a in AXES)
     slab = 8 * yh + z
-    own, given = quarters(w_output.reshape(64, 7168))
+    weight_rows = w_output.reshape(64, 7168)
+    given = quarter(1, weight_rows)
     other = xor_y(given, 3)
+    own_keys = key_rows.T
+    half = lax.dynamic_slice_in_dim(after(own_keys, given), 128 * c, 128, 1)
+    own = quarter(0, after(weight_rows, half))
     u1, d1 = up_z(own), down_z(own)
-
-    own_keys = key_rows.T
-    half = lax.dynamic_slice_in_dim(own_keys, 128 * c, 128, 1)
     near, far = (
         lax.ppermute(half, CTX, [(i, i + by) for i in range(16 - by)]) for by in (1, 2)
     )
@@ -308,21 +327,23 @@
     queries = call(
         queries_kernel,
         [array((1024, 640))] * 2,
-        kept(2) + whole(3),
+        kept(3) + whole(2),
         (query_latent, w_query, w_key_up, cosines, sines),
         "queries",
         2 * 256 * 1536 * 1536 + 2 * 2048 * 128 * 512,
         8 << 20,
         60,
         [
-            pltpu.VMEM((2, 1536, 768), BF),
+            pltpu.VMEM((1536, 1536), BF),
             pltpu.VMEM((256, 1536), BF),
-            pltpu.SemaphoreType.DMA((3,)),
+            pltpu.VMEM((8, 128, 512), BF),
+            pltpu.VMEM((256, 1536), F32),
+            pltpu.SemaphoreType.DMA((6,)),
         ],
     )
     swapped = other_core(jnp.concatenate([near, far], 1))
-    u2, d2 = up_z(after(u1, queries[0])), down_z(after(d1, queries[0]))
-    v1, e1 = up_z(other), down_z(other)
+    u2 = up_z(jnp.concatenate([u1, other], 0))
+    d2 = down_z(jnp.concatenate([d1, other], 0))
 
     keys, hidden = call(
         keys_kernel,
@@ -357,12 +378,11 @@
     three = [xor_y(part, 3) for part in rows]
     two = [xor_y(one[0], 3), xor_y(three[1], 1)]
     groups = [*rows, *one, *two, *three]
-    u3 = up_z(after(jnp.concatenate([u2, v1], 0), rows[0]))
-    d3 = down_z(after(jnp.concatenate([d2, e1], 0), rows[0]))
+    u3, d3 = up_z(after(u2, rows[0])), down_z(after(d2, rows[0]))
     u4 = up_z(u3)
     e3 = down_z(d3[64:])
     e4 = down_z(e3)
-    blocks = [own, d1, d2, d3, u4, u3, u2, u1, other, e1, e3, e4, v1]
+    blocks = [own, d1, d2, d3, u4, u3, u2, u1, other, e3, e4]
 
     first, rest = project(1, groups, blocks, BF)
     first, rest = other_core(first), other_core(rest)

time: 110 us -> 113 us (1.027)
  waiting for transfers between devices: 30.7 us -> 32.4 us
  Pallas kernels: 21.9 us -> 23.4 us
    pallas_call x6 -> x8, Pallas kernels: 19.7 us -> 23.4 us  [call(): pl.pallas_call(kernel, out_shape=shapes, in_specs=specs, out_specs=whole(...]
    pallas_call x1 -> x0, Pallas kernels: 2.22 us -> none  [quarters(): pl.pallas_call(quarter_kernel, out_shape=[jax.ShapeDtypeStruct((64, 1792)...]
    ppermute x29 -> x27, waiting for transfers between devices: 30.7 us -> 32.4 us  [moved(): return lax.ppermute(a, AXES, pairs)]
    ppermute x29 -> x27, starting transfers between devices: 42.1 us -> 42.3 us  [moved(): return lax.ppermute(a, AXES, pairs)]
  transfers between devices with their start and end apart: 31 -> 29, of which waited for: 13 -> 11; matrix products, arithmetic and copies ran while one was open for 2% -> 2% of each run, Pallas kernels for 18% -> 17%
where the time goes in v7:
time: 113 us
  starting transfers between devices  51.6 us (46%)
  waiting for transfers between devices  32.4 us (29%)
  Pallas kernels  23.4 us (21%)
  other arithmetic  2.99 us (3%)
  local copies, waits for them, and re-layouts  1.41 us (1%)
    ppermute x27, starting transfers between devices, moved(): return lax.ppermute(a, AXES, pairs)  42.3 us
    ppermute x27, waiting for transfers between devices, moved(): return lax.ppermute(a, AXES, pairs)  32.4 us
    pallas_call x8, Pallas kernels, call(): pl.pallas_call(kernel, out_shape=shapes, in_specs=specs, out_specs=whole(...  23.4 us
    ppermute x2, starting transfers between devices, local(): lax.ppermute(half, CTX, [(i, i + by) for i in range(16 - by)])  9.28 us
  transfers between devices with their start and end apart: 29, of which 11 were waited for; matrix products, arithmetic and copies ran while one was open for 2% of the time, Pallas kernels for 17%

profile of v7, /device:TPU:1, one launch (start us, length us, event | category | flops | bytes accessed | tf_op | source)
XLA Modules:
  0.0 112.8 jit_solution(13630978605855330645)
XLA Ops:
  0.0 1.9 %quarter.2 = bf16[64,1792]{1,0:T(8,128)(2,1)} custom-call(bf16[64,7168]{1,0:T(8,128)(2,1)} %bitcast.38), custom_call_target="tpu_custom_call" | custom-call | bytes 524288 | tf_op jit(solution)/shard_map/quarter/pallas_call | solution.py:263
  1.9 1.0 constant_dynamic-slice_fusion
  2.9 5.7 %collective-permute-start.1 = (bf16[576,128]{1,0:T(8,128)(2,1)S(1)}, bf16[576,128]{1,0:T(8,128)(2,1)S(1)}, u32[]{:S(2)}, u32[]{:S(2)}) collective-permute-start(bf16[576,128]{1,0:T(8,128)(2,1)S(1)} %constant_dynamic-slice_fusion), channel_id=1, source_target_pairs={{0,32},{16,48},{32,64},{48,80},{64,96},{80,112},{96,128},{112,144}... | collective-permute-start | bytes 442376 | tf_op jit(solution)/shard_map/ppermute | solution.py:324
  8.6 3.5 %collective-permute-start = (bf16[576,128]{1,0:T(8,128)(2,1)S(1)}, bf16[576,128]{1,0:T(8,128)(2,1)S(1)}, u32[]{:S(2)}, u32[]{:S(2)}) collective-permute-start(bf16[576,128]{1,0:T(8,128)(2,1)S(1)} %constant_dynamic-slice_fusion), channel_id=1, source_target_pairs={{0,16},{16,32},{32,48},{48,64},{64,80},{80,96},{96,112},{112,128},... | collective-permute-start | bytes 442376 | tf_op jit(solution)/shard_map/ppermute | solution.py:324
  12.2 1.9 %quarter.3.refs_8_ = bf16[64,1792]{1,0:T(8,128)(2,1)} custom-call(bf16[64,7168]{1,0:T(8,128)(2,1)} %bitcast.39), custom_call_target="tpu_custom_call" | custom-call | bytes 524288 | tf_op jit(solution)/shard_map/quarter/pallas_call | solution.py:263
  14.0 2.9 %collective-permute-start.13 = (bf16[64,1792]{1,0:T(8,128)(2,1)}, bf16[64,1792]{1,0:T(8,128)(2,1)S(1)}, u32[]{:S(2)}, u32[]{:S(2)}) collective-permute-start(bf16[64,1792]{1,0:T(8,128)(2,1)} %quarter.3.refs_8_), channel_id=1, source_target_pairs={{0,16},{1,17},{2,18},{3,19},{4,20},{5,21},{6,22},{7,23},{8,24},{9,... | collective-permute-start | bytes 688136 | tf_op jit(solution)/shard_map/ppermute | solution.py:33
  17.0 0.9 collective-permute-start.9
  17.9 1.8 %collective-permute-start.10 = (bf16[64,1792]{1,0:T(8,128)(2,1)S(1)}, bf16[64,1792]{1,0:T(8,128)(2,1)S(1)}, u32[]{:S(2)}, u32[]{:S(2)}) collective-permute-start(bf16[64,1792]{1,0:T(8,128)(2,1)S(1)} %copy-done.6), channel_id=1, source_target_pairs={{0,129},{1,128},{2,131},{3,130},{4,133},{5,132},{6,135},{7,134},{8... | collective-permute-start | bytes 688136 | tf_op jit(solution)/shard_map/ppermute | solution.py:33
  19.8 0.4 multiply_sine_fusion
  20.3 0.8 fusion.13
  21.0 6.9 %queries.1 = (bf16[1024,640]{1,0:T(8,128)(2,1)}, bf16[1024,640]{1,0:T(8,128)(2,1)}) custom-call(bf16[256,1536]{1,0:T(8,128)(2,1)} %rows.1, bf16[1536,1536]{1,0:T(8,128)(2,1)} %w_query.1, bf16[8,128,512]{2,1,0:T(8,128)(2,1)} %w_key_up.1, f32[64,128]{1,0:T(8,128)} %get-tuple-element.51.cosines, f32[64,128]{1,0:T(8,128)} %get-tuple-element.50.sines), custom_call_target="tpu_custom_call" | custom-call | flops 1476395008 | bytes 8388608 | tf_op jit(solution)/shard_map/queries/pallas_call | solution.py:263
  28.0 2.0 %collective-permute-start.2 = (bf16[576,256]{1,0:T(8,128)(2,1)S(1)}, bf16[576,256]{1,0:T(8,128)(2,1)S(1)}, u32[]{:S(2)}, u32[]{:S(2)}) collective-permute-start(bf16[576,256]{1,0:T(8,128)(2,1)S(1)} %pad_maximum_fusion.2), channel_id=1, source_target_pairs={{0,2},{1,3},{2,0},{3,1},{4,6},{5,7},{6,4},{7,5},{8,10},{9,11},{10,... | collective-permute-start | bytes 884744 | tf_op jit(solution)/shard_map/ppermute | solution.py:33
  30.1 1.7 %collective-permute-start.14 = (bf16[128,1792]{1,0:T(8,128)(2,1)S(1)}, bf16[128,1792]{1,0:T(8,128)(2,1)S(1)}, u32[]{:S(2)}, u32[]{:S(2)}) collective-permute-start(bf16[128,1792]{1,0:T(8,128)(2,1)S(1)} %get-tuple-element.46), channel_id=1, source_target_pairs={{0,16},{1,17},{2,18},{3,19},{4,20},{5,21},{6,22},{7,23},{8,24},{9,... | collective-permute-start | bytes 1376264 | tf_op jit(solution)/shard_map/ppermute | solution.py:33
  31.8 1.0 collective-permute-start.11
  33.7 0.4 keys.1
  34.2 3.8 %attend.2.refs_0_ = bf16[256,512]{1,0:T(8,128)(2,1)S(1)} custom-call(bf16[1024,640]{1,0:T(8,128)(2,1)S(1)} %copy-done.4, bf16[640,768]{1,0:T(8,128)(2,1)S(1)} %get-tuple-element.21.keys, f32[256,768]{1,0:T(8,128)S(1)} %get-tuple-element.22.hidden, bf16[8,512,128]{2,1,0:T(8,128)(2,1)S(1)} %copy-done.5, bf16[512,512]{1,0:T(8,128)(2,1)S(1)} %fusion.reorder), custom_call_target="tpu_custom_call" | custom-call | flops 1946157056 | bytes 5242880 | tf_op jit(solution)/shard_map/attend/pallas_call | solution.py:263
  37.9 5.7 %collective-permute-done.11.refs_10_ = bf16[128,1792]{1,0:T(8,128)(2,1)S(1)} collective-permute-done((bf16[128,1792]{1,0:T(8,128)(2,1)S(1)}, bf16[128,1792]{1,0:T(8,128)(2,1)S(1)}, u32[]{:S(2)}, u32[]{:S(2)}) %collective-permute-start.11) | collective-permute-done | bytes 458784 | tf_op jit(solution)/shard_map/ppermute | solution.py:33
  43.6 2.2 %collective-permute-start.12 = (bf16[128,1792]{1,0:T(8,128)(2,1)S(1)}, bf16[128,1792]{1,0:T(8,128)(2,1)S(1)}, u32[]{:S(2)}, u32[]{:S(2)}) collective-permute-start(bf16[128,1792]{1,0:T(8,128)(2,1)S(1)} %collective-permute-done.11.refs_10_), channel_id=1, source_target_pairs={{0,112},{1,113},{2,114},{3,115},{4,116},{5,117},{6,118},{7,119},{8... | collective-permute-start | bytes 1376264 | tf_op jit(solution)/shard_map/ppermute | solution.py:33
  45.9 3.8 %attend.3.refs_1_ = bf16[256,512]{1,0:T(8,128)(2,1)S(1)} custom-call(bf16[1024,640]{1,0:T(8,128)(2,1)S(1)} %copy-done.3, bf16[640,768]{1,0:T(8,128)(2,1)S(1)} %get-tuple-element.21.keys, f32[256,768]{1,0:T(8,128)S(1)} %get-tuple-element.22.hidden, bf16[8,512,128]{2,1,0:T(8,128)(2,1)S(1)} %copy-done.5, bf16[512,512]{1,0:T(8,128)(2,1)S(1)} %fusion.reorder), custom_call_target="tpu_custom_call" | custom-call | flops 1946157056 | bytes 5242880 | tf_op jit(solution)/shard_map/attend/pallas_call | solution.py:263
  49.7 0.8 collective-permute-start.6
  50.5 1.5 %collective-permute-start.3 = (bf16[256,512]{1,0:T(8,128)(2,1)S(1)}, bf16[256,512]{1,0:T(8,128)(2,1)S(1)}, u32[]{:S(2)}, u32[]{:S(2)}) collective-permute-start(bf16[256,512]{1,0:T(8,128)(2,1)S(1)} %attend.2.refs_0_), channel_id=1, source_target_pairs={{0,1},{1,0},{2,3},{3,2},{4,5},{5,4},{6,7},{7,6},{8,9},{9,8},{10,11... | collective-permute-start | bytes 786440 | tf_op jit(solution)/shard_map/ppermute | solution.py:33
  52.0 2.6 %collective-permute-done.12.refs_11_ = bf16[128,1792]{1,0:T(8,128)(2,1)S(1)} collective-permute-done((bf16[128,1792]{1,0:T(8,128)(2,1)S(1)}, bf16[128,1792]{1,0:T(8,128)(2,1)S(1)}, u32[]{:S(2)}, u32[]{:S(2)}) %collective-permute-start.12) | collective-permute-done | bytes 458784 | tf_op jit(solution)/shard_map/ppermute | solution.py:33
  54.6 3.5 %collective-permute-start.17 = (bf16[64,1792]{1,0:T(8,128)(2,1)S(1)}, bf16[64,1792]{1,0:T(8,128)(2,1)S(1)}, u32[]{:S(2)}, u32[]{:S(2)}) collective-permute-start(bf16[64,1792]{1,0:T(8,128)(2,1)S(1)} %slice.96), channel_id=1, source_target_pairs={{0,112},{1,113},{2,114},{3,115},{4,116},{5,117},{6,118},{7,119},{8... | collective-permute-start | bytes 688136 | tf_op jit(solution)/shard_map/ppermute | solution.py:33
  58.1 0.8 collective-permute-start.8
  58.9 3.3 %collective-permute-done.3.refs_2_ = bf16[256,512]{1,0:T(8,128)(2,1)S(1)} collective-permute-done((bf16[256,512]{1,0:T(8,128)(2,1)S(1)}, bf16[256,512]{1,0:T(8,128)(2,1)S(1)}, u32[]{:S(2)}, u32[]{:S(2)}) %collective-permute-start.3) | collective-permute-done | bytes 262176 | tf_op jit(solution)/shard_map/ppermute | solution.py:33
  62.2 1.9 %collective-permute-start.5 = (bf16[256,512]{1,0:T(8,128)(2,1)S(1)}, bf16[256,512]{1,0:T(8,128)(2,1)S(1)}, u32[]{:S(2)}, u32[]{:S(2)}) collective-permute-start(bf16[256,512]{1,0:T(8,128)(2,1)S(1)} %collective-permute-done.3.refs_2_), channel_id=1, source_target_pairs={{0,129},{1,128},{2,131},{3,130},{4,133},{5,132},{6,135},{7,134},{8... | collective-permute-start | bytes 786440 | tf_op jit(solution)/shard_map/ppermute | solution.py:33
  64.2 2.4 %collective-permute-start.18 = (bf16[64,1792]{1,0:T(8,128)(2,1)S(1)}, bf16[64,1792]{1,0:T(8,128)(2,1)S(1)}, u32[]{:S(2)}, u32[]{:S(2)}) collective-permute-start(bf16[64,1792]{1,0:T(8,128)(2,1)S(1)} %collective-permute-done.17.refs_17_), channel_id=1, source_target_pairs={{0,112},{1,113},{2,114},{3,115},{4,116},{5,117},{6,118},{7,119},{8... | collective-permute-start | bytes 688136 | tf_op jit(solution)/shard_map/ppermute | solution.py:33
  66.6 1.3 %collective-permute-done.7.refs_5_ = bf16[256,512]{1,0:T(8,128)(2,1)S(1)} collective-permute-done((bf16[256,512]{1,0:T(8,128)(2,1)S(1)}, bf16[256,512]{1,0:T(8,128)(2,1)S(1)}, u32[]{:S(2)}, u32[]{:S(2)}) %collective-permute-start.7) | collective-permute-done | bytes 262176 | tf_op jit(solution)/shard_map/ppermute | solution.py:33
  67.9 2.6 %collective-permute-done.5.refs_4_ = bf16[256,512]{1,0:T(8,128)(2,1)S(1)} collective-permute-done((bf16[256,512]{1,0:T(8,128)(2,1)S(1)}, bf16[256,512]{1,0:T(8,128)(2,1)S(1)}, u32[]{:S(2)}, u32[]{:S(2)}) %collective-permute-start.5) | collective-permute-done | bytes 262176 | tf_op jit(solution)/shard_map/ppermute | solution.py:33
  70.5 2.3 %project.3 = (bf16[256,896]{1,0:T(8,128)(2,1)S(1)}, bf16[3,256,896]{2,1,0:T(8,128)(2,1)S(1)}) custom-call(bf16[256,512]{1,0:T(8,128)(2,1)S(1)} %attend.2.refs_0_, bf16[256,512]{1,0:T(8,128)(2,1)S(1)} %attend.3.refs_1_, bf16[256,512]{1,0:T(8,128)(2,1)S(1)} %collective-permute-done.3.refs_2_, bf16[256,512]{1,0:T(8,128)(2,1)S(1)} %collective-permute-done.4.refs_3_, ...), custom_call_target="tpu_custom_call" | custom-call | flops 1879048192 | bytes 8388608 | tf_op jit(solution)/shard_map/project/pallas_call | solution.py:263
  72.8 5.6 %collective-permute-start.19 = (bf16[3,256,896]{2,1,0:T(8,128)(2,1)S(1)}, bf16[3,256,896]{2,1,0:T(8,128)(2,1)S(1)}, u32[]{:S(2)}, u32[]{:S(2)}) collective-permute-start(bf16[3,256,896]{2,1,0:T(8,128)(2,1)S(1)} %get-tuple-element.28), channel_id=1, source_target_pairs={{0,2},{1,3},{2,0},{3,1},{4,6},{5,7},{6,4},{7,5},{8,10},{9,11},{10,... | collective-permute-start | bytes 4128776 | tf_op jit(solution)/shard_map/ppermute | solution.py:33
  78.5 2.5 %project.2 = (f32[256,896]{1,0:T(8,128)S(1)}, f32[3,256,896]{2,1,0:T(8,128)S(1)}) custom-call(bf16[256,512]{1,0:T(8,128)(2,1)S(1)} %attend.2.refs_0_, bf16[256,512]{1,0:T(8,128)(2,1)S(1)} %attend.3.refs_1_, bf16[256,512]{1,0:T(8,128)(2,1)S(1)} %collective-permute-done.3.refs_2_, bf16[256,512]{1,0:T(8,128)(2,1)S(1)} %collective-permute-done.4.refs_3_, ...), custom_call_target="tpu_custom_call" | custom-call | flops 1879048192 | bytes 8388608 | tf_op jit(solution)/shard_map/project/pallas_call | solution.py:263
  81.1 0.8 collective-permute-done.20
  82.0 1.3 %collective-permute-start.21 = (bf16[128,896]{1,0:T(8,128)(2,1)S(1)}, bf16[128,896]{1,0:T(8,128)(2,1)S(1)}, u32[]{:S(2)}, u32[]{:S(2)}) collective-permute-start(bf16[128,896]{1,0:T(8,128)(2,1)S(1)} %get-tuple-element.40), channel_id=1, source_target_pairs={{0,4},{1,5},{2,6},{3,7},{4,8},{5,9},{6,10},{7,11},{8,12},{9,13},{1... | collective-permute-start | bytes 688136 | tf_op jit(solution)/shard_map/ppermute | solution.py:33
  83.3 1.5 %collective-permute-start.26 = (bf16[128,896]{1,0:T(8,128)(2,1)S(1)}, bf16[128,896]{1,0:T(8,128)(2,1)S(1)}, u32[]{:S(2)}, u32[]{:S(2)}) collective-permute-start(bf16[128,896]{1,0:T(8,128)(2,1)S(1)} %get-tuple-element.41), channel_id=1, source_target_pairs={{0,12},{1,13},{2,14},{3,15},{4,0},{5,1},{6,2},{7,3},{8,4},{9,5},{1... | collective-permute-start | bytes 688136 | tf_op jit(solution)/shard_map/ppermute | solution.py:33
  84.7 0.2 convert_add_fusion.1
  85.0 1.3 %collective-permute-start.23 = (bf16[128,896]{1,0:T(8,128)(2,1)S(1)}, bf16[128,896]{1,0:T(8,128)(2,1)S(1)}, u32[]{:S(2)}, u32[]{:S(2)}) collective-permute-start(bf16[128,896]{1,0:T(8,128)(2,1)S(1)} %fusion.12), channel_id=1, source_target_pairs={{0,12},{1,13},{2,14},{3,15},{4,0},{5,1},{6,2},{7,3},{8,4},{9,5},{1... | collective-permute-start | bytes 688136 | tf_op jit(solution)/shard_map/ppermute | solution.py:33
  86.4 0.2 collective-permute-start.25
  86.6 3.2 %collective-permute-done.26 = bf16[128,896]{1,0:T(8,128)(2,1)S(1)} collective-permute-done((bf16[128,896]{1,0:T(8,128)(2,1)S(1)}, bf16[128,896]{1,0:T(8,128)(2,1)S(1)}, u32[]{:S(2)}, u32[]{:S(2)}) %collective-permute-start.26) | collective-permute-done | bytes 229408 | tf_op jit(solution)/shard_map/ppermute | solution.py:33
  89.8 2.7 %collective-permute-start.27 = (bf16[128,896]{1,0:T(8,128)(2,1)S(1)}, bf16[128,896]{1,0:T(8,128)(2,1)S(1)}, u32[]{:S(2)}, u32[]{:S(2)}) collective-permute-start(bf16[128,896]{1,0:T(8,128)(2,1)S(1)} %fusion.2), channel_id=1, source_target_pairs={{0,12},{1,13},{2,14},{3,15},{4,0},{5,1},{6,2},{7,3},{8,4},{9,5},{1... | collective-permute-start | bytes 688136 | tf_op jit(solution)/shard_map/ppermute | solution.py:33
  92.7 2.0 %collective-permute-done.23 = bf16[128,896]{1,0:T(8,128)(2,1)S(1)} collective-permute-done((bf16[128,896]{1,0:T(8,128)(2,1)S(1)}, bf16[128,896]{1,0:T(8,128)(2,1)S(1)}, u32[]{:S(2)}, u32[]{:S(2)}) %collective-permute-start.23) | collective-permute-done | bytes 229408 | tf_op jit(solution)/shard_map/ppermute | solution.py:33
  94.7 4.9 %collective-permute-done.27 = bf16[128,896]{1,0:T(8,128)(2,1)S(1)} collective-permute-done((bf16[128,896]{1,0:T(8,128)(2,1)S(1)}, bf16[128,896]{1,0:T(8,128)(2,1)S(1)}, u32[]{:S(2)}, u32[]{:S(2)}) %collective-permute-start.27) | collective-permute-done | bytes 229408 | tf_op jit(solution)/shard_map/ppermute | solution.py:33
  99.6 0.2 fusion.10
  99.8 4.6 %collective-permute-start.24 = (bf16[128,896]{1,0:T(8,128)(2,1)S(1)}, bf16[128,896]{1,0:T(8,128)(2,1)S(1)}, u32[]{:S(2)}, u32[]{:S(2)}) collective-permute-start(bf16[128,896]{1,0:T(8,128)(2,1)S(1)} %get-tuple-element.36), channel_id=1, source_target_pairs={{0,0},{1,1},{2,128},{3,129},{4,4},{5,5},{6,132},{7,133},{8,8},{9,9... | collective-permute-start | bytes 688136 | tf_op jit(solution)/shard_map/ppermute | solution.py:33
  104.4 1.3 %collective-permute-start.28 = (bf16[128,896]{1,0:T(8,128)(2,1)S(1)}, bf16[128,896]{1,0:T(8,128)(2,1)S(1)}, u32[]{:S(2)}, u32[]{:S(2)}) collective-permute-start(bf16[128,896]{1,0:T(8,128)(2,1)S(1)} %get-tuple-element.37), channel_id=1, source_target_pairs={{0,1},{1,0},{2,129},{3,128},{4,5},{5,4},{6,133},{7,132},{8,9},{9,8... | collective-permute-start | bytes 688136 | tf_op jit(solution)/shard_map/ppermute | solution.py:33
  105.6 4.5 %collective-permute-done.24 = bf16[128,896]{1,0:T(8,128)(2,1)S(1)} collective-permute-done((bf16[128,896]{1,0:T(8,128)(2,1)S(1)}, bf16[128,896]{1,0:T(8,128)(2,1)S(1)}, u32[]{:S(2)}, u32[]{:S(2)}) %collective-permute-start.24) | collective-permute-done | bytes 229408 | tf_op jit(solution)/shard_map/ppermute | solution.py:33
  110.2 1.4 %collective-permute-done.28 = bf16[128,896]{1,0:T(8,128)(2,1)S(1)} collective-permute-done((bf16[128,896]{1,0:T(8,128)(2,1)S(1)}, bf16[128,896]{1,0:T(8,128)(2,1)S(1)}, u32[]{:S(2)}, u32[]{:S(2)}) %collective-permute-start.28) | collective-permute-done | bytes 229408 | tf_op jit(solution)/shard_map/ppermute | solution.py:33
  111.8 0.9 maximum_maximum_fusion
  (58 shorter events, 1.2 us)
Async XLA Ops:
  1.9 16.0 %copy-start.6 = (bf16[64,1792]{1,0:T(8,128)(2,1)S(1)}, bf16[64,1792]{1,0:T(8,128)(2,1)}, u32[]{:S(2)}) copy-start(bf16[64,1792]{1,0:T(8,128)(2,1)} %quarter.2) | copy-start | bytes 688132
  2.9 25.1 %collective-permute-start.1 = (bf16[576,128]{1,0:T(8,128)(2,1)S(1)}, bf16[576,128]{1,0:T(8,128)(2,1)S(1)}, u32[]{:S(2)}, u32[]{:S(2)}) collective-permute-start(bf16[576,128]{1,0:T(8,128)(2,1)S(1)} %constant_dynamic-slice_fusion), channel_id=1, source_target_pairs={{0,32},{16,48},{32,64},{48,80},{64,96},{80,112},{96,128},{112,144}... | collective-permute-start | bytes 442376 | tf_op jit(solution)/shard_map/ppermute | solution.py:324
  8.6 19.4 %collective-permute-start = (bf16[576,128]{1,0:T(8,128)(2,1)S(1)}, bf16[576,128]{1,0:T(8,128)(2,1)S(1)}, u32[]{:S(2)}, u32[]{:S(2)}) collective-permute-start(bf16[576,128]{1,0:T(8,128)(2,1)S(1)} %constant_dynamic-slice_fusion), channel_id=1, source_target_pairs={{0,16},{16,32},{32,48},{48,64},{64,80},{80,96},{96,112},{112,128},... | collective-permute-start | bytes 442376 | tf_op jit(solution)/shard_map/ppermute | solution.py:324
  14.0 16.0 %collective-permute-start.13 = (bf16[64,1792]{1,0:T(8,128)(2,1)}, bf16[64,1792]{1,0:T(8,128)(2,1)S(1)}, u32[]{:S(2)}, u32[]{:S(2)}) collective-permute-start(bf16[64,1792]{1,0:T(8,128)(2,1)} %quarter.3.refs_8_), channel_id=1, source_target_pairs={{0,16},{1,17},{2,18},{3,19},{4,20},{5,21},{6,22},{7,23},{8,24},{9,... | collective-permute-start | bytes 688136 | tf_op jit(solution)/shard_map/ppermute | solution.py:33
  17.0 13.1 %collective-permute-start.9 = (bf16[64,1792]{1,0:T(8,128)(2,1)}, bf16[64,1792]{1,0:T(8,128)(2,1)S(1)}, u32[]{:S(2)}, u32[]{:S(2)}) collective-permute-start(bf16[64,1792]{1,0:T(8,128)(2,1)} %quarter.3.refs_8_), channel_id=1, source_target_pairs={{0,112},{1,113},{2,114},{3,115},{4,116},{5,117},{6,118},{7,119},{8... | collective-permute-start | bytes 688136 | tf_op jit(solution)/shard_map/ppermute | solution.py:33
  17.9 12.1 %collective-permute-start.10 = (bf16[64,1792]{1,0:T(8,128)(2,1)S(1)}, bf16[64,1792]{1,0:T(8,128)(2,1)S(1)}, u32[]{:S(2)}, u32[]{:S(2)}) collective-permute-start(bf16[64,1792]{1,0:T(8,128)(2,1)S(1)} %copy-done.6), channel_id=1, source_target_pairs={{0,129},{1,128},{2,131},{3,130},{4,133},{5,132},{6,135},{7,134},{8... | collective-permute-start | bytes 688136 | tf_op jit(solution)/shard_map/ppermute | solution.py:33
  27.9 5.7 %copy-start = (bf16[256,576]{0,1:T(8,128)(2,1)S(1)}, bf16[256,576]{0,1:T(8,128)(2,1)}, u32[]{:S(2)}) copy-start(bf16[256,576]{0,1:T(8,128)(2,1)} %param.9) | copy-start | bytes 884740
  27.9 5.7 %copy-start.1 = (bf16[512,576]{0,1:T(8,128)(2,1)S(1)}, bf16[512,576]{0,1:T(8,128)(2,1)}, u32[]{:S(2)}) copy-start(bf16[512,576]{0,1:T(8,128)(2,1)} %param.10) | copy-start | bytes 1769476
  28.0 5.7 %collective-permute-start.2 = (bf16[576,256]{1,0:T(8,128)(2,1)S(1)}, bf16[576,256]{1,0:T(8,128)(2,1)S(1)}, u32[]{:S(2)}, u32[]{:S(2)}) collective-permute-start(bf16[576,256]{1,0:T(8,128)(2,1)S(1)} %pad_maximum_fusion.2), channel_id=1, source_target_pairs={{0,2},{1,3},{2,0},{3,1},{4,6},{5,7},{6,4},{7,5},{8,10},{9,11},{10,... | collective-permute-start | bytes 884744 | tf_op jit(solution)/shard_map/ppermute | solution.py:33
  30.0 4.1 %copy-start.5 = (bf16[8,512,128]{2,1,0:T(8,128)(2,1)S(1)}, bf16[8,512,128]{2,1,0:T(8,128)(2,1)}, u32[]{:S(2)}) copy-start(bf16[8,512,128]{2,1,0:T(8,128)(2,1)} %w_value_up.3) | copy-start | bytes 3145732
  30.1 4.0 %copy-start.4 = (bf16[1024,640]{1,0:T(8,128)(2,1)S(1)}, bf16[1024,640]{1,0:T(8,128)(2,1)}, u32[]{:S(2)}) copy-start(bf16[1024,640]{1,0:T(8,128)(2,1)} %get-tuple-element.19.queries) | copy-start | bytes 3932164
  30.1 15.8 %collective-permute-start.14 = (bf16[128,1792]{1,0:T(8,128)(2,1)S(1)}, bf16[128,1792]{1,0:T(8,128)(2,1)S(1)}, u32[]{:S(2)}, u32[]{:S(2)}) collective-permute-start(bf16[128,1792]{1,0:T(8,128)(2,1)S(1)} %get-tuple-element.46), channel_id=1, source_target_pairs={{0,16},{1,17},{2,18},{3,19},{4,20},{5,21},{6,22},{7,23},{8,24},{9,... | collective-permute-start | bytes 1376264 | tf_op jit(solution)/shard_map/ppermute | solution.py:33
  31.8 11.8 %collective-permute-start.11 = (bf16[128,1792]{1,0:T(8,128)(2,1)S(1)}, bf16[128,1792]{1,0:T(8,128)(2,1)S(1)}, u32[]{:S(2)}, u32[]{:S(2)}) collective-permute-start(bf16[128,1792]{1,0:T(8,128)(2,1)S(1)} %get-tuple-element.47), channel_id=1, source_target_pairs={{0,112},{1,113},{2,114},{3,115},{4,116},{5,117},{6,118},{7,119},{8... | collective-permute-start | bytes 1376264 | tf_op jit(solution)/shard_map/ppermute | solution.py:33
  34.2 11.7 %copy-start.3 = (bf16[1024,640]{1,0:T(8,128)(2,1)S(1)}, bf16[1024,640]{1,0:T(8,128)(2,1)}, u32[]{:S(2)}) copy-start(bf16[1024,640]{1,0:T(8,128)(2,1)} %get-tuple-element.23.queries) | copy-start | bytes 3932164
  43.6 10.9 %collective-permute-start.12 = (bf16[128,1792]{1,0:T(8,128)(2,1)S(1)}, bf16[128,1792]{1,0:T(8,128)(2,1)S(1)}, u32[]{:S(2)}, u32[]{:S(2)}) collective-permute-start(bf16[128,1792]{1,0:T(8,128)(2,1)S(1)} %collective-permute-done.11.refs_10_), channel_id=1, source_target_pairs={{0,112},{1,113},{2,114},{3,115},{4,116},{5,117},{6,118},{7,119},{8... | collective-permute-start | bytes 1376264 | tf_op jit(solution)/shard_map/ppermute | solution.py:33
  45.9 12.2 %collective-permute-start.15 = (bf16[128,1792]{1,0:T(8,128)(2,1)S(1)}, bf16[128,1792]{1,0:T(8,128)(2,1)S(1)}, u32[]{:S(2)}, u32[]{:S(2)}) collective-permute-start(bf16[128,1792]{1,0:T(8,128)(2,1)S(1)} %collective-permute-done.14.refs_14_), channel_id=1, source_target_pairs={{0,16},{1,17},{2,18},{3,19},{4,20},{5,21},{6,22},{7,23},{8,24},{9,... | collective-permute-start | bytes 1376264 | tf_op jit(solution)/shard_map/ppermute | solution.py:33
  45.9 24.6 %copy-start.2 = (bf16[64,1792]{1,0:T(8,128)(2,1)S(1)}, bf16[64,1792]{1,0:T(8,128)(2,1)}, u32[]{:S(2)}) copy-start(bf16[64,1792]{1,0:T(8,128)(2,1)} %quarter.3.refs_8_) | copy-start | bytes 688132
  49.7 8.4 %collective-permute-start.6 = (bf16[256,512]{1,0:T(8,128)(2,1)S(1)}, bf16[256,512]{1,0:T(8,128)(2,1)S(1)}, u32[]{:S(2)}, u32[]{:S(2)}) collective-permute-start(bf16[256,512]{1,0:T(8,128)(2,1)S(1)} %attend.3.refs_1_), channel_id=1, source_target_pairs={{0,129},{1,128},{2,131},{3,130},{4,133},{5,132},{6,135},{7,134},{8... | collective-permute-start | bytes 786440 | tf_op jit(solution)/shard_map/ppermute | solution.py:33
  50.5 8.4 %collective-permute-start.4 = (bf16[256,512]{1,0:T(8,128)(2,1)S(1)}, bf16[256,512]{1,0:T(8,128)(2,1)S(1)}, u32[]{:S(2)}, u32[]{:S(2)}) collective-permute-start(bf16[256,512]{1,0:T(8,128)(2,1)S(1)} %attend.3.refs_1_), channel_id=1, source_target_pairs={{0,1},{1,0},{2,3},{3,2},{4,5},{5,4},{6,7},{7,6},{8,9},{9,8},{10,11... | collective-permute-start | bytes 786440 | tf_op jit(solution)/shard_map/ppermute | solution.py:33
  50.5 11.7 %collective-permute-start.3 = (bf16[256,512]{1,0:T(8,128)(2,1)S(1)}, bf16[256,512]{1,0:T(8,128)(2,1)S(1)}, u32[]{:S(2)}, u32[]{:S(2)}) collective-permute-start(bf16[256,512]{1,0:T(8,128)(2,1)S(1)} %attend.2.refs_0_), channel_id=1, source_target_pairs={{0,1},{1,0},{2,3},{3,2},{4,5},{5,4},{6,7},{7,6},{8,9},{9,8},{10,11... | collective-permute-start | bytes 786440 | tf_op jit(solution)/shard_map/ppermute | solution.py:33
  54.6 9.6 %collective-permute-start.17 = (bf16[64,1792]{1,0:T(8,128)(2,1)S(1)}, bf16[64,1792]{1,0:T(8,128)(2,1)S(1)}, u32[]{:S(2)}, u32[]{:S(2)}) collective-permute-start(bf16[64,1792]{1,0:T(8,128)(2,1)S(1)} %slice.96), channel_id=1, source_target_pairs={{0,112},{1,113},{2,114},{3,115},{4,116},{5,117},{6,118},{7,119},{8... | collective-permute-start | bytes 688136 | tf_op jit(solution)/shard_map/ppermute | solution.py:33
  58.1 12.4 %collective-permute-start.16 = (bf16[128,1792]{1,0:T(8,128)(2,1)S(1)}, bf16[128,1792]{1,0:T(8,128)(2,1)S(1)}, u32[]{:S(2)}, u32[]{:S(2)}) collective-permute-start(bf16[128,1792]{1,0:T(8,128)(2,1)S(1)} %collective-permute-done.15.refs_13_), channel_id=1, source_target_pairs={{0,16},{1,17},{2,18},{3,19},{4,20},{5,21},{6,22},{7,23},{8,24},{9,... | collective-permute-start | bytes 1376264 | tf_op jit(solution)/shard_map/ppermute | solution.py:33
  58.1 8.5 %collective-permute-start.8 = (bf16[256,512]{1,0:T(8,128)(2,1)S(1)}, bf16[256,512]{1,0:T(8,128)(2,1)S(1)}, u32[]{:S(2)}, u32[]{:S(2)}) collective-permute-start(bf16[256,512]{1,0:T(8,128)(2,1)S(1)} %attend.2.refs_0_), channel_id=1, source_target_pairs={{0,129},{1,128},{2,131},{3,130},{4,133},{5,132},{6,135},{7,134},{8... | collective-permute-start | bytes 786440 | tf_op jit(solution)/shard_map/ppermute | solution.py:33
  58.9 8.9 %collective-permute-start.7 = (bf16[256,512]{1,0:T(8,128)(2,1)S(1)}, bf16[256,512]{1,0:T(8,128)(2,1)S(1)}, u32[]{:S(2)}, u32[]{:S(2)}) collective-permute-start(bf16[256,512]{1,0:T(8,128)(2,1)S(1)} %collective-permute-done.6.refs_7_), channel_id=1, source_target_pairs={{0,1},{1,0},{2,3},{3,2},{4,5},{5,4},{6,7},{7,6},{8,9},{9,8},{10,11... | collective-permute-start | bytes 786440 | tf_op jit(solution)/shard_map/ppermute | solution.py:33
  62.2 8.3 %collective-permute-start.5 = (bf16[256,512]{1,0:T(8,128)(2,1)S(1)}, bf16[256,512]{1,0:T(8,128)(2,1)S(1)}, u32[]{:S(2)}, u32[]{:S(2)}) collective-permute-start(bf16[256,512]{1,0:T(8,128)(2,1)S(1)} %collective-permute-done.3.refs_2_), channel_id=1, source_target_pairs={{0,129},{1,128},{2,131},{3,130},{4,133},{5,132},{6,135},{7,134},{8... | collective-permute-start | bytes 786440 | tf_op jit(solution)/shard_map/ppermute | solution.py:33
  64.2 6.3 %collective-permute-start.18 = (bf16[64,1792]{1,0:T(8,128)(2,1)S(1)}, bf16[64,1792]{1,0:T(8,128)(2,1)S(1)}, u32[]{:S(2)}, u32[]{:S(2)}) collective-permute-start(bf16[64,1792]{1,0:T(8,128)(2,1)S(1)} %collective-permute-done.17.refs_17_), channel_id=1, source_target_pairs={{0,112},{1,113},{2,114},{3,115},{4,116},{5,117},{6,118},{7,119},{8... | collective-permute-start | bytes 688136 | tf_op jit(solution)/shard_map/ppermute | solution.py:33
  72.8 11.9 %collective-permute-start.19 = (bf16[3,256,896]{2,1,0:T(8,128)(2,1)S(1)}, bf16[3,256,896]{2,1,0:T(8,128)(2,1)S(1)}, u32[]{:S(2)}, u32[]{:S(2)}) collective-permute-start(bf16[3,256,896]{2,1,0:T(8,128)(2,1)S(1)} %get-tuple-element.28), channel_id=1, source_target_pairs={{0,2},{1,3},{2,0},{3,1},{4,6},{5,7},{6,4},{7,5},{8,10},{9,11},{10,... | collective-permute-start | bytes 4128776 | tf_op jit(solution)/shard_map/ppermute | solution.py:33
  78.4 3.4 %collective-permute-start.20 = (bf16[256,896]{1,0:T(8,128)(2,1)S(1)}, bf16[256,896]{1,0:T(8,128)(2,1)S(1)}, u32[]{:S(2)}, u32[]{:S(2)}) collective-permute-start(bf16[256,896]{1,0:T(8,128)(2,1)S(1)} %get-tuple-element.30), channel_id=1, source_target_pairs={{0,2},{1,3},{2,0},{3,1},{4,6},{5,7},{6,4},{7,5},{8,10},{9,11},{10,... | collective-permute-start | bytes 1376264 | tf_op jit(solution)/shard_map/ppermute | solution.py:33
  82.0 10.6 %collective-permute-start.21 = (bf16[128,896]{1,0:T(8,128)(2,1)S(1)}, bf16[128,896]{1,0:T(8,128)(2,1)S(1)}, u32[]{:S(2)}, u32[]{:S(2)}) collective-permute-start(bf16[128,896]{1,0:T(8,128)(2,1)S(1)} %get-tuple-element.40), channel_id=1, source_target_pairs={{0,4},{1,5},{2,6},{3,7},{4,8},{5,9},{6,10},{7,11},{8,12},{9,13},{1... | collective-permute-start | bytes 688136 | tf_op jit(solution)/shard_map/ppermute | solution.py:33
  83.3 6.5 %collective-permute-start.26 = (bf16[128,896]{1,0:T(8,128)(2,1)S(1)}, bf16[128,896]{1,0:T(8,128)(2,1)S(1)}, u32[]{:S(2)}, u32[]{:S(2)}) collective-permute-start(bf16[128,896]{1,0:T(8,128)(2,1)S(1)} %get-tuple-element.41), channel_id=1, source_target_pairs={{0,12},{1,13},{2,14},{3,15},{4,0},{5,1},{6,2},{7,3},{8,4},{9,5},{1... | collective-permute-start | bytes 688136 | tf_op jit(solution)/shard_map/ppermute | solution.py:33
  85.0 9.6 %collective-permute-start.23 = (bf16[128,896]{1,0:T(8,128)(2,1)S(1)}, bf16[128,896]{1,0:T(8,128)(2,1)S(1)}, u32[]{:S(2)}, u32[]{:S(2)}) collective-permute-start(bf16[128,896]{1,0:T(8,128)(2,1)S(1)} %fusion.12), channel_id=1, source_target_pairs={{0,12},{1,13},{2,14},{3,15},{4,0},{5,1},{6,2},{7,3},{8,4},{9,5},{1... | collective-permute-start | bytes 688136 | tf_op jit(solution)/shard_map/ppermute | solution.py:33
  86.4 8.3 %collective-permute-start.25 = (bf16[128,896]{1,0:T(8,128)(2,1)S(1)}, bf16[128,896]{1,0:T(8,128)(2,1)S(1)}, u32[]{:S(2)}, u32[]{:S(2)}) collective-permute-start(bf16[128,896]{1,0:T(8,128)(2,1)S(1)} %fusion.11), channel_id=1, source_target_pairs={{0,4},{1,5},{2,6},{3,7},{4,8},{5,9},{6,10},{7,11},{8,12},{9,13},{1... | collective-permute-start | bytes 688136 | tf_op jit(solution)/shard_map/ppermute | solution.py:33
  89.8 9.8 %collective-permute-start.27 = (bf16[128,896]{1,0:T(8,128)(2,1)S(1)}, bf16[128,896]{1,0:T(8,128)(2,1)S(1)}, u32[]{:S(2)}, u32[]{:S(2)}) collective-permute-start(bf16[128,896]{1,0:T(8,128)(2,1)S(1)} %fusion.2), channel_id=1, source_target_pairs={{0,12},{1,13},{2,14},{3,15},{4,0},{5,1},{6,2},{7,3},{8,4},{9,5},{1... | collective-permute-start | bytes 688136 | tf_op jit(solution)/shard_map/ppermute | solution.py:33
  92.6 7.0 %collective-permute-start.22 = (bf16[128,896]{1,0:T(8,128)(2,1)S(1)}, bf16[128,896]{1,0:T(8,128)(2,1)S(1)}, u32[]{:S(2)}, u32[]{:S(2)}) collective-permute-start(bf16[128,896]{1,0:T(8,128)(2,1)S(1)} %fusion.7), channel_id=1, source_target_pairs={{0,4},{1,5},{2,6},{3,7},{4,8},{5,9},{6,10},{7,11},{8,12},{9,13},{1... | collective-permute-start | bytes 688136 | tf_op jit(solution)/shard_map/ppermute | solution.py:33
  99.8 10.4 %collective-permute-start.24 = (bf16[128,896]{1,0:T(8,128)(2,1)S(1)}, bf16[128,896]{1,0:T(8,128)(2,1)S(1)}, u32[]{:S(2)}, u32[]{:S(2)}) collective-permute-start(bf16[128,896]{1,0:T(8,128)(2,1)S(1)} %get-tuple-element.36), channel_id=1, source_target_pairs={{0,0},{1,1},{2,128},{3,129},{4,4},{5,5},{6,132},{7,133},{8,8},{9,9... | collective-permute-start | bytes 688136 | tf_op jit(solution)/shard_map/ppermute | solution.py:33
  104.4 7.2 %collective-permute-start.28 = (bf16[128,896]{1,0:T(8,128)(2,1)S(1)}, bf16[128,896]{1,0:T(8,128)(2,1)S(1)}, u32[]{:S(2)}, u32[]{:S(2)}) collective-permute-start(bf16[128,896]{1,0:T(8,128)(2,1)S(1)} %get-tuple-element.37), channel_id=1, source_target_pairs={{0,1},{1,0},{2,129},{3,128},{4,5},{5,4},{6,133},{7,132},{8,9},{9,8... | collective-permute-start | bytes 688136 | tf_op jit(solution)/shard_map/ppermute | solution.py:33

commit v8 on v6

--- a/solution.py
+++ b/solution.py
@@ -69,23 +69,14 @@
     return jnp.concatenate([rot, jnp.zeros_like(rot)], 1).astype(BF)
 
 
-def queries_kernel(rows, w_query, w_key_up, cosines, sines, out, out_next, held, rows_held, sem):
-    copies = [
-        pltpu.make_async_copy(w_query.at[:, pl.ds(768 * part, 768)], held.at[part], sem.at[part])
-        for part in range(2)
-    ]
-    copies.append(pltpu.make_async_copy(rows, rows_held, sem.at[2]))
-    for i in (2, 0, 1):
-        copies[i].start()
+def queries_kernel(rows, w_query, w_key_up, cosines, sines, out, out_next):
     cosine, sine = turn_of(cosines), turn_of(sines)
-    copies[2].wait()
     for part in range(2):
-        copies[part].wait()
-        queries = jnp.dot(rows_held[...], held[part], preferred_element_type=F32).astype(BF)
+        span = slice(768 * part, 768 * part + 768)
+        queries = jnp.dot(rows[...], w_query[:, span], preferred_element_type=F32).astype(BF)
         for i in range(4):
-            h = 4 * part + i
             plain = queries[:, 192 * i : 192 * i + 128]
-            lat = jnp.dot(plain, w_key_up[h], preferred_element_type=F32)
+            lat = jnp.dot(plain, w_key_up[4 * part + i], preferred_element_type=F32)
             rot = queries[:, 192 * i + 128 : 192 * i + 192].astype(F32)
             tokens = slice(256 * i, 256 * i + 256)
             to = out_next if part else out
@@ -190,10 +181,9 @@
 
 
 def project_kernel(theirs, *refs):
-    groups, held, outs, (rows, total) = refs[:8], refs[8:21], refs[21:-2], refs[-2:]
-    own, d1, d2, d3, u4, u3, u2, u1, other, e1, e3, e4, v1 = held
-    blocks = [own, d1, d2, d3.at[:64], u4.at[:64], u3.at[:64], u2, u1]
-    blocks += [other, e1, d3.at[64:], e3, e4, u4.at[64:], u3.at[64:], v1]
+    groups, held, outs, (rows, total) = refs[:8], refs[8:23], refs[23:-2], refs[-2:]
+    both = held[4]
+    blocks = [*held[:4], both.at[:64], *held[5:14], both.at[64:], held[14]]
     first = 2 * (lax.axis_index("c") ^ theirs)
     yh = lax.axis_index("yh")
     for pick in (0, 2):
@@ -282,7 +272,7 @@
     return call(
         functools.partial(project_kernel, theirs),
         [array((256, 896), kind), array((3, 256, 896), kind)],
-        whole(21),
+        whole(23),
         (*groups, *blocks),
         "project",
         2 * 512 * 1024 * 1792,
@@ -308,17 +298,12 @@
     queries = call(
         queries_kernel,
         [array((1024, 640))] * 2,
-        kept(2) + whole(3),
+        whole(5),
         (query_latent, w_query, w_key_up, cosines, sines),
         "queries",
         2 * 256 * 1536 * 1536 + 2 * 2048 * 128 * 512,
         8 << 20,
-        60,
-        [
-            pltpu.VMEM((2, 1536, 768), BF),
-            pltpu.VMEM((256, 1536), BF),
-            pltpu.SemaphoreType.DMA((3,)),
-        ],
+        10,
     )
     swapped = other_core(jnp.concatenate([near, far], 1))
     u2, d2 = up_z(after(u1, queries[0])), down_z(after(d1, queries[0]))
@@ -357,12 +342,13 @@
     three = [xor_y(part, 3) for part in rows]
     two = [xor_y(one[0], 3), xor_y(three[1], 1)]
     groups = [*rows, *one, *two, *three]
-    u3 = up_z(after(jnp.concatenate([u2, v1], 0), rows[0]))
-    d3 = down_z(after(jnp.concatenate([d2, e1], 0), rows[0]))
-    u4 = up_z(u3)
-    e3 = down_z(d3[64:])
+    u3, d3 = up_z(after(u2, rows[0])), down_z(after(d2, rows[0]))
+    u4 = up_z(after(jnp.concatenate([u3, v1], 0), *rows))
+    e2 = down_z(after(e1, *rows))
+    v3 = up_z(u4[64:])
+    e3 = down_z(e2)
     e4 = down_z(e3)
-    blocks = [own, d1, d2, d3, u4, u3, u2, u1, other, e1, e3, e4, v1]
+    blocks = [own, d1, d2, d3, u4, u3, u2, u1, other, e1, e2, e3, e4, v3, v1]
 
     first, rest = project(1, groups, blocks, BF)
     first, rest = other_core(first), other_core(rest)

time: 110 us -> 115 us (1.045)
  Pallas kernels: 21.9 us -> 17.3 us
  waiting for transfers between devices: 30.7 us -> 34.7 us
  local copies, waits for them, and re-layouts: 1.35 us -> 4.36 us
  starting transfers between devices: 51.4 us -> 52.8 us
    pallas_call x6, Pallas kernels: 19.7 us -> 15.1 us  [call(): pl.pallas_call(kernel, out_shape=shapes, in_specs=specs, out_specs=whole(...]
    ppermute x29 -> x31, waiting for transfers between devices: 30.7 us -> 34.7 us  [moved(): return lax.ppermute(a, AXES, pairs)]
    unnamed x12 -> x18, local copies, waits for them, and re-layouts: 0.03 us -> 2.37 us
    ppermute x29 -> x31, starting transfers between devices: 42.1 us -> 43.5 us  [moved(): return lax.ppermute(a, AXES, pairs)]
  transfers between devices with their start and end apart: 31 -> 33, of which waited for: 13 -> 13; matrix products, arithmetic and copies ran while one was open for 2% -> 3% of each run, Pallas kernels for 18% -> 13%
where the time goes in v8:
time: 115 us; the launch traced here: 114 us
  starting transfers between devices  52.8 us (46%)
  waiting for transfers between devices  34.7 us (30%)
  Pallas kernels  17.3 us (15%)
  local copies, waits for them, and re-layouts  4.36 us (4%)
  other arithmetic  4.11 us (4%)
    ppermute x31, starting transfers between devices, moved(): return lax.ppermute(a, AXES, pairs)  43.5 us
    ppermute x31, waiting for transfers between devices, moved(): return lax.ppermute(a, AXES, pairs)  34.7 us
    pallas_call x6, Pallas kernels, call(): pl.pallas_call(kernel, out_shape=shapes, in_specs=specs, out_specs=whole(...  15.1 us
    ppermute x2, starting transfers between devices, local(): lax.ppermute(half, CTX, [(i, i + by) for i in range(16 - by)])  9.28 us
    unnamed x18, local copies, waits for them, and re-layouts  2.37 us
  transfers between devices with their start and end apart: 33, of which 13 were waited for; matrix products, arithmetic and copies ran while one was open for 3% of the time, Pallas kernels for 13%

profile of v8, /device:TPU:1, one launch (start us, length us, event | category | flops | bytes accessed | tf_op | source)
XLA Modules:
  0.0 114.3 jit_solution(6701091624577683108)
XLA Ops:
  0.0 1.1 dynamic-slice_bitcast_fusion
  1.1 5.7 %collective-permute-start.1 = (bf16[576,128]{1,0:T(8,128)(2,1)S(1)}, bf16[576,128]{1,0:T(8,128)(2,1)S(1)}, u32[]{:S(2)}, u32[]{:S(2)}) collective-permute-start(bf16[576,128]{1,0:T(8,128)(2,1)S(1)} %dynamic-slice_bitcast_fusion), channel_id=1, source_target_pairs={{0,32},{16,48},{32,64},{48,80},{64,96},{80,112},{96,128},{112,144}... | collective-permute-start | bytes 442376 | tf_op jit(solution)/shard_map/ppermute | solution.py:295
  6.8 3.5 %collective-permute-start = (bf16[576,128]{1,0:T(8,128)(2,1)S(1)}, bf16[576,128]{1,0:T(8,128)(2,1)S(1)}, u32[]{:S(2)}, u32[]{:S(2)}) collective-permute-start(bf16[576,128]{1,0:T(8,128)(2,1)S(1)} %dynamic-slice_bitcast_fusion), channel_id=1, source_target_pairs={{0,16},{16,32},{32,48},{48,64},{64,80},{80,96},{96,112},{112,128},... | collective-permute-start | bytes 442376 | tf_op jit(solution)/shard_map/ppermute | solution.py:295
  10.4 2.2 %quarters.1 = (bf16[64,1792]{1,0:T(8,128)(2,1)}, bf16[64,1792]{1,0:T(8,128)(2,1)}) custom-call(bf16[64,7168]{1,0:T(8,128)(2,1)} %bitcast.39), custom_call_target="tpu_custom_call" | custom-call | bytes 2097152 | tf_op jit(solution)/shard_map/quarters/pallas_call | solution.py:237
  12.6 2.8 %collective-permute-start.12 = (bf16[64,1792]{1,0:T(8,128)(2,1)}, bf16[64,1792]{1,0:T(8,128)(2,1)S(1)}, u32[]{:S(2)}, u32[]{:S(2)}) collective-permute-start(bf16[64,1792]{1,0:T(8,128)(2,1)} %get-tuple-element.27.refs_8_), channel_id=1, source_target_pairs={{0,16},{1,17},{2,18},{3,19},{4,20},{5,21},{6,22},{7,23},{8,24},{9,... | collective-permute-start | bytes 688136 | tf_op jit(solution)/shard_map/ppermute | solution.py:33
  15.4 0.8 collective-permute-start.9
  16.2 1.9 %collective-permute-start.15 = (bf16[64,1792]{1,0:T(8,128)(2,1)}, bf16[64,1792]{1,0:T(8,128)(2,1)S(1)}, u32[]{:S(2)}, u32[]{:S(2)}) collective-permute-start(bf16[64,1792]{1,0:T(8,128)(2,1)} %get-tuple-element.32), channel_id=1, source_target_pairs={{0,129},{1,128},{2,131},{3,130},{4,133},{5,132},{6,135},{7,134},{8... | collective-permute-start | bytes 688136 | tf_op jit(solution)/shard_map/ppermute | solution.py:33
  18.2 0.5 compare_and_fusion
  18.7 0.6 iota_shift-right-logical_fusion.3
  19.3 0.6 mul.83
  20.1 0.8 fusion.13
  20.9 2.3 %copy-done = bf16[1536,1536]{1,0:T(8,128)(2,1)S(1)} copy-done((bf16[1536,1536]{1,0:T(8,128)(2,1)S(1)}, bf16[1536,1536]{1,0:T(8,128)(2,1)}, u32[]{:S(2)}) %copy-start) | copy-done | bytes 4718616
  23.3 2.3 %queries.1 = (bf16[1024,640]{1,0:T(8,128)(2,1)S(1)}, bf16[1024,640]{1,0:T(8,128)(2,1)S(1)}) custom-call(bf16[256,1536]{1,0:T(8,128)(2,1)S(1)} %copy-done.2, bf16[1536,1536]{1,0:T(8,128)(2,1)S(1)} %copy-done, bf16[8,128,512]{2,1,0:T(8,128)(2,1)S(1)} %copy-done.1, f32[64,128]{1,0:T(8,128)S(1)} %get-tuple-element.57.cosines, f32[64,128]{1,0:T(8,128)S(1)} %get-tuple-element.56.sines), custom_call_target="tpu_custom_call" | custom-call | flops 1476395008 | bytes 8388608 | tf_op jit(solution)/shard_map/queries/pallas_call | solution.py:249
  25.7 2.0 %collective-permute-start.2 = (bf16[576,256]{1,0:T(8,128)(2,1)S(1)}, bf16[576,256]{1,0:T(8,128)(2,1)S(1)}, u32[]{:S(2)}, u32[]{:S(2)}) collective-permute-start(bf16[576,256]{1,0:T(8,128)(2,1)S(1)} %pad_maximum_fusion.1), channel_id=1, source_target_pairs={{0,2},{1,3},{2,0},{3,1},{4,6},{5,7},{6,4},{7,5},{8,10},{9,11},{10,... | collective-permute-start | bytes 884744 | tf_op jit(solution)/shard_map/ppermute | solution.py:33
  27.7 1.7 %collective-permute-start.13 = (bf16[64,1792]{1,0:T(8,128)(2,1)S(1)}, bf16[64,1792]{1,0:T(8,128)(2,1)S(1)}, u32[]{:S(2)}, u32[]{:S(2)}) collective-permute-start(bf16[64,1792]{1,0:T(8,128)(2,1)S(1)} %collective-permute-done.12.refs_15_), channel_id=1, source_target_pairs={{0,16},{1,17},{2,18},{3,19},{4,20},{5,21},{6,22},{7,23},{8,24},{9,... | collective-permute-start | bytes 688136 | tf_op jit(solution)/shard_map/ppermute | solution.py:33
  30.4 1.1 collective-permute-start.10
  32.4 3.8 %attend.2.refs_0_ = bf16[256,512]{1,0:T(8,128)(2,1)S(1)} custom-call(bf16[1024,640]{1,0:T(8,128)(2,1)S(1)} %get-tuple-element.23.queries, bf16[640,768]{1,0:T(8,128)(2,1)S(1)} %get-tuple-element.24.keys, f32[256,768]{1,0:T(8,128)S(1)} %get-tuple-element.25.hidden, bf16[8,512,128]{2,1,0:T(8,128)(2,1)S(1)} %copy-done.5, bf16[512,512]{1,0:T(8,128)(2,1)S(1)} %fusion.reorder), custom_call_target="tpu_custom_call" | custom-call | flops 1946157056 | bytes 5242880 | tf_op jit(solution)/shard_map/attend/pallas_call | solution.py:249
  36.2 1.0 collective-permute-start.14
  37.2 2.0 %collective-permute-start.18 = (bf16[64,1792]{1,0:T(8,128)(2,1)S(1)}, bf16[64,1792]{1,0:T(8,128)(2,1)S(1)}, u32[]{:S(2)}, u32[]{:S(2)}) collective-permute-start(bf16[64,1792]{1,0:T(8,128)(2,1)S(1)} %collective-permute-done.15.refs_16_), channel_id=1, source_target_pairs={{0,112},{1,113},{2,114},{3,115},{4,116},{5,117},{6,118},{7,119},{8... | collective-permute-start | bytes 688136 | tf_op jit(solution)/shard_map/ppermute | solution.py:33
  39.2 3.8 %attend.3.refs_1_ = bf16[256,512]{1,0:T(8,128)(2,1)S(1)} custom-call(bf16[1024,640]{1,0:T(8,128)(2,1)S(1)} %get-tuple-element.26.queries, bf16[640,768]{1,0:T(8,128)(2,1)S(1)} %get-tuple-element.24.keys, f32[256,768]{1,0:T(8,128)S(1)} %get-tuple-element.25.hidden, bf16[8,512,128]{2,1,0:T(8,128)(2,1)S(1)} %copy-done.5, bf16[512,512]{1,0:T(8,128)(2,1)S(1)} %fusion.reorder), custom_call_target="tpu_custom_call" | custom-call | flops 1946157056 | bytes 5242880 | tf_op jit(solution)/shard_map/attend/pallas_call | solution.py:249
  43.0 2.9 %collective-permute-done.14.refs_13_ = bf16[64,1792]{1,0:T(8,128)(2,1)S(1)} collective-permute-done((bf16[64,1792]{1,0:T(8,128)(2,1)S(1)}, bf16[64,1792]{1,0:T(8,128)(2,1)S(1)}, u32[]{:S(2)}, u32[]{:S(2)}) %collective-permute-start.14) | collective-permute-done | bytes 229408 | tf_op jit(solution)/shard_map/ppermute | solution.py:33
  46.4 2.3 %collective-permute-start.11 = (bf16[64,1792]{1,0:T(8,128)(2,1)S(1)}, bf16[64,1792]{1,0:T(8,128)(2,1)S(1)}, u32[]{:S(2)}, u32[]{:S(2)}) collective-permute-start(bf16[64,1792]{1,0:T(8,128)(2,1)S(1)} %collective-permute-done.10.refs_10_), channel_id=1, source_target_pairs={{0,112},{1,113},{2,114},{3,115},{4,116},{5,117},{6,118},{7,119},{8... | collective-permute-start | bytes 688136 | tf_op jit(solution)/shard_map/ppermute | solution.py:33
  48.7 0.7 collective-permute-start.6
  49.4 3.0 %collective-permute-done.11.refs_11_ = bf16[64,1792]{1,0:T(8,128)(2,1)S(1)} collective-permute-done((bf16[64,1792]{1,0:T(8,128)(2,1)S(1)}, bf16[64,1792]{1,0:T(8,128)(2,1)S(1)}, u32[]{:S(2)}, u32[]{:S(2)}) %collective-permute-start.11) | collective-permute-done | bytes 229408 | tf_op jit(solution)/shard_map/ppermute | solution.py:33
  52.4 0.7 collective-permute-start.8
  53.1 4.3 %collective-permute-done.19.refs_18_ = bf16[64,1792]{1,0:T(8,128)(2,1)S(1)} collective-permute-done((bf16[64,1792]{1,0:T(8,128)(2,1)S(1)}, bf16[64,1792]{1,0:T(8,128)(2,1)S(1)}, u32[]{:S(2)}, u32[]{:S(2)}) %collective-permute-start.19) | collective-permute-done | bytes 229408 | tf_op jit(solution)/shard_map/ppermute | solution.py:33
  57.3 3.4 %collective-permute-start.20 = (bf16[64,1792]{1,0:T(8,128)(2,1)S(1)}, bf16[64,1792]{1,0:T(8,128)(2,1)S(1)}, u32[]{:S(2)}, u32[]{:S(2)}) collective-permute-start(bf16[64,1792]{1,0:T(8,128)(2,1)S(1)} %collective-permute-done.19.refs_18_), channel_id=1, source_target_pairs={{0,112},{1,113},{2,114},{3,115},{4,116},{5,117},{6,118},{7,119},{8... | collective-permute-start | bytes 688136 | tf_op jit(solution)/shard_map/ppermute | solution.py:33
  60.8 0.7 collective-permute-start.5
  61.5 0.8 collective-permute-start.7
  62.3 1.4 %collective-permute-done.20.refs_19_ = bf16[64,1792]{1,0:T(8,128)(2,1)S(1)} collective-permute-done((bf16[64,1792]{1,0:T(8,128)(2,1)S(1)}, bf16[64,1792]{1,0:T(8,128)(2,1)S(1)}, u32[]{:S(2)}, u32[]{:S(2)}) %collective-permute-start.20) | collective-permute-done | bytes 229408 | tf_op jit(solution)/shard_map/ppermute | solution.py:33
  63.7 3.4 %collective-permute-start.21 = (bf16[64,1792]{1,0:T(8,128)(2,1)S(1)}, bf16[64,1792]{1,0:T(8,128)(2,1)S(1)}, u32[]{:S(2)}, u32[]{:S(2)}) collective-permute-start(bf16[64,1792]{1,0:T(8,128)(2,1)S(1)} %collective-permute-done.20.refs_19_), channel_id=1, source_target_pairs={{0,112},{1,113},{2,114},{3,115},{4,116},{5,117},{6,118},{7,119},{8... | collective-permute-start | bytes 688136 | tf_op jit(solution)/shard_map/ppermute | solution.py:33
  67.3 4.5 %collective-permute-done.7.refs_5_ = bf16[256,512]{1,0:T(8,128)(2,1)S(1)} collective-permute-done((bf16[256,512]{1,0:T(8,128)(2,1)S(1)}, bf16[256,512]{1,0:T(8,128)(2,1)S(1)}, u32[]{:S(2)}, u32[]{:S(2)}) %collective-permute-start.7) | collective-permute-done | bytes 262176 | tf_op jit(solution)/shard_map/ppermute | solution.py:33
  71.8 1.4 %collective-permute-done.22.refs_21_ = bf16[64,1792]{1,0:T(8,128)(2,1)S(1)} collective-permute-done((bf16[64,1792]{1,0:T(8,128)(2,1)S(1)}, bf16[64,1792]{1,0:T(8,128)(2,1)S(1)}, u32[]{:S(2)}, u32[]{:S(2)}) %collective-permute-start.22) | collective-permute-done | bytes 229408 | tf_op jit(solution)/shard_map/ppermute | solution.py:33
  73.2 2.5 %project.3 = (bf16[256,896]{1,0:T(8,128)(2,1)S(1)}, bf16[3,256,896]{2,1,0:T(8,128)(2,1)S(1)}) custom-call(bf16[256,512]{1,0:T(8,128)(2,1)S(1)} %attend.2.refs_0_, bf16[256,512]{1,0:T(8,128)(2,1)S(1)} %attend.3.refs_1_, bf16[256,512]{1,0:T(8,128)(2,1)S(1)} %collective-permute-done.3.refs_2_, bf16[256,512]{1,0:T(8,128)(2,1)S(1)} %collective-permute-done.4.refs_3_, ...), custom_call_target="tpu_custom_call" | custom-call | flops 1879048192 | bytes 8388608 | tf_op jit(solution)/shard_map/project/pallas_call | solution.py:249
  75.7 4.2 %collective-permute-start.23 = (bf16[3,256,896]{2,1,0:T(8,128)(2,1)S(1)}, bf16[3,256,896]{2,1,0:T(8,128)(2,1)S(1)}, u32[]{:S(2)}, u32[]{:S(2)}) collective-permute-start(bf16[3,256,896]{2,1,0:T(8,128)(2,1)S(1)} %get-tuple-element.36), channel_id=1, source_target_pairs={{0,2},{1,3},{2,0},{3,1},{4,6},{5,7},{6,4},{7,5},{8,10},{9,11},{10,... | collective-permute-start | bytes 4128776 | tf_op jit(solution)/shard_map/ppermute | solution.py:33
  80.1 2.3 %project.2 = (f32[256,896]{1,0:T(8,128)S(1)}, f32[3,256,896]{2,1,0:T(8,128)S(1)}) custom-call(bf16[256,512]{1,0:T(8,128)(2,1)S(1)} %attend.2.refs_0_, bf16[256,512]{1,0:T(8,128)(2,1)S(1)} %attend.3.refs_1_, bf16[256,512]{1,0:T(8,128)(2,1)S(1)} %collective-permute-done.3.refs_2_, bf16[256,512]{1,0:T(8,128)(2,1)S(1)} %collective-permute-done.4.refs_3_, ...), custom_call_target="tpu_custom_call" | custom-call | flops 1879048192 | bytes 8388608 | tf_op jit(solution)/shard_map/project/pallas_call | solution.py:249
  82.4 1.0 collective-permute-done.24
  83.5 1.3 %collective-permute-start.25 = (bf16[128,896]{1,0:T(8,128)(2,1)S(1)}, bf16[128,896]{1,0:T(8,128)(2,1)S(1)}, u32[]{:S(2)}, u32[]{:S(2)}) collective-permute-start(bf16[128,896]{1,0:T(8,128)(2,1)S(1)} %get-tuple-element.48), channel_id=1, source_target_pairs={{0,4},{1,5},{2,6},{3,7},{4,8},{5,9},{6,10},{7,11},{8,12},{9,13},{1... | collective-permute-start | bytes 688136 | tf_op jit(solution)/shard_map/ppermute | solution.py:33
  84.8 1.5 %collective-permute-start.30 = (bf16[128,896]{1,0:T(8,128)(2,1)S(1)}, bf16[128,896]{1,0:T(8,128)(2,1)S(1)}, u32[]{:S(2)}, u32[]{:S(2)}) collective-permute-start(bf16[128,896]{1,0:T(8,128)(2,1)S(1)} %get-tuple-element.49), channel_id=1, source_target_pairs={{0,12},{1,13},{2,14},{3,15},{4,0},{5,1},{6,2},{7,3},{8,4},{9,5},{1... | collective-permute-start | bytes 688136 | tf_op jit(solution)/shard_map/ppermute | solution.py:33
  86.6 1.3 %collective-permute-start.27 = (bf16[128,896]{1,0:T(8,128)(2,1)S(1)}, bf16[128,896]{1,0:T(8,128)(2,1)S(1)}, u32[]{:S(2)}, u32[]{:S(2)}) collective-permute-start(bf16[128,896]{1,0:T(8,128)(2,1)S(1)} %fusion.12), channel_id=1, source_target_pairs={{0,12},{1,13},{2,14},{3,15},{4,0},{5,1},{6,2},{7,3},{8,4},{9,5},{1... | collective-permute-start | bytes 688136 | tf_op jit(solution)/shard_map/ppermute | solution.py:33
  88.1 3.2 %collective-permute-done.30 = bf16[128,896]{1,0:T(8,128)(2,1)S(1)} collective-permute-done((bf16[128,896]{1,0:T(8,128)(2,1)S(1)}, bf16[128,896]{1,0:T(8,128)(2,1)S(1)}, u32[]{:S(2)}, u32[]{:S(2)}) %collective-permute-start.30) | collective-permute-done | bytes 229408 | tf_op jit(solution)/shard_map/ppermute | solution.py:33
  91.3 2.8 %collective-permute-start.31 = (bf16[128,896]{1,0:T(8,128)(2,1)S(1)}, bf16[128,896]{1,0:T(8,128)(2,1)S(1)}, u32[]{:S(2)}, u32[]{:S(2)}) collective-permute-start(bf16[128,896]{1,0:T(8,128)(2,1)S(1)} %fusion.2), channel_id=1, source_target_pairs={{0,12},{1,13},{2,14},{3,15},{4,0},{5,1},{6,2},{7,3},{8,4},{9,5},{1... | collective-permute-start | bytes 688136 | tf_op jit(solution)/shard_map/ppermute | solution.py:33
  94.2 2.0 %collective-permute-done.27 = bf16[128,896]{1,0:T(8,128)(2,1)S(1)} collective-permute-done((bf16[128,896]{1,0:T(8,128)(2,1)S(1)}, bf16[128,896]{1,0:T(8,128)(2,1)S(1)}, u32[]{:S(2)}, u32[]{:S(2)}) %collective-permute-start.27) | collective-permute-done | bytes 229408 | tf_op jit(solution)/shard_map/ppermute | solution.py:33
  96.2 4.9 %collective-permute-done.31 = bf16[128,896]{1,0:T(8,128)(2,1)S(1)} collective-permute-done((bf16[128,896]{1,0:T(8,128)(2,1)S(1)}, bf16[128,896]{1,0:T(8,128)(2,1)S(1)}, u32[]{:S(2)}, u32[]{:S(2)}) %collective-permute-start.31) | collective-permute-done | bytes 229408 | tf_op jit(solution)/shard_map/ppermute | solution.py:33
  101.3 5.4 %collective-permute-start.28 = (bf16[128,896]{1,0:T(8,128)(2,1)S(1)}, bf16[128,896]{1,0:T(8,128)(2,1)S(1)}, u32[]{:S(2)}, u32[]{:S(2)}) collective-permute-start(bf16[128,896]{1,0:T(8,128)(2,1)S(1)} %get-tuple-element.44), channel_id=1, source_target_pairs={{0,0},{1,1},{2,128},{3,129},{4,4},{5,5},{6,132},{7,133},{8,8},{9,9... | collective-permute-start | bytes 688136 | tf_op jit(solution)/shard_map/ppermute | solution.py:33
  107.1 4.0 %collective-permute-done.28 = bf16[128,896]{1,0:T(8,128)(2,1)S(1)} collective-permute-done((bf16[128,896]{1,0:T(8,128)(2,1)S(1)}, bf16[128,896]{1,0:T(8,128)(2,1)S(1)}, u32[]{:S(2)}, u32[]{:S(2)}) %collective-permute-start.28) | collective-permute-done | bytes 229408 | tf_op jit(solution)/shard_map/ppermute | solution.py:33
  111.0 2.0 %collective-permute-done.32 = bf16[128,896]{1,0:T(8,128)(2,1)S(1)} collective-permute-done((bf16[128,896]{1,0:T(8,128)(2,1)S(1)}, bf16[128,896]{1,0:T(8,128)(2,1)S(1)}, u32[]{:S(2)}, u32[]{:S(2)}) %collective-permute-start.32) | collective-permute-done | bytes 229408 | tf_op jit(solution)/shard_map/ppermute | solution.py:33
  113.4 0.9 maximum_maximum_fusion
  (69 shorter events, 4.0 us)
Async XLA Ops:
  0.0 20.9 %copy-start.1 = (bf16[8,128,512]{2,1,0:T(8,128)(2,1)S(1)}, bf16[8,128,512]{2,1,0:T(8,128)(2,1)}, u32[]{:S(2)}) copy-start(bf16[8,128,512]{2,1,0:T(8,128)(2,1)} %w_key_up.1) | copy-start | bytes 3145732
  0.0 20.9 %copy-start.2 = (bf16[256,1536]{1,0:T(8,128)(2,1)S(1)}, bf16[256,1536]{1,0:T(8,128)(2,1)}, u32[]{:S(2)}) copy-start(bf16[256,1536]{1,0:T(8,128)(2,1)} %rows.1) | copy-start | bytes 2359300
  1.1 24.6 %collective-permute-start.1 = (bf16[576,128]{1,0:T(8,128)(2,1)S(1)}, bf16[576,128]{1,0:T(8,128)(2,1)S(1)}, u32[]{:S(2)}, u32[]{:S(2)}) collective-permute-start(bf16[576,128]{1,0:T(8,128)(2,1)S(1)} %dynamic-slice_bitcast_fusion), channel_id=1, source_target_pairs={{0,32},{16,48},{32,64},{48,80},{64,96},{80,112},{96,128},{112,144}... | collective-permute-start | bytes 442376 | tf_op jit(solution)/shard_map/ppermute | solution.py:295
  6.8 18.8 %collective-permute-start = (bf16[576,128]{1,0:T(8,128)(2,1)S(1)}, bf16[576,128]{1,0:T(8,128)(2,1)S(1)}, u32[]{:S(2)}, u32[]{:S(2)}) collective-permute-start(bf16[576,128]{1,0:T(8,128)(2,1)S(1)} %dynamic-slice_bitcast_fusion), channel_id=1, source_target_pairs={{0,16},{16,32},{32,48},{48,64},{64,80},{80,96},{96,112},{112,128},... | collective-permute-start | bytes 442376 | tf_op jit(solution)/shard_map/ppermute | solution.py:295
  12.6 15.1 %collective-permute-start.12 = (bf16[64,1792]{1,0:T(8,128)(2,1)}, bf16[64,1792]{1,0:T(8,128)(2,1)S(1)}, u32[]{:S(2)}, u32[]{:S(2)}) collective-permute-start(bf16[64,1792]{1,0:T(8,128)(2,1)} %get-tuple-element.27.refs_8_), channel_id=1, source_target_pairs={{0,16},{1,17},{2,18},{3,19},{4,20},{5,21},{6,22},{7,23},{8,24},{9,... | collective-permute-start | bytes 688136 | tf_op jit(solution)/shard_map/ppermute | solution.py:33
  15.4 15.0 %collective-permute-start.9 = (bf16[64,1792]{1,0:T(8,128)(2,1)}, bf16[64,1792]{1,0:T(8,128)(2,1)S(1)}, u32[]{:S(2)}, u32[]{:S(2)}) collective-permute-start(bf16[64,1792]{1,0:T(8,128)(2,1)} %get-tuple-element.27.refs_8_), channel_id=1, source_target_pairs={{0,112},{1,113},{2,114},{3,115},{4,116},{5,117},{6,118},{7,119},{8... | collective-permute-start | bytes 688136 | tf_op jit(solution)/shard_map/ppermute | solution.py:33
  16.2 15.3 %collective-permute-start.15 = (bf16[64,1792]{1,0:T(8,128)(2,1)}, bf16[64,1792]{1,0:T(8,128)(2,1)S(1)}, u32[]{:S(2)}, u32[]{:S(2)}) collective-permute-start(bf16[64,1792]{1,0:T(8,128)(2,1)} %get-tuple-element.32), channel_id=1, source_target_pairs={{0,129},{1,128},{2,131},{3,130},{4,133},{5,132},{6,135},{7,134},{8... | collective-permute-start | bytes 688136 | tf_op jit(solution)/shard_map/ppermute | solution.py:33
  18.2 1.9 %copy-start.7 = (f32[32]{0:T(128)}, f32[32]{0:T(128)S(1)}, u32[]{:S(2)}) copy-start(f32[32]{0:T(128)S(1)} %multiply_power_fusion) | copy-start | bytes 388
  20.9 2.3 %copy-start = (bf16[1536,1536]{1,0:T(8,128)(2,1)S(1)}, bf16[1536,1536]{1,0:T(8,128)(2,1)}, u32[]{:S(2)}) copy-start(bf16[1536,1536]{1,0:T(8,128)(2,1)} %w_query.1) | copy-start | bytes 14155780
  23.3 6.1 %copy-start.8 = (f32[32]{0:T(128)S(1)}, f32[32]{0:T(128)}, u32[]{:S(2)}) copy-start(f32[32]{0:T(128)} %copy-done.7) | copy-start | bytes 388
  23.3 8.7 %copy-start.3 = (bf16[256,576]{0,1:T(8,128)(2,1)S(1)}, bf16[256,576]{0,1:T(8,128)(2,1)}, u32[]{:S(2)}) copy-start(bf16[256,576]{0,1:T(8,128)(2,1)} %param.9) | copy-start | bytes 884740
  23.3 8.7 %copy-start.4 = (bf16[512,576]{0,1:T(8,128)(2,1)S(1)}, bf16[512,576]{0,1:T(8,128)(2,1)}, u32[]{:S(2)}) copy-start(bf16[512,576]{0,1:T(8,128)(2,1)} %param.10) | copy-start | bytes 1769476
  25.6 6.8 %copy-start.5 = (bf16[8,512,128]{2,1,0:T(8,128)(2,1)S(1)}, bf16[8,512,128]{2,1,0:T(8,128)(2,1)}, u32[]{:S(2)}) copy-start(bf16[8,512,128]{2,1,0:T(8,128)(2,1)} %w_value_up.3) | copy-start | bytes 3145732
  25.7 6.3 %collective-permute-start.2 = (bf16[576,256]{1,0:T(8,128)(2,1)S(1)}, bf16[576,256]{1,0:T(8,128)(2,1)S(1)}, u32[]{:S(2)}, u32[]{:S(2)}) collective-permute-start(bf16[576,256]{1,0:T(8,128)(2,1)S(1)} %pad_maximum_fusion.1), channel_id=1, source_target_pairs={{0,2},{1,3},{2,0},{3,1},{4,6},{5,7},{6,4},{7,5},{8,10},{9,11},{10,... | collective-permute-start | bytes 884744 | tf_op jit(solution)/shard_map/ppermute | solution.py:33
  27.7 8.5 %collective-permute-start.13 = (bf16[64,1792]{1,0:T(8,128)(2,1)S(1)}, bf16[64,1792]{1,0:T(8,128)(2,1)S(1)}, u32[]{:S(2)}, u32[]{:S(2)}) collective-permute-start(bf16[64,1792]{1,0:T(8,128)(2,1)S(1)} %collective-permute-done.12.refs_15_), channel_id=1, source_target_pairs={{0,16},{1,17},{2,18},{3,19},{4,20},{5,21},{6,22},{7,23},{8,24},{9,... | collective-permute-start | bytes 688136 | tf_op jit(solution)/shard_map/ppermute | solution.py:33
  30.4 12.5 %collective-permute-start.10 = (bf16[64,1792]{1,0:T(8,128)(2,1)S(1)}, bf16[64,1792]{1,0:T(8,128)(2,1)S(1)}, u32[]{:S(2)}, u32[]{:S(2)}) collective-permute-start(bf16[64,1792]{1,0:T(8,128)(2,1)S(1)} %collective-permute-done.9.refs_9_), channel_id=1, source_target_pairs={{0,112},{1,113},{2,114},{3,115},{4,116},{5,117},{6,118},{7,119},{8... | collective-permute-start | bytes 688136 | tf_op jit(solution)/shard_map/ppermute | solution.py:33
  31.6 11.4 %collective-permute-start.16 = (bf16[64,1792]{1,0:T(8,128)(2,1)S(1)}, bf16[64,1792]{1,0:T(8,128)(2,1)S(1)}, u32[]{:S(2)}, u32[]{:S(2)}) collective-permute-start(bf16[64,1792]{1,0:T(8,128)(2,1)S(1)} %collective-permute-done.15.refs_16_), channel_id=1, source_target_pairs={{0,16},{1,17},{2,18},{3,19},{4,20},{5,21},{6,22},{7,23},{8,24},{9,... | collective-permute-start | bytes 688136 | tf_op jit(solution)/shard_map/ppermute | solution.py:33
  36.2 9.7 %collective-permute-start.14 = (bf16[64,1792]{1,0:T(8,128)(2,1)S(1)}, bf16[64,1792]{1,0:T(8,128)(2,1)S(1)}, u32[]{:S(2)}, u32[]{:S(2)}) collective-permute-start(bf16[64,1792]{1,0:T(8,128)(2,1)S(1)} %collective-permute-done.13.refs_14_), channel_id=1, source_target_pairs={{0,16},{1,17},{2,18},{3,19},{4,20},{5,21},{6,22},{7,23},{8,24},{9,... | collective-permute-start | bytes 688136 | tf_op jit(solution)/shard_map/ppermute | solution.py:33
  37.2 11.5 %collective-permute-start.18 = (bf16[64,1792]{1,0:T(8,128)(2,1)S(1)}, bf16[64,1792]{1,0:T(8,128)(2,1)S(1)}, u32[]{:S(2)}, u32[]{:S(2)}) collective-permute-start(bf16[64,1792]{1,0:T(8,128)(2,1)S(1)} %collective-permute-done.15.refs_16_), channel_id=1, source_target_pairs={{0,112},{1,113},{2,114},{3,115},{4,116},{5,117},{6,118},{7,119},{8... | collective-permute-start | bytes 688136 | tf_op jit(solution)/shard_map/ppermute | solution.py:33
  42.9 30.3 %copy-start.6 = (bf16[64,1792]{1,0:T(8,128)(2,1)S(1)}, bf16[64,1792]{1,0:T(8,128)(2,1)}, u32[]{:S(2)}) copy-start(bf16[64,1792]{1,0:T(8,128)(2,1)} %get-tuple-element.27.refs_8_) | copy-start | bytes 688132
  45.9 15.6 %collective-permute-start.17 = (bf16[128,1792]{1,0:T(8,128)(2,1)S(1)}, bf16[128,1792]{1,0:T(8,128)(2,1)S(1)}, u32[]{:S(2)}, u32[]{:S(2)}) collective-permute-start(bf16[128,1792]{1,0:T(8,128)(2,1)S(1)} %pad_maximum_fusion), channel_id=1, source_target_pairs={{0,16},{1,17},{2,18},{3,19},{4,20},{5,21},{6,22},{7,23},{8,24},{9,... | collective-permute-start | bytes 1376264 | tf_op jit(solution)/shard_map/ppermute | solution.py:33
  46.4 6.0 %collective-permute-start.11 = (bf16[64,1792]{1,0:T(8,128)(2,1)S(1)}, bf16[64,1792]{1,0:T(8,128)(2,1)S(1)}, u32[]{:S(2)}, u32[]{:S(2)}) collective-permute-start(bf16[64,1792]{1,0:T(8,128)(2,1)S(1)} %collective-permute-done.10.refs_10_), channel_id=1, source_target_pairs={{0,112},{1,113},{2,114},{3,115},{4,116},{5,117},{6,118},{7,119},{8... | collective-permute-start | bytes 688136 | tf_op jit(solution)/shard_map/ppermute | solution.py:33
  48.7 8.7 %collective-permute-start.19 = (bf16[64,1792]{1,0:T(8,128)(2,1)S(1)}, bf16[64,1792]{1,0:T(8,128)(2,1)S(1)}, u32[]{:S(2)}, u32[]{:S(2)}) collective-permute-start(bf16[64,1792]{1,0:T(8,128)(2,1)S(1)} %collective-permute-done.18.refs_17_), channel_id=1, source_target_pairs={{0,112},{1,113},{2,114},{3,115},{4,116},{5,117},{6,118},{7,119},{8... | collective-permute-start | bytes 688136 | tf_op jit(solution)/shard_map/ppermute | solution.py:33
  48.7 12.0 %collective-permute-start.3 = (bf16[256,512]{1,0:T(8,128)(2,1)S(1)}, bf16[256,512]{1,0:T(8,128)(2,1)S(1)}, u32[]{:S(2)}, u32[]{:S(2)}) collective-permute-start(bf16[256,512]{1,0:T(8,128)(2,1)S(1)} %attend.2.refs_0_), channel_id=1, source_target_pairs={{0,1},{1,0},{2,3},{3,2},{4,5},{5,4},{6,7},{7,6},{8,9},{9,8},{10,11... | collective-permute-start | bytes 786440 | tf_op jit(solution)/shard_map/ppermute | solution.py:33
  48.7 12.0 %collective-permute-start.6 = (bf16[256,512]{1,0:T(8,128)(2,1)S(1)}, bf16[256,512]{1,0:T(8,128)(2,1)S(1)}, u32[]{:S(2)}, u32[]{:S(2)}) collective-permute-start(bf16[256,512]{1,0:T(8,128)(2,1)S(1)} %attend.3.refs_1_), channel_id=1, source_target_pairs={{0,129},{1,128},{2,131},{3,130},{4,133},{5,132},{6,135},{7,134},{8... | collective-permute-start | bytes 786440 | tf_op jit(solution)/shard_map/ppermute | solution.py:33
  52.4 14.7 %collective-permute-start.8 = (bf16[256,512]{1,0:T(8,128)(2,1)S(1)}, bf16[256,512]{1,0:T(8,128)(2,1)S(1)}, u32[]{:S(2)}, u32[]{:S(2)}) collective-permute-start(bf16[256,512]{1,0:T(8,128)(2,1)S(1)} %attend.2.refs_0_), channel_id=1, source_target_pairs={{0,129},{1,128},{2,131},{3,130},{4,133},{5,132},{6,135},{7,134},{8... | collective-permute-start | bytes 786440 | tf_op jit(solution)/shard_map/ppermute | solution.py:33
  57.3 6.4 %collective-permute-start.20 = (bf16[64,1792]{1,0:T(8,128)(2,1)S(1)}, bf16[64,1792]{1,0:T(8,128)(2,1)S(1)}, u32[]{:S(2)}, u32[]{:S(2)}) collective-permute-start(bf16[64,1792]{1,0:T(8,128)(2,1)S(1)} %collective-permute-done.19.refs_18_), channel_id=1, source_target_pairs={{0,112},{1,113},{2,114},{3,115},{4,116},{5,117},{6,118},{7,119},{8... | collective-permute-start | bytes 688136 | tf_op jit(solution)/shard_map/ppermute | solution.py:33
  60.8 6.4 %collective-permute-start.4 = (bf16[256,512]{1,0:T(8,128)(2,1)S(1)}, bf16[256,512]{1,0:T(8,128)(2,1)S(1)}, u32[]{:S(2)}, u32[]{:S(2)}) collective-permute-start(bf16[256,512]{1,0:T(8,128)(2,1)S(1)} %attend.3.refs_1_), channel_id=1, source_target_pairs={{0,1},{1,0},{2,3},{3,2},{4,5},{5,4},{6,7},{7,6},{8,9},{9,8},{10,11... | collective-permute-start | bytes 786440 | tf_op jit(solution)/shard_map/ppermute | solution.py:33
  60.8 6.5 %collective-permute-start.5 = (bf16[256,512]{1,0:T(8,128)(2,1)S(1)}, bf16[256,512]{1,0:T(8,128)(2,1)S(1)}, u32[]{:S(2)}, u32[]{:S(2)}) collective-permute-start(bf16[256,512]{1,0:T(8,128)(2,1)S(1)} %collective-permute-done.3.refs_2_), channel_id=1, source_target_pairs={{0,129},{1,128},{2,131},{3,130},{4,133},{5,132},{6,135},{7,134},{8... | collective-permute-start | bytes 786440 | tf_op jit(solution)/shard_map/ppermute | solution.py:33
  61.5 10.3 %collective-permute-start.7 = (bf16[256,512]{1,0:T(8,128)(2,1)S(1)}, bf16[256,512]{1,0:T(8,128)(2,1)S(1)}, u32[]{:S(2)}, u32[]{:S(2)}) collective-permute-start(bf16[256,512]{1,0:T(8,128)(2,1)S(1)} %collective-permute-done.6.refs_7_), channel_id=1, source_target_pairs={{0,1},{1,0},{2,3},{3,2},{4,5},{5,4},{6,7},{7,6},{8,9},{9,8},{10,11... | collective-permute-start | bytes 786440 | tf_op jit(solution)/shard_map/ppermute | solution.py:33
  63.7 8.1 %collective-permute-start.21 = (bf16[64,1792]{1,0:T(8,128)(2,1)S(1)}, bf16[64,1792]{1,0:T(8,128)(2,1)S(1)}, u32[]{:S(2)}, u32[]{:S(2)}) collective-permute-start(bf16[64,1792]{1,0:T(8,128)(2,1)S(1)} %collective-permute-done.20.refs_19_), channel_id=1, source_target_pairs={{0,112},{1,113},{2,114},{3,115},{4,116},{5,117},{6,118},{7,119},{8... | collective-permute-start | bytes 688136 | tf_op jit(solution)/shard_map/ppermute | solution.py:33
  67.1 6.1 %collective-permute-start.22 = (bf16[64,1792]{1,0:T(8,128)(2,1)S(1)}, bf16[64,1792]{1,0:T(8,128)(2,1)S(1)}, u32[]{:S(2)}, u32[]{:S(2)}) collective-permute-start(bf16[64,1792]{1,0:T(8,128)(2,1)S(1)} %slice.96), channel_id=1, source_target_pairs={{0,16},{1,17},{2,18},{3,19},{4,20},{5,21},{6,22},{7,23},{8,24},{9,... | collective-permute-start | bytes 688136 | tf_op jit(solution)/shard_map/ppermute | solution.py:33
  75.7 10.5 %collective-permute-start.23 = (bf16[3,256,896]{2,1,0:T(8,128)(2,1)S(1)}, bf16[3,256,896]{2,1,0:T(8,128)(2,1)S(1)}, u32[]{:S(2)}, u32[]{:S(2)}) collective-permute-start(bf16[3,256,896]{2,1,0:T(8,128)(2,1)S(1)} %get-tuple-element.36), channel_id=1, source_target_pairs={{0,2},{1,3},{2,0},{3,1},{4,6},{5,7},{6,4},{7,5},{8,10},{9,11},{10,... | collective-permute-start | bytes 4128776 | tf_op jit(solution)/shard_map/ppermute | solution.py:33
  80.0 3.4 %collective-permute-start.24 = (bf16[256,896]{1,0:T(8,128)(2,1)S(1)}, bf16[256,896]{1,0:T(8,128)(2,1)S(1)}, u32[]{:S(2)}, u32[]{:S(2)}) collective-permute-start(bf16[256,896]{1,0:T(8,128)(2,1)S(1)} %get-tuple-element.38), channel_id=1, source_target_pairs={{0,2},{1,3},{2,0},{3,1},{4,6},{5,7},{6,4},{7,5},{8,10},{9,11},{10,... | collective-permute-start | bytes 1376264 | tf_op jit(solution)/shard_map/ppermute | solution.py:33
  83.5 10.6 %collective-permute-start.25 = (bf16[128,896]{1,0:T(8,128)(2,1)S(1)}, bf16[128,896]{1,0:T(8,128)(2,1)S(1)}, u32[]{:S(2)}, u32[]{:S(2)}) collective-permute-start(bf16[128,896]{1,0:T(8,128)(2,1)S(1)} %get-tuple-element.48), channel_id=1, source_target_pairs={{0,4},{1,5},{2,6},{3,7},{4,8},{5,9},{6,10},{7,11},{8,12},{9,13},{1... | collective-permute-start | bytes 688136 | tf_op jit(solution)/shard_map/ppermute | solution.py:33
  84.8 6.5 %collective-permute-start.30 = (bf16[128,896]{1,0:T(8,128)(2,1)S(1)}, bf16[128,896]{1,0:T(8,128)(2,1)S(1)}, u32[]{:S(2)}, u32[]{:S(2)}) collective-permute-start(bf16[128,896]{1,0:T(8,128)(2,1)S(1)} %get-tuple-element.49), channel_id=1, source_target_pairs={{0,12},{1,13},{2,14},{3,15},{4,0},{5,1},{6,2},{7,3},{8,4},{9,5},{1... | collective-permute-start | bytes 688136 | tf_op jit(solution)/shard_map/ppermute | solution.py:33
  86.6 9.6 %collective-permute-start.27 = (bf16[128,896]{1,0:T(8,128)(2,1)S(1)}, bf16[128,896]{1,0:T(8,128)(2,1)S(1)}, u32[]{:S(2)}, u32[]{:S(2)}) collective-permute-start(bf16[128,896]{1,0:T(8,128)(2,1)S(1)} %fusion.12), channel_id=1, source_target_pairs={{0,12},{1,13},{2,14},{3,15},{4,0},{5,1},{6,2},{7,3},{8,4},{9,5},{1... | collective-permute-start | bytes 688136 | tf_op jit(solution)/shard_map/ppermute | solution.py:33
  87.9 8.3 %collective-permute-start.29 = (bf16[128,896]{1,0:T(8,128)(2,1)S(1)}, bf16[128,896]{1,0:T(8,128)(2,1)S(1)}, u32[]{:S(2)}, u32[]{:S(2)}) collective-permute-start(bf16[128,896]{1,0:T(8,128)(2,1)S(1)} %fusion.11), channel_id=1, source_target_pairs={{0,4},{1,5},{2,6},{3,7},{4,8},{5,9},{6,10},{7,11},{8,12},{9,13},{1... | collective-permute-start | bytes 688136 | tf_op jit(solution)/shard_map/ppermute | solution.py:33
  91.3 9.8 %collective-permute-start.31 = (bf16[128,896]{1,0:T(8,128)(2,1)S(1)}, bf16[128,896]{1,0:T(8,128)(2,1)S(1)}, u32[]{:S(2)}, u32[]{:S(2)}) collective-permute-start(bf16[128,896]{1,0:T(8,128)(2,1)S(1)} %fusion.2), channel_id=1, source_target_pairs={{0,12},{1,13},{2,14},{3,15},{4,0},{5,1},{6,2},{7,3},{8,4},{9,5},{1... | collective-permute-start | bytes 688136 | tf_op jit(solution)/shard_map/ppermute | solution.py:33
  94.1 7.0 %collective-permute-start.26 = (bf16[128,896]{1,0:T(8,128)(2,1)S(1)}, bf16[128,896]{1,0:T(8,128)(2,1)S(1)}, u32[]{:S(2)}, u32[]{:S(2)}) collective-permute-start(bf16[128,896]{1,0:T(8,128)(2,1)S(1)} %fusion.7), channel_id=1, source_target_pairs={{0,4},{1,5},{2,6},{3,7},{4,8},{5,9},{6,10},{7,11},{8,12},{9,13},{1... | collective-permute-start | bytes 688136 | tf_op jit(solution)/shard_map/ppermute | solution.py:33
  101.3 9.8 %collective-permute-start.28 = (bf16[128,896]{1,0:T(8,128)(2,1)S(1)}, bf16[128,896]{1,0:T(8,128)(2,1)S(1)}, u32[]{:S(2)}, u32[]{:S(2)}) collective-permute-start(bf16[128,896]{1,0:T(8,128)(2,1)S(1)} %get-tuple-element.44), channel_id=1, source_target_pairs={{0,0},{1,1},{2,128},{3,129},{4,4},{5,5},{6,132},{7,133},{8,8},{9,9... | collective-permute-start | bytes 688136 | tf_op jit(solution)/shard_map/ppermute | solution.py:33
  106.7 6.4 %collective-permute-start.32 = (bf16[128,896]{1,0:T(8,128)(2,1)S(1)}, bf16[128,896]{1,0:T(8,128)(2,1)S(1)}, u32[]{:S(2)}, u32[]{:S(2)}) collective-permute-start(bf16[128,896]{1,0:T(8,128)(2,1)S(1)} %get-tuple-element.45), channel_id=1, source_target_pairs={{0,1},{1,0},{2,129},{3,128},{4,5},{5,4},{6,133},{7,132},{8,9},{9,8... | collective-permute-start | bytes 688136 | tf_op jit(solution)/shard_map/ppermute | solution.py:33

commit v9 on v6

--- a/solution.py
+++ b/solution.py
@@ -53,8 +53,8 @@
     return moved(a, lambda yh, z, x, c, yl: (yh, z, (x + d) % 4, c, yl))
 
 
-def home(a, r):
-    return moved(a, lambda yh, z, x, c, yl: (yh ^ c, z, x, yh, yl ^ r))
+def home(a, r, d=0):
+    return moved(a, lambda yh, z, x, c, yl: (yh ^ c, z, (x + d) % 4, yh, yl ^ r))
 
 
 def turn_of(table):
@@ -371,16 +371,21 @@
     passing_up = along_x(far_sum[:128], 1)
     passing_down = along_x(far_sum[128:], 3)
     sums = [mine_rest[i] + rest[i].astype(F32) for i in range(3)]
-    early_up, early_down = lax.optimization_barrier(
-        (sums[1][128:].astype(BF), sums[2][:128].astype(BF))
-    )
-    early_up, early_down = along_x(early_up, 1), along_x(early_down, 3)
-    late_up = along_x((sums[1][:128] + passing_up.astype(F32)).astype(BF), 1)
-    late_down = along_x((sums[2][128:] + passing_down.astype(F32)).astype(BF), 3)
-    pieces = [
-        home((sums[0][:128] + late_up.astype(F32) + early_down.astype(F32)).astype(BF), 0),
-        home((sums[0][128:] + early_up.astype(F32) + late_down.astype(F32)).astype(BF), 1),
+    early_up, early_down, *own_sum = lax.optimization_barrier(
+        (
+            sums[1][128:].astype(BF),
+            sums[2][:128].astype(BF),
+            sums[0][:128].astype(BF),
+            sums[0][128:].astype(BF),
+        )
+    )
+    parts = [
+        [home(own_sum[0], 0), home(early_down, 0, 3)],
+        [home(own_sum[1], 1), home(early_up, 1, 1)],
     ]
+    parts[0].append(home((sums[1][:128] + passing_up.astype(F32)).astype(BF), 0, 1))
+    parts[1].append(home((sums[2][128:] + passing_down.astype(F32)).astype(BF), 1, 3))
+    pieces = [sum(part.astype(F32) for part in piece).astype(BF) for piece in parts]
     even = yl == 0
     pair = jnp.where(even, pieces[0], pieces[1]), jnp.where(even, pieces[1], pieces[0])
     return jnp.concatenate(

time: 110 us -> 110 us (level)
  starting transfers between devices: 51.4 us -> 64.8 us
  waiting for transfers between devices: 30.7 us -> 17.6 us
    ppermute x29, starting transfers between devices: 42.1 us -> 55.6 us  [moved(): return lax.ppermute(a, AXES, pairs)]
    ppermute x29, waiting for transfers between devices: 30.7 us -> 17.6 us  [moved(): return lax.ppermute(a, AXES, pairs)]
  transfers between devices with their start and end apart: 31 -> 31, of which waited for: 13 -> 10; matrix products, arithmetic and copies ran while one was open for 2% -> 2% of each run, Pallas kernels for 18% -> 18%
where the time goes in v9:
time: 110 us
  starting transfers between devices  64.8 us (59%)
  Pallas kernels  21.9 us (20%)
  waiting for transfers between devices  17.6 us (16%)
  other arithmetic  2.96 us (3%)
  local copies, waits for them, and re-layouts  1.39 us (1%)
    ppermute x29, starting transfers between devices, moved(): return lax.ppermute(a, AXES, pairs)  55.6 us
    pallas_call x6, Pallas kernels, call(): pl.pallas_call(kernel, out_shape=shapes, in_specs=specs, out_specs=whole(...  19.7 us
    ppermute x29, waiting for transfers between devices, moved(): return lax.ppermute(a, AXES, pairs)  17.6 us
    ppermute x2, starting transfers between devices, local(): lax.ppermute(half, CTX, [(i, i + by) for i in range(16 - by)])  9.28 us
    pallas_call x1, Pallas kernels, quarters(): pl.pallas_call(quarter_kernel, out_shape=[jax.ShapeDtypeStruct((64, 1792)...  2.22 us
  transfers between devices with their start and end apart: 31, of which 10 were waited for; matrix products, arithmetic and copies ran while one was open for 2% of the time, Pallas kernels for 18%

profile of v9, /device:TPU:1, one launch (start us, length us, event | category | flops | bytes accessed | tf_op | source)
XLA Modules:
  0.0 109.7 jit_solution(17780028575647648513)
XLA Ops:
  0.0 0.9 dynamic-slice_bitcast_fusion
  0.9 5.7 %collective-permute-start.1 = (bf16[576,128]{1,0:T(8,128)(2,1)S(1)}, bf16[576,128]{1,0:T(8,128)(2,1)S(1)}, u32[]{:S(2)}, u32[]{:S(2)}) collective-permute-start(bf16[576,128]{1,0:T(8,128)(2,1)S(1)} %dynamic-slice_bitcast_fusion), channel_id=1, source_target_pairs={{0,32},{16,48},{32,64},{48,80},{64,96},{80,112},{96,128},{112,144}... | collective-permute-start | bytes 442376 | tf_op jit(solution)/shard_map/ppermute | solution.py:305
  6.7 3.5 %collective-permute-start = (bf16[576,128]{1,0:T(8,128)(2,1)S(1)}, bf16[576,128]{1,0:T(8,128)(2,1)S(1)}, u32[]{:S(2)}, u32[]{:S(2)}) collective-permute-start(bf16[576,128]{1,0:T(8,128)(2,1)S(1)} %dynamic-slice_bitcast_fusion), channel_id=1, source_target_pairs={{0,16},{16,32},{32,48},{48,64},{64,80},{80,96},{96,112},{112,128},... | collective-permute-start | bytes 442376 | tf_op jit(solution)/shard_map/ppermute | solution.py:305
  10.2 2.2 %quarters.1 = (bf16[64,1792]{1,0:T(8,128)(2,1)}, bf16[64,1792]{1,0:T(8,128)(2,1)}) custom-call(bf16[64,7168]{1,0:T(8,128)(2,1)} %bitcast.27), custom_call_target="tpu_custom_call" | custom-call | bytes 2097152 | tf_op jit(solution)/shard_map/quarters/pallas_call | solution.py:247
  12.4 2.8 %collective-permute-start.14 = (bf16[64,1792]{1,0:T(8,128)(2,1)}, bf16[64,1792]{1,0:T(8,128)(2,1)S(1)}, u32[]{:S(2)}, u32[]{:S(2)}) collective-permute-start(bf16[64,1792]{1,0:T(8,128)(2,1)} %get-tuple-element.27.refs_8_), channel_id=1, source_target_pairs={{0,16},{1,17},{2,18},{3,19},{4,20},{5,21},{6,22},{7,23},{8,24},{9,... | collective-permute-start | bytes 688136 | tf_op jit(solution)/shard_map/ppermute | solution.py:33
  15.3 0.8 collective-permute-start.9
  16.1 1.9 %collective-permute-start.11 = (bf16[64,1792]{1,0:T(8,128)(2,1)}, bf16[64,1792]{1,0:T(8,128)(2,1)S(1)}, u32[]{:S(2)}, u32[]{:S(2)}) collective-permute-start(bf16[64,1792]{1,0:T(8,128)(2,1)} %get-tuple-element.29), channel_id=1, source_target_pairs={{0,129},{1,128},{2,131},{3,130},{4,133},{5,132},{6,135},{7,134},{8... | collective-permute-start | bytes 688136 | tf_op jit(solution)/shard_map/ppermute | solution.py:33
  18.2 0.1 fusion.reorder
  18.3 0.8 fusion.7
  19.1 6.9 %queries.1 = (bf16[1024,640]{1,0:T(8,128)(2,1)}, bf16[1024,640]{1,0:T(8,128)(2,1)}) custom-call(bf16[256,1536]{1,0:T(8,128)(2,1)} %rows.1, bf16[1536,1536]{1,0:T(8,128)(2,1)} %w_query.1, bf16[8,128,512]{2,1,0:T(8,128)(2,1)} %w_key_up.1, f32[64,128]{1,0:T(8,128)} %get-tuple-element.57.cosines, f32[64,128]{1,0:T(8,128)} %get-tuple-element.56.sines), custom_call_target="tpu_custom_call" | custom-call | flops 1476395008 | bytes 8388608 | tf_op jit(solution)/shard_map/queries/pallas_call | solution.py:259
  26.1 2.0 %collective-permute-start.2 = (bf16[576,256]{1,0:T(8,128)(2,1)S(1)}, bf16[576,256]{1,0:T(8,128)(2,1)S(1)}, u32[]{:S(2)}, u32[]{:S(2)}) collective-permute-start(bf16[576,256]{1,0:T(8,128)(2,1)S(1)} %pad_maximum_fusion.2), channel_id=1, source_target_pairs={{0,2},{1,3},{2,0},{3,1},{4,6},{5,7},{6,4},{7,5},{8,10},{9,11},{10,... | collective-permute-start | bytes 884744 | tf_op jit(solution)/shard_map/ppermute | solution.py:33
  28.1 1.7 %collective-permute-start.15 = (bf16[64,1792]{1,0:T(8,128)(2,1)S(1)}, bf16[64,1792]{1,0:T(8,128)(2,1)S(1)}, u32[]{:S(2)}, u32[]{:S(2)}) collective-permute-start(bf16[64,1792]{1,0:T(8,128)(2,1)S(1)} %collective-permute-done.14.refs_15_), channel_id=1, source_target_pairs={{0,16},{1,17},{2,18},{3,19},{4,20},{5,21},{6,22},{7,23},{8,24},{9,... | collective-permute-start | bytes 688136 | tf_op jit(solution)/shard_map/ppermute | solution.py:33
  29.8 0.7 collective-permute-start.16
  30.5 0.4 multiply_sine_fusion
  31.6 2.0 %collective-permute-start.10 = (bf16[64,1792]{1,0:T(8,128)(2,1)S(1)}, bf16[64,1792]{1,0:T(8,128)(2,1)S(1)}, u32[]{:S(2)}, u32[]{:S(2)}) collective-permute-start(bf16[64,1792]{1,0:T(8,128)(2,1)S(1)} %collective-permute-done.9.refs_9_), channel_id=1, source_target_pairs={{0,112},{1,113},{2,114},{3,115},{4,116},{5,117},{6,118},{7,119},{8... | collective-permute-start | bytes 688136 | tf_op jit(solution)/shard_map/ppermute | solution.py:33
  33.7 0.6 keys.1
  34.3 3.8 %attend.2.refs_0_ = bf16[256,512]{1,0:T(8,128)(2,1)S(1)} custom-call(bf16[1024,640]{1,0:T(8,128)(2,1)S(1)} %copy-done.3, bf16[640,768]{1,0:T(8,128)(2,1)S(1)} %get-tuple-element.24.keys, f32[256,768]{1,0:T(8,128)S(1)} %get-tuple-element.25.hidden, bf16[8,512,128]{2,1,0:T(8,128)(2,1)S(1)} %copy-done.4, bf16[512,512]{1,0:T(8,128)(2,1)S(1)} %fusion.reorder), custom_call_target="tpu_custom_call" | custom-call | flops 1946157056 | bytes 5242880 | tf_op jit(solution)/shard_map/attend/pallas_call | solution.py:259
  38.1 3.3 %collective-permute-done.16.refs_20_ = bf16[64,1792]{1,0:T(8,128)(2,1)S(1)} collective-permute-done((bf16[64,1792]{1,0:T(8,128)(2,1)S(1)}, bf16[64,1792]{1,0:T(8,128)(2,1)S(1)}, u32[]{:S(2)}, u32[]{:S(2)}) %collective-permute-start.16) | collective-permute-done | bytes 229408 | tf_op jit(solution)/shard_map/ppermute | solution.py:33
  41.4 1.7 %collective-permute-done.12.refs_17_ = bf16[64,1792]{1,0:T(8,128)(2,1)S(1)} collective-permute-done((bf16[64,1792]{1,0:T(8,128)(2,1)S(1)}, bf16[64,1792]{1,0:T(8,128)(2,1)S(1)}, u32[]{:S(2)}, u32[]{:S(2)}) %collective-permute-start.12) | collective-permute-done | bytes 229408 | tf_op jit(solution)/shard_map/ppermute | solution.py:33
  43.1 3.2 %collective-permute-start.13 = (bf16[128,1792]{1,0:T(8,128)(2,1)S(1)}, bf16[128,1792]{1,0:T(8,128)(2,1)S(1)}, u32[]{:S(2)}, u32[]{:S(2)}) collective-permute-start(bf16[128,1792]{1,0:T(8,128)(2,1)S(1)} %pad_maximum_fusion), channel_id=1, source_target_pairs={{0,112},{1,113},{2,114},{3,115},{4,116},{5,117},{6,118},{7,119},{8... | collective-permute-start | bytes 1376264 | tf_op jit(solution)/shard_map/ppermute | solution.py:33
  46.4 3.8 %attend.3.refs_1_ = bf16[256,512]{1,0:T(8,128)(2,1)S(1)} custom-call(bf16[1024,640]{1,0:T(8,128)(2,1)S(1)} %copy-done.2, bf16[640,768]{1,0:T(8,128)(2,1)S(1)} %get-tuple-element.24.keys, f32[256,768]{1,0:T(8,128)S(1)} %get-tuple-element.25.hidden, bf16[8,512,128]{2,1,0:T(8,128)(2,1)S(1)} %copy-done.4, bf16[512,512]{1,0:T(8,128)(2,1)S(1)} %fusion.reorder), custom_call_target="tpu_custom_call" | custom-call | flops 1946157056 | bytes 5242880 | tf_op jit(solution)/shard_map/attend/pallas_call | solution.py:259
  50.2 2.7 %collective-permute-start.6 = (bf16[256,512]{1,0:T(8,128)(2,1)S(1)}, bf16[256,512]{1,0:T(8,128)(2,1)S(1)}, u32[]{:S(2)}, u32[]{:S(2)}) collective-permute-start(bf16[256,512]{1,0:T(8,128)(2,1)S(1)} %attend.3.refs_1_), channel_id=1, source_target_pairs={{0,129},{1,128},{2,131},{3,130},{4,133},{5,132},{6,135},{7,134},{8... | collective-permute-start | bytes 786440 | tf_op jit(solution)/shard_map/ppermute | solution.py:33
  52.9 1.7 %collective-permute-done.13.refs_11_ = bf16[128,1792]{1,0:T(8,128)(2,1)S(1)} collective-permute-done((bf16[128,1792]{1,0:T(8,128)(2,1)S(1)}, bf16[128,1792]{1,0:T(8,128)(2,1)S(1)}, u32[]{:S(2)}, u32[]{:S(2)}) %collective-permute-start.13) | collective-permute-done | bytes 458784 | tf_op jit(solution)/shard_map/ppermute | solution.py:33
  54.7 3.5 %collective-permute-start.19 = (bf16[64,1792]{1,0:T(8,128)(2,1)S(1)}, bf16[64,1792]{1,0:T(8,128)(2,1)S(1)}, u32[]{:S(2)}, u32[]{:S(2)}) collective-permute-start(bf16[64,1792]{1,0:T(8,128)(2,1)S(1)} %slice.92), channel_id=1, source_target_pairs={{0,112},{1,113},{2,114},{3,115},{4,116},{5,117},{6,118},{7,119},{8... | collective-permute-start | bytes 688136 | tf_op jit(solution)/shard_map/ppermute | solution.py:33
  58.3 0.6 collective-permute-start.5
  58.9 1.0 collective-permute-done.6.refs_7_
  59.8 0.2 collective-permute-start.7
  60.0 1.1 collective-permute-done.19.refs_18_
  61.1 3.1 %collective-permute-start.20 = (bf16[64,1792]{1,0:T(8,128)(2,1)S(1)}, bf16[64,1792]{1,0:T(8,128)(2,1)S(1)}, u32[]{:S(2)}, u32[]{:S(2)}) collective-permute-start(bf16[64,1792]{1,0:T(8,128)(2,1)S(1)} %collective-permute-done.19.refs_18_), channel_id=1, source_target_pairs={{0,112},{1,113},{2,114},{3,115},{4,116},{5,117},{6,118},{7,119},{8... | collective-permute-start | bytes 688136 | tf_op jit(solution)/shard_map/ppermute | solution.py:33
  64.2 0.6 collective-permute-done.5.refs_4_
  64.8 4.2 %collective-permute-done.7.refs_5_ = bf16[256,512]{1,0:T(8,128)(2,1)S(1)} collective-permute-done((bf16[256,512]{1,0:T(8,128)(2,1)S(1)}, bf16[256,512]{1,0:T(8,128)(2,1)S(1)}, u32[]{:S(2)}, u32[]{:S(2)}) %collective-permute-start.7) | collective-permute-done | bytes 262176 | tf_op jit(solution)/shard_map/ppermute | solution.py:33
  69.0 2.3 %project.3 = (bf16[256,896]{1,0:T(8,128)(2,1)S(1)}, bf16[3,256,896]{2,1,0:T(8,128)(2,1)S(1)}) custom-call(bf16[256,512]{1,0:T(8,128)(2,1)S(1)} %attend.2.refs_0_, bf16[256,512]{1,0:T(8,128)(2,1)S(1)} %attend.3.refs_1_, bf16[256,512]{1,0:T(8,128)(2,1)S(1)} %collective-permute-done.3.refs_2_, bf16[256,512]{1,0:T(8,128)(2,1)S(1)} %collective-permute-done.4.refs_3_, ...), custom_call_target="tpu_custom_call" | custom-call | flops 1879048192 | bytes 8388608 | tf_op jit(solution)/shard_map/project/pallas_call | solution.py:259
  71.3 3.7 %collective-permute-start.21 = (bf16[3,256,896]{2,1,0:T(8,128)(2,1)S(1)}, bf16[3,256,896]{2,1,0:T(8,128)(2,1)S(1)}, u32[]{:S(2)}, u32[]{:S(2)}) collective-permute-start(bf16[3,256,896]{2,1,0:T(8,128)(2,1)S(1)} %get-tuple-element.34), channel_id=1, source_target_pairs={{0,2},{1,3},{2,0},{3,1},{4,6},{5,7},{6,4},{7,5},{8,10},{9,11},{10,... | collective-permute-start | bytes 4128776 | tf_op jit(solution)/shard_map/ppermute | solution.py:33
  75.1 2.3 %project.2 = (f32[256,896]{1,0:T(8,128)S(1)}, f32[3,256,896]{2,1,0:T(8,128)S(1)}) custom-call(bf16[256,512]{1,0:T(8,128)(2,1)S(1)} %attend.2.refs_0_, bf16[256,512]{1,0:T(8,128)(2,1)S(1)} %attend.3.refs_1_, bf16[256,512]{1,0:T(8,128)(2,1)S(1)} %collective-permute-done.3.refs_2_, bf16[256,512]{1,0:T(8,128)(2,1)S(1)} %collective-permute-done.4.refs_3_, ...), custom_call_target="tpu_custom_call" | custom-call | flops 1879048192 | bytes 8388608 | tf_op jit(solution)/shard_map/project/pallas_call | solution.py:259
  77.4 1.0 collective-permute-done.24
  78.5 2.6 %collective-permute-start.29 = (bf16[128,896]{1,0:T(8,128)(2,1)S(1)}, bf16[128,896]{1,0:T(8,128)(2,1)S(1)}, u32[]{:S(2)}, u32[]{:S(2)}) collective-permute-start(bf16[128,896]{1,0:T(8,128)(2,1)S(1)} %get-tuple-element.46), channel_id=1, source_target_pairs={{0,12},{1,13},{2,14},{3,15},{4,0},{5,1},{6,2},{7,3},{8,4},{9,5},{1... | collective-permute-start | bytes 688136 | tf_op jit(solution)/shard_map/ppermute | solution.py:33
  81.1 0.2 add_convert_fusion.1
  81.4 2.9 %collective-permute-start.22 = (bf16[128,896]{1,0:T(8,128)(2,1)S(1)}, bf16[128,896]{1,0:T(8,128)(2,1)S(1)}, u32[]{:S(2)}, u32[]{:S(2)}) collective-permute-start(bf16[128,896]{1,0:T(8,128)(2,1)S(1)} %get-tuple-element.35), channel_id=1, source_target_pairs={{0,0},{1,1},{2,128},{3,129},{4,4},{5,5},{6,132},{7,133},{8,8},{9,9... | collective-permute-start | bytes 688136 | tf_op jit(solution)/shard_map/ppermute | solution.py:33
  84.3 2.8 %collective-permute-start.23 = (bf16[128,896]{1,0:T(8,128)(2,1)S(1)}, bf16[128,896]{1,0:T(8,128)(2,1)S(1)}, u32[]{:S(2)}, u32[]{:S(2)}) collective-permute-start(bf16[128,896]{1,0:T(8,128)(2,1)S(1)} %fusion.6), channel_id=1, source_target_pairs={{0,12},{1,13},{2,140},{3,141},{4,0},{5,1},{6,128},{7,129},{8,4},{9... | collective-permute-start | bytes 688136 | tf_op jit(solution)/shard_map/ppermute | solution.py:33
  87.1 1.7 %collective-permute-start.27 = (bf16[128,896]{1,0:T(8,128)(2,1)S(1)}, bf16[128,896]{1,0:T(8,128)(2,1)S(1)}, u32[]{:S(2)}, u32[]{:S(2)}) collective-permute-start(bf16[128,896]{1,0:T(8,128)(2,1)S(1)} %get-tuple-element.39), channel_id=1, source_target_pairs={{0,1},{1,0},{2,129},{3,128},{4,5},{5,4},{6,133},{7,132},{8,9},{9,8... | collective-permute-start | bytes 688136 | tf_op jit(solution)/shard_map/ppermute | solution.py:33
  88.9 1.0 collective-permute-start.26
  90.0 0.2 collective-permute-done.22
  90.2 15.2 %collective-permute-start.30 = (bf16[128,896]{1,0:T(8,128)(2,1)S(1)}, bf16[128,896]{1,0:T(8,128)(2,1)S(1)}, u32[]{:S(2)}, u32[]{:S(2)}) collective-permute-start(bf16[128,896]{1,0:T(8,128)(2,1)S(1)} %fusion.2), channel_id=1, source_target_pairs={{0,13},{1,12},{2,141},{3,140},{4,1},{5,0},{6,129},{7,128},{8,5},{9... | collective-permute-start | bytes 688136 | tf_op jit(solution)/shard_map/ppermute | solution.py:33
  105.4 2.9 %collective-permute-done.30 = bf16[128,896]{1,0:T(8,128)(2,1)S(1)} collective-permute-done((bf16[128,896]{1,0:T(8,128)(2,1)S(1)}, bf16[128,896]{1,0:T(8,128)(2,1)S(1)}, u32[]{:S(2)}, u32[]{:S(2)}) %collective-permute-start.30) | collective-permute-done | bytes 229408 | tf_op jit(solution)/shard_map/ppermute | solution.py:33
  108.3 0.2 broadcast_select_fusion.1
  108.5 0.1 fusion.29
  108.7 0.1 fusion.30
  108.8 0.9 maximum_maximum_fusion
  (60 shorter events, 1.0 us)
Async XLA Ops:
  0.9 25.1 %collective-permute-start.1 = (bf16[576,128]{1,0:T(8,128)(2,1)S(1)}, bf16[576,128]{1,0:T(8,128)(2,1)S(1)}, u32[]{:S(2)}, u32[]{:S(2)}) collective-permute-start(bf16[576,128]{1,0:T(8,128)(2,1)S(1)} %dynamic-slice_bitcast_fusion), channel_id=1, source_target_pairs={{0,32},{16,48},{32,64},{48,80},{64,96},{80,112},{96,128},{112,144}... | collective-permute-start | bytes 442376 | tf_op jit(solution)/shard_map/ppermute | solution.py:305
  6.7 19.4 %collective-permute-start = (bf16[576,128]{1,0:T(8,128)(2,1)S(1)}, bf16[576,128]{1,0:T(8,128)(2,1)S(1)}, u32[]{:S(2)}, u32[]{:S(2)}) collective-permute-start(bf16[576,128]{1,0:T(8,128)(2,1)S(1)} %dynamic-slice_bitcast_fusion), channel_id=1, source_target_pairs={{0,16},{16,32},{32,48},{48,64},{64,80},{80,96},{96,112},{112,128},... | collective-permute-start | bytes 442376 | tf_op jit(solution)/shard_map/ppermute | solution.py:305
  12.4 15.6 %collective-permute-start.14 = (bf16[64,1792]{1,0:T(8,128)(2,1)}, bf16[64,1792]{1,0:T(8,128)(2,1)S(1)}, u32[]{:S(2)}, u32[]{:S(2)}) collective-permute-start(bf16[64,1792]{1,0:T(8,128)(2,1)} %get-tuple-element.27.refs_8_), channel_id=1, source_target_pairs={{0,16},{1,17},{2,18},{3,19},{4,20},{5,21},{6,22},{7,23},{8,24},{9,... | collective-permute-start | bytes 688136 | tf_op jit(solution)/shard_map/ppermute | solution.py:33
  15.3 16.3 %collective-permute-start.9 = (bf16[64,1792]{1,0:T(8,128)(2,1)}, bf16[64,1792]{1,0:T(8,128)(2,1)S(1)}, u32[]{:S(2)}, u32[]{:S(2)}) collective-permute-start(bf16[64,1792]{1,0:T(8,128)(2,1)} %get-tuple-element.27.refs_8_), channel_id=1, source_target_pairs={{0,112},{1,113},{2,114},{3,115},{4,116},{5,117},{6,118},{7,119},{8... | collective-permute-start | bytes 688136 | tf_op jit(solution)/shard_map/ppermute | solution.py:33
  16.1 13.6 %collective-permute-start.11 = (bf16[64,1792]{1,0:T(8,128)(2,1)}, bf16[64,1792]{1,0:T(8,128)(2,1)S(1)}, u32[]{:S(2)}, u32[]{:S(2)}) collective-permute-start(bf16[64,1792]{1,0:T(8,128)(2,1)} %get-tuple-element.29), channel_id=1, source_target_pairs={{0,129},{1,128},{2,131},{3,130},{4,133},{5,132},{6,135},{7,134},{8... | collective-permute-start | bytes 688136 | tf_op jit(solution)/shard_map/ppermute | solution.py:33
  19.1 14.6 %copy-start = (bf16[256,576]{0,1:T(8,128)(2,1)S(1)}, bf16[256,576]{0,1:T(8,128)(2,1)}, u32[]{:S(2)}) copy-start(bf16[256,576]{0,1:T(8,128)(2,1)} %param.9) | copy-start | bytes 884740
  19.1 14.6 %copy-start.1 = (bf16[512,576]{0,1:T(8,128)(2,1)S(1)}, bf16[512,576]{0,1:T(8,128)(2,1)}, u32[]{:S(2)}) copy-start(bf16[512,576]{0,1:T(8,128)(2,1)} %param.10) | copy-start | bytes 1769476
  26.0 8.3 %copy-start.3 = (bf16[1024,640]{1,0:T(8,128)(2,1)S(1)}, bf16[1024,640]{1,0:T(8,128)(2,1)}, u32[]{:S(2)}) copy-start(bf16[1024,640]{1,0:T(8,128)(2,1)} %get-tuple-element.23.queries) | copy-start | bytes 3932164
  26.0 8.3 %copy-start.4 = (bf16[8,512,128]{2,1,0:T(8,128)(2,1)S(1)}, bf16[8,512,128]{2,1,0:T(8,128)(2,1)}, u32[]{:S(2)}) copy-start(bf16[8,512,128]{2,1,0:T(8,128)(2,1)} %w_value_up.3) | copy-start | bytes 3145732
  26.1 7.6 %collective-permute-start.2 = (bf16[576,256]{1,0:T(8,128)(2,1)S(1)}, bf16[576,256]{1,0:T(8,128)(2,1)S(1)}, u32[]{:S(2)}, u32[]{:S(2)}) collective-permute-start(bf16[576,256]{1,0:T(8,128)(2,1)S(1)} %pad_maximum_fusion.2), channel_id=1, source_target_pairs={{0,2},{1,3},{2,0},{3,1},{4,6},{5,7},{6,4},{7,5},{8,10},{9,11},{10,... | collective-permute-start | bytes 884744 | tf_op jit(solution)/shard_map/ppermute | solution.py:33
  28.1 13.3 %collective-permute-start.15 = (bf16[64,1792]{1,0:T(8,128)(2,1)S(1)}, bf16[64,1792]{1,0:T(8,128)(2,1)S(1)}, u32[]{:S(2)}, u32[]{:S(2)}) collective-permute-start(bf16[64,1792]{1,0:T(8,128)(2,1)S(1)} %collective-permute-done.14.refs_15_), channel_id=1, source_target_pairs={{0,16},{1,17},{2,18},{3,19},{4,20},{5,21},{6,22},{7,23},{8,24},{9,... | collective-permute-start | bytes 688136 | tf_op jit(solution)/shard_map/ppermute | solution.py:33
  29.8 11.6 %collective-permute-start.16 = (bf16[64,1792]{1,0:T(8,128)(2,1)S(1)}, bf16[64,1792]{1,0:T(8,128)(2,1)S(1)}, u32[]{:S(2)}, u32[]{:S(2)}) collective-permute-start(bf16[64,1792]{1,0:T(8,128)(2,1)S(1)} %collective-permute-done.11.refs_16_), channel_id=1, source_target_pairs={{0,16},{1,17},{2,18},{3,19},{4,20},{5,21},{6,22},{7,23},{8,24},{9,... | collective-permute-start | bytes 688136 | tf_op jit(solution)/shard_map/ppermute | solution.py:33
  31.6 11.5 %collective-permute-start.10 = (bf16[64,1792]{1,0:T(8,128)(2,1)S(1)}, bf16[64,1792]{1,0:T(8,128)(2,1)S(1)}, u32[]{:S(2)}, u32[]{:S(2)}) collective-permute-start(bf16[64,1792]{1,0:T(8,128)(2,1)S(1)} %collective-permute-done.9.refs_9_), channel_id=1, source_target_pairs={{0,112},{1,113},{2,114},{3,115},{4,116},{5,117},{6,118},{7,119},{8... | collective-permute-start | bytes 688136 | tf_op jit(solution)/shard_map/ppermute | solution.py:33
  33.6 9.5 %collective-permute-start.12 = (bf16[64,1792]{1,0:T(8,128)(2,1)S(1)}, bf16[64,1792]{1,0:T(8,128)(2,1)S(1)}, u32[]{:S(2)}, u32[]{:S(2)}) collective-permute-start(bf16[64,1792]{1,0:T(8,128)(2,1)S(1)} %collective-permute-done.11.refs_16_), channel_id=1, source_target_pairs={{0,112},{1,113},{2,114},{3,115},{4,116},{5,117},{6,118},{7,119},{8... | collective-permute-start | bytes 688136 | tf_op jit(solution)/shard_map/ppermute | solution.py:33
  38.1 8.3 %copy-start.2 = (bf16[1024,640]{1,0:T(8,128)(2,1)S(1)}, bf16[1024,640]{1,0:T(8,128)(2,1)}, u32[]{:S(2)}) copy-start(bf16[1024,640]{1,0:T(8,128)(2,1)} %get-tuple-element.26.queries) | copy-start | bytes 3932164
  43.1 11.5 %collective-permute-start.13 = (bf16[128,1792]{1,0:T(8,128)(2,1)S(1)}, bf16[128,1792]{1,0:T(8,128)(2,1)S(1)}, u32[]{:S(2)}, u32[]{:S(2)}) collective-permute-start(bf16[128,1792]{1,0:T(8,128)(2,1)S(1)} %pad_maximum_fusion), channel_id=1, source_target_pairs={{0,112},{1,113},{2,114},{3,115},{4,116},{5,117},{6,118},{7,119},{8... | collective-permute-start | bytes 1376264 | tf_op jit(solution)/shard_map/ppermute | solution.py:33
  46.3 11.8 %collective-permute-start.17 = (bf16[128,1792]{1,0:T(8,128)(2,1)S(1)}, bf16[128,1792]{1,0:T(8,128)(2,1)S(1)}, u32[]{:S(2)}, u32[]{:S(2)}) collective-permute-start(bf16[128,1792]{1,0:T(8,128)(2,1)S(1)} %pad_maximum_fusion.1), channel_id=1, source_target_pairs={{0,16},{1,17},{2,18},{3,19},{4,20},{5,21},{6,22},{7,23},{8,24},{9,... | collective-permute-start | bytes 1376264 | tf_op jit(solution)/shard_map/ppermute | solution.py:33
  46.3 11.8 %collective-permute-start.8 = (bf16[256,512]{1,0:T(8,128)(2,1)S(1)}, bf16[256,512]{1,0:T(8,128)(2,1)S(1)}, u32[]{:S(2)}, u32[]{:S(2)}) collective-permute-start(bf16[256,512]{1,0:T(8,128)(2,1)S(1)} %attend.2.refs_0_), channel_id=1, source_target_pairs={{0,129},{1,128},{2,131},{3,130},{4,133},{5,132},{6,135},{7,134},{8... | collective-permute-start | bytes 786440 | tf_op jit(solution)/shard_map/ppermute | solution.py:33
  46.4 11.9 %collective-permute-start.3 = (bf16[256,512]{1,0:T(8,128)(2,1)S(1)}, bf16[256,512]{1,0:T(8,128)(2,1)S(1)}, u32[]{:S(2)}, u32[]{:S(2)}) collective-permute-start(bf16[256,512]{1,0:T(8,128)(2,1)S(1)} %attend.2.refs_0_), channel_id=1, source_target_pairs={{0,1},{1,0},{2,3},{3,2},{4,5},{5,4},{6,7},{7,6},{8,9},{9,8},{10,11... | collective-permute-start | bytes 786440 | tf_op jit(solution)/shard_map/ppermute | solution.py:33
  46.4 22.6 %copy-start.5 = (bf16[64,1792]{1,0:T(8,128)(2,1)S(1)}, bf16[64,1792]{1,0:T(8,128)(2,1)}, u32[]{:S(2)}) copy-start(bf16[64,1792]{1,0:T(8,128)(2,1)} %get-tuple-element.27.refs_8_) | copy-start | bytes 688132
  50.2 9.7 %collective-permute-start.6 = (bf16[256,512]{1,0:T(8,128)(2,1)S(1)}, bf16[256,512]{1,0:T(8,128)(2,1)S(1)}, u32[]{:S(2)}, u32[]{:S(2)}) collective-permute-start(bf16[256,512]{1,0:T(8,128)(2,1)S(1)} %attend.3.refs_1_), channel_id=1, source_target_pairs={{0,129},{1,128},{2,131},{3,130},{4,133},{5,132},{6,135},{7,134},{8... | collective-permute-start | bytes 786440 | tf_op jit(solution)/shard_map/ppermute | solution.py:33
  54.7 6.5 %collective-permute-start.19 = (bf16[64,1792]{1,0:T(8,128)(2,1)S(1)}, bf16[64,1792]{1,0:T(8,128)(2,1)S(1)}, u32[]{:S(2)}, u32[]{:S(2)}) collective-permute-start(bf16[64,1792]{1,0:T(8,128)(2,1)S(1)} %slice.92), channel_id=1, source_target_pairs={{0,112},{1,113},{2,114},{3,115},{4,116},{5,117},{6,118},{7,119},{8... | collective-permute-start | bytes 688136 | tf_op jit(solution)/shard_map/ppermute | solution.py:33
  58.2 10.8 %collective-permute-start.18 = (bf16[128,1792]{1,0:T(8,128)(2,1)S(1)}, bf16[128,1792]{1,0:T(8,128)(2,1)S(1)}, u32[]{:S(2)}, u32[]{:S(2)}) collective-permute-start(bf16[128,1792]{1,0:T(8,128)(2,1)S(1)} %collective-permute-done.17.refs_13_), channel_id=1, source_target_pairs={{0,16},{1,17},{2,18},{3,19},{4,20},{5,21},{6,22},{7,23},{8,24},{9,... | collective-permute-start | bytes 1376264 | tf_op jit(solution)/shard_map/ppermute | solution.py:33
  58.2 6.1 %collective-permute-start.4 = (bf16[256,512]{1,0:T(8,128)(2,1)S(1)}, bf16[256,512]{1,0:T(8,128)(2,1)S(1)}, u32[]{:S(2)}, u32[]{:S(2)}) collective-permute-start(bf16[256,512]{1,0:T(8,128)(2,1)S(1)} %attend.3.refs_1_), channel_id=1, source_target_pairs={{0,1},{1,0},{2,3},{3,2},{4,5},{5,4},{6,7},{7,6},{8,9},{9,8},{10,11... | collective-permute-start | bytes 786440 | tf_op jit(solution)/shard_map/ppermute | solution.py:33
  58.3 6.5 %collective-permute-start.5 = (bf16[256,512]{1,0:T(8,128)(2,1)S(1)}, bf16[256,512]{1,0:T(8,128)(2,1)S(1)}, u32[]{:S(2)}, u32[]{:S(2)}) collective-permute-start(bf16[256,512]{1,0:T(8,128)(2,1)S(1)} %collective-permute-done.3.refs_2_), channel_id=1, source_target_pairs={{0,129},{1,128},{2,131},{3,130},{4,133},{5,132},{6,135},{7,134},{8... | collective-permute-start | bytes 786440 | tf_op jit(solution)/shard_map/ppermute | solution.py:33
  59.8 9.1 %collective-permute-start.7 = (bf16[256,512]{1,0:T(8,128)(2,1)S(1)}, bf16[256,512]{1,0:T(8,128)(2,1)S(1)}, u32[]{:S(2)}, u32[]{:S(2)}) collective-permute-start(bf16[256,512]{1,0:T(8,128)(2,1)S(1)} %collective-permute-done.6.refs_7_), channel_id=1, source_target_pairs={{0,1},{1,0},{2,3},{3,2},{4,5},{5,4},{6,7},{7,6},{8,9},{9,8},{10,11... | collective-permute-start | bytes 786440 | tf_op jit(solution)/shard_map/ppermute | solution.py:33
  61.1 7.8 %collective-permute-start.20 = (bf16[64,1792]{1,0:T(8,128)(2,1)S(1)}, bf16[64,1792]{1,0:T(8,128)(2,1)S(1)}, u32[]{:S(2)}, u32[]{:S(2)}) collective-permute-start(bf16[64,1792]{1,0:T(8,128)(2,1)S(1)} %collective-permute-done.19.refs_18_), channel_id=1, source_target_pairs={{0,112},{1,113},{2,114},{3,115},{4,116},{5,117},{6,118},{7,119},{8... | collective-permute-start | bytes 688136 | tf_op jit(solution)/shard_map/ppermute | solution.py:33
  71.3 9.8 %collective-permute-start.21 = (bf16[3,256,896]{2,1,0:T(8,128)(2,1)S(1)}, bf16[3,256,896]{2,1,0:T(8,128)(2,1)S(1)}, u32[]{:S(2)}, u32[]{:S(2)}) collective-permute-start(bf16[3,256,896]{2,1,0:T(8,128)(2,1)S(1)} %get-tuple-element.34), channel_id=1, source_target_pairs={{0,2},{1,3},{2,0},{3,1},{4,6},{5,7},{6,4},{7,5},{8,10},{9,11},{10,... | collective-permute-start | bytes 4128776 | tf_op jit(solution)/shard_map/ppermute | solution.py:33
  75.0 3.4 %collective-permute-start.24 = (bf16[256,896]{1,0:T(8,128)(2,1)S(1)}, bf16[256,896]{1,0:T(8,128)(2,1)S(1)}, u32[]{:S(2)}, u32[]{:S(2)}) collective-permute-start(bf16[256,896]{1,0:T(8,128)(2,1)S(1)} %get-tuple-element.38), channel_id=1, source_target_pairs={{0,2},{1,3},{2,0},{3,1},{4,6},{5,7},{6,4},{7,5},{8,10},{9,11},{10,... | collective-permute-start | bytes 1376264 | tf_op jit(solution)/shard_map/ppermute | solution.py:33
  78.5 10.4 %collective-permute-start.29 = (bf16[128,896]{1,0:T(8,128)(2,1)S(1)}, bf16[128,896]{1,0:T(8,128)(2,1)S(1)}, u32[]{:S(2)}, u32[]{:S(2)}) collective-permute-start(bf16[128,896]{1,0:T(8,128)(2,1)S(1)} %get-tuple-element.46), channel_id=1, source_target_pairs={{0,12},{1,13},{2,14},{3,15},{4,0},{5,1},{6,2},{7,3},{8,4},{9,5},{1... | collective-permute-start | bytes 688136 | tf_op jit(solution)/shard_map/ppermute | solution.py:33
  81.1 7.7 %collective-permute-start.25 = (bf16[128,896]{1,0:T(8,128)(2,1)S(1)}, bf16[128,896]{1,0:T(8,128)(2,1)S(1)}, u32[]{:S(2)}, u32[]{:S(2)}) collective-permute-start(bf16[128,896]{1,0:T(8,128)(2,1)S(1)} %get-tuple-element.47), channel_id=1, source_target_pairs={{0,4},{1,5},{2,6},{3,7},{4,8},{5,9},{6,10},{7,11},{8,12},{9,13},{1... | collective-permute-start | bytes 688136 | tf_op jit(solution)/shard_map/ppermute | solution.py:33
  81.4 8.7 %collective-permute-start.22 = (bf16[128,896]{1,0:T(8,128)(2,1)S(1)}, bf16[128,896]{1,0:T(8,128)(2,1)S(1)}, u32[]{:S(2)}, u32[]{:S(2)}) collective-permute-start(bf16[128,896]{1,0:T(8,128)(2,1)S(1)} %get-tuple-element.35), channel_id=1, source_target_pairs={{0,0},{1,1},{2,128},{3,129},{4,4},{5,5},{6,132},{7,133},{8,8},{9,9... | collective-permute-start | bytes 688136 | tf_op jit(solution)/shard_map/ppermute | solution.py:33
  84.3 21.0 %collective-permute-start.23 = (bf16[128,896]{1,0:T(8,128)(2,1)S(1)}, bf16[128,896]{1,0:T(8,128)(2,1)S(1)}, u32[]{:S(2)}, u32[]{:S(2)}) collective-permute-start(bf16[128,896]{1,0:T(8,128)(2,1)S(1)} %fusion.6), channel_id=1, source_target_pairs={{0,12},{1,13},{2,140},{3,141},{4,0},{5,1},{6,128},{7,129},{8,4},{9... | collective-permute-start | bytes 688136 | tf_op jit(solution)/shard_map/ppermute | solution.py:33
  87.1 18.3 %collective-permute-start.27 = (bf16[128,896]{1,0:T(8,128)(2,1)S(1)}, bf16[128,896]{1,0:T(8,128)(2,1)S(1)}, u32[]{:S(2)}, u32[]{:S(2)}) collective-permute-start(bf16[128,896]{1,0:T(8,128)(2,1)S(1)} %get-tuple-element.39), channel_id=1, source_target_pairs={{0,1},{1,0},{2,129},{3,128},{4,5},{5,4},{6,133},{7,132},{8,9},{9,8... | collective-permute-start | bytes 688136 | tf_op jit(solution)/shard_map/ppermute | solution.py:33
  88.8 16.6 %collective-permute-start.28 = (bf16[128,896]{1,0:T(8,128)(2,1)S(1)}, bf16[128,896]{1,0:T(8,128)(2,1)S(1)}, u32[]{:S(2)}, u32[]{:S(2)}) collective-permute-start(bf16[128,896]{1,0:T(8,128)(2,1)S(1)} %fusion.5), channel_id=1, source_target_pairs={{0,5},{1,4},{2,133},{3,132},{4,9},{5,8},{6,137},{7,136},{8,13},{9,... | collective-permute-start | bytes 688136 | tf_op jit(solution)/shard_map/ppermute | solution.py:33
  88.9 16.5 %collective-permute-start.26 = (bf16[128,896]{1,0:T(8,128)(2,1)S(1)}, bf16[128,896]{1,0:T(8,128)(2,1)S(1)}, u32[]{:S(2)}, u32[]{:S(2)}) collective-permute-start(bf16[128,896]{1,0:T(8,128)(2,1)S(1)} %fusion.4), channel_id=1, source_target_pairs={{0,4},{1,5},{2,132},{3,133},{4,8},{5,9},{6,136},{7,137},{8,12},{9,... | collective-permute-start | bytes 688136 | tf_op jit(solution)/shard_map/ppermute | solution.py:33
  90.2 18.2 %collective-permute-start.30 = (bf16[128,896]{1,0:T(8,128)(2,1)S(1)}, bf16[128,896]{1,0:T(8,128)(2,1)S(1)}, u32[]{:S(2)}, u32[]{:S(2)}) collective-permute-start(bf16[128,896]{1,0:T(8,128)(2,1)S(1)} %fusion.2), channel_id=1, source_target_pairs={{0,13},{1,12},{2,141},{3,140},{4,1},{5,0},{6,129},{7,128},{8,5},{9... | collective-permute-start | bytes 688136 | tf_op jit(solution)/shard_map/ppermute | solution.py:33

commit v10 on v6

--- a/solution.py
+++ b/solution.py
@@ -53,8 +53,8 @@
     return moved(a, lambda yh, z, x, c, yl: (yh, z, (x + d) % 4, c, yl))
 
 
-def home(a, r):
-    return moved(a, lambda yh, z, x, c, yl: (yh ^ c, z, x, yh, yl ^ r))
+def home(a, r, d=0):
+    return moved(a, lambda yh, z, x, c, yl: (yh ^ c, z, (x + d) % 4, yh, yl ^ r))
 
 
 def turn_of(table):
@@ -375,12 +375,13 @@
         (sums[1][128:].astype(BF), sums[2][:128].astype(BF))
     )
     early_up, early_down = along_x(early_up, 1), along_x(early_down, 3)
-    late_up = along_x((sums[1][:128] + passing_up.astype(F32)).astype(BF), 1)
-    late_down = along_x((sums[2][128:] + passing_down.astype(F32)).astype(BF), 3)
-    pieces = [
-        home((sums[0][:128] + late_up.astype(F32) + early_down.astype(F32)).astype(BF), 0),
-        home((sums[0][128:] + early_up.astype(F32) + late_down.astype(F32)).astype(BF), 1),
+    late_up = home((sums[1][:128] + passing_up.astype(F32)).astype(BF), 0, 1)
+    late_down = home((sums[2][128:] + passing_down.astype(F32)).astype(BF), 1, 3)
+    parts = [
+        [home((sums[0][:128] + early_down.astype(F32)).astype(BF), 0), late_up],
+        [home((sums[0][128:] + early_up.astype(F32)).astype(BF), 1), late_down],
     ]
+    pieces = [sum(part.astype(F32) for part in piece).astype(BF) for piece in parts]
     even = yl == 0
     pair = jnp.where(even, pieces[0], pieces[1]), jnp.where(even, pieces[1], pieces[0])
     return jnp.concatenate(

time: 110 us -> 106 us (0.964)
  waiting for transfers between devices: 30.7 us -> 25.4 us
  starting transfers between devices: 51.4 us -> 53.4 us
    ppermute x29, waiting for transfers between devices: 30.7 us -> 25.4 us  [moved(): return lax.ppermute(a, AXES, pairs)]
    ppermute x29, starting transfers between devices: 42.1 us -> 44.1 us  [moved(): return lax.ppermute(a, AXES, pairs)]
  transfers between devices with their start and end apart: 31 -> 31, of which waited for: 13 -> 12; matrix products, arithmetic and copies ran while one was open for 2% -> 2% of each run, Pallas kernels for 18% -> 18%
where the time goes in v10:
time: 106 us
  starting transfers between devices  53.4 us (50%)
  waiting for transfers between devices  25.4 us (24%)
  Pallas kernels  21.9 us (21%)
  other arithmetic  3 us (3%)
  local copies, waits for them, and re-layouts  1.35 us (1%)
    ppermute x29, starting transfers between devices, moved(): return lax.ppermute(a, AXES, pairs)  44.1 us
    ppermute x29, waiting for transfers between devices, moved(): return lax.ppermute(a, AXES, pairs)  25.4 us
    pallas_call x6, Pallas kernels, call(): pl.pallas_call(kernel, out_shape=shapes, in_specs=specs, out_specs=whole(...  19.7 us
    ppermute x2, starting transfers between devices, local(): lax.ppermute(half, CTX, [(i, i + by) for i in range(16 - by)])  9.28 us
    pallas_call x1, Pallas kernels, quarters(): pl.pallas_call(quarter_kernel, out_shape=[jax.ShapeDtypeStruct((64, 1792)...  2.22 us
  transfers between devices with their start and end apart: 31, of which 12 were waited for; matrix products, arithmetic and copies ran while one was open for 2% of the time, Pallas kernels for 18%

profile of v10, /device:TPU:1, one launch (start us, length us, event | category | flops | bytes accessed | tf_op | source)
XLA Modules:
  0.0 106.0 jit_solution(110440120952301708)
XLA Ops:
  0.0 0.9 dynamic-slice_bitcast_fusion
  0.9 5.7 %collective-permute-start.1 = (bf16[576,128]{1,0:T(8,128)(2,1)S(1)}, bf16[576,128]{1,0:T(8,128)(2,1)S(1)}, u32[]{:S(2)}, u32[]{:S(2)}) collective-permute-start(bf16[576,128]{1,0:T(8,128)(2,1)S(1)} %dynamic-slice_bitcast_fusion), channel_id=1, source_target_pairs={{0,32},{16,48},{32,64},{48,80},{64,96},{80,112},{96,128},{112,144}... | collective-permute-start | bytes 442376 | tf_op jit(solution)/shard_map/ppermute | solution.py:305
  6.7 3.5 %collective-permute-start = (bf16[576,128]{1,0:T(8,128)(2,1)S(1)}, bf16[576,128]{1,0:T(8,128)(2,1)S(1)}, u32[]{:S(2)}, u32[]{:S(2)}) collective-permute-start(bf16[576,128]{1,0:T(8,128)(2,1)S(1)} %dynamic-slice_bitcast_fusion), channel_id=1, source_target_pairs={{0,16},{16,32},{32,48},{48,64},{64,80},{80,96},{96,112},{112,128},... | collective-permute-start | bytes 442376 | tf_op jit(solution)/shard_map/ppermute | solution.py:305
  10.2 2.2 %quarters.1 = (bf16[64,1792]{1,0:T(8,128)(2,1)}, bf16[64,1792]{1,0:T(8,128)(2,1)}) custom-call(bf16[64,7168]{1,0:T(8,128)(2,1)} %bitcast.35), custom_call_target="tpu_custom_call" | custom-call | bytes 2097152 | tf_op jit(solution)/shard_map/quarters/pallas_call | solution.py:247
  12.4 2.8 %collective-permute-start.14 = (bf16[64,1792]{1,0:T(8,128)(2,1)}, bf16[64,1792]{1,0:T(8,128)(2,1)S(1)}, u32[]{:S(2)}, u32[]{:S(2)}) collective-permute-start(bf16[64,1792]{1,0:T(8,128)(2,1)} %get-tuple-element.25.refs_8_), channel_id=1, source_target_pairs={{0,16},{1,17},{2,18},{3,19},{4,20},{5,21},{6,22},{7,23},{8,24},{9,... | collective-permute-start | bytes 688136 | tf_op jit(solution)/shard_map/ppermute | solution.py:33
  15.3 0.8 collective-permute-start.9
  16.1 1.9 %collective-permute-start.11 = (bf16[64,1792]{1,0:T(8,128)(2,1)}, bf16[64,1792]{1,0:T(8,128)(2,1)S(1)}, u32[]{:S(2)}, u32[]{:S(2)}) collective-permute-start(bf16[64,1792]{1,0:T(8,128)(2,1)} %get-tuple-element.27), channel_id=1, source_target_pairs={{0,129},{1,128},{2,131},{3,130},{4,133},{5,132},{6,135},{7,134},{8... | collective-permute-start | bytes 688136 | tf_op jit(solution)/shard_map/ppermute | solution.py:33
  18.2 0.1 fusion.reorder
  18.3 0.8 fusion.11
  19.1 6.9 %queries.1 = (bf16[1024,640]{1,0:T(8,128)(2,1)}, bf16[1024,640]{1,0:T(8,128)(2,1)}) custom-call(bf16[256,1536]{1,0:T(8,128)(2,1)} %rows.1, bf16[1536,1536]{1,0:T(8,128)(2,1)} %w_query.1, bf16[8,128,512]{2,1,0:T(8,128)(2,1)} %w_key_up.1, f32[64,128]{1,0:T(8,128)} %get-tuple-element.53.cosines, f32[64,128]{1,0:T(8,128)} %get-tuple-element.52.sines), custom_call_target="tpu_custom_call" | custom-call | flops 1476395008 | bytes 8388608 | tf_op jit(solution)/shard_map/queries/pallas_call | solution.py:259
  26.1 2.0 %collective-permute-start.2 = (bf16[576,256]{1,0:T(8,128)(2,1)S(1)}, bf16[576,256]{1,0:T(8,128)(2,1)S(1)}, u32[]{:S(2)}, u32[]{:S(2)}) collective-permute-start(bf16[576,256]{1,0:T(8,128)(2,1)S(1)} %pad_maximum_fusion.2), channel_id=1, source_target_pairs={{0,2},{1,3},{2,0},{3,1},{4,6},{5,7},{6,4},{7,5},{8,10},{9,11},{10,... | collective-permute-start | bytes 884744 | tf_op jit(solution)/shard_map/ppermute | solution.py:33
  28.1 1.7 %collective-permute-start.15 = (bf16[64,1792]{1,0:T(8,128)(2,1)S(1)}, bf16[64,1792]{1,0:T(8,128)(2,1)S(1)}, u32[]{:S(2)}, u32[]{:S(2)}) collective-permute-start(bf16[64,1792]{1,0:T(8,128)(2,1)S(1)} %collective-permute-done.14.refs_15_), channel_id=1, source_target_pairs={{0,16},{1,17},{2,18},{3,19},{4,20},{5,21},{6,22},{7,23},{8,24},{9,... | collective-permute-start | bytes 688136 | tf_op jit(solution)/shard_map/ppermute | solution.py:33
  29.8 0.7 collective-permute-start.16
  30.5 0.4 multiply_sine_fusion
  31.6 2.0 %collective-permute-start.10 = (bf16[64,1792]{1,0:T(8,128)(2,1)S(1)}, bf16[64,1792]{1,0:T(8,128)(2,1)S(1)}, u32[]{:S(2)}, u32[]{:S(2)}) collective-permute-start(bf16[64,1792]{1,0:T(8,128)(2,1)S(1)} %collective-permute-done.9.refs_9_), channel_id=1, source_target_pairs={{0,112},{1,113},{2,114},{3,115},{4,116},{5,117},{6,118},{7,119},{8... | collective-permute-start | bytes 688136 | tf_op jit(solution)/shard_map/ppermute | solution.py:33
  33.7 0.6 keys.1
  34.3 3.8 %attend.2.refs_0_ = bf16[256,512]{1,0:T(8,128)(2,1)S(1)} custom-call(bf16[1024,640]{1,0:T(8,128)(2,1)S(1)} %copy-done.3, bf16[640,768]{1,0:T(8,128)(2,1)S(1)} %get-tuple-element.22.keys, f32[256,768]{1,0:T(8,128)S(1)} %get-tuple-element.23.hidden, bf16[8,512,128]{2,1,0:T(8,128)(2,1)S(1)} %copy-done.4, bf16[512,512]{1,0:T(8,128)(2,1)S(1)} %fusion.reorder), custom_call_target="tpu_custom_call" | custom-call | flops 1946157056 | bytes 5242880 | tf_op jit(solution)/shard_map/attend/pallas_call | solution.py:259
  38.1 3.3 %collective-permute-done.16.refs_20_ = bf16[64,1792]{1,0:T(8,128)(2,1)S(1)} collective-permute-done((bf16[64,1792]{1,0:T(8,128)(2,1)S(1)}, bf16[64,1792]{1,0:T(8,128)(2,1)S(1)}, u32[]{:S(2)}, u32[]{:S(2)}) %collective-permute-start.16) | collective-permute-done | bytes 229408 | tf_op jit(solution)/shard_map/ppermute | solution.py:33
  41.4 1.7 %collective-permute-done.12.refs_17_ = bf16[64,1792]{1,0:T(8,128)(2,1)S(1)} collective-permute-done((bf16[64,1792]{1,0:T(8,128)(2,1)S(1)}, bf16[64,1792]{1,0:T(8,128)(2,1)S(1)}, u32[]{:S(2)}, u32[]{:S(2)}) %collective-permute-start.12) | collective-permute-done | bytes 229408 | tf_op jit(solution)/shard_map/ppermute | solution.py:33
  43.1 3.2 %collective-permute-start.13 = (bf16[128,1792]{1,0:T(8,128)(2,1)S(1)}, bf16[128,1792]{1,0:T(8,128)(2,1)S(1)}, u32[]{:S(2)}, u32[]{:S(2)}) collective-permute-start(bf16[128,1792]{1,0:T(8,128)(2,1)S(1)} %pad_maximum_fusion), channel_id=1, source_target_pairs={{0,112},{1,113},{2,114},{3,115},{4,116},{5,117},{6,118},{7,119},{8... | collective-permute-start | bytes 1376264 | tf_op jit(solution)/shard_map/ppermute | solution.py:33
  46.4 3.8 %attend.3.refs_1_ = bf16[256,512]{1,0:T(8,128)(2,1)S(1)} custom-call(bf16[1024,640]{1,0:T(8,128)(2,1)S(1)} %copy-done.2, bf16[640,768]{1,0:T(8,128)(2,1)S(1)} %get-tuple-element.22.keys, f32[256,768]{1,0:T(8,128)S(1)} %get-tuple-element.23.hidden, bf16[8,512,128]{2,1,0:T(8,128)(2,1)S(1)} %copy-done.4, bf16[512,512]{1,0:T(8,128)(2,1)S(1)} %fusion.reorder), custom_call_target="tpu_custom_call" | custom-call | flops 1946157056 | bytes 5242880 | tf_op jit(solution)/shard_map/attend/pallas_call | solution.py:259
  50.2 2.7 %collective-permute-start.6 = (bf16[256,512]{1,0:T(8,128)(2,1)S(1)}, bf16[256,512]{1,0:T(8,128)(2,1)S(1)}, u32[]{:S(2)}, u32[]{:S(2)}) collective-permute-start(bf16[256,512]{1,0:T(8,128)(2,1)S(1)} %attend.3.refs_1_), channel_id=1, source_target_pairs={{0,129},{1,128},{2,131},{3,130},{4,133},{5,132},{6,135},{7,134},{8... | collective-permute-start | bytes 786440 | tf_op jit(solution)/shard_map/ppermute | solution.py:33
  52.9 1.7 %collective-permute-done.13.refs_11_ = bf16[128,1792]{1,0:T(8,128)(2,1)S(1)} collective-permute-done((bf16[128,1792]{1,0:T(8,128)(2,1)S(1)}, bf16[128,1792]{1,0:T(8,128)(2,1)S(1)}, u32[]{:S(2)}, u32[]{:S(2)}) %collective-permute-start.13) | collective-permute-done | bytes 458784 | tf_op jit(solution)/shard_map/ppermute | solution.py:33
  54.7 3.5 %collective-permute-start.19 = (bf16[64,1792]{1,0:T(8,128)(2,1)S(1)}, bf16[64,1792]{1,0:T(8,128)(2,1)S(1)}, u32[]{:S(2)}, u32[]{:S(2)}) collective-permute-start(bf16[64,1792]{1,0:T(8,128)(2,1)S(1)} %slice.96), channel_id=1, source_target_pairs={{0,112},{1,113},{2,114},{3,115},{4,116},{5,117},{6,118},{7,119},{8... | collective-permute-start | bytes 688136 | tf_op jit(solution)/shard_map/ppermute | solution.py:33
  58.3 0.6 collective-permute-start.5
  58.9 1.0 collective-permute-done.6.refs_7_
  59.8 0.2 collective-permute-start.7
  60.0 1.1 %collective-permute-done.19.refs_18_ = bf16[64,1792]{1,0:T(8,128)(2,1)S(1)} collective-permute-done((bf16[64,1792]{1,0:T(8,128)(2,1)S(1)}, bf16[64,1792]{1,0:T(8,128)(2,1)S(1)}, u32[]{:S(2)}, u32[]{:S(2)}) %collective-permute-start.19) | collective-permute-done | bytes 229408 | tf_op jit(solution)/shard_map/ppermute | solution.py:33
  61.1 3.1 %collective-permute-start.20 = (bf16[64,1792]{1,0:T(8,128)(2,1)S(1)}, bf16[64,1792]{1,0:T(8,128)(2,1)S(1)}, u32[]{:S(2)}, u32[]{:S(2)}) collective-permute-start(bf16[64,1792]{1,0:T(8,128)(2,1)S(1)} %collective-permute-done.19.refs_18_), channel_id=1, source_target_pairs={{0,112},{1,113},{2,114},{3,115},{4,116},{5,117},{6,118},{7,119},{8... | collective-permute-start | bytes 688136 | tf_op jit(solution)/shard_map/ppermute | solution.py:33
  64.2 0.6 collective-permute-done.5.refs_4_
  64.8 4.2 %collective-permute-done.7.refs_5_ = bf16[256,512]{1,0:T(8,128)(2,1)S(1)} collective-permute-done((bf16[256,512]{1,0:T(8,128)(2,1)S(1)}, bf16[256,512]{1,0:T(8,128)(2,1)S(1)}, u32[]{:S(2)}, u32[]{:S(2)}) %collective-permute-start.7) | collective-permute-done | bytes 262176 | tf_op jit(solution)/shard_map/ppermute | solution.py:33
  69.0 2.3 %project.3 = (bf16[256,896]{1,0:T(8,128)(2,1)S(1)}, bf16[3,256,896]{2,1,0:T(8,128)(2,1)S(1)}) custom-call(bf16[256,512]{1,0:T(8,128)(2,1)S(1)} %attend.2.refs_0_, bf16[256,512]{1,0:T(8,128)(2,1)S(1)} %attend.3.refs_1_, bf16[256,512]{1,0:T(8,128)(2,1)S(1)} %collective-permute-done.3.refs_2_, bf16[256,512]{1,0:T(8,128)(2,1)S(1)} %collective-permute-done.4.refs_3_, ...), custom_call_target="tpu_custom_call" | custom-call | flops 1879048192 | bytes 8388608 | tf_op jit(solution)/shard_map/project/pallas_call | solution.py:259
  71.3 3.7 %collective-permute-start.21 = (bf16[3,256,896]{2,1,0:T(8,128)(2,1)S(1)}, bf16[3,256,896]{2,1,0:T(8,128)(2,1)S(1)}, u32[]{:S(2)}, u32[]{:S(2)}) collective-permute-start(bf16[3,256,896]{2,1,0:T(8,128)(2,1)S(1)} %get-tuple-element.32), channel_id=1, source_target_pairs={{0,2},{1,3},{2,0},{3,1},{4,6},{5,7},{6,4},{7,5},{8,10},{9,11},{10,... | collective-permute-start | bytes 4128776 | tf_op jit(solution)/shard_map/ppermute | solution.py:33
  75.1 2.3 %project.2 = (f32[256,896]{1,0:T(8,128)S(1)}, f32[3,256,896]{2,1,0:T(8,128)S(1)}) custom-call(bf16[256,512]{1,0:T(8,128)(2,1)S(1)} %attend.2.refs_0_, bf16[256,512]{1,0:T(8,128)(2,1)S(1)} %attend.3.refs_1_, bf16[256,512]{1,0:T(8,128)(2,1)S(1)} %collective-permute-done.3.refs_2_, bf16[256,512]{1,0:T(8,128)(2,1)S(1)} %collective-permute-done.4.refs_3_, ...), custom_call_target="tpu_custom_call" | custom-call | flops 1879048192 | bytes 8388608 | tf_op jit(solution)/shard_map/project/pallas_call | solution.py:259
  77.4 1.0 collective-permute-done.24
  78.5 2.6 %collective-permute-start.29 = (bf16[128,896]{1,0:T(8,128)(2,1)S(1)}, bf16[128,896]{1,0:T(8,128)(2,1)S(1)}, u32[]{:S(2)}, u32[]{:S(2)}) collective-permute-start(bf16[128,896]{1,0:T(8,128)(2,1)S(1)} %get-tuple-element.44), channel_id=1, source_target_pairs={{0,12},{1,13},{2,14},{3,15},{4,0},{5,1},{6,2},{7,3},{8,4},{9,5},{1... | collective-permute-start | bytes 688136 | tf_op jit(solution)/shard_map/ppermute | solution.py:33
  81.1 0.2 convert_add_fusion
  81.4 2.8 %collective-permute-start.22 = (bf16[128,896]{1,0:T(8,128)(2,1)S(1)}, bf16[128,896]{1,0:T(8,128)(2,1)S(1)}, u32[]{:S(2)}, u32[]{:S(2)}) collective-permute-start(bf16[128,896]{1,0:T(8,128)(2,1)S(1)} %fusion.10), channel_id=1, source_target_pairs={{0,12},{1,13},{2,14},{3,15},{4,0},{5,1},{6,2},{7,3},{8,4},{9,5},{1... | collective-permute-start | bytes 688136 | tf_op jit(solution)/shard_map/ppermute | solution.py:33
  84.2 4.6 %collective-permute-done.25 = bf16[128,896]{1,0:T(8,128)(2,1)S(1)} collective-permute-done((bf16[128,896]{1,0:T(8,128)(2,1)S(1)}, bf16[128,896]{1,0:T(8,128)(2,1)S(1)}, u32[]{:S(2)}, u32[]{:S(2)}) %collective-permute-start.25) | collective-permute-done | bytes 229408 | tf_op jit(solution)/shard_map/ppermute | solution.py:33
  88.9 1.2 %collective-permute-start.26 = (bf16[128,896]{1,0:T(8,128)(2,1)S(1)}, bf16[128,896]{1,0:T(8,128)(2,1)S(1)}, u32[]{:S(2)}, u32[]{:S(2)}) collective-permute-start(bf16[128,896]{1,0:T(8,128)(2,1)S(1)} %fusion.6), channel_id=1, source_target_pairs={{0,4},{1,5},{2,132},{3,133},{4,8},{5,9},{6,136},{7,137},{8,12},{9,... | collective-permute-start | bytes 688136 | tf_op jit(solution)/shard_map/ppermute | solution.py:33
  90.1 1.6 %collective-permute-start.30 = (bf16[128,896]{1,0:T(8,128)(2,1)S(1)}, bf16[128,896]{1,0:T(8,128)(2,1)S(1)}, u32[]{:S(2)}, u32[]{:S(2)}) collective-permute-start(bf16[128,896]{1,0:T(8,128)(2,1)S(1)} %fusion.2), channel_id=1, source_target_pairs={{0,13},{1,12},{2,141},{3,140},{4,1},{5,0},{6,129},{7,128},{8,5},{9... | collective-permute-start | bytes 688136 | tf_op jit(solution)/shard_map/ppermute | solution.py:33
  91.7 2.0 %collective-permute-done.27 = bf16[128,896]{1,0:T(8,128)(2,1)S(1)} collective-permute-done((bf16[128,896]{1,0:T(8,128)(2,1)S(1)}, bf16[128,896]{1,0:T(8,128)(2,1)S(1)}, u32[]{:S(2)}, u32[]{:S(2)}) %collective-permute-start.27) | collective-permute-done | bytes 229408 | tf_op jit(solution)/shard_map/ppermute | solution.py:33
  93.8 1.5 %collective-permute-start.28 = (bf16[128,896]{1,0:T(8,128)(2,1)S(1)}, bf16[128,896]{1,0:T(8,128)(2,1)S(1)}, u32[]{:S(2)}, u32[]{:S(2)}) collective-permute-start(bf16[128,896]{1,0:T(8,128)(2,1)S(1)} %get-tuple-element.42), channel_id=1, source_target_pairs={{0,1},{1,0},{2,129},{3,128},{4,5},{5,4},{6,133},{7,132},{8,9},{9,8... | collective-permute-start | bytes 688136 | tf_op jit(solution)/shard_map/ppermute | solution.py:33
  95.3 5.1 %collective-permute-start.23 = (bf16[128,896]{1,0:T(8,128)(2,1)S(1)}, bf16[128,896]{1,0:T(8,128)(2,1)S(1)}, u32[]{:S(2)}, u32[]{:S(2)}) collective-permute-start(bf16[128,896]{1,0:T(8,128)(2,1)S(1)} %get-tuple-element.43), channel_id=1, source_target_pairs={{0,0},{1,1},{2,128},{3,129},{4,4},{5,5},{6,132},{7,133},{8,8},{9,9... | collective-permute-start | bytes 688136 | tf_op jit(solution)/shard_map/ppermute | solution.py:33
  100.4 2.9 %collective-permute-done.28 = bf16[128,896]{1,0:T(8,128)(2,1)S(1)} collective-permute-done((bf16[128,896]{1,0:T(8,128)(2,1)S(1)}, bf16[128,896]{1,0:T(8,128)(2,1)S(1)}, u32[]{:S(2)}, u32[]{:S(2)}) %collective-permute-start.28) | collective-permute-done | bytes 229408 | tf_op jit(solution)/shard_map/ppermute | solution.py:33
  103.3 1.4 %collective-permute-done.23 = bf16[128,896]{1,0:T(8,128)(2,1)S(1)} collective-permute-done((bf16[128,896]{1,0:T(8,128)(2,1)S(1)}, bf16[128,896]{1,0:T(8,128)(2,1)S(1)}, u32[]{:S(2)}, u32[]{:S(2)}) %collective-permute-start.23) | collective-permute-done | bytes 229408 | tf_op jit(solution)/shard_map/ppermute | solution.py:33
  104.7 0.1 broadcast_select_fusion.1
  105.1 0.9 maximum_maximum_fusion
  (60 shorter events, 1.2 us)
Async XLA Ops:
  0.9 25.1 %collective-permute-start.1 = (bf16[576,128]{1,0:T(8,128)(2,1)S(1)}, bf16[576,128]{1,0:T(8,128)(2,1)S(1)}, u32[]{:S(2)}, u32[]{:S(2)}) collective-permute-start(bf16[576,128]{1,0:T(8,128)(2,1)S(1)} %dynamic-slice_bitcast_fusion), channel_id=1, source_target_pairs={{0,32},{16,48},{32,64},{48,80},{64,96},{80,112},{96,128},{112,144}... | collective-permute-start | bytes 442376 | tf_op jit(solution)/shard_map/ppermute | solution.py:305
  6.7 19.4 %collective-permute-start = (bf16[576,128]{1,0:T(8,128)(2,1)S(1)}, bf16[576,128]{1,0:T(8,128)(2,1)S(1)}, u32[]{:S(2)}, u32[]{:S(2)}) collective-permute-start(bf16[576,128]{1,0:T(8,128)(2,1)S(1)} %dynamic-slice_bitcast_fusion), channel_id=1, source_target_pairs={{0,16},{16,32},{32,48},{48,64},{64,80},{80,96},{96,112},{112,128},... | collective-permute-start | bytes 442376 | tf_op jit(solution)/shard_map/ppermute | solution.py:305
  12.4 15.6 %collective-permute-start.14 = (bf16[64,1792]{1,0:T(8,128)(2,1)}, bf16[64,1792]{1,0:T(8,128)(2,1)S(1)}, u32[]{:S(2)}, u32[]{:S(2)}) collective-permute-start(bf16[64,1792]{1,0:T(8,128)(2,1)} %get-tuple-element.25.refs_8_), channel_id=1, source_target_pairs={{0,16},{1,17},{2,18},{3,19},{4,20},{5,21},{6,22},{7,23},{8,24},{9,... | collective-permute-start | bytes 688136 | tf_op jit(solution)/shard_map/ppermute | solution.py:33
  15.3 16.3 %collective-permute-start.9 = (bf16[64,1792]{1,0:T(8,128)(2,1)}, bf16[64,1792]{1,0:T(8,128)(2,1)S(1)}, u32[]{:S(2)}, u32[]{:S(2)}) collective-permute-start(bf16[64,1792]{1,0:T(8,128)(2,1)} %get-tuple-element.25.refs_8_), channel_id=1, source_target_pairs={{0,112},{1,113},{2,114},{3,115},{4,116},{5,117},{6,118},{7,119},{8... | collective-permute-start | bytes 688136 | tf_op jit(solution)/shard_map/ppermute | solution.py:33
  16.1 13.6 %collective-permute-start.11 = (bf16[64,1792]{1,0:T(8,128)(2,1)}, bf16[64,1792]{1,0:T(8,128)(2,1)S(1)}, u32[]{:S(2)}, u32[]{:S(2)}) collective-permute-start(bf16[64,1792]{1,0:T(8,128)(2,1)} %get-tuple-element.27), channel_id=1, source_target_pairs={{0,129},{1,128},{2,131},{3,130},{4,133},{5,132},{6,135},{7,134},{8... | collective-permute-start | bytes 688136 | tf_op jit(solution)/shard_map/ppermute | solution.py:33
  19.1 14.6 %copy-start = (bf16[256,576]{0,1:T(8,128)(2,1)S(1)}, bf16[256,576]{0,1:T(8,128)(2,1)}, u32[]{:S(2)}) copy-start(bf16[256,576]{0,1:T(8,128)(2,1)} %param.9) | copy-start | bytes 884740
  19.1 14.6 %copy-start.1 = (bf16[512,576]{0,1:T(8,128)(2,1)S(1)}, bf16[512,576]{0,1:T(8,128)(2,1)}, u32[]{:S(2)}) copy-start(bf16[512,576]{0,1:T(8,128)(2,1)} %param.10) | copy-start | bytes 1769476
  26.0 8.3 %copy-start.3 = (bf16[1024,640]{1,0:T(8,128)(2,1)S(1)}, bf16[1024,640]{1,0:T(8,128)(2,1)}, u32[]{:S(2)}) copy-start(bf16[1024,640]{1,0:T(8,128)(2,1)} %get-tuple-element.21.queries) | copy-start | bytes 3932164
  26.0 8.3 %copy-start.4 = (bf16[8,512,128]{2,1,0:T(8,128)(2,1)S(1)}, bf16[8,512,128]{2,1,0:T(8,128)(2,1)}, u32[]{:S(2)}) copy-start(bf16[8,512,128]{2,1,0:T(8,128)(2,1)} %w_value_up.3) | copy-start | bytes 3145732
  26.1 7.6 %collective-permute-start.2 = (bf16[576,256]{1,0:T(8,128)(2,1)S(1)}, bf16[576,256]{1,0:T(8,128)(2,1)S(1)}, u32[]{:S(2)}, u32[]{:S(2)}) collective-permute-start(bf16[576,256]{1,0:T(8,128)(2,1)S(1)} %pad_maximum_fusion.2), channel_id=1, source_target_pairs={{0,2},{1,3},{2,0},{3,1},{4,6},{5,7},{6,4},{7,5},{8,10},{9,11},{10,... | collective-permute-start | bytes 884744 | tf_op jit(solution)/shard_map/ppermute | solution.py:33
  28.1 13.3 %collective-permute-start.15 = (bf16[64,1792]{1,0:T(8,128)(2,1)S(1)}, bf16[64,1792]{1,0:T(8,128)(2,1)S(1)}, u32[]{:S(2)}, u32[]{:S(2)}) collective-permute-start(bf16[64,1792]{1,0:T(8,128)(2,1)S(1)} %collective-permute-done.14.refs_15_), channel_id=1, source_target_pairs={{0,16},{1,17},{2,18},{3,19},{4,20},{5,21},{6,22},{7,23},{8,24},{9,... | collective-permute-start | bytes 688136 | tf_op jit(solution)/shard_map/ppermute | solution.py:33
  29.8 11.6 %collective-permute-start.16 = (bf16[64,1792]{1,0:T(8,128)(2,1)S(1)}, bf16[64,1792]{1,0:T(8,128)(2,1)S(1)}, u32[]{:S(2)}, u32[]{:S(2)}) collective-permute-start(bf16[64,1792]{1,0:T(8,128)(2,1)S(1)} %collective-permute-done.11.refs_16_), channel_id=1, source_target_pairs={{0,16},{1,17},{2,18},{3,19},{4,20},{5,21},{6,22},{7,23},{8,24},{9,... | collective-permute-start | bytes 688136 | tf_op jit(solution)/shard_map/ppermute | solution.py:33
  31.6 11.5 %collective-permute-start.10 = (bf16[64,1792]{1,0:T(8,128)(2,1)S(1)}, bf16[64,1792]{1,0:T(8,128)(2,1)S(1)}, u32[]{:S(2)}, u32[]{:S(2)}) collective-permute-start(bf16[64,1792]{1,0:T(8,128)(2,1)S(1)} %collective-permute-done.9.refs_9_), channel_id=1, source_target_pairs={{0,112},{1,113},{2,114},{3,115},{4,116},{5,117},{6,118},{7,119},{8... | collective-permute-start | bytes 688136 | tf_op jit(solution)/shard_map/ppermute | solution.py:33
  33.6 9.5 %collective-permute-start.12 = (bf16[64,1792]{1,0:T(8,128)(2,1)S(1)}, bf16[64,1792]{1,0:T(8,128)(2,1)S(1)}, u32[]{:S(2)}, u32[]{:S(2)}) collective-permute-start(bf16[64,1792]{1,0:T(8,128)(2,1)S(1)} %collective-permute-done.11.refs_16_), channel_id=1, source_target_pairs={{0,112},{1,113},{2,114},{3,115},{4,116},{5,117},{6,118},{7,119},{8... | collective-permute-start | bytes 688136 | tf_op jit(solution)/shard_map/ppermute | solution.py:33
  38.1 8.3 %copy-start.2 = (bf16[1024,640]{1,0:T(8,128)(2,1)S(1)}, bf16[1024,640]{1,0:T(8,128)(2,1)}, u32[]{:S(2)}) copy-start(bf16[1024,640]{1,0:T(8,128)(2,1)} %get-tuple-element.24.queries) | copy-start | bytes 3932164
  43.1 11.5 %collective-permute-start.13 = (bf16[128,1792]{1,0:T(8,128)(2,1)S(1)}, bf16[128,1792]{1,0:T(8,128)(2,1)S(1)}, u32[]{:S(2)}, u32[]{:S(2)}) collective-permute-start(bf16[128,1792]{1,0:T(8,128)(2,1)S(1)} %pad_maximum_fusion), channel_id=1, source_target_pairs={{0,112},{1,113},{2,114},{3,115},{4,116},{5,117},{6,118},{7,119},{8... | collective-permute-start | bytes 1376264 | tf_op jit(solution)/shard_map/ppermute | solution.py:33
  46.3 11.8 %collective-permute-start.17 = (bf16[128,1792]{1,0:T(8,128)(2,1)S(1)}, bf16[128,1792]{1,0:T(8,128)(2,1)S(1)}, u32[]{:S(2)}, u32[]{:S(2)}) collective-permute-start(bf16[128,1792]{1,0:T(8,128)(2,1)S(1)} %pad_maximum_fusion.1), channel_id=1, source_target_pairs={{0,16},{1,17},{2,18},{3,19},{4,20},{5,21},{6,22},{7,23},{8,24},{9,... | collective-permute-start | bytes 1376264 | tf_op jit(solution)/shard_map/ppermute | solution.py:33
  46.3 11.8 %collective-permute-start.8 = (bf16[256,512]{1,0:T(8,128)(2,1)S(1)}, bf16[256,512]{1,0:T(8,128)(2,1)S(1)}, u32[]{:S(2)}, u32[]{:S(2)}) collective-permute-start(bf16[256,512]{1,0:T(8,128)(2,1)S(1)} %attend.2.refs_0_), channel_id=1, source_target_pairs={{0,129},{1,128},{2,131},{3,130},{4,133},{5,132},{6,135},{7,134},{8... | collective-permute-start | bytes 786440 | tf_op jit(solution)/shard_map/ppermute | solution.py:33
  46.4 11.9 %collective-permute-start.3 = (bf16[256,512]{1,0:T(8,128)(2,1)S(1)}, bf16[256,512]{1,0:T(8,128)(2,1)S(1)}, u32[]{:S(2)}, u32[]{:S(2)}) collective-permute-start(bf16[256,512]{1,0:T(8,128)(2,1)S(1)} %attend.2.refs_0_), channel_id=1, source_target_pairs={{0,1},{1,0},{2,3},{3,2},{4,5},{5,4},{6,7},{7,6},{8,9},{9,8},{10,11... | collective-permute-start | bytes 786440 | tf_op jit(solution)/shard_map/ppermute | solution.py:33
  46.4 22.6 %copy-start.5 = (bf16[64,1792]{1,0:T(8,128)(2,1)S(1)}, bf16[64,1792]{1,0:T(8,128)(2,1)}, u32[]{:S(2)}) copy-start(bf16[64,1792]{1,0:T(8,128)(2,1)} %get-tuple-element.25.refs_8_) | copy-start | bytes 688132
  50.2 9.7 %collective-permute-start.6 = (bf16[256,512]{1,0:T(8,128)(2,1)S(1)}, bf16[256,512]{1,0:T(8,128)(2,1)S(1)}, u32[]{:S(2)}, u32[]{:S(2)}) collective-permute-start(bf16[256,512]{1,0:T(8,128)(2,1)S(1)} %attend.3.refs_1_), channel_id=1, source_target_pairs={{0,129},{1,128},{2,131},{3,130},{4,133},{5,132},{6,135},{7,134},{8... | collective-permute-start | bytes 786440 | tf_op jit(solution)/shard_map/ppermute | solution.py:33
  54.7 6.5 %collective-permute-start.19 = (bf16[64,1792]{1,0:T(8,128)(2,1)S(1)}, bf16[64,1792]{1,0:T(8,128)(2,1)S(1)}, u32[]{:S(2)}, u32[]{:S(2)}) collective-permute-start(bf16[64,1792]{1,0:T(8,128)(2,1)S(1)} %slice.96), channel_id=1, source_target_pairs={{0,112},{1,113},{2,114},{3,115},{4,116},{5,117},{6,118},{7,119},{8... | collective-permute-start | bytes 688136 | tf_op jit(solution)/shard_map/ppermute | solution.py:33
  58.2 10.8 %collective-permute-start.18 = (bf16[128,1792]{1,0:T(8,128)(2,1)S(1)}, bf16[128,1792]{1,0:T(8,128)(2,1)S(1)}, u32[]{:S(2)}, u32[]{:S(2)}) collective-permute-start(bf16[128,1792]{1,0:T(8,128)(2,1)S(1)} %collective-permute-done.17.refs_13_), channel_id=1, source_target_pairs={{0,16},{1,17},{2,18},{3,19},{4,20},{5,21},{6,22},{7,23},{8,24},{9,... | collective-permute-start | bytes 1376264 | tf_op jit(solution)/shard_map/ppermute | solution.py:33
  58.2 6.1 %collective-permute-start.4 = (bf16[256,512]{1,0:T(8,128)(2,1)S(1)}, bf16[256,512]{1,0:T(8,128)(2,1)S(1)}, u32[]{:S(2)}, u32[]{:S(2)}) collective-permute-start(bf16[256,512]{1,0:T(8,128)(2,1)S(1)} %attend.3.refs_1_), channel_id=1, source_target_pairs={{0,1},{1,0},{2,3},{3,2},{4,5},{5,4},{6,7},{7,6},{8,9},{9,8},{10,11... | collective-permute-start | bytes 786440 | tf_op jit(solution)/shard_map/ppermute | solution.py:33
  58.3 6.5 %collective-permute-start.5 = (bf16[256,512]{1,0:T(8,128)(2,1)S(1)}, bf16[256,512]{1,0:T(8,128)(2,1)S(1)}, u32[]{:S(2)}, u32[]{:S(2)}) collective-permute-start(bf16[256,512]{1,0:T(8,128)(2,1)S(1)} %collective-permute-done.3.refs_2_), channel_id=1, source_target_pairs={{0,129},{1,128},{2,131},{3,130},{4,133},{5,132},{6,135},{7,134},{8... | collective-permute-start | bytes 786440 | tf_op jit(solution)/shard_map/ppermute | solution.py:33
  59.8 9.1 %collective-permute-start.7 = (bf16[256,512]{1,0:T(8,128)(2,1)S(1)}, bf16[256,512]{1,0:T(8,128)(2,1)S(1)}, u32[]{:S(2)}, u32[]{:S(2)}) collective-permute-start(bf16[256,512]{1,0:T(8,128)(2,1)S(1)} %collective-permute-done.6.refs_7_), channel_id=1, source_target_pairs={{0,1},{1,0},{2,3},{3,2},{4,5},{5,4},{6,7},{7,6},{8,9},{9,8},{10,11... | collective-permute-start | bytes 786440 | tf_op jit(solution)/shard_map/ppermute | solution.py:33
  61.1 7.8 %collective-permute-start.20 = (bf16[64,1792]{1,0:T(8,128)(2,1)S(1)}, bf16[64,1792]{1,0:T(8,128)(2,1)S(1)}, u32[]{:S(2)}, u32[]{:S(2)}) collective-permute-start(bf16[64,1792]{1,0:T(8,128)(2,1)S(1)} %collective-permute-done.19.refs_18_), channel_id=1, source_target_pairs={{0,112},{1,113},{2,114},{3,115},{4,116},{5,117},{6,118},{7,119},{8... | collective-permute-start | bytes 688136 | tf_op jit(solution)/shard_map/ppermute | solution.py:33
  71.3 9.8 %collective-permute-start.21 = (bf16[3,256,896]{2,1,0:T(8,128)(2,1)S(1)}, bf16[3,256,896]{2,1,0:T(8,128)(2,1)S(1)}, u32[]{:S(2)}, u32[]{:S(2)}) collective-permute-start(bf16[3,256,896]{2,1,0:T(8,128)(2,1)S(1)} %get-tuple-element.32), channel_id=1, source_target_pairs={{0,2},{1,3},{2,0},{3,1},{4,6},{5,7},{6,4},{7,5},{8,10},{9,11},{10,... | collective-permute-start | bytes 4128776 | tf_op jit(solution)/shard_map/ppermute | solution.py:33
  75.0 3.4 %collective-permute-start.24 = (bf16[256,896]{1,0:T(8,128)(2,1)S(1)}, bf16[256,896]{1,0:T(8,128)(2,1)S(1)}, u32[]{:S(2)}, u32[]{:S(2)}) collective-permute-start(bf16[256,896]{1,0:T(8,128)(2,1)S(1)} %get-tuple-element.35), channel_id=1, source_target_pairs={{0,2},{1,3},{2,0},{3,1},{4,6},{5,7},{6,4},{7,5},{8,10},{9,11},{10,... | collective-permute-start | bytes 1376264 | tf_op jit(solution)/shard_map/ppermute | solution.py:33
  78.5 11.6 %collective-permute-start.29 = (bf16[128,896]{1,0:T(8,128)(2,1)S(1)}, bf16[128,896]{1,0:T(8,128)(2,1)S(1)}, u32[]{:S(2)}, u32[]{:S(2)}) collective-permute-start(bf16[128,896]{1,0:T(8,128)(2,1)S(1)} %get-tuple-element.44), channel_id=1, source_target_pairs={{0,12},{1,13},{2,14},{3,15},{4,0},{5,1},{6,2},{7,3},{8,4},{9,5},{1... | collective-permute-start | bytes 688136 | tf_op jit(solution)/shard_map/ppermute | solution.py:33
  81.1 7.7 %collective-permute-start.25 = (bf16[128,896]{1,0:T(8,128)(2,1)S(1)}, bf16[128,896]{1,0:T(8,128)(2,1)S(1)}, u32[]{:S(2)}, u32[]{:S(2)}) collective-permute-start(bf16[128,896]{1,0:T(8,128)(2,1)S(1)} %get-tuple-element.45), channel_id=1, source_target_pairs={{0,4},{1,5},{2,6},{3,7},{4,8},{5,9},{6,10},{7,11},{8,12},{9,13},{1... | collective-permute-start | bytes 688136 | tf_op jit(solution)/shard_map/ppermute | solution.py:33
  81.4 10.3 %collective-permute-start.22 = (bf16[128,896]{1,0:T(8,128)(2,1)S(1)}, bf16[128,896]{1,0:T(8,128)(2,1)S(1)}, u32[]{:S(2)}, u32[]{:S(2)}) collective-permute-start(bf16[128,896]{1,0:T(8,128)(2,1)S(1)} %fusion.10), channel_id=1, source_target_pairs={{0,12},{1,13},{2,14},{3,15},{4,0},{5,1},{6,2},{7,3},{8,4},{9,5},{1... | collective-permute-start | bytes 688136 | tf_op jit(solution)/shard_map/ppermute | solution.py:33
  84.2 9.6 %collective-permute-start.27 = (bf16[128,896]{1,0:T(8,128)(2,1)S(1)}, bf16[128,896]{1,0:T(8,128)(2,1)S(1)}, u32[]{:S(2)}, u32[]{:S(2)}) collective-permute-start(bf16[128,896]{1,0:T(8,128)(2,1)S(1)} %fusion.9), channel_id=1, source_target_pairs={{0,4},{1,5},{2,6},{3,7},{4,8},{5,9},{6,10},{7,11},{8,12},{9,13},{1... | collective-permute-start | bytes 688136 | tf_op jit(solution)/shard_map/ppermute | solution.py:33
  88.9 11.5 %collective-permute-start.26 = (bf16[128,896]{1,0:T(8,128)(2,1)S(1)}, bf16[128,896]{1,0:T(8,128)(2,1)S(1)}, u32[]{:S(2)}, u32[]{:S(2)}) collective-permute-start(bf16[128,896]{1,0:T(8,128)(2,1)S(1)} %fusion.6), channel_id=1, source_target_pairs={{0,4},{1,5},{2,132},{3,133},{4,8},{5,9},{6,136},{7,137},{8,12},{9,... | collective-permute-start | bytes 688136 | tf_op jit(solution)/shard_map/ppermute | solution.py:33
  90.1 10.3 %collective-permute-start.30 = (bf16[128,896]{1,0:T(8,128)(2,1)S(1)}, bf16[128,896]{1,0:T(8,128)(2,1)S(1)}, u32[]{:S(2)}, u32[]{:S(2)}) collective-permute-start(bf16[128,896]{1,0:T(8,128)(2,1)S(1)} %fusion.2), channel_id=1, source_target_pairs={{0,13},{1,12},{2,141},{3,140},{4,1},{5,0},{6,129},{7,128},{8,5},{9... | collective-permute-start | bytes 688136 | tf_op jit(solution)/shard_map/ppermute | solution.py:33
  93.8 9.5 %collective-permute-start.28 = (bf16[128,896]{1,0:T(8,128)(2,1)S(1)}, bf16[128,896]{1,0:T(8,128)(2,1)S(1)}, u32[]{:S(2)}, u32[]{:S(2)}) collective-permute-start(bf16[128,896]{1,0:T(8,128)(2,1)S(1)} %get-tuple-element.42), channel_id=1, source_target_pairs={{0,1},{1,0},{2,129},{3,128},{4,5},{5,4},{6,133},{7,132},{8,9},{9,8... | collective-permute-start | bytes 688136 | tf_op jit(solution)/shard_map/ppermute | solution.py:33
  95.3 9.5 %collective-permute-start.23 = (bf16[128,896]{1,0:T(8,128)(2,1)S(1)}, bf16[128,896]{1,0:T(8,128)(2,1)S(1)}, u32[]{:S(2)}, u32[]{:S(2)}) collective-permute-start(bf16[128,896]{1,0:T(8,128)(2,1)S(1)} %get-tuple-element.43), channel_id=1, source_target_pairs={{0,0},{1,1},{2,128},{3,129},{4,4},{5,5},{6,132},{7,133},{8,8},{9,9... | collective-permute-start | bytes 688136 | tf_op jit(solution)/shard_map/ppermute | solution.py:33

commit v11 on v10

--- a/solution.py
+++ b/solution.py
@@ -190,10 +190,10 @@
 
 
 def project_kernel(theirs, *refs):
-    groups, held, outs, (rows, total) = refs[:8], refs[8:21], refs[21:-2], refs[-2:]
-    own, d1, d2, d3, u4, u3, u2, u1, other, e1, e3, e4, v1 = held
-    blocks = [own, d1, d2, d3.at[:64], u4.at[:64], u3.at[:64], u2, u1]
-    blocks += [other, e1, d3.at[64:], e3, e4, u4.at[64:], u3.at[64:], v1]
+    groups, held, outs, (rows, total) = refs[:8], refs[8:19], refs[19:-2], refs[-2:]
+    own, d1, d2, d3, u4, u3, u2, u1, other, e3, e4 = held
+    blocks = [own, d1, *(both.at[:64] for both in (d2, d3, u4, u3, u2)), u1]
+    blocks += [other, d2.at[64:], d3.at[64:], e3, e4, *(both.at[64:] for both in (u4, u3, u2))]
     first = 2 * (lax.axis_index("c") ^ theirs)
     yh = lax.axis_index("yh")
     for pick in (0, 2):
@@ -282,7 +282,7 @@
     return call(
         functools.partial(project_kernel, theirs),
         [array((256, 896), kind), array((3, 256, 896), kind)],
-        whole(21),
+        whole(19),
         (*groups, *blocks),
         "project",
         2 * 512 * 1024 * 1792,
@@ -321,8 +321,8 @@
         ],
     )
     swapped = other_core(jnp.concatenate([near, far], 1))
-    u2, d2 = up_z(after(u1, queries[0])), down_z(after(d1, queries[0]))
-    v1, e1 = up_z(other), down_z(other)
+    u2 = up_z(after(jnp.concatenate([u1, other], 0), queries[0]))
+    d2 = down_z(after(jnp.concatenate([d1, other], 0), queries[0]))
 
     keys, hidden = call(
         keys_kernel,
@@ -357,23 +357,22 @@
     three = [xor_y(part, 3) for part in rows]
     two = [xor_y(one[0], 3), xor_y(three[1], 1)]
     groups = [*rows, *one, *two, *three]
-    u3 = up_z(after(jnp.concatenate([u2, v1], 0), rows[0]))
-    d3 = down_z(after(jnp.concatenate([d2, e1], 0), rows[0]))
+    u3, d3 = up_z(after(u2, *rows)), down_z(after(d2, *rows))
     u4 = up_z(u3)
     e3 = down_z(d3[64:])
     e4 = down_z(e3)
-    blocks = [own, d1, d2, d3, u4, u3, u2, u1, other, e1, e3, e4, v1]
+    blocks = [own, d1, d2, d3, u4, u3, u2, u1, other, e3, e4]
 
     first, rest = project(1, groups, blocks, BF)
     first, rest = other_core(first), other_core(rest)
     mine, mine_rest = project(0, groups, blocks, F32)
+    sums = [mine_rest[i] + rest[i].astype(F32) for i in range(3)]
+    early_up, early_down, first, mine = lax.optimization_barrier(
+        (sums[1][128:].astype(BF), sums[2][:128].astype(BF), first, mine)
+    )
     far_sum = (mine + first.astype(F32)).astype(BF)
     passing_up = along_x(far_sum[:128], 1)
     passing_down = along_x(far_sum[128:], 3)
-    sums = [mine_rest[i] + rest[i].astype(F32) for i in range(3)]
-    early_up, early_down = lax.optimization_barrier(
-        (sums[1][128:].astype(BF), sums[2][:128].astype(BF))
-    )
     early_up, early_down = along_x(early_up, 1), along_x(early_down, 3)
     late_up = home((sums[1][:128] + passing_up.astype(F32)).astype(BF), 0, 1)
     late_down = home((sums[2][128:] + passing_down.astype(F32)).astype(BF), 1, 3)

time: 106 us -> 105 us (level)
  starting transfers between devices: 53.4 us -> 50.5 us
  waiting for transfers between devices: 25.4 us -> 27.2 us
    ppermute x29 -> x27, starting transfers between devices: 44.1 us -> 41.2 us  [moved(): return lax.ppermute(a, AXES, pairs)]
    ppermute x29 -> x27, waiting for transfers between devices: 25.4 us -> 27.2 us  [moved(): return lax.ppermute(a, AXES, pairs)]
  transfers between devices with their start and end apart: 31 -> 29, of which waited for: 12 -> 12; matrix products, arithmetic and copies ran while one was open for 2% -> 2% of each run, Pallas kernels for 18% -> 19%
where the time goes in v11:
time: 105 us
  starting transfers between devices  50.5 us (48%)
  waiting for transfers between devices  27.2 us (26%)
  Pallas kernels  21.8 us (21%)
  other arithmetic  3 us (3%)
  local copies, waits for them, and re-layouts  1.36 us (1%)
    ppermute x27, starting transfers between devices, moved(): return lax.ppermute(a, AXES, pairs)  41.2 us
    ppermute x27, waiting for transfers between devices, moved(): return lax.ppermute(a, AXES, pairs)  27.2 us
    pallas_call x6, Pallas kernels, call(): pl.pallas_call(kernel, out_shape=shapes, in_specs=specs, out_specs=whole(...  19.6 us
    ppermute x2, starting transfers between devices, local(): lax.ppermute(half, CTX, [(i, i + by) for i in range(16 - by)])  9.28 us
    pallas_call x1, Pallas kernels, quarters(): pl.pallas_call(quarter_kernel, out_shape=[jax.ShapeDtypeStruct((64, 1792)...  2.22 us
  transfers between devices with their start and end apart: 29, of which 12 were waited for; matrix products, arithmetic and copies ran while one was open for 2% of the time, Pallas kernels for 19%

profile of v11, /device:TPU:1, one launch (start us, length us, event | category | flops | bytes accessed | tf_op | source)
XLA Modules:
  0.0 104.9 jit_solution(16909267552747694794)
XLA Ops:
  0.0 0.9 dynamic-slice_bitcast_fusion
  0.9 5.7 %collective-permute-start.1 = (bf16[576,128]{1,0:T(8,128)(2,1)S(1)}, bf16[576,128]{1,0:T(8,128)(2,1)S(1)}, u32[]{:S(2)}, u32[]{:S(2)}) collective-permute-start(bf16[576,128]{1,0:T(8,128)(2,1)S(1)} %dynamic-slice_bitcast_fusion), channel_id=1, source_target_pairs={{0,32},{16,48},{32,64},{48,80},{64,96},{80,112},{96,128},{112,144}... | collective-permute-start | bytes 442376 | tf_op jit(solution)/shard_map/ppermute | solution.py:305
  6.7 3.5 %collective-permute-start = (bf16[576,128]{1,0:T(8,128)(2,1)S(1)}, bf16[576,128]{1,0:T(8,128)(2,1)S(1)}, u32[]{:S(2)}, u32[]{:S(2)}) collective-permute-start(bf16[576,128]{1,0:T(8,128)(2,1)S(1)} %dynamic-slice_bitcast_fusion), channel_id=1, source_target_pairs={{0,16},{16,32},{32,48},{48,64},{64,80},{80,96},{96,112},{112,128},... | collective-permute-start | bytes 442376 | tf_op jit(solution)/shard_map/ppermute | solution.py:305
  10.2 2.2 %quarters.1 = (bf16[64,1792]{1,0:T(8,128)(2,1)}, bf16[64,1792]{1,0:T(8,128)(2,1)}) custom-call(bf16[64,7168]{1,0:T(8,128)(2,1)} %bitcast.35), custom_call_target="tpu_custom_call" | custom-call | bytes 2097152 | tf_op jit(solution)/shard_map/quarters/pallas_call | solution.py:247
  12.4 2.8 %collective-permute-start.13 = (bf16[64,1792]{1,0:T(8,128)(2,1)}, bf16[64,1792]{1,0:T(8,128)(2,1)S(1)}, u32[]{:S(2)}, u32[]{:S(2)}) collective-permute-start(bf16[64,1792]{1,0:T(8,128)(2,1)} %get-tuple-element.27.refs_8_), channel_id=1, source_target_pairs={{0,16},{1,17},{2,18},{3,19},{4,20},{5,21},{6,22},{7,23},{8,24},{9,... | collective-permute-start | bytes 688136 | tf_op jit(solution)/shard_map/ppermute | solution.py:33
  15.3 0.8 collective-permute-start.9
  16.1 1.9 %collective-permute-start.10 = (bf16[64,1792]{1,0:T(8,128)(2,1)}, bf16[64,1792]{1,0:T(8,128)(2,1)S(1)}, u32[]{:S(2)}, u32[]{:S(2)}) collective-permute-start(bf16[64,1792]{1,0:T(8,128)(2,1)} %get-tuple-element.28), channel_id=1, source_target_pairs={{0,129},{1,128},{2,131},{3,130},{4,133},{5,132},{6,135},{7,134},{8... | collective-permute-start | bytes 688136 | tf_op jit(solution)/shard_map/ppermute | solution.py:33
  18.2 0.1 fusion.reorder
  18.3 0.8 fusion.11
  19.1 6.8 %queries.1 = (bf16[1024,640]{1,0:T(8,128)(2,1)}, bf16[1024,640]{1,0:T(8,128)(2,1)}) custom-call(bf16[256,1536]{1,0:T(8,128)(2,1)} %rows.1, bf16[1536,1536]{1,0:T(8,128)(2,1)} %w_query.1, bf16[8,128,512]{2,1,0:T(8,128)(2,1)} %w_key_up.1, f32[64,128]{1,0:T(8,128)} %get-tuple-element.59.cosines, f32[64,128]{1,0:T(8,128)} %get-tuple-element.58.sines), custom_call_target="tpu_custom_call" | custom-call | flops 1476395008 | bytes 8388608 | tf_op jit(solution)/shard_map/queries/pallas_call | solution.py:259
  26.0 2.0 %collective-permute-start.2 = (bf16[576,256]{1,0:T(8,128)(2,1)S(1)}, bf16[576,256]{1,0:T(8,128)(2,1)S(1)}, u32[]{:S(2)}, u32[]{:S(2)}) collective-permute-start(bf16[576,256]{1,0:T(8,128)(2,1)S(1)} %pad_maximum_fusion.2), channel_id=1, source_target_pairs={{0,2},{1,3},{2,0},{3,1},{4,6},{5,7},{6,4},{7,5},{8,10},{9,11},{10,... | collective-permute-start | bytes 884744 | tf_op jit(solution)/shard_map/ppermute | solution.py:33
  28.2 1.7 %collective-permute-start.14 = (bf16[128,1792]{1,0:T(8,128)(2,1)S(1)}, bf16[128,1792]{1,0:T(8,128)(2,1)S(1)}, u32[]{:S(2)}, u32[]{:S(2)}) collective-permute-start(bf16[128,1792]{1,0:T(8,128)(2,1)S(1)} %get-tuple-element.31), channel_id=1, source_target_pairs={{0,16},{1,17},{2,18},{3,19},{4,20},{5,21},{6,22},{7,23},{8,24},{9,... | collective-permute-start | bytes 1376264 | tf_op jit(solution)/shard_map/ppermute | solution.py:33
  29.9 0.4 multiply_sine_fusion
  31.0 0.6 keys.1
  31.7 3.8 %attend.2.refs_0_ = bf16[256,512]{1,0:T(8,128)(2,1)S(1)} custom-call(bf16[1024,640]{1,0:T(8,128)(2,1)S(1)} %copy-done.3, bf16[640,768]{1,0:T(8,128)(2,1)S(1)} %get-tuple-element.24.keys, f32[256,768]{1,0:T(8,128)S(1)} %get-tuple-element.25.hidden, bf16[8,512,128]{2,1,0:T(8,128)(2,1)S(1)} %copy-done.4, bf16[512,512]{1,0:T(8,128)(2,1)S(1)} %fusion.reorder), custom_call_target="tpu_custom_call" | custom-call | flops 1946157056 | bytes 5242880 | tf_op jit(solution)/shard_map/attend/pallas_call | solution.py:259
  35.5 3.8 %attend.3.refs_1_ = bf16[256,512]{1,0:T(8,128)(2,1)S(1)} custom-call(bf16[1024,640]{1,0:T(8,128)(2,1)S(1)} %copy-done.2, bf16[640,768]{1,0:T(8,128)(2,1)S(1)} %get-tuple-element.24.keys, f32[256,768]{1,0:T(8,128)S(1)} %get-tuple-element.25.hidden, bf16[8,512,128]{2,1,0:T(8,128)(2,1)S(1)} %copy-done.4, bf16[512,512]{1,0:T(8,128)(2,1)S(1)} %fusion.reorder), custom_call_target="tpu_custom_call" | custom-call | flops 1946157056 | bytes 5242880 | tf_op jit(solution)/shard_map/attend/pallas_call | solution.py:259
  39.2 1.3 %collective-permute-done.11.refs_10_ = bf16[128,1792]{1,0:T(8,128)(2,1)S(1)} collective-permute-done((bf16[128,1792]{1,0:T(8,128)(2,1)S(1)}, bf16[128,1792]{1,0:T(8,128)(2,1)S(1)}, u32[]{:S(2)}, u32[]{:S(2)}) %collective-permute-start.11) | collective-permute-done | bytes 458784 | tf_op jit(solution)/shard_map/ppermute | solution.py:33
  40.6 1.1 %collective-permute-start.12 = (bf16[128,1792]{1,0:T(8,128)(2,1)S(1)}, bf16[128,1792]{1,0:T(8,128)(2,1)S(1)}, u32[]{:S(2)}, u32[]{:S(2)}) collective-permute-start(bf16[128,1792]{1,0:T(8,128)(2,1)S(1)} %collective-permute-done.11.refs_10_), channel_id=1, source_target_pairs={{0,112},{1,113},{2,114},{3,115},{4,116},{5,117},{6,118},{7,119},{8... | collective-permute-start | bytes 1376264 | tf_op jit(solution)/shard_map/ppermute | solution.py:33
  41.7 0.3 collective-permute-start.15
  42.1 1.9 %collective-permute-start.8 = (bf16[256,512]{1,0:T(8,128)(2,1)S(1)}, bf16[256,512]{1,0:T(8,128)(2,1)S(1)}, u32[]{:S(2)}, u32[]{:S(2)}) collective-permute-start(bf16[256,512]{1,0:T(8,128)(2,1)S(1)} %attend.2.refs_0_), channel_id=1, source_target_pairs={{0,129},{1,128},{2,131},{3,130},{4,133},{5,132},{6,135},{7,134},{8... | collective-permute-start | bytes 786440 | tf_op jit(solution)/shard_map/ppermute | solution.py:33
  43.9 0.8 collective-permute-start.6
  44.7 7.2 %collective-permute-done.12.refs_11_ = bf16[128,1792]{1,0:T(8,128)(2,1)S(1)} collective-permute-done((bf16[128,1792]{1,0:T(8,128)(2,1)S(1)}, bf16[128,1792]{1,0:T(8,128)(2,1)S(1)}, u32[]{:S(2)}, u32[]{:S(2)}) %collective-permute-start.12) | collective-permute-done | bytes 458784 | tf_op jit(solution)/shard_map/ppermute | solution.py:33
  52.0 2.5 %collective-permute-start.17 = (bf16[64,1792]{1,0:T(8,128)(2,1)S(1)}, bf16[64,1792]{1,0:T(8,128)(2,1)S(1)}, u32[]{:S(2)}, u32[]{:S(2)}) collective-permute-start(bf16[64,1792]{1,0:T(8,128)(2,1)S(1)} %slice.96), channel_id=1, source_target_pairs={{0,112},{1,113},{2,114},{3,115},{4,116},{5,117},{6,118},{7,119},{8... | collective-permute-start | bytes 688136 | tf_op jit(solution)/shard_map/ppermute | solution.py:33
  54.6 2.0 %collective-permute-start.5 = (bf16[256,512]{1,0:T(8,128)(2,1)S(1)}, bf16[256,512]{1,0:T(8,128)(2,1)S(1)}, u32[]{:S(2)}, u32[]{:S(2)}) collective-permute-start(bf16[256,512]{1,0:T(8,128)(2,1)S(1)} %collective-permute-done.3.refs_2_), channel_id=1, source_target_pairs={{0,129},{1,128},{2,131},{3,130},{4,133},{5,132},{6,135},{7,134},{8... | collective-permute-start | bytes 786440 | tf_op jit(solution)/shard_map/ppermute | solution.py:33
  56.7 0.8 collective-permute-start.7
  57.4 0.5 collective-permute-done.17.refs_17_
  57.9 3.4 %collective-permute-start.18 = (bf16[64,1792]{1,0:T(8,128)(2,1)S(1)}, bf16[64,1792]{1,0:T(8,128)(2,1)S(1)}, u32[]{:S(2)}, u32[]{:S(2)}) collective-permute-start(bf16[64,1792]{1,0:T(8,128)(2,1)S(1)} %collective-permute-done.17.refs_17_), channel_id=1, source_target_pairs={{0,112},{1,113},{2,114},{3,115},{4,116},{5,117},{6,118},{7,119},{8... | collective-permute-start | bytes 688136 | tf_op jit(solution)/shard_map/ppermute | solution.py:33
  61.3 0.6 collective-permute-done.5.refs_4_
  62.0 4.3 %collective-permute-done.7.refs_5_ = bf16[256,512]{1,0:T(8,128)(2,1)S(1)} collective-permute-done((bf16[256,512]{1,0:T(8,128)(2,1)S(1)}, bf16[256,512]{1,0:T(8,128)(2,1)S(1)}, u32[]{:S(2)}, u32[]{:S(2)}) %collective-permute-start.7) | collective-permute-done | bytes 262176 | tf_op jit(solution)/shard_map/ppermute | solution.py:33
  66.3 2.3 %project.3 = (bf16[256,896]{1,0:T(8,128)(2,1)S(1)}, bf16[3,256,896]{2,1,0:T(8,128)(2,1)S(1)}) custom-call(bf16[256,512]{1,0:T(8,128)(2,1)S(1)} %attend.2.refs_0_, bf16[256,512]{1,0:T(8,128)(2,1)S(1)} %attend.3.refs_1_, bf16[256,512]{1,0:T(8,128)(2,1)S(1)} %collective-permute-done.3.refs_2_, bf16[256,512]{1,0:T(8,128)(2,1)S(1)} %collective-permute-done.4.refs_3_, ...), custom_call_target="tpu_custom_call" | custom-call | flops 1879048192 | bytes 8388608 | tf_op jit(solution)/shard_map/project/pallas_call | solution.py:259
  68.6 2.8 %collective-permute-start.19 = (bf16[3,256,896]{2,1,0:T(8,128)(2,1)S(1)}, bf16[3,256,896]{2,1,0:T(8,128)(2,1)S(1)}, u32[]{:S(2)}, u32[]{:S(2)}) collective-permute-start(bf16[3,256,896]{2,1,0:T(8,128)(2,1)S(1)} %get-tuple-element.34), channel_id=1, source_target_pairs={{0,2},{1,3},{2,0},{3,1},{4,6},{5,7},{6,4},{7,5},{8,10},{9,11},{10,... | collective-permute-start | bytes 4128776 | tf_op jit(solution)/shard_map/ppermute | solution.py:33
  71.4 2.3 %project.2 = (f32[256,896]{1,0:T(8,128)S(1)}, f32[3,256,896]{2,1,0:T(8,128)S(1)}) custom-call(bf16[256,512]{1,0:T(8,128)(2,1)S(1)} %attend.2.refs_0_, bf16[256,512]{1,0:T(8,128)(2,1)S(1)} %attend.3.refs_1_, bf16[256,512]{1,0:T(8,128)(2,1)S(1)} %collective-permute-done.3.refs_2_, bf16[256,512]{1,0:T(8,128)(2,1)S(1)} %collective-permute-done.4.refs_3_, ...), custom_call_target="tpu_custom_call" | custom-call | flops 1879048192 | bytes 8388608 | tf_op jit(solution)/shard_map/project/pallas_call | solution.py:259
  73.8 0.3 collective-permute-done.19
  74.1 0.2 convert_add_fusion.2
  74.4 0.4 collective-permute-done.20
  74.8 2.5 %collective-permute-start.21 = (bf16[128,896]{1,0:T(8,128)(2,1)S(1)}, bf16[128,896]{1,0:T(8,128)(2,1)S(1)}, u32[]{:S(2)}, u32[]{:S(2)}) collective-permute-start(bf16[128,896]{1,0:T(8,128)(2,1)S(1)} %fusion.10), channel_id=1, source_target_pairs={{0,12},{1,13},{2,14},{3,15},{4,0},{5,1},{6,2},{7,3},{8,4},{9,5},{1... | collective-permute-start | bytes 688136 | tf_op jit(solution)/shard_map/ppermute | solution.py:33
  77.4 2.8 %collective-permute-start.27 = (bf16[128,896]{1,0:T(8,128)(2,1)S(1)}, bf16[128,896]{1,0:T(8,128)(2,1)S(1)}, u32[]{:S(2)}, u32[]{:S(2)}) collective-permute-start(bf16[128,896]{1,0:T(8,128)(2,1)S(1)} %get-tuple-element.48), channel_id=1, source_target_pairs={{0,12},{1,13},{2,14},{3,15},{4,0},{5,1},{6,2},{7,3},{8,4},{9,5},{1... | collective-permute-start | bytes 688136 | tf_op jit(solution)/shard_map/ppermute | solution.py:33
  80.1 1.7 %collective-permute-done.21 = bf16[128,896]{1,0:T(8,128)(2,1)S(1)} collective-permute-done((bf16[128,896]{1,0:T(8,128)(2,1)S(1)}, bf16[128,896]{1,0:T(8,128)(2,1)S(1)}, u32[]{:S(2)}, u32[]{:S(2)}) %collective-permute-start.21) | collective-permute-done | bytes 229408 | tf_op jit(solution)/shard_map/ppermute | solution.py:33
  81.9 3.1 %collective-permute-done.25 = bf16[128,896]{1,0:T(8,128)(2,1)S(1)} collective-permute-done((bf16[128,896]{1,0:T(8,128)(2,1)S(1)}, bf16[128,896]{1,0:T(8,128)(2,1)S(1)}, u32[]{:S(2)}, u32[]{:S(2)}) %collective-permute-start.25) | collective-permute-done | bytes 229408 | tf_op jit(solution)/shard_map/ppermute | solution.py:33
  85.0 4.5 %collective-permute-start.26 = (bf16[128,896]{1,0:T(8,128)(2,1)S(1)}, bf16[128,896]{1,0:T(8,128)(2,1)S(1)}, u32[]{:S(2)}, u32[]{:S(2)}) collective-permute-start(bf16[128,896]{1,0:T(8,128)(2,1)S(1)} %get-tuple-element.46), channel_id=1, source_target_pairs={{0,1},{1,0},{2,129},{3,128},{4,5},{5,4},{6,133},{7,132},{8,9},{9,8... | collective-permute-start | bytes 688136 | tf_op jit(solution)/shard_map/ppermute | solution.py:33
  89.6 1.9 %collective-permute-start.22 = (bf16[128,896]{1,0:T(8,128)(2,1)S(1)}, bf16[128,896]{1,0:T(8,128)(2,1)S(1)}, u32[]{:S(2)}, u32[]{:S(2)}) collective-permute-start(bf16[128,896]{1,0:T(8,128)(2,1)S(1)} %get-tuple-element.47), channel_id=1, source_target_pairs={{0,0},{1,1},{2,128},{3,129},{4,4},{5,5},{6,132},{7,133},{8,8},{9,9... | collective-permute-start | bytes 688136 | tf_op jit(solution)/shard_map/ppermute | solution.py:33
  91.6 1.5 %collective-permute-start.28 = (bf16[128,896]{1,0:T(8,128)(2,1)S(1)}, bf16[128,896]{1,0:T(8,128)(2,1)S(1)}, u32[]{:S(2)}, u32[]{:S(2)}) collective-permute-start(bf16[128,896]{1,0:T(8,128)(2,1)S(1)} %fusion.2), channel_id=1, source_target_pairs={{0,13},{1,12},{2,141},{3,140},{4,1},{5,0},{6,129},{7,128},{8,5},{9... | collective-permute-start | bytes 688136 | tf_op jit(solution)/shard_map/ppermute | solution.py:33
  93.1 2.8 %collective-permute-start.24 = (bf16[128,896]{1,0:T(8,128)(2,1)S(1)}, bf16[128,896]{1,0:T(8,128)(2,1)S(1)}, u32[]{:S(2)}, u32[]{:S(2)}) collective-permute-start(bf16[128,896]{1,0:T(8,128)(2,1)S(1)} %fusion.6), channel_id=1, source_target_pairs={{0,4},{1,5},{2,132},{3,133},{4,8},{5,9},{6,136},{7,137},{8,12},{9,... | collective-permute-start | bytes 688136 | tf_op jit(solution)/shard_map/ppermute | solution.py:33
  95.9 3.6 %collective-permute-done.22 = bf16[128,896]{1,0:T(8,128)(2,1)S(1)} collective-permute-done((bf16[128,896]{1,0:T(8,128)(2,1)S(1)}, bf16[128,896]{1,0:T(8,128)(2,1)S(1)}, u32[]{:S(2)}, u32[]{:S(2)}) %collective-permute-start.22) | collective-permute-done | bytes 229408 | tf_op jit(solution)/shard_map/ppermute | solution.py:33
  99.5 1.2 %collective-permute-done.28 = bf16[128,896]{1,0:T(8,128)(2,1)S(1)} collective-permute-done((bf16[128,896]{1,0:T(8,128)(2,1)S(1)}, bf16[128,896]{1,0:T(8,128)(2,1)S(1)}, u32[]{:S(2)}, u32[]{:S(2)}) %collective-permute-start.28) | collective-permute-done | bytes 229408 | tf_op jit(solution)/shard_map/ppermute | solution.py:33
  100.7 2.9 %collective-permute-done.24 = bf16[128,896]{1,0:T(8,128)(2,1)S(1)} collective-permute-done((bf16[128,896]{1,0:T(8,128)(2,1)S(1)}, bf16[128,896]{1,0:T(8,128)(2,1)S(1)}, u32[]{:S(2)}, u32[]{:S(2)}) %collective-permute-start.24) | collective-permute-done | bytes 229408 | tf_op jit(solution)/shard_map/ppermute | solution.py:33
  103.6 0.1 broadcast_select_fusion.1
  104.0 0.9 maximum_maximum_fusion
  (55 shorter events, 1.2 us)
Async XLA Ops:
  0.9 25.0 %collective-permute-start.1 = (bf16[576,128]{1,0:T(8,128)(2,1)S(1)}, bf16[576,128]{1,0:T(8,128)(2,1)S(1)}, u32[]{:S(2)}, u32[]{:S(2)}) collective-permute-start(bf16[576,128]{1,0:T(8,128)(2,1)S(1)} %dynamic-slice_bitcast_fusion), channel_id=1, source_target_pairs={{0,32},{16,48},{32,64},{48,80},{64,96},{80,112},{96,128},{112,144}... | collective-permute-start | bytes 442376 | tf_op jit(solution)/shard_map/ppermute | solution.py:305
  6.7 19.3 %collective-permute-start = (bf16[576,128]{1,0:T(8,128)(2,1)S(1)}, bf16[576,128]{1,0:T(8,128)(2,1)S(1)}, u32[]{:S(2)}, u32[]{:S(2)}) collective-permute-start(bf16[576,128]{1,0:T(8,128)(2,1)S(1)} %dynamic-slice_bitcast_fusion), channel_id=1, source_target_pairs={{0,16},{16,32},{32,48},{48,64},{64,80},{80,96},{96,112},{112,128},... | collective-permute-start | bytes 442376 | tf_op jit(solution)/shard_map/ppermute | solution.py:305
  12.4 15.6 %collective-permute-start.13 = (bf16[64,1792]{1,0:T(8,128)(2,1)}, bf16[64,1792]{1,0:T(8,128)(2,1)S(1)}, u32[]{:S(2)}, u32[]{:S(2)}) collective-permute-start(bf16[64,1792]{1,0:T(8,128)(2,1)} %get-tuple-element.27.refs_8_), channel_id=1, source_target_pairs={{0,16},{1,17},{2,18},{3,19},{4,20},{5,21},{6,22},{7,23},{8,24},{9,... | collective-permute-start | bytes 688136 | tf_op jit(solution)/shard_map/ppermute | solution.py:33
  15.3 12.8 %collective-permute-start.9 = (bf16[64,1792]{1,0:T(8,128)(2,1)}, bf16[64,1792]{1,0:T(8,128)(2,1)S(1)}, u32[]{:S(2)}, u32[]{:S(2)}) collective-permute-start(bf16[64,1792]{1,0:T(8,128)(2,1)} %get-tuple-element.27.refs_8_), channel_id=1, source_target_pairs={{0,112},{1,113},{2,114},{3,115},{4,116},{5,117},{6,118},{7,119},{8... | collective-permute-start | bytes 688136 | tf_op jit(solution)/shard_map/ppermute | solution.py:33
  16.1 11.9 %collective-permute-start.10 = (bf16[64,1792]{1,0:T(8,128)(2,1)}, bf16[64,1792]{1,0:T(8,128)(2,1)S(1)}, u32[]{:S(2)}, u32[]{:S(2)}) collective-permute-start(bf16[64,1792]{1,0:T(8,128)(2,1)} %get-tuple-element.28), channel_id=1, source_target_pairs={{0,129},{1,128},{2,131},{3,130},{4,133},{5,132},{6,135},{7,134},{8... | collective-permute-start | bytes 688136 | tf_op jit(solution)/shard_map/ppermute | solution.py:33
  25.9 5.1 %copy-start = (bf16[256,576]{0,1:T(8,128)(2,1)S(1)}, bf16[256,576]{0,1:T(8,128)(2,1)}, u32[]{:S(2)}) copy-start(bf16[256,576]{0,1:T(8,128)(2,1)} %param.9) | copy-start | bytes 884740
  25.9 5.1 %copy-start.1 = (bf16[512,576]{0,1:T(8,128)(2,1)S(1)}, bf16[512,576]{0,1:T(8,128)(2,1)}, u32[]{:S(2)}) copy-start(bf16[512,576]{0,1:T(8,128)(2,1)} %param.10) | copy-start | bytes 1769476
  26.0 5.6 %copy-start.3 = (bf16[1024,640]{1,0:T(8,128)(2,1)S(1)}, bf16[1024,640]{1,0:T(8,128)(2,1)}, u32[]{:S(2)}) copy-start(bf16[1024,640]{1,0:T(8,128)(2,1)} %get-tuple-element.23.queries) | copy-start | bytes 3932164
  26.0 5.6 %copy-start.4 = (bf16[8,512,128]{2,1,0:T(8,128)(2,1)S(1)}, bf16[8,512,128]{2,1,0:T(8,128)(2,1)}, u32[]{:S(2)}) copy-start(bf16[8,512,128]{2,1,0:T(8,128)(2,1)} %w_value_up.3) | copy-start | bytes 3145732
  26.0 5.0 %collective-permute-start.2 = (bf16[576,256]{1,0:T(8,128)(2,1)S(1)}, bf16[576,256]{1,0:T(8,128)(2,1)S(1)}, u32[]{:S(2)}, u32[]{:S(2)}) collective-permute-start(bf16[576,256]{1,0:T(8,128)(2,1)S(1)} %pad_maximum_fusion.2), channel_id=1, source_target_pairs={{0,2},{1,3},{2,0},{3,1},{4,6},{5,7},{6,4},{7,5},{8,10},{9,11},{10,... | collective-permute-start | bytes 884744 | tf_op jit(solution)/shard_map/ppermute | solution.py:33
  28.1 12.5 %collective-permute-start.11 = (bf16[128,1792]{1,0:T(8,128)(2,1)S(1)}, bf16[128,1792]{1,0:T(8,128)(2,1)S(1)}, u32[]{:S(2)}, u32[]{:S(2)}) collective-permute-start(bf16[128,1792]{1,0:T(8,128)(2,1)S(1)} %get-tuple-element.29), channel_id=1, source_target_pairs={{0,112},{1,113},{2,114},{3,115},{4,116},{5,117},{6,118},{7,119},{8... | collective-permute-start | bytes 1376264 | tf_op jit(solution)/shard_map/ppermute | solution.py:33
  28.2 13.5 %collective-permute-start.14 = (bf16[128,1792]{1,0:T(8,128)(2,1)S(1)}, bf16[128,1792]{1,0:T(8,128)(2,1)S(1)}, u32[]{:S(2)}, u32[]{:S(2)}) collective-permute-start(bf16[128,1792]{1,0:T(8,128)(2,1)S(1)} %get-tuple-element.31), channel_id=1, source_target_pairs={{0,16},{1,17},{2,18},{3,19},{4,20},{5,21},{6,22},{7,23},{8,24},{9,... | collective-permute-start | bytes 1376264 | tf_op jit(solution)/shard_map/ppermute | solution.py:33
  31.7 3.8 %copy-start.2 = (bf16[1024,640]{1,0:T(8,128)(2,1)S(1)}, bf16[1024,640]{1,0:T(8,128)(2,1)}, u32[]{:S(2)}) copy-start(bf16[1024,640]{1,0:T(8,128)(2,1)} %get-tuple-element.26.queries) | copy-start | bytes 3932164
  35.5 30.8 %copy-start.5 = (bf16[64,1792]{1,0:T(8,128)(2,1)S(1)}, bf16[64,1792]{1,0:T(8,128)(2,1)}, u32[]{:S(2)}) copy-start(bf16[64,1792]{1,0:T(8,128)(2,1)} %get-tuple-element.27.refs_8_) | copy-start | bytes 688132
  40.6 11.3 %collective-permute-start.12 = (bf16[128,1792]{1,0:T(8,128)(2,1)S(1)}, bf16[128,1792]{1,0:T(8,128)(2,1)S(1)}, u32[]{:S(2)}, u32[]{:S(2)}) collective-permute-start(bf16[128,1792]{1,0:T(8,128)(2,1)S(1)} %collective-permute-done.11.refs_10_), channel_id=1, source_target_pairs={{0,112},{1,113},{2,114},{3,115},{4,116},{5,117},{6,118},{7,119},{8... | collective-permute-start | bytes 1376264 | tf_op jit(solution)/shard_map/ppermute | solution.py:33
  41.7 12.8 %collective-permute-start.15 = (bf16[128,1792]{1,0:T(8,128)(2,1)S(1)}, bf16[128,1792]{1,0:T(8,128)(2,1)S(1)}, u32[]{:S(2)}, u32[]{:S(2)}) collective-permute-start(bf16[128,1792]{1,0:T(8,128)(2,1)S(1)} %collective-permute-done.14.refs_14_), channel_id=1, source_target_pairs={{0,16},{1,17},{2,18},{3,19},{4,20},{5,21},{6,22},{7,23},{8,24},{9,... | collective-permute-start | bytes 1376264 | tf_op jit(solution)/shard_map/ppermute | solution.py:33
  42.1 12.5 %collective-permute-start.8 = (bf16[256,512]{1,0:T(8,128)(2,1)S(1)}, bf16[256,512]{1,0:T(8,128)(2,1)S(1)}, u32[]{:S(2)}, u32[]{:S(2)}) collective-permute-start(bf16[256,512]{1,0:T(8,128)(2,1)S(1)} %attend.2.refs_0_), channel_id=1, source_target_pairs={{0,129},{1,128},{2,131},{3,130},{4,133},{5,132},{6,135},{7,134},{8... | collective-permute-start | bytes 786440 | tf_op jit(solution)/shard_map/ppermute | solution.py:33
  43.9 10.7 %collective-permute-start.3 = (bf16[256,512]{1,0:T(8,128)(2,1)S(1)}, bf16[256,512]{1,0:T(8,128)(2,1)S(1)}, u32[]{:S(2)}, u32[]{:S(2)}) collective-permute-start(bf16[256,512]{1,0:T(8,128)(2,1)S(1)} %attend.2.refs_0_), channel_id=1, source_target_pairs={{0,1},{1,0},{2,3},{3,2},{4,5},{5,4},{6,7},{7,6},{8,9},{9,8},{10,11... | collective-permute-start | bytes 786440 | tf_op jit(solution)/shard_map/ppermute | solution.py:33
  43.9 12.7 %collective-permute-start.6 = (bf16[256,512]{1,0:T(8,128)(2,1)S(1)}, bf16[256,512]{1,0:T(8,128)(2,1)S(1)}, u32[]{:S(2)}, u32[]{:S(2)}) collective-permute-start(bf16[256,512]{1,0:T(8,128)(2,1)S(1)} %attend.3.refs_1_), channel_id=1, source_target_pairs={{0,129},{1,128},{2,131},{3,130},{4,133},{5,132},{6,135},{7,134},{8... | collective-permute-start | bytes 786440 | tf_op jit(solution)/shard_map/ppermute | solution.py:33
  52.0 6.0 %collective-permute-start.17 = (bf16[64,1792]{1,0:T(8,128)(2,1)S(1)}, bf16[64,1792]{1,0:T(8,128)(2,1)S(1)}, u32[]{:S(2)}, u32[]{:S(2)}) collective-permute-start(bf16[64,1792]{1,0:T(8,128)(2,1)S(1)} %slice.96), channel_id=1, source_target_pairs={{0,112},{1,113},{2,114},{3,115},{4,116},{5,117},{6,118},{7,119},{8... | collective-permute-start | bytes 688136 | tf_op jit(solution)/shard_map/ppermute | solution.py:33
  54.5 11.8 %collective-permute-start.16 = (bf16[128,1792]{1,0:T(8,128)(2,1)S(1)}, bf16[128,1792]{1,0:T(8,128)(2,1)S(1)}, u32[]{:S(2)}, u32[]{:S(2)}) collective-permute-start(bf16[128,1792]{1,0:T(8,128)(2,1)S(1)} %collective-permute-done.15.refs_13_), channel_id=1, source_target_pairs={{0,16},{1,17},{2,18},{3,19},{4,20},{5,21},{6,22},{7,23},{8,24},{9,... | collective-permute-start | bytes 1376264 | tf_op jit(solution)/shard_map/ppermute | solution.py:33
  54.5 6.8 %collective-permute-start.4 = (bf16[256,512]{1,0:T(8,128)(2,1)S(1)}, bf16[256,512]{1,0:T(8,128)(2,1)S(1)}, u32[]{:S(2)}, u32[]{:S(2)}) collective-permute-start(bf16[256,512]{1,0:T(8,128)(2,1)S(1)} %attend.3.refs_1_), channel_id=1, source_target_pairs={{0,1},{1,0},{2,3},{3,2},{4,5},{5,4},{6,7},{7,6},{8,9},{9,8},{10,11... | collective-permute-start | bytes 786440 | tf_op jit(solution)/shard_map/ppermute | solution.py:33
  54.6 7.3 %collective-permute-start.5 = (bf16[256,512]{1,0:T(8,128)(2,1)S(1)}, bf16[256,512]{1,0:T(8,128)(2,1)S(1)}, u32[]{:S(2)}, u32[]{:S(2)}) collective-permute-start(bf16[256,512]{1,0:T(8,128)(2,1)S(1)} %collective-permute-done.3.refs_2_), channel_id=1, source_target_pairs={{0,129},{1,128},{2,131},{3,130},{4,133},{5,132},{6,135},{7,134},{8... | collective-permute-start | bytes 786440 | tf_op jit(solution)/shard_map/ppermute | solution.py:33
  56.7 9.6 %collective-permute-start.7 = (bf16[256,512]{1,0:T(8,128)(2,1)S(1)}, bf16[256,512]{1,0:T(8,128)(2,1)S(1)}, u32[]{:S(2)}, u32[]{:S(2)}) collective-permute-start(bf16[256,512]{1,0:T(8,128)(2,1)S(1)} %collective-permute-done.6.refs_7_), channel_id=1, source_target_pairs={{0,1},{1,0},{2,3},{3,2},{4,5},{5,4},{6,7},{7,6},{8,9},{9,8},{10,11... | collective-permute-start | bytes 786440 | tf_op jit(solution)/shard_map/ppermute | solution.py:33
  57.9 8.3 %collective-permute-start.18 = (bf16[64,1792]{1,0:T(8,128)(2,1)S(1)}, bf16[64,1792]{1,0:T(8,128)(2,1)S(1)}, u32[]{:S(2)}, u32[]{:S(2)}) collective-permute-start(bf16[64,1792]{1,0:T(8,128)(2,1)S(1)} %collective-permute-done.17.refs_17_), channel_id=1, source_target_pairs={{0,112},{1,113},{2,114},{3,115},{4,116},{5,117},{6,118},{7,119},{8... | collective-permute-start | bytes 688136 | tf_op jit(solution)/shard_map/ppermute | solution.py:33
  68.6 5.5 %collective-permute-start.19 = (bf16[3,256,896]{2,1,0:T(8,128)(2,1)S(1)}, bf16[3,256,896]{2,1,0:T(8,128)(2,1)S(1)}, u32[]{:S(2)}, u32[]{:S(2)}) collective-permute-start(bf16[3,256,896]{2,1,0:T(8,128)(2,1)S(1)} %get-tuple-element.34), channel_id=1, source_target_pairs={{0,2},{1,3},{2,0},{3,1},{4,6},{5,7},{6,4},{7,5},{8,10},{9,11},{10,... | collective-permute-start | bytes 4128776 | tf_op jit(solution)/shard_map/ppermute | solution.py:33
  71.3 3.4 %collective-permute-start.20 = (bf16[256,896]{1,0:T(8,128)(2,1)S(1)}, bf16[256,896]{1,0:T(8,128)(2,1)S(1)}, u32[]{:S(2)}, u32[]{:S(2)}) collective-permute-start(bf16[256,896]{1,0:T(8,128)(2,1)S(1)} %get-tuple-element.35), channel_id=1, source_target_pairs={{0,2},{1,3},{2,0},{3,1},{4,6},{5,7},{6,4},{7,5},{8,10},{9,11},{10,... | collective-permute-start | bytes 1376264 | tf_op jit(solution)/shard_map/ppermute | solution.py:33
  74.8 7.1 %collective-permute-start.21 = (bf16[128,896]{1,0:T(8,128)(2,1)S(1)}, bf16[128,896]{1,0:T(8,128)(2,1)S(1)}, u32[]{:S(2)}, u32[]{:S(2)}) collective-permute-start(bf16[128,896]{1,0:T(8,128)(2,1)S(1)} %fusion.10), channel_id=1, source_target_pairs={{0,12},{1,13},{2,14},{3,15},{4,0},{5,1},{6,2},{7,3},{8,4},{9,5},{1... | collective-permute-start | bytes 688136 | tf_op jit(solution)/shard_map/ppermute | solution.py:33
  77.2 7.7 %collective-permute-start.25 = (bf16[128,896]{1,0:T(8,128)(2,1)S(1)}, bf16[128,896]{1,0:T(8,128)(2,1)S(1)}, u32[]{:S(2)}, u32[]{:S(2)}) collective-permute-start(bf16[128,896]{1,0:T(8,128)(2,1)S(1)} %fusion.9), channel_id=1, source_target_pairs={{0,4},{1,5},{2,6},{3,7},{4,8},{5,9},{6,10},{7,11},{8,12},{9,13},{1... | collective-permute-start | bytes 688136 | tf_op jit(solution)/shard_map/ppermute | solution.py:33
  77.4 14.1 %collective-permute-start.27 = (bf16[128,896]{1,0:T(8,128)(2,1)S(1)}, bf16[128,896]{1,0:T(8,128)(2,1)S(1)}, u32[]{:S(2)}, u32[]{:S(2)}) collective-permute-start(bf16[128,896]{1,0:T(8,128)(2,1)S(1)} %get-tuple-element.48), channel_id=1, source_target_pairs={{0,12},{1,13},{2,14},{3,15},{4,0},{5,1},{6,2},{7,3},{8,4},{9,5},{1... | collective-permute-start | bytes 688136 | tf_op jit(solution)/shard_map/ppermute | solution.py:33
  80.1 12.9 %collective-permute-start.23 = (bf16[128,896]{1,0:T(8,128)(2,1)S(1)}, bf16[128,896]{1,0:T(8,128)(2,1)S(1)}, u32[]{:S(2)}, u32[]{:S(2)}) collective-permute-start(bf16[128,896]{1,0:T(8,128)(2,1)S(1)} %get-tuple-element.49), channel_id=1, source_target_pairs={{0,4},{1,5},{2,6},{3,7},{4,8},{5,9},{6,10},{7,11},{8,12},{9,13},{1... | collective-permute-start | bytes 688136 | tf_op jit(solution)/shard_map/ppermute | solution.py:33
  85.0 10.9 %collective-permute-start.26 = (bf16[128,896]{1,0:T(8,128)(2,1)S(1)}, bf16[128,896]{1,0:T(8,128)(2,1)S(1)}, u32[]{:S(2)}, u32[]{:S(2)}) collective-permute-start(bf16[128,896]{1,0:T(8,128)(2,1)S(1)} %get-tuple-element.46), channel_id=1, source_target_pairs={{0,1},{1,0},{2,129},{3,128},{4,5},{5,4},{6,133},{7,132},{8,9},{9,8... | collective-permute-start | bytes 688136 | tf_op jit(solution)/shard_map/ppermute | solution.py:33
  89.6 10.0 %collective-permute-start.22 = (bf16[128,896]{1,0:T(8,128)(2,1)S(1)}, bf16[128,896]{1,0:T(8,128)(2,1)S(1)}, u32[]{:S(2)}, u32[]{:S(2)}) collective-permute-start(bf16[128,896]{1,0:T(8,128)(2,1)S(1)} %get-tuple-element.47), channel_id=1, source_target_pairs={{0,0},{1,1},{2,128},{3,129},{4,4},{5,5},{6,132},{7,133},{8,8},{9,9... | collective-permute-start | bytes 688136 | tf_op jit(solution)/shard_map/ppermute | solution.py:33
  91.6 9.2 %collective-permute-start.28 = (bf16[128,896]{1,0:T(8,128)(2,1)S(1)}, bf16[128,896]{1,0:T(8,128)(2,1)S(1)}, u32[]{:S(2)}, u32[]{:S(2)}) collective-permute-start(bf16[128,896]{1,0:T(8,128)(2,1)S(1)} %fusion.2), channel_id=1, source_target_pairs={{0,13},{1,12},{2,141},{3,140},{4,1},{5,0},{6,129},{7,128},{8,5},{9... | collective-permute-start | bytes 688136 | tf_op jit(solution)/shard_map/ppermute | solution.py:33
  93.1 10.5 %collective-permute-start.24 = (bf16[128,896]{1,0:T(8,128)(2,1)S(1)}, bf16[128,896]{1,0:T(8,128)(2,1)S(1)}, u32[]{:S(2)}, u32[]{:S(2)}) collective-permute-start(bf16[128,896]{1,0:T(8,128)(2,1)S(1)} %fusion.6), channel_id=1, source_target_pairs={{0,4},{1,5},{2,132},{3,133},{4,8},{5,9},{6,136},{7,137},{8,12},{9,... | collective-permute-start | bytes 688136 | tf_op jit(solution)/shard_map/ppermute | solution.py:33

commit v12 on v11

--- a/solution.py
+++ b/solution.py
@@ -2,6 +2,7 @@
 
 import jax
 import jax.numpy as jnp
+import numpy as np
 from jax import lax
 from jax.experimental import pallas as pl
 from jax.experimental.pallas import tpu as pltpu
@@ -138,41 +139,44 @@
         keys[:576, :256] = raw[:, 256:512]
 
 
-def attend_kernel(group, queries, keys, hidden, w_value_up, reorder, out):
+def attend_kernel(queries, queries_next, keys, hidden, w_value_up, reorder, out):
     scale = 192.0**-0.5 * 1.4426950408889634
-    heads = []
-    for pair in range(2):
-        scores = jnp.dot(
-            queries[512 * pair : 512 * pair + 512, :], keys[...], preferred_element_type=F32
-        )
-        for i in range(2):
-            part = scores[256 * i : 256 * i + 256] * scale + hidden[...]
-            top = jnp.max(part, axis=1, keepdims=True)
-            powers = jnp.exp2(part - top)
-            share = 1.0 / jnp.sum(powers, axis=1, keepdims=True)
-            mixed = lax.dot_general(
-                powers.astype(BF),
-                keys[:512, :],
-                (((1,), (1,)), ((), ())),
-                preferred_element_type=F32,
+    for group, held in enumerate((queries, queries_next)):
+        heads = []
+        for pair in range(2):
+            scores = jnp.dot(
+                held[512 * pair : 512 * pair + 512, :], keys[...], preferred_element_type=F32
             )
-            attention = jnp.dot(
-                (mixed * share).astype(BF),
-                w_value_up[4 * group + 2 * pair + i],
-                preferred_element_type=F32,
-            )
-            heads.append(attention.astype(BF))
-    rows = jnp.concatenate(heads, 1)
-    out[...] = jnp.dot(rows, reorder[...], preferred_element_type=F32).astype(BF)
+            for i in range(2):
+                part = scores[256 * i : 256 * i + 256] * scale + hidden[...]
+                top = jnp.max(part, axis=1, keepdims=True)
+                powers = jnp.exp2(part - top)
+                share = 1.0 / jnp.sum(powers, axis=1, keepdims=True)
+                mixed = lax.dot_general(
+                    powers.astype(BF),
+                    keys[:512, :],
+                    (((1,), (1,)), ((), ())),
+                    preferred_element_type=F32,
+                )
+                attention = jnp.dot(
+                    (mixed * share).astype(BF),
+                    w_value_up[4 * group + 2 * pair + i],
+                    preferred_element_type=F32,
+                )
+                heads.append(attention.astype(BF))
+        rows = jnp.concatenate(heads, 1)
+        out[:, 512 * group : 512 * group + 512] = jnp.dot(
+            rows, reorder[...], preferred_element_type=F32
+        ).astype(BF)
 
 
 def turns(first):
-    inverse = jnp.power(jnp.float32(10000.0), -jnp.arange(32, dtype=F32) * (2.0 / 64))
-    row = lax.broadcasted_iota(jnp.int32, (64, 128), 0)
-    lane = lax.broadcasted_iota(jnp.int32, (64, 128), 1)
-    own = (first + (lane // 32) * 64 + row).astype(F32) * jnp.tile(inverse, 4)[None, :]
-    place = first - 512 + lax.broadcasted_iota(jnp.int32, (32, 768), 1)
-    every = place.astype(F32) * inverse[:, None]
+    inverse = (10000.0 ** (-np.arange(32) * (2.0 / 64))).astype(np.float32)
+    lane = np.arange(128)[None, :]
+    place = (np.arange(64)[:, None] + (lane // 32) * 64).astype(np.float32)
+    start = first.astype(F32)
+    own = (start + place) * np.tile(inverse, 4)[None, :]
+    every = (start - 512 + np.arange(768, dtype=np.float32)[None, :]) * inverse[:, None]
     return jnp.cos(own), jnp.sin(own), jnp.cos(every), jnp.sin(every)
 
 
@@ -190,7 +194,7 @@
 
 
 def project_kernel(theirs, *refs):
-    groups, held, outs, (rows, total) = refs[:8], refs[8:19], refs[19:-2], refs[-2:]
+    groups, held, outs, (rows, total) = refs[:5], refs[5:16], refs[16:-2], refs[-2:]
     own, d1, d2, d3, u4, u3, u2, u1, other, e3, e4 = held
     blocks = [own, d1, *(both.at[:64] for both in (d2, d3, u4, u3, u2)), u1]
     blocks += [other, d2.at[64:], d3.at[64:], e3, e4, *(both.at[64:] for both in (u4, u3, u2))]
@@ -200,13 +204,14 @@
 
         @pl.when(first == pick)
         def _():
-            for g in range(2):
-                for j in range(2):
+            at = 0
+            for part in groups[2:] if pick else groups[:2]:
+                for g in range(2):
                     for p in range(2):
-                        half = pl.ds(pl.multiple_of(256 * (yh ^ p), 256), 256)
-                        rows[256 * j : 256 * j + 256, 512 * g + 256 * p : 512 * g + 256 * p + 256] = (
-                            groups[2 * (pick + j) + g][:, half]
-                        )
+                        half = pl.ds(pl.multiple_of(512 * g + 256 * (yh ^ p), 256), 256)
+                        to = 512 * g + 256 * p
+                        rows[at : at + part.shape[0], to : to + 256] = part[:, half]
+                at += part.shape[0]
 
     for n in range(7):
         columns = slice(256 * n, 256 * n + 256)
@@ -282,7 +287,7 @@
     return call(
         functools.partial(project_kernel, theirs),
         [array((256, 896), kind), array((3, 256, 896), kind)],
-        whole(19),
+        whole(16),
         (*groups, *blocks),
         "project",
         2 * 512 * 1024 * 1792,
@@ -340,24 +345,19 @@
         (column // 8 % 4) * 128 + (column // 256) * 64 + ((z + column // 32) % 8) * 8 + column % 8
     )
     reorder = (column[:, None] == source[None, :]).astype(BF)
-    rows = [
-        call(
-            functools.partial(attend_kernel, g),
-            array((256, 512)),
-            whole(5),
-            (queries[g], keys, hidden, w_value_up, reorder),
-            "attend",
-            2 * 1024 * 768 * 1152 + 2 * 1024 * 512 * 128,
-            5 << 20,
-            14,
-        )
-        for g in range(2)
-    ]
-    one = [xor_y(part, 1) for part in rows]
-    three = [xor_y(part, 3) for part in rows]
-    two = [xor_y(one[0], 3), xor_y(three[1], 1)]
-    groups = [*rows, *one, *two, *three]
-    u3, d3 = up_z(after(u2, *rows)), down_z(after(d2, *rows))
+    rows = call(
+        attend_kernel,
+        array((256, 1024)),
+        whole(6),
+        (*queries, keys, hidden, w_value_up, reorder),
+        "attend",
+        4 * 1024 * 768 * 1152 + 4 * 1024 * 512 * 128,
+        10 << 20,
+        16,
+    )
+    one, three = xor_y(rows, 1), xor_y(rows, 3)
+    groups = [rows, one, xor_y(one[:128], 3), xor_y(three[128:], 1), three]
+    u3, d3 = up_z(after(u2, rows)), down_z(after(d2, rows))
     u4 = up_z(u3)
     e3 = down_z(d3[64:])
     e4 = down_z(e3)

time: 105 us -> 105 us (level)
  starting transfers between devices: 50.5 us -> 48.4 us
  waiting for transfers between devices: 27.2 us -> 29.1 us
    ppermute x27 -> x25, starting transfers between devices: 41.2 us -> 39.1 us  [moved(): return lax.ppermute(a, AXES, pairs)]
    ppermute x27 -> x25, waiting for transfers between devices: 27.2 us -> 29.1 us  [moved(): return lax.ppermute(a, AXES, pairs)]
    pallas_call x6 -> x5, Pallas kernels: 19.6 us -> 19.5 us  [call(): pl.pallas_call(kernel, out_shape=shapes, in_specs=specs, out_specs=whole(...]
  transfers between devices with their start and end apart: 29 -> 27, of which waited for: 12 -> 15; matrix products, arithmetic and copies ran while one was open for 2% -> 2% of each run, Pallas kernels for 19% -> 18%
where the time goes in v12:
time: 105 us
  starting transfers between devices  48.4 us (46%)
  waiting for transfers between devices  29.1 us (28%)
  Pallas kernels  21.7 us (21%)
  other arithmetic  2.99 us (3%)
  local copies, waits for them, and re-layouts  1.99 us (2%)
    ppermute x25, starting transfers between devices, moved(): return lax.ppermute(a, AXES, pairs)  39.1 us
    ppermute x25, waiting for transfers between devices, moved(): return lax.ppermute(a, AXES, pairs)  29.1 us
    pallas_call x5, Pallas kernels, call(): pl.pallas_call(kernel, out_shape=shapes, in_specs=specs, out_specs=whole(...  19.5 us
    ppermute x2, starting transfers between devices, local(): lax.ppermute(half, CTX, [(i, i + by) for i in range(16 - by)])  9.27 us
    pallas_call x1, Pallas kernels, quarters(): pl.pallas_call(quarter_kernel, out_shape=[jax.ShapeDtypeStruct((64, 1792)...  2.22 us
  transfers between devices with their start and end apart: 27, of which 15 were waited for; matrix products, arithmetic and copies ran while one was open for 2% of the time, Pallas kernels for 18%

profile of v12, /device:TPU:1, one launch (start us, length us, event | category | flops | bytes accessed | tf_op | source)
XLA Modules:
  0.0 105.2 jit_solution(13119112124719446517)
XLA Ops:
  0.0 1.6 %dynamic-slice_bitcast_fusion = bf16[576,128]{1,0:T(8,128)(2,1)} fusion(bf16[256,576]{0,1:T(8,128)(2,1)} %param.13, s32[]{:T(128)S(6)} %select_n.66), kind=kLoop, calls=%fused_computation.30 | loop fusion | bytes 294916 | tf_op jit(solution)/shard_map/dynamic_slice | solution.py:308
  1.6 5.7 %collective-permute-start.1 = (bf16[576,128]{1,0:T(8,128)(2,1)}, bf16[576,128]{1,0:T(8,128)(2,1)S(1)}, u32[]{:S(2)}, u32[]{:S(2)}) collective-permute-start(bf16[576,128]{1,0:T(8,128)(2,1)} %dynamic-slice_bitcast_fusion), channel_id=1, source_target_pairs={{0,32},{16,48},{32,64},{48,80},{64,96},{80,112},{96,128},{112,144}... | collective-permute-start | bytes 442376 | tf_op jit(solution)/shard_map/ppermute | solution.py:310
  7.3 3.5 %collective-permute-start = (bf16[576,128]{1,0:T(8,128)(2,1)}, bf16[576,128]{1,0:T(8,128)(2,1)S(1)}, u32[]{:S(2)}, u32[]{:S(2)}) collective-permute-start(bf16[576,128]{1,0:T(8,128)(2,1)} %dynamic-slice_bitcast_fusion), channel_id=1, source_target_pairs={{0,16},{16,32},{32,48},{48,64},{64,80},{80,96},{96,112},{112,128},... | collective-permute-start | bytes 442376 | tf_op jit(solution)/shard_map/ppermute | solution.py:310
  10.9 2.2 %quarters.1 = (bf16[64,1792]{1,0:T(8,128)(2,1)}, bf16[64,1792]{1,0:T(8,128)(2,1)}) custom-call(bf16[64,7168]{1,0:T(8,128)(2,1)} %bitcast.35), custom_call_target="tpu_custom_call" | custom-call | bytes 2097152 | tf_op jit(solution)/shard_map/quarters/pallas_call | solution.py:252
  13.1 2.8 %collective-permute-start.11 = (bf16[64,1792]{1,0:T(8,128)(2,1)}, bf16[64,1792]{1,0:T(8,128)(2,1)S(1)}, u32[]{:S(2)}, u32[]{:S(2)}) collective-permute-start(bf16[64,1792]{1,0:T(8,128)(2,1)} %get-tuple-element.27.refs_5_), channel_id=1, source_target_pairs={{0,16},{1,17},{2,18},{3,19},{4,20},{5,21},{6,22},{7,23},{8,24},{9,... | collective-permute-start | bytes 688136 | tf_op jit(solution)/shard_map/ppermute | solution.py:34
  15.9 0.8 collective-permute-start.7
  16.8 1.9 %collective-permute-start.8 = (bf16[64,1792]{1,0:T(8,128)(2,1)}, bf16[64,1792]{1,0:T(8,128)(2,1)S(1)}, u32[]{:S(2)}, u32[]{:S(2)}) collective-permute-start(bf16[64,1792]{1,0:T(8,128)(2,1)} %get-tuple-element.28), channel_id=1, source_target_pairs={{0,129},{1,128},{2,131},{3,130},{4,133},{5,132},{6,135},{7,134},{8... | collective-permute-start | bytes 688136 | tf_op jit(solution)/shard_map/ppermute | solution.py:34
  18.7 0.1 fusion.reorder
  18.9 0.8 fusion.11
  19.6 6.9 %queries.1 = (bf16[1024,640]{1,0:T(8,128)(2,1)}, bf16[1024,640]{1,0:T(8,128)(2,1)}) custom-call(bf16[256,1536]{1,0:T(8,128)(2,1)} %rows.1, bf16[1536,1536]{1,0:T(8,128)(2,1)} %w_query.1, bf16[8,128,512]{2,1,0:T(8,128)(2,1)} %w_key_up.1, f32[64,128]{1,0:T(8,128)} %get-tuple-element.57.cosines, f32[64,128]{1,0:T(8,128)} %get-tuple-element.56.sines), custom_call_target="tpu_custom_call" | custom-call | flops 1476395008 | bytes 8388608 | tf_op jit(solution)/shard_map/queries/pallas_call | solution.py:264
  26.7 2.0 %collective-permute-start.2 = (bf16[576,256]{1,0:T(8,128)(2,1)S(1)}, bf16[576,256]{1,0:T(8,128)(2,1)S(1)}, u32[]{:S(2)}, u32[]{:S(2)}) collective-permute-start(bf16[576,256]{1,0:T(8,128)(2,1)S(1)} %pad_maximum_fusion.2), channel_id=1, source_target_pairs={{0,2},{1,3},{2,0},{3,1},{4,6},{5,7},{6,4},{7,5},{8,10},{9,11},{10,... | collective-permute-start | bytes 884744 | tf_op jit(solution)/shard_map/ppermute | solution.py:34
  28.9 1.7 %collective-permute-start.12 = (bf16[128,1792]{1,0:T(8,128)(2,1)S(1)}, bf16[128,1792]{1,0:T(8,128)(2,1)S(1)}, u32[]{:S(2)}, u32[]{:S(2)}) collective-permute-start(bf16[128,1792]{1,0:T(8,128)(2,1)S(1)} %get-tuple-element.31), channel_id=1, source_target_pairs={{0,16},{1,17},{2,18},{3,19},{4,20},{5,21},{6,22},{7,23},{8,24},{9,... | collective-permute-start | bytes 1376264 | tf_op jit(solution)/shard_map/ppermute | solution.py:34
  30.6 0.4 multiply_sine_fusion
  31.7 0.6 keys.1
  32.3 7.4 %attend.1.refs_0_ = bf16[256,1024]{1,0:T(8,128)(2,1)S(1)} custom-call(bf16[1024,640]{1,0:T(8,128)(2,1)S(1)} %copy-done.2, bf16[1024,640]{1,0:T(8,128)(2,1)S(1)} %copy-done.3, bf16[640,768]{1,0:T(8,128)(2,1)S(1)} %get-tuple-element.25.keys, f32[256,768]{1,0:T(8,128)S(1)} %get-tuple-element.26.hidden, bf16[8,512,128]{2,1,0:T(8,128)(2,1)S(1)} %copy-done.4, ...), custom_call_target="tpu_custom_call" | custom-call | flops 3892314112 | bytes 10485760 | tf_op jit(solution)/shard_map/attend/pallas_call | solution.py:264
  39.7 1.5 %collective-permute-done.9.refs_7_ = bf16[128,1792]{1,0:T(8,128)(2,1)S(1)} collective-permute-done((bf16[128,1792]{1,0:T(8,128)(2,1)S(1)}, bf16[128,1792]{1,0:T(8,128)(2,1)S(1)}, u32[]{:S(2)}, u32[]{:S(2)}) %collective-permute-start.9) | collective-permute-done | bytes 458784 | tf_op jit(solution)/shard_map/ppermute | solution.py:34
  41.2 1.1 %collective-permute-start.10 = (bf16[128,1792]{1,0:T(8,128)(2,1)S(1)}, bf16[128,1792]{1,0:T(8,128)(2,1)S(1)}, u32[]{:S(2)}, u32[]{:S(2)}) collective-permute-start(bf16[128,1792]{1,0:T(8,128)(2,1)S(1)} %collective-permute-done.9.refs_7_), channel_id=1, source_target_pairs={{0,112},{1,113},{2,114},{3,115},{4,116},{5,117},{6,118},{7,119},{8... | collective-permute-start | bytes 1376264 | tf_op jit(solution)/shard_map/ppermute | solution.py:34
  42.4 0.3 collective-permute-start.13
  42.7 1.9 %collective-permute-start.5 = (bf16[256,1024]{1,0:T(8,128)(2,1)S(1)}, bf16[256,1024]{1,0:T(8,128)(2,1)S(1)}, u32[]{:S(2)}, u32[]{:S(2)}) collective-permute-start(bf16[256,1024]{1,0:T(8,128)(2,1)S(1)} %attend.1.refs_0_), channel_id=1, source_target_pairs={{0,129},{1,128},{2,131},{3,130},{4,133},{5,132},{6,135},{7,134},{8... | collective-permute-start | bytes 1572872 | tf_op jit(solution)/shard_map/ppermute | solution.py:34
  44.6 8.0 %collective-permute-done.10.refs_8_ = bf16[128,1792]{1,0:T(8,128)(2,1)S(1)} collective-permute-done((bf16[128,1792]{1,0:T(8,128)(2,1)S(1)}, bf16[128,1792]{1,0:T(8,128)(2,1)S(1)}, u32[]{:S(2)}, u32[]{:S(2)}) %collective-permute-start.10) | collective-permute-done | bytes 458784 | tf_op jit(solution)/shard_map/ppermute | solution.py:34
  52.6 2.6 %collective-permute-start.15 = (bf16[64,1792]{1,0:T(8,128)(2,1)S(1)}, bf16[64,1792]{1,0:T(8,128)(2,1)S(1)}, u32[]{:S(2)}, u32[]{:S(2)}) collective-permute-start(bf16[64,1792]{1,0:T(8,128)(2,1)S(1)} %slice.106), channel_id=1, source_target_pairs={{0,112},{1,113},{2,114},{3,115},{4,116},{5,117},{6,118},{7,119},{8... | collective-permute-start | bytes 688136 | tf_op jit(solution)/shard_map/ppermute | solution.py:34
  55.2 0.9 collective-permute-done.5.refs_4_
  56.2 0.4 collective-permute-done.3.refs_1_
  56.6 1.7 %collective-permute-start.4 = (bf16[128,1024]{1,0:T(8,128)(2,1)S(1)}, bf16[128,1024]{1,0:T(8,128)(2,1)S(1)}, u32[]{:S(2)}, u32[]{:S(2)}) collective-permute-start(bf16[128,1024]{1,0:T(8,128)(2,1)S(1)} %slice.104), channel_id=1, source_target_pairs={{0,129},{1,128},{2,131},{3,130},{4,133},{5,132},{6,135},{7,134},{8... | collective-permute-start | bytes 786440 | tf_op jit(solution)/shard_map/ppermute | solution.py:34
  58.4 0.2 collective-permute-done.15.refs_14_
  58.6 3.4 %collective-permute-start.16 = (bf16[64,1792]{1,0:T(8,128)(2,1)S(1)}, bf16[64,1792]{1,0:T(8,128)(2,1)S(1)}, u32[]{:S(2)}, u32[]{:S(2)}) collective-permute-start(bf16[64,1792]{1,0:T(8,128)(2,1)S(1)} %collective-permute-done.15.refs_14_), channel_id=1, source_target_pairs={{0,112},{1,113},{2,114},{3,115},{4,116},{5,117},{6,118},{7,119},{8... | collective-permute-start | bytes 688136 | tf_op jit(solution)/shard_map/ppermute | solution.py:34
  62.0 1.5 %collective-permute-done.4.refs_2_ = bf16[128,1024]{1,0:T(8,128)(2,1)S(1)} collective-permute-done((bf16[128,1024]{1,0:T(8,128)(2,1)S(1)}, bf16[128,1024]{1,0:T(8,128)(2,1)S(1)}, u32[]{:S(2)}, u32[]{:S(2)}) %collective-permute-start.4) | collective-permute-done | bytes 262176 | tf_op jit(solution)/shard_map/ppermute | solution.py:34
  63.5 1.5 %collective-permute-done.16.refs_15_ = bf16[64,1792]{1,0:T(8,128)(2,1)S(1)} collective-permute-done((bf16[64,1792]{1,0:T(8,128)(2,1)S(1)}, bf16[64,1792]{1,0:T(8,128)(2,1)S(1)}, u32[]{:S(2)}, u32[]{:S(2)}) %collective-permute-start.16) | collective-permute-done | bytes 229408 | tf_op jit(solution)/shard_map/ppermute | solution.py:34
  65.0 1.7 %collective-permute-done.14.refs_9_ = bf16[128,1792]{1,0:T(8,128)(2,1)S(1)} collective-permute-done((bf16[128,1792]{1,0:T(8,128)(2,1)S(1)}, bf16[128,1792]{1,0:T(8,128)(2,1)S(1)}, u32[]{:S(2)}, u32[]{:S(2)}) %collective-permute-start.14) | collective-permute-done | bytes 458784 | tf_op jit(solution)/shard_map/ppermute | solution.py:34
  66.6 2.3 %project.3 = (bf16[256,896]{1,0:T(8,128)(2,1)S(1)}, bf16[3,256,896]{2,1,0:T(8,128)(2,1)S(1)}) custom-call(bf16[256,1024]{1,0:T(8,128)(2,1)S(1)} %attend.1.refs_0_, bf16[256,1024]{1,0:T(8,128)(2,1)S(1)} %collective-permute-done.3.refs_1_, bf16[128,1024]{1,0:T(8,128)(2,1)S(1)} %collective-permute-done.4.refs_2_, ...), custom_call_target="tpu_custom_call" | custom-call | flops 1879048192 | bytes 8388608 | tf_op jit(solution)/shard_map/project/pallas_call | solution.py:264
  68.9 2.8 %collective-permute-start.17 = (bf16[3,256,896]{2,1,0:T(8,128)(2,1)S(1)}, bf16[3,256,896]{2,1,0:T(8,128)(2,1)S(1)}, u32[]{:S(2)}, u32[]{:S(2)}) collective-permute-start(bf16[3,256,896]{2,1,0:T(8,128)(2,1)S(1)} %get-tuple-element.34), channel_id=1, source_target_pairs={{0,2},{1,3},{2,0},{3,1},{4,6},{5,7},{6,4},{7,5},{8,10},{9,11},{10,... | collective-permute-start | bytes 4128776 | tf_op jit(solution)/shard_map/ppermute | solution.py:34
  71.8 2.3 %project.2 = (f32[256,896]{1,0:T(8,128)S(1)}, f32[3,256,896]{2,1,0:T(8,128)S(1)}) custom-call(bf16[256,1024]{1,0:T(8,128)(2,1)S(1)} %attend.1.refs_0_, bf16[256,1024]{1,0:T(8,128)(2,1)S(1)} %collective-permute-done.3.refs_1_, bf16[128,1024]{1,0:T(8,128)(2,1)S(1)} %collective-permute-done.4.refs_2_, bf16[128,1024]{1,0:T(8,128)(2,1)S(1)} %collective-permute-done.6.refs_3_, ...), custom_call_target="tpu_custom_call" | custom-call | flops 1879048192 | bytes 8388608 | tf_op jit(solution)/shard_map/project/pallas_call | solution.py:264
  74.1 0.3 collective-permute-done.17
  74.4 0.2 convert_add_fusion.2
  74.7 0.4 collective-permute-done.18
  75.1 2.5 %collective-permute-start.19 = (bf16[128,896]{1,0:T(8,128)(2,1)S(1)}, bf16[128,896]{1,0:T(8,128)(2,1)S(1)}, u32[]{:S(2)}, u32[]{:S(2)}) collective-permute-start(bf16[128,896]{1,0:T(8,128)(2,1)S(1)} %get-tuple-element.37), channel_id=1, source_target_pairs={{0,12},{1,13},{2,14},{3,15},{4,0},{5,1},{6,2},{7,3},{8,4},{9,5},{1... | collective-permute-start | bytes 688136 | tf_op jit(solution)/shard_map/ppermute | solution.py:34
  77.7 2.8 %collective-permute-start.25 = (bf16[128,896]{1,0:T(8,128)(2,1)S(1)}, bf16[128,896]{1,0:T(8,128)(2,1)S(1)}, u32[]{:S(2)}, u32[]{:S(2)}) collective-permute-start(bf16[128,896]{1,0:T(8,128)(2,1)S(1)} %get-tuple-element.48), channel_id=1, source_target_pairs={{0,12},{1,13},{2,14},{3,15},{4,0},{5,1},{6,2},{7,3},{8,4},{9,5},{1... | collective-permute-start | bytes 688136 | tf_op jit(solution)/shard_map/ppermute | solution.py:34
  80.5 1.7 %collective-permute-done.19 = bf16[128,896]{1,0:T(8,128)(2,1)S(1)} collective-permute-done((bf16[128,896]{1,0:T(8,128)(2,1)S(1)}, bf16[128,896]{1,0:T(8,128)(2,1)S(1)}, u32[]{:S(2)}, u32[]{:S(2)}) %collective-permute-start.19) | collective-permute-done | bytes 229408 | tf_op jit(solution)/shard_map/ppermute | solution.py:34
  82.2 3.1 %collective-permute-done.23 = bf16[128,896]{1,0:T(8,128)(2,1)S(1)} collective-permute-done((bf16[128,896]{1,0:T(8,128)(2,1)S(1)}, bf16[128,896]{1,0:T(8,128)(2,1)S(1)}, u32[]{:S(2)}, u32[]{:S(2)}) %collective-permute-start.23) | collective-permute-done | bytes 229408 | tf_op jit(solution)/shard_map/ppermute | solution.py:34
  85.4 4.6 %collective-permute-start.24 = (bf16[128,896]{1,0:T(8,128)(2,1)S(1)}, bf16[128,896]{1,0:T(8,128)(2,1)S(1)}, u32[]{:S(2)}, u32[]{:S(2)}) collective-permute-start(bf16[128,896]{1,0:T(8,128)(2,1)S(1)} %get-tuple-element.46), channel_id=1, source_target_pairs={{0,1},{1,0},{2,129},{3,128},{4,5},{5,4},{6,133},{7,132},{8,9},{9,8... | collective-permute-start | bytes 688136 | tf_op jit(solution)/shard_map/ppermute | solution.py:34
  89.9 1.9 %collective-permute-start.20 = (bf16[128,896]{1,0:T(8,128)(2,1)S(1)}, bf16[128,896]{1,0:T(8,128)(2,1)S(1)}, u32[]{:S(2)}, u32[]{:S(2)}) collective-permute-start(bf16[128,896]{1,0:T(8,128)(2,1)S(1)} %get-tuple-element.47), channel_id=1, source_target_pairs={{0,0},{1,1},{2,128},{3,129},{4,4},{5,5},{6,132},{7,133},{8,8},{9,9... | collective-permute-start | bytes 688136 | tf_op jit(solution)/shard_map/ppermute | solution.py:34
  91.9 1.5 %collective-permute-start.26 = (bf16[128,896]{1,0:T(8,128)(2,1)S(1)}, bf16[128,896]{1,0:T(8,128)(2,1)S(1)}, u32[]{:S(2)}, u32[]{:S(2)}) collective-permute-start(bf16[128,896]{1,0:T(8,128)(2,1)S(1)} %fusion.2), channel_id=1, source_target_pairs={{0,13},{1,12},{2,141},{3,140},{4,1},{5,0},{6,129},{7,128},{8,5},{9... | collective-permute-start | bytes 688136 | tf_op jit(solution)/shard_map/ppermute | solution.py:34
  93.5 2.6 %collective-permute-start.22 = (bf16[128,896]{1,0:T(8,128)(2,1)S(1)}, bf16[128,896]{1,0:T(8,128)(2,1)S(1)}, u32[]{:S(2)}, u32[]{:S(2)}) collective-permute-start(bf16[128,896]{1,0:T(8,128)(2,1)S(1)} %fusion.6), channel_id=1, source_target_pairs={{0,4},{1,5},{2,132},{3,133},{4,8},{5,9},{6,136},{7,137},{8,12},{9,... | collective-permute-start | bytes 688136 | tf_op jit(solution)/shard_map/ppermute | solution.py:34
  96.1 4.0 %collective-permute-done.20 = bf16[128,896]{1,0:T(8,128)(2,1)S(1)} collective-permute-done((bf16[128,896]{1,0:T(8,128)(2,1)S(1)}, bf16[128,896]{1,0:T(8,128)(2,1)S(1)}, u32[]{:S(2)}, u32[]{:S(2)}) %collective-permute-start.20) | collective-permute-done | bytes 229408 | tf_op jit(solution)/shard_map/ppermute | solution.py:34
  100.0 1.0 collective-permute-done.26
  101.1 2.9 %collective-permute-done.22 = bf16[128,896]{1,0:T(8,128)(2,1)S(1)} collective-permute-done((bf16[128,896]{1,0:T(8,128)(2,1)S(1)}, bf16[128,896]{1,0:T(8,128)(2,1)S(1)}, u32[]{:S(2)}, u32[]{:S(2)}) %collective-permute-start.22) | collective-permute-done | bytes 229408 | tf_op jit(solution)/shard_map/ppermute | solution.py:34
  103.9 0.1 broadcast_select_fusion.1
  104.3 0.9 maximum_maximum_fusion
  (54 shorter events, 1.1 us)
Async XLA Ops:
  0.0 18.8 %copy-start.9 = (f32[128]{0:T(128)S(1)}, f32[128]{0:T(128)}, u32[]{:S(2)}) copy-start(f32[128]{0:T(128)} %constant.111) | copy-start | bytes 1540
  0.0 18.8 %copy-start.6 = (f32[64,128]{1,0:T(8,128)S(1)}, f32[64,128]{1,0:T(8,128)}, u32[]{:S(2)}) copy-start(f32[64,128]{1,0:T(8,128)} %constant.105.clone) | copy-start | bytes 98308
  1.6 25.0 %collective-permute-start.1 = (bf16[576,128]{1,0:T(8,128)(2,1)}, bf16[576,128]{1,0:T(8,128)(2,1)S(1)}, u32[]{:S(2)}, u32[]{:S(2)}) collective-permute-start(bf16[576,128]{1,0:T(8,128)(2,1)} %dynamic-slice_bitcast_fusion), channel_id=1, source_target_pairs={{0,32},{16,48},{32,64},{48,80},{64,96},{80,112},{96,128},{112,144}... | collective-permute-start | bytes 442376 | tf_op jit(solution)/shard_map/ppermute | solution.py:310
  7.3 19.3 %collective-permute-start = (bf16[576,128]{1,0:T(8,128)(2,1)}, bf16[576,128]{1,0:T(8,128)(2,1)S(1)}, u32[]{:S(2)}, u32[]{:S(2)}) collective-permute-start(bf16[576,128]{1,0:T(8,128)(2,1)} %dynamic-slice_bitcast_fusion), channel_id=1, source_target_pairs={{0,16},{16,32},{32,48},{48,64},{64,80},{80,96},{96,112},{112,128},... | collective-permute-start | bytes 442376 | tf_op jit(solution)/shard_map/ppermute | solution.py:310
  13.1 15.6 %collective-permute-start.11 = (bf16[64,1792]{1,0:T(8,128)(2,1)}, bf16[64,1792]{1,0:T(8,128)(2,1)S(1)}, u32[]{:S(2)}, u32[]{:S(2)}) collective-permute-start(bf16[64,1792]{1,0:T(8,128)(2,1)} %get-tuple-element.27.refs_5_), channel_id=1, source_target_pairs={{0,16},{1,17},{2,18},{3,19},{4,20},{5,21},{6,22},{7,23},{8,24},{9,... | collective-permute-start | bytes 688136 | tf_op jit(solution)/shard_map/ppermute | solution.py:34
  15.9 12.8 %collective-permute-start.7 = (bf16[64,1792]{1,0:T(8,128)(2,1)}, bf16[64,1792]{1,0:T(8,128)(2,1)S(1)}, u32[]{:S(2)}, u32[]{:S(2)}) collective-permute-start(bf16[64,1792]{1,0:T(8,128)(2,1)} %get-tuple-element.27.refs_5_), channel_id=1, source_target_pairs={{0,112},{1,113},{2,114},{3,115},{4,116},{5,117},{6,118},{7,119},{8... | collective-permute-start | bytes 688136 | tf_op jit(solution)/shard_map/ppermute | solution.py:34
  16.8 11.9 %collective-permute-start.8 = (bf16[64,1792]{1,0:T(8,128)(2,1)}, bf16[64,1792]{1,0:T(8,128)(2,1)S(1)}, u32[]{:S(2)}, u32[]{:S(2)}) collective-permute-start(bf16[64,1792]{1,0:T(8,128)(2,1)} %get-tuple-element.28), channel_id=1, source_target_pairs={{0,129},{1,128},{2,131},{3,130},{4,133},{5,132},{6,135},{7,134},{8... | collective-permute-start | bytes 688136 | tf_op jit(solution)/shard_map/ppermute | solution.py:34
  19.6 7.0 %copy-start.7 = (f32[1,768]{1,0:T(1,128)S(1)}, f32[1,768]{1,0:T(1,128)}, u32[]{:S(2)}) copy-start(f32[1,768]{1,0:T(1,128)} %constant.107.clone) | copy-start | bytes 9220
  19.6 12.7 %copy-start.4 = (bf16[8,512,128]{2,1,0:T(8,128)(2,1)S(1)}, bf16[8,512,128]{2,1,0:T(8,128)(2,1)}, u32[]{:S(2)}) copy-start(bf16[8,512,128]{2,1,0:T(8,128)(2,1)} %w_value_up.1) | copy-start | bytes 3145732
  26.5 4.0 %copy-start.8 = (f32[32]{0:T(128)S(1)}, f32[32]{0:T(128)}, u32[]{:S(2)}) copy-start(f32[32]{0:T(128)} %constant.112) | copy-start | bytes 388
  26.6 5.1 %copy-start = (bf16[256,576]{0,1:T(8,128)(2,1)S(1)}, bf16[256,576]{0,1:T(8,128)(2,1)}, u32[]{:S(2)}) copy-start(bf16[256,576]{0,1:T(8,128)(2,1)} %param.13) | copy-start | bytes 884740
  26.6 5.1 %copy-start.1 = (bf16[512,576]{0,1:T(8,128)(2,1)S(1)}, bf16[512,576]{0,1:T(8,128)(2,1)}, u32[]{:S(2)}) copy-start(bf16[512,576]{0,1:T(8,128)(2,1)} %param.14) | copy-start | bytes 1769476
  26.7 5.6 %copy-start.2 = (bf16[1024,640]{1,0:T(8,128)(2,1)S(1)}, bf16[1024,640]{1,0:T(8,128)(2,1)}, u32[]{:S(2)}) copy-start(bf16[1024,640]{1,0:T(8,128)(2,1)} %get-tuple-element.23.queries) | copy-start | bytes 3932164
  26.7 5.6 %copy-start.3 = (bf16[1024,640]{1,0:T(8,128)(2,1)S(1)}, bf16[1024,640]{1,0:T(8,128)(2,1)}, u32[]{:S(2)}) copy-start(bf16[1024,640]{1,0:T(8,128)(2,1)} %get-tuple-element.24.queries_next) | copy-start | bytes 3932164
  26.7 5.0 %collective-permute-start.2 = (bf16[576,256]{1,0:T(8,128)(2,1)S(1)}, bf16[576,256]{1,0:T(8,128)(2,1)S(1)}, u32[]{:S(2)}, u32[]{:S(2)}) collective-permute-start(bf16[576,256]{1,0:T(8,128)(2,1)S(1)} %pad_maximum_fusion.2), channel_id=1, source_target_pairs={{0,2},{1,3},{2,0},{3,1},{4,6},{5,7},{6,4},{7,5},{8,10},{9,11},{10,... | collective-permute-start | bytes 884744 | tf_op jit(solution)/shard_map/ppermute | solution.py:34
  28.8 12.5 %collective-permute-start.9 = (bf16[128,1792]{1,0:T(8,128)(2,1)S(1)}, bf16[128,1792]{1,0:T(8,128)(2,1)S(1)}, u32[]{:S(2)}, u32[]{:S(2)}) collective-permute-start(bf16[128,1792]{1,0:T(8,128)(2,1)S(1)} %get-tuple-element.29), channel_id=1, source_target_pairs={{0,112},{1,113},{2,114},{3,115},{4,116},{5,117},{6,118},{7,119},{8... | collective-permute-start | bytes 1376264 | tf_op jit(solution)/shard_map/ppermute | solution.py:34
  28.9 13.5 %collective-permute-start.12 = (bf16[128,1792]{1,0:T(8,128)(2,1)S(1)}, bf16[128,1792]{1,0:T(8,128)(2,1)S(1)}, u32[]{:S(2)}, u32[]{:S(2)}) collective-permute-start(bf16[128,1792]{1,0:T(8,128)(2,1)S(1)} %get-tuple-element.31), channel_id=1, source_target_pairs={{0,16},{1,17},{2,18},{3,19},{4,20},{5,21},{6,22},{7,23},{8,24},{9,... | collective-permute-start | bytes 1376264 | tf_op jit(solution)/shard_map/ppermute | solution.py:34
  39.7 26.9 %copy-start.5 = (bf16[64,1792]{1,0:T(8,128)(2,1)S(1)}, bf16[64,1792]{1,0:T(8,128)(2,1)}, u32[]{:S(2)}) copy-start(bf16[64,1792]{1,0:T(8,128)(2,1)} %get-tuple-element.27.refs_5_) | copy-start | bytes 688132
  41.2 11.3 %collective-permute-start.10 = (bf16[128,1792]{1,0:T(8,128)(2,1)S(1)}, bf16[128,1792]{1,0:T(8,128)(2,1)S(1)}, u32[]{:S(2)}, u32[]{:S(2)}) collective-permute-start(bf16[128,1792]{1,0:T(8,128)(2,1)S(1)} %collective-permute-done.9.refs_7_), channel_id=1, source_target_pairs={{0,112},{1,113},{2,114},{3,115},{4,116},{5,117},{6,118},{7,119},{8... | collective-permute-start | bytes 1376264 | tf_op jit(solution)/shard_map/ppermute | solution.py:34
  42.4 12.8 %collective-permute-start.13 = (bf16[128,1792]{1,0:T(8,128)(2,1)S(1)}, bf16[128,1792]{1,0:T(8,128)(2,1)S(1)}, u32[]{:S(2)}, u32[]{:S(2)}) collective-permute-start(bf16[128,1792]{1,0:T(8,128)(2,1)S(1)} %collective-permute-done.12.refs_11_), channel_id=1, source_target_pairs={{0,16},{1,17},{2,18},{3,19},{4,20},{5,21},{6,22},{7,23},{8,24},{9,... | collective-permute-start | bytes 1376264 | tf_op jit(solution)/shard_map/ppermute | solution.py:34
  42.7 13.4 %collective-permute-start.5 = (bf16[256,1024]{1,0:T(8,128)(2,1)S(1)}, bf16[256,1024]{1,0:T(8,128)(2,1)S(1)}, u32[]{:S(2)}, u32[]{:S(2)}) collective-permute-start(bf16[256,1024]{1,0:T(8,128)(2,1)S(1)} %attend.1.refs_0_), channel_id=1, source_target_pairs={{0,129},{1,128},{2,131},{3,130},{4,133},{5,132},{6,135},{7,134},{8... | collective-permute-start | bytes 1572872 | tf_op jit(solution)/shard_map/ppermute | solution.py:34
  44.6 12.0 %collective-permute-start.3 = (bf16[256,1024]{1,0:T(8,128)(2,1)S(1)}, bf16[256,1024]{1,0:T(8,128)(2,1)S(1)}, u32[]{:S(2)}, u32[]{:S(2)}) collective-permute-start(bf16[256,1024]{1,0:T(8,128)(2,1)S(1)} %attend.1.refs_0_), channel_id=1, source_target_pairs={{0,1},{1,0},{2,3},{3,2},{4,5},{5,4},{6,7},{7,6},{8,9},{9,8},{10,11... | collective-permute-start | bytes 1572872 | tf_op jit(solution)/shard_map/ppermute | solution.py:34
  52.6 6.0 %collective-permute-start.15 = (bf16[64,1792]{1,0:T(8,128)(2,1)S(1)}, bf16[64,1792]{1,0:T(8,128)(2,1)S(1)}, u32[]{:S(2)}, u32[]{:S(2)}) collective-permute-start(bf16[64,1792]{1,0:T(8,128)(2,1)S(1)} %slice.106), channel_id=1, source_target_pairs={{0,112},{1,113},{2,114},{3,115},{4,116},{5,117},{6,118},{7,119},{8... | collective-permute-start | bytes 688136 | tf_op jit(solution)/shard_map/ppermute | solution.py:34
  55.2 11.5 %collective-permute-start.14 = (bf16[128,1792]{1,0:T(8,128)(2,1)S(1)}, bf16[128,1792]{1,0:T(8,128)(2,1)S(1)}, u32[]{:S(2)}, u32[]{:S(2)}) collective-permute-start(bf16[128,1792]{1,0:T(8,128)(2,1)S(1)} %collective-permute-done.13.refs_10_), channel_id=1, source_target_pairs={{0,16},{1,17},{2,18},{3,19},{4,20},{5,21},{6,22},{7,23},{8,24},{9,... | collective-permute-start | bytes 1376264 | tf_op jit(solution)/shard_map/ppermute | solution.py:34
  56.1 5.9 %collective-permute-start.6 = (bf16[128,1024]{1,0:T(8,128)(2,1)S(1)}, bf16[128,1024]{1,0:T(8,128)(2,1)S(1)}, u32[]{:S(2)}, u32[]{:S(2)}) collective-permute-start(bf16[128,1024]{1,0:T(8,128)(2,1)S(1)} %slice.105), channel_id=1, source_target_pairs={{0,1},{1,0},{2,3},{3,2},{4,5},{5,4},{6,7},{7,6},{8,9},{9,8},{10,11... | collective-permute-start | bytes 786440 | tf_op jit(solution)/shard_map/ppermute | solution.py:34
  56.6 6.8 %collective-permute-start.4 = (bf16[128,1024]{1,0:T(8,128)(2,1)S(1)}, bf16[128,1024]{1,0:T(8,128)(2,1)S(1)}, u32[]{:S(2)}, u32[]{:S(2)}) collective-permute-start(bf16[128,1024]{1,0:T(8,128)(2,1)S(1)} %slice.104), channel_id=1, source_target_pairs={{0,129},{1,128},{2,131},{3,130},{4,133},{5,132},{6,135},{7,134},{8... | collective-permute-start | bytes 786440 | tf_op jit(solution)/shard_map/ppermute | solution.py:34
  58.6 6.4 %collective-permute-start.16 = (bf16[64,1792]{1,0:T(8,128)(2,1)S(1)}, bf16[64,1792]{1,0:T(8,128)(2,1)S(1)}, u32[]{:S(2)}, u32[]{:S(2)}) collective-permute-start(bf16[64,1792]{1,0:T(8,128)(2,1)S(1)} %collective-permute-done.15.refs_14_), channel_id=1, source_target_pairs={{0,112},{1,113},{2,114},{3,115},{4,116},{5,117},{6,118},{7,119},{8... | collective-permute-start | bytes 688136 | tf_op jit(solution)/shard_map/ppermute | solution.py:34
  68.9 5.5 %collective-permute-start.17 = (bf16[3,256,896]{2,1,0:T(8,128)(2,1)S(1)}, bf16[3,256,896]{2,1,0:T(8,128)(2,1)S(1)}, u32[]{:S(2)}, u32[]{:S(2)}) collective-permute-start(bf16[3,256,896]{2,1,0:T(8,128)(2,1)S(1)} %get-tuple-element.34), channel_id=1, source_target_pairs={{0,2},{1,3},{2,0},{3,1},{4,6},{5,7},{6,4},{7,5},{8,10},{9,11},{10,... | collective-permute-start | bytes 4128776 | tf_op jit(solution)/shard_map/ppermute | solution.py:34
  71.7 3.4 %collective-permute-start.18 = (bf16[256,896]{1,0:T(8,128)(2,1)S(1)}, bf16[256,896]{1,0:T(8,128)(2,1)S(1)}, u32[]{:S(2)}, u32[]{:S(2)}) collective-permute-start(bf16[256,896]{1,0:T(8,128)(2,1)S(1)} %get-tuple-element.35), channel_id=1, source_target_pairs={{0,2},{1,3},{2,0},{3,1},{4,6},{5,7},{6,4},{7,5},{8,10},{9,11},{10,... | collective-permute-start | bytes 1376264 | tf_op jit(solution)/shard_map/ppermute | solution.py:34
  75.1 7.1 %collective-permute-start.19 = (bf16[128,896]{1,0:T(8,128)(2,1)S(1)}, bf16[128,896]{1,0:T(8,128)(2,1)S(1)}, u32[]{:S(2)}, u32[]{:S(2)}) collective-permute-start(bf16[128,896]{1,0:T(8,128)(2,1)S(1)} %get-tuple-element.37), channel_id=1, source_target_pairs={{0,12},{1,13},{2,14},{3,15},{4,0},{5,1},{6,2},{7,3},{8,4},{9,5},{1... | collective-permute-start | bytes 688136 | tf_op jit(solution)/shard_map/ppermute | solution.py:34
  77.6 7.7 %collective-permute-start.23 = (bf16[128,896]{1,0:T(8,128)(2,1)S(1)}, bf16[128,896]{1,0:T(8,128)(2,1)S(1)}, u32[]{:S(2)}, u32[]{:S(2)}) collective-permute-start(bf16[128,896]{1,0:T(8,128)(2,1)S(1)} %get-tuple-element.40), channel_id=1, source_target_pairs={{0,4},{1,5},{2,6},{3,7},{4,8},{5,9},{6,10},{7,11},{8,12},{9,13},{1... | collective-permute-start | bytes 688136 | tf_op jit(solution)/shard_map/ppermute | solution.py:34
  77.7 14.1 %collective-permute-start.25 = (bf16[128,896]{1,0:T(8,128)(2,1)S(1)}, bf16[128,896]{1,0:T(8,128)(2,1)S(1)}, u32[]{:S(2)}, u32[]{:S(2)}) collective-permute-start(bf16[128,896]{1,0:T(8,128)(2,1)S(1)} %get-tuple-element.48), channel_id=1, source_target_pairs={{0,12},{1,13},{2,14},{3,15},{4,0},{5,1},{6,2},{7,3},{8,4},{9,5},{1... | collective-permute-start | bytes 688136 | tf_op jit(solution)/shard_map/ppermute | solution.py:34
  80.5 12.9 %collective-permute-start.21 = (bf16[128,896]{1,0:T(8,128)(2,1)S(1)}, bf16[128,896]{1,0:T(8,128)(2,1)S(1)}, u32[]{:S(2)}, u32[]{:S(2)}) collective-permute-start(bf16[128,896]{1,0:T(8,128)(2,1)S(1)} %get-tuple-element.49), channel_id=1, source_target_pairs={{0,4},{1,5},{2,6},{3,7},{4,8},{5,9},{6,10},{7,11},{8,12},{9,13},{1... | collective-permute-start | bytes 688136 | tf_op jit(solution)/shard_map/ppermute | solution.py:34
  85.4 10.7 %collective-permute-start.24 = (bf16[128,896]{1,0:T(8,128)(2,1)S(1)}, bf16[128,896]{1,0:T(8,128)(2,1)S(1)}, u32[]{:S(2)}, u32[]{:S(2)}) collective-permute-start(bf16[128,896]{1,0:T(8,128)(2,1)S(1)} %get-tuple-element.46), channel_id=1, source_target_pairs={{0,1},{1,0},{2,129},{3,128},{4,5},{5,4},{6,133},{7,132},{8,9},{9,8... | collective-permute-start | bytes 688136 | tf_op jit(solution)/shard_map/ppermute | solution.py:34
  89.9 10.1 %collective-permute-start.20 = (bf16[128,896]{1,0:T(8,128)(2,1)S(1)}, bf16[128,896]{1,0:T(8,128)(2,1)S(1)}, u32[]{:S(2)}, u32[]{:S(2)}) collective-permute-start(bf16[128,896]{1,0:T(8,128)(2,1)S(1)} %get-tuple-element.47), channel_id=1, source_target_pairs={{0,0},{1,1},{2,128},{3,129},{4,4},{5,5},{6,132},{7,133},{8,8},{9,9... | collective-permute-start | bytes 688136 | tf_op jit(solution)/shard_map/ppermute | solution.py:34
  91.9 9.2 %collective-permute-start.26 = (bf16[128,896]{1,0:T(8,128)(2,1)S(1)}, bf16[128,896]{1,0:T(8,128)(2,1)S(1)}, u32[]{:S(2)}, u32[]{:S(2)}) collective-permute-start(bf16[128,896]{1,0:T(8,128)(2,1)S(1)} %fusion.2), channel_id=1, source_target_pairs={{0,13},{1,12},{2,141},{3,140},{4,1},{5,0},{6,129},{7,128},{8,5},{9... | collective-permute-start | bytes 688136 | tf_op jit(solution)/shard_map/ppermute | solution.py:34
  93.5 10.5 %collective-permute-start.22 = (bf16[128,896]{1,0:T(8,128)(2,1)S(1)}, bf16[128,896]{1,0:T(8,128)(2,1)S(1)}, u32[]{:S(2)}, u32[]{:S(2)}) collective-permute-start(bf16[128,896]{1,0:T(8,128)(2,1)S(1)} %fusion.6), channel_id=1, source_target_pairs={{0,4},{1,5},{2,132},{3,133},{4,8},{5,9},{6,136},{7,137},{8,12},{9,... | collective-permute-start | bytes 688136 | tf_op jit(solution)/shard_map/ppermute | solution.py:34

commit v13 on v11

--- a/solution.py
+++ b/solution.py
@@ -302,7 +302,7 @@
     own_keys = key_rows.T
     half = lax.dynamic_slice_in_dim(own_keys, 128 * c, 128, 1)
     near, far = (
-        lax.ppermute(half, CTX, [(i, i + by) for i in range(16 - by)]) for by in (1, 2)
+        lax.ppermute(half, CTX, [(i, (i + by) % 16) for i in range(16)]) for by in (1, 2)
     )
     cosines, sines, all_cosines, all_sines = turns(slab * 256)
     queries = call(

time: 105 us -> 101 us (0.962)
  starting transfers between devices: 50.5 us -> 47.4 us
  waiting for transfers between devices: 27.2 us -> 25.9 us
    ppermute x2, starting transfers between devices: 9.28 us -> 5.53 us  [local(): lax.ppermute(half, CTX, [(i, (i + by) % 16) for i in range(16)])]
    ppermute x27, waiting for transfers between devices: 27.2 us -> 25.9 us  [moved(): return lax.ppermute(a, AXES, pairs)]
where the time goes in v13:
time: 101 us
  starting transfers between devices  47.4 us (47%)
  waiting for transfers between devices  25.9 us (26%)
  Pallas kernels  21.8 us (22%)
  other arithmetic  3 us (3%)
  local copies, waits for them, and re-layouts  1.36 us (1%)
  between operations  1.01 us (1%)
    ppermute x27, starting transfers between devices, moved(): return lax.ppermute(a, AXES, pairs)  41.9 us
    ppermute x27, waiting for transfers between devices, moved(): return lax.ppermute(a, AXES, pairs)  25.9 us
    pallas_call x6, Pallas kernels, call(): pl.pallas_call(kernel, out_shape=shapes, in_specs=specs, out_specs=whole(...  19.6 us
    ppermute x2, starting transfers between devices, local(): lax.ppermute(half, CTX, [(i, (i + by) % 16) for i in range(16)])  5.53 us
    pallas_call x1, Pallas kernels, quarters(): pl.pallas_call(quarter_kernel, out_shape=[jax.ShapeDtypeStruct((64, 1792)...  2.22 us
  transfers between devices with their start and end apart: 29, of which 12 were waited for; matrix products, arithmetic and copies ran while one was open for 2% of the time, Pallas kernels for 19%

profile of v13, /device:TPU:1, one launch (start us, length us, event | category | flops | bytes accessed | tf_op | source)
XLA Modules:
  0.0 100.5 jit_solution(4580509270515595763)
XLA Ops:
  0.0 0.9 dynamic-slice_bitcast_fusion
  0.9 3.9 %collective-permute-start.1 = (bf16[576,128]{1,0:T(8,128)(2,1)S(1)}, bf16[576,128]{1,0:T(8,128)(2,1)S(1)}, u32[]{:S(2)}, u32[]{:S(2)}) collective-permute-start(bf16[576,128]{1,0:T(8,128)(2,1)S(1)} %dynamic-slice_bitcast_fusion), channel_id=1, source_target_pairs={{0,32},{16,48},{32,64},{48,80},{64,96},{80,112},{96,128},{112,144}... | collective-permute-start | bytes 442376 | tf_op jit(solution)/shard_map/ppermute | solution.py:305
  4.8 1.6 %collective-permute-start = (bf16[576,128]{1,0:T(8,128)(2,1)S(1)}, bf16[576,128]{1,0:T(8,128)(2,1)S(1)}, u32[]{:S(2)}, u32[]{:S(2)}) collective-permute-start(bf16[576,128]{1,0:T(8,128)(2,1)S(1)} %dynamic-slice_bitcast_fusion), channel_id=1, source_target_pairs={{0,16},{16,32},{32,48},{48,64},{64,80},{80,96},{96,112},{112,128},... | collective-permute-start | bytes 442376 | tf_op jit(solution)/shard_map/ppermute | solution.py:305
  6.5 2.2 %quarters.1 = (bf16[64,1792]{1,0:T(8,128)(2,1)}, bf16[64,1792]{1,0:T(8,128)(2,1)}) custom-call(bf16[64,7168]{1,0:T(8,128)(2,1)} %bitcast.35), custom_call_target="tpu_custom_call" | custom-call | bytes 2097152 | tf_op jit(solution)/shard_map/quarters/pallas_call | solution.py:247
  8.7 2.8 %collective-permute-start.13 = (bf16[64,1792]{1,0:T(8,128)(2,1)}, bf16[64,1792]{1,0:T(8,128)(2,1)S(1)}, u32[]{:S(2)}, u32[]{:S(2)}) collective-permute-start(bf16[64,1792]{1,0:T(8,128)(2,1)} %get-tuple-element.27.refs_8_), channel_id=1, source_target_pairs={{0,16},{1,17},{2,18},{3,19},{4,20},{5,21},{6,22},{7,23},{8,24},{9,... | collective-permute-start | bytes 688136 | tf_op jit(solution)/shard_map/ppermute | solution.py:33
  11.5 0.8 collective-permute-start.9
  12.3 1.9 %collective-permute-start.10 = (bf16[64,1792]{1,0:T(8,128)(2,1)}, bf16[64,1792]{1,0:T(8,128)(2,1)S(1)}, u32[]{:S(2)}, u32[]{:S(2)}) collective-permute-start(bf16[64,1792]{1,0:T(8,128)(2,1)} %get-tuple-element.28), channel_id=1, source_target_pairs={{0,129},{1,128},{2,131},{3,130},{4,133},{5,132},{6,135},{7,134},{8... | collective-permute-start | bytes 688136 | tf_op jit(solution)/shard_map/ppermute | solution.py:33
  14.4 0.1 fusion.reorder
  14.6 0.8 fusion.11
  15.3 6.8 %queries.1 = (bf16[1024,640]{1,0:T(8,128)(2,1)}, bf16[1024,640]{1,0:T(8,128)(2,1)}) custom-call(bf16[256,1536]{1,0:T(8,128)(2,1)} %rows.1, bf16[1536,1536]{1,0:T(8,128)(2,1)} %w_query.1, bf16[8,128,512]{2,1,0:T(8,128)(2,1)} %w_key_up.1, f32[64,128]{1,0:T(8,128)} %get-tuple-element.59.cosines, f32[64,128]{1,0:T(8,128)} %get-tuple-element.58.sines), custom_call_target="tpu_custom_call" | custom-call | flops 1476395008 | bytes 8388608 | tf_op jit(solution)/shard_map/queries/pallas_call | solution.py:259
  22.3 2.0 %collective-permute-start.2 = (bf16[576,256]{1,0:T(8,128)(2,1)S(1)}, bf16[576,256]{1,0:T(8,128)(2,1)S(1)}, u32[]{:S(2)}, u32[]{:S(2)}) collective-permute-start(bf16[576,256]{1,0:T(8,128)(2,1)S(1)} %pad_maximum_fusion.2), channel_id=1, source_target_pairs={{0,2},{1,3},{2,0},{3,1},{4,6},{5,7},{6,4},{7,5},{8,10},{9,11},{10,... | collective-permute-start | bytes 884744 | tf_op jit(solution)/shard_map/ppermute | solution.py:33
  24.4 0.6 collective-permute-start.11
  24.9 1.2 %collective-permute-start.14 = (bf16[128,1792]{1,0:T(8,128)(2,1)S(1)}, bf16[128,1792]{1,0:T(8,128)(2,1)S(1)}, u32[]{:S(2)}, u32[]{:S(2)}) collective-permute-start(bf16[128,1792]{1,0:T(8,128)(2,1)S(1)} %get-tuple-element.31), channel_id=1, source_target_pairs={{0,16},{1,17},{2,18},{3,19},{4,20},{5,21},{6,22},{7,23},{8,24},{9,... | collective-permute-start | bytes 1376264 | tf_op jit(solution)/shard_map/ppermute | solution.py:33
  26.2 0.4 multiply_sine_fusion
  27.3 0.6 keys.1
  27.9 3.8 %attend.2.refs_0_ = bf16[256,512]{1,0:T(8,128)(2,1)S(1)} custom-call(bf16[1024,640]{1,0:T(8,128)(2,1)S(1)} %copy-done.3, bf16[640,768]{1,0:T(8,128)(2,1)S(1)} %get-tuple-element.24.keys, f32[256,768]{1,0:T(8,128)S(1)} %get-tuple-element.25.hidden, bf16[8,512,128]{2,1,0:T(8,128)(2,1)S(1)} %copy-done.4, bf16[512,512]{1,0:T(8,128)(2,1)S(1)} %fusion.reorder), custom_call_target="tpu_custom_call" | custom-call | flops 1946157056 | bytes 5242880 | tf_op jit(solution)/shard_map/attend/pallas_call | solution.py:259
  31.7 3.8 %attend.3.refs_1_ = bf16[256,512]{1,0:T(8,128)(2,1)S(1)} custom-call(bf16[1024,640]{1,0:T(8,128)(2,1)S(1)} %copy-done.2, bf16[640,768]{1,0:T(8,128)(2,1)S(1)} %get-tuple-element.24.keys, f32[256,768]{1,0:T(8,128)S(1)} %get-tuple-element.25.hidden, bf16[8,512,128]{2,1,0:T(8,128)(2,1)S(1)} %copy-done.4, bf16[512,512]{1,0:T(8,128)(2,1)S(1)} %fusion.reorder), custom_call_target="tpu_custom_call" | custom-call | flops 1946157056 | bytes 5242880 | tf_op jit(solution)/shard_map/attend/pallas_call | solution.py:259
  35.5 0.4 collective-permute-done.11.refs_10_
  35.9 2.2 %collective-permute-start.12 = (bf16[128,1792]{1,0:T(8,128)(2,1)S(1)}, bf16[128,1792]{1,0:T(8,128)(2,1)S(1)}, u32[]{:S(2)}, u32[]{:S(2)}) collective-permute-start(bf16[128,1792]{1,0:T(8,128)(2,1)S(1)} %collective-permute-done.11.refs_10_), channel_id=1, source_target_pairs={{0,112},{1,113},{2,114},{3,115},{4,116},{5,117},{6,118},{7,119},{8... | collective-permute-start | bytes 1376264 | tf_op jit(solution)/shard_map/ppermute | solution.py:33
  38.2 1.7 %collective-permute-start.8 = (bf16[256,512]{1,0:T(8,128)(2,1)S(1)}, bf16[256,512]{1,0:T(8,128)(2,1)S(1)}, u32[]{:S(2)}, u32[]{:S(2)}) collective-permute-start(bf16[256,512]{1,0:T(8,128)(2,1)S(1)} %attend.2.refs_0_), channel_id=1, source_target_pairs={{0,129},{1,128},{2,131},{3,130},{4,133},{5,132},{6,135},{7,134},{8... | collective-permute-start | bytes 786440 | tf_op jit(solution)/shard_map/ppermute | solution.py:33
  39.9 1.0 collective-permute-start.6
  40.9 7.1 %collective-permute-done.12.refs_11_ = bf16[128,1792]{1,0:T(8,128)(2,1)S(1)} collective-permute-done((bf16[128,1792]{1,0:T(8,128)(2,1)S(1)}, bf16[128,1792]{1,0:T(8,128)(2,1)S(1)}, u32[]{:S(2)}, u32[]{:S(2)}) %collective-permute-start.12) | collective-permute-done | bytes 458784 | tf_op jit(solution)/shard_map/ppermute | solution.py:33
  48.0 2.5 %collective-permute-start.17 = (bf16[64,1792]{1,0:T(8,128)(2,1)S(1)}, bf16[64,1792]{1,0:T(8,128)(2,1)S(1)}, u32[]{:S(2)}, u32[]{:S(2)}) collective-permute-start(bf16[64,1792]{1,0:T(8,128)(2,1)S(1)} %slice.96), channel_id=1, source_target_pairs={{0,112},{1,113},{2,114},{3,115},{4,116},{5,117},{6,118},{7,119},{8... | collective-permute-start | bytes 688136 | tf_op jit(solution)/shard_map/ppermute | solution.py:33
  50.6 1.8 %collective-permute-start.5 = (bf16[256,512]{1,0:T(8,128)(2,1)S(1)}, bf16[256,512]{1,0:T(8,128)(2,1)S(1)}, u32[]{:S(2)}, u32[]{:S(2)}) collective-permute-start(bf16[256,512]{1,0:T(8,128)(2,1)S(1)} %collective-permute-done.3.refs_2_), channel_id=1, source_target_pairs={{0,129},{1,128},{2,131},{3,130},{4,133},{5,132},{6,135},{7,134},{8... | collective-permute-start | bytes 786440 | tf_op jit(solution)/shard_map/ppermute | solution.py:33
  52.3 0.8 collective-permute-start.7
  53.1 0.3 collective-permute-done.17.refs_17_
  53.4 3.4 %collective-permute-start.18 = (bf16[64,1792]{1,0:T(8,128)(2,1)S(1)}, bf16[64,1792]{1,0:T(8,128)(2,1)S(1)}, u32[]{:S(2)}, u32[]{:S(2)}) collective-permute-start(bf16[64,1792]{1,0:T(8,128)(2,1)S(1)} %collective-permute-done.17.refs_17_), channel_id=1, source_target_pairs={{0,112},{1,113},{2,114},{3,115},{4,116},{5,117},{6,118},{7,119},{8... | collective-permute-start | bytes 688136 | tf_op jit(solution)/shard_map/ppermute | solution.py:33
  56.8 0.6 collective-permute-done.5.refs_4_
  57.5 4.3 %collective-permute-done.7.refs_5_ = bf16[256,512]{1,0:T(8,128)(2,1)S(1)} collective-permute-done((bf16[256,512]{1,0:T(8,128)(2,1)S(1)}, bf16[256,512]{1,0:T(8,128)(2,1)S(1)}, u32[]{:S(2)}, u32[]{:S(2)}) %collective-permute-start.7) | collective-permute-done | bytes 262176 | tf_op jit(solution)/shard_map/ppermute | solution.py:33
  61.8 2.3 %project.3 = (bf16[256,896]{1,0:T(8,128)(2,1)S(1)}, bf16[3,256,896]{2,1,0:T(8,128)(2,1)S(1)}) custom-call(bf16[256,512]{1,0:T(8,128)(2,1)S(1)} %attend.2.refs_0_, bf16[256,512]{1,0:T(8,128)(2,1)S(1)} %attend.3.refs_1_, bf16[256,512]{1,0:T(8,128)(2,1)S(1)} %collective-permute-done.3.refs_2_, bf16[256,512]{1,0:T(8,128)(2,1)S(1)} %collective-permute-done.4.refs_3_, ...), custom_call_target="tpu_custom_call" | custom-call | flops 1879048192 | bytes 8388608 | tf_op jit(solution)/shard_map/project/pallas_call | solution.py:259
  64.1 3.2 %collective-permute-start.19 = (bf16[3,256,896]{2,1,0:T(8,128)(2,1)S(1)}, bf16[3,256,896]{2,1,0:T(8,128)(2,1)S(1)}, u32[]{:S(2)}, u32[]{:S(2)}) collective-permute-start(bf16[3,256,896]{2,1,0:T(8,128)(2,1)S(1)} %get-tuple-element.34), channel_id=1, source_target_pairs={{0,2},{1,3},{2,0},{3,1},{4,6},{5,7},{6,4},{7,5},{8,10},{9,11},{10,... | collective-permute-start | bytes 4128776 | tf_op jit(solution)/shard_map/ppermute | solution.py:33
  67.4 2.3 %project.2 = (f32[256,896]{1,0:T(8,128)S(1)}, f32[3,256,896]{2,1,0:T(8,128)S(1)}) custom-call(bf16[256,512]{1,0:T(8,128)(2,1)S(1)} %attend.2.refs_0_, bf16[256,512]{1,0:T(8,128)(2,1)S(1)} %attend.3.refs_1_, bf16[256,512]{1,0:T(8,128)(2,1)S(1)} %collective-permute-done.3.refs_2_, bf16[256,512]{1,0:T(8,128)(2,1)S(1)} %collective-permute-done.4.refs_3_, ...), custom_call_target="tpu_custom_call" | custom-call | flops 1879048192 | bytes 8388608 | tf_op jit(solution)/shard_map/project/pallas_call | solution.py:259
  69.7 0.3 collective-permute-done.19
  70.0 0.2 convert_add_fusion.2
  70.3 0.4 collective-permute-done.20
  70.7 2.5 %collective-permute-start.21 = (bf16[128,896]{1,0:T(8,128)(2,1)S(1)}, bf16[128,896]{1,0:T(8,128)(2,1)S(1)}, u32[]{:S(2)}, u32[]{:S(2)}) collective-permute-start(bf16[128,896]{1,0:T(8,128)(2,1)S(1)} %fusion.10), channel_id=1, source_target_pairs={{0,12},{1,13},{2,14},{3,15},{4,0},{5,1},{6,2},{7,3},{8,4},{9,5},{1... | collective-permute-start | bytes 688136 | tf_op jit(solution)/shard_map/ppermute | solution.py:33
  73.3 2.8 %collective-permute-start.27 = (bf16[128,896]{1,0:T(8,128)(2,1)S(1)}, bf16[128,896]{1,0:T(8,128)(2,1)S(1)}, u32[]{:S(2)}, u32[]{:S(2)}) collective-permute-start(bf16[128,896]{1,0:T(8,128)(2,1)S(1)} %get-tuple-element.48), channel_id=1, source_target_pairs={{0,12},{1,13},{2,14},{3,15},{4,0},{5,1},{6,2},{7,3},{8,4},{9,5},{1... | collective-permute-start | bytes 688136 | tf_op jit(solution)/shard_map/ppermute | solution.py:33
  76.1 1.7 %collective-permute-done.21 = bf16[128,896]{1,0:T(8,128)(2,1)S(1)} collective-permute-done((bf16[128,896]{1,0:T(8,128)(2,1)S(1)}, bf16[128,896]{1,0:T(8,128)(2,1)S(1)}, u32[]{:S(2)}, u32[]{:S(2)}) %collective-permute-start.21) | collective-permute-done | bytes 229408 | tf_op jit(solution)/shard_map/ppermute | solution.py:33
  77.8 3.1 %collective-permute-done.25 = bf16[128,896]{1,0:T(8,128)(2,1)S(1)} collective-permute-done((bf16[128,896]{1,0:T(8,128)(2,1)S(1)}, bf16[128,896]{1,0:T(8,128)(2,1)S(1)}, u32[]{:S(2)}, u32[]{:S(2)}) %collective-permute-start.25) | collective-permute-done | bytes 229408 | tf_op jit(solution)/shard_map/ppermute | solution.py:33
  81.0 4.3 %collective-permute-start.26 = (bf16[128,896]{1,0:T(8,128)(2,1)S(1)}, bf16[128,896]{1,0:T(8,128)(2,1)S(1)}, u32[]{:S(2)}, u32[]{:S(2)}) collective-permute-start(bf16[128,896]{1,0:T(8,128)(2,1)S(1)} %get-tuple-element.46), channel_id=1, source_target_pairs={{0,1},{1,0},{2,129},{3,128},{4,5},{5,4},{6,133},{7,132},{8,9},{9,8... | collective-permute-start | bytes 688136 | tf_op jit(solution)/shard_map/ppermute | solution.py:33
  85.2 1.9 %collective-permute-start.22 = (bf16[128,896]{1,0:T(8,128)(2,1)S(1)}, bf16[128,896]{1,0:T(8,128)(2,1)S(1)}, u32[]{:S(2)}, u32[]{:S(2)}) collective-permute-start(bf16[128,896]{1,0:T(8,128)(2,1)S(1)} %get-tuple-element.47), channel_id=1, source_target_pairs={{0,0},{1,1},{2,128},{3,129},{4,4},{5,5},{6,132},{7,133},{8,8},{9,9... | collective-permute-start | bytes 688136 | tf_op jit(solution)/shard_map/ppermute | solution.py:33
  87.2 1.5 %collective-permute-start.28 = (bf16[128,896]{1,0:T(8,128)(2,1)S(1)}, bf16[128,896]{1,0:T(8,128)(2,1)S(1)}, u32[]{:S(2)}, u32[]{:S(2)}) collective-permute-start(bf16[128,896]{1,0:T(8,128)(2,1)S(1)} %fusion.2), channel_id=1, source_target_pairs={{0,13},{1,12},{2,141},{3,140},{4,1},{5,0},{6,129},{7,128},{8,5},{9... | collective-permute-start | bytes 688136 | tf_op jit(solution)/shard_map/ppermute | solution.py:33
  88.8 2.8 %collective-permute-start.24 = (bf16[128,896]{1,0:T(8,128)(2,1)S(1)}, bf16[128,896]{1,0:T(8,128)(2,1)S(1)}, u32[]{:S(2)}, u32[]{:S(2)}) collective-permute-start(bf16[128,896]{1,0:T(8,128)(2,1)S(1)} %fusion.6), channel_id=1, source_target_pairs={{0,4},{1,5},{2,132},{3,133},{4,8},{5,9},{6,136},{7,137},{8,12},{9,... | collective-permute-start | bytes 688136 | tf_op jit(solution)/shard_map/ppermute | solution.py:33
  91.6 3.6 %collective-permute-done.22 = bf16[128,896]{1,0:T(8,128)(2,1)S(1)} collective-permute-done((bf16[128,896]{1,0:T(8,128)(2,1)S(1)}, bf16[128,896]{1,0:T(8,128)(2,1)S(1)}, u32[]{:S(2)}, u32[]{:S(2)}) %collective-permute-start.22) | collective-permute-done | bytes 229408 | tf_op jit(solution)/shard_map/ppermute | solution.py:33
  95.2 1.2 %collective-permute-done.28 = bf16[128,896]{1,0:T(8,128)(2,1)S(1)} collective-permute-done((bf16[128,896]{1,0:T(8,128)(2,1)S(1)}, bf16[128,896]{1,0:T(8,128)(2,1)S(1)}, u32[]{:S(2)}, u32[]{:S(2)}) %collective-permute-start.28) | collective-permute-done | bytes 229408 | tf_op jit(solution)/shard_map/ppermute | solution.py:33
  96.4 2.9 %collective-permute-done.24 = bf16[128,896]{1,0:T(8,128)(2,1)S(1)} collective-permute-done((bf16[128,896]{1,0:T(8,128)(2,1)S(1)}, bf16[128,896]{1,0:T(8,128)(2,1)S(1)}, u32[]{:S(2)}, u32[]{:S(2)}) %collective-permute-start.24) | collective-permute-done | bytes 229408 | tf_op jit(solution)/shard_map/ppermute | solution.py:33
  99.3 0.1 broadcast_select_fusion.1
  99.6 0.9 maximum_maximum_fusion
  (55 shorter events, 1.2 us)
Async XLA Ops:
  0.9 21.3 %collective-permute-start.1 = (bf16[576,128]{1,0:T(8,128)(2,1)S(1)}, bf16[576,128]{1,0:T(8,128)(2,1)S(1)}, u32[]{:S(2)}, u32[]{:S(2)}) collective-permute-start(bf16[576,128]{1,0:T(8,128)(2,1)S(1)} %dynamic-slice_bitcast_fusion), channel_id=1, source_target_pairs={{0,32},{16,48},{32,64},{48,80},{64,96},{80,112},{96,128},{112,144}... | collective-permute-start | bytes 442376 | tf_op jit(solution)/shard_map/ppermute | solution.py:305
  4.8 17.4 %collective-permute-start = (bf16[576,128]{1,0:T(8,128)(2,1)S(1)}, bf16[576,128]{1,0:T(8,128)(2,1)S(1)}, u32[]{:S(2)}, u32[]{:S(2)}) collective-permute-start(bf16[576,128]{1,0:T(8,128)(2,1)S(1)} %dynamic-slice_bitcast_fusion), channel_id=1, source_target_pairs={{0,16},{16,32},{32,48},{48,64},{64,80},{80,96},{96,112},{112,128},... | collective-permute-start | bytes 442376 | tf_op jit(solution)/shard_map/ppermute | solution.py:305
  8.7 15.6 %collective-permute-start.13 = (bf16[64,1792]{1,0:T(8,128)(2,1)}, bf16[64,1792]{1,0:T(8,128)(2,1)S(1)}, u32[]{:S(2)}, u32[]{:S(2)}) collective-permute-start(bf16[64,1792]{1,0:T(8,128)(2,1)} %get-tuple-element.27.refs_8_), channel_id=1, source_target_pairs={{0,16},{1,17},{2,18},{3,19},{4,20},{5,21},{6,22},{7,23},{8,24},{9,... | collective-permute-start | bytes 688136 | tf_op jit(solution)/shard_map/ppermute | solution.py:33
  11.5 12.8 %collective-permute-start.9 = (bf16[64,1792]{1,0:T(8,128)(2,1)}, bf16[64,1792]{1,0:T(8,128)(2,1)S(1)}, u32[]{:S(2)}, u32[]{:S(2)}) collective-permute-start(bf16[64,1792]{1,0:T(8,128)(2,1)} %get-tuple-element.27.refs_8_), channel_id=1, source_target_pairs={{0,112},{1,113},{2,114},{3,115},{4,116},{5,117},{6,118},{7,119},{8... | collective-permute-start | bytes 688136 | tf_op jit(solution)/shard_map/ppermute | solution.py:33
  12.3 11.9 %collective-permute-start.10 = (bf16[64,1792]{1,0:T(8,128)(2,1)}, bf16[64,1792]{1,0:T(8,128)(2,1)S(1)}, u32[]{:S(2)}, u32[]{:S(2)}) collective-permute-start(bf16[64,1792]{1,0:T(8,128)(2,1)} %get-tuple-element.28), channel_id=1, source_target_pairs={{0,129},{1,128},{2,131},{3,130},{4,133},{5,132},{6,135},{7,134},{8... | collective-permute-start | bytes 688136 | tf_op jit(solution)/shard_map/ppermute | solution.py:33
  22.2 5.1 %copy-start = (bf16[256,576]{0,1:T(8,128)(2,1)S(1)}, bf16[256,576]{0,1:T(8,128)(2,1)}, u32[]{:S(2)}) copy-start(bf16[256,576]{0,1:T(8,128)(2,1)} %param.9) | copy-start | bytes 884740
  22.2 5.1 %copy-start.1 = (bf16[512,576]{0,1:T(8,128)(2,1)S(1)}, bf16[512,576]{0,1:T(8,128)(2,1)}, u32[]{:S(2)}) copy-start(bf16[512,576]{0,1:T(8,128)(2,1)} %param.10) | copy-start | bytes 1769476
  22.3 5.6 %copy-start.3 = (bf16[1024,640]{1,0:T(8,128)(2,1)S(1)}, bf16[1024,640]{1,0:T(8,128)(2,1)}, u32[]{:S(2)}) copy-start(bf16[1024,640]{1,0:T(8,128)(2,1)} %get-tuple-element.23.queries) | copy-start | bytes 3932164
  22.3 5.6 %copy-start.4 = (bf16[8,512,128]{2,1,0:T(8,128)(2,1)S(1)}, bf16[8,512,128]{2,1,0:T(8,128)(2,1)}, u32[]{:S(2)}) copy-start(bf16[8,512,128]{2,1,0:T(8,128)(2,1)} %w_value_up.3) | copy-start | bytes 3145732
  22.3 5.0 %collective-permute-start.2 = (bf16[576,256]{1,0:T(8,128)(2,1)S(1)}, bf16[576,256]{1,0:T(8,128)(2,1)S(1)}, u32[]{:S(2)}, u32[]{:S(2)}) collective-permute-start(bf16[576,256]{1,0:T(8,128)(2,1)S(1)} %pad_maximum_fusion.2), channel_id=1, source_target_pairs={{0,2},{1,3},{2,0},{3,1},{4,6},{5,7},{6,4},{7,5},{8,10},{9,11},{10,... | collective-permute-start | bytes 884744 | tf_op jit(solution)/shard_map/ppermute | solution.py:33
  24.4 11.5 %collective-permute-start.11 = (bf16[128,1792]{1,0:T(8,128)(2,1)S(1)}, bf16[128,1792]{1,0:T(8,128)(2,1)S(1)}, u32[]{:S(2)}, u32[]{:S(2)}) collective-permute-start(bf16[128,1792]{1,0:T(8,128)(2,1)S(1)} %get-tuple-element.29), channel_id=1, source_target_pairs={{0,112},{1,113},{2,114},{3,115},{4,116},{5,117},{6,118},{7,119},{8... | collective-permute-start | bytes 1376264 | tf_op jit(solution)/shard_map/ppermute | solution.py:33
  24.9 13.2 %collective-permute-start.14 = (bf16[128,1792]{1,0:T(8,128)(2,1)S(1)}, bf16[128,1792]{1,0:T(8,128)(2,1)S(1)}, u32[]{:S(2)}, u32[]{:S(2)}) collective-permute-start(bf16[128,1792]{1,0:T(8,128)(2,1)S(1)} %get-tuple-element.31), channel_id=1, source_target_pairs={{0,16},{1,17},{2,18},{3,19},{4,20},{5,21},{6,22},{7,23},{8,24},{9,... | collective-permute-start | bytes 1376264 | tf_op jit(solution)/shard_map/ppermute | solution.py:33
  27.9 3.8 %copy-start.2 = (bf16[1024,640]{1,0:T(8,128)(2,1)S(1)}, bf16[1024,640]{1,0:T(8,128)(2,1)}, u32[]{:S(2)}) copy-start(bf16[1024,640]{1,0:T(8,128)(2,1)} %get-tuple-element.26.queries) | copy-start | bytes 3932164
  31.7 30.1 %copy-start.5 = (bf16[64,1792]{1,0:T(8,128)(2,1)S(1)}, bf16[64,1792]{1,0:T(8,128)(2,1)}, u32[]{:S(2)}) copy-start(bf16[64,1792]{1,0:T(8,128)(2,1)} %get-tuple-element.27.refs_8_) | copy-start | bytes 688132
  35.9 12.1 %collective-permute-start.12 = (bf16[128,1792]{1,0:T(8,128)(2,1)S(1)}, bf16[128,1792]{1,0:T(8,128)(2,1)S(1)}, u32[]{:S(2)}, u32[]{:S(2)}) collective-permute-start(bf16[128,1792]{1,0:T(8,128)(2,1)S(1)} %collective-permute-done.11.refs_10_), channel_id=1, source_target_pairs={{0,112},{1,113},{2,114},{3,115},{4,116},{5,117},{6,118},{7,119},{8... | collective-permute-start | bytes 1376264 | tf_op jit(solution)/shard_map/ppermute | solution.py:33
  38.1 12.3 %collective-permute-start.15 = (bf16[128,1792]{1,0:T(8,128)(2,1)S(1)}, bf16[128,1792]{1,0:T(8,128)(2,1)S(1)}, u32[]{:S(2)}, u32[]{:S(2)}) collective-permute-start(bf16[128,1792]{1,0:T(8,128)(2,1)S(1)} %collective-permute-done.14.refs_14_), channel_id=1, source_target_pairs={{0,16},{1,17},{2,18},{3,19},{4,20},{5,21},{6,22},{7,23},{8,24},{9,... | collective-permute-start | bytes 1376264 | tf_op jit(solution)/shard_map/ppermute | solution.py:33
  38.2 12.3 %collective-permute-start.8 = (bf16[256,512]{1,0:T(8,128)(2,1)S(1)}, bf16[256,512]{1,0:T(8,128)(2,1)S(1)}, u32[]{:S(2)}, u32[]{:S(2)}) collective-permute-start(bf16[256,512]{1,0:T(8,128)(2,1)S(1)} %attend.2.refs_0_), channel_id=1, source_target_pairs={{0,129},{1,128},{2,131},{3,130},{4,133},{5,132},{6,135},{7,134},{8... | collective-permute-start | bytes 786440 | tf_op jit(solution)/shard_map/ppermute | solution.py:33
  39.9 10.7 %collective-permute-start.3 = (bf16[256,512]{1,0:T(8,128)(2,1)S(1)}, bf16[256,512]{1,0:T(8,128)(2,1)S(1)}, u32[]{:S(2)}, u32[]{:S(2)}) collective-permute-start(bf16[256,512]{1,0:T(8,128)(2,1)S(1)} %attend.2.refs_0_), channel_id=1, source_target_pairs={{0,1},{1,0},{2,3},{3,2},{4,5},{5,4},{6,7},{7,6},{8,9},{9,8},{10,11... | collective-permute-start | bytes 786440 | tf_op jit(solution)/shard_map/ppermute | solution.py:33
  39.9 12.4 %collective-permute-start.6 = (bf16[256,512]{1,0:T(8,128)(2,1)S(1)}, bf16[256,512]{1,0:T(8,128)(2,1)S(1)}, u32[]{:S(2)}, u32[]{:S(2)}) collective-permute-start(bf16[256,512]{1,0:T(8,128)(2,1)S(1)} %attend.3.refs_1_), channel_id=1, source_target_pairs={{0,129},{1,128},{2,131},{3,130},{4,133},{5,132},{6,135},{7,134},{8... | collective-permute-start | bytes 786440 | tf_op jit(solution)/shard_map/ppermute | solution.py:33
  48.0 5.5 %collective-permute-start.17 = (bf16[64,1792]{1,0:T(8,128)(2,1)S(1)}, bf16[64,1792]{1,0:T(8,128)(2,1)S(1)}, u32[]{:S(2)}, u32[]{:S(2)}) collective-permute-start(bf16[64,1792]{1,0:T(8,128)(2,1)S(1)} %slice.96), channel_id=1, source_target_pairs={{0,112},{1,113},{2,114},{3,115},{4,116},{5,117},{6,118},{7,119},{8... | collective-permute-start | bytes 688136 | tf_op jit(solution)/shard_map/ppermute | solution.py:33
  50.4 11.3 %collective-permute-start.16 = (bf16[128,1792]{1,0:T(8,128)(2,1)S(1)}, bf16[128,1792]{1,0:T(8,128)(2,1)S(1)}, u32[]{:S(2)}, u32[]{:S(2)}) collective-permute-start(bf16[128,1792]{1,0:T(8,128)(2,1)S(1)} %collective-permute-done.15.refs_13_), channel_id=1, source_target_pairs={{0,16},{1,17},{2,18},{3,19},{4,20},{5,21},{6,22},{7,23},{8,24},{9,... | collective-permute-start | bytes 1376264 | tf_op jit(solution)/shard_map/ppermute | solution.py:33
  50.4 6.4 %collective-permute-start.4 = (bf16[256,512]{1,0:T(8,128)(2,1)S(1)}, bf16[256,512]{1,0:T(8,128)(2,1)S(1)}, u32[]{:S(2)}, u32[]{:S(2)}) collective-permute-start(bf16[256,512]{1,0:T(8,128)(2,1)S(1)} %attend.3.refs_1_), channel_id=1, source_target_pairs={{0,1},{1,0},{2,3},{3,2},{4,5},{5,4},{6,7},{7,6},{8,9},{9,8},{10,11... | collective-permute-start | bytes 786440 | tf_op jit(solution)/shard_map/ppermute | solution.py:33
  50.6 6.9 %collective-permute-start.5 = (bf16[256,512]{1,0:T(8,128)(2,1)S(1)}, bf16[256,512]{1,0:T(8,128)(2,1)S(1)}, u32[]{:S(2)}, u32[]{:S(2)}) collective-permute-start(bf16[256,512]{1,0:T(8,128)(2,1)S(1)} %collective-permute-done.3.refs_2_), channel_id=1, source_target_pairs={{0,129},{1,128},{2,131},{3,130},{4,133},{5,132},{6,135},{7,134},{8... | collective-permute-start | bytes 786440 | tf_op jit(solution)/shard_map/ppermute | solution.py:33
  52.3 9.4 %collective-permute-start.7 = (bf16[256,512]{1,0:T(8,128)(2,1)S(1)}, bf16[256,512]{1,0:T(8,128)(2,1)S(1)}, u32[]{:S(2)}, u32[]{:S(2)}) collective-permute-start(bf16[256,512]{1,0:T(8,128)(2,1)S(1)} %collective-permute-done.6.refs_7_), channel_id=1, source_target_pairs={{0,1},{1,0},{2,3},{3,2},{4,5},{5,4},{6,7},{7,6},{8,9},{9,8},{10,11... | collective-permute-start | bytes 786440 | tf_op jit(solution)/shard_map/ppermute | solution.py:33
  53.4 8.3 %collective-permute-start.18 = (bf16[64,1792]{1,0:T(8,128)(2,1)S(1)}, bf16[64,1792]{1,0:T(8,128)(2,1)S(1)}, u32[]{:S(2)}, u32[]{:S(2)}) collective-permute-start(bf16[64,1792]{1,0:T(8,128)(2,1)S(1)} %collective-permute-done.17.refs_17_), channel_id=1, source_target_pairs={{0,112},{1,113},{2,114},{3,115},{4,116},{5,117},{6,118},{7,119},{8... | collective-permute-start | bytes 688136 | tf_op jit(solution)/shard_map/ppermute | solution.py:33
  64.1 6.0 %collective-permute-start.19 = (bf16[3,256,896]{2,1,0:T(8,128)(2,1)S(1)}, bf16[3,256,896]{2,1,0:T(8,128)(2,1)S(1)}, u32[]{:S(2)}, u32[]{:S(2)}) collective-permute-start(bf16[3,256,896]{2,1,0:T(8,128)(2,1)S(1)} %get-tuple-element.34), channel_id=1, source_target_pairs={{0,2},{1,3},{2,0},{3,1},{4,6},{5,7},{6,4},{7,5},{8,10},{9,11},{10,... | collective-permute-start | bytes 4128776 | tf_op jit(solution)/shard_map/ppermute | solution.py:33
  67.3 3.4 %collective-permute-start.20 = (bf16[256,896]{1,0:T(8,128)(2,1)S(1)}, bf16[256,896]{1,0:T(8,128)(2,1)S(1)}, u32[]{:S(2)}, u32[]{:S(2)}) collective-permute-start(bf16[256,896]{1,0:T(8,128)(2,1)S(1)} %get-tuple-element.35), channel_id=1, source_target_pairs={{0,2},{1,3},{2,0},{3,1},{4,6},{5,7},{6,4},{7,5},{8,10},{9,11},{10,... | collective-permute-start | bytes 1376264 | tf_op jit(solution)/shard_map/ppermute | solution.py:33
  70.7 7.1 %collective-permute-start.21 = (bf16[128,896]{1,0:T(8,128)(2,1)S(1)}, bf16[128,896]{1,0:T(8,128)(2,1)S(1)}, u32[]{:S(2)}, u32[]{:S(2)}) collective-permute-start(bf16[128,896]{1,0:T(8,128)(2,1)S(1)} %fusion.10), channel_id=1, source_target_pairs={{0,12},{1,13},{2,14},{3,15},{4,0},{5,1},{6,2},{7,3},{8,4},{9,5},{1... | collective-permute-start | bytes 688136 | tf_op jit(solution)/shard_map/ppermute | solution.py:33
  73.2 7.7 %collective-permute-start.25 = (bf16[128,896]{1,0:T(8,128)(2,1)S(1)}, bf16[128,896]{1,0:T(8,128)(2,1)S(1)}, u32[]{:S(2)}, u32[]{:S(2)}) collective-permute-start(bf16[128,896]{1,0:T(8,128)(2,1)S(1)} %fusion.9), channel_id=1, source_target_pairs={{0,4},{1,5},{2,6},{3,7},{4,8},{5,9},{6,10},{7,11},{8,12},{9,13},{1... | collective-permute-start | bytes 688136 | tf_op jit(solution)/shard_map/ppermute | solution.py:33
  73.3 13.8 %collective-permute-start.27 = (bf16[128,896]{1,0:T(8,128)(2,1)S(1)}, bf16[128,896]{1,0:T(8,128)(2,1)S(1)}, u32[]{:S(2)}, u32[]{:S(2)}) collective-permute-start(bf16[128,896]{1,0:T(8,128)(2,1)S(1)} %get-tuple-element.48), channel_id=1, source_target_pairs={{0,12},{1,13},{2,14},{3,15},{4,0},{5,1},{6,2},{7,3},{8,4},{9,5},{1... | collective-permute-start | bytes 688136 | tf_op jit(solution)/shard_map/ppermute | solution.py:33
  76.1 12.7 %collective-permute-start.23 = (bf16[128,896]{1,0:T(8,128)(2,1)S(1)}, bf16[128,896]{1,0:T(8,128)(2,1)S(1)}, u32[]{:S(2)}, u32[]{:S(2)}) collective-permute-start(bf16[128,896]{1,0:T(8,128)(2,1)S(1)} %get-tuple-element.49), channel_id=1, source_target_pairs={{0,4},{1,5},{2,6},{3,7},{4,8},{5,9},{6,10},{7,11},{8,12},{9,13},{1... | collective-permute-start | bytes 688136 | tf_op jit(solution)/shard_map/ppermute | solution.py:33
  81.0 10.6 %collective-permute-start.26 = (bf16[128,896]{1,0:T(8,128)(2,1)S(1)}, bf16[128,896]{1,0:T(8,128)(2,1)S(1)}, u32[]{:S(2)}, u32[]{:S(2)}) collective-permute-start(bf16[128,896]{1,0:T(8,128)(2,1)S(1)} %get-tuple-element.46), channel_id=1, source_target_pairs={{0,1},{1,0},{2,129},{3,128},{4,5},{5,4},{6,133},{7,132},{8,9},{9,8... | collective-permute-start | bytes 688136 | tf_op jit(solution)/shard_map/ppermute | solution.py:33
  85.2 10.0 %collective-permute-start.22 = (bf16[128,896]{1,0:T(8,128)(2,1)S(1)}, bf16[128,896]{1,0:T(8,128)(2,1)S(1)}, u32[]{:S(2)}, u32[]{:S(2)}) collective-permute-start(bf16[128,896]{1,0:T(8,128)(2,1)S(1)} %get-tuple-element.47), channel_id=1, source_target_pairs={{0,0},{1,1},{2,128},{3,129},{4,4},{5,5},{6,132},{7,133},{8,8},{9,9... | collective-permute-start | bytes 688136 | tf_op jit(solution)/shard_map/ppermute | solution.py:33
  87.2 9.2 %collective-permute-start.28 = (bf16[128,896]{1,0:T(8,128)(2,1)S(1)}, bf16[128,896]{1,0:T(8,128)(2,1)S(1)}, u32[]{:S(2)}, u32[]{:S(2)}) collective-permute-start(bf16[128,896]{1,0:T(8,128)(2,1)S(1)} %fusion.2), channel_id=1, source_target_pairs={{0,13},{1,12},{2,141},{3,140},{4,1},{5,0},{6,129},{7,128},{8,5},{9... | collective-permute-start | bytes 688136 | tf_op jit(solution)/shard_map/ppermute | solution.py:33
  88.8 10.5 %collective-permute-start.24 = (bf16[128,896]{1,0:T(8,128)(2,1)S(1)}, bf16[128,896]{1,0:T(8,128)(2,1)S(1)}, u32[]{:S(2)}, u32[]{:S(2)}) collective-permute-start(bf16[128,896]{1,0:T(8,128)(2,1)S(1)} %fusion.6), channel_id=1, source_target_pairs={{0,4},{1,5},{2,132},{3,133},{4,8},{5,9},{6,136},{7,137},{8,12},{9,... | collective-permute-start | bytes 688136 | tf_op jit(solution)/shard_map/ppermute | solution.py:33

commit v14 on v12

--- a/solution.py
+++ b/solution.py
@@ -2,7 +2,6 @@
 
 import jax
 import jax.numpy as jnp
-import numpy as np
 from jax import lax
 from jax.experimental import pallas as pl
 from jax.experimental.pallas import tpu as pltpu
@@ -171,12 +170,12 @@
 
 
 def turns(first):
-    inverse = (10000.0 ** (-np.arange(32) * (2.0 / 64))).astype(np.float32)
-    lane = np.arange(128)[None, :]
-    place = (np.arange(64)[:, None] + (lane // 32) * 64).astype(np.float32)
-    start = first.astype(F32)
-    own = (start + place) * np.tile(inverse, 4)[None, :]
-    every = (start - 512 + np.arange(768, dtype=np.float32)[None, :]) * inverse[:, None]
+    inverse = jnp.power(jnp.float32(10000.0), -jnp.arange(32, dtype=F32) * (2.0 / 64))
+    row = lax.broadcasted_iota(jnp.int32, (64, 128), 0)
+    lane = lax.broadcasted_iota(jnp.int32, (64, 128), 1)
+    own = (first + (lane // 32) * 64 + row).astype(F32) * jnp.tile(inverse, 4)[None, :]
+    place = first - 512 + lax.broadcasted_iota(jnp.int32, (32, 768), 1)
+    every = place.astype(F32) * inverse[:, None]
     return jnp.cos(own), jnp.sin(own), jnp.cos(every), jnp.sin(every)
 
 
@@ -307,7 +306,7 @@
     own_keys = key_rows.T
     half = lax.dynamic_slice_in_dim(own_keys, 128 * c, 128, 1)
     near, far = (
-        lax.ppermute(half, CTX, [(i, i + by) for i in range(16 - by)]) for by in (1, 2)
+        lax.ppermute(half, CTX, [(i, (i + by) % 16) for i in range(16)]) for by in (1, 2)
     )
     cosines, sines, all_cosines, all_sines = turns(slab * 256)
     queries = call(

time: 105 us -> 101 us (0.962)
  starting transfers between devices: 48.4 us -> 43.5 us
    ppermute x2, starting transfers between devices: 9.27 us -> 5.46 us  [local(): lax.ppermute(half, CTX, [(i, (i + by) % 16) for i in range(16)])]
    ppermute x25, starting transfers between devices: 39.1 us -> 38 us  [moved(): return lax.ppermute(a, AXES, pairs)]
  transfers between devices with their start and end apart: 27 -> 27, of which waited for: 15 -> 13; matrix products, arithmetic and copies ran while one was open for 2% -> 2% of each run, Pallas kernels for 18% -> 19%
where the time goes in v14:
time: 101 us
  starting transfers between devices  43.5 us (43%)
  waiting for transfers between devices  29.4 us (29%)
  Pallas kernels  21.7 us (21%)
  other arithmetic  3.02 us (3%)
  local copies, waits for them, and re-layouts  2.03 us (2%)
    ppermute x25, starting transfers between devices, moved(): return lax.ppermute(a, AXES, pairs)  38 us
    ppermute x25, waiting for transfers between devices, moved(): return lax.ppermute(a, AXES, pairs)  29.4 us
    pallas_call x5, Pallas kernels, call(): pl.pallas_call(kernel, out_shape=shapes, in_specs=specs, out_specs=whole(...  19.5 us
    ppermute x2, starting transfers between devices, local(): lax.ppermute(half, CTX, [(i, (i + by) % 16) for i in range(16)])  5.46 us
    pallas_call x1, Pallas kernels, quarters(): pl.pallas_call(quarter_kernel, out_shape=[jax.ShapeDtypeStruct((64, 1792)...  2.21 us
  transfers between devices with their start and end apart: 27, of which 13 were waited for; matrix products, arithmetic and copies ran while one was open for 2% of the time, Pallas kernels for 19%

profile of v14, /device:TPU:1, one launch (start us, length us, event | category | flops | bytes accessed | tf_op | source)
XLA Modules:
  0.0 100.6 jit_solution(15811364436357082465)
XLA Ops:
  0.0 1.6 %dynamic-slice_bitcast_fusion = bf16[576,128]{1,0:T(8,128)(2,1)} fusion(bf16[256,576]{0,1:T(8,128)(2,1)} %param.9, s32[]{:T(128)S(6)} %select_n.72), kind=kLoop, calls=%fused_computation.30 | loop fusion | bytes 294916 | tf_op jit(solution)/shard_map/dynamic_slice | solution.py:307
  1.6 3.8 %collective-permute-start.1 = (bf16[576,128]{1,0:T(8,128)(2,1)}, bf16[576,128]{1,0:T(8,128)(2,1)S(1)}, u32[]{:S(2)}, u32[]{:S(2)}) collective-permute-start(bf16[576,128]{1,0:T(8,128)(2,1)} %dynamic-slice_bitcast_fusion), channel_id=1, source_target_pairs={{0,32},{16,48},{32,64},{48,80},{64,96},{80,112},{96,128},{112,144}... | collective-permute-start | bytes 442376 | tf_op jit(solution)/shard_map/ppermute | solution.py:309
  5.4 1.6 %collective-permute-start = (bf16[576,128]{1,0:T(8,128)(2,1)}, bf16[576,128]{1,0:T(8,128)(2,1)S(1)}, u32[]{:S(2)}, u32[]{:S(2)}) collective-permute-start(bf16[576,128]{1,0:T(8,128)(2,1)} %dynamic-slice_bitcast_fusion), channel_id=1, source_target_pairs={{0,16},{16,32},{32,48},{48,64},{64,80},{80,96},{96,112},{112,128},... | collective-permute-start | bytes 442376 | tf_op jit(solution)/shard_map/ppermute | solution.py:309
  7.0 2.2 %quarters.1 = (bf16[64,1792]{1,0:T(8,128)(2,1)}, bf16[64,1792]{1,0:T(8,128)(2,1)}) custom-call(bf16[64,7168]{1,0:T(8,128)(2,1)} %bitcast.35), custom_call_target="tpu_custom_call" | custom-call | bytes 2097152 | tf_op jit(solution)/shard_map/quarters/pallas_call | solution.py:251
  9.2 2.8 %collective-permute-start.11 = (bf16[64,1792]{1,0:T(8,128)(2,1)}, bf16[64,1792]{1,0:T(8,128)(2,1)S(1)}, u32[]{:S(2)}, u32[]{:S(2)}) collective-permute-start(bf16[64,1792]{1,0:T(8,128)(2,1)} %get-tuple-element.27.refs_5_), channel_id=1, source_target_pairs={{0,16},{1,17},{2,18},{3,19},{4,20},{5,21},{6,22},{7,23},{8,24},{9,... | collective-permute-start | bytes 688136 | tf_op jit(solution)/shard_map/ppermute | solution.py:33
  12.1 0.8 collective-permute-start.7
  12.9 1.9 %collective-permute-start.8 = (bf16[64,1792]{1,0:T(8,128)(2,1)}, bf16[64,1792]{1,0:T(8,128)(2,1)S(1)}, u32[]{:S(2)}, u32[]{:S(2)}) collective-permute-start(bf16[64,1792]{1,0:T(8,128)(2,1)} %get-tuple-element.28), channel_id=1, source_target_pairs={{0,129},{1,128},{2,131},{3,130},{4,133},{5,132},{6,135},{7,134},{8... | collective-permute-start | bytes 688136 | tf_op jit(solution)/shard_map/ppermute | solution.py:33
  15.0 0.1 fusion.reorder
  15.1 0.8 fusion.11
  15.9 6.9 %queries.1 = (bf16[1024,640]{1,0:T(8,128)(2,1)}, bf16[1024,640]{1,0:T(8,128)(2,1)}) custom-call(bf16[256,1536]{1,0:T(8,128)(2,1)} %rows.1, bf16[1536,1536]{1,0:T(8,128)(2,1)} %w_query.1, bf16[8,128,512]{2,1,0:T(8,128)(2,1)} %w_key_up.1, f32[64,128]{1,0:T(8,128)} %get-tuple-element.59.cosines, f32[64,128]{1,0:T(8,128)} %get-tuple-element.58.sines), custom_call_target="tpu_custom_call" | custom-call | flops 1476395008 | bytes 8388608 | tf_op jit(solution)/shard_map/queries/pallas_call | solution.py:263
  22.9 2.0 %collective-permute-start.2 = (bf16[576,256]{1,0:T(8,128)(2,1)S(1)}, bf16[576,256]{1,0:T(8,128)(2,1)S(1)}, u32[]{:S(2)}, u32[]{:S(2)}) collective-permute-start(bf16[576,256]{1,0:T(8,128)(2,1)S(1)} %pad_maximum_fusion.2), channel_id=1, source_target_pairs={{0,2},{1,3},{2,0},{3,1},{4,6},{5,7},{6,4},{7,5},{8,10},{9,11},{10,... | collective-permute-start | bytes 884744 | tf_op jit(solution)/shard_map/ppermute | solution.py:33
  25.0 0.6 collective-permute-start.9
  25.6 1.2 %collective-permute-start.12 = (bf16[128,1792]{1,0:T(8,128)(2,1)S(1)}, bf16[128,1792]{1,0:T(8,128)(2,1)S(1)}, u32[]{:S(2)}, u32[]{:S(2)}) collective-permute-start(bf16[128,1792]{1,0:T(8,128)(2,1)S(1)} %get-tuple-element.31), channel_id=1, source_target_pairs={{0,16},{1,17},{2,18},{3,19},{4,20},{5,21},{6,22},{7,23},{8,24},{9,... | collective-permute-start | bytes 1376264 | tf_op jit(solution)/shard_map/ppermute | solution.py:33
  26.8 0.4 multiply_sine_fusion
  27.9 0.6 keys.1
  28.6 7.4 %attend.1.refs_0_ = bf16[256,1024]{1,0:T(8,128)(2,1)S(1)} custom-call(bf16[1024,640]{1,0:T(8,128)(2,1)S(1)} %copy-done.2, bf16[1024,640]{1,0:T(8,128)(2,1)S(1)} %copy-done.3, bf16[640,768]{1,0:T(8,128)(2,1)S(1)} %get-tuple-element.25.keys, f32[256,768]{1,0:T(8,128)S(1)} %get-tuple-element.26.hidden, bf16[8,512,128]{2,1,0:T(8,128)(2,1)S(1)} %copy-done.4, ...), custom_call_target="tpu_custom_call" | custom-call | flops 3892314112 | bytes 10485760 | tf_op jit(solution)/shard_map/attend/pallas_call | solution.py:263
  36.0 0.7 collective-permute-done.9.refs_7_
  36.6 2.2 %collective-permute-start.10 = (bf16[128,1792]{1,0:T(8,128)(2,1)S(1)}, bf16[128,1792]{1,0:T(8,128)(2,1)S(1)}, u32[]{:S(2)}, u32[]{:S(2)}) collective-permute-start(bf16[128,1792]{1,0:T(8,128)(2,1)S(1)} %collective-permute-done.9.refs_7_), channel_id=1, source_target_pairs={{0,112},{1,113},{2,114},{3,115},{4,116},{5,117},{6,118},{7,119},{8... | collective-permute-start | bytes 1376264 | tf_op jit(solution)/shard_map/ppermute | solution.py:33
  38.9 1.6 %collective-permute-start.5 = (bf16[256,1024]{1,0:T(8,128)(2,1)S(1)}, bf16[256,1024]{1,0:T(8,128)(2,1)S(1)}, u32[]{:S(2)}, u32[]{:S(2)}) collective-permute-start(bf16[256,1024]{1,0:T(8,128)(2,1)S(1)} %attend.1.refs_0_), channel_id=1, source_target_pairs={{0,129},{1,128},{2,131},{3,130},{4,133},{5,132},{6,135},{7,134},{8... | collective-permute-start | bytes 1572872 | tf_op jit(solution)/shard_map/ppermute | solution.py:33
  40.4 8.2 %collective-permute-done.10.refs_8_ = bf16[128,1792]{1,0:T(8,128)(2,1)S(1)} collective-permute-done((bf16[128,1792]{1,0:T(8,128)(2,1)S(1)}, bf16[128,1792]{1,0:T(8,128)(2,1)S(1)}, u32[]{:S(2)}, u32[]{:S(2)}) %collective-permute-start.10) | collective-permute-done | bytes 458784 | tf_op jit(solution)/shard_map/ppermute | solution.py:33
  48.6 2.7 %collective-permute-start.15 = (bf16[64,1792]{1,0:T(8,128)(2,1)S(1)}, bf16[64,1792]{1,0:T(8,128)(2,1)S(1)}, u32[]{:S(2)}, u32[]{:S(2)}) collective-permute-start(bf16[64,1792]{1,0:T(8,128)(2,1)S(1)} %slice.106), channel_id=1, source_target_pairs={{0,112},{1,113},{2,114},{3,115},{4,116},{5,117},{6,118},{7,119},{8... | collective-permute-start | bytes 688136 | tf_op jit(solution)/shard_map/ppermute | solution.py:33
  51.3 0.8 collective-permute-done.5.refs_4_
  52.3 1.5 %collective-permute-start.4 = (bf16[128,1024]{1,0:T(8,128)(2,1)S(1)}, bf16[128,1024]{1,0:T(8,128)(2,1)S(1)}, u32[]{:S(2)}, u32[]{:S(2)}) collective-permute-start(bf16[128,1024]{1,0:T(8,128)(2,1)S(1)} %slice.104), channel_id=1, source_target_pairs={{0,129},{1,128},{2,131},{3,130},{4,133},{5,132},{6,135},{7,134},{8... | collective-permute-start | bytes 786440 | tf_op jit(solution)/shard_map/ppermute | solution.py:33
  53.8 0.5 collective-permute-done.15.refs_14_
  54.3 3.6 %collective-permute-start.16 = (bf16[64,1792]{1,0:T(8,128)(2,1)S(1)}, bf16[64,1792]{1,0:T(8,128)(2,1)S(1)}, u32[]{:S(2)}, u32[]{:S(2)}) collective-permute-start(bf16[64,1792]{1,0:T(8,128)(2,1)S(1)} %collective-permute-done.15.refs_14_), channel_id=1, source_target_pairs={{0,112},{1,113},{2,114},{3,115},{4,116},{5,117},{6,118},{7,119},{8... | collective-permute-start | bytes 688136 | tf_op jit(solution)/shard_map/ppermute | solution.py:33
  57.9 1.2 %collective-permute-done.4.refs_2_ = bf16[128,1024]{1,0:T(8,128)(2,1)S(1)} collective-permute-done((bf16[128,1024]{1,0:T(8,128)(2,1)S(1)}, bf16[128,1024]{1,0:T(8,128)(2,1)S(1)}, u32[]{:S(2)}, u32[]{:S(2)}) %collective-permute-start.4) | collective-permute-done | bytes 262176 | tf_op jit(solution)/shard_map/ppermute | solution.py:33
  59.1 1.7 %collective-permute-done.16.refs_15_ = bf16[64,1792]{1,0:T(8,128)(2,1)S(1)} collective-permute-done((bf16[64,1792]{1,0:T(8,128)(2,1)S(1)}, bf16[64,1792]{1,0:T(8,128)(2,1)S(1)}, u32[]{:S(2)}, u32[]{:S(2)}) %collective-permute-start.16) | collective-permute-done | bytes 229408 | tf_op jit(solution)/shard_map/ppermute | solution.py:33
  60.8 1.7 %collective-permute-done.14.refs_9_ = bf16[128,1792]{1,0:T(8,128)(2,1)S(1)} collective-permute-done((bf16[128,1792]{1,0:T(8,128)(2,1)S(1)}, bf16[128,1792]{1,0:T(8,128)(2,1)S(1)}, u32[]{:S(2)}, u32[]{:S(2)}) %collective-permute-start.14) | collective-permute-done | bytes 458784 | tf_op jit(solution)/shard_map/ppermute | solution.py:33
  62.5 2.3 %project.3 = (bf16[256,896]{1,0:T(8,128)(2,1)S(1)}, bf16[3,256,896]{2,1,0:T(8,128)(2,1)S(1)}) custom-call(bf16[256,1024]{1,0:T(8,128)(2,1)S(1)} %attend.1.refs_0_, bf16[256,1024]{1,0:T(8,128)(2,1)S(1)} %collective-permute-done.3.refs_1_, bf16[128,1024]{1,0:T(8,128)(2,1)S(1)} %collective-permute-done.4.refs_2_, ...), custom_call_target="tpu_custom_call" | custom-call | flops 1879048192 | bytes 8388608 | tf_op jit(solution)/shard_map/project/pallas_call | solution.py:263
  64.8 3.1 %collective-permute-start.17 = (bf16[3,256,896]{2,1,0:T(8,128)(2,1)S(1)}, bf16[3,256,896]{2,1,0:T(8,128)(2,1)S(1)}, u32[]{:S(2)}, u32[]{:S(2)}) collective-permute-start(bf16[3,256,896]{2,1,0:T(8,128)(2,1)S(1)} %get-tuple-element.34), channel_id=1, source_target_pairs={{0,2},{1,3},{2,0},{3,1},{4,6},{5,7},{6,4},{7,5},{8,10},{9,11},{10,... | collective-permute-start | bytes 4128776 | tf_op jit(solution)/shard_map/ppermute | solution.py:33
  67.9 2.3 %project.2 = (f32[256,896]{1,0:T(8,128)S(1)}, f32[3,256,896]{2,1,0:T(8,128)S(1)}) custom-call(bf16[256,1024]{1,0:T(8,128)(2,1)S(1)} %attend.1.refs_0_, bf16[256,1024]{1,0:T(8,128)(2,1)S(1)} %collective-permute-done.3.refs_1_, bf16[128,1024]{1,0:T(8,128)(2,1)S(1)} %collective-permute-done.4.refs_2_, bf16[128,1024]{1,0:T(8,128)(2,1)S(1)} %collective-permute-done.6.refs_3_, ...), custom_call_target="tpu_custom_call" | custom-call | flops 1879048192 | bytes 8388608 | tf_op jit(solution)/shard_map/project/pallas_call | solution.py:263
  70.3 0.3 collective-permute-done.17
  70.6 0.2 convert_add_fusion.2
  70.9 0.4 collective-permute-done.18
  71.2 2.5 %collective-permute-start.19 = (bf16[128,896]{1,0:T(8,128)(2,1)S(1)}, bf16[128,896]{1,0:T(8,128)(2,1)S(1)}, u32[]{:S(2)}, u32[]{:S(2)}) collective-permute-start(bf16[128,896]{1,0:T(8,128)(2,1)S(1)} %fusion.10), channel_id=1, source_target_pairs={{0,12},{1,13},{2,14},{3,15},{4,0},{5,1},{6,2},{7,3},{8,4},{9,5},{1... | collective-permute-start | bytes 688136 | tf_op jit(solution)/shard_map/ppermute | solution.py:33
  73.9 2.8 %collective-permute-start.25 = (bf16[128,896]{1,0:T(8,128)(2,1)S(1)}, bf16[128,896]{1,0:T(8,128)(2,1)S(1)}, u32[]{:S(2)}, u32[]{:S(2)}) collective-permute-start(bf16[128,896]{1,0:T(8,128)(2,1)S(1)} %get-tuple-element.48), channel_id=1, source_target_pairs={{0,12},{1,13},{2,14},{3,15},{4,0},{5,1},{6,2},{7,3},{8,4},{9,5},{1... | collective-permute-start | bytes 688136 | tf_op jit(solution)/shard_map/ppermute | solution.py:33
  76.6 1.7 %collective-permute-done.19 = bf16[128,896]{1,0:T(8,128)(2,1)S(1)} collective-permute-done((bf16[128,896]{1,0:T(8,128)(2,1)S(1)}, bf16[128,896]{1,0:T(8,128)(2,1)S(1)}, u32[]{:S(2)}, u32[]{:S(2)}) %collective-permute-start.19) | collective-permute-done | bytes 229408 | tf_op jit(solution)/shard_map/ppermute | solution.py:33
  78.3 3.1 %collective-permute-done.23 = bf16[128,896]{1,0:T(8,128)(2,1)S(1)} collective-permute-done((bf16[128,896]{1,0:T(8,128)(2,1)S(1)}, bf16[128,896]{1,0:T(8,128)(2,1)S(1)}, u32[]{:S(2)}, u32[]{:S(2)}) %collective-permute-start.23) | collective-permute-done | bytes 229408 | tf_op jit(solution)/shard_map/ppermute | solution.py:33
  81.5 3.8 %collective-permute-start.24 = (bf16[128,896]{1,0:T(8,128)(2,1)S(1)}, bf16[128,896]{1,0:T(8,128)(2,1)S(1)}, u32[]{:S(2)}, u32[]{:S(2)}) collective-permute-start(bf16[128,896]{1,0:T(8,128)(2,1)S(1)} %get-tuple-element.46), channel_id=1, source_target_pairs={{0,1},{1,0},{2,129},{3,128},{4,5},{5,4},{6,133},{7,132},{8,9},{9,8... | collective-permute-start | bytes 688136 | tf_op jit(solution)/shard_map/ppermute | solution.py:33
  85.3 1.9 %collective-permute-start.20 = (bf16[128,896]{1,0:T(8,128)(2,1)S(1)}, bf16[128,896]{1,0:T(8,128)(2,1)S(1)}, u32[]{:S(2)}, u32[]{:S(2)}) collective-permute-start(bf16[128,896]{1,0:T(8,128)(2,1)S(1)} %get-tuple-element.47), channel_id=1, source_target_pairs={{0,0},{1,1},{2,128},{3,129},{4,4},{5,5},{6,132},{7,133},{8,8},{9,9... | collective-permute-start | bytes 688136 | tf_op jit(solution)/shard_map/ppermute | solution.py:33
  87.3 1.5 %collective-permute-start.26 = (bf16[128,896]{1,0:T(8,128)(2,1)S(1)}, bf16[128,896]{1,0:T(8,128)(2,1)S(1)}, u32[]{:S(2)}, u32[]{:S(2)}) collective-permute-start(bf16[128,896]{1,0:T(8,128)(2,1)S(1)} %fusion.2), channel_id=1, source_target_pairs={{0,13},{1,12},{2,141},{3,140},{4,1},{5,0},{6,129},{7,128},{8,5},{9... | collective-permute-start | bytes 688136 | tf_op jit(solution)/shard_map/ppermute | solution.py:33
  88.9 1.4 %collective-permute-start.22 = (bf16[128,896]{1,0:T(8,128)(2,1)S(1)}, bf16[128,896]{1,0:T(8,128)(2,1)S(1)}, u32[]{:S(2)}, u32[]{:S(2)}) collective-permute-start(bf16[128,896]{1,0:T(8,128)(2,1)S(1)} %fusion.6), channel_id=1, source_target_pairs={{0,4},{1,5},{2,132},{3,133},{4,8},{5,9},{6,136},{7,137},{8,12},{9,... | collective-permute-start | bytes 688136 | tf_op jit(solution)/shard_map/ppermute | solution.py:33
  90.2 7.7 %collective-permute-done.20 = bf16[128,896]{1,0:T(8,128)(2,1)S(1)} collective-permute-done((bf16[128,896]{1,0:T(8,128)(2,1)S(1)}, bf16[128,896]{1,0:T(8,128)(2,1)S(1)}, u32[]{:S(2)}, u32[]{:S(2)}) %collective-permute-start.20) | collective-permute-done | bytes 229408 | tf_op jit(solution)/shard_map/ppermute | solution.py:33
  98.0 1.4 %collective-permute-done.22 = bf16[128,896]{1,0:T(8,128)(2,1)S(1)} collective-permute-done((bf16[128,896]{1,0:T(8,128)(2,1)S(1)}, bf16[128,896]{1,0:T(8,128)(2,1)S(1)}, u32[]{:S(2)}, u32[]{:S(2)}) %collective-permute-start.22) | collective-permute-done | bytes 229408 | tf_op jit(solution)/shard_map/ppermute | solution.py:33
  99.4 0.1 broadcast_select_fusion.1
  99.5 0.1 fusion.33
  99.6 0.1 fusion.34
  99.7 0.9 maximum_maximum_fusion
  (52 shorter events, 0.9 us)
Async XLA Ops:
  1.6 21.3 %collective-permute-start.1 = (bf16[576,128]{1,0:T(8,128)(2,1)}, bf16[576,128]{1,0:T(8,128)(2,1)S(1)}, u32[]{:S(2)}, u32[]{:S(2)}) collective-permute-start(bf16[576,128]{1,0:T(8,128)(2,1)} %dynamic-slice_bitcast_fusion), channel_id=1, source_target_pairs={{0,32},{16,48},{32,64},{48,80},{64,96},{80,112},{96,128},{112,144}... | collective-permute-start | bytes 442376 | tf_op jit(solution)/shard_map/ppermute | solution.py:309
  5.4 17.5 %collective-permute-start = (bf16[576,128]{1,0:T(8,128)(2,1)}, bf16[576,128]{1,0:T(8,128)(2,1)S(1)}, u32[]{:S(2)}, u32[]{:S(2)}) collective-permute-start(bf16[576,128]{1,0:T(8,128)(2,1)} %dynamic-slice_bitcast_fusion), channel_id=1, source_target_pairs={{0,16},{16,32},{32,48},{48,64},{64,80},{80,96},{96,112},{112,128},... | collective-permute-start | bytes 442376 | tf_op jit(solution)/shard_map/ppermute | solution.py:309
  9.2 15.7 %collective-permute-start.11 = (bf16[64,1792]{1,0:T(8,128)(2,1)}, bf16[64,1792]{1,0:T(8,128)(2,1)S(1)}, u32[]{:S(2)}, u32[]{:S(2)}) collective-permute-start(bf16[64,1792]{1,0:T(8,128)(2,1)} %get-tuple-element.27.refs_5_), channel_id=1, source_target_pairs={{0,16},{1,17},{2,18},{3,19},{4,20},{5,21},{6,22},{7,23},{8,24},{9,... | collective-permute-start | bytes 688136 | tf_op jit(solution)/shard_map/ppermute | solution.py:33
  12.1 12.9 %collective-permute-start.7 = (bf16[64,1792]{1,0:T(8,128)(2,1)}, bf16[64,1792]{1,0:T(8,128)(2,1)S(1)}, u32[]{:S(2)}, u32[]{:S(2)}) collective-permute-start(bf16[64,1792]{1,0:T(8,128)(2,1)} %get-tuple-element.27.refs_5_), channel_id=1, source_target_pairs={{0,112},{1,113},{2,114},{3,115},{4,116},{5,117},{6,118},{7,119},{8... | collective-permute-start | bytes 688136 | tf_op jit(solution)/shard_map/ppermute | solution.py:33
  12.9 12.0 %collective-permute-start.8 = (bf16[64,1792]{1,0:T(8,128)(2,1)}, bf16[64,1792]{1,0:T(8,128)(2,1)S(1)}, u32[]{:S(2)}, u32[]{:S(2)}) collective-permute-start(bf16[64,1792]{1,0:T(8,128)(2,1)} %get-tuple-element.28), channel_id=1, source_target_pairs={{0,129},{1,128},{2,131},{3,130},{4,133},{5,132},{6,135},{7,134},{8... | collective-permute-start | bytes 688136 | tf_op jit(solution)/shard_map/ppermute | solution.py:33
  15.9 12.6 %copy-start.4 = (bf16[8,512,128]{2,1,0:T(8,128)(2,1)S(1)}, bf16[8,512,128]{2,1,0:T(8,128)(2,1)}, u32[]{:S(2)}) copy-start(bf16[8,512,128]{2,1,0:T(8,128)(2,1)} %w_value_up.1) | copy-start | bytes 3145732
  22.8 5.1 %copy-start = (bf16[256,576]{0,1:T(8,128)(2,1)S(1)}, bf16[256,576]{0,1:T(8,128)(2,1)}, u32[]{:S(2)}) copy-start(bf16[256,576]{0,1:T(8,128)(2,1)} %param.9) | copy-start | bytes 884740
  22.8 5.1 %copy-start.1 = (bf16[512,576]{0,1:T(8,128)(2,1)S(1)}, bf16[512,576]{0,1:T(8,128)(2,1)}, u32[]{:S(2)}) copy-start(bf16[512,576]{0,1:T(8,128)(2,1)} %param.10) | copy-start | bytes 1769476
  22.9 5.6 %copy-start.2 = (bf16[1024,640]{1,0:T(8,128)(2,1)S(1)}, bf16[1024,640]{1,0:T(8,128)(2,1)}, u32[]{:S(2)}) copy-start(bf16[1024,640]{1,0:T(8,128)(2,1)} %get-tuple-element.23.queries) | copy-start | bytes 3932164
  22.9 5.6 %copy-start.3 = (bf16[1024,640]{1,0:T(8,128)(2,1)S(1)}, bf16[1024,640]{1,0:T(8,128)(2,1)}, u32[]{:S(2)}) copy-start(bf16[1024,640]{1,0:T(8,128)(2,1)} %get-tuple-element.24.queries_next) | copy-start | bytes 3932164
  22.9 5.0 %collective-permute-start.2 = (bf16[576,256]{1,0:T(8,128)(2,1)S(1)}, bf16[576,256]{1,0:T(8,128)(2,1)S(1)}, u32[]{:S(2)}, u32[]{:S(2)}) collective-permute-start(bf16[576,256]{1,0:T(8,128)(2,1)S(1)} %pad_maximum_fusion.2), channel_id=1, source_target_pairs={{0,2},{1,3},{2,0},{3,1},{4,6},{5,7},{6,4},{7,5},{8,10},{9,11},{10,... | collective-permute-start | bytes 884744 | tf_op jit(solution)/shard_map/ppermute | solution.py:33
  25.0 11.6 %collective-permute-start.9 = (bf16[128,1792]{1,0:T(8,128)(2,1)S(1)}, bf16[128,1792]{1,0:T(8,128)(2,1)S(1)}, u32[]{:S(2)}, u32[]{:S(2)}) collective-permute-start(bf16[128,1792]{1,0:T(8,128)(2,1)S(1)} %get-tuple-element.29), channel_id=1, source_target_pairs={{0,112},{1,113},{2,114},{3,115},{4,116},{5,117},{6,118},{7,119},{8... | collective-permute-start | bytes 1376264 | tf_op jit(solution)/shard_map/ppermute | solution.py:33
  25.6 13.3 %collective-permute-start.12 = (bf16[128,1792]{1,0:T(8,128)(2,1)S(1)}, bf16[128,1792]{1,0:T(8,128)(2,1)S(1)}, u32[]{:S(2)}, u32[]{:S(2)}) collective-permute-start(bf16[128,1792]{1,0:T(8,128)(2,1)S(1)} %get-tuple-element.31), channel_id=1, source_target_pairs={{0,16},{1,17},{2,18},{3,19},{4,20},{5,21},{6,22},{7,23},{8,24},{9,... | collective-permute-start | bytes 1376264 | tf_op jit(solution)/shard_map/ppermute | solution.py:33
  35.9 26.6 %copy-start.5 = (bf16[64,1792]{1,0:T(8,128)(2,1)S(1)}, bf16[64,1792]{1,0:T(8,128)(2,1)}, u32[]{:S(2)}) copy-start(bf16[64,1792]{1,0:T(8,128)(2,1)} %get-tuple-element.27.refs_5_) | copy-start | bytes 688132
  36.6 12.0 %collective-permute-start.10 = (bf16[128,1792]{1,0:T(8,128)(2,1)S(1)}, bf16[128,1792]{1,0:T(8,128)(2,1)S(1)}, u32[]{:S(2)}, u32[]{:S(2)}) collective-permute-start(bf16[128,1792]{1,0:T(8,128)(2,1)S(1)} %collective-permute-done.9.refs_7_), channel_id=1, source_target_pairs={{0,112},{1,113},{2,114},{3,115},{4,116},{5,117},{6,118},{7,119},{8... | collective-permute-start | bytes 1376264 | tf_op jit(solution)/shard_map/ppermute | solution.py:33
  38.9 12.5 %collective-permute-start.13 = (bf16[128,1792]{1,0:T(8,128)(2,1)S(1)}, bf16[128,1792]{1,0:T(8,128)(2,1)S(1)}, u32[]{:S(2)}, u32[]{:S(2)}) collective-permute-start(bf16[128,1792]{1,0:T(8,128)(2,1)S(1)} %collective-permute-done.12.refs_11_), channel_id=1, source_target_pairs={{0,16},{1,17},{2,18},{3,19},{4,20},{5,21},{6,22},{7,23},{8,24},{9,... | collective-permute-start | bytes 1376264 | tf_op jit(solution)/shard_map/ppermute | solution.py:33
  38.9 13.3 %collective-permute-start.5 = (bf16[256,1024]{1,0:T(8,128)(2,1)S(1)}, bf16[256,1024]{1,0:T(8,128)(2,1)S(1)}, u32[]{:S(2)}, u32[]{:S(2)}) collective-permute-start(bf16[256,1024]{1,0:T(8,128)(2,1)S(1)} %attend.1.refs_0_), channel_id=1, source_target_pairs={{0,129},{1,128},{2,131},{3,130},{4,133},{5,132},{6,135},{7,134},{8... | collective-permute-start | bytes 1572872 | tf_op jit(solution)/shard_map/ppermute | solution.py:33
  40.4 11.8 %collective-permute-start.3 = (bf16[256,1024]{1,0:T(8,128)(2,1)S(1)}, bf16[256,1024]{1,0:T(8,128)(2,1)S(1)}, u32[]{:S(2)}, u32[]{:S(2)}) collective-permute-start(bf16[256,1024]{1,0:T(8,128)(2,1)S(1)} %attend.1.refs_0_), channel_id=1, source_target_pairs={{0,1},{1,0},{2,3},{3,2},{4,5},{5,4},{6,7},{7,6},{8,9},{9,8},{10,11... | collective-permute-start | bytes 1572872 | tf_op jit(solution)/shard_map/ppermute | solution.py:33
  48.6 5.7 %collective-permute-start.15 = (bf16[64,1792]{1,0:T(8,128)(2,1)S(1)}, bf16[64,1792]{1,0:T(8,128)(2,1)S(1)}, u32[]{:S(2)}, u32[]{:S(2)}) collective-permute-start(bf16[64,1792]{1,0:T(8,128)(2,1)S(1)} %slice.106), channel_id=1, source_target_pairs={{0,112},{1,113},{2,114},{3,115},{4,116},{5,117},{6,118},{7,119},{8... | collective-permute-start | bytes 688136 | tf_op jit(solution)/shard_map/ppermute | solution.py:33
  51.3 11.2 %collective-permute-start.14 = (bf16[128,1792]{1,0:T(8,128)(2,1)S(1)}, bf16[128,1792]{1,0:T(8,128)(2,1)S(1)}, u32[]{:S(2)}, u32[]{:S(2)}) collective-permute-start(bf16[128,1792]{1,0:T(8,128)(2,1)S(1)} %collective-permute-done.13.refs_10_), channel_id=1, source_target_pairs={{0,16},{1,17},{2,18},{3,19},{4,20},{5,21},{6,22},{7,23},{8,24},{9,... | collective-permute-start | bytes 1376264 | tf_op jit(solution)/shard_map/ppermute | solution.py:33
  52.1 5.7 %collective-permute-start.6 = (bf16[128,1024]{1,0:T(8,128)(2,1)S(1)}, bf16[128,1024]{1,0:T(8,128)(2,1)S(1)}, u32[]{:S(2)}, u32[]{:S(2)}) collective-permute-start(bf16[128,1024]{1,0:T(8,128)(2,1)S(1)} %slice.105), channel_id=1, source_target_pairs={{0,1},{1,0},{2,3},{3,2},{4,5},{5,4},{6,7},{7,6},{8,9},{9,8},{10,11... | collective-permute-start | bytes 786440 | tf_op jit(solution)/shard_map/ppermute | solution.py:33
  52.3 6.8 %collective-permute-start.4 = (bf16[128,1024]{1,0:T(8,128)(2,1)S(1)}, bf16[128,1024]{1,0:T(8,128)(2,1)S(1)}, u32[]{:S(2)}, u32[]{:S(2)}) collective-permute-start(bf16[128,1024]{1,0:T(8,128)(2,1)S(1)} %slice.104), channel_id=1, source_target_pairs={{0,129},{1,128},{2,131},{3,130},{4,133},{5,132},{6,135},{7,134},{8... | collective-permute-start | bytes 786440 | tf_op jit(solution)/shard_map/ppermute | solution.py:33
  54.3 6.5 %collective-permute-start.16 = (bf16[64,1792]{1,0:T(8,128)(2,1)S(1)}, bf16[64,1792]{1,0:T(8,128)(2,1)S(1)}, u32[]{:S(2)}, u32[]{:S(2)}) collective-permute-start(bf16[64,1792]{1,0:T(8,128)(2,1)S(1)} %collective-permute-done.15.refs_14_), channel_id=1, source_target_pairs={{0,112},{1,113},{2,114},{3,115},{4,116},{5,117},{6,118},{7,119},{8... | collective-permute-start | bytes 688136 | tf_op jit(solution)/shard_map/ppermute | solution.py:33
  64.8 5.8 %collective-permute-start.17 = (bf16[3,256,896]{2,1,0:T(8,128)(2,1)S(1)}, bf16[3,256,896]{2,1,0:T(8,128)(2,1)S(1)}, u32[]{:S(2)}, u32[]{:S(2)}) collective-permute-start(bf16[3,256,896]{2,1,0:T(8,128)(2,1)S(1)} %get-tuple-element.34), channel_id=1, source_target_pairs={{0,2},{1,3},{2,0},{3,1},{4,6},{5,7},{6,4},{7,5},{8,10},{9,11},{10,... | collective-permute-start | bytes 4128776 | tf_op jit(solution)/shard_map/ppermute | solution.py:33
  67.8 3.4 %collective-permute-start.18 = (bf16[256,896]{1,0:T(8,128)(2,1)S(1)}, bf16[256,896]{1,0:T(8,128)(2,1)S(1)}, u32[]{:S(2)}, u32[]{:S(2)}) collective-permute-start(bf16[256,896]{1,0:T(8,128)(2,1)S(1)} %get-tuple-element.35), channel_id=1, source_target_pairs={{0,2},{1,3},{2,0},{3,1},{4,6},{5,7},{6,4},{7,5},{8,10},{9,11},{10,... | collective-permute-start | bytes 1376264 | tf_op jit(solution)/shard_map/ppermute | solution.py:33
  71.2 7.1 %collective-permute-start.19 = (bf16[128,896]{1,0:T(8,128)(2,1)S(1)}, bf16[128,896]{1,0:T(8,128)(2,1)S(1)}, u32[]{:S(2)}, u32[]{:S(2)}) collective-permute-start(bf16[128,896]{1,0:T(8,128)(2,1)S(1)} %fusion.10), channel_id=1, source_target_pairs={{0,12},{1,13},{2,14},{3,15},{4,0},{5,1},{6,2},{7,3},{8,4},{9,5},{1... | collective-permute-start | bytes 688136 | tf_op jit(solution)/shard_map/ppermute | solution.py:33
  73.7 7.7 %collective-permute-start.23 = (bf16[128,896]{1,0:T(8,128)(2,1)S(1)}, bf16[128,896]{1,0:T(8,128)(2,1)S(1)}, u32[]{:S(2)}, u32[]{:S(2)}) collective-permute-start(bf16[128,896]{1,0:T(8,128)(2,1)S(1)} %fusion.9), channel_id=1, source_target_pairs={{0,4},{1,5},{2,6},{3,7},{4,8},{5,9},{6,10},{7,11},{8,12},{9,13},{1... | collective-permute-start | bytes 688136 | tf_op jit(solution)/shard_map/ppermute | solution.py:33
  73.9 13.4 %collective-permute-start.25 = (bf16[128,896]{1,0:T(8,128)(2,1)S(1)}, bf16[128,896]{1,0:T(8,128)(2,1)S(1)}, u32[]{:S(2)}, u32[]{:S(2)}) collective-permute-start(bf16[128,896]{1,0:T(8,128)(2,1)S(1)} %get-tuple-element.48), channel_id=1, source_target_pairs={{0,12},{1,13},{2,14},{3,15},{4,0},{5,1},{6,2},{7,3},{8,4},{9,5},{1... | collective-permute-start | bytes 688136 | tf_op jit(solution)/shard_map/ppermute | solution.py:33
  76.6 12.2 %collective-permute-start.21 = (bf16[128,896]{1,0:T(8,128)(2,1)S(1)}, bf16[128,896]{1,0:T(8,128)(2,1)S(1)}, u32[]{:S(2)}, u32[]{:S(2)}) collective-permute-start(bf16[128,896]{1,0:T(8,128)(2,1)S(1)} %get-tuple-element.49), channel_id=1, source_target_pairs={{0,4},{1,5},{2,6},{3,7},{4,8},{5,9},{6,10},{7,11},{8,12},{9,13},{1... | collective-permute-start | bytes 688136 | tf_op jit(solution)/shard_map/ppermute | solution.py:33
  81.5 8.7 %collective-permute-start.24 = (bf16[128,896]{1,0:T(8,128)(2,1)S(1)}, bf16[128,896]{1,0:T(8,128)(2,1)S(1)}, u32[]{:S(2)}, u32[]{:S(2)}) collective-permute-start(bf16[128,896]{1,0:T(8,128)(2,1)S(1)} %get-tuple-element.46), channel_id=1, source_target_pairs={{0,1},{1,0},{2,129},{3,128},{4,5},{5,4},{6,133},{7,132},{8,9},{9,8... | collective-permute-start | bytes 688136 | tf_op jit(solution)/shard_map/ppermute | solution.py:33
  85.3 12.6 %collective-permute-start.20 = (bf16[128,896]{1,0:T(8,128)(2,1)S(1)}, bf16[128,896]{1,0:T(8,128)(2,1)S(1)}, u32[]{:S(2)}, u32[]{:S(2)}) collective-permute-start(bf16[128,896]{1,0:T(8,128)(2,1)S(1)} %get-tuple-element.47), channel_id=1, source_target_pairs={{0,0},{1,1},{2,128},{3,129},{4,4},{5,5},{6,132},{7,133},{8,8},{9,9... | collective-permute-start | bytes 688136 | tf_op jit(solution)/shard_map/ppermute | solution.py:33
  87.3 10.7 %collective-permute-start.26 = (bf16[128,896]{1,0:T(8,128)(2,1)S(1)}, bf16[128,896]{1,0:T(8,128)(2,1)S(1)}, u32[]{:S(2)}, u32[]{:S(2)}) collective-permute-start(bf16[128,896]{1,0:T(8,128)(2,1)S(1)} %fusion.2), channel_id=1, source_target_pairs={{0,13},{1,12},{2,141},{3,140},{4,1},{5,0},{6,129},{7,128},{8,5},{9... | collective-permute-start | bytes 688136 | tf_op jit(solution)/shard_map/ppermute | solution.py:33
  88.9 10.5 %collective-permute-start.22 = (bf16[128,896]{1,0:T(8,128)(2,1)S(1)}, bf16[128,896]{1,0:T(8,128)(2,1)S(1)}, u32[]{:S(2)}, u32[]{:S(2)}) collective-permute-start(bf16[128,896]{1,0:T(8,128)(2,1)S(1)} %fusion.6), channel_id=1, source_target_pairs={{0,4},{1,5},{2,132},{3,133},{4,8},{5,9},{6,136},{7,137},{8,12},{9,... | collective-permute-start | bytes 688136 | tf_op jit(solution)/shard_map/ppermute | solution.py:33

commit v15 on v13

--- a/solution.py
+++ b/solution.py
@@ -368,17 +368,17 @@
     mine, mine_rest = project(0, groups, blocks, F32)
     sums = [mine_rest[i] + rest[i].astype(F32) for i in range(3)]
     early_up, early_down, first, mine = lax.optimization_barrier(
-        (sums[1][128:].astype(BF), sums[2][:128].astype(BF), first, mine)
+        (sums[1][:128].astype(BF), sums[2][128:].astype(BF), first, mine)
     )
     far_sum = (mine + first.astype(F32)).astype(BF)
-    passing_up = along_x(far_sum[:128], 1)
-    passing_down = along_x(far_sum[128:], 3)
+    passing_up = along_x(far_sum[128:], 1)
+    passing_down = along_x(far_sum[:128], 3)
     early_up, early_down = along_x(early_up, 1), along_x(early_down, 3)
-    late_up = home((sums[1][:128] + passing_up.astype(F32)).astype(BF), 0, 1)
-    late_down = home((sums[2][128:] + passing_down.astype(F32)).astype(BF), 1, 3)
+    late_up = home((sums[1][128:] + passing_up.astype(F32)).astype(BF), 1, 1)
+    late_down = home((sums[2][:128] + passing_down.astype(F32)).astype(BF), 0, 3)
     parts = [
-        [home((sums[0][:128] + early_down.astype(F32)).astype(BF), 0), late_up],
-        [home((sums[0][128:] + early_up.astype(F32)).astype(BF), 1), late_down],
+        [home((sums[0][:128] + early_up.astype(F32)).astype(BF), 0), late_down],
+        [home((sums[0][128:] + early_down.astype(F32)).astype(BF), 1), late_up],
     ]
     pieces = [sum(part.astype(F32) for part in piece).astype(BF) for piece in parts]
     even = yl == 0

time: 101 us -> 97.6 us (0.966)
  waiting for transfers between devices: 25.9 us -> 21.7 us
  starting transfers between devices: 47.4 us -> 48.5 us
    ppermute x27, waiting for transfers between devices: 25.9 us -> 21.7 us  [moved(): return lax.ppermute(a, AXES, pairs)]
    ppermute x27, starting transfers between devices: 41.9 us -> 43 us  [moved(): return lax.ppermute(a, AXES, pairs)]
  transfers between devices with their start and end apart: 29 -> 29, of which waited for: 12 -> 11; matrix products, arithmetic and copies ran while one was open for 2% -> 2% of each run, Pallas kernels for 19% -> 20%
where the time goes in v15:
time: 97.6 us; the launch traced here: 97.4 us
  starting transfers between devices  48.5 us (50%)
  Pallas kernels  21.8 us (22%)
  waiting for transfers between devices  21.7 us (22%)
  other arithmetic  3 us (3%)
  local copies, waits for them, and re-layouts  1.36 us (1%)
  between operations  1.01 us (1%)
    ppermute x27, starting transfers between devices, moved(): return lax.ppermute(a, AXES, pairs)  43 us
    ppermute x27, waiting for transfers between devices, moved(): return lax.ppermute(a, AXES, pairs)  21.7 us
    pallas_call x6, Pallas kernels, call(): pl.pallas_call(kernel, out_shape=shapes, in_specs=specs, out_specs=whole(...  19.6 us
    ppermute x2, starting transfers between devices, local(): lax.ppermute(half, CTX, [(i, (i + by) % 16) for i in range(16)])  5.53 us
    pallas_call x1, Pallas kernels, quarters(): pl.pallas_call(quarter_kernel, out_shape=[jax.ShapeDtypeStruct((64, 1792)...  2.22 us
  transfers between devices with their start and end apart: 29, of which 11 were waited for; matrix products, arithmetic and copies ran while one was open for 2% of the time, Pallas kernels for 20%

profile of v15, /device:TPU:1, one launch (start us, length us, event | category | flops | bytes accessed | tf_op | source)
XLA Modules:
  0.0 97.4 jit_solution(5219235218807416251)
XLA Ops:
  0.0 0.9 dynamic-slice_bitcast_fusion
  0.9 3.9 %collective-permute-start.1 = (bf16[576,128]{1,0:T(8,128)(2,1)S(1)}, bf16[576,128]{1,0:T(8,128)(2,1)S(1)}, u32[]{:S(2)}, u32[]{:S(2)}) collective-permute-start(bf16[576,128]{1,0:T(8,128)(2,1)S(1)} %dynamic-slice_bitcast_fusion), channel_id=1, source_target_pairs={{0,32},{16,48},{32,64},{48,80},{64,96},{80,112},{96,128},{112,144}... | collective-permute-start | bytes 442376 | tf_op jit(solution)/shard_map/ppermute | solution.py:305
  4.8 1.6 %collective-permute-start = (bf16[576,128]{1,0:T(8,128)(2,1)S(1)}, bf16[576,128]{1,0:T(8,128)(2,1)S(1)}, u32[]{:S(2)}, u32[]{:S(2)}) collective-permute-start(bf16[576,128]{1,0:T(8,128)(2,1)S(1)} %dynamic-slice_bitcast_fusion), channel_id=1, source_target_pairs={{0,16},{16,32},{32,48},{48,64},{64,80},{80,96},{96,112},{112,128},... | collective-permute-start | bytes 442376 | tf_op jit(solution)/shard_map/ppermute | solution.py:305
  6.5 2.2 %quarters.1 = (bf16[64,1792]{1,0:T(8,128)(2,1)}, bf16[64,1792]{1,0:T(8,128)(2,1)}) custom-call(bf16[64,7168]{1,0:T(8,128)(2,1)} %bitcast.35), custom_call_target="tpu_custom_call" | custom-call | bytes 2097152 | tf_op jit(solution)/shard_map/quarters/pallas_call | solution.py:247
  8.7 2.8 %collective-permute-start.13 = (bf16[64,1792]{1,0:T(8,128)(2,1)}, bf16[64,1792]{1,0:T(8,128)(2,1)S(1)}, u32[]{:S(2)}, u32[]{:S(2)}) collective-permute-start(bf16[64,1792]{1,0:T(8,128)(2,1)} %get-tuple-element.27.refs_8_), channel_id=1, source_target_pairs={{0,16},{1,17},{2,18},{3,19},{4,20},{5,21},{6,22},{7,23},{8,24},{9,... | collective-permute-start | bytes 688136 | tf_op jit(solution)/shard_map/ppermute | solution.py:33
  11.5 0.8 collective-permute-start.9
  12.3 1.9 %collective-permute-start.10 = (bf16[64,1792]{1,0:T(8,128)(2,1)}, bf16[64,1792]{1,0:T(8,128)(2,1)S(1)}, u32[]{:S(2)}, u32[]{:S(2)}) collective-permute-start(bf16[64,1792]{1,0:T(8,128)(2,1)} %get-tuple-element.28), channel_id=1, source_target_pairs={{0,129},{1,128},{2,131},{3,130},{4,133},{5,132},{6,135},{7,134},{8... | collective-permute-start | bytes 688136 | tf_op jit(solution)/shard_map/ppermute | solution.py:33
  14.4 0.1 fusion.reorder
  14.6 0.8 fusion.11
  15.3 6.8 %queries.1 = (bf16[1024,640]{1,0:T(8,128)(2,1)}, bf16[1024,640]{1,0:T(8,128)(2,1)}) custom-call(bf16[256,1536]{1,0:T(8,128)(2,1)} %rows.1, bf16[1536,1536]{1,0:T(8,128)(2,1)} %w_query.1, bf16[8,128,512]{2,1,0:T(8,128)(2,1)} %w_key_up.1, f32[64,128]{1,0:T(8,128)} %get-tuple-element.59.cosines, f32[64,128]{1,0:T(8,128)} %get-tuple-element.58.sines), custom_call_target="tpu_custom_call" | custom-call | flops 1476395008 | bytes 8388608 | tf_op jit(solution)/shard_map/queries/pallas_call | solution.py:259
  22.3 2.0 %collective-permute-start.2 = (bf16[576,256]{1,0:T(8,128)(2,1)S(1)}, bf16[576,256]{1,0:T(8,128)(2,1)S(1)}, u32[]{:S(2)}, u32[]{:S(2)}) collective-permute-start(bf16[576,256]{1,0:T(8,128)(2,1)S(1)} %pad_maximum_fusion.2), channel_id=1, source_target_pairs={{0,2},{1,3},{2,0},{3,1},{4,6},{5,7},{6,4},{7,5},{8,10},{9,11},{10,... | collective-permute-start | bytes 884744 | tf_op jit(solution)/shard_map/ppermute | solution.py:33
  24.4 0.6 collective-permute-start.11
  24.9 1.2 %collective-permute-start.14 = (bf16[128,1792]{1,0:T(8,128)(2,1)S(1)}, bf16[128,1792]{1,0:T(8,128)(2,1)S(1)}, u32[]{:S(2)}, u32[]{:S(2)}) collective-permute-start(bf16[128,1792]{1,0:T(8,128)(2,1)S(1)} %get-tuple-element.31), channel_id=1, source_target_pairs={{0,16},{1,17},{2,18},{3,19},{4,20},{5,21},{6,22},{7,23},{8,24},{9,... | collective-permute-start | bytes 1376264 | tf_op jit(solution)/shard_map/ppermute | solution.py:33
  26.2 0.4 multiply_sine_fusion
  27.3 0.6 keys.1
  27.9 3.8 %attend.2.refs_0_ = bf16[256,512]{1,0:T(8,128)(2,1)S(1)} custom-call(bf16[1024,640]{1,0:T(8,128)(2,1)S(1)} %copy-done.3, bf16[640,768]{1,0:T(8,128)(2,1)S(1)} %get-tuple-element.24.keys, f32[256,768]{1,0:T(8,128)S(1)} %get-tuple-element.25.hidden, bf16[8,512,128]{2,1,0:T(8,128)(2,1)S(1)} %copy-done.4, bf16[512,512]{1,0:T(8,128)(2,1)S(1)} %fusion.reorder), custom_call_target="tpu_custom_call" | custom-call | flops 1946157056 | bytes 5242880 | tf_op jit(solution)/shard_map/attend/pallas_call | solution.py:259
  31.7 3.8 %attend.3.refs_1_ = bf16[256,512]{1,0:T(8,128)(2,1)S(1)} custom-call(bf16[1024,640]{1,0:T(8,128)(2,1)S(1)} %copy-done.2, bf16[640,768]{1,0:T(8,128)(2,1)S(1)} %get-tuple-element.24.keys, f32[256,768]{1,0:T(8,128)S(1)} %get-tuple-element.25.hidden, bf16[8,512,128]{2,1,0:T(8,128)(2,1)S(1)} %copy-done.4, bf16[512,512]{1,0:T(8,128)(2,1)S(1)} %fusion.reorder), custom_call_target="tpu_custom_call" | custom-call | flops 1946157056 | bytes 5242880 | tf_op jit(solution)/shard_map/attend/pallas_call | solution.py:259
  35.5 0.4 collective-permute-done.11.refs_10_
  35.9 2.2 %collective-permute-start.12 = (bf16[128,1792]{1,0:T(8,128)(2,1)S(1)}, bf16[128,1792]{1,0:T(8,128)(2,1)S(1)}, u32[]{:S(2)}, u32[]{:S(2)}) collective-permute-start(bf16[128,1792]{1,0:T(8,128)(2,1)S(1)} %collective-permute-done.11.refs_10_), channel_id=1, source_target_pairs={{0,112},{1,113},{2,114},{3,115},{4,116},{5,117},{6,118},{7,119},{8... | collective-permute-start | bytes 1376264 | tf_op jit(solution)/shard_map/ppermute | solution.py:33
  38.2 1.7 %collective-permute-start.8 = (bf16[256,512]{1,0:T(8,128)(2,1)S(1)}, bf16[256,512]{1,0:T(8,128)(2,1)S(1)}, u32[]{:S(2)}, u32[]{:S(2)}) collective-permute-start(bf16[256,512]{1,0:T(8,128)(2,1)S(1)} %attend.2.refs_0_), channel_id=1, source_target_pairs={{0,129},{1,128},{2,131},{3,130},{4,133},{5,132},{6,135},{7,134},{8... | collective-permute-start | bytes 786440 | tf_op jit(solution)/shard_map/ppermute | solution.py:33
  39.9 1.0 collective-permute-start.6
  40.9 7.1 %collective-permute-done.12.refs_11_ = bf16[128,1792]{1,0:T(8,128)(2,1)S(1)} collective-permute-done((bf16[128,1792]{1,0:T(8,128)(2,1)S(1)}, bf16[128,1792]{1,0:T(8,128)(2,1)S(1)}, u32[]{:S(2)}, u32[]{:S(2)}) %collective-permute-start.12) | collective-permute-done | bytes 458784 | tf_op jit(solution)/shard_map/ppermute | solution.py:33
  48.0 2.5 %collective-permute-start.17 = (bf16[64,1792]{1,0:T(8,128)(2,1)S(1)}, bf16[64,1792]{1,0:T(8,128)(2,1)S(1)}, u32[]{:S(2)}, u32[]{:S(2)}) collective-permute-start(bf16[64,1792]{1,0:T(8,128)(2,1)S(1)} %slice.96), channel_id=1, source_target_pairs={{0,112},{1,113},{2,114},{3,115},{4,116},{5,117},{6,118},{7,119},{8... | collective-permute-start | bytes 688136 | tf_op jit(solution)/shard_map/ppermute | solution.py:33
  50.6 1.8 %collective-permute-start.5 = (bf16[256,512]{1,0:T(8,128)(2,1)S(1)}, bf16[256,512]{1,0:T(8,128)(2,1)S(1)}, u32[]{:S(2)}, u32[]{:S(2)}) collective-permute-start(bf16[256,512]{1,0:T(8,128)(2,1)S(1)} %collective-permute-done.3.refs_2_), channel_id=1, source_target_pairs={{0,129},{1,128},{2,131},{3,130},{4,133},{5,132},{6,135},{7,134},{8... | collective-permute-start | bytes 786440 | tf_op jit(solution)/shard_map/ppermute | solution.py:33
  52.3 0.8 collective-permute-start.7
  53.1 0.3 collective-permute-done.17.refs_17_
  53.4 3.4 %collective-permute-start.18 = (bf16[64,1792]{1,0:T(8,128)(2,1)S(1)}, bf16[64,1792]{1,0:T(8,128)(2,1)S(1)}, u32[]{:S(2)}, u32[]{:S(2)}) collective-permute-start(bf16[64,1792]{1,0:T(8,128)(2,1)S(1)} %collective-permute-done.17.refs_17_), channel_id=1, source_target_pairs={{0,112},{1,113},{2,114},{3,115},{4,116},{5,117},{6,118},{7,119},{8... | collective-permute-start | bytes 688136 | tf_op jit(solution)/shard_map/ppermute | solution.py:33
  56.8 0.6 collective-permute-done.5.refs_4_
  57.5 4.3 %collective-permute-done.7.refs_5_ = bf16[256,512]{1,0:T(8,128)(2,1)S(1)} collective-permute-done((bf16[256,512]{1,0:T(8,128)(2,1)S(1)}, bf16[256,512]{1,0:T(8,128)(2,1)S(1)}, u32[]{:S(2)}, u32[]{:S(2)}) %collective-permute-start.7) | collective-permute-done | bytes 262176 | tf_op jit(solution)/shard_map/ppermute | solution.py:33
  61.8 2.3 %project.3 = (bf16[256,896]{1,0:T(8,128)(2,1)S(1)}, bf16[3,256,896]{2,1,0:T(8,128)(2,1)S(1)}) custom-call(bf16[256,512]{1,0:T(8,128)(2,1)S(1)} %attend.2.refs_0_, bf16[256,512]{1,0:T(8,128)(2,1)S(1)} %attend.3.refs_1_, bf16[256,512]{1,0:T(8,128)(2,1)S(1)} %collective-permute-done.3.refs_2_, bf16[256,512]{1,0:T(8,128)(2,1)S(1)} %collective-permute-done.4.refs_3_, ...), custom_call_target="tpu_custom_call" | custom-call | flops 1879048192 | bytes 8388608 | tf_op jit(solution)/shard_map/project/pallas_call | solution.py:259
  64.1 3.2 %collective-permute-start.19 = (bf16[3,256,896]{2,1,0:T(8,128)(2,1)S(1)}, bf16[3,256,896]{2,1,0:T(8,128)(2,1)S(1)}, u32[]{:S(2)}, u32[]{:S(2)}) collective-permute-start(bf16[3,256,896]{2,1,0:T(8,128)(2,1)S(1)} %get-tuple-element.34), channel_id=1, source_target_pairs={{0,2},{1,3},{2,0},{3,1},{4,6},{5,7},{6,4},{7,5},{8,10},{9,11},{10,... | collective-permute-start | bytes 4128776 | tf_op jit(solution)/shard_map/ppermute | solution.py:33
  67.4 2.3 %project.2 = (f32[256,896]{1,0:T(8,128)S(1)}, f32[3,256,896]{2,1,0:T(8,128)S(1)}) custom-call(bf16[256,512]{1,0:T(8,128)(2,1)S(1)} %attend.2.refs_0_, bf16[256,512]{1,0:T(8,128)(2,1)S(1)} %attend.3.refs_1_, bf16[256,512]{1,0:T(8,128)(2,1)S(1)} %collective-permute-done.3.refs_2_, bf16[256,512]{1,0:T(8,128)(2,1)S(1)} %collective-permute-done.4.refs_3_, ...), custom_call_target="tpu_custom_call" | custom-call | flops 1879048192 | bytes 8388608 | tf_op jit(solution)/shard_map/project/pallas_call | solution.py:259
  69.7 0.3 collective-permute-done.19
  70.0 0.2 convert_add_fusion.2
  70.3 0.4 collective-permute-done.20
  70.7 1.2 %collective-permute-start.21 = (bf16[128,896]{1,0:T(8,128)(2,1)S(1)}, bf16[128,896]{1,0:T(8,128)(2,1)S(1)}, u32[]{:S(2)}, u32[]{:S(2)}) collective-permute-start(bf16[128,896]{1,0:T(8,128)(2,1)S(1)} %fusion.9), channel_id=1, source_target_pairs={{0,4},{1,5},{2,6},{3,7},{4,8},{5,9},{6,10},{7,11},{8,12},{9,13},{1... | collective-permute-start | bytes 688136 | tf_op jit(solution)/shard_map/ppermute | solution.py:33
  71.9 1.5 %collective-permute-start.25 = (bf16[128,896]{1,0:T(8,128)(2,1)S(1)}, bf16[128,896]{1,0:T(8,128)(2,1)S(1)}, u32[]{:S(2)}, u32[]{:S(2)}) collective-permute-start(bf16[128,896]{1,0:T(8,128)(2,1)S(1)} %fusion.10), channel_id=1, source_target_pairs={{0,12},{1,13},{2,14},{3,15},{4,0},{5,1},{6,2},{7,3},{8,4},{9,5},{1... | collective-permute-start | bytes 688136 | tf_op jit(solution)/shard_map/ppermute | solution.py:33
  73.6 2.7 %collective-permute-start.23 = (bf16[128,896]{1,0:T(8,128)(2,1)S(1)}, bf16[128,896]{1,0:T(8,128)(2,1)S(1)}, u32[]{:S(2)}, u32[]{:S(2)}) collective-permute-start(bf16[128,896]{1,0:T(8,128)(2,1)S(1)} %get-tuple-element.49), channel_id=1, source_target_pairs={{0,12},{1,13},{2,14},{3,15},{4,0},{5,1},{6,2},{7,3},{8,4},{9,5},{1... | collective-permute-start | bytes 688136 | tf_op jit(solution)/shard_map/ppermute | solution.py:33
  76.3 2.5 %collective-permute-done.21 = bf16[128,896]{1,0:T(8,128)(2,1)S(1)} collective-permute-done((bf16[128,896]{1,0:T(8,128)(2,1)S(1)}, bf16[128,896]{1,0:T(8,128)(2,1)S(1)}, u32[]{:S(2)}, u32[]{:S(2)}) %collective-permute-start.21) | collective-permute-done | bytes 229408 | tf_op jit(solution)/shard_map/ppermute | solution.py:33
  78.8 3.9 %collective-permute-start.26 = (bf16[128,896]{1,0:T(8,128)(2,1)S(1)}, bf16[128,896]{1,0:T(8,128)(2,1)S(1)}, u32[]{:S(2)}, u32[]{:S(2)}) collective-permute-start(bf16[128,896]{1,0:T(8,128)(2,1)S(1)} %get-tuple-element.46), channel_id=1, source_target_pairs={{0,1},{1,0},{2,129},{3,128},{4,5},{5,4},{6,133},{7,132},{8,9},{9,8... | collective-permute-start | bytes 688136 | tf_op jit(solution)/shard_map/ppermute | solution.py:33
  82.8 1.9 %collective-permute-start.22 = (bf16[128,896]{1,0:T(8,128)(2,1)S(1)}, bf16[128,896]{1,0:T(8,128)(2,1)S(1)}, u32[]{:S(2)}, u32[]{:S(2)}) collective-permute-start(bf16[128,896]{1,0:T(8,128)(2,1)S(1)} %get-tuple-element.47), channel_id=1, source_target_pairs={{0,0},{1,1},{2,128},{3,129},{4,4},{5,5},{6,132},{7,133},{8,8},{9,9... | collective-permute-start | bytes 688136 | tf_op jit(solution)/shard_map/ppermute | solution.py:33
  84.7 1.5 %collective-permute-start.28 = (bf16[128,896]{1,0:T(8,128)(2,1)S(1)}, bf16[128,896]{1,0:T(8,128)(2,1)S(1)}, u32[]{:S(2)}, u32[]{:S(2)}) collective-permute-start(bf16[128,896]{1,0:T(8,128)(2,1)S(1)} %fusion.2), channel_id=1, source_target_pairs={{0,5},{1,4},{2,133},{3,132},{4,9},{5,8},{6,137},{7,136},{8,13},{9,... | collective-permute-start | bytes 688136 | tf_op jit(solution)/shard_map/ppermute | solution.py:33
  86.3 4.0 %collective-permute-start.24 = (bf16[128,896]{1,0:T(8,128)(2,1)S(1)}, bf16[128,896]{1,0:T(8,128)(2,1)S(1)}, u32[]{:S(2)}, u32[]{:S(2)}) collective-permute-start(bf16[128,896]{1,0:T(8,128)(2,1)S(1)} %fusion.6), channel_id=1, source_target_pairs={{0,12},{1,13},{2,140},{3,141},{4,0},{5,1},{6,128},{7,129},{8,4},{9... | collective-permute-start | bytes 688136 | tf_op jit(solution)/shard_map/ppermute | solution.py:33
  90.3 1.1 %collective-permute-done.22 = bf16[128,896]{1,0:T(8,128)(2,1)S(1)} collective-permute-done((bf16[128,896]{1,0:T(8,128)(2,1)S(1)}, bf16[128,896]{1,0:T(8,128)(2,1)S(1)}, u32[]{:S(2)}, u32[]{:S(2)}) %collective-permute-start.22) | collective-permute-done | bytes 229408 | tf_op jit(solution)/shard_map/ppermute | solution.py:33
  91.5 3.6 %collective-permute-done.28 = bf16[128,896]{1,0:T(8,128)(2,1)S(1)} collective-permute-done((bf16[128,896]{1,0:T(8,128)(2,1)S(1)}, bf16[128,896]{1,0:T(8,128)(2,1)S(1)}, u32[]{:S(2)}, u32[]{:S(2)}) %collective-permute-start.28) | collective-permute-done | bytes 229408 | tf_op jit(solution)/shard_map/ppermute | solution.py:33
  95.0 1.1 %collective-permute-done.24 = bf16[128,896]{1,0:T(8,128)(2,1)S(1)} collective-permute-done((bf16[128,896]{1,0:T(8,128)(2,1)S(1)}, bf16[128,896]{1,0:T(8,128)(2,1)S(1)}, u32[]{:S(2)}, u32[]{:S(2)}) %collective-permute-start.24) | collective-permute-done | bytes 229408 | tf_op jit(solution)/shard_map/ppermute | solution.py:33
  96.1 0.1 broadcast_select_fusion.1
  96.5 0.9 maximum_maximum_fusion
  (55 shorter events, 1.3 us)
Async XLA Ops:
  0.9 21.3 %collective-permute-start.1 = (bf16[576,128]{1,0:T(8,128)(2,1)S(1)}, bf16[576,128]{1,0:T(8,128)(2,1)S(1)}, u32[]{:S(2)}, u32[]{:S(2)}) collective-permute-start(bf16[576,128]{1,0:T(8,128)(2,1)S(1)} %dynamic-slice_bitcast_fusion), channel_id=1, source_target_pairs={{0,32},{16,48},{32,64},{48,80},{64,96},{80,112},{96,128},{112,144}... | collective-permute-start | bytes 442376 | tf_op jit(solution)/shard_map/ppermute | solution.py:305
  4.8 17.4 %collective-permute-start = (bf16[576,128]{1,0:T(8,128)(2,1)S(1)}, bf16[576,128]{1,0:T(8,128)(2,1)S(1)}, u32[]{:S(2)}, u32[]{:S(2)}) collective-permute-start(bf16[576,128]{1,0:T(8,128)(2,1)S(1)} %dynamic-slice_bitcast_fusion), channel_id=1, source_target_pairs={{0,16},{16,32},{32,48},{48,64},{64,80},{80,96},{96,112},{112,128},... | collective-permute-start | bytes 442376 | tf_op jit(solution)/shard_map/ppermute | solution.py:305
  8.7 15.6 %collective-permute-start.13 = (bf16[64,1792]{1,0:T(8,128)(2,1)}, bf16[64,1792]{1,0:T(8,128)(2,1)S(1)}, u32[]{:S(2)}, u32[]{:S(2)}) collective-permute-start(bf16[64,1792]{1,0:T(8,128)(2,1)} %get-tuple-element.27.refs_8_), channel_id=1, source_target_pairs={{0,16},{1,17},{2,18},{3,19},{4,20},{5,21},{6,22},{7,23},{8,24},{9,... | collective-permute-start | bytes 688136 | tf_op jit(solution)/shard_map/ppermute | solution.py:33
  11.5 12.8 %collective-permute-start.9 = (bf16[64,1792]{1,0:T(8,128)(2,1)}, bf16[64,1792]{1,0:T(8,128)(2,1)S(1)}, u32[]{:S(2)}, u32[]{:S(2)}) collective-permute-start(bf16[64,1792]{1,0:T(8,128)(2,1)} %get-tuple-element.27.refs_8_), channel_id=1, source_target_pairs={{0,112},{1,113},{2,114},{3,115},{4,116},{5,117},{6,118},{7,119},{8... | collective-permute-start | bytes 688136 | tf_op jit(solution)/shard_map/ppermute | solution.py:33
  12.3 11.9 %collective-permute-start.10 = (bf16[64,1792]{1,0:T(8,128)(2,1)}, bf16[64,1792]{1,0:T(8,128)(2,1)S(1)}, u32[]{:S(2)}, u32[]{:S(2)}) collective-permute-start(bf16[64,1792]{1,0:T(8,128)(2,1)} %get-tuple-element.28), channel_id=1, source_target_pairs={{0,129},{1,128},{2,131},{3,130},{4,133},{5,132},{6,135},{7,134},{8... | collective-permute-start | bytes 688136 | tf_op jit(solution)/shard_map/ppermute | solution.py:33
  22.2 5.1 %copy-start = (bf16[256,576]{0,1:T(8,128)(2,1)S(1)}, bf16[256,576]{0,1:T(8,128)(2,1)}, u32[]{:S(2)}) copy-start(bf16[256,576]{0,1:T(8,128)(2,1)} %param.9) | copy-start | bytes 884740
  22.2 5.1 %copy-start.1 = (bf16[512,576]{0,1:T(8,128)(2,1)S(1)}, bf16[512,576]{0,1:T(8,128)(2,1)}, u32[]{:S(2)}) copy-start(bf16[512,576]{0,1:T(8,128)(2,1)} %param.10) | copy-start | bytes 1769476
  22.3 5.6 %copy-start.3 = (bf16[1024,640]{1,0:T(8,128)(2,1)S(1)}, bf16[1024,640]{1,0:T(8,128)(2,1)}, u32[]{:S(2)}) copy-start(bf16[1024,640]{1,0:T(8,128)(2,1)} %get-tuple-element.23.queries) | copy-start | bytes 3932164
  22.3 5.6 %copy-start.4 = (bf16[8,512,128]{2,1,0:T(8,128)(2,1)S(1)}, bf16[8,512,128]{2,1,0:T(8,128)(2,1)}, u32[]{:S(2)}) copy-start(bf16[8,512,128]{2,1,0:T(8,128)(2,1)} %w_value_up.3) | copy-start | bytes 3145732
  22.3 5.0 %collective-permute-start.2 = (bf16[576,256]{1,0:T(8,128)(2,1)S(1)}, bf16[576,256]{1,0:T(8,128)(2,1)S(1)}, u32[]{:S(2)}, u32[]{:S(2)}) collective-permute-start(bf16[576,256]{1,0:T(8,128)(2,1)S(1)} %pad_maximum_fusion.2), channel_id=1, source_target_pairs={{0,2},{1,3},{2,0},{3,1},{4,6},{5,7},{6,4},{7,5},{8,10},{9,11},{10,... | collective-permute-start | bytes 884744 | tf_op jit(solution)/shard_map/ppermute | solution.py:33
  24.4 11.5 %collective-permute-start.11 = (bf16[128,1792]{1,0:T(8,128)(2,1)S(1)}, bf16[128,1792]{1,0:T(8,128)(2,1)S(1)}, u32[]{:S(2)}, u32[]{:S(2)}) collective-permute-start(bf16[128,1792]{1,0:T(8,128)(2,1)S(1)} %get-tuple-element.29), channel_id=1, source_target_pairs={{0,112},{1,113},{2,114},{3,115},{4,116},{5,117},{6,118},{7,119},{8... | collective-permute-start | bytes 1376264 | tf_op jit(solution)/shard_map/ppermute | solution.py:33
  24.9 13.2 %collective-permute-start.14 = (bf16[128,1792]{1,0:T(8,128)(2,1)S(1)}, bf16[128,1792]{1,0:T(8,128)(2,1)S(1)}, u32[]{:S(2)}, u32[]{:S(2)}) collective-permute-start(bf16[128,1792]{1,0:T(8,128)(2,1)S(1)} %get-tuple-element.31), channel_id=1, source_target_pairs={{0,16},{1,17},{2,18},{3,19},{4,20},{5,21},{6,22},{7,23},{8,24},{9,... | collective-permute-start | bytes 1376264 | tf_op jit(solution)/shard_map/ppermute | solution.py:33
  27.9 3.8 %copy-start.2 = (bf16[1024,640]{1,0:T(8,128)(2,1)S(1)}, bf16[1024,640]{1,0:T(8,128)(2,1)}, u32[]{:S(2)}) copy-start(bf16[1024,640]{1,0:T(8,128)(2,1)} %get-tuple-element.26.queries) | copy-start | bytes 3932164
  31.7 30.1 %copy-start.5 = (bf16[64,1792]{1,0:T(8,128)(2,1)S(1)}, bf16[64,1792]{1,0:T(8,128)(2,1)}, u32[]{:S(2)}) copy-start(bf16[64,1792]{1,0:T(8,128)(2,1)} %get-tuple-element.27.refs_8_) | copy-start | bytes 688132
  35.9 12.1 %collective-permute-start.12 = (bf16[128,1792]{1,0:T(8,128)(2,1)S(1)}, bf16[128,1792]{1,0:T(8,128)(2,1)S(1)}, u32[]{:S(2)}, u32[]{:S(2)}) collective-permute-start(bf16[128,1792]{1,0:T(8,128)(2,1)S(1)} %collective-permute-done.11.refs_10_), channel_id=1, source_target_pairs={{0,112},{1,113},{2,114},{3,115},{4,116},{5,117},{6,118},{7,119},{8... | collective-permute-start | bytes 1376264 | tf_op jit(solution)/shard_map/ppermute | solution.py:33
  38.1 12.3 %collective-permute-start.15 = (bf16[128,1792]{1,0:T(8,128)(2,1)S(1)}, bf16[128,1792]{1,0:T(8,128)(2,1)S(1)}, u32[]{:S(2)}, u32[]{:S(2)}) collective-permute-start(bf16[128,1792]{1,0:T(8,128)(2,1)S(1)} %collective-permute-done.14.refs_14_), channel_id=1, source_target_pairs={{0,16},{1,17},{2,18},{3,19},{4,20},{5,21},{6,22},{7,23},{8,24},{9,... | collective-permute-start | bytes 1376264 | tf_op jit(solution)/shard_map/ppermute | solution.py:33
  38.2 12.3 %collective-permute-start.8 = (bf16[256,512]{1,0:T(8,128)(2,1)S(1)}, bf16[256,512]{1,0:T(8,128)(2,1)S(1)}, u32[]{:S(2)}, u32[]{:S(2)}) collective-permute-start(bf16[256,512]{1,0:T(8,128)(2,1)S(1)} %attend.2.refs_0_), channel_id=1, source_target_pairs={{0,129},{1,128},{2,131},{3,130},{4,133},{5,132},{6,135},{7,134},{8... | collective-permute-start | bytes 786440 | tf_op jit(solution)/shard_map/ppermute | solution.py:33
  39.9 10.7 %collective-permute-start.3 = (bf16[256,512]{1,0:T(8,128)(2,1)S(1)}, bf16[256,512]{1,0:T(8,128)(2,1)S(1)}, u32[]{:S(2)}, u32[]{:S(2)}) collective-permute-start(bf16[256,512]{1,0:T(8,128)(2,1)S(1)} %attend.2.refs_0_), channel_id=1, source_target_pairs={{0,1},{1,0},{2,3},{3,2},{4,5},{5,4},{6,7},{7,6},{8,9},{9,8},{10,11... | collective-permute-start | bytes 786440 | tf_op jit(solution)/shard_map/ppermute | solution.py:33
  39.9 12.4 %collective-permute-start.6 = (bf16[256,512]{1,0:T(8,128)(2,1)S(1)}, bf16[256,512]{1,0:T(8,128)(2,1)S(1)}, u32[]{:S(2)}, u32[]{:S(2)}) collective-permute-start(bf16[256,512]{1,0:T(8,128)(2,1)S(1)} %attend.3.refs_1_), channel_id=1, source_target_pairs={{0,129},{1,128},{2,131},{3,130},{4,133},{5,132},{6,135},{7,134},{8... | collective-permute-start | bytes 786440 | tf_op jit(solution)/shard_map/ppermute | solution.py:33
  48.0 5.5 %collective-permute-start.17 = (bf16[64,1792]{1,0:T(8,128)(2,1)S(1)}, bf16[64,1792]{1,0:T(8,128)(2,1)S(1)}, u32[]{:S(2)}, u32[]{:S(2)}) collective-permute-start(bf16[64,1792]{1,0:T(8,128)(2,1)S(1)} %slice.96), channel_id=1, source_target_pairs={{0,112},{1,113},{2,114},{3,115},{4,116},{5,117},{6,118},{7,119},{8... | collective-permute-start | bytes 688136 | tf_op jit(solution)/shard_map/ppermute | solution.py:33
  50.4 11.3 %collective-permute-start.16 = (bf16[128,1792]{1,0:T(8,128)(2,1)S(1)}, bf16[128,1792]{1,0:T(8,128)(2,1)S(1)}, u32[]{:S(2)}, u32[]{:S(2)}) collective-permute-start(bf16[128,1792]{1,0:T(8,128)(2,1)S(1)} %collective-permute-done.15.refs_13_), channel_id=1, source_target_pairs={{0,16},{1,17},{2,18},{3,19},{4,20},{5,21},{6,22},{7,23},{8,24},{9,... | collective-permute-start | bytes 1376264 | tf_op jit(solution)/shard_map/ppermute | solution.py:33
  50.4 6.4 %collective-permute-start.4 = (bf16[256,512]{1,0:T(8,128)(2,1)S(1)}, bf16[256,512]{1,0:T(8,128)(2,1)S(1)}, u32[]{:S(2)}, u32[]{:S(2)}) collective-permute-start(bf16[256,512]{1,0:T(8,128)(2,1)S(1)} %attend.3.refs_1_), channel_id=1, source_target_pairs={{0,1},{1,0},{2,3},{3,2},{4,5},{5,4},{6,7},{7,6},{8,9},{9,8},{10,11... | collective-permute-start | bytes 786440 | tf_op jit(solution)/shard_map/ppermute | solution.py:33
  50.6 6.9 %collective-permute-start.5 = (bf16[256,512]{1,0:T(8,128)(2,1)S(1)}, bf16[256,512]{1,0:T(8,128)(2,1)S(1)}, u32[]{:S(2)}, u32[]{:S(2)}) collective-permute-start(bf16[256,512]{1,0:T(8,128)(2,1)S(1)} %collective-permute-done.3.refs_2_), channel_id=1, source_target_pairs={{0,129},{1,128},{2,131},{3,130},{4,133},{5,132},{6,135},{7,134},{8... | collective-permute-start | bytes 786440 | tf_op jit(solution)/shard_map/ppermute | solution.py:33
  52.3 9.4 %collective-permute-start.7 = (bf16[256,512]{1,0:T(8,128)(2,1)S(1)}, bf16[256,512]{1,0:T(8,128)(2,1)S(1)}, u32[]{:S(2)}, u32[]{:S(2)}) collective-permute-start(bf16[256,512]{1,0:T(8,128)(2,1)S(1)} %collective-permute-done.6.refs_7_), channel_id=1, source_target_pairs={{0,1},{1,0},{2,3},{3,2},{4,5},{5,4},{6,7},{7,6},{8,9},{9,8},{10,11... | collective-permute-start | bytes 786440 | tf_op jit(solution)/shard_map/ppermute | solution.py:33
  53.4 8.3 %collective-permute-start.18 = (bf16[64,1792]{1,0:T(8,128)(2,1)S(1)}, bf16[64,1792]{1,0:T(8,128)(2,1)S(1)}, u32[]{:S(2)}, u32[]{:S(2)}) collective-permute-start(bf16[64,1792]{1,0:T(8,128)(2,1)S(1)} %collective-permute-done.17.refs_17_), channel_id=1, source_target_pairs={{0,112},{1,113},{2,114},{3,115},{4,116},{5,117},{6,118},{7,119},{8... | collective-permute-start | bytes 688136 | tf_op jit(solution)/shard_map/ppermute | solution.py:33
  64.1 6.0 %collective-permute-start.19 = (bf16[3,256,896]{2,1,0:T(8,128)(2,1)S(1)}, bf16[3,256,896]{2,1,0:T(8,128)(2,1)S(1)}, u32[]{:S(2)}, u32[]{:S(2)}) collective-permute-start(bf16[3,256,896]{2,1,0:T(8,128)(2,1)S(1)} %get-tuple-element.34), channel_id=1, source_target_pairs={{0,2},{1,3},{2,0},{3,1},{4,6},{5,7},{6,4},{7,5},{8,10},{9,11},{10,... | collective-permute-start | bytes 4128776 | tf_op jit(solution)/shard_map/ppermute | solution.py:33
  67.3 3.4 %collective-permute-start.20 = (bf16[256,896]{1,0:T(8,128)(2,1)S(1)}, bf16[256,896]{1,0:T(8,128)(2,1)S(1)}, u32[]{:S(2)}, u32[]{:S(2)}) collective-permute-start(bf16[256,896]{1,0:T(8,128)(2,1)S(1)} %get-tuple-element.35), channel_id=1, source_target_pairs={{0,2},{1,3},{2,0},{3,1},{4,6},{5,7},{6,4},{7,5},{8,10},{9,11},{10,... | collective-permute-start | bytes 1376264 | tf_op jit(solution)/shard_map/ppermute | solution.py:33
  70.7 8.0 %collective-permute-start.21 = (bf16[128,896]{1,0:T(8,128)(2,1)S(1)}, bf16[128,896]{1,0:T(8,128)(2,1)S(1)}, u32[]{:S(2)}, u32[]{:S(2)}) collective-permute-start(bf16[128,896]{1,0:T(8,128)(2,1)S(1)} %fusion.9), channel_id=1, source_target_pairs={{0,4},{1,5},{2,6},{3,7},{4,8},{5,9},{6,10},{7,11},{8,12},{9,13},{1... | collective-permute-start | bytes 688136 | tf_op jit(solution)/shard_map/ppermute | solution.py:33
  71.9 6.8 %collective-permute-start.25 = (bf16[128,896]{1,0:T(8,128)(2,1)S(1)}, bf16[128,896]{1,0:T(8,128)(2,1)S(1)}, u32[]{:S(2)}, u32[]{:S(2)}) collective-permute-start(bf16[128,896]{1,0:T(8,128)(2,1)S(1)} %fusion.10), channel_id=1, source_target_pairs={{0,12},{1,13},{2,14},{3,15},{4,0},{5,1},{6,2},{7,3},{8,4},{9,5},{1... | collective-permute-start | bytes 688136 | tf_op jit(solution)/shard_map/ppermute | solution.py:33
  73.5 11.2 %collective-permute-start.27 = (bf16[128,896]{1,0:T(8,128)(2,1)S(1)}, bf16[128,896]{1,0:T(8,128)(2,1)S(1)}, u32[]{:S(2)}, u32[]{:S(2)}) collective-permute-start(bf16[128,896]{1,0:T(8,128)(2,1)S(1)} %get-tuple-element.48), channel_id=1, source_target_pairs={{0,4},{1,5},{2,6},{3,7},{4,8},{5,9},{6,10},{7,11},{8,12},{9,13},{1... | collective-permute-start | bytes 688136 | tf_op jit(solution)/shard_map/ppermute | solution.py:33
  73.6 12.6 %collective-permute-start.23 = (bf16[128,896]{1,0:T(8,128)(2,1)S(1)}, bf16[128,896]{1,0:T(8,128)(2,1)S(1)}, u32[]{:S(2)}, u32[]{:S(2)}) collective-permute-start(bf16[128,896]{1,0:T(8,128)(2,1)S(1)} %get-tuple-element.49), channel_id=1, source_target_pairs={{0,12},{1,13},{2,14},{3,15},{4,0},{5,1},{6,2},{7,3},{8,4},{9,5},{1... | collective-permute-start | bytes 688136 | tf_op jit(solution)/shard_map/ppermute | solution.py:33
  78.8 11.5 %collective-permute-start.26 = (bf16[128,896]{1,0:T(8,128)(2,1)S(1)}, bf16[128,896]{1,0:T(8,128)(2,1)S(1)}, u32[]{:S(2)}, u32[]{:S(2)}) collective-permute-start(bf16[128,896]{1,0:T(8,128)(2,1)S(1)} %get-tuple-element.46), channel_id=1, source_target_pairs={{0,1},{1,0},{2,129},{3,128},{4,5},{5,4},{6,133},{7,132},{8,9},{9,8... | collective-permute-start | bytes 688136 | tf_op jit(solution)/shard_map/ppermute | solution.py:33
  82.8 8.7 %collective-permute-start.22 = (bf16[128,896]{1,0:T(8,128)(2,1)S(1)}, bf16[128,896]{1,0:T(8,128)(2,1)S(1)}, u32[]{:S(2)}, u32[]{:S(2)}) collective-permute-start(bf16[128,896]{1,0:T(8,128)(2,1)S(1)} %get-tuple-element.47), channel_id=1, source_target_pairs={{0,0},{1,1},{2,128},{3,129},{4,4},{5,5},{6,132},{7,133},{8,8},{9,9... | collective-permute-start | bytes 688136 | tf_op jit(solution)/shard_map/ppermute | solution.py:33
  84.7 10.3 %collective-permute-start.28 = (bf16[128,896]{1,0:T(8,128)(2,1)S(1)}, bf16[128,896]{1,0:T(8,128)(2,1)S(1)}, u32[]{:S(2)}, u32[]{:S(2)}) collective-permute-start(bf16[128,896]{1,0:T(8,128)(2,1)S(1)} %fusion.2), channel_id=1, source_target_pairs={{0,5},{1,4},{2,133},{3,132},{4,9},{5,8},{6,137},{7,136},{8,13},{9,... | collective-permute-start | bytes 688136 | tf_op jit(solution)/shard_map/ppermute | solution.py:33
  86.3 9.8 %collective-permute-start.24 = (bf16[128,896]{1,0:T(8,128)(2,1)S(1)}, bf16[128,896]{1,0:T(8,128)(2,1)S(1)}, u32[]{:S(2)}, u32[]{:S(2)}) collective-permute-start(bf16[128,896]{1,0:T(8,128)(2,1)S(1)} %fusion.6), channel_id=1, source_target_pairs={{0,12},{1,13},{2,140},{3,141},{4,0},{5,1},{6,128},{7,129},{8,4},{9... | collective-permute-start | bytes 688136 | tf_op jit(solution)/shard_map/ppermute | solution.py:33

commit v16 on v14

--- a/solution.py
+++ b/solution.py
@@ -367,17 +367,17 @@
     mine, mine_rest = project(0, groups, blocks, F32)
     sums = [mine_rest[i] + rest[i].astype(F32) for i in range(3)]
     early_up, early_down, first, mine = lax.optimization_barrier(
-        (sums[1][128:].astype(BF), sums[2][:128].astype(BF), first, mine)
+        (sums[1][:128].astype(BF), sums[2][128:].astype(BF), first, mine)
     )
     far_sum = (mine + first.astype(F32)).astype(BF)
-    passing_up = along_x(far_sum[:128], 1)
-    passing_down = along_x(far_sum[128:], 3)
+    passing_up = along_x(far_sum[128:], 1)
+    passing_down = along_x(far_sum[:128], 3)
     early_up, early_down = along_x(early_up, 1), along_x(early_down, 3)
-    late_up = home((sums[1][:128] + passing_up.astype(F32)).astype(BF), 0, 1)
-    late_down = home((sums[2][128:] + passing_down.astype(F32)).astype(BF), 1, 3)
+    late_up = home((sums[1][128:] + passing_up.astype(F32)).astype(BF), 1, 1)
+    late_down = home((sums[2][:128] + passing_down.astype(F32)).astype(BF), 0, 3)
     parts = [
-        [home((sums[0][:128] + early_down.astype(F32)).astype(BF), 0), late_up],
-        [home((sums[0][128:] + early_up.astype(F32)).astype(BF), 1), late_down],
+        [home((sums[0][:128] + early_up.astype(F32)).astype(BF), 0), late_down],
+        [home((sums[0][128:] + early_down.astype(F32)).astype(BF), 1), late_up],
     ]
     pieces = [sum(part.astype(F32) for part in piece).astype(BF) for piece in parts]
     even = yl == 0

time: 101 us -> 97.7 us (0.967)
  waiting for transfers between devices: 29.4 us -> 24.9 us
  starting transfers between devices: 43.5 us -> 44.8 us
    ppermute x25, waiting for transfers between devices: 29.4 us -> 24.9 us  [moved(): return lax.ppermute(a, AXES, pairs)]
    ppermute x25, starting transfers between devices: 38 us -> 39.4 us  [moved(): return lax.ppermute(a, AXES, pairs)]
  transfers between devices with their start and end apart: 27 -> 27, of which waited for: 13 -> 11; matrix products, arithmetic and copies ran while one was open for 2% -> 2% of each run, Pallas kernels for 19% -> 20%
where the time goes in v16:
time: 97.7 us; the launch traced here: 97.5 us
  starting transfers between devices  44.8 us (46%)
  waiting for transfers between devices  24.9 us (25%)
  Pallas kernels  21.7 us (22%)
  other arithmetic  3.02 us (3%)
  local copies, waits for them, and re-layouts  2.03 us (2%)
  between operations  1.01 us (1%)
    ppermute x25, starting transfers between devices, moved(): return lax.ppermute(a, AXES, pairs)  39.4 us
    ppermute x25, waiting for transfers between devices, moved(): return lax.ppermute(a, AXES, pairs)  24.9 us
    pallas_call x5, Pallas kernels, call(): pl.pallas_call(kernel, out_shape=shapes, in_specs=specs, out_specs=whole(...  19.5 us
    ppermute x2, starting transfers between devices, local(): lax.ppermute(half, CTX, [(i, (i + by) % 16) for i in range(16)])  5.46 us
    pallas_call x1, Pallas kernels, quarters(): pl.pallas_call(quarter_kernel, out_shape=[jax.ShapeDtypeStruct((64, 1792)...  2.21 us
  transfers between devices with their start and end apart: 27, of which 11 were waited for; matrix products, arithmetic and copies ran while one was open for 2% of the time, Pallas kernels for 20%

profile of v16, /device:TPU:1, one launch (start us, length us, event | category | flops | bytes accessed | tf_op | source)
XLA Modules:
  0.0 97.5 jit_solution(11346455360722829650)
XLA Ops:
  0.0 1.6 %dynamic-slice_bitcast_fusion = bf16[576,128]{1,0:T(8,128)(2,1)} fusion(bf16[256,576]{0,1:T(8,128)(2,1)} %param.9, s32[]{:T(128)S(6)} %select_n.72), kind=kLoop, calls=%fused_computation.30 | loop fusion | bytes 294916 | tf_op jit(solution)/shard_map/dynamic_slice | solution.py:307
  1.6 3.8 %collective-permute-start.1 = (bf16[576,128]{1,0:T(8,128)(2,1)}, bf16[576,128]{1,0:T(8,128)(2,1)S(1)}, u32[]{:S(2)}, u32[]{:S(2)}) collective-permute-start(bf16[576,128]{1,0:T(8,128)(2,1)} %dynamic-slice_bitcast_fusion), channel_id=1, source_target_pairs={{0,32},{16,48},{32,64},{48,80},{64,96},{80,112},{96,128},{112,144}... | collective-permute-start | bytes 442376 | tf_op jit(solution)/shard_map/ppermute | solution.py:309
  5.4 1.6 %collective-permute-start = (bf16[576,128]{1,0:T(8,128)(2,1)}, bf16[576,128]{1,0:T(8,128)(2,1)S(1)}, u32[]{:S(2)}, u32[]{:S(2)}) collective-permute-start(bf16[576,128]{1,0:T(8,128)(2,1)} %dynamic-slice_bitcast_fusion), channel_id=1, source_target_pairs={{0,16},{16,32},{32,48},{48,64},{64,80},{80,96},{96,112},{112,128},... | collective-permute-start | bytes 442376 | tf_op jit(solution)/shard_map/ppermute | solution.py:309
  7.0 2.2 %quarters.1 = (bf16[64,1792]{1,0:T(8,128)(2,1)}, bf16[64,1792]{1,0:T(8,128)(2,1)}) custom-call(bf16[64,7168]{1,0:T(8,128)(2,1)} %bitcast.35), custom_call_target="tpu_custom_call" | custom-call | bytes 2097152 | tf_op jit(solution)/shard_map/quarters/pallas_call | solution.py:251
  9.2 2.8 %collective-permute-start.11 = (bf16[64,1792]{1,0:T(8,128)(2,1)}, bf16[64,1792]{1,0:T(8,128)(2,1)S(1)}, u32[]{:S(2)}, u32[]{:S(2)}) collective-permute-start(bf16[64,1792]{1,0:T(8,128)(2,1)} %get-tuple-element.27.refs_5_), channel_id=1, source_target_pairs={{0,16},{1,17},{2,18},{3,19},{4,20},{5,21},{6,22},{7,23},{8,24},{9,... | collective-permute-start | bytes 688136 | tf_op jit(solution)/shard_map/ppermute | solution.py:33
  12.1 0.8 collective-permute-start.7
  12.9 1.9 %collective-permute-start.8 = (bf16[64,1792]{1,0:T(8,128)(2,1)}, bf16[64,1792]{1,0:T(8,128)(2,1)S(1)}, u32[]{:S(2)}, u32[]{:S(2)}) collective-permute-start(bf16[64,1792]{1,0:T(8,128)(2,1)} %get-tuple-element.28), channel_id=1, source_target_pairs={{0,129},{1,128},{2,131},{3,130},{4,133},{5,132},{6,135},{7,134},{8... | collective-permute-start | bytes 688136 | tf_op jit(solution)/shard_map/ppermute | solution.py:33
  15.0 0.1 fusion.reorder
  15.1 0.8 fusion.11
  15.9 6.9 %queries.1 = (bf16[1024,640]{1,0:T(8,128)(2,1)}, bf16[1024,640]{1,0:T(8,128)(2,1)}) custom-call(bf16[256,1536]{1,0:T(8,128)(2,1)} %rows.1, bf16[1536,1536]{1,0:T(8,128)(2,1)} %w_query.1, bf16[8,128,512]{2,1,0:T(8,128)(2,1)} %w_key_up.1, f32[64,128]{1,0:T(8,128)} %get-tuple-element.59.cosines, f32[64,128]{1,0:T(8,128)} %get-tuple-element.58.sines), custom_call_target="tpu_custom_call" | custom-call | flops 1476395008 | bytes 8388608 | tf_op jit(solution)/shard_map/queries/pallas_call | solution.py:263
  22.9 2.0 %collective-permute-start.2 = (bf16[576,256]{1,0:T(8,128)(2,1)S(1)}, bf16[576,256]{1,0:T(8,128)(2,1)S(1)}, u32[]{:S(2)}, u32[]{:S(2)}) collective-permute-start(bf16[576,256]{1,0:T(8,128)(2,1)S(1)} %pad_maximum_fusion.2), channel_id=1, source_target_pairs={{0,2},{1,3},{2,0},{3,1},{4,6},{5,7},{6,4},{7,5},{8,10},{9,11},{10,... | collective-permute-start | bytes 884744 | tf_op jit(solution)/shard_map/ppermute | solution.py:33
  25.0 0.6 collective-permute-start.9
  25.6 1.2 %collective-permute-start.12 = (bf16[128,1792]{1,0:T(8,128)(2,1)S(1)}, bf16[128,1792]{1,0:T(8,128)(2,1)S(1)}, u32[]{:S(2)}, u32[]{:S(2)}) collective-permute-start(bf16[128,1792]{1,0:T(8,128)(2,1)S(1)} %get-tuple-element.31), channel_id=1, source_target_pairs={{0,16},{1,17},{2,18},{3,19},{4,20},{5,21},{6,22},{7,23},{8,24},{9,... | collective-permute-start | bytes 1376264 | tf_op jit(solution)/shard_map/ppermute | solution.py:33
  26.8 0.4 multiply_sine_fusion
  27.9 0.6 keys.1
  28.6 7.4 %attend.1.refs_0_ = bf16[256,1024]{1,0:T(8,128)(2,1)S(1)} custom-call(bf16[1024,640]{1,0:T(8,128)(2,1)S(1)} %copy-done.2, bf16[1024,640]{1,0:T(8,128)(2,1)S(1)} %copy-done.3, bf16[640,768]{1,0:T(8,128)(2,1)S(1)} %get-tuple-element.25.keys, f32[256,768]{1,0:T(8,128)S(1)} %get-tuple-element.26.hidden, bf16[8,512,128]{2,1,0:T(8,128)(2,1)S(1)} %copy-done.4, ...), custom_call_target="tpu_custom_call" | custom-call | flops 3892314112 | bytes 10485760 | tf_op jit(solution)/shard_map/attend/pallas_call | solution.py:263
  36.0 0.7 collective-permute-done.9.refs_7_
  36.6 2.2 %collective-permute-start.10 = (bf16[128,1792]{1,0:T(8,128)(2,1)S(1)}, bf16[128,1792]{1,0:T(8,128)(2,1)S(1)}, u32[]{:S(2)}, u32[]{:S(2)}) collective-permute-start(bf16[128,1792]{1,0:T(8,128)(2,1)S(1)} %collective-permute-done.9.refs_7_), channel_id=1, source_target_pairs={{0,112},{1,113},{2,114},{3,115},{4,116},{5,117},{6,118},{7,119},{8... | collective-permute-start | bytes 1376264 | tf_op jit(solution)/shard_map/ppermute | solution.py:33
  38.9 1.6 %collective-permute-start.5 = (bf16[256,1024]{1,0:T(8,128)(2,1)S(1)}, bf16[256,1024]{1,0:T(8,128)(2,1)S(1)}, u32[]{:S(2)}, u32[]{:S(2)}) collective-permute-start(bf16[256,1024]{1,0:T(8,128)(2,1)S(1)} %attend.1.refs_0_), channel_id=1, source_target_pairs={{0,129},{1,128},{2,131},{3,130},{4,133},{5,132},{6,135},{7,134},{8... | collective-permute-start | bytes 1572872 | tf_op jit(solution)/shard_map/ppermute | solution.py:33
  40.4 8.2 %collective-permute-done.10.refs_8_ = bf16[128,1792]{1,0:T(8,128)(2,1)S(1)} collective-permute-done((bf16[128,1792]{1,0:T(8,128)(2,1)S(1)}, bf16[128,1792]{1,0:T(8,128)(2,1)S(1)}, u32[]{:S(2)}, u32[]{:S(2)}) %collective-permute-start.10) | collective-permute-done | bytes 458784 | tf_op jit(solution)/shard_map/ppermute | solution.py:33
  48.6 2.7 %collective-permute-start.15 = (bf16[64,1792]{1,0:T(8,128)(2,1)S(1)}, bf16[64,1792]{1,0:T(8,128)(2,1)S(1)}, u32[]{:S(2)}, u32[]{:S(2)}) collective-permute-start(bf16[64,1792]{1,0:T(8,128)(2,1)S(1)} %slice.106), channel_id=1, source_target_pairs={{0,112},{1,113},{2,114},{3,115},{4,116},{5,117},{6,118},{7,119},{8... | collective-permute-start | bytes 688136 | tf_op jit(solution)/shard_map/ppermute | solution.py:33
  51.3 0.8 collective-permute-done.5.refs_4_
  52.3 1.5 %collective-permute-start.4 = (bf16[128,1024]{1,0:T(8,128)(2,1)S(1)}, bf16[128,1024]{1,0:T(8,128)(2,1)S(1)}, u32[]{:S(2)}, u32[]{:S(2)}) collective-permute-start(bf16[128,1024]{1,0:T(8,128)(2,1)S(1)} %slice.104), channel_id=1, source_target_pairs={{0,129},{1,128},{2,131},{3,130},{4,133},{5,132},{6,135},{7,134},{8... | collective-permute-start | bytes 786440 | tf_op jit(solution)/shard_map/ppermute | solution.py:33
  53.8 0.5 collective-permute-done.15.refs_14_
  54.3 3.6 %collective-permute-start.16 = (bf16[64,1792]{1,0:T(8,128)(2,1)S(1)}, bf16[64,1792]{1,0:T(8,128)(2,1)S(1)}, u32[]{:S(2)}, u32[]{:S(2)}) collective-permute-start(bf16[64,1792]{1,0:T(8,128)(2,1)S(1)} %collective-permute-done.15.refs_14_), channel_id=1, source_target_pairs={{0,112},{1,113},{2,114},{3,115},{4,116},{5,117},{6,118},{7,119},{8... | collective-permute-start | bytes 688136 | tf_op jit(solution)/shard_map/ppermute | solution.py:33
  57.9 1.2 %collective-permute-done.4.refs_2_ = bf16[128,1024]{1,0:T(8,128)(2,1)S(1)} collective-permute-done((bf16[128,1024]{1,0:T(8,128)(2,1)S(1)}, bf16[128,1024]{1,0:T(8,128)(2,1)S(1)}, u32[]{:S(2)}, u32[]{:S(2)}) %collective-permute-start.4) | collective-permute-done | bytes 262176 | tf_op jit(solution)/shard_map/ppermute | solution.py:33
  59.1 1.7 %collective-permute-done.16.refs_15_ = bf16[64,1792]{1,0:T(8,128)(2,1)S(1)} collective-permute-done((bf16[64,1792]{1,0:T(8,128)(2,1)S(1)}, bf16[64,1792]{1,0:T(8,128)(2,1)S(1)}, u32[]{:S(2)}, u32[]{:S(2)}) %collective-permute-start.16) | collective-permute-done | bytes 229408 | tf_op jit(solution)/shard_map/ppermute | solution.py:33
  60.8 1.7 %collective-permute-done.14.refs_9_ = bf16[128,1792]{1,0:T(8,128)(2,1)S(1)} collective-permute-done((bf16[128,1792]{1,0:T(8,128)(2,1)S(1)}, bf16[128,1792]{1,0:T(8,128)(2,1)S(1)}, u32[]{:S(2)}, u32[]{:S(2)}) %collective-permute-start.14) | collective-permute-done | bytes 458784 | tf_op jit(solution)/shard_map/ppermute | solution.py:33
  62.5 2.3 %project.3 = (bf16[256,896]{1,0:T(8,128)(2,1)S(1)}, bf16[3,256,896]{2,1,0:T(8,128)(2,1)S(1)}) custom-call(bf16[256,1024]{1,0:T(8,128)(2,1)S(1)} %attend.1.refs_0_, bf16[256,1024]{1,0:T(8,128)(2,1)S(1)} %collective-permute-done.3.refs_1_, bf16[128,1024]{1,0:T(8,128)(2,1)S(1)} %collective-permute-done.4.refs_2_, ...), custom_call_target="tpu_custom_call" | custom-call | flops 1879048192 | bytes 8388608 | tf_op jit(solution)/shard_map/project/pallas_call | solution.py:263
  64.8 3.1 %collective-permute-start.17 = (bf16[3,256,896]{2,1,0:T(8,128)(2,1)S(1)}, bf16[3,256,896]{2,1,0:T(8,128)(2,1)S(1)}, u32[]{:S(2)}, u32[]{:S(2)}) collective-permute-start(bf16[3,256,896]{2,1,0:T(8,128)(2,1)S(1)} %get-tuple-element.34), channel_id=1, source_target_pairs={{0,2},{1,3},{2,0},{3,1},{4,6},{5,7},{6,4},{7,5},{8,10},{9,11},{10,... | collective-permute-start | bytes 4128776 | tf_op jit(solution)/shard_map/ppermute | solution.py:33
  67.8 0.1 collective-permute-start.18
  67.9 2.3 %project.2 = (f32[256,896]{1,0:T(8,128)S(1)}, f32[3,256,896]{2,1,0:T(8,128)S(1)}) custom-call(bf16[256,1024]{1,0:T(8,128)(2,1)S(1)} %attend.1.refs_0_, bf16[256,1024]{1,0:T(8,128)(2,1)S(1)} %collective-permute-done.3.refs_1_, bf16[128,1024]{1,0:T(8,128)(2,1)S(1)} %collective-permute-done.4.refs_2_, bf16[128,1024]{1,0:T(8,128)(2,1)S(1)} %collective-permute-done.6.refs_3_, ...), custom_call_target="tpu_custom_call" | custom-call | flops 1879048192 | bytes 8388608 | tf_op jit(solution)/shard_map/project/pallas_call | solution.py:263
  70.3 0.3 collective-permute-done.17
  70.6 0.2 convert_add_fusion.2
  70.9 0.4 collective-permute-done.18
  71.2 1.2 %collective-permute-start.19 = (bf16[128,896]{1,0:T(8,128)(2,1)S(1)}, bf16[128,896]{1,0:T(8,128)(2,1)S(1)}, u32[]{:S(2)}, u32[]{:S(2)}) collective-permute-start(bf16[128,896]{1,0:T(8,128)(2,1)S(1)} %fusion.9), channel_id=1, source_target_pairs={{0,4},{1,5},{2,6},{3,7},{4,8},{5,9},{6,10},{7,11},{8,12},{9,13},{1... | collective-permute-start | bytes 688136 | tf_op jit(solution)/shard_map/ppermute | solution.py:33
  72.5 1.5 %collective-permute-start.23 = (bf16[128,896]{1,0:T(8,128)(2,1)S(1)}, bf16[128,896]{1,0:T(8,128)(2,1)S(1)}, u32[]{:S(2)}, u32[]{:S(2)}) collective-permute-start(bf16[128,896]{1,0:T(8,128)(2,1)S(1)} %fusion.10), channel_id=1, source_target_pairs={{0,12},{1,13},{2,14},{3,15},{4,0},{5,1},{6,2},{7,3},{8,4},{9,5},{1... | collective-permute-start | bytes 688136 | tf_op jit(solution)/shard_map/ppermute | solution.py:33
  74.1 2.7 %collective-permute-start.21 = (bf16[128,896]{1,0:T(8,128)(2,1)S(1)}, bf16[128,896]{1,0:T(8,128)(2,1)S(1)}, u32[]{:S(2)}, u32[]{:S(2)}) collective-permute-start(bf16[128,896]{1,0:T(8,128)(2,1)S(1)} %get-tuple-element.49), channel_id=1, source_target_pairs={{0,12},{1,13},{2,14},{3,15},{4,0},{5,1},{6,2},{7,3},{8,4},{9,5},{1... | collective-permute-start | bytes 688136 | tf_op jit(solution)/shard_map/ppermute | solution.py:33
  76.8 2.5 %collective-permute-done.19 = bf16[128,896]{1,0:T(8,128)(2,1)S(1)} collective-permute-done((bf16[128,896]{1,0:T(8,128)(2,1)S(1)}, bf16[128,896]{1,0:T(8,128)(2,1)S(1)}, u32[]{:S(2)}, u32[]{:S(2)}) %collective-permute-start.19) | collective-permute-done | bytes 229408 | tf_op jit(solution)/shard_map/ppermute | solution.py:33
  79.4 3.5 %collective-permute-start.24 = (bf16[128,896]{1,0:T(8,128)(2,1)S(1)}, bf16[128,896]{1,0:T(8,128)(2,1)S(1)}, u32[]{:S(2)}, u32[]{:S(2)}) collective-permute-start(bf16[128,896]{1,0:T(8,128)(2,1)S(1)} %get-tuple-element.46), channel_id=1, source_target_pairs={{0,1},{1,0},{2,129},{3,128},{4,5},{5,4},{6,133},{7,132},{8,9},{9,8... | collective-permute-start | bytes 688136 | tf_op jit(solution)/shard_map/ppermute | solution.py:33
  82.9 1.9 %collective-permute-start.20 = (bf16[128,896]{1,0:T(8,128)(2,1)S(1)}, bf16[128,896]{1,0:T(8,128)(2,1)S(1)}, u32[]{:S(2)}, u32[]{:S(2)}) collective-permute-start(bf16[128,896]{1,0:T(8,128)(2,1)S(1)} %get-tuple-element.47), channel_id=1, source_target_pairs={{0,0},{1,1},{2,128},{3,129},{4,4},{5,5},{6,132},{7,133},{8,8},{9,9... | collective-permute-start | bytes 688136 | tf_op jit(solution)/shard_map/ppermute | solution.py:33
  84.8 1.5 %collective-permute-start.26 = (bf16[128,896]{1,0:T(8,128)(2,1)S(1)}, bf16[128,896]{1,0:T(8,128)(2,1)S(1)}, u32[]{:S(2)}, u32[]{:S(2)}) collective-permute-start(bf16[128,896]{1,0:T(8,128)(2,1)S(1)} %fusion.2), channel_id=1, source_target_pairs={{0,5},{1,4},{2,133},{3,132},{4,9},{5,8},{6,137},{7,136},{8,13},{9,... | collective-permute-start | bytes 688136 | tf_op jit(solution)/shard_map/ppermute | solution.py:33
  86.4 2.9 %collective-permute-start.22 = (bf16[128,896]{1,0:T(8,128)(2,1)S(1)}, bf16[128,896]{1,0:T(8,128)(2,1)S(1)}, u32[]{:S(2)}, u32[]{:S(2)}) collective-permute-start(bf16[128,896]{1,0:T(8,128)(2,1)S(1)} %fusion.6), channel_id=1, source_target_pairs={{0,12},{1,13},{2,140},{3,141},{4,0},{5,1},{6,128},{7,129},{8,4},{9... | collective-permute-start | bytes 688136 | tf_op jit(solution)/shard_map/ppermute | solution.py:33
  89.2 7.0 %collective-permute-done.20 = bf16[128,896]{1,0:T(8,128)(2,1)S(1)} collective-permute-done((bf16[128,896]{1,0:T(8,128)(2,1)S(1)}, bf16[128,896]{1,0:T(8,128)(2,1)S(1)}, u32[]{:S(2)}, u32[]{:S(2)}) %collective-permute-start.20) | collective-permute-done | bytes 229408 | tf_op jit(solution)/shard_map/ppermute | solution.py:33
  96.2 0.1 broadcast_select_fusion.1
  96.4 0.1 fusion.33
  96.5 0.1 fusion.34
  96.6 0.9 maximum_maximum_fusion
  (52 shorter events, 0.9 us)
Async XLA Ops:
  1.6 21.3 %collective-permute-start.1 = (bf16[576,128]{1,0:T(8,128)(2,1)}, bf16[576,128]{1,0:T(8,128)(2,1)S(1)}, u32[]{:S(2)}, u32[]{:S(2)}) collective-permute-start(bf16[576,128]{1,0:T(8,128)(2,1)} %dynamic-slice_bitcast_fusion), channel_id=1, source_target_pairs={{0,32},{16,48},{32,64},{48,80},{64,96},{80,112},{96,128},{112,144}... | collective-permute-start | bytes 442376 | tf_op jit(solution)/shard_map/ppermute | solution.py:309
  5.4 17.5 %collective-permute-start = (bf16[576,128]{1,0:T(8,128)(2,1)}, bf16[576,128]{1,0:T(8,128)(2,1)S(1)}, u32[]{:S(2)}, u32[]{:S(2)}) collective-permute-start(bf16[576,128]{1,0:T(8,128)(2,1)} %dynamic-slice_bitcast_fusion), channel_id=1, source_target_pairs={{0,16},{16,32},{32,48},{48,64},{64,80},{80,96},{96,112},{112,128},... | collective-permute-start | bytes 442376 | tf_op jit(solution)/shard_map/ppermute | solution.py:309
  9.2 15.7 %collective-permute-start.11 = (bf16[64,1792]{1,0:T(8,128)(2,1)}, bf16[64,1792]{1,0:T(8,128)(2,1)S(1)}, u32[]{:S(2)}, u32[]{:S(2)}) collective-permute-start(bf16[64,1792]{1,0:T(8,128)(2,1)} %get-tuple-element.27.refs_5_), channel_id=1, source_target_pairs={{0,16},{1,17},{2,18},{3,19},{4,20},{5,21},{6,22},{7,23},{8,24},{9,... | collective-permute-start | bytes 688136 | tf_op jit(solution)/shard_map/ppermute | solution.py:33
  12.1 12.9 %collective-permute-start.7 = (bf16[64,1792]{1,0:T(8,128)(2,1)}, bf16[64,1792]{1,0:T(8,128)(2,1)S(1)}, u32[]{:S(2)}, u32[]{:S(2)}) collective-permute-start(bf16[64,1792]{1,0:T(8,128)(2,1)} %get-tuple-element.27.refs_5_), channel_id=1, source_target_pairs={{0,112},{1,113},{2,114},{3,115},{4,116},{5,117},{6,118},{7,119},{8... | collective-permute-start | bytes 688136 | tf_op jit(solution)/shard_map/ppermute | solution.py:33
  12.9 12.0 %collective-permute-start.8 = (bf16[64,1792]{1,0:T(8,128)(2,1)}, bf16[64,1792]{1,0:T(8,128)(2,1)S(1)}, u32[]{:S(2)}, u32[]{:S(2)}) collective-permute-start(bf16[64,1792]{1,0:T(8,128)(2,1)} %get-tuple-element.28), channel_id=1, source_target_pairs={{0,129},{1,128},{2,131},{3,130},{4,133},{5,132},{6,135},{7,134},{8... | collective-permute-start | bytes 688136 | tf_op jit(solution)/shard_map/ppermute | solution.py:33
  15.9 12.6 %copy-start.4 = (bf16[8,512,128]{2,1,0:T(8,128)(2,1)S(1)}, bf16[8,512,128]{2,1,0:T(8,128)(2,1)}, u32[]{:S(2)}) copy-start(bf16[8,512,128]{2,1,0:T(8,128)(2,1)} %w_value_up.1) | copy-start | bytes 3145732
  22.8 5.1 %copy-start = (bf16[256,576]{0,1:T(8,128)(2,1)S(1)}, bf16[256,576]{0,1:T(8,128)(2,1)}, u32[]{:S(2)}) copy-start(bf16[256,576]{0,1:T(8,128)(2,1)} %param.9) | copy-start | bytes 884740
  22.8 5.1 %copy-start.1 = (bf16[512,576]{0,1:T(8,128)(2,1)S(1)}, bf16[512,576]{0,1:T(8,128)(2,1)}, u32[]{:S(2)}) copy-start(bf16[512,576]{0,1:T(8,128)(2,1)} %param.10) | copy-start | bytes 1769476
  22.9 5.6 %copy-start.2 = (bf16[1024,640]{1,0:T(8,128)(2,1)S(1)}, bf16[1024,640]{1,0:T(8,128)(2,1)}, u32[]{:S(2)}) copy-start(bf16[1024,640]{1,0:T(8,128)(2,1)} %get-tuple-element.23.queries) | copy-start | bytes 3932164
  22.9 5.6 %copy-start.3 = (bf16[1024,640]{1,0:T(8,128)(2,1)S(1)}, bf16[1024,640]{1,0:T(8,128)(2,1)}, u32[]{:S(2)}) copy-start(bf16[1024,640]{1,0:T(8,128)(2,1)} %get-tuple-element.24.queries_next) | copy-start | bytes 3932164
  22.9 5.0 %collective-permute-start.2 = (bf16[576,256]{1,0:T(8,128)(2,1)S(1)}, bf16[576,256]{1,0:T(8,128)(2,1)S(1)}, u32[]{:S(2)}, u32[]{:S(2)}) collective-permute-start(bf16[576,256]{1,0:T(8,128)(2,1)S(1)} %pad_maximum_fusion.2), channel_id=1, source_target_pairs={{0,2},{1,3},{2,0},{3,1},{4,6},{5,7},{6,4},{7,5},{8,10},{9,11},{10,... | collective-permute-start | bytes 884744 | tf_op jit(solution)/shard_map/ppermute | solution.py:33
  25.0 11.6 %collective-permute-start.9 = (bf16[128,1792]{1,0:T(8,128)(2,1)S(1)}, bf16[128,1792]{1,0:T(8,128)(2,1)S(1)}, u32[]{:S(2)}, u32[]{:S(2)}) collective-permute-start(bf16[128,1792]{1,0:T(8,128)(2,1)S(1)} %get-tuple-element.29), channel_id=1, source_target_pairs={{0,112},{1,113},{2,114},{3,115},{4,116},{5,117},{6,118},{7,119},{8... | collective-permute-start | bytes 1376264 | tf_op jit(solution)/shard_map/ppermute | solution.py:33
  25.6 13.3 %collective-permute-start.12 = (bf16[128,1792]{1,0:T(8,128)(2,1)S(1)}, bf16[128,1792]{1,0:T(8,128)(2,1)S(1)}, u32[]{:S(2)}, u32[]{:S(2)}) collective-permute-start(bf16[128,1792]{1,0:T(8,128)(2,1)S(1)} %get-tuple-element.31), channel_id=1, source_target_pairs={{0,16},{1,17},{2,18},{3,19},{4,20},{5,21},{6,22},{7,23},{8,24},{9,... | collective-permute-start | bytes 1376264 | tf_op jit(solution)/shard_map/ppermute | solution.py:33
  35.9 26.6 %copy-start.5 = (bf16[64,1792]{1,0:T(8,128)(2,1)S(1)}, bf16[64,1792]{1,0:T(8,128)(2,1)}, u32[]{:S(2)}) copy-start(bf16[64,1792]{1,0:T(8,128)(2,1)} %get-tuple-element.27.refs_5_) | copy-start | bytes 688132
  36.6 12.0 %collective-permute-start.10 = (bf16[128,1792]{1,0:T(8,128)(2,1)S(1)}, bf16[128,1792]{1,0:T(8,128)(2,1)S(1)}, u32[]{:S(2)}, u32[]{:S(2)}) collective-permute-start(bf16[128,1792]{1,0:T(8,128)(2,1)S(1)} %collective-permute-done.9.refs_7_), channel_id=1, source_target_pairs={{0,112},{1,113},{2,114},{3,115},{4,116},{5,117},{6,118},{7,119},{8... | collective-permute-start | bytes 1376264 | tf_op jit(solution)/shard_map/ppermute | solution.py:33
  38.9 12.5 %collective-permute-start.13 = (bf16[128,1792]{1,0:T(8,128)(2,1)S(1)}, bf16[128,1792]{1,0:T(8,128)(2,1)S(1)}, u32[]{:S(2)}, u32[]{:S(2)}) collective-permute-start(bf16[128,1792]{1,0:T(8,128)(2,1)S(1)} %collective-permute-done.12.refs_11_), channel_id=1, source_target_pairs={{0,16},{1,17},{2,18},{3,19},{4,20},{5,21},{6,22},{7,23},{8,24},{9,... | collective-permute-start | bytes 1376264 | tf_op jit(solution)/shard_map/ppermute | solution.py:33
  38.9 13.3 %collective-permute-start.5 = (bf16[256,1024]{1,0:T(8,128)(2,1)S(1)}, bf16[256,1024]{1,0:T(8,128)(2,1)S(1)}, u32[]{:S(2)}, u32[]{:S(2)}) collective-permute-start(bf16[256,1024]{1,0:T(8,128)(2,1)S(1)} %attend.1.refs_0_), channel_id=1, source_target_pairs={{0,129},{1,128},{2,131},{3,130},{4,133},{5,132},{6,135},{7,134},{8... | collective-permute-start | bytes 1572872 | tf_op jit(solution)/shard_map/ppermute | solution.py:33
  40.4 11.8 %collective-permute-start.3 = (bf16[256,1024]{1,0:T(8,128)(2,1)S(1)}, bf16[256,1024]{1,0:T(8,128)(2,1)S(1)}, u32[]{:S(2)}, u32[]{:S(2)}) collective-permute-start(bf16[256,1024]{1,0:T(8,128)(2,1)S(1)} %attend.1.refs_0_), channel_id=1, source_target_pairs={{0,1},{1,0},{2,3},{3,2},{4,5},{5,4},{6,7},{7,6},{8,9},{9,8},{10,11... | collective-permute-start | bytes 1572872 | tf_op jit(solution)/shard_map/ppermute | solution.py:33
  48.6 5.7 %collective-permute-start.15 = (bf16[64,1792]{1,0:T(8,128)(2,1)S(1)}, bf16[64,1792]{1,0:T(8,128)(2,1)S(1)}, u32[]{:S(2)}, u32[]{:S(2)}) collective-permute-start(bf16[64,1792]{1,0:T(8,128)(2,1)S(1)} %slice.106), channel_id=1, source_target_pairs={{0,112},{1,113},{2,114},{3,115},{4,116},{5,117},{6,118},{7,119},{8... | collective-permute-start | bytes 688136 | tf_op jit(solution)/shard_map/ppermute | solution.py:33
  51.3 11.2 %collective-permute-start.14 = (bf16[128,1792]{1,0:T(8,128)(2,1)S(1)}, bf16[128,1792]{1,0:T(8,128)(2,1)S(1)}, u32[]{:S(2)}, u32[]{:S(2)}) collective-permute-start(bf16[128,1792]{1,0:T(8,128)(2,1)S(1)} %collective-permute-done.13.refs_10_), channel_id=1, source_target_pairs={{0,16},{1,17},{2,18},{3,19},{4,20},{5,21},{6,22},{7,23},{8,24},{9,... | collective-permute-start | bytes 1376264 | tf_op jit(solution)/shard_map/ppermute | solution.py:33
  52.1 5.7 %collective-permute-start.6 = (bf16[128,1024]{1,0:T(8,128)(2,1)S(1)}, bf16[128,1024]{1,0:T(8,128)(2,1)S(1)}, u32[]{:S(2)}, u32[]{:S(2)}) collective-permute-start(bf16[128,1024]{1,0:T(8,128)(2,1)S(1)} %slice.105), channel_id=1, source_target_pairs={{0,1},{1,0},{2,3},{3,2},{4,5},{5,4},{6,7},{7,6},{8,9},{9,8},{10,11... | collective-permute-start | bytes 786440 | tf_op jit(solution)/shard_map/ppermute | solution.py:33
  52.3 6.8 %collective-permute-start.4 = (bf16[128,1024]{1,0:T(8,128)(2,1)S(1)}, bf16[128,1024]{1,0:T(8,128)(2,1)S(1)}, u32[]{:S(2)}, u32[]{:S(2)}) collective-permute-start(bf16[128,1024]{1,0:T(8,128)(2,1)S(1)} %slice.104), channel_id=1, source_target_pairs={{0,129},{1,128},{2,131},{3,130},{4,133},{5,132},{6,135},{7,134},{8... | collective-permute-start | bytes 786440 | tf_op jit(solution)/shard_map/ppermute | solution.py:33
  54.3 6.5 %collective-permute-start.16 = (bf16[64,1792]{1,0:T(8,128)(2,1)S(1)}, bf16[64,1792]{1,0:T(8,128)(2,1)S(1)}, u32[]{:S(2)}, u32[]{:S(2)}) collective-permute-start(bf16[64,1792]{1,0:T(8,128)(2,1)S(1)} %collective-permute-done.15.refs_14_), channel_id=1, source_target_pairs={{0,112},{1,113},{2,114},{3,115},{4,116},{5,117},{6,118},{7,119},{8... | collective-permute-start | bytes 688136 | tf_op jit(solution)/shard_map/ppermute | solution.py:33
  64.8 5.8 %collective-permute-start.17 = (bf16[3,256,896]{2,1,0:T(8,128)(2,1)S(1)}, bf16[3,256,896]{2,1,0:T(8,128)(2,1)S(1)}, u32[]{:S(2)}, u32[]{:S(2)}) collective-permute-start(bf16[3,256,896]{2,1,0:T(8,128)(2,1)S(1)} %get-tuple-element.34), channel_id=1, source_target_pairs={{0,2},{1,3},{2,0},{3,1},{4,6},{5,7},{6,4},{7,5},{8,10},{9,11},{10,... | collective-permute-start | bytes 4128776 | tf_op jit(solution)/shard_map/ppermute | solution.py:33
  67.8 3.4 %collective-permute-start.18 = (bf16[256,896]{1,0:T(8,128)(2,1)S(1)}, bf16[256,896]{1,0:T(8,128)(2,1)S(1)}, u32[]{:S(2)}, u32[]{:S(2)}) collective-permute-start(bf16[256,896]{1,0:T(8,128)(2,1)S(1)} %get-tuple-element.35), channel_id=1, source_target_pairs={{0,2},{1,3},{2,0},{3,1},{4,6},{5,7},{6,4},{7,5},{8,10},{9,11},{10,... | collective-permute-start | bytes 1376264 | tf_op jit(solution)/shard_map/ppermute | solution.py:33
  71.2 8.0 %collective-permute-start.19 = (bf16[128,896]{1,0:T(8,128)(2,1)S(1)}, bf16[128,896]{1,0:T(8,128)(2,1)S(1)}, u32[]{:S(2)}, u32[]{:S(2)}) collective-permute-start(bf16[128,896]{1,0:T(8,128)(2,1)S(1)} %fusion.9), channel_id=1, source_target_pairs={{0,4},{1,5},{2,6},{3,7},{4,8},{5,9},{6,10},{7,11},{8,12},{9,13},{1... | collective-permute-start | bytes 688136 | tf_op jit(solution)/shard_map/ppermute | solution.py:33
  72.5 6.8 %collective-permute-start.23 = (bf16[128,896]{1,0:T(8,128)(2,1)S(1)}, bf16[128,896]{1,0:T(8,128)(2,1)S(1)}, u32[]{:S(2)}, u32[]{:S(2)}) collective-permute-start(bf16[128,896]{1,0:T(8,128)(2,1)S(1)} %fusion.10), channel_id=1, source_target_pairs={{0,12},{1,13},{2,14},{3,15},{4,0},{5,1},{6,2},{7,3},{8,4},{9,5},{1... | collective-permute-start | bytes 688136 | tf_op jit(solution)/shard_map/ppermute | solution.py:33
  74.1 10.7 %collective-permute-start.25 = (bf16[128,896]{1,0:T(8,128)(2,1)S(1)}, bf16[128,896]{1,0:T(8,128)(2,1)S(1)}, u32[]{:S(2)}, u32[]{:S(2)}) collective-permute-start(bf16[128,896]{1,0:T(8,128)(2,1)S(1)} %get-tuple-element.48), channel_id=1, source_target_pairs={{0,4},{1,5},{2,6},{3,7},{4,8},{5,9},{6,10},{7,11},{8,12},{9,13},{1... | collective-permute-start | bytes 688136 | tf_op jit(solution)/shard_map/ppermute | solution.py:33
  74.1 12.2 %collective-permute-start.21 = (bf16[128,896]{1,0:T(8,128)(2,1)S(1)}, bf16[128,896]{1,0:T(8,128)(2,1)S(1)}, u32[]{:S(2)}, u32[]{:S(2)}) collective-permute-start(bf16[128,896]{1,0:T(8,128)(2,1)S(1)} %get-tuple-element.49), channel_id=1, source_target_pairs={{0,12},{1,13},{2,14},{3,15},{4,0},{5,1},{6,2},{7,3},{8,4},{9,5},{1... | collective-permute-start | bytes 688136 | tf_op jit(solution)/shard_map/ppermute | solution.py:33
  79.4 9.9 %collective-permute-start.24 = (bf16[128,896]{1,0:T(8,128)(2,1)S(1)}, bf16[128,896]{1,0:T(8,128)(2,1)S(1)}, u32[]{:S(2)}, u32[]{:S(2)}) collective-permute-start(bf16[128,896]{1,0:T(8,128)(2,1)S(1)} %get-tuple-element.46), channel_id=1, source_target_pairs={{0,1},{1,0},{2,129},{3,128},{4,5},{5,4},{6,133},{7,132},{8,9},{9,8... | collective-permute-start | bytes 688136 | tf_op jit(solution)/shard_map/ppermute | solution.py:33
  82.9 13.4 %collective-permute-start.20 = (bf16[128,896]{1,0:T(8,128)(2,1)S(1)}, bf16[128,896]{1,0:T(8,128)(2,1)S(1)}, u32[]{:S(2)}, u32[]{:S(2)}) collective-permute-start(bf16[128,896]{1,0:T(8,128)(2,1)S(1)} %get-tuple-element.47), channel_id=1, source_target_pairs={{0,0},{1,1},{2,128},{3,129},{4,4},{5,5},{6,132},{7,133},{8,8},{9,9... | collective-permute-start | bytes 688136 | tf_op jit(solution)/shard_map/ppermute | solution.py:33
  84.8 11.4 %collective-permute-start.26 = (bf16[128,896]{1,0:T(8,128)(2,1)S(1)}, bf16[128,896]{1,0:T(8,128)(2,1)S(1)}, u32[]{:S(2)}, u32[]{:S(2)}) collective-permute-start(bf16[128,896]{1,0:T(8,128)(2,1)S(1)} %fusion.2), channel_id=1, source_target_pairs={{0,5},{1,4},{2,133},{3,132},{4,9},{5,8},{6,137},{7,136},{8,13},{9,... | collective-permute-start | bytes 688136 | tf_op jit(solution)/shard_map/ppermute | solution.py:33
  86.4 9.9 %collective-permute-start.22 = (bf16[128,896]{1,0:T(8,128)(2,1)S(1)}, bf16[128,896]{1,0:T(8,128)(2,1)S(1)}, u32[]{:S(2)}, u32[]{:S(2)}) collective-permute-start(bf16[128,896]{1,0:T(8,128)(2,1)S(1)} %fusion.6), channel_id=1, source_target_pairs={{0,12},{1,13},{2,140},{3,141},{4,0},{5,1},{6,128},{7,129},{8,4},{9... | collective-permute-start | bytes 688136 | tf_op jit(solution)/shard_map/ppermute | solution.py:33
